TPU v7x, 32 devices: a whole 2x2x4 slice. The times are simulated.
32 devices in a mesh: groups: 2 (over x), tile: 16 (over z, y, core).
Axes of the slice: x: 2, y: 2, z: 4, core: 2. Of those that a mesh axis runs over, the one named last changes fastest.
Arguments:
- probes: float32 [8, 262144], P(None, ('groups', 'tile')), parts along dimension 1, may hold values from -6 to 6
- level_set: float32 [262144], P(('groups', 'tile')), parts along dimension 0, may hold values from -6 to 6
- unit_label: int32 [262144], P(('groups', 'tile')), parts along dimension 0, may hold values from 0 to 3
- contrast: float32 [8], P('groups'), parts along dimension 0, may hold values from 0.2 to 1.5
- station_weight: float32 [65536], P('groups'), parts along dimension 0, may hold values from 0.2 to 2
- u_factor: bfloat16 [4096, 32, 512], P(('groups', 'tile')), parts along dimension 0, may hold values from -1 to 1
- v_factor: bfloat16 [4096, 32, 512], P(('groups', 'tile')), parts along dimension 0, may hold values from -0.25 to 0.25
- col_owner: int32 [4096, 1], P('groups'), parts along dimension 0, may hold values from 0 to 15; in each aligned block of 128 rows (0 to 127, 128 to 255, ...) at most 16 rows name the same one
- col_local: int32 [4096], P('groups'), parts along dimension 0, may hold values from 0 to 15
- row_owner: int32 [4096, 1], P('groups'), parts along dimension 0, may hold values from 0 to 15; in each aligned block of 128 rows (0 to 127, 128 to 255, ...) at most 16 rows name the same one
- row_local: int32 [4096], P('groups'), parts along dimension 0, may hold values from 0 to 3
- tile_rank: int32 [4096], P('groups'), parts along dimension 0, may hold values from 8 to 32
Outputs:
- hessian_probes: float32 [8, 262144], P(None, ('groups', 'tile')), parts along dimension 1
There are 2 independent parts, one for each index of `groups`. A program takes and returns all parts, laid end to end along the dimension named above; each array names one. Nothing has to cross between parts.
Inputs may be any that keep to these rules, and one draw needn't show every extreme that they name: `col_owner`: among the 128 tiles of one device (aligned blocks of 128 entries) no owner is named more than 16 times, a bound that some block reaches. `row_owner`: among the 128 tiles of one device (aligned blocks of 128 entries) no owner is named more than 16 times, a bound that some block reaches.
All inputs are finite; a program needn't handle non-finite values.
Results may differ from a plain program's by a relative error of at most 0.005.
Values may be sent and summed in bfloat16 or wider, within the bound.
No kernel may reach another device: no remote copies, remote signals or barrier semaphores. Data moves between devices by JAX's collectives and lax.ppermute only.
A program may use at most 64 MiB of HBM per device.

v0:
```python
import jax
import jax.numpy as jnp
from jax import lax
from jax.sharding import PartitionSpec as P

HIGHEST = lax.Precision.HIGHEST


def rank_within(owner_table, target, capacity):
    matches = (owner_table == target).astype(jnp.int32)
    position = jnp.cumsum(matches, axis=-1) - 1
    slot_ids = jnp.arange(capacity, dtype=jnp.int32)
    chosen = (matches[:, None, :] == 1) & (position[:, None, :] == slot_ids[None, :, None])
    return chosen.astype(jnp.float32)


def sender_table(owner_table, local_table, target, capacity, block_count):
    chosen = rank_within(owner_table, target, capacity)
    local_match = (
        local_table[:, :, None] == jnp.arange(block_count, dtype=jnp.int32)[None, None, :]
    ).astype(jnp.float32)
    return jnp.einsum(
        "pqs,psb->pqb", chosen, local_match, precision=HIGHEST, preferred_element_type=jnp.float32
    )


def receiver_table(owner_mine, capacity, peer_count):
    count = owner_mine.shape[0]
    positions = jnp.arange(count, dtype=jnp.int32)
    earlier = (owner_mine[None, :] == owner_mine[:, None]) & (
        positions[None, :] < positions[:, None]
    )
    order = jnp.sum(earlier.astype(jnp.int32), axis=1)
    target = owner_mine * capacity + order
    return (target[:, None] == jnp.arange(peer_count * capacity, dtype=jnp.int32)[None, :]).astype(
        jnp.float32
    )


def shards(
    probes,
    level_set,
    unit_label,
    contrast,
    station_weight,
    u_factor,
    v_factor,
    col_owner,
    col_local,
    row_owner,
    row_local,
    tile_rank,
):
    peer_count = lax.axis_size("tile")
    own_index = lax.axis_index("tile")
    tile_count, rank_max, station_width = u_factor.shape
    cell_width = v_factor.shape[2]
    probe_count, cell_total = probes.shape
    cell_blocks = cell_total // cell_width
    station_blocks = station_weight.shape[0] // (peer_count * station_width)
    capacity = max(2, 2 * tile_count // peer_count)
    flat_cells = probe_count * cell_width
    flat_stations = probe_count * station_width
    col_owner_all = col_owner.reshape(peer_count, tile_count)
    col_local_all = col_local.reshape(peer_count, tile_count)
    row_owner_all = row_owner.reshape(peer_count, tile_count)
    row_local_all = row_local.reshape(peer_count, tile_count)
    col_owner_mine = lax.dynamic_index_in_dim(col_owner_all, own_index, 0, keepdims=False)
    col_local_mine = lax.dynamic_index_in_dim(col_local_all, own_index, 0, keepdims=False)
    row_owner_mine = lax.dynamic_index_in_dim(row_owner_all, own_index, 0, keepdims=False)
    row_local_mine = lax.dynamic_index_in_dim(row_local_all, own_index, 0, keepdims=False)
    rank_mine = lax.dynamic_index_in_dim(
        tile_rank.reshape(peer_count, tile_count), own_index, 0, keepdims=False
    )
    unit_count = contrast.shape[0]
    unit_match = (unit_label[None, :] == jnp.arange(unit_count, dtype=jnp.int32)[:, None]).astype(
        jnp.float32
    )
    scaling = jnp.sum(unit_match * contrast[:, None], axis=0) / (1.0 + level_set * level_set)
    scaled = (probes * scaling[None, :]).astype(jnp.bfloat16)
    cell_rows = (
        scaled.reshape(probe_count, cell_blocks, cell_width)
        .transpose(1, 0, 2)
        .reshape(cell_blocks, flat_cells)
    )
    col_global = col_owner_mine * cell_blocks + col_local_mine
    col_slots = receiver_table(col_owner_mine, capacity, peer_count)
    col_choice = sender_table(col_owner_all, col_local_all, own_index, capacity, cell_blocks)
    piece = lax.all_gather(cell_rows, "tile", axis=0, tiled=True)
    rows_here = piece.shape[0]
    match = (col_global[:, None] == jnp.arange(rows_here, dtype=jnp.int32)[None, :]).astype(
        jnp.bfloat16
    )
    fetched = jnp.dot(match, piece, preferred_element_type=jnp.float32)
    tile_cells = fetched.astype(jnp.bfloat16).reshape(tile_count, probe_count, cell_width)
    keep = (jnp.arange(rank_max, dtype=jnp.int32)[None, :] < rank_mine[:, None]).astype(
        jnp.float32
    )[:, None, :]
    coeff = jnp.einsum("tkc,trc->tkr", tile_cells, v_factor, preferred_element_type=jnp.float32)
    coeff = (coeff * keep).astype(jnp.bfloat16)
    partial_value = jnp.einsum(
        "tkr,trs->tks", coeff, u_factor, preferred_element_type=jnp.float32
    ).reshape(tile_count, flat_stations)
    row_global = row_owner_mine * station_blocks + row_local_mine
    match = (
        jnp.arange(station_blocks * lax.axis_size("tile"), dtype=jnp.int32)[:, None]
        == row_global[None, :]
    ).astype(jnp.float32)
    predicted = lax.psum_scatter(
        jnp.dot(match, partial_value, precision=HIGHEST, preferred_element_type=jnp.float32),
        "tile",
        scatter_dimension=0,
        tiled=True,
    )
    weight_mine = lax.dynamic_slice_in_dim(
        station_weight, own_index * station_blocks * station_width, station_blocks * station_width
    )
    weighted = (
        predicted.reshape(station_blocks, probe_count, station_width)
        * weight_mine.reshape(station_blocks, 1, station_width)
    ).astype(jnp.bfloat16)
    weighted = weighted.reshape(station_blocks, flat_stations)
    row_choice = sender_table(row_owner_all, row_local_all, own_index, capacity, station_blocks)
    outgoing_data = jnp.einsum(
        "pqb,bf->pqf", row_choice.astype(jnp.bfloat16), weighted, preferred_element_type=jnp.float32
    ).astype(jnp.bfloat16)
    incoming_data = lax.all_to_all(outgoing_data, "tile", split_axis=0, concat_axis=0, tiled=True)
    row_slots = receiver_table(row_owner_mine, capacity, peer_count)
    tile_data = jnp.dot(
        row_slots.astype(jnp.bfloat16),
        incoming_data.reshape(peer_count * capacity, flat_stations),
        preferred_element_type=jnp.float32,
    )
    tile_weighted = tile_data.astype(jnp.bfloat16).reshape(tile_count, probe_count, station_width)
    back = jnp.einsum("tks,trs->tkr", tile_weighted, u_factor, preferred_element_type=jnp.float32)
    back = (back * keep).astype(jnp.bfloat16)
    spread = jnp.einsum("tkr,trc->tkc", back, v_factor, preferred_element_type=jnp.float32).reshape(
        tile_count, flat_cells
    )
    slot_rows = col_slots.T.reshape(peer_count, capacity, tile_count)
    returned = jnp.einsum(
        "pqt,tf->pqf", slot_rows, spread, precision=HIGHEST, preferred_element_type=jnp.float32
    )
    arrived = lax.all_to_all(returned, "tile", split_axis=0, concat_axis=0, tiled=True)
    summed = jnp.einsum(
        "pqb,pqf->bf", col_choice, arrived, precision=HIGHEST, preferred_element_type=jnp.float32
    )
    gradient = (
        summed.reshape(cell_blocks, probe_count, cell_width)
        .transpose(1, 0, 2)
        .reshape(probe_count, cell_total)
    )
    return scaling[None, :] * gradient


def solution(mesh):
    placed = (
        P(None, ("groups", "tile")),
        P(("groups", "tile")),
        P(("groups", "tile")),
        P("groups"),
        P("groups"),
        P(("groups", "tile"), None, None),
        P(("groups", "tile"), None, None),
        P("groups", None),
        P("groups"),
        P("groups", None),
        P("groups"),
        P("groups"),
    )
    return jax.shard_map(
        shards, mesh=mesh, in_specs=placed, out_specs=P(None, ("groups", "tile")), check_vma=False
    )
```

profile of v0, /device:TPU:13, one launch (start us, length us, event | category | flops | bytes accessed | tf_op | source)
XLA Modules:
  0.0 335.7 jit_solution(17233125049416313303)
XLA Ops:
  6.5 0.0 all-gather.2.cloned.1.call-start
  6.5 0.9 select_reduce_fusion
  7.5 0.8 add_divide_fusion
  8.2 1.0 multiply_convert_fusion
  9.2 0.7 copy.15
  9.9 0.0 all-gather.2.cloned.1.call-update
  10.0 0.0 all-reduce.3.cloned.1.call-start
  10.0 0.7 dynamic_slice.24
  10.7 0.7 fusion.35
  11.4 0.7 fusion.38
  12.2 0.1 fusion.23
  12.3 38.9 %all-gather.2.cloned.1.call-done = bf16[256,4096]{1,0:T(8,128)(2,1)} async-done(((bf16[16,4096]{1,0:T(8,128)(2,1)}), bf16[256,4096]{1,0:T(8,128)(2,1)}) %all-gather.2.cloned.1.call-update) | async-done | bytes 2097168 | tf_op jit(solution)/shard_map/all_gather | solution.py:89
  51.2 2.1 convolution_convert_fusion.2
  53.2 0.4 copy.16
  53.6 5.2 %fusion.3 = f32[128,8,512]{2,1,0:T(8,128)S(1)} fusion(bf16[128,32,512]{2,1,0:T(8,128)(2,1)} %param.17, bf16[128,8,512]{2,1,0:T(8,128)(2,1)S(1)} %bitcast.63, bf16[128,32,512]{2,1,0:T(8,128)(2,1)} %param.18, f32[128,32]{1,0:T(8,128)S(1)} %fusion.23), kind=kOutput, calls=%fused_computation.8 | convolution fusion | flops 67174400 | bytes 11550720 | tf_op jit(solution)/shard_map/tkr,trs->tks/dot_general | solution.py:101
  58.8 1.6 copy.17
  60.5 0.0 copy-start.1
  60.5 0.0 copy-start.2
  60.5 0.0 copy-start.4
  60.5 0.0 copy-start.3
  60.5 1.9 fusion.28
  62.4 0.0 all-reduce.3.cloned.1.call-update
  62.5 0.0 copy-done.1
  62.5 0.0 copy-done.2
  62.5 0.3 reduce_window_sum.18
  62.8 0.0 copy-done.4
  62.8 0.6 dynamic-slice
  64.1 0.0 copy-done.3
  64.1 0.2 convolution_convert_fusion.3
  64.3 89.8 %all-reduce.3.cloned.1.call-done = f32[64,4096]{1,0:T(8,128)} async-done(((f32[64,4096]{1,0:T(8,128)}), f32[64,4096]{1,0:T(8,128)}) %all-reduce.3.cloned.1.call-update) | async-done | bytes 1048592
  154.0 3.1 convolution_convert_fusion
  157.1 6.8 %all-to-all-start = ((bf16[16,16,4096]{2,1,0:T(8,128)(2,1)}), bf16[16,16,4096]{2,1,0:T(8,128)(2,1)S(1)}, u32[]{:S(2)}, u32[]{:S(2)}) async-start(bf16[16,16,4096]{2,1,0:T(8,128)(2,1)} %convolution_convert_fusion), calls=%async_computation | async-start | bytes 4194304 | tf_op jit(solution)/shard_map/all_to_all | solution.py:127
  163.9 0.2 convert_reduce_fusion
  164.0 0.2 convert_reduce_fusion.1
  164.3 47.0 %all-to-all-done = bf16[16,16,4096]{2,1,0:T(8,128)(2,1)S(1)} async-done(((bf16[16,16,4096]{2,1,0:T(8,128)(2,1)}), bf16[16,16,4096]{2,1,0:T(8,128)(2,1)S(1)}, u32[]{:S(2)}, u32[]{:S(2)}) %all-to-all-start) | async-done | bytes 2097184 | tf_op jit(solution)/shard_map/all_to_all | solution.py:127
  211.3 0.5 convolution_convert_fusion.1
  211.8 0.4 copy.19
  212.2 6.5 %fusion.2 = f32[128,8,512]{2,1,0:T(8,128)} fusion(bf16[128,32,512]{2,1,0:T(8,128)(2,1)} %param.18, bf16[128,8,512]{2,1,0:T(8,128)(2,1)S(1)} %bitcast.62, bf16[128,32,512]{2,1,0:T(8,128)(2,1)} %param.17, f32[128,32]{1,0:T(8,128)S(1)} %fusion.23), kind=kOutput, calls=%fused_computation.7 | convolution fusion | flops 67174400 | bytes 11550720 | tf_op jit(solution)/shard_map/tkr,trc->tkc/dot_general | solution.py:137
  218.7 1.7 reshape.169
  220.5 3.8 %fusion.11 = f32[16,16,4096]{2,1,0:T(8,128)} fusion(f32[128,4096,1]{1,0,2:T(8,128)S(1)} %reshape.169, s32[16,16]{1,0:T(8,128)S(1)} %multiply_add_fusion, s32[128]{0:T(128)S(1)} %multiply_add_fusion.2), kind=kOutput, calls=%fused_computation.25 | convolution fusion | flops 1610645504 | bytes 6292992 | tf_op jit(solution)/shard_map/pqt,tf->pqf/dot_general | solution.py:141
  224.3 5.0 %all-to-all-start.1 = ((f32[16,16,4096]{2,1,0:T(8,128)}), f32[16,16,4096]{2,1,0:T(8,128)}, u32[]{:S(2)}, u32[]{:S(2)}) async-start(f32[16,16,4096]{2,1,0:T(8,128)} %fusion.11), calls=%async_computation.1 | async-start | bytes 8388608 | tf_op jit(solution)/shard_map/all_to_all | solution.py:144
  229.4 0.3 reduce_window_sum.17
  229.7 0.0 copy-done
  229.7 0.2 fusion.7
  229.8 92.0 %all-to-all-done.1 = f32[16,16,4096]{2,1,0:T(8,128)} async-done(((f32[16,16,4096]{2,1,0:T(8,128)}), f32[16,16,4096]{2,1,0:T(8,128)}, u32[]{:S(2)}, u32[]{:S(2)}) %all-to-all-start.1) | async-done | bytes 4194336 | tf_op jit(solution)/shard_map/all_to_all | solution.py:144
  321.8 6.2 %fusion.40 = f32[16,4096,1]{1,0,2:T(8,128)S(1)} fusion(f32[16,16,16]{1,2,0:T(8,128)S(1)} %fusion.7, f32[16,16,4096]{2,1,0:T(8,128)} %all-to-all-done.1), kind=kOutput, calls=%fused_computation.75 | convolution fusion | flops 201326592 | bytes 4472832 | tf_op jit(solution)/shard_map/pqb,pqf->bf/dot_general | solution.py:145
  328.0 0.2 copy.20
  328.2 0.7 broadcast_multiply_fusion
  (10 shorter events, 0.1 us)
Async XLA Ops:
  6.5 44.6 %all-gather.2.cloned.1.call-start = ((), (), s32[]{:S(2)}) async-start(), calls=%async_computation.2 | async-start | bytes 2228224 | tf_op jit(solution)/shard_map/all_gather | solution.py:89
  10.0 144.1 %all-reduce.3.cloned.1.call-start = ((), (), s32[]{:S(2)}) async-start(), calls=%async_computation.3 | async-start | bytes 2097152
  60.5 2.0 copy-start.1
  60.5 2.0 copy-start.2
  60.5 2.3 copy-start.4
  60.5 3.6 %copy-start.3 = (s32[2048]{0:T(1024)S(1)}, s32[2048]{0:T(1024)}, u32[]{:S(2)}) copy-start(s32[2048]{0:T(1024)} %param.22) | copy-start | bytes 24580
  157.1 54.2 %all-to-all-start = ((bf16[16,16,4096]{2,1,0:T(8,128)(2,1)}), bf16[16,16,4096]{2,1,0:T(8,128)(2,1)S(1)}, u32[]{:S(2)}, u32[]{:S(2)}) async-start(bf16[16,16,4096]{2,1,0:T(8,128)(2,1)} %convolution_convert_fusion), calls=%async_computation | async-start | bytes 4194304 | tf_op jit(solution)/shard_map/all_to_all | solution.py:127
  224.3 5.3 %copy-start = (s32[2048]{0:T(1024)S(1)}, s32[2048]{0:T(1024)}, u32[]{:S(2)}) copy-start(s32[2048]{0:T(1024)} %param.20) | copy-start | bytes 24580
  224.3 97.5 %all-to-all-start.1 = ((f32[16,16,4096]{2,1,0:T(8,128)}), f32[16,16,4096]{2,1,0:T(8,128)}, u32[]{:S(2)}, u32[]{:S(2)}) async-start(f32[16,16,4096]{2,1,0:T(8,128)} %fusion.11), calls=%async_computation.1 | async-start | bytes 8388608 | tf_op jit(solution)/shard_map/all_to_all | solution.py:144
Sparse Core Ops, SparseCore 0:
  10.1 41.0 all-gather.1
  62.6 91.4 all-reduce.2
where the time goes:
time: 336 us
  waiting for transfers between devices  268 us (80%)
  matrix products  29.6 us (9%)
  between operations  14.3 us (4%)
  starting transfers between devices  11.8 us (4%)
  local copies, waits for them, and re-layouts  6.41 us (2%)
  other arithmetic  5.89 us (2%)
    all_to_all x1, waiting for transfers between devices, shards(): lax.all_to_all(returned, 'tile', split_axis=0, concat_axis=0, tiled=True)  92 us
    unnamed x3, waiting for transfers between devices  89.8 us
    all_to_all x1, waiting for transfers between devices, shards(): lax.all_to_all(outgoing_data, 'tile', split_axis=0, concat_axis=0, tiled=...  47 us
    all_gather x1, waiting for transfers between devices, shards(): piece = lax.all_gather(cell_rows, 'tile', axis=0, tiled=True)  38.9 us
    all_to_all x1, starting transfers between devices, shards(): lax.all_to_all(outgoing_data, 'tile', split_axis=0, concat_axis=0, tiled=...  6.76 us
  transfers between devices with their start and end apart: 4, of which 4 were waited for; matrix products, arithmetic and copies ran while one was open for 1% of the time, Pallas kernels for 0%

commit v1 on v0

v1 whole, which is shorter than its diff:
```python
import jax
import jax.numpy as jnp
from jax import lax
from jax.experimental import pallas as pl
from jax.experimental.pallas import tpu as pltpu
from jax.sharding import PartitionSpec as P

BF16 = jnp.bfloat16
F32 = jnp.float32
GROUP = 8
VMEM_LIMIT = 56 * 1024 * 1024


def whole(space=pltpu.VMEM):
    return pl.BlockSpec(memory_space=space)


def swap(array, bit):
    count = lax.axis_size("tile")
    return lax.ppermute(array, "tile", [(i, i ^ bit) for i in range(count)])


def local(body, outs, *ins, name, scratch=(), specs=None, flops=0):
    nbytes = sum(a.size * a.dtype.itemsize for a in ins) + sum(a.size * a.dtype.itemsize for a in outs)
    return pl.pallas_call(
        body,
        out_shape=list(outs),
        in_specs=specs or [whole()] * len(ins),
        out_specs=[whole()] * len(outs),
        scratch_shapes=list(scratch),
        compiler_params=pltpu.CompilerParams(vmem_limit_bytes=VMEM_LIMIT),
        cost_estimate=pl.CostEstimate(flops=flops, bytes_accessed=nbytes, transcendentals=0),
        name=name,
    )(*ins)


def shape(dims, dtype):
    return jax.ShapeDtypeStruct(tuple(dims), dtype)


def scale_body(contrast, level, label, probes, first, second, scaling):
    value = level[...]
    unit = label[...]
    factor = jnp.zeros_like(value)
    for k in range(contrast.shape[0]):
        factor = jnp.where(unit == k, contrast[k], factor)
    scaling[...] = factor / (1.0 + value * value)
    blocks, _, width = first.shape
    rows = width // 128
    for half, out in enumerate((first, second)):
        for b in range(blocks):
            for c in range(rows):
                j = (half * blocks + b) * rows + c
                piece = probes[:, j * 128 : (j + 1) * 128] * scaling[j : j + 1, :]
                out[b, :, c * 128 : (c + 1) * 128] = piece.astype(BF16)


def final_body(keep_p, recv_p, keep_q, recv_q, scaling, out):
    blocks, _, width = keep_p.shape
    rows = width // 128
    for half, (keep, recv) in enumerate(((keep_p, recv_p), (keep_q, recv_q))):
        for b in range(blocks):
            for c in range(rows):
                j = (half * blocks + b) * rows + c
                lanes = slice(c * 128, (c + 1) * 128)
                total = keep[b, :, lanes] + recv[b, :, lanes].astype(F32)
                out[:, j * 128 : (j + 1) * 128] = total * scaling[j : j + 1, :]


def join_body(*refs):
    count = len(refs) // 3
    for i in range(count):
        a, b, out = refs[2 * i], refs[2 * i + 1], refs[2 * count + i]
        out[: a.shape[0]] = a[...]
        out[a.shape[0] :] = b[...]


def join(*pairs):
    outs = [shape((2 * a.shape[0],) + a.shape[1:], a.dtype) for a, _ in pairs]
    return local(join_body, outs, *[x for pair in pairs for x in pair], name="join")


def fold_body(*refs):
    count = len(refs) // 4
    for i in range(count):
        keep, recv = refs[2 * i], refs[2 * i + 1]
        mine, send = refs[2 * count + 2 * i], refs[2 * count + 2 * i + 1]
        half = mine.shape[0]
        mine[...] = keep[:half] + recv[:half].astype(F32)
        send[...] = (keep[half:] + recv[half:].astype(F32)).astype(BF16)


def fold(*pairs):
    outs = []
    for keep, _ in pairs:
        dims = (keep.shape[0] // 2,) + keep.shape[1:]
        outs += [shape(dims, F32), shape(dims, BF16)]
    flat = local(fold_body, outs, *[x for pair in pairs for x in pair], name="fold")
    return [(flat[2 * i], flat[2 * i + 1]) for i in range(len(pairs))]


def tiles_body(piece_count, src_at, dst_at, keep, *refs):
    pieces = refs[:piece_count]
    first_hbm, second_hbm, mine, send, table, first, second, acc, sems = refs[piece_count:]
    groups = keep.shape[0]
    rank = first.shape[1]
    width = table.shape[2]
    copies = []
    for g in range(groups):
        rows = pl.ds(g * GROUP, GROUP)
        pair = (
            pltpu.make_async_copy(first_hbm.at[rows], first.at[rows], sems.at[0, g]),
            pltpu.make_async_copy(second_hbm.at[rows], second.at[rows], sems.at[1, g]),
        )
        for copy in pair:
            copy.start()
        copies.append(pair)
    acc[...] = jnp.zeros_like(acc)
    per = pieces[0].shape[0]
    for i, piece in enumerate(pieces):
        table[i * per : (i + 1) * per] = piece[...]
    probes = table.shape[1]
    span = GROUP * rank
    row_tile = lax.broadcasted_iota(jnp.int32, (GROUP * probes, span), 0) // probes
    col_tile = lax.broadcasted_iota(jnp.int32, (GROUP * probes, span), 1) // rank
    own = row_tile == col_tile
    for g in range(groups):
        for copy in copies[g]:
            copy.wait()
        taken = jnp.concatenate(
            [table[src_at[g * GROUP + i]].astype(F32) for i in range(GROUP)], axis=0
        ).astype(BF16)
        left = first[g * GROUP : (g + 1) * GROUP].reshape(span, width)
        right = second[g * GROUP : (g + 1) * GROUP].reshape(span, width)
        inner = lax.dot_general(taken, left, (((1,), (1,)), ((), ())), preferred_element_type=F32)
        kept = jnp.where(own & (keep[g : g + 1, :] > 0), inner, 0.0).astype(BF16)
        outer = jnp.dot(kept, right, preferred_element_type=F32)
        for i in range(GROUP):
            at = dst_at[g * GROUP + i]
            acc[at] = acc[at] + outer[i * probes : (i + 1) * probes]
    half = mine.shape[0]
    mine[...] = acc[:half].astype(mine.dtype)
    send[...] = acc[half:].astype(send.dtype)


def tiles(pieces, src_at, dst_at, keep, first, second, blocks, send_dtype, name):
    count, rank, width = first.shape
    probes = pieces[0].shape[1]
    groups = keep.shape[0]
    rows = len(pieces) * pieces[0].shape[0]
    half = (blocks // 2, probes, width)

    def body(*refs):
        tiles_body(len(pieces), *refs)

    smem = whole(pltpu.SMEM)
    specs = [smem, smem, whole()] + [whole()] * len(pieces) + [whole(pl.ANY)] * 2
    return local(
        body,
        [shape(half, F32), shape(half, send_dtype)],
        src_at,
        dst_at,
        keep,
        *pieces,
        first,
        second,
        name=name,
        specs=specs,
        flops=4 * count * rank * width * probes * GROUP,
        scratch=[
            pltpu.VMEM((rows, probes, width), BF16),
            pltpu.VMEM((count, rank, width), BF16),
            pltpu.VMEM((count, rank, width), BF16),
            pltpu.VMEM((blocks, probes, width), F32),
            pltpu.SemaphoreType.DMA((2, groups)),
        ],
    )


def place(relative, order):
    at = jnp.zeros_like(relative)
    for k, bit in enumerate(order):
        at = at + jnp.where((relative & bit) != 0, 1 << k, 0)
    return at


def shards(
    probes,
    level_set,
    unit_label,
    contrast,
    station_weight,
    u_factor,
    v_factor,
    col_owner,
    col_local,
    row_owner,
    row_local,
    tile_rank,
):
    peers = lax.axis_size("tile")
    me = lax.axis_index("tile")
    tile_count, rank_max, station_width = u_factor.shape
    cell_width = v_factor.shape[2]
    probe_count, cell_total = probes.shape
    cell_blocks = cell_total // cell_width
    station_blocks = station_weight.shape[0] // (peers * station_width)
    half_blocks = cell_blocks // 2
    far = [1 << k for k in range(2, peers.bit_length() - 1)][::-1]
    order_p = [2] + far
    order_q = far + [2]
    split_bits = [1 << k for k in range(peers.bit_length() - 3)]
    join_bits = [peers // 4, peers // 2]

    start = me * tile_count

    def mine_of(table):
        return lax.dynamic_slice_in_dim(table.reshape(-1), start, tile_count)

    col_relative = mine_of(col_owner) ^ me
    col_here = mine_of(col_local)
    row_holder = mine_of(row_owner)
    row_here = mine_of(row_local)
    rank_mine = mine_of(tile_rank)
    is_q = col_here >= half_blocks
    span = peers // 2
    cell_at = (
        (col_relative & 1) * (span * cell_blocks)
        + jnp.where(is_q, place(col_relative, order_q), place(col_relative, order_p)) * half_blocks
        + jnp.where(is_q, span * half_blocks - half_blocks, 0)
        + col_here
    )
    row_at = place(row_holder ^ me, split_bits[::-1]) * (4 * station_blocks)
    row_at = row_at + (row_holder // (peers // 4)) * station_blocks + row_here
    keep = (jnp.arange(rank_max, dtype=jnp.int32)[None, :] < rank_mine[:, None]).astype(F32)
    keep = keep.reshape(tile_count // GROUP, GROUP * rank_max)
    weight = lax.dynamic_slice_in_dim(
        station_weight.reshape(4, peers // 4, station_blocks, station_width), me % (peers // 4), 1, 1
    ).reshape(4 * station_blocks, 1, station_width)

    half_dims = (half_blocks, probe_count, cell_width)
    lanes = (cell_total // 128, 128)
    part_p, part_q, scaling = local(
        scale_body,
        [shape(half_dims, BF16), shape(half_dims, BF16), shape(lanes, F32)],
        contrast,
        level_set.reshape(lanes),
        unit_label.reshape(lanes),
        probes,
        name="scale",
        specs=[whole(pltpu.SMEM)] + [whole()] * 3,
    )
    for step in range(len(order_p)):
        got_p = swap(part_p, order_p[step])
        got_q = swap(part_q, order_q[step])
        if step < len(order_p) - 1:
            part_p, part_q = join((part_p, got_p), (part_q, got_q))
    pieces = [part_p, got_p, part_q, got_q]
    pieces = pieces + [swap(piece, 1) for piece in pieces]

    total, send = tiles(
        pieces, cell_at, row_at, keep, v_factor, u_factor, peers * station_blocks, F32, "forward"
    )
    total = total + swap(send, split_bits[0])
    for bit in split_bits[1:]:
        half = total.shape[0] // 2
        got = swap(total[half:].astype(BF16), bit)
        total = total[:half] + got.astype(F32)
    for bit in join_bits:
        total = total + swap(total.astype(BF16), bit).astype(F32)
    weighted = (total * weight).astype(BF16)
    pieces = [weighted]
    for bit in split_bits[::-1]:
        pieces = pieces + [swap(piece, bit) for piece in pieces]

    keep_all, send_all = tiles(
        pieces, row_at, cell_at, keep, u_factor, v_factor, peers * cell_blocks, BF16, "adjoint"
    )
    got_all = swap(send_all, 1)
    half = keep_all.shape[0] // 2
    pair_p = (keep_all[:half], got_all[:half])
    pair_q = (keep_all[half:], got_all[half:])
    for bit_p, bit_q in zip(order_p[::-1], order_q[::-1]):
        (keep_p, send_p), (keep_q, send_q) = fold(pair_p, pair_q)
        pair_p = (keep_p, swap(send_p, bit_p))
        pair_q = (keep_q, swap(send_q, bit_q))
    return local(
        final_body,
        [shape((probe_count, cell_total), F32)],
        *pair_p,
        *pair_q,
        scaling,
        name="final",
    )[0]


def solution(mesh):
    placed = (
        P(None, ("groups", "tile")),
        P(("groups", "tile")),
        P(("groups", "tile")),
        P("groups"),
        P("groups"),
        P(("groups", "tile"), None, None),
        P(("groups", "tile"), None, None),
        P("groups", None),
        P("groups"),
        P("groups", None),
        P("groups"),
        P("groups"),
    )
    return jax.shard_map(
        shards, mesh=mesh, in_specs=placed, out_specs=P(None, ("groups", "tile")), check_vma=False
    )
```

time: 336 us -> 126 us (0.38)
  the two profiles are of different devices: /device:TPU:13 before, /device:TPU:0 now
where the time goes in v1:
time: 126 us
  waiting for transfers between devices  53 us (42%)
  Pallas kernels  36.1 us (29%)
  starting transfers between devices  22.7 us (18%)
  local copies, waits for them, and re-layouts  10.5 us (8%)
  other arithmetic  3.37 us (3%)
    ppermute x24, waiting for transfers between devices, swap(): return lax.ppermute(array, 'tile', [(i, i ^ bit) for i in range(count)])  53 us
    pallas_call x9, Pallas kernels, local(): pl.pallas_call(body, out_shape=list(outs), in_specs=specs or [whole()] *...  36.1 us
    ppermute x24, starting transfers between devices, swap(): return lax.ppermute(array, 'tile', [(i, i ^ bit) for i in range(count)])  22.7 us
    unnamed x42, local copies, waits for them, and re-layouts  5.27 us
    slice x2, local copies, waits for them, and re-layouts, shards(): pair_q = (keep_all[half:], got_all[half:])  4.09 us
  transfers between devices with their start and end apart: 24, of which 16 were waited for; matrix products, arithmetic and copies ran while one was open for 5% of the time, Pallas kernels for 0%

profile of v1, /device:TPU:0, one launch (start us, length us, event | category | flops | bytes accessed | tf_op | source)
XLA Modules:
  0.0 125.9 jit_solution(14344802430774730529)
XLA Ops:
  0.0 1.7 %scale.1 = (bf16[8,8,512]{2,1,0:T(8,128)(2,1)}, bf16[8,8,512]{2,1,0:T(8,128)(2,1)}, f32[64,128]{1,0:T(8,128)}) custom-call(f32[4]{0:T(128)} %contrast.1, f32[64,128]{1,0:T(8,128)} %bitcast.14, s32[64,128]{1,0:T(8,128)} %bitcast.15, f32[8,8192]{1,0:T(8,128)} %probes.1), custom_call_target="tpu_custom_call" | custom-call | bytes 491536 | tf_op jit(solution)/shard_map/scale/pallas_call | solution.py:25
  1.7 3.0 %collective-permute-start = (bf16[8,8,512]{2,1,0:T(8,128)(2,1)}, bf16[8,8,512]{2,1,0:T(8,128)(2,1)S(1)}, u32[]{:S(2)}, u32[]{:S(2)}) collective-permute-start(bf16[8,8,512]{2,1,0:T(8,128)(2,1)} %get-tuple-element.28.refs_0_), channel_id=1, source_target_pairs={{0,2},{1,3},{2,0},{3,1},{4,6},{5,7},{6,4},{7,5},{8,10},{9,11},{10,... | collective-permute-start | bytes 196616 | tf_op jit(solution)/shard_map/ppermute | solution.py:20
  4.7 2.6 %collective-permute-start.1 = (bf16[8,8,512]{2,1,0:T(8,128)(2,1)}, bf16[8,8,512]{2,1,0:T(8,128)(2,1)S(1)}, u32[]{:S(2)}, u32[]{:S(2)}) collective-permute-start(bf16[8,8,512]{2,1,0:T(8,128)(2,1)} %get-tuple-element.29.refs_2_), channel_id=1, source_target_pairs={{0,8},{1,9},{2,10},{3,11},{4,12},{5,13},{6,14},{7,15},{8,0},{9,1},... | collective-permute-start | bytes 196616 | tf_op jit(solution)/shard_map/ppermute | solution.py:20
  7.3 3.1 %collective-permute-done.1.refs_3_ = bf16[8,8,512]{2,1,0:T(8,128)(2,1)S(1)} collective-permute-done((bf16[8,8,512]{2,1,0:T(8,128)(2,1)}, bf16[8,8,512]{2,1,0:T(8,128)(2,1)S(1)}, u32[]{:S(2)}, u32[]{:S(2)}) %collective-permute-start.1) | collective-permute-done | bytes 65568 | tf_op jit(solution)/shard_map/ppermute | solution.py:20
  10.3 0.6 copy-done.18
  10.9 1.6 %join.2 = (bf16[16,8,512]{2,1,0:T(8,128)(2,1)}, bf16[16,8,512]{2,1,0:T(8,128)(2,1)}) custom-call(bf16[8,8,512]{2,1,0:T(8,128)(2,1)} %get-tuple-element.28.refs_0_, bf16[8,8,512]{2,1,0:T(8,128)(2,1)} %copy-done.17, bf16[8,8,512]{2,1,0:T(8,128)(2,1)} %get-tuple-element.29.refs_2_, bf16[8,8,512]{2,1,0:T(8,128)(2,1)} %copy-done.18), custom_call_target="tpu_custom_call" | custom-call | bytes 524288 | tf_op jit(solution)/shard_map/join/pallas_call | solution.py:25
  12.6 2.3 %collective-permute-start.2 = (bf16[16,8,512]{2,1,0:T(8,128)(2,1)}, bf16[16,8,512]{2,1,0:T(8,128)(2,1)S(1)}, u32[]{:S(2)}, u32[]{:S(2)}) collective-permute-start(bf16[16,8,512]{2,1,0:T(8,128)(2,1)} %get-tuple-element.30.refs_0_), channel_id=1, source_target_pairs={{0,8},{1,9},{2,10},{3,11},{4,12},{5,13},{6,14},{7,15},{8,0},{9,1},... | collective-permute-start | bytes 393224 | tf_op jit(solution)/shard_map/ppermute | solution.py:20
  14.9 2.1 %collective-permute-start.3 = (bf16[16,8,512]{2,1,0:T(8,128)(2,1)}, bf16[16,8,512]{2,1,0:T(8,128)(2,1)S(1)}, u32[]{:S(2)}, u32[]{:S(2)}) collective-permute-start(bf16[16,8,512]{2,1,0:T(8,128)(2,1)} %get-tuple-element.31.refs_2_), channel_id=1, source_target_pairs={{0,4},{1,5},{2,6},{3,7},{4,0},{5,1},{6,2},{7,3},{8,12},{9,13},{10,... | collective-permute-start | bytes 393224 | tf_op jit(solution)/shard_map/ppermute | solution.py:20
  17.0 3.1 %collective-permute-done.2.refs_1_ = bf16[16,8,512]{2,1,0:T(8,128)(2,1)S(1)} collective-permute-done((bf16[16,8,512]{2,1,0:T(8,128)(2,1)}, bf16[16,8,512]{2,1,0:T(8,128)(2,1)S(1)}, u32[]{:S(2)}, u32[]{:S(2)}) %collective-permute-start.2) | collective-permute-done | bytes 131104 | tf_op jit(solution)/shard_map/ppermute | solution.py:20
  20.8 0.6 copy-done.16
  21.5 1.9 %join.3 = (bf16[32,8,512]{2,1,0:T(8,128)(2,1)}, bf16[32,8,512]{2,1,0:T(8,128)(2,1)}) custom-call(bf16[16,8,512]{2,1,0:T(8,128)(2,1)} %get-tuple-element.30.refs_0_, bf16[16,8,512]{2,1,0:T(8,128)(2,1)} %copy-done.15, bf16[16,8,512]{2,1,0:T(8,128)(2,1)} %get-tuple-element.31.refs_2_, bf16[16,8,512]{2,1,0:T(8,128)(2,1)} %copy-done.16), custom_call_target="tpu_custom_call" | custom-call | bytes 1048576 | tf_op jit(solution)/shard_map/join/pallas_call | solution.py:25
  23.4 1.4 %collective-permute-start.4 = (bf16[32,8,512]{2,1,0:T(8,128)(2,1)}, bf16[32,8,512]{2,1,0:T(8,128)(2,1)S(1)}, u32[]{:S(2)}, u32[]{:S(2)}) collective-permute-start(bf16[32,8,512]{2,1,0:T(8,128)(2,1)} %get-tuple-element.32.refs_3_), channel_id=1, source_target_pairs={{0,4},{1,5},{2,6},{3,7},{4,0},{5,1},{6,2},{7,3},{8,12},{9,13},{10,... | collective-permute-start | bytes 786440 | tf_op jit(solution)/shard_map/ppermute | solution.py:20
  25.8 4.2 %collective-permute-done.4.refs_4_ = bf16[32,8,512]{2,1,0:T(8,128)(2,1)S(1)} collective-permute-done((bf16[32,8,512]{2,1,0:T(8,128)(2,1)}, bf16[32,8,512]{2,1,0:T(8,128)(2,1)S(1)}, u32[]{:S(2)}, u32[]{:S(2)}) %collective-permute-start.4) | collective-permute-done | bytes 262176 | tf_op jit(solution)/shard_map/ppermute | solution.py:20
  30.0 1.4 %collective-permute-done.5.refs_6_ = bf16[32,8,512]{2,1,0:T(8,128)(2,1)S(1)} collective-permute-done((bf16[32,8,512]{2,1,0:T(8,128)(2,1)}, bf16[32,8,512]{2,1,0:T(8,128)(2,1)S(1)}, u32[]{:S(2)}, u32[]{:S(2)}) %collective-permute-start.5) | collective-permute-done | bytes 262176 | tf_op jit(solution)/shard_map/ppermute | solution.py:20
  31.4 1.5 %fusion.7 = (s32[128]{0:T(128)}, s32[128]{0:T(128)}) fusion(s32[2048]{0:T(1024)} %param.20, s32[]{:T(128)S(6)} %select_n.71, s32[2048,1]{0,1:T(1,128)} %param.19, s32[]{:T(128)S(6)} %axis_index.12, s32[2048]{0:T(1024)} %param.22, s32[2048,1]{0,1:T(1,128)} %param.21), kind=kLoop, calls=%fused_computation.29 | loop fusion | flops 6784 | bytes 4608 | tf_op jit(solution)/shard_map/add | solution.py:228
  32.8 0.8 dynamic_slice.25
  34.0 0.6 compare_convert_fusion.refs_2_
  34.6 0.6 copy-done.3
  35.5 10.8 %forward.1 = (f32[32,8,512]{2,1,0:T(8,128)}, f32[32,8,512]{2,1,0:T(8,128)}) custom-call(s32[128]{0:T(128)} %get-tuple-element.55.refs_0_.refs_1_, s32[128]{0:T(128)} %get-tuple-element.56.refs_1_.refs_0_, f32[16,256]{1,0:T(8,128)} %compare_convert_fusion.refs_2_, bf16[32,8,512]{2,1,0:T(8,128)(2,1)} %get-tuple-element.32.refs_3_, ...), custom_call_target="tpu_custom_call" | custom-call | flops 536870912 | bytes 11551744 | tf_op jit(solution)/shard_map/forward/pallas_call | solution.py:25
  46.9 1.7 %collective-permute-done.10 = f32[32,8,512]{2,1,0:T(8,128)S(1)} collective-permute-done((f32[32,8,512]{2,1,0:T(8,128)}, f32[32,8,512]{2,1,0:T(8,128)S(1)}, u32[]{:S(2)}, u32[]{:S(2)}) %collective-permute-start.10) | collective-permute-done | bytes 524320 | tf_op jit(solution)/shard_map/ppermute | solution.py:20
  48.6 1.1 add.68
  49.8 0.6 collective-permute-start.11
  50.3 5.3 %collective-permute-done.11 = bf16[16,8,512]{2,1,0:T(8,128)(2,1)S(1)} collective-permute-done((bf16[16,8,512]{2,1,0:T(8,128)(2,1)S(1)}, bf16[16,8,512]{2,1,0:T(8,128)(2,1)S(1)}, u32[]{:S(2)}, u32[]{:S(2)}) %collective-permute-start.11) | collective-permute-done | bytes 131104 | tf_op jit(solution)/shard_map/ppermute | solution.py:20
  55.6 0.7 collective-permute-start.12
  56.3 4.3 %collective-permute-done.12 = bf16[16,8,512]{2,1,0:T(8,128)(2,1)S(1)} collective-permute-done((bf16[16,8,512]{2,1,0:T(8,128)(2,1)S(1)}, bf16[16,8,512]{2,1,0:T(8,128)(2,1)S(1)}, u32[]{:S(2)}, u32[]{:S(2)}) %collective-permute-start.12) | collective-permute-done | bytes 131104 | tf_op jit(solution)/shard_map/ppermute | solution.py:20
  60.7 2.7 %collective-permute-start.13 = (bf16[16,8,512]{2,1,0:T(8,128)(2,1)S(1)}, bf16[16,8,512]{2,1,0:T(8,128)(2,1)S(1)}, u32[]{:S(2)}, u32[]{:S(2)}) collective-permute-start(bf16[16,8,512]{2,1,0:T(8,128)(2,1)S(1)} %fusion), channel_id=1, source_target_pairs={{0,8},{1,9},{2,10},{3,11},{4,12},{5,13},{6,14},{7,15},{8,0},{9,1},... | collective-permute-start | bytes 393224 | tf_op jit(solution)/shard_map/ppermute | solution.py:20
  63.5 4.8 %collective-permute-done.13 = bf16[16,8,512]{2,1,0:T(8,128)(2,1)S(1)} collective-permute-done((bf16[16,8,512]{2,1,0:T(8,128)(2,1)S(1)}, bf16[16,8,512]{2,1,0:T(8,128)(2,1)S(1)}, u32[]{:S(2)}, u32[]{:S(2)}) %collective-permute-start.13) | collective-permute-done | bytes 131104 | tf_op jit(solution)/shard_map/ppermute | solution.py:20
  68.4 0.6 collective-permute-start.14
  69.0 4.5 %collective-permute-done.14.refs_4_ = bf16[16,8,512]{2,1,0:T(8,128)(2,1)S(1)} collective-permute-done((bf16[16,8,512]{2,1,0:T(8,128)(2,1)S(1)}, bf16[16,8,512]{2,1,0:T(8,128)(2,1)S(1)}, u32[]{:S(2)}, u32[]{:S(2)}) %collective-permute-start.14) | collective-permute-done | bytes 131104 | tf_op jit(solution)/shard_map/ppermute | solution.py:20
  73.5 1.3 %collective-permute-done.16.refs_6_ = bf16[16,8,512]{2,1,0:T(8,128)(2,1)S(1)} collective-permute-done((bf16[16,8,512]{2,1,0:T(8,128)(2,1)S(1)}, bf16[16,8,512]{2,1,0:T(8,128)(2,1)S(1)}, u32[]{:S(2)}, u32[]{:S(2)}) %collective-permute-start.16) | collective-permute-done | bytes 131104 | tf_op jit(solution)/shard_map/ppermute | solution.py:20
  74.8 0.6 copy-done.11
  75.4 11.1 %adjoint.1 = (f32[128,8,512]{2,1,0:T(8,128)}, bf16[128,8,512]{2,1,0:T(8,128)(2,1)}) custom-call(s32[128]{0:T(128)} %get-tuple-element.56.refs_1_.refs_0_, s32[128]{0:T(128)} %get-tuple-element.55.refs_0_.refs_1_, f32[16,256]{1,0:T(8,128)} %compare_convert_fusion.refs_2_, bf16[16,8,512]{2,1,0:T(8,128)(2,1)} %copy-done, bf16[16,8,512]{2,1,0:T(8,128)(2,1)} %copy-done.9, ...), custom_call_target="tpu_custom_call" | custom-call | flops 536870912 | bytes 12076032 | tf_op jit(solution)/shard_map/adjoint/pallas_call | solution.py:25
  86.8 3.1 %fusion.13 = (f32[64,8,512]{2,1,0:T(8,128)}, f32[64,8,512]{2,1,0:T(8,128)}) fusion(f32[128,8,512]{2,1,0:T(8,128)} %get-tuple-element.36), kind=kLoop, calls=%fused_computation.36 | loop fusion | bytes 4194304 | tf_op jit(solution)/shard_map/slice | solution.py:282
  89.8 1.0 fusion.14
  90.9 3.0 %fold.3 = (f32[32,8,512]{2,1,0:T(8,128)}, bf16[32,8,512]{2,1,0:T(8,128)(2,1)}, f32[32,8,512]{2,1,0:T(8,128)}, bf16[32,8,512]{2,1,0:T(8,128)(2,1)}) custom-call(f32[64,8,512]{2,1,0:T(8,128)} %get-tuple-element.52.refs_0_, bf16[64,8,512]{2,1,0:T(8,128)(2,1)} %get-tuple-element.54.refs_1_, f32[64,8,512]{2,1,0:T(8,128)} %get-tuple-element.51.refs_2_, ...), custom_call_target="tpu_custom_call" | custom-call | bytes 4718592 | tf_op jit(solution)/shard_map/fold/pallas_call | solution.py:25
  93.9 0.5 collective-permute-start.19
  94.4 8.3 %collective-permute-done.18.refs_1_ = bf16[32,8,512]{2,1,0:T(8,128)(2,1)S(1)} collective-permute-done((bf16[32,8,512]{2,1,0:T(8,128)(2,1)}, bf16[32,8,512]{2,1,0:T(8,128)(2,1)S(1)}, u32[]{:S(2)}, u32[]{:S(2)}) %collective-permute-start.18) | collective-permute-done | bytes 262176 | tf_op jit(solution)/shard_map/ppermute | solution.py:20
  102.7 0.7 copy-done.7
  103.5 2.2 %fold.4 = (f32[16,8,512]{2,1,0:T(8,128)}, bf16[16,8,512]{2,1,0:T(8,128)(2,1)}, f32[16,8,512]{2,1,0:T(8,128)}, bf16[16,8,512]{2,1,0:T(8,128)(2,1)}) custom-call(f32[32,8,512]{2,1,0:T(8,128)} %get-tuple-element.38.refs_0_, bf16[32,8,512]{2,1,0:T(8,128)(2,1)} %copy-done.7, f32[32,8,512]{2,1,0:T(8,128)} %get-tuple-element.40.refs_2_, bf16[32,8,512]{2,1,0:T(8,128)(2,1)} %copy-done.8), custom_call_target="tpu_custom_call" | custom-call | bytes 2359296 | tf_op jit(solution)/shard_map/fold/pallas_call | solution.py:25
  105.7 2.9 %collective-permute-start.20 = (bf16[16,8,512]{2,1,0:T(8,128)(2,1)}, bf16[16,8,512]{2,1,0:T(8,128)(2,1)S(1)}, u32[]{:S(2)}, u32[]{:S(2)}) collective-permute-start(bf16[16,8,512]{2,1,0:T(8,128)(2,1)} %get-tuple-element.43), channel_id=1, source_target_pairs={{0,8},{1,9},{2,10},{3,11},{4,12},{5,13},{6,14},{7,15},{8,0},{9,1},... | collective-permute-start | bytes 393224 | tf_op jit(solution)/shard_map/ppermute | solution.py:20
  109.0 5.7 %collective-permute-done.20.refs_1_ = bf16[16,8,512]{2,1,0:T(8,128)(2,1)S(1)} collective-permute-done((bf16[16,8,512]{2,1,0:T(8,128)(2,1)}, bf16[16,8,512]{2,1,0:T(8,128)(2,1)S(1)}, u32[]{:S(2)}, u32[]{:S(2)}) %collective-permute-start.20) | collective-permute-done | bytes 131104 | tf_op jit(solution)/shard_map/ppermute | solution.py:20
  115.7 1.9 %fold.5 = (f32[8,8,512]{2,1,0:T(8,128)}, bf16[8,8,512]{2,1,0:T(8,128)(2,1)}, f32[8,8,512]{2,1,0:T(8,128)}, bf16[8,8,512]{2,1,0:T(8,128)(2,1)}) custom-call(f32[16,8,512]{2,1,0:T(8,128)} %get-tuple-element.42.refs_0_, bf16[16,8,512]{2,1,0:T(8,128)(2,1)} %copy-done.13, f32[16,8,512]{2,1,0:T(8,128)} %get-tuple-element.44.refs_2_, bf16[16,8,512]{2,1,0:T(8,128)(2,1)} %copy-done.14), custom_call_target="tpu_custom_call" | custom-call | bytes 1179648 | tf_op jit(solution)/shard_map/fold/pallas_call | solution.py:25
  117.6 0.5 collective-permute-start.22
  118.1 0.8 collective-permute-start.23
  119.0 3.1 %collective-permute-done.22.recv_p = bf16[8,8,512]{2,1,0:T(8,128)(2,1)S(1)} collective-permute-done((bf16[8,8,512]{2,1,0:T(8,128)(2,1)}, bf16[8,8,512]{2,1,0:T(8,128)(2,1)S(1)}, u32[]{:S(2)}, u32[]{:S(2)}) %collective-permute-start.22) | collective-permute-done | bytes 65568 | tf_op jit(solution)/shard_map/ppermute | solution.py:20
  122.1 1.4 %collective-permute-done.23.recv_q = bf16[8,8,512]{2,1,0:T(8,128)(2,1)S(1)} collective-permute-done((bf16[8,8,512]{2,1,0:T(8,128)(2,1)}, bf16[8,8,512]{2,1,0:T(8,128)(2,1)S(1)}, u32[]{:S(2)}, u32[]{:S(2)}) %collective-permute-start.23) | collective-permute-done | bytes 65568 | tf_op jit(solution)/shard_map/ppermute | solution.py:20
  123.5 0.6 copy-done.20
  124.1 1.8 %final.1 = f32[8,8192]{1,0:T(8,128)} custom-call(f32[8,8,512]{2,1,0:T(8,128)} %get-tuple-element.46.keep_p, bf16[8,8,512]{2,1,0:T(8,128)(2,1)} %copy-done.19, f32[8,8,512]{2,1,0:T(8,128)} %get-tuple-element.48.keep_q, bf16[8,8,512]{2,1,0:T(8,128)(2,1)} %copy-done.20, f32[64,128]{1,0:T(8,128)} %get-tuple-element.50.scaling), custom_call_target="tpu_custom_call" | custom-call | bytes 688128 | tf_op jit(solution)/shard_map/final/pallas_call | solution.py:25
  (69 shorter events, 4.9 us)
Async XLA Ops:
  1.7 5.6 %collective-permute-start = (bf16[8,8,512]{2,1,0:T(8,128)(2,1)}, bf16[8,8,512]{2,1,0:T(8,128)(2,1)S(1)}, u32[]{:S(2)}, u32[]{:S(2)}) collective-permute-start(bf16[8,8,512]{2,1,0:T(8,128)(2,1)} %get-tuple-element.28.refs_0_), channel_id=1, source_target_pairs={{0,2},{1,3},{2,0},{3,1},{4,6},{5,7},{6,4},{7,5},{8,10},{9,11},{10,... | collective-permute-start | bytes 196616 | tf_op jit(solution)/shard_map/ppermute | solution.py:20
  4.7 5.7 %collective-permute-start.1 = (bf16[8,8,512]{2,1,0:T(8,128)(2,1)}, bf16[8,8,512]{2,1,0:T(8,128)(2,1)S(1)}, u32[]{:S(2)}, u32[]{:S(2)}) collective-permute-start(bf16[8,8,512]{2,1,0:T(8,128)(2,1)} %get-tuple-element.29.refs_2_), channel_id=1, source_target_pairs={{0,8},{1,9},{2,10},{3,11},{4,12},{5,13},{6,14},{7,15},{8,0},{9,1},... | collective-permute-start | bytes 196616 | tf_op jit(solution)/shard_map/ppermute | solution.py:20
  7.3 3.1 %copy-start.17 = (bf16[8,8,512]{2,1,0:T(8,128)(2,1)}, bf16[8,8,512]{2,1,0:T(8,128)(2,1)S(1)}, u32[]{:S(2)}) copy-start(bf16[8,8,512]{2,1,0:T(8,128)(2,1)S(1)} %collective-permute-done.refs_1_) | copy-start | bytes 196612
  10.3 0.6 copy-start.18
  12.6 7.6 %collective-permute-start.2 = (bf16[16,8,512]{2,1,0:T(8,128)(2,1)}, bf16[16,8,512]{2,1,0:T(8,128)(2,1)S(1)}, u32[]{:S(2)}, u32[]{:S(2)}) collective-permute-start(bf16[16,8,512]{2,1,0:T(8,128)(2,1)} %get-tuple-element.30.refs_0_), channel_id=1, source_target_pairs={{0,8},{1,9},{2,10},{3,11},{4,12},{5,13},{6,14},{7,15},{8,0},{9,1},... | collective-permute-start | bytes 393224 | tf_op jit(solution)/shard_map/ppermute | solution.py:20
  14.9 5.5 %collective-permute-start.3 = (bf16[16,8,512]{2,1,0:T(8,128)(2,1)}, bf16[16,8,512]{2,1,0:T(8,128)(2,1)S(1)}, u32[]{:S(2)}, u32[]{:S(2)}) collective-permute-start(bf16[16,8,512]{2,1,0:T(8,128)(2,1)} %get-tuple-element.31.refs_2_), channel_id=1, source_target_pairs={{0,4},{1,5},{2,6},{3,7},{4,0},{5,1},{6,2},{7,3},{8,12},{9,13},{10,... | collective-permute-start | bytes 393224 | tf_op jit(solution)/shard_map/ppermute | solution.py:20
  20.2 0.7 copy-start.15
  20.8 0.6 copy-start.16
  23.4 6.6 %collective-permute-start.4 = (bf16[32,8,512]{2,1,0:T(8,128)(2,1)}, bf16[32,8,512]{2,1,0:T(8,128)(2,1)S(1)}, u32[]{:S(2)}, u32[]{:S(2)}) collective-permute-start(bf16[32,8,512]{2,1,0:T(8,128)(2,1)} %get-tuple-element.32.refs_3_), channel_id=1, source_target_pairs={{0,4},{1,5},{2,6},{3,7},{4,0},{5,1},{6,2},{7,3},{8,12},{9,13},{10,... | collective-permute-start | bytes 786440 | tf_op jit(solution)/shard_map/ppermute | solution.py:20
  24.8 6.6 %collective-permute-start.5 = (bf16[32,8,512]{2,1,0:T(8,128)(2,1)}, bf16[32,8,512]{2,1,0:T(8,128)(2,1)S(1)}, u32[]{:S(2)}, u32[]{:S(2)}) collective-permute-start(bf16[32,8,512]{2,1,0:T(8,128)(2,1)} %get-tuple-element.33.refs_5_), channel_id=1, source_target_pairs={{0,2},{1,3},{2,0},{3,1},{4,6},{5,7},{6,4},{7,5},{8,10},{9,11},{10,... | collective-permute-start | bytes 786440 | tf_op jit(solution)/shard_map/ppermute | solution.py:20
  25.3 9.3 %collective-permute-start.6 = (bf16[32,8,512]{2,1,0:T(8,128)(2,1)}, bf16[32,8,512]{2,1,0:T(8,128)(2,1)S(1)}, u32[]{:S(2)}, u32[]{:S(2)}) collective-permute-start(bf16[32,8,512]{2,1,0:T(8,128)(2,1)} %get-tuple-element.32.refs_3_), channel_id=1, source_target_pairs={{0,1},{1,0},{2,3},{3,2},{4,5},{5,4},{6,7},{7,6},{8,9},{9,8},{10,11... | collective-permute-start | bytes 786440 | tf_op jit(solution)/shard_map/ppermute | solution.py:20
  25.3 9.3 %collective-permute-start.8 = (bf16[32,8,512]{2,1,0:T(8,128)(2,1)}, bf16[32,8,512]{2,1,0:T(8,128)(2,1)S(1)}, u32[]{:S(2)}, u32[]{:S(2)}) collective-permute-start(bf16[32,8,512]{2,1,0:T(8,128)(2,1)} %get-tuple-element.33.refs_5_), channel_id=1, source_target_pairs={{0,1},{1,0},{2,3},{3,2},{4,5},{5,4},{6,7},{7,6},{8,9},{9,8},{10,11... | collective-permute-start | bytes 786440 | tf_op jit(solution)/shard_map/ppermute | solution.py:20
  29.9 4.7 %copy-start.1 = (bf16[32,8,512]{2,1,0:T(8,128)(2,1)}, bf16[32,8,512]{2,1,0:T(8,128)(2,1)S(1)}, u32[]{:S(2)}) copy-start(bf16[32,8,512]{2,1,0:T(8,128)(2,1)S(1)} %collective-permute-done.4.refs_4_) | copy-start | bytes 786436
  30.0 4.6 %collective-permute-start.7 = (bf16[32,8,512]{2,1,0:T(8,128)(2,1)S(1)}, bf16[32,8,512]{2,1,0:T(8,128)(2,1)S(1)}, u32[]{:S(2)}, u32[]{:S(2)}) collective-permute-start(bf16[32,8,512]{2,1,0:T(8,128)(2,1)S(1)} %collective-permute-done.4.refs_4_), channel_id=1, source_target_pairs={{0,1},{1,0},{2,3},{3,2},{4,5},{5,4},{6,7},{7,6},{8,9},{9,8},{10,11... | collective-permute-start | bytes 786440 | tf_op jit(solution)/shard_map/ppermute | solution.py:20
  31.3 3.3 %copy-start.2 = (bf16[32,8,512]{2,1,0:T(8,128)(2,1)}, bf16[32,8,512]{2,1,0:T(8,128)(2,1)S(1)}, u32[]{:S(2)}) copy-start(bf16[32,8,512]{2,1,0:T(8,128)(2,1)S(1)} %collective-permute-done.5.refs_6_) | copy-start | bytes 786436
  31.4 3.3 %collective-permute-start.9 = (bf16[32,8,512]{2,1,0:T(8,128)(2,1)S(1)}, bf16[32,8,512]{2,1,0:T(8,128)(2,1)S(1)}, u32[]{:S(2)}, u32[]{:S(2)}) collective-permute-start(bf16[32,8,512]{2,1,0:T(8,128)(2,1)S(1)} %collective-permute-done.5.refs_6_), channel_id=1, source_target_pairs={{0,1},{1,0},{2,3},{3,2},{4,5},{5,4},{6,7},{7,6},{8,9},{9,8},{10,11... | collective-permute-start | bytes 786440 | tf_op jit(solution)/shard_map/ppermute | solution.py:20
  34.6 0.7 copy-start.3
  34.6 0.8 copy-start.4
  34.6 0.9 copy-start.5
  34.6 0.9 copy-start.6
  35.5 27.9 %copy-start.12 = (f32[32768]{0:T(1024)S(1)}, f32[32768]{0:T(1024)}, u32[]{:S(2)}) copy-start(f32[32768]{0:T(1024)} %param.16) | copy-start | bytes 393220
  46.4 2.2 %collective-permute-start.10 = (f32[32,8,512]{2,1,0:T(8,128)}, f32[32,8,512]{2,1,0:T(8,128)S(1)}, u32[]{:S(2)}, u32[]{:S(2)}) collective-permute-start(f32[32,8,512]{2,1,0:T(8,128)} %get-tuple-element.35), channel_id=1, source_target_pairs={{0,1},{1,0},{2,3},{3,2},{4,5},{5,4},{6,7},{7,6},{8,9},{9,8},{10,11... | collective-permute-start | bytes 1572872 | tf_op jit(solution)/shard_map/ppermute | solution.py:20
  49.8 5.8 %collective-permute-start.11 = (bf16[16,8,512]{2,1,0:T(8,128)(2,1)S(1)}, bf16[16,8,512]{2,1,0:T(8,128)(2,1)S(1)}, u32[]{:S(2)}, u32[]{:S(2)}) collective-permute-start(bf16[16,8,512]{2,1,0:T(8,128)(2,1)S(1)} %slice.37), channel_id=1, source_target_pairs={{0,2},{1,3},{2,0},{3,1},{4,6},{5,7},{6,4},{7,5},{8,10},{9,11},{10,... | collective-permute-start | bytes 393224 | tf_op jit(solution)/shard_map/ppermute | solution.py:20
  55.6 5.0 %collective-permute-start.12 = (bf16[16,8,512]{2,1,0:T(8,128)(2,1)S(1)}, bf16[16,8,512]{2,1,0:T(8,128)(2,1)S(1)}, u32[]{:S(2)}, u32[]{:S(2)}) collective-permute-start(bf16[16,8,512]{2,1,0:T(8,128)(2,1)S(1)} %fusion.1), channel_id=1, source_target_pairs={{0,4},{1,5},{2,6},{3,7},{4,0},{5,1},{6,2},{7,3},{8,12},{9,13},{10,... | collective-permute-start | bytes 393224 | tf_op jit(solution)/shard_map/ppermute | solution.py:20
  60.7 7.6 %collective-permute-start.13 = (bf16[16,8,512]{2,1,0:T(8,128)(2,1)S(1)}, bf16[16,8,512]{2,1,0:T(8,128)(2,1)S(1)}, u32[]{:S(2)}, u32[]{:S(2)}) collective-permute-start(bf16[16,8,512]{2,1,0:T(8,128)(2,1)S(1)} %fusion), channel_id=1, source_target_pairs={{0,8},{1,9},{2,10},{3,11},{4,12},{5,13},{6,14},{7,15},{8,0},{9,1},... | collective-permute-start | bytes 393224 | tf_op jit(solution)/shard_map/ppermute | solution.py:20
  68.4 6.4 %copy-start = (bf16[16,8,512]{2,1,0:T(8,128)(2,1)}, bf16[16,8,512]{2,1,0:T(8,128)(2,1)S(1)}, u32[]{:S(2)}) copy-start(bf16[16,8,512]{2,1,0:T(8,128)(2,1)S(1)} %multiply_convert_fusion.refs_3_) | copy-start | bytes 393220
  68.4 5.0 %collective-permute-start.14 = (bf16[16,8,512]{2,1,0:T(8,128)(2,1)S(1)}, bf16[16,8,512]{2,1,0:T(8,128)(2,1)S(1)}, u32[]{:S(2)}, u32[]{:S(2)}) collective-permute-start(bf16[16,8,512]{2,1,0:T(8,128)(2,1)S(1)} %multiply_convert_fusion.refs_3_), channel_id=1, source_target_pairs={{0,2},{1,3},{2,0},{3,1},{4,6},{5,7},{6,4},{7,5},{8,10},{9,11},{10,... | collective-permute-start | bytes 393224 | tf_op jit(solution)/shard_map/ppermute | solution.py:20
  69.0 4.5 %collective-permute-start.15 = (bf16[16,8,512]{2,1,0:T(8,128)(2,1)S(1)}, bf16[16,8,512]{2,1,0:T(8,128)(2,1)S(1)}, u32[]{:S(2)}, u32[]{:S(2)}) collective-permute-start(bf16[16,8,512]{2,1,0:T(8,128)(2,1)S(1)} %multiply_convert_fusion.refs_3_), channel_id=1, source_target_pairs={{0,1},{1,0},{2,3},{3,2},{4,5},{5,4},{6,7},{7,6},{8,9},{9,8},{10,11... | collective-permute-start | bytes 393224 | tf_op jit(solution)/shard_map/ppermute | solution.py:20
  73.4 1.4 %copy-start.9 = (bf16[16,8,512]{2,1,0:T(8,128)(2,1)}, bf16[16,8,512]{2,1,0:T(8,128)(2,1)S(1)}, u32[]{:S(2)}) copy-start(bf16[16,8,512]{2,1,0:T(8,128)(2,1)S(1)} %collective-permute-done.14.refs_4_) | copy-start | bytes 393220
  73.4 1.3 %collective-permute-start.16 = (bf16[16,8,512]{2,1,0:T(8,128)(2,1)S(1)}, bf16[16,8,512]{2,1,0:T(8,128)(2,1)S(1)}, u32[]{:S(2)}, u32[]{:S(2)}) collective-permute-start(bf16[16,8,512]{2,1,0:T(8,128)(2,1)S(1)} %collective-permute-done.14.refs_4_), channel_id=1, source_target_pairs={{0,1},{1,0},{2,3},{3,2},{4,5},{5,4},{6,7},{7,6},{8,9},{9,8},{10,11... | collective-permute-start | bytes 393224 | tf_op jit(solution)/shard_map/ppermute | solution.py:20
  73.4 1.3 %copy-start.10 = (bf16[16,8,512]{2,1,0:T(8,128)(2,1)}, bf16[16,8,512]{2,1,0:T(8,128)(2,1)S(1)}, u32[]{:S(2)}) copy-start(bf16[16,8,512]{2,1,0:T(8,128)(2,1)S(1)} %collective-permute-done.15.refs_5_) | copy-start | bytes 393220
  74.8 0.6 copy-start.11
  86.5 3.3 %collective-permute-start.17 = (bf16[128,8,512]{2,1,0:T(8,128)(2,1)}, bf16[128,8,512]{2,1,0:T(8,128)(2,1)S(1)}, u32[]{:S(2)}, u32[]{:S(2)}) collective-permute-start(bf16[128,8,512]{2,1,0:T(8,128)(2,1)} %get-tuple-element.37), channel_id=1, source_target_pairs={{0,1},{1,0},{2,3},{3,2},{4,5},{5,4},{6,7},{7,6},{8,9},{9,8},{10,11... | collective-permute-start | bytes 3145736 | tf_op jit(solution)/shard_map/ppermute | solution.py:20
  93.9 8.8 %collective-permute-start.18 = (bf16[32,8,512]{2,1,0:T(8,128)(2,1)}, bf16[32,8,512]{2,1,0:T(8,128)(2,1)S(1)}, u32[]{:S(2)}, u32[]{:S(2)}) collective-permute-start(bf16[32,8,512]{2,1,0:T(8,128)(2,1)} %get-tuple-element.39), channel_id=1, source_target_pairs={{0,4},{1,5},{2,6},{3,7},{4,0},{5,1},{6,2},{7,3},{8,12},{9,13},{10,... | collective-permute-start | bytes 786440 | tf_op jit(solution)/shard_map/ppermute | solution.py:20
  93.9 8.8 %collective-permute-start.19 = (bf16[32,8,512]{2,1,0:T(8,128)(2,1)}, bf16[32,8,512]{2,1,0:T(8,128)(2,1)S(1)}, u32[]{:S(2)}, u32[]{:S(2)}) collective-permute-start(bf16[32,8,512]{2,1,0:T(8,128)(2,1)} %get-tuple-element.41), channel_id=1, source_target_pairs={{0,2},{1,3},{2,0},{3,1},{4,6},{5,7},{6,4},{7,5},{8,10},{9,11},{10,... | collective-permute-start | bytes 786440 | tf_op jit(solution)/shard_map/ppermute | solution.py:20
  102.7 0.7 copy-start.7
  102.7 0.8 copy-start.8
  105.7 8.9 %collective-permute-start.20 = (bf16[16,8,512]{2,1,0:T(8,128)(2,1)}, bf16[16,8,512]{2,1,0:T(8,128)(2,1)S(1)}, u32[]{:S(2)}, u32[]{:S(2)}) collective-permute-start(bf16[16,8,512]{2,1,0:T(8,128)(2,1)} %get-tuple-element.43), channel_id=1, source_target_pairs={{0,8},{1,9},{2,10},{3,11},{4,12},{5,13},{6,14},{7,15},{8,0},{9,1},... | collective-permute-start | bytes 393224 | tf_op jit(solution)/shard_map/ppermute | solution.py:20
  108.6 6.5 %collective-permute-start.21 = (bf16[16,8,512]{2,1,0:T(8,128)(2,1)}, bf16[16,8,512]{2,1,0:T(8,128)(2,1)S(1)}, u32[]{:S(2)}, u32[]{:S(2)}) collective-permute-start(bf16[16,8,512]{2,1,0:T(8,128)(2,1)} %get-tuple-element.45), channel_id=1, source_target_pairs={{0,4},{1,5},{2,6},{3,7},{4,0},{5,1},{6,2},{7,3},{8,12},{9,13},{10,... | collective-permute-start | bytes 393224 | tf_op jit(solution)/shard_map/ppermute | solution.py:20
  114.6 0.7 copy-start.13
  115.1 0.7 copy-start.14
  117.6 4.5 %collective-permute-start.22 = (bf16[8,8,512]{2,1,0:T(8,128)(2,1)}, bf16[8,8,512]{2,1,0:T(8,128)(2,1)S(1)}, u32[]{:S(2)}, u32[]{:S(2)}) collective-permute-start(bf16[8,8,512]{2,1,0:T(8,128)(2,1)} %get-tuple-element.47), channel_id=1, source_target_pairs={{0,2},{1,3},{2,0},{3,1},{4,6},{5,7},{6,4},{7,5},{8,10},{9,11},{10,... | collective-permute-start | bytes 196616 | tf_op jit(solution)/shard_map/ppermute | solution.py:20
  118.1 5.4 %collective-permute-start.23 = (bf16[8,8,512]{2,1,0:T(8,128)(2,1)}, bf16[8,8,512]{2,1,0:T(8,128)(2,1)S(1)}, u32[]{:S(2)}, u32[]{:S(2)}) collective-permute-start(bf16[8,8,512]{2,1,0:T(8,128)(2,1)} %get-tuple-element.49), channel_id=1, source_target_pairs={{0,8},{1,9},{2,10},{3,11},{4,12},{5,13},{6,14},{7,15},{8,0},{9,1},... | collective-permute-start | bytes 196616 | tf_op jit(solution)/shard_map/ppermute | solution.py:20
  122.1 1.4 %copy-start.19 = (bf16[8,8,512]{2,1,0:T(8,128)(2,1)}, bf16[8,8,512]{2,1,0:T(8,128)(2,1)S(1)}, u32[]{:S(2)}) copy-start(bf16[8,8,512]{2,1,0:T(8,128)(2,1)S(1)} %collective-permute-done.22.recv_p) | copy-start | bytes 196612
  123.5 0.6 copy-start.20

commit v2 on v1

--- a/solution.py
+++ b/solution.py
@@ -1,3 +1,5 @@
+import math
+
 import jax
 import jax.numpy as jnp
 from jax import lax
@@ -8,7 +10,7 @@
 BF16 = jnp.bfloat16
 F32 = jnp.float32
 GROUP = 8
-VMEM_LIMIT = 56 * 1024 * 1024
+MIB = 1024 * 1024
 
 
 def whole(space=pltpu.VMEM):
@@ -20,15 +22,25 @@
     return lax.ppermute(array, "tile", [(i, i ^ bit) for i in range(count)])
 
 
-def local(body, outs, *ins, name, scratch=(), specs=None, flops=0):
-    nbytes = sum(a.size * a.dtype.itemsize for a in ins) + sum(a.size * a.dtype.itemsize for a in outs)
+def size_of(array):
+    return math.prod(array.shape) * jnp.dtype(array.dtype).itemsize
+
+
+def near(array):
+    return pltpu.with_memory_space_constraint(array, pltpu.VMEM)
+
+
+def local(body, outs, *ins, name, scratch=0, scratches=(), specs=None, flops=0, far_out=False):
+    nbytes = sum(size_of(a) for a in (*ins, *outs))
+    specs = specs or [whole()] * len(ins)
+    ins = [near(a) if s.memory_space == pltpu.VMEM else a for a, s in zip(ins, specs)]
     return pl.pallas_call(
         body,
-        out_shape=list(outs),
-        in_specs=specs or [whole()] * len(ins),
+        out_shape=[a if far_out else pltpu.VMEM(a.shape, a.dtype) for a in outs],
+        in_specs=specs,
         out_specs=[whole()] * len(outs),
-        scratch_shapes=list(scratch),
-        compiler_params=pltpu.CompilerParams(vmem_limit_bytes=VMEM_LIMIT),
+        scratch_shapes=list(scratches),
+        compiler_params=pltpu.CompilerParams(vmem_limit_bytes=scratch + 8 * MIB),
         cost_estimate=pl.CostEstimate(flops=flops, bytes_accessed=nbytes, transcendentals=0),
         name=name,
     )(*ins)
@@ -80,41 +92,30 @@
     return local(join_body, outs, *[x for pair in pairs for x in pair], name="join")
 
 
-def fold_body(*refs):
-    count = len(refs) // 4
-    for i in range(count):
-        keep, recv = refs[2 * i], refs[2 * i + 1]
-        mine, send = refs[2 * count + 2 * i], refs[2 * count + 2 * i + 1]
-        half = mine.shape[0]
-        mine[...] = keep[:half] + recv[:half].astype(F32)
-        send[...] = (keep[half:] + recv[half:].astype(F32)).astype(BF16)
-
-
 def fold(*pairs):
+    per = 4 // len(pairs)
     outs = []
     for keep, _ in pairs:
-        dims = (keep.shape[0] // 2,) + keep.shape[1:]
-        outs += [shape(dims, F32), shape(dims, BF16)]
-    flat = local(fold_body, outs, *[x for pair in pairs for x in pair], name="fold")
-    return [(flat[2 * i], flat[2 * i + 1]) for i in range(len(pairs))]
+        dims = (keep.shape[0] // per,) + keep.shape[1:]
+        outs += [shape(dims, F32), shape(dims, BF16)] * (per // 2)
+
+    def body(*refs):
+        done = refs[2 * len(pairs) :]
+        for i in range(4):
+            keep, recv = refs[2 * (i // per)], refs[2 * (i // per) + 1]
+            n = done[i].shape[0]
+            at = slice((i % per) * n, (i % per + 1) * n)
+            done[i][...] = (keep[at] + recv[at].astype(F32)).astype(done[i].dtype)
+
+    return local(body, outs, *[x for pair in pairs for x in pair], name="fold")
 
 
 def tiles_body(piece_count, src_at, dst_at, keep, *refs):
     pieces = refs[:piece_count]
-    first_hbm, second_hbm, mine, send, table, first, second, acc, sems = refs[piece_count:]
+    first, second, mine, send, table, acc = refs[piece_count:]
     groups = keep.shape[0]
     rank = first.shape[1]
     width = table.shape[2]
-    copies = []
-    for g in range(groups):
-        rows = pl.ds(g * GROUP, GROUP)
-        pair = (
-            pltpu.make_async_copy(first_hbm.at[rows], first.at[rows], sems.at[0, g]),
-            pltpu.make_async_copy(second_hbm.at[rows], second.at[rows], sems.at[1, g]),
-        )
-        for copy in pair:
-            copy.start()
-        copies.append(pair)
     acc[...] = jnp.zeros_like(acc)
     per = pieces[0].shape[0]
     for i, piece in enumerate(pieces):
@@ -125,8 +126,6 @@
     col_tile = lax.broadcasted_iota(jnp.int32, (GROUP * probes, span), 1) // rank
     own = row_tile == col_tile
     for g in range(groups):
-        for copy in copies[g]:
-            copy.wait()
         taken = jnp.concatenate(
             [table[src_at[g * GROUP + i]].astype(F32) for i in range(GROUP)], axis=0
         ).astype(BF16)
@@ -146,7 +145,6 @@
 def tiles(pieces, src_at, dst_at, keep, first, second, blocks, send_dtype, name):
     count, rank, width = first.shape
     probes = pieces[0].shape[1]
-    groups = keep.shape[0]
     rows = len(pieces) * pieces[0].shape[0]
     half = (blocks // 2, probes, width)
 
@@ -154,7 +152,7 @@
         tiles_body(len(pieces), *refs)
 
     smem = whole(pltpu.SMEM)
-    specs = [smem, smem, whole()] + [whole()] * len(pieces) + [whole(pl.ANY)] * 2
+    specs = [smem, smem] + [whole()] * (len(pieces) + 3)
     return local(
         body,
         [shape(half, F32), shape(half, send_dtype)],
@@ -167,12 +165,10 @@
         name=name,
         specs=specs,
         flops=4 * count * rank * width * probes * GROUP,
-        scratch=[
+        scratch=(2 * rows + 4 * blocks) * probes * width,
+        scratches=[
             pltpu.VMEM((rows, probes, width), BF16),
-            pltpu.VMEM((count, rank, width), BF16),
-            pltpu.VMEM((count, rank, width), BF16),
             pltpu.VMEM((blocks, probes, width), F32),
-            pltpu.SemaphoreType.DMA((2, groups)),
         ],
     )
 
@@ -277,20 +273,18 @@
         pieces, row_at, cell_at, keep, u_factor, v_factor, peers * cell_blocks, BF16, "adjoint"
     )
     got_all = swap(send_all, 1)
-    half = keep_all.shape[0] // 2
-    pair_p = (keep_all[:half], got_all[:half])
-    pair_q = (keep_all[half:], got_all[half:])
+    pairs = [(keep_all, got_all)]
     for bit_p, bit_q in zip(order_p[::-1], order_q[::-1]):
-        (keep_p, send_p), (keep_q, send_q) = fold(pair_p, pair_q)
-        pair_p = (keep_p, swap(send_p, bit_p))
-        pair_q = (keep_q, swap(send_q, bit_q))
+        keep_p, send_p, keep_q, send_q = fold(*pairs)
+        pairs = [(keep_p, swap(send_p, bit_p)), (keep_q, swap(send_q, bit_q))]
     return local(
         final_body,
         [shape((probe_count, cell_total), F32)],
-        *pair_p,
-        *pair_q,
+        *pairs[0],
+        *pairs[1],
         scaling,
         name="final",
+        far_out=True,
     )[0]
 
 

time: 126 us -> 105 us (0.83)
  Pallas kernels: 36.1 us -> 13.1 us
  local copies, waits for them, and re-layouts: 10.5 us -> 13.1 us
  other arithmetic: 3.37 us -> 1.04 us
  waiting for transfers between devices: 53 us -> 54.7 us
    pallas_call x9, Pallas kernels: 36.1 us -> 13.1 us  [local(): pl.pallas_call(body, out_shape=[a if far_out else pltpu.VMEM(a.shape, a.d...]
    unnamed x42 -> x18, local copies, waits for them, and re-layouts: 5.27 us -> 11.9 us
    slice x2 -> x0, local copies, waits for them, and re-layouts: 4.09 us -> none  [shards(): pair_q = (keep_all[half:], got_all[half:])]
    ppermute x24, waiting for transfers between devices: 53 us -> 54.7 us  [swap(): return lax.ppermute(array, 'tile', [(i, i ^ bit) for i in range(count)])]
  transfers between devices with their start and end apart: 24 -> 24, of which waited for: 16 -> 18; matrix products, arithmetic and copies ran while one was open for 5% -> 2% of each run, Pallas kernels for 0% -> 0%
where the time goes in v2:
time: 105 us
  waiting for transfers between devices  54.7 us (52%)
  starting transfers between devices  22.7 us (22%)
  local copies, waits for them, and re-layouts  13.1 us (12%)
  Pallas kernels  13.1 us (12%)
    ppermute x24, waiting for transfers between devices, swap(): return lax.ppermute(array, 'tile', [(i, i ^ bit) for i in range(count)])  54.7 us
    ppermute x24, starting transfers between devices, swap(): return lax.ppermute(array, 'tile', [(i, i ^ bit) for i in range(count)])  22.7 us
    pallas_call x9, Pallas kernels, local(): pl.pallas_call(body, out_shape=[a if far_out else pltpu.VMEM(a.shape, a.d...  13.1 us
    unnamed x18, local copies, waits for them, and re-layouts  11.9 us
  transfers between devices with their start and end apart: 24, of which 18 were waited for; matrix products, arithmetic and copies ran while one was open for 2% of the time, Pallas kernels for 0%

profile of v2, /device:TPU:0, one launch (start us, length us, event | category | flops | bytes accessed | tf_op | source)
XLA Modules:
  0.0 104.7 jit_solution(15524165146358473070)
XLA Ops:
  0.0 0.9 copy-done.4
  1.0 0.8 copy-done.5
  1.7 0.8 copy-done.6
  2.5 0.7 copy-done.7
  3.1 0.6 scale.1
  3.7 3.0 %collective-permute-start = (bf16[8,8,512]{2,1,0:T(8,128)(2,1)S(1)}, bf16[8,8,512]{2,1,0:T(8,128)(2,1)S(1)}, u32[]{:S(2)}, u32[]{:S(2)}) collective-permute-start(bf16[8,8,512]{2,1,0:T(8,128)(2,1)S(1)} %get-tuple-element.28.refs_0_), channel_id=1, source_target_pairs={{0,2},{1,3},{2,0},{3,1},{4,6},{5,7},{6,4},{7,5},{8,10},{9,11},{10,... | collective-permute-start | bytes 196616 | tf_op jit(solution)/shard_map/ppermute | solution.py:22
  6.7 2.6 %collective-permute-start.1 = (bf16[8,8,512]{2,1,0:T(8,128)(2,1)S(1)}, bf16[8,8,512]{2,1,0:T(8,128)(2,1)S(1)}, u32[]{:S(2)}, u32[]{:S(2)}) collective-permute-start(bf16[8,8,512]{2,1,0:T(8,128)(2,1)S(1)} %get-tuple-element.29.refs_2_), channel_id=1, source_target_pairs={{0,8},{1,9},{2,10},{3,11},{4,12},{5,13},{6,14},{7,15},{8,0},{9,1},... | collective-permute-start | bytes 196616 | tf_op jit(solution)/shard_map/ppermute | solution.py:22
  9.3 2.9 %collective-permute-done.1.refs_3_ = bf16[8,8,512]{2,1,0:T(8,128)(2,1)S(1)} collective-permute-done((bf16[8,8,512]{2,1,0:T(8,128)(2,1)S(1)}, bf16[8,8,512]{2,1,0:T(8,128)(2,1)S(1)}, u32[]{:S(2)}, u32[]{:S(2)}) %collective-permute-start.1) | collective-permute-done | bytes 65568 | tf_op jit(solution)/shard_map/ppermute | solution.py:22
  12.2 2.4 %collective-permute-start.2 = (bf16[16,8,512]{2,1,0:T(8,128)(2,1)S(1)}, bf16[16,8,512]{2,1,0:T(8,128)(2,1)S(1)}, u32[]{:S(2)}, u32[]{:S(2)}) collective-permute-start(bf16[16,8,512]{2,1,0:T(8,128)(2,1)S(1)} %get-tuple-element.30.refs_0_), channel_id=1, source_target_pairs={{0,8},{1,9},{2,10},{3,11},{4,12},{5,13},{6,14},{7,15},{8,0},{9,1},... | collective-permute-start | bytes 393224 | tf_op jit(solution)/shard_map/ppermute | solution.py:22
  14.7 2.1 %collective-permute-start.3 = (bf16[16,8,512]{2,1,0:T(8,128)(2,1)S(1)}, bf16[16,8,512]{2,1,0:T(8,128)(2,1)S(1)}, u32[]{:S(2)}, u32[]{:S(2)}) collective-permute-start(bf16[16,8,512]{2,1,0:T(8,128)(2,1)S(1)} %get-tuple-element.31.refs_2_), channel_id=1, source_target_pairs={{0,4},{1,5},{2,6},{3,7},{4,0},{5,1},{6,2},{7,3},{8,12},{9,13},{10,... | collective-permute-start | bytes 393224 | tf_op jit(solution)/shard_map/ppermute | solution.py:22
  16.8 2.9 %collective-permute-done.2.refs_1_ = bf16[16,8,512]{2,1,0:T(8,128)(2,1)S(1)} collective-permute-done((bf16[16,8,512]{2,1,0:T(8,128)(2,1)S(1)}, bf16[16,8,512]{2,1,0:T(8,128)(2,1)S(1)}, u32[]{:S(2)}, u32[]{:S(2)}) %collective-permute-start.2) | collective-permute-done | bytes 131104 | tf_op jit(solution)/shard_map/ppermute | solution.py:22
  19.7 0.3 collective-permute-done.3.refs_3_
  20.0 1.8 %collective-permute-start.4 = (bf16[32,8,512]{2,1,0:T(8,128)(2,1)S(1)}, bf16[32,8,512]{2,1,0:T(8,128)(2,1)S(1)}, u32[]{:S(2)}, u32[]{:S(2)}) collective-permute-start(bf16[32,8,512]{2,1,0:T(8,128)(2,1)S(1)} %get-tuple-element.32.refs_3_), channel_id=1, source_target_pairs={{0,4},{1,5},{2,6},{3,7},{4,0},{5,1},{6,2},{7,3},{8,12},{9,13},{10,... | collective-permute-start | bytes 786440 | tf_op jit(solution)/shard_map/ppermute | solution.py:22
  21.8 0.5 collective-permute-start.5
  22.3 0.5 collective-permute-start.8
  22.8 3.9 %collective-permute-done.4.refs_4_ = bf16[32,8,512]{2,1,0:T(8,128)(2,1)S(1)} collective-permute-done((bf16[32,8,512]{2,1,0:T(8,128)(2,1)S(1)}, bf16[32,8,512]{2,1,0:T(8,128)(2,1)S(1)}, u32[]{:S(2)}, u32[]{:S(2)}) %collective-permute-start.4) | collective-permute-done | bytes 262176 | tf_op jit(solution)/shard_map/ppermute | solution.py:22
  26.8 1.4 %collective-permute-done.5.refs_6_ = bf16[32,8,512]{2,1,0:T(8,128)(2,1)S(1)} collective-permute-done((bf16[32,8,512]{2,1,0:T(8,128)(2,1)S(1)}, bf16[32,8,512]{2,1,0:T(8,128)(2,1)S(1)}, u32[]{:S(2)}, u32[]{:S(2)}) %collective-permute-start.5) | collective-permute-done | bytes 262176 | tf_op jit(solution)/shard_map/ppermute | solution.py:22
  28.2 0.8 fusion.7
  29.0 0.8 dynamic_slice.25
  30.2 2.2 %copy-done = bf16[128,32,512]{2,1,0:T(8,128)(2,1)S(1)} copy-done((bf16[128,32,512]{2,1,0:T(8,128)(2,1)S(1)}, bf16[128,32,512]{2,1,0:T(8,128)(2,1)}, u32[]{:S(2)}) %copy-start) | copy-done | bytes 4194328
  32.4 2.2 %copy-done.2 = bf16[128,32,512]{2,1,0:T(8,128)(2,1)S(1)} copy-done((bf16[128,32,512]{2,1,0:T(8,128)(2,1)S(1)}, bf16[128,32,512]{2,1,0:T(8,128)(2,1)}, u32[]{:S(2)}) %copy-start.2) | copy-done | bytes 4194328
  34.5 5.5 %forward.1 = (f32[32,8,512]{2,1,0:T(8,128)S(1)}, f32[32,8,512]{2,1,0:T(8,128)S(1)}) custom-call(s32[128]{0:T(128)S(1)} %get-tuple-element.51.refs_0_.refs_1_, s32[128]{0:T(128)S(1)} %get-tuple-element.52.refs_1_.refs_0_, f32[16,256]{1,0:T(8,128)S(1)} %compare_convert_fusion.refs_2_, bf16[32,8,512]{2,1,0:T(8,128)(2,1)S(1)} %get-tuple-element.32.refs_3_, ...), custom_call_target="tpu_custom_call" | custom-call | flops 536870912 | bytes 11551744 | tf_op jit(solution)/shard_map/forward/pallas_call | solution.py:37
  40.1 0.6 collective-permute-start.10
  40.7 1.5 %collective-permute-done.10 = f32[32,8,512]{2,1,0:T(8,128)S(1)} collective-permute-done((f32[32,8,512]{2,1,0:T(8,128)S(1)}, f32[32,8,512]{2,1,0:T(8,128)S(1)}, u32[]{:S(2)}, u32[]{:S(2)}) %collective-permute-start.10) | collective-permute-done | bytes 524320 | tf_op jit(solution)/shard_map/ppermute | solution.py:22
  42.3 0.6 collective-permute-start.11
  42.9 5.3 %collective-permute-done.11 = bf16[16,8,512]{2,1,0:T(8,128)(2,1)S(1)} collective-permute-done((bf16[16,8,512]{2,1,0:T(8,128)(2,1)S(1)}, bf16[16,8,512]{2,1,0:T(8,128)(2,1)S(1)}, u32[]{:S(2)}, u32[]{:S(2)}) %collective-permute-start.11) | collective-permute-done | bytes 131104 | tf_op jit(solution)/shard_map/ppermute | solution.py:22
  48.2 0.4 collective-permute-start.12
  48.6 4.7 %collective-permute-done.12 = bf16[16,8,512]{2,1,0:T(8,128)(2,1)S(1)} collective-permute-done((bf16[16,8,512]{2,1,0:T(8,128)(2,1)S(1)}, bf16[16,8,512]{2,1,0:T(8,128)(2,1)S(1)}, u32[]{:S(2)}, u32[]{:S(2)}) %collective-permute-start.12) | collective-permute-done | bytes 131104 | tf_op jit(solution)/shard_map/ppermute | solution.py:22
  53.3 2.0 %collective-permute-start.13 = (bf16[16,8,512]{2,1,0:T(8,128)(2,1)S(1)}, bf16[16,8,512]{2,1,0:T(8,128)(2,1)S(1)}, u32[]{:S(2)}, u32[]{:S(2)}) collective-permute-start(bf16[16,8,512]{2,1,0:T(8,128)(2,1)S(1)} %fusion), channel_id=1, source_target_pairs={{0,8},{1,9},{2,10},{3,11},{4,12},{5,13},{6,14},{7,15},{8,0},{9,1},... | collective-permute-start | bytes 393224 | tf_op jit(solution)/shard_map/ppermute | solution.py:22
  55.4 5.2 %collective-permute-done.13 = bf16[16,8,512]{2,1,0:T(8,128)(2,1)S(1)} collective-permute-done((bf16[16,8,512]{2,1,0:T(8,128)(2,1)S(1)}, bf16[16,8,512]{2,1,0:T(8,128)(2,1)S(1)}, u32[]{:S(2)}, u32[]{:S(2)}) %collective-permute-start.13) | collective-permute-done | bytes 131104 | tf_op jit(solution)/shard_map/ppermute | solution.py:22
  60.7 0.6 collective-permute-start.14
  61.2 4.5 %collective-permute-done.14.refs_4_ = bf16[16,8,512]{2,1,0:T(8,128)(2,1)S(1)} collective-permute-done((bf16[16,8,512]{2,1,0:T(8,128)(2,1)S(1)}, bf16[16,8,512]{2,1,0:T(8,128)(2,1)S(1)}, u32[]{:S(2)}, u32[]{:S(2)}) %collective-permute-start.14) | collective-permute-done | bytes 131104 | tf_op jit(solution)/shard_map/ppermute | solution.py:22
  65.7 1.3 %collective-permute-done.16.refs_6_ = bf16[16,8,512]{2,1,0:T(8,128)(2,1)S(1)} collective-permute-done((bf16[16,8,512]{2,1,0:T(8,128)(2,1)S(1)}, bf16[16,8,512]{2,1,0:T(8,128)(2,1)S(1)}, u32[]{:S(2)}, u32[]{:S(2)}) %collective-permute-start.16) | collective-permute-done | bytes 131104 | tf_op jit(solution)/shard_map/ppermute | solution.py:22
  67.0 2.2 %copy-done.1 = bf16[128,32,512]{2,1,0:T(8,128)(2,1)S(1)} copy-done((bf16[128,32,512]{2,1,0:T(8,128)(2,1)S(1)}, bf16[128,32,512]{2,1,0:T(8,128)(2,1)}, u32[]{:S(2)}) %copy-start.1) | copy-done | bytes 4194328
  69.2 2.2 %copy-done.3 = bf16[128,32,512]{2,1,0:T(8,128)(2,1)S(1)} copy-done((bf16[128,32,512]{2,1,0:T(8,128)(2,1)S(1)}, bf16[128,32,512]{2,1,0:T(8,128)(2,1)}, u32[]{:S(2)}) %copy-start.3) | copy-done | bytes 4194328
  71.4 5.8 %adjoint.1 = (f32[128,8,512]{2,1,0:T(8,128)S(1)}, bf16[128,8,512]{2,1,0:T(8,128)(2,1)S(1)}) custom-call(s32[128]{0:T(128)S(1)} %get-tuple-element.52.refs_1_.refs_0_, s32[128]{0:T(128)S(1)} %get-tuple-element.51.refs_0_.refs_1_, f32[16,256]{1,0:T(8,128)S(1)} %compare_convert_fusion.refs_2_, bf16[16,8,512]{2,1,0:T(8,128)(2,1)S(1)} %multiply_convert_fusion.refs_3_, ...), custom_call_target="tpu_custom_call" | custom-call | flops 536870912 | bytes 12076032 | tf_op jit(solution)/shard_map/adjoint/pallas_call | solution.py:37
  77.4 2.5 %collective-permute-done.17.refs_1_ = bf16[128,8,512]{2,1,0:T(8,128)(2,1)S(1)} collective-permute-done((bf16[128,8,512]{2,1,0:T(8,128)(2,1)S(1)}, bf16[128,8,512]{2,1,0:T(8,128)(2,1)S(1)}, u32[]{:S(2)}, u32[]{:S(2)}) %collective-permute-start.17) | collective-permute-done | bytes 1048608 | tf_op jit(solution)/shard_map/ppermute | solution.py:22
  79.9 0.2 fold.3
  80.3 0.6 collective-permute-start.19
  80.8 7.8 %collective-permute-done.18.refs_1_ = bf16[32,8,512]{2,1,0:T(8,128)(2,1)S(1)} collective-permute-done((bf16[32,8,512]{2,1,0:T(8,128)(2,1)S(1)}, bf16[32,8,512]{2,1,0:T(8,128)(2,1)S(1)}, u32[]{:S(2)}, u32[]{:S(2)}) %collective-permute-start.18) | collective-permute-done | bytes 262176 | tf_op jit(solution)/shard_map/ppermute | solution.py:22
  88.8 2.6 %collective-permute-start.20 = (bf16[16,8,512]{2,1,0:T(8,128)(2,1)S(1)}, bf16[16,8,512]{2,1,0:T(8,128)(2,1)S(1)}, u32[]{:S(2)}, u32[]{:S(2)}) collective-permute-start(bf16[16,8,512]{2,1,0:T(8,128)(2,1)S(1)} %get-tuple-element.43), channel_id=1, source_target_pairs={{0,8},{1,9},{2,10},{3,11},{4,12},{5,13},{6,14},{7,15},{8,0},{9,1},... | collective-permute-start | bytes 393224 | tf_op jit(solution)/shard_map/ppermute | solution.py:22
  91.4 0.4 collective-permute-start.21
  91.8 5.6 %collective-permute-done.20.refs_1_ = bf16[16,8,512]{2,1,0:T(8,128)(2,1)S(1)} collective-permute-done((bf16[16,8,512]{2,1,0:T(8,128)(2,1)S(1)}, bf16[16,8,512]{2,1,0:T(8,128)(2,1)S(1)}, u32[]{:S(2)}, u32[]{:S(2)}) %collective-permute-start.20) | collective-permute-done | bytes 131104 | tf_op jit(solution)/shard_map/ppermute | solution.py:22
  97.6 0.6 collective-permute-start.22
  98.1 1.1 %collective-permute-start.23 = (bf16[8,8,512]{2,1,0:T(8,128)(2,1)S(1)}, bf16[8,8,512]{2,1,0:T(8,128)(2,1)S(1)}, u32[]{:S(2)}, u32[]{:S(2)}) collective-permute-start(bf16[8,8,512]{2,1,0:T(8,128)(2,1)S(1)} %get-tuple-element.49), channel_id=1, source_target_pairs={{0,8},{1,9},{2,10},{3,11},{4,12},{5,13},{6,14},{7,15},{8,0},{9,1},... | collective-permute-start | bytes 196616 | tf_op jit(solution)/shard_map/ppermute | solution.py:22
  99.3 2.6 %collective-permute-done.22.recv_p = bf16[8,8,512]{2,1,0:T(8,128)(2,1)S(1)} collective-permute-done((bf16[8,8,512]{2,1,0:T(8,128)(2,1)S(1)}, bf16[8,8,512]{2,1,0:T(8,128)(2,1)S(1)}, u32[]{:S(2)}, u32[]{:S(2)}) %collective-permute-start.22) | collective-permute-done | bytes 65568 | tf_op jit(solution)/shard_map/ppermute | solution.py:22
  101.9 2.1 %collective-permute-done.23.recv_q = bf16[8,8,512]{2,1,0:T(8,128)(2,1)S(1)} collective-permute-done((bf16[8,8,512]{2,1,0:T(8,128)(2,1)S(1)}, bf16[8,8,512]{2,1,0:T(8,128)(2,1)S(1)}, u32[]{:S(2)}, u32[]{:S(2)}) %collective-permute-start.23) | collective-permute-done | bytes 65568 | tf_op jit(solution)/shard_map/ppermute | solution.py:22
  104.0 0.7 final.1
  (43 shorter events, 1.4 us)
Async XLA Ops:
  0.0 0.9 copy-start.4
  1.0 0.8 copy-start.5
  1.7 0.8 copy-start.6
  2.5 0.7 copy-start.7
  3.7 5.6 %collective-permute-start = (bf16[8,8,512]{2,1,0:T(8,128)(2,1)S(1)}, bf16[8,8,512]{2,1,0:T(8,128)(2,1)S(1)}, u32[]{:S(2)}, u32[]{:S(2)}) collective-permute-start(bf16[8,8,512]{2,1,0:T(8,128)(2,1)S(1)} %get-tuple-element.28.refs_0_), channel_id=1, source_target_pairs={{0,2},{1,3},{2,0},{3,1},{4,6},{5,7},{6,4},{7,5},{8,10},{9,11},{10,... | collective-permute-start | bytes 196616 | tf_op jit(solution)/shard_map/ppermute | solution.py:22
  6.7 5.5 %collective-permute-start.1 = (bf16[8,8,512]{2,1,0:T(8,128)(2,1)S(1)}, bf16[8,8,512]{2,1,0:T(8,128)(2,1)S(1)}, u32[]{:S(2)}, u32[]{:S(2)}) collective-permute-start(bf16[8,8,512]{2,1,0:T(8,128)(2,1)S(1)} %get-tuple-element.29.refs_2_), channel_id=1, source_target_pairs={{0,8},{1,9},{2,10},{3,11},{4,12},{5,13},{6,14},{7,15},{8,0},{9,1},... | collective-permute-start | bytes 196616 | tf_op jit(solution)/shard_map/ppermute | solution.py:22
  12.2 7.4 %collective-permute-start.2 = (bf16[16,8,512]{2,1,0:T(8,128)(2,1)S(1)}, bf16[16,8,512]{2,1,0:T(8,128)(2,1)S(1)}, u32[]{:S(2)}, u32[]{:S(2)}) collective-permute-start(bf16[16,8,512]{2,1,0:T(8,128)(2,1)S(1)} %get-tuple-element.30.refs_0_), channel_id=1, source_target_pairs={{0,8},{1,9},{2,10},{3,11},{4,12},{5,13},{6,14},{7,15},{8,0},{9,1},... | collective-permute-start | bytes 393224 | tf_op jit(solution)/shard_map/ppermute | solution.py:22
  14.7 5.3 %collective-permute-start.3 = (bf16[16,8,512]{2,1,0:T(8,128)(2,1)S(1)}, bf16[16,8,512]{2,1,0:T(8,128)(2,1)S(1)}, u32[]{:S(2)}, u32[]{:S(2)}) collective-permute-start(bf16[16,8,512]{2,1,0:T(8,128)(2,1)S(1)} %get-tuple-element.31.refs_2_), channel_id=1, source_target_pairs={{0,4},{1,5},{2,6},{3,7},{4,0},{5,1},{6,2},{7,3},{8,12},{9,13},{10,... | collective-permute-start | bytes 393224 | tf_op jit(solution)/shard_map/ppermute | solution.py:22
  20.0 6.8 %collective-permute-start.4 = (bf16[32,8,512]{2,1,0:T(8,128)(2,1)S(1)}, bf16[32,8,512]{2,1,0:T(8,128)(2,1)S(1)}, u32[]{:S(2)}, u32[]{:S(2)}) collective-permute-start(bf16[32,8,512]{2,1,0:T(8,128)(2,1)S(1)} %get-tuple-element.32.refs_3_), channel_id=1, source_target_pairs={{0,4},{1,5},{2,6},{3,7},{4,0},{5,1},{6,2},{7,3},{8,12},{9,13},{10,... | collective-permute-start | bytes 786440 | tf_op jit(solution)/shard_map/ppermute | solution.py:22
  21.8 6.4 %collective-permute-start.5 = (bf16[32,8,512]{2,1,0:T(8,128)(2,1)S(1)}, bf16[32,8,512]{2,1,0:T(8,128)(2,1)S(1)}, u32[]{:S(2)}, u32[]{:S(2)}) collective-permute-start(bf16[32,8,512]{2,1,0:T(8,128)(2,1)S(1)} %get-tuple-element.33.refs_5_), channel_id=1, source_target_pairs={{0,2},{1,3},{2,0},{3,1},{4,6},{5,7},{6,4},{7,5},{8,10},{9,11},{10,... | collective-permute-start | bytes 786440 | tf_op jit(solution)/shard_map/ppermute | solution.py:22
  22.3 7.8 %collective-permute-start.6 = (bf16[32,8,512]{2,1,0:T(8,128)(2,1)S(1)}, bf16[32,8,512]{2,1,0:T(8,128)(2,1)S(1)}, u32[]{:S(2)}, u32[]{:S(2)}) collective-permute-start(bf16[32,8,512]{2,1,0:T(8,128)(2,1)S(1)} %get-tuple-element.32.refs_3_), channel_id=1, source_target_pairs={{0,1},{1,0},{2,3},{3,2},{4,5},{5,4},{6,7},{7,6},{8,9},{9,8},{10,11... | collective-permute-start | bytes 786440 | tf_op jit(solution)/shard_map/ppermute | solution.py:22
  22.3 7.8 %collective-permute-start.8 = (bf16[32,8,512]{2,1,0:T(8,128)(2,1)S(1)}, bf16[32,8,512]{2,1,0:T(8,128)(2,1)S(1)}, u32[]{:S(2)}, u32[]{:S(2)}) collective-permute-start(bf16[32,8,512]{2,1,0:T(8,128)(2,1)S(1)} %get-tuple-element.33.refs_5_), channel_id=1, source_target_pairs={{0,1},{1,0},{2,3},{3,2},{4,5},{5,4},{6,7},{7,6},{8,9},{9,8},{10,11... | collective-permute-start | bytes 786440 | tf_op jit(solution)/shard_map/ppermute | solution.py:22
  26.8 3.4 %collective-permute-start.7 = (bf16[32,8,512]{2,1,0:T(8,128)(2,1)S(1)}, bf16[32,8,512]{2,1,0:T(8,128)(2,1)S(1)}, u32[]{:S(2)}, u32[]{:S(2)}) collective-permute-start(bf16[32,8,512]{2,1,0:T(8,128)(2,1)S(1)} %collective-permute-done.4.refs_4_), channel_id=1, source_target_pairs={{0,1},{1,0},{2,3},{3,2},{4,5},{5,4},{6,7},{7,6},{8,9},{9,8},{10,11... | collective-permute-start | bytes 786440 | tf_op jit(solution)/shard_map/ppermute | solution.py:22
  28.2 2.0 %collective-permute-start.9 = (bf16[32,8,512]{2,1,0:T(8,128)(2,1)S(1)}, bf16[32,8,512]{2,1,0:T(8,128)(2,1)S(1)}, u32[]{:S(2)}, u32[]{:S(2)}) collective-permute-start(bf16[32,8,512]{2,1,0:T(8,128)(2,1)S(1)} %collective-permute-done.5.refs_6_), channel_id=1, source_target_pairs={{0,1},{1,0},{2,3},{3,2},{4,5},{5,4},{6,7},{7,6},{8,9},{9,8},{10,11... | collective-permute-start | bytes 786440 | tf_op jit(solution)/shard_map/ppermute | solution.py:22
  30.2 2.2 %copy-start = (bf16[128,32,512]{2,1,0:T(8,128)(2,1)S(1)}, bf16[128,32,512]{2,1,0:T(8,128)(2,1)}, u32[]{:S(2)}) copy-start(bf16[128,32,512]{2,1,0:T(8,128)(2,1)} %refs_8_.1) | copy-start | bytes 12582916
  32.4 2.2 %copy-start.2 = (bf16[128,32,512]{2,1,0:T(8,128)(2,1)S(1)}, bf16[128,32,512]{2,1,0:T(8,128)(2,1)}, u32[]{:S(2)}) copy-start(bf16[128,32,512]{2,1,0:T(8,128)(2,1)} %refs_7_.1) | copy-start | bytes 12582916
  34.5 20.8 %copy-start.8 = (f32[32768]{0:T(1024)S(1)}, f32[32768]{0:T(1024)}, u32[]{:S(2)}) copy-start(f32[32768]{0:T(1024)} %param.16) | copy-start | bytes 393220
  40.1 2.1 %collective-permute-start.10 = (f32[32,8,512]{2,1,0:T(8,128)S(1)}, f32[32,8,512]{2,1,0:T(8,128)S(1)}, u32[]{:S(2)}, u32[]{:S(2)}) collective-permute-start(f32[32,8,512]{2,1,0:T(8,128)S(1)} %get-tuple-element.35), channel_id=1, source_target_pairs={{0,1},{1,0},{2,3},{3,2},{4,5},{5,4},{6,7},{7,6},{8,9},{9,8},{10,11... | collective-permute-start | bytes 1572872 | tf_op jit(solution)/shard_map/ppermute | solution.py:22
  42.3 5.8 %collective-permute-start.11 = (bf16[16,8,512]{2,1,0:T(8,128)(2,1)S(1)}, bf16[16,8,512]{2,1,0:T(8,128)(2,1)S(1)}, u32[]{:S(2)}, u32[]{:S(2)}) collective-permute-start(bf16[16,8,512]{2,1,0:T(8,128)(2,1)S(1)} %slice.19), channel_id=1, source_target_pairs={{0,2},{1,3},{2,0},{3,1},{4,6},{5,7},{6,4},{7,5},{8,10},{9,11},{10,... | collective-permute-start | bytes 393224 | tf_op jit(solution)/shard_map/ppermute | solution.py:22
  48.2 5.0 %collective-permute-start.12 = (bf16[16,8,512]{2,1,0:T(8,128)(2,1)S(1)}, bf16[16,8,512]{2,1,0:T(8,128)(2,1)S(1)}, u32[]{:S(2)}, u32[]{:S(2)}) collective-permute-start(bf16[16,8,512]{2,1,0:T(8,128)(2,1)S(1)} %fusion.1), channel_id=1, source_target_pairs={{0,4},{1,5},{2,6},{3,7},{4,0},{5,1},{6,2},{7,3},{8,12},{9,13},{10,... | collective-permute-start | bytes 393224 | tf_op jit(solution)/shard_map/ppermute | solution.py:22
  53.3 7.3 %collective-permute-start.13 = (bf16[16,8,512]{2,1,0:T(8,128)(2,1)S(1)}, bf16[16,8,512]{2,1,0:T(8,128)(2,1)S(1)}, u32[]{:S(2)}, u32[]{:S(2)}) collective-permute-start(bf16[16,8,512]{2,1,0:T(8,128)(2,1)S(1)} %fusion), channel_id=1, source_target_pairs={{0,8},{1,9},{2,10},{3,11},{4,12},{5,13},{6,14},{7,15},{8,0},{9,1},... | collective-permute-start | bytes 393224 | tf_op jit(solution)/shard_map/ppermute | solution.py:22
  60.7 5.0 %collective-permute-start.14 = (bf16[16,8,512]{2,1,0:T(8,128)(2,1)S(1)}, bf16[16,8,512]{2,1,0:T(8,128)(2,1)S(1)}, u32[]{:S(2)}, u32[]{:S(2)}) collective-permute-start(bf16[16,8,512]{2,1,0:T(8,128)(2,1)S(1)} %multiply_convert_fusion.refs_3_), channel_id=1, source_target_pairs={{0,2},{1,3},{2,0},{3,1},{4,6},{5,7},{6,4},{7,5},{8,10},{9,11},{10,... | collective-permute-start | bytes 393224 | tf_op jit(solution)/shard_map/ppermute | solution.py:22
  61.2 4.5 %collective-permute-start.15 = (bf16[16,8,512]{2,1,0:T(8,128)(2,1)S(1)}, bf16[16,8,512]{2,1,0:T(8,128)(2,1)S(1)}, u32[]{:S(2)}, u32[]{:S(2)}) collective-permute-start(bf16[16,8,512]{2,1,0:T(8,128)(2,1)S(1)} %multiply_convert_fusion.refs_3_), channel_id=1, source_target_pairs={{0,1},{1,0},{2,3},{3,2},{4,5},{5,4},{6,7},{7,6},{8,9},{9,8},{10,11... | collective-permute-start | bytes 393224 | tf_op jit(solution)/shard_map/ppermute | solution.py:22
  65.7 1.3 %collective-permute-start.16 = (bf16[16,8,512]{2,1,0:T(8,128)(2,1)S(1)}, bf16[16,8,512]{2,1,0:T(8,128)(2,1)S(1)}, u32[]{:S(2)}, u32[]{:S(2)}) collective-permute-start(bf16[16,8,512]{2,1,0:T(8,128)(2,1)S(1)} %collective-permute-done.14.refs_4_), channel_id=1, source_target_pairs={{0,1},{1,0},{2,3},{3,2},{4,5},{5,4},{6,7},{7,6},{8,9},{9,8},{10,11... | collective-permute-start | bytes 393224 | tf_op jit(solution)/shard_map/ppermute | solution.py:22
  67.0 2.2 %copy-start.1 = (bf16[128,32,512]{2,1,0:T(8,128)(2,1)S(1)}, bf16[128,32,512]{2,1,0:T(8,128)(2,1)}, u32[]{:S(2)}) copy-start(bf16[128,32,512]{2,1,0:T(8,128)(2,1)} %refs_8_.1) | copy-start | bytes 12582916
  69.2 2.2 %copy-start.3 = (bf16[128,32,512]{2,1,0:T(8,128)(2,1)S(1)}, bf16[128,32,512]{2,1,0:T(8,128)(2,1)}, u32[]{:S(2)}) copy-start(bf16[128,32,512]{2,1,0:T(8,128)(2,1)} %refs_7_.1) | copy-start | bytes 12582916
  77.2 2.7 %collective-permute-start.17 = (bf16[128,8,512]{2,1,0:T(8,128)(2,1)S(1)}, bf16[128,8,512]{2,1,0:T(8,128)(2,1)S(1)}, u32[]{:S(2)}, u32[]{:S(2)}) collective-permute-start(bf16[128,8,512]{2,1,0:T(8,128)(2,1)S(1)} %get-tuple-element.37), channel_id=1, source_target_pairs={{0,1},{1,0},{2,3},{3,2},{4,5},{5,4},{6,7},{7,6},{8,9},{9,8},{10,11... | collective-permute-start | bytes 3145736 | tf_op jit(solution)/shard_map/ppermute | solution.py:22
  80.2 8.4 %collective-permute-start.18 = (bf16[32,8,512]{2,1,0:T(8,128)(2,1)S(1)}, bf16[32,8,512]{2,1,0:T(8,128)(2,1)S(1)}, u32[]{:S(2)}, u32[]{:S(2)}) collective-permute-start(bf16[32,8,512]{2,1,0:T(8,128)(2,1)S(1)} %get-tuple-element.39), channel_id=1, source_target_pairs={{0,4},{1,5},{2,6},{3,7},{4,0},{5,1},{6,2},{7,3},{8,12},{9,13},{10,... | collective-permute-start | bytes 786440 | tf_op jit(solution)/shard_map/ppermute | solution.py:22
  80.3 8.4 %collective-permute-start.19 = (bf16[32,8,512]{2,1,0:T(8,128)(2,1)S(1)}, bf16[32,8,512]{2,1,0:T(8,128)(2,1)S(1)}, u32[]{:S(2)}, u32[]{:S(2)}) collective-permute-start(bf16[32,8,512]{2,1,0:T(8,128)(2,1)S(1)} %get-tuple-element.41), channel_id=1, source_target_pairs={{0,2},{1,3},{2,0},{3,1},{4,6},{5,7},{6,4},{7,5},{8,10},{9,11},{10,... | collective-permute-start | bytes 786440 | tf_op jit(solution)/shard_map/ppermute | solution.py:22
  88.8 8.6 %collective-permute-start.20 = (bf16[16,8,512]{2,1,0:T(8,128)(2,1)S(1)}, bf16[16,8,512]{2,1,0:T(8,128)(2,1)S(1)}, u32[]{:S(2)}, u32[]{:S(2)}) collective-permute-start(bf16[16,8,512]{2,1,0:T(8,128)(2,1)S(1)} %get-tuple-element.43), channel_id=1, source_target_pairs={{0,8},{1,9},{2,10},{3,11},{4,12},{5,13},{6,14},{7,15},{8,0},{9,1},... | collective-permute-start | bytes 393224 | tf_op jit(solution)/shard_map/ppermute | solution.py:22
  91.4 6.1 %collective-permute-start.21 = (bf16[16,8,512]{2,1,0:T(8,128)(2,1)S(1)}, bf16[16,8,512]{2,1,0:T(8,128)(2,1)S(1)}, u32[]{:S(2)}, u32[]{:S(2)}) collective-permute-start(bf16[16,8,512]{2,1,0:T(8,128)(2,1)S(1)} %get-tuple-element.45), channel_id=1, source_target_pairs={{0,4},{1,5},{2,6},{3,7},{4,0},{5,1},{6,2},{7,3},{8,12},{9,13},{10,... | collective-permute-start | bytes 393224 | tf_op jit(solution)/shard_map/ppermute | solution.py:22
  97.6 4.3 %collective-permute-start.22 = (bf16[8,8,512]{2,1,0:T(8,128)(2,1)S(1)}, bf16[8,8,512]{2,1,0:T(8,128)(2,1)S(1)}, u32[]{:S(2)}, u32[]{:S(2)}) collective-permute-start(bf16[8,8,512]{2,1,0:T(8,128)(2,1)S(1)} %get-tuple-element.47), channel_id=1, source_target_pairs={{0,2},{1,3},{2,0},{3,1},{4,6},{5,7},{6,4},{7,5},{8,10},{9,11},{10,... | collective-permute-start | bytes 196616 | tf_op jit(solution)/shard_map/ppermute | solution.py:22
  98.1 5.9 %collective-permute-start.23 = (bf16[8,8,512]{2,1,0:T(8,128)(2,1)S(1)}, bf16[8,8,512]{2,1,0:T(8,128)(2,1)S(1)}, u32[]{:S(2)}, u32[]{:S(2)}) collective-permute-start(bf16[8,8,512]{2,1,0:T(8,128)(2,1)S(1)} %get-tuple-element.49), channel_id=1, source_target_pairs={{0,8},{1,9},{2,10},{3,11},{4,12},{5,13},{6,14},{7,15},{8,0},{9,1},... | collective-permute-start | bytes 196616 | tf_op jit(solution)/shard_map/ppermute | solution.py:22

commit v3 on v2

--- a/solution.py
+++ b/solution.py
@@ -26,16 +26,21 @@
     return math.prod(array.shape) * jnp.dtype(array.dtype).itemsize
 
 
-def near(array):
-    return pltpu.with_memory_space_constraint(array, pltpu.VMEM)
-
-
-def local(body, outs, *ins, name, scratch=0, scratches=(), specs=None, flops=0, far_out=False):
+def near(array, space):
+    return pltpu.with_memory_space_constraint(array, space)
+
+
+def local(body, outs, *ins, name, scratch=0, scratches=(), specs=None, flops=0, far_out=False, after=()):
     nbytes = sum(size_of(a) for a in (*ins, *outs))
-    specs = specs or [whole()] * len(ins)
-    ins = [near(a) if s.memory_space == pltpu.VMEM else a for a, s in zip(ins, specs)]
+    specs = list(specs or [whole()] * len(ins)) + [whole()] * len(after)
+    own = len(ins)
+    ins = [a if s.memory_space == pltpu.SMEM else near(a, s.memory_space) for a, s in zip((*ins, *after), specs)]
+
+    def run(*refs):
+        body(*refs[:own], *refs[len(ins) :])
+
     return pl.pallas_call(
-        body,
+        run,
         out_shape=[a if far_out else pltpu.VMEM(a.shape, a.dtype) for a in outs],
         in_specs=specs,
         out_specs=[whole()] * len(outs),
@@ -50,7 +55,38 @@
     return jax.ShapeDtypeStruct(tuple(dims), dtype)
 
 
-def scale_body(contrast, level, label, probes, first, second, scaling):
+def load_body(source, out, sems):
+    copies = []
+    for i in range(sems.shape[0]):
+        n = source.shape[0] // sems.shape[0]
+        rows = pl.ds(i * n, n)
+        copies.append(pltpu.make_async_copy(source.at[rows], out.at[rows], sems.at[i]))
+    for copy in copies:
+        copy.start()
+    for copy in copies:
+        copy.wait()
+
+
+def load(array, after, name):
+    return local(
+        load_body,
+        [shape(array.shape, array.dtype)],
+        array,
+        name=name,
+        specs=[whole(pltpu.HBM)],
+        scratches=[pltpu.SemaphoreType.DMA((8,))],
+        after=after,
+    )[0]
+
+
+def scale_body(contrast, *refs):
+    far, (first, second, scaling), near_refs, sems = refs[:3], refs[3:6], refs[6:9], refs[9]
+    copies = [pltpu.make_async_copy(a, b, sems.at[i]) for i, (a, b) in enumerate(zip(far, near_refs))]
+    for copy in copies:
+        copy.start()
+    for copy in copies:
+        copy.wait()
+    level, label, probes = near_refs
     value = level[...]
     unit = label[...]
     factor = jnp.zeros_like(value)
@@ -87,13 +123,27 @@
         out[a.shape[0] :] = b[...]
 
 
-def join(*pairs):
+def join(*pairs, after=()):
     outs = [shape((2 * a.shape[0],) + a.shape[1:], a.dtype) for a, _ in pairs]
-    return local(join_body, outs, *[x for pair in pairs for x in pair], name="join")
-
-
-def fold(*pairs):
-    per = 4 // len(pairs)
+    return local(join_body, outs, *[x for pair in pairs for x in pair], name="join", after=after)
+
+
+def plus(total, got, weight=None):
+    outs = [shape(total.shape, BF16)] if weight is not None else [shape(total.shape, F32), shape(total.shape, BF16)]
+    ins = (total, got) if weight is None else (total, got, weight)
+
+    def body(*refs):
+        done = refs[0][...] + refs[1][...].astype(F32)
+        if weight is not None:
+            done = done * refs[2][...]
+        for out in refs[len(ins) :]:
+            out[...] = done.astype(out.dtype)
+
+    return local(body, outs, *ins, name="plus")
+
+
+def fold(*pairs, parts=4):
+    per = parts // len(pairs)
     outs = []
     for keep, _ in pairs:
         dims = (keep.shape[0] // per,) + keep.shape[1:]
@@ -101,7 +151,7 @@
 
     def body(*refs):
         done = refs[2 * len(pairs) :]
-        for i in range(4):
+        for i in range(parts):
             keep, recv = refs[2 * (i // per)], refs[2 * (i // per) + 1]
             n = done[i].shape[0]
             at = slice((i % per) * n, (i % per + 1) * n)
@@ -208,6 +258,28 @@
     split_bits = [1 << k for k in range(peers.bit_length() - 3)]
     join_bits = [peers // 4, peers // 2]
 
+    half_dims = (half_blocks, probe_count, cell_width)
+    lanes = (cell_total // 128, 128)
+    part_p, part_q, scaling = local(
+        scale_body,
+        [shape(half_dims, BF16), shape(half_dims, BF16), shape(lanes, F32)],
+        contrast,
+        level_set.reshape(lanes),
+        unit_label.reshape(lanes),
+        probes,
+        name="scale",
+        specs=[whole(pltpu.SMEM)] + [whole(pltpu.HBM)] * 3,
+        scratches=[
+            pltpu.VMEM(lanes, F32),
+            pltpu.VMEM(lanes, jnp.int32),
+            pltpu.VMEM(probes.shape, F32),
+            pltpu.SemaphoreType.DMA((3,)),
+        ],
+    )
+    scaling, station_weight, col_owner, col_local, row_owner, row_local, tile_rank = lax.optimization_barrier(
+        (scaling, station_weight, col_owner, col_local, row_owner, row_local, tile_rank)
+    )
+
     start = me * tile_count
 
     def mine_of(table):
@@ -234,43 +306,38 @@
         station_weight.reshape(4, peers // 4, station_blocks, station_width), me % (peers // 4), 1, 1
     ).reshape(4 * station_blocks, 1, station_width)
 
-    half_dims = (half_blocks, probe_count, cell_width)
-    lanes = (cell_total // 128, 128)
-    part_p, part_q, scaling = local(
-        scale_body,
-        [shape(half_dims, BF16), shape(half_dims, BF16), shape(lanes, F32)],
-        contrast,
-        level_set.reshape(lanes),
-        unit_label.reshape(lanes),
-        probes,
-        name="scale",
-        specs=[whole(pltpu.SMEM)] + [whole()] * 3,
-    )
     for step in range(len(order_p)):
         got_p = swap(part_p, order_p[step])
         got_q = swap(part_q, order_q[step])
         if step < len(order_p) - 1:
-            part_p, part_q = join((part_p, got_p), (part_q, got_q))
+            after = ()
+            if step == 0:
+                after = (cell_at, row_at, keep, weight)
+            if step == 1:
+                v_here = load(v_factor, (part_p, part_q), "load_v")
+                u_here = load(u_factor, (part_p, part_q, v_here), "load_u")
+                after = (u_here,)
+            part_p, part_q = join((part_p, got_p), (part_q, got_q), after=after)
     pieces = [part_p, got_p, part_q, got_q]
     pieces = pieces + [swap(piece, 1) for piece in pieces]
 
     total, send = tiles(
-        pieces, cell_at, row_at, keep, v_factor, u_factor, peers * station_blocks, F32, "forward"
-    )
-    total = total + swap(send, split_bits[0])
+        pieces, cell_at, row_at, keep, v_here, u_here, peers * station_blocks, F32, "forward"
+    )
+    got = swap(send, split_bits[0])
     for bit in split_bits[1:]:
-        half = total.shape[0] // 2
-        got = swap(total[half:].astype(BF16), bit)
-        total = total[:half] + got.astype(F32)
+        total, send = fold((total, got), parts=2)
+        got = swap(send, bit)
     for bit in join_bits:
-        total = total + swap(total.astype(BF16), bit).astype(F32)
-    weighted = (total * weight).astype(BF16)
+        total, send = plus(total, got)
+        got = swap(send, bit)
+    weighted = plus(total, got, weight)[0]
     pieces = [weighted]
     for bit in split_bits[::-1]:
         pieces = pieces + [swap(piece, bit) for piece in pieces]
 
     keep_all, send_all = tiles(
-        pieces, row_at, cell_at, keep, u_factor, v_factor, peers * cell_blocks, BF16, "adjoint"
+        pieces, row_at, cell_at, keep, u_here, v_here, peers * cell_blocks, BF16, "adjoint"
     )
     got_all = swap(send_all, 1)
     pairs = [(keep_all, got_all)]

time: 105 us -> 93.8 us (0.89)
  local copies, waits for them, and re-layouts: 13.1 us -> 2.77 us
  waiting for transfers between devices: 54.7 us -> 48.3 us
  Pallas kernels: 13.1 us -> 18.7 us
    unnamed x18 -> x2, local copies, waits for them, and re-layouts: 11.9 us -> 0.65 us
    ppermute x24, waiting for transfers between devices: 54.7 us -> 48.3 us  [swap(): return lax.ppermute(array, 'tile', [(i, i ^ bit) for i in range(count)])]
    pallas_call x9 -> x15, Pallas kernels: 13.1 us -> 18.7 us  [local(): pl.pallas_call(run, out_shape=[a if far_out else pltpu.VMEM(a.shape, a.dt...]
  transfers between devices with their start and end apart: 24 -> 24, of which waited for: 18 -> 17; matrix products, arithmetic and copies ran while one was open for 2% -> 3% of each run, Pallas kernels for 0% -> 5%
where the time goes in v3:
time: 93.8 us; the launch traced here: 93.6 us
  waiting for transfers between devices  48.3 us (51%)
  starting transfers between devices  22.8 us (24%)
  Pallas kernels  18.7 us (20%)
  local copies, waits for them, and re-layouts  2.77 us (3%)
    ppermute x24, waiting for transfers between devices, swap(): return lax.ppermute(array, 'tile', [(i, i ^ bit) for i in range(count)])  48.3 us
    ppermute x24, starting transfers between devices, swap(): return lax.ppermute(array, 'tile', [(i, i ^ bit) for i in range(count)])  22.8 us
    pallas_call x15, Pallas kernels, local(): pl.pallas_call(run, out_shape=[a if far_out else pltpu.VMEM(a.shape, a.dt...  18.7 us
  transfers between devices with their start and end apart: 24, of which 17 were waited for; matrix products, arithmetic and copies ran while one was open for 3% of the time, Pallas kernels for 5%

profile of v3, /device:TPU:0, one launch (start us, length us, event | category | flops | bytes accessed | tf_op | source)
XLA Modules:
  0.0 93.6 jit_solution(17728617301615751277)
XLA Ops:
  0.0 0.7 copy-done
  0.7 1.6 %scale.1 = (bf16[8,8,512]{2,1,0:T(8,128)(2,1)S(1)}, bf16[8,8,512]{2,1,0:T(8,128)(2,1)S(1)}, f32[64,128]{1,0:T(8,128)S(1)}) custom-call(f32[4]{0:T(128)S(1)} %copy-done, f32[64,128]{1,0:T(8,128)} %bitcast.14, s32[64,128]{1,0:T(8,128)} %bitcast.15, f32[8,8192]{1,0:T(8,128)} %refs_3_.1), custom_call_target="tpu_custom_call" | custom-call | bytes 491536 | tf_op jit(solution)/shard_map/scale/pallas_call | solution.py:42
  2.3 3.0 %collective-permute-start = (bf16[8,8,512]{2,1,0:T(8,128)(2,1)S(1)}, bf16[8,8,512]{2,1,0:T(8,128)(2,1)S(1)}, u32[]{:S(2)}, u32[]{:S(2)}) collective-permute-start(bf16[8,8,512]{2,1,0:T(8,128)(2,1)S(1)} %get-tuple-element.47.refs_0_), channel_id=1, source_target_pairs={{0,2},{1,3},{2,0},{3,1},{4,6},{5,7},{6,4},{7,5},{8,10},{9,11},{10,... | collective-permute-start | bytes 196616 | tf_op jit(solution)/shard_map/ppermute | solution.py:22
  5.3 2.6 %collective-permute-start.1 = (bf16[8,8,512]{2,1,0:T(8,128)(2,1)S(1)}, bf16[8,8,512]{2,1,0:T(8,128)(2,1)S(1)}, u32[]{:S(2)}, u32[]{:S(2)}) collective-permute-start(bf16[8,8,512]{2,1,0:T(8,128)(2,1)S(1)} %get-tuple-element.48.refs_2_), channel_id=1, source_target_pairs={{0,8},{1,9},{2,10},{3,11},{4,12},{5,13},{6,14},{7,15},{8,0},{9,1},... | collective-permute-start | bytes 196616 | tf_op jit(solution)/shard_map/ppermute | solution.py:22
  8.0 0.8 dynamic_slice.25
  8.7 0.1 lt.42
  8.9 0.1 lt.44
  9.0 0.9 %reshape.60 = f32[4,4,4,512]{3,2,1,0:T(4,128)S(1)} reshape(f32[32768]{0:T(1024)} %param.16) | data formatting | bytes 262144 | tf_op jit(solution)/shard_map/reshape | solution.py:306
  10.0 0.8 fusion.5
  10.9 2.3 %collective-permute-start.2 = (bf16[16,8,512]{2,1,0:T(8,128)(2,1)S(1)}, bf16[16,8,512]{2,1,0:T(8,128)(2,1)S(1)}, u32[]{:S(2)}, u32[]{:S(2)}) collective-permute-start(bf16[16,8,512]{2,1,0:T(8,128)(2,1)S(1)} %get-tuple-element.50.refs_1_.refs_0_), channel_id=1, source_target_pairs={{0,8},{1,9},{2,10},{3,11},{4,12},{5,13},{6,14},{7,15},{8,0},{9,1},... | collective-permute-start | bytes 393224 | tf_op jit(solution)/shard_map/ppermute | solution.py:22
  13.2 2.1 %collective-permute-start.3 = (bf16[16,8,512]{2,1,0:T(8,128)(2,1)S(1)}, bf16[16,8,512]{2,1,0:T(8,128)(2,1)S(1)}, u32[]{:S(2)}, u32[]{:S(2)}) collective-permute-start(bf16[16,8,512]{2,1,0:T(8,128)(2,1)S(1)} %get-tuple-element.51.refs_2_), channel_id=1, source_target_pairs={{0,4},{1,5},{2,6},{3,7},{4,0},{5,1},{6,2},{7,3},{8,12},{9,13},{10,... | collective-permute-start | bytes 393224 | tf_op jit(solution)/shard_map/ppermute | solution.py:22
  15.3 2.2 %load_v.1.refs_3_.refs_11_.refs_8_ = bf16[128,32,512]{2,1,0:T(8,128)(2,1)S(1)} custom-call(bf16[128,32,512]{2,1,0:T(8,128)(2,1)} %refs_0_.4, bf16[16,8,512]{2,1,0:T(8,128)(2,1)S(1)} %get-tuple-element.50.refs_1_.refs_0_, bf16[16,8,512]{2,1,0:T(8,128)(2,1)S(1)} %get-tuple-element.51.refs_2_), custom_call_target="tpu_custom_call" | custom-call | bytes 8388608 | tf_op jit(solution)/shard_map/load_v/pallas_call | solution.py:42
  17.5 2.2 %load_u.1.refs_4_.refs_12_.refs_7_ = bf16[128,32,512]{2,1,0:T(8,128)(2,1)S(1)} custom-call(bf16[128,32,512]{2,1,0:T(8,128)(2,1)} %refs_0_.5, bf16[16,8,512]{2,1,0:T(8,128)(2,1)S(1)} %get-tuple-element.50.refs_1_.refs_0_, bf16[16,8,512]{2,1,0:T(8,128)(2,1)S(1)} %get-tuple-element.51.refs_2_, bf16[128,32,512]{2,1,0:T(8,128)(2,1)S(1)} %load_v.1.refs_3_.refs_11_.refs_8_), custom_call_target="tpu_custom_call" | custom-call | bytes 8388608 | tf_op jit(solution)/shard_map/load_u/pallas_call | solution.py:42
  19.8 0.6 collective-permute-start.4
  20.4 0.5 collective-permute-start.5
  20.9 0.5 collective-permute-start.8
  21.4 4.9 %collective-permute-done.4.refs_4_ = bf16[32,8,512]{2,1,0:T(8,128)(2,1)S(1)} collective-permute-done((bf16[32,8,512]{2,1,0:T(8,128)(2,1)S(1)}, bf16[32,8,512]{2,1,0:T(8,128)(2,1)S(1)}, u32[]{:S(2)}, u32[]{:S(2)}) %collective-permute-start.4) | collective-permute-done | bytes 262176 | tf_op jit(solution)/shard_map/ppermute | solution.py:22
  26.3 0.5 collective-permute-done.5.refs_6_
  26.8 1.0 %collective-permute-done.7.refs_8_ = bf16[32,8,512]{2,1,0:T(8,128)(2,1)S(1)} collective-permute-done((bf16[32,8,512]{2,1,0:T(8,128)(2,1)S(1)}, bf16[32,8,512]{2,1,0:T(8,128)(2,1)S(1)}, u32[]{:S(2)}, u32[]{:S(2)}) %collective-permute-start.7) | collective-permute-done | bytes 262176 | tf_op jit(solution)/shard_map/ppermute | solution.py:22
  27.8 0.5 collective-permute-done.9.refs_10_
  28.3 5.5 %forward.1 = (f32[32,8,512]{2,1,0:T(8,128)S(1)}, f32[32,8,512]{2,1,0:T(8,128)S(1)}) custom-call(s32[128]{0:T(128)S(1)} %get-tuple-element.77.refs_4_.refs_0_.refs_1_, s32[128]{0:T(128)S(1)} %get-tuple-element.78.refs_5_.refs_1_.refs_0_, f32[16,256]{1,0:T(8,128)S(1)} %compare_convert_fusion.refs_6_.refs_2_, ...), custom_call_target="tpu_custom_call" | custom-call | flops 536870912 | bytes 11551744 | tf_op jit(solution)/shard_map/forward/pallas_call | solution.py:42
  33.8 0.2 collective-permute-start.10
  34.0 1.8 %collective-permute-done.10.refs_1_ = f32[32,8,512]{2,1,0:T(8,128)S(1)} collective-permute-done((f32[32,8,512]{2,1,0:T(8,128)S(1)}, f32[32,8,512]{2,1,0:T(8,128)S(1)}, u32[]{:S(2)}, u32[]{:S(2)}) %collective-permute-start.10) | collective-permute-done | bytes 524320 | tf_op jit(solution)/shard_map/ppermute | solution.py:22
  35.9 0.6 collective-permute-start.11
  36.5 5.0 %collective-permute-done.11.refs_1_ = bf16[16,8,512]{2,1,0:T(8,128)(2,1)S(1)} collective-permute-done((bf16[16,8,512]{2,1,0:T(8,128)(2,1)S(1)}, bf16[16,8,512]{2,1,0:T(8,128)(2,1)S(1)}, u32[]{:S(2)}, u32[]{:S(2)}) %collective-permute-start.11) | collective-permute-done | bytes 131104 | tf_op jit(solution)/shard_map/ppermute | solution.py:22
  41.5 1.6 %collective-permute-start.12 = (bf16[16,8,512]{2,1,0:T(8,128)(2,1)S(1)}, bf16[16,8,512]{2,1,0:T(8,128)(2,1)S(1)}, u32[]{:S(2)}, u32[]{:S(2)}) collective-permute-start(bf16[16,8,512]{2,1,0:T(8,128)(2,1)S(1)} %get-tuple-element.59), channel_id=1, source_target_pairs={{0,4},{1,5},{2,6},{3,7},{4,0},{5,1},{6,2},{7,3},{8,12},{9,13},{10,... | collective-permute-start | bytes 393224 | tf_op jit(solution)/shard_map/ppermute | solution.py:22
  43.1 3.4 %collective-permute-done.12.refs_1_ = bf16[16,8,512]{2,1,0:T(8,128)(2,1)S(1)} collective-permute-done((bf16[16,8,512]{2,1,0:T(8,128)(2,1)S(1)}, bf16[16,8,512]{2,1,0:T(8,128)(2,1)S(1)}, u32[]{:S(2)}, u32[]{:S(2)}) %collective-permute-start.12) | collective-permute-done | bytes 131104 | tf_op jit(solution)/shard_map/ppermute | solution.py:22
  46.6 2.5 %collective-permute-start.13 = (bf16[16,8,512]{2,1,0:T(8,128)(2,1)S(1)}, bf16[16,8,512]{2,1,0:T(8,128)(2,1)S(1)}, u32[]{:S(2)}, u32[]{:S(2)}) collective-permute-start(bf16[16,8,512]{2,1,0:T(8,128)(2,1)S(1)} %get-tuple-element.61), channel_id=1, source_target_pairs={{0,8},{1,9},{2,10},{3,11},{4,12},{5,13},{6,14},{7,15},{8,0},{9,1},... | collective-permute-start | bytes 393224 | tf_op jit(solution)/shard_map/ppermute | solution.py:22
  49.1 4.9 %collective-permute-done.13.refs_1_ = bf16[16,8,512]{2,1,0:T(8,128)(2,1)S(1)} collective-permute-done((bf16[16,8,512]{2,1,0:T(8,128)(2,1)S(1)}, bf16[16,8,512]{2,1,0:T(8,128)(2,1)S(1)}, u32[]{:S(2)}, u32[]{:S(2)}) %collective-permute-start.13) | collective-permute-done | bytes 131104 | tf_op jit(solution)/shard_map/ppermute | solution.py:22
  54.0 0.6 collective-permute-start.14
  54.6 4.4 %collective-permute-done.14.refs_4_ = bf16[16,8,512]{2,1,0:T(8,128)(2,1)S(1)} collective-permute-done((bf16[16,8,512]{2,1,0:T(8,128)(2,1)S(1)}, bf16[16,8,512]{2,1,0:T(8,128)(2,1)S(1)}, u32[]{:S(2)}, u32[]{:S(2)}) %collective-permute-start.14) | collective-permute-done | bytes 131104 | tf_op jit(solution)/shard_map/ppermute | solution.py:22
  59.0 1.3 %collective-permute-done.16.refs_6_ = bf16[16,8,512]{2,1,0:T(8,128)(2,1)S(1)} collective-permute-done((bf16[16,8,512]{2,1,0:T(8,128)(2,1)S(1)}, bf16[16,8,512]{2,1,0:T(8,128)(2,1)S(1)}, u32[]{:S(2)}, u32[]{:S(2)}) %collective-permute-start.16) | collective-permute-done | bytes 131104 | tf_op jit(solution)/shard_map/ppermute | solution.py:22
  60.4 5.8 %adjoint.1 = (f32[128,8,512]{2,1,0:T(8,128)S(1)}, bf16[128,8,512]{2,1,0:T(8,128)(2,1)S(1)}) custom-call(s32[128]{0:T(128)S(1)} %get-tuple-element.78.refs_5_.refs_1_.refs_0_, s32[128]{0:T(128)S(1)} %get-tuple-element.77.refs_4_.refs_0_.refs_1_, f32[16,256]{1,0:T(8,128)S(1)} %compare_convert_fusion.refs_6_.refs_2_, bf16[16,8,512]{2,1,0:T(8,128)(2,1)S(1)} %plus.5.refs_3_, ...), custom_call_target="tpu_custom_call" | custom-call | flops 536870912 | bytes 12076032 | tf_op jit(solution)/shard_map/adjoint/pallas_call | solution.py:42
  66.2 0.2 collective-permute-start.17
  66.4 2.5 %collective-permute-done.17.refs_1_ = bf16[128,8,512]{2,1,0:T(8,128)(2,1)S(1)} collective-permute-done((bf16[128,8,512]{2,1,0:T(8,128)(2,1)S(1)}, bf16[128,8,512]{2,1,0:T(8,128)(2,1)S(1)}, u32[]{:S(2)}, u32[]{:S(2)}) %collective-permute-start.17) | collective-permute-done | bytes 1048608 | tf_op jit(solution)/shard_map/ppermute | solution.py:22
  68.9 0.2 fold.5
  69.1 0.3 collective-permute-start.18
  69.4 0.5 collective-permute-start.19
  69.9 7.6 %collective-permute-done.18.refs_1_ = bf16[32,8,512]{2,1,0:T(8,128)(2,1)S(1)} collective-permute-done((bf16[32,8,512]{2,1,0:T(8,128)(2,1)S(1)}, bf16[32,8,512]{2,1,0:T(8,128)(2,1)S(1)}, u32[]{:S(2)}, u32[]{:S(2)}) %collective-permute-start.18) | collective-permute-done | bytes 262176 | tf_op jit(solution)/shard_map/ppermute | solution.py:22
  77.6 0.1 fold.6
  77.7 2.5 %collective-permute-start.20 = (bf16[16,8,512]{2,1,0:T(8,128)(2,1)S(1)}, bf16[16,8,512]{2,1,0:T(8,128)(2,1)S(1)}, u32[]{:S(2)}, u32[]{:S(2)}) collective-permute-start(bf16[16,8,512]{2,1,0:T(8,128)(2,1)S(1)} %get-tuple-element.69), channel_id=1, source_target_pairs={{0,8},{1,9},{2,10},{3,11},{4,12},{5,13},{6,14},{7,15},{8,0},{9,1},... | collective-permute-start | bytes 393224 | tf_op jit(solution)/shard_map/ppermute | solution.py:22
  80.2 0.4 collective-permute-start.21
  80.6 5.7 %collective-permute-done.20.refs_1_ = bf16[16,8,512]{2,1,0:T(8,128)(2,1)S(1)} collective-permute-done((bf16[16,8,512]{2,1,0:T(8,128)(2,1)S(1)}, bf16[16,8,512]{2,1,0:T(8,128)(2,1)S(1)}, u32[]{:S(2)}, u32[]{:S(2)}) %collective-permute-start.20) | collective-permute-done | bytes 131104 | tf_op jit(solution)/shard_map/ppermute | solution.py:22
  86.4 0.6 collective-permute-start.22
  86.9 1.3 %collective-permute-start.23 = (bf16[8,8,512]{2,1,0:T(8,128)(2,1)S(1)}, bf16[8,8,512]{2,1,0:T(8,128)(2,1)S(1)}, u32[]{:S(2)}, u32[]{:S(2)}) collective-permute-start(bf16[8,8,512]{2,1,0:T(8,128)(2,1)S(1)} %get-tuple-element.75), channel_id=1, source_target_pairs={{0,8},{1,9},{2,10},{3,11},{4,12},{5,13},{6,14},{7,15},{8,0},{9,1},... | collective-permute-start | bytes 196616 | tf_op jit(solution)/shard_map/ppermute | solution.py:22
  88.2 2.4 %collective-permute-done.22.refs_1_ = bf16[8,8,512]{2,1,0:T(8,128)(2,1)S(1)} collective-permute-done((bf16[8,8,512]{2,1,0:T(8,128)(2,1)S(1)}, bf16[8,8,512]{2,1,0:T(8,128)(2,1)S(1)}, u32[]{:S(2)}, u32[]{:S(2)}) %collective-permute-start.22) | collective-permute-done | bytes 65568 | tf_op jit(solution)/shard_map/ppermute | solution.py:22
  90.7 2.1 %collective-permute-done.23.refs_3_ = bf16[8,8,512]{2,1,0:T(8,128)(2,1)S(1)} collective-permute-done((bf16[8,8,512]{2,1,0:T(8,128)(2,1)S(1)}, bf16[8,8,512]{2,1,0:T(8,128)(2,1)S(1)}, u32[]{:S(2)}, u32[]{:S(2)}) %collective-permute-start.23) | collective-permute-done | bytes 65568 | tf_op jit(solution)/shard_map/ppermute | solution.py:22
  92.8 0.7 final.1
  (28 shorter events, 0.7 us)
Async XLA Ops:
  0.0 0.7 copy-start
  2.3 8.6 %collective-permute-start = (bf16[8,8,512]{2,1,0:T(8,128)(2,1)S(1)}, bf16[8,8,512]{2,1,0:T(8,128)(2,1)S(1)}, u32[]{:S(2)}, u32[]{:S(2)}) collective-permute-start(bf16[8,8,512]{2,1,0:T(8,128)(2,1)S(1)} %get-tuple-element.47.refs_0_), channel_id=1, source_target_pairs={{0,2},{1,3},{2,0},{3,1},{4,6},{5,7},{6,4},{7,5},{8,10},{9,11},{10,... | collective-permute-start | bytes 196616 | tf_op jit(solution)/shard_map/ppermute | solution.py:22
  5.3 5.6 %collective-permute-start.1 = (bf16[8,8,512]{2,1,0:T(8,128)(2,1)S(1)}, bf16[8,8,512]{2,1,0:T(8,128)(2,1)S(1)}, u32[]{:S(2)}, u32[]{:S(2)}) collective-permute-start(bf16[8,8,512]{2,1,0:T(8,128)(2,1)S(1)} %get-tuple-element.48.refs_2_), channel_id=1, source_target_pairs={{0,8},{1,9},{2,10},{3,11},{4,12},{5,13},{6,14},{7,15},{8,0},{9,1},... | collective-permute-start | bytes 196616 | tf_op jit(solution)/shard_map/ppermute | solution.py:22
  10.9 8.9 %collective-permute-start.2 = (bf16[16,8,512]{2,1,0:T(8,128)(2,1)S(1)}, bf16[16,8,512]{2,1,0:T(8,128)(2,1)S(1)}, u32[]{:S(2)}, u32[]{:S(2)}) collective-permute-start(bf16[16,8,512]{2,1,0:T(8,128)(2,1)S(1)} %get-tuple-element.50.refs_1_.refs_0_), channel_id=1, source_target_pairs={{0,8},{1,9},{2,10},{3,11},{4,12},{5,13},{6,14},{7,15},{8,0},{9,1},... | collective-permute-start | bytes 393224 | tf_op jit(solution)/shard_map/ppermute | solution.py:22
  13.2 6.6 %collective-permute-start.3 = (bf16[16,8,512]{2,1,0:T(8,128)(2,1)S(1)}, bf16[16,8,512]{2,1,0:T(8,128)(2,1)S(1)}, u32[]{:S(2)}, u32[]{:S(2)}) collective-permute-start(bf16[16,8,512]{2,1,0:T(8,128)(2,1)S(1)} %get-tuple-element.51.refs_2_), channel_id=1, source_target_pairs={{0,4},{1,5},{2,6},{3,7},{4,0},{5,1},{6,2},{7,3},{8,12},{9,13},{10,... | collective-permute-start | bytes 393224 | tf_op jit(solution)/shard_map/ppermute | solution.py:22
  19.8 6.4 %collective-permute-start.4 = (bf16[32,8,512]{2,1,0:T(8,128)(2,1)S(1)}, bf16[32,8,512]{2,1,0:T(8,128)(2,1)S(1)}, u32[]{:S(2)}, u32[]{:S(2)}) collective-permute-start(bf16[32,8,512]{2,1,0:T(8,128)(2,1)S(1)} %get-tuple-element.52.refs_3_), channel_id=1, source_target_pairs={{0,4},{1,5},{2,6},{3,7},{4,0},{5,1},{6,2},{7,3},{8,12},{9,13},{10,... | collective-permute-start | bytes 786440 | tf_op jit(solution)/shard_map/ppermute | solution.py:22
  20.4 6.4 %collective-permute-start.5 = (bf16[32,8,512]{2,1,0:T(8,128)(2,1)S(1)}, bf16[32,8,512]{2,1,0:T(8,128)(2,1)S(1)}, u32[]{:S(2)}, u32[]{:S(2)}) collective-permute-start(bf16[32,8,512]{2,1,0:T(8,128)(2,1)S(1)} %get-tuple-element.53.refs_5_), channel_id=1, source_target_pairs={{0,2},{1,3},{2,0},{3,1},{4,6},{5,7},{6,4},{7,5},{8,10},{9,11},{10,... | collective-permute-start | bytes 786440 | tf_op jit(solution)/shard_map/ppermute | solution.py:22
  20.9 5.9 %collective-permute-start.6 = (bf16[32,8,512]{2,1,0:T(8,128)(2,1)S(1)}, bf16[32,8,512]{2,1,0:T(8,128)(2,1)S(1)}, u32[]{:S(2)}, u32[]{:S(2)}) collective-permute-start(bf16[32,8,512]{2,1,0:T(8,128)(2,1)S(1)} %get-tuple-element.52.refs_3_), channel_id=1, source_target_pairs={{0,1},{1,0},{2,3},{3,2},{4,5},{5,4},{6,7},{7,6},{8,9},{9,8},{10,11... | collective-permute-start | bytes 786440 | tf_op jit(solution)/shard_map/ppermute | solution.py:22
  20.9 5.9 %collective-permute-start.8 = (bf16[32,8,512]{2,1,0:T(8,128)(2,1)S(1)}, bf16[32,8,512]{2,1,0:T(8,128)(2,1)S(1)}, u32[]{:S(2)}, u32[]{:S(2)}) collective-permute-start(bf16[32,8,512]{2,1,0:T(8,128)(2,1)S(1)} %get-tuple-element.53.refs_5_), channel_id=1, source_target_pairs={{0,1},{1,0},{2,3},{3,2},{4,5},{5,4},{6,7},{7,6},{8,9},{9,8},{10,11... | collective-permute-start | bytes 786440 | tf_op jit(solution)/shard_map/ppermute | solution.py:22
  26.3 1.5 %collective-permute-start.7 = (bf16[32,8,512]{2,1,0:T(8,128)(2,1)S(1)}, bf16[32,8,512]{2,1,0:T(8,128)(2,1)S(1)}, u32[]{:S(2)}, u32[]{:S(2)}) collective-permute-start(bf16[32,8,512]{2,1,0:T(8,128)(2,1)S(1)} %collective-permute-done.4.refs_4_), channel_id=1, source_target_pairs={{0,1},{1,0},{2,3},{3,2},{4,5},{5,4},{6,7},{7,6},{8,9},{9,8},{10,11... | collective-permute-start | bytes 786440 | tf_op jit(solution)/shard_map/ppermute | solution.py:22
  26.7 1.5 %collective-permute-start.9 = (bf16[32,8,512]{2,1,0:T(8,128)(2,1)S(1)}, bf16[32,8,512]{2,1,0:T(8,128)(2,1)S(1)}, u32[]{:S(2)}, u32[]{:S(2)}) collective-permute-start(bf16[32,8,512]{2,1,0:T(8,128)(2,1)S(1)} %collective-permute-done.5.refs_6_), channel_id=1, source_target_pairs={{0,1},{1,0},{2,3},{3,2},{4,5},{5,4},{6,7},{7,6},{8,9},{9,8},{10,11... | collective-permute-start | bytes 786440 | tf_op jit(solution)/shard_map/ppermute | solution.py:22
  33.8 2.0 %collective-permute-start.10 = (f32[32,8,512]{2,1,0:T(8,128)S(1)}, f32[32,8,512]{2,1,0:T(8,128)S(1)}, u32[]{:S(2)}, u32[]{:S(2)}) collective-permute-start(f32[32,8,512]{2,1,0:T(8,128)S(1)} %get-tuple-element.55), channel_id=1, source_target_pairs={{0,1},{1,0},{2,3},{3,2},{4,5},{5,4},{6,7},{7,6},{8,9},{9,8},{10,11... | collective-permute-start | bytes 1572872 | tf_op jit(solution)/shard_map/ppermute | solution.py:22
  35.9 5.6 %collective-permute-start.11 = (bf16[16,8,512]{2,1,0:T(8,128)(2,1)S(1)}, bf16[16,8,512]{2,1,0:T(8,128)(2,1)S(1)}, u32[]{:S(2)}, u32[]{:S(2)}) collective-permute-start(bf16[16,8,512]{2,1,0:T(8,128)(2,1)S(1)} %get-tuple-element.57), channel_id=1, source_target_pairs={{0,2},{1,3},{2,0},{3,1},{4,6},{5,7},{6,4},{7,5},{8,10},{9,11},{10,... | collective-permute-start | bytes 393224 | tf_op jit(solution)/shard_map/ppermute | solution.py:22
  41.5 5.0 %collective-permute-start.12 = (bf16[16,8,512]{2,1,0:T(8,128)(2,1)S(1)}, bf16[16,8,512]{2,1,0:T(8,128)(2,1)S(1)}, u32[]{:S(2)}, u32[]{:S(2)}) collective-permute-start(bf16[16,8,512]{2,1,0:T(8,128)(2,1)S(1)} %get-tuple-element.59), channel_id=1, source_target_pairs={{0,4},{1,5},{2,6},{3,7},{4,0},{5,1},{6,2},{7,3},{8,12},{9,13},{10,... | collective-permute-start | bytes 393224 | tf_op jit(solution)/shard_map/ppermute | solution.py:22
  46.6 7.3 %collective-permute-start.13 = (bf16[16,8,512]{2,1,0:T(8,128)(2,1)S(1)}, bf16[16,8,512]{2,1,0:T(8,128)(2,1)S(1)}, u32[]{:S(2)}, u32[]{:S(2)}) collective-permute-start(bf16[16,8,512]{2,1,0:T(8,128)(2,1)S(1)} %get-tuple-element.61), channel_id=1, source_target_pairs={{0,8},{1,9},{2,10},{3,11},{4,12},{5,13},{6,14},{7,15},{8,0},{9,1},... | collective-permute-start | bytes 393224 | tf_op jit(solution)/shard_map/ppermute | solution.py:22
  54.0 5.0 %collective-permute-start.14 = (bf16[16,8,512]{2,1,0:T(8,128)(2,1)S(1)}, bf16[16,8,512]{2,1,0:T(8,128)(2,1)S(1)}, u32[]{:S(2)}, u32[]{:S(2)}) collective-permute-start(bf16[16,8,512]{2,1,0:T(8,128)(2,1)S(1)} %plus.5.refs_3_), channel_id=1, source_target_pairs={{0,2},{1,3},{2,0},{3,1},{4,6},{5,7},{6,4},{7,5},{8,10},{9,11},{10,... | collective-permute-start | bytes 393224 | tf_op jit(solution)/shard_map/ppermute | solution.py:22
  54.6 4.5 %collective-permute-start.15 = (bf16[16,8,512]{2,1,0:T(8,128)(2,1)S(1)}, bf16[16,8,512]{2,1,0:T(8,128)(2,1)S(1)}, u32[]{:S(2)}, u32[]{:S(2)}) collective-permute-start(bf16[16,8,512]{2,1,0:T(8,128)(2,1)S(1)} %plus.5.refs_3_), channel_id=1, source_target_pairs={{0,1},{1,0},{2,3},{3,2},{4,5},{5,4},{6,7},{7,6},{8,9},{9,8},{10,11... | collective-permute-start | bytes 393224 | tf_op jit(solution)/shard_map/ppermute | solution.py:22
  59.0 1.3 %collective-permute-start.16 = (bf16[16,8,512]{2,1,0:T(8,128)(2,1)S(1)}, bf16[16,8,512]{2,1,0:T(8,128)(2,1)S(1)}, u32[]{:S(2)}, u32[]{:S(2)}) collective-permute-start(bf16[16,8,512]{2,1,0:T(8,128)(2,1)S(1)} %collective-permute-done.14.refs_4_), channel_id=1, source_target_pairs={{0,1},{1,0},{2,3},{3,2},{4,5},{5,4},{6,7},{7,6},{8,9},{9,8},{10,11... | collective-permute-start | bytes 393224 | tf_op jit(solution)/shard_map/ppermute | solution.py:22
  66.2 2.7 %collective-permute-start.17 = (bf16[128,8,512]{2,1,0:T(8,128)(2,1)S(1)}, bf16[128,8,512]{2,1,0:T(8,128)(2,1)S(1)}, u32[]{:S(2)}, u32[]{:S(2)}) collective-permute-start(bf16[128,8,512]{2,1,0:T(8,128)(2,1)S(1)} %get-tuple-element.63), channel_id=1, source_target_pairs={{0,1},{1,0},{2,3},{3,2},{4,5},{5,4},{6,7},{7,6},{8,9},{9,8},{10,11... | collective-permute-start | bytes 3145736 | tf_op jit(solution)/shard_map/ppermute | solution.py:22
  69.1 8.4 %collective-permute-start.18 = (bf16[32,8,512]{2,1,0:T(8,128)(2,1)S(1)}, bf16[32,8,512]{2,1,0:T(8,128)(2,1)S(1)}, u32[]{:S(2)}, u32[]{:S(2)}) collective-permute-start(bf16[32,8,512]{2,1,0:T(8,128)(2,1)S(1)} %get-tuple-element.65), channel_id=1, source_target_pairs={{0,4},{1,5},{2,6},{3,7},{4,0},{5,1},{6,2},{7,3},{8,12},{9,13},{10,... | collective-permute-start | bytes 786440 | tf_op jit(solution)/shard_map/ppermute | solution.py:22
  69.4 8.2 %collective-permute-start.19 = (bf16[32,8,512]{2,1,0:T(8,128)(2,1)S(1)}, bf16[32,8,512]{2,1,0:T(8,128)(2,1)S(1)}, u32[]{:S(2)}, u32[]{:S(2)}) collective-permute-start(bf16[32,8,512]{2,1,0:T(8,128)(2,1)S(1)} %get-tuple-element.67), channel_id=1, source_target_pairs={{0,2},{1,3},{2,0},{3,1},{4,6},{5,7},{6,4},{7,5},{8,10},{9,11},{10,... | collective-permute-start | bytes 786440 | tf_op jit(solution)/shard_map/ppermute | solution.py:22
  77.7 8.5 %collective-permute-start.20 = (bf16[16,8,512]{2,1,0:T(8,128)(2,1)S(1)}, bf16[16,8,512]{2,1,0:T(8,128)(2,1)S(1)}, u32[]{:S(2)}, u32[]{:S(2)}) collective-permute-start(bf16[16,8,512]{2,1,0:T(8,128)(2,1)S(1)} %get-tuple-element.69), channel_id=1, source_target_pairs={{0,8},{1,9},{2,10},{3,11},{4,12},{5,13},{6,14},{7,15},{8,0},{9,1},... | collective-permute-start | bytes 393224 | tf_op jit(solution)/shard_map/ppermute | solution.py:22
  80.2 6.1 %collective-permute-start.21 = (bf16[16,8,512]{2,1,0:T(8,128)(2,1)S(1)}, bf16[16,8,512]{2,1,0:T(8,128)(2,1)S(1)}, u32[]{:S(2)}, u32[]{:S(2)}) collective-permute-start(bf16[16,8,512]{2,1,0:T(8,128)(2,1)S(1)} %get-tuple-element.71), channel_id=1, source_target_pairs={{0,4},{1,5},{2,6},{3,7},{4,0},{5,1},{6,2},{7,3},{8,12},{9,13},{10,... | collective-permute-start | bytes 393224 | tf_op jit(solution)/shard_map/ppermute | solution.py:22
  86.4 4.3 %collective-permute-start.22 = (bf16[8,8,512]{2,1,0:T(8,128)(2,1)S(1)}, bf16[8,8,512]{2,1,0:T(8,128)(2,1)S(1)}, u32[]{:S(2)}, u32[]{:S(2)}) collective-permute-start(bf16[8,8,512]{2,1,0:T(8,128)(2,1)S(1)} %get-tuple-element.73), channel_id=1, source_target_pairs={{0,2},{1,3},{2,0},{3,1},{4,6},{5,7},{6,4},{7,5},{8,10},{9,11},{10,... | collective-permute-start | bytes 196616 | tf_op jit(solution)/shard_map/ppermute | solution.py:22
  86.9 5.9 %collective-permute-start.23 = (bf16[8,8,512]{2,1,0:T(8,128)(2,1)S(1)}, bf16[8,8,512]{2,1,0:T(8,128)(2,1)S(1)}, u32[]{:S(2)}, u32[]{:S(2)}) collective-permute-start(bf16[8,8,512]{2,1,0:T(8,128)(2,1)S(1)} %get-tuple-element.75), channel_id=1, source_target_pairs={{0,8},{1,9},{2,10},{3,11},{4,12},{5,13},{6,14},{7,15},{8,0},{9,1},... | collective-permute-start | bytes 196616 | tf_op jit(solution)/shard_map/ppermute | solution.py:22

commit v4 on v2

v4 whole, which is shorter than its diff:
```python
import math

import jax
import jax.numpy as jnp
from jax import lax
from jax.experimental import pallas as pl
from jax.experimental.pallas import tpu as pltpu
from jax.sharding import PartitionSpec as P

BF16 = jnp.bfloat16
F32 = jnp.float32
I32 = jnp.int32
GROUP = 8
LANES = 128
MIB = 1024 * 1024


def whole(space=pltpu.VMEM):
    return pl.BlockSpec(memory_space=space)


def shape(dims, dtype):
    return jax.ShapeDtypeStruct(tuple(dims), dtype)


def size_of(array):
    return math.prod(array.shape) * jnp.dtype(array.dtype).itemsize


def swap(array, bits):
    count = lax.axis_size("tile")
    return lax.ppermute(array, "tile", [(i, i ^ bits[i & 1]) for i in range(count)])


def local(body, outs, *ins, name, scratch=0, scratches=(), specs=None, flops=0, far_out=False, after=()):
    nbytes = sum(size_of(a) for a in (*ins, *outs))
    specs = list(specs or [whole()] * len(ins)) + [whole()] * len(after)
    own = len(ins)
    ins = [pltpu.with_memory_space_constraint(a, s.memory_space) for a, s in zip((*ins, *after), specs)]

    def run(*refs):
        body(*refs[:own], *refs[len(ins) :])

    return pl.pallas_call(
        run,
        out_shape=[a if far_out else pltpu.VMEM(a.shape, a.dtype) for a in outs],
        in_specs=specs,
        out_specs=[whole()] * len(outs),
        scratch_shapes=list(scratches),
        compiler_params=pltpu.CompilerParams(vmem_limit_bytes=scratch + 8 * MIB),
        cost_estimate=pl.CostEstimate(flops=flops, bytes_accessed=nbytes, transcendentals=0),
        name=name,
    )(*ins)


def fetch(pairs, sems):
    copies = [pltpu.make_async_copy(a, b, sems.at[i]) for i, (a, b) in enumerate(pairs)]
    for copy in copies:
        copy.start()
    for copy in copies:
        copy.wait()


def load_body(source, out, sems):
    n = source.shape[0] // sems.shape[0]
    rows = [pl.ds(i * n, n) for i in range(sems.shape[0])]
    fetch([(source.at[r], out.at[r]) for r in rows], sems)


def load(array, after, name):
    return local(
        load_body,
        [shape(array.shape, array.dtype)],
        array,
        name=name,
        specs=[whole(pltpu.HBM)],
        scratches=[pltpu.SemaphoreType.DMA((8,))],
        after=after,
    )[0]


def scale_body(contrast, level, label, probes, part, scaling, contrast_near, level_near, label_near, probes_near, sems):
    fetch(
        [(contrast, contrast_near), (level, level_near), (label, label_near), (probes, probes_near)],
        sems,
    )
    value = level_near[...]
    unit = label_near[...]
    factor = jnp.zeros_like(value)
    for k in range(contrast.shape[0]):
        factor = jnp.where(unit == k, contrast_near[k], factor)
    scaling[...] = factor / (1.0 + value * value)
    blocks, _, width = part.shape
    rows = width // LANES
    for b in range(blocks):
        for c in range(rows):
            j = b * rows + c
            piece = probes_near[:, j * LANES : (j + 1) * LANES] * scaling[j : j + 1, :]
            part[b, :, c * LANES : (c + 1) * LANES] = piece.astype(BF16)


def final_body(keep, recv, scaling, out):
    blocks, _, width = keep.shape
    rows = width // LANES
    for b in range(blocks):
        for c in range(rows):
            j = b * rows + c
            lanes = slice(c * LANES, (c + 1) * LANES)
            total = keep[b, :, lanes] + recv[b, :, lanes].astype(F32)
            out[:, j * LANES : (j + 1) * LANES] = total * scaling[j : j + 1, :]


def join_body(first, second, out):
    n = first.shape[0]
    out[:n] = first[...]
    out[n:] = second[...]


def join(first, second, after=()):
    out = shape((2 * first.shape[0],) + first.shape[1:], first.dtype)
    return local(join_body, [out], first, second, name="join", after=after)[0]


def plus(total, got):
    def body(total, got, out, send):
        done = total[...] + got[...].astype(F32)
        out[...] = done
        send[...] = done.astype(BF16)

    return local(body, [shape(total.shape, F32), shape(total.shape, BF16)], total, got, name="plus")


def weigh(total, got, weight):
    def body(total, got, weight, out):
        blocks, _, width = out.shape
        rows = width // LANES
        for b in range(blocks):
            for c in range(rows):
                lanes = slice(c * LANES, (c + 1) * LANES)
                done = total[b, :, lanes] + got[b, :, lanes].astype(F32)
                j = b * rows + c
                out[b, :, lanes] = (done * weight[j : j + 1, :]).astype(BF16)

    return local(body, [shape(total.shape, BF16)], total, got, weight, name="weigh")[0]


def fold(keep, recv):
    half = keep.shape[0] // 2
    dims = (half,) + keep.shape[1:]

    def body(keep, recv, mine, send):
        mine[...] = keep[:half] + recv[:half].astype(F32)
        send[...] = (keep[half:] + recv[half:].astype(F32)).astype(BF16)

    return local(body, [shape(dims, F32), shape(dims, BF16)], keep, recv, name="fold")


def tiles_body(piece_count, src_row, dst_row, table_near, *refs):
    pieces = refs[:piece_count]
    first, second, mine, send, at, table, acc, sem = refs[piece_count:]
    count, rank, width = first.shape
    groups = count // GROUP
    copy = pltpu.make_async_copy(table_near, at, sem)
    copy.start()
    acc[...] = jnp.zeros_like(acc)
    per = pieces[0].shape[0]
    for i, piece in enumerate(pieces):
        table[i * per : (i + 1) * per] = piece[...]
    probes = table.shape[1]
    span = GROUP * rank
    row_tile = lax.broadcasted_iota(I32, (GROUP * probes, span), 0) // probes
    col_tile = lax.broadcasted_iota(I32, (GROUP * probes, span), 1) // rank
    component = lax.broadcasted_iota(I32, (GROUP * probes, span), 1) % rank
    own = jnp.where(row_tile == col_tile, component, rank)
    lane_tile = lax.broadcasted_iota(I32, (1, span), 1) // rank
    copy.wait()
    for g in range(groups):
        taken = jnp.concatenate(
            [table[at[src_row, g * GROUP + i]].astype(F32) for i in range(GROUP)], axis=0
        ).astype(BF16)
        left = first[g * GROUP : (g + 1) * GROUP].reshape(span, width)
        right = second[g * GROUP : (g + 1) * GROUP].reshape(span, width)
        inner = lax.dot_general(taken, left, (((1,), (1,)), ((), ())), preferred_element_type=F32)
        limit = jnp.zeros((1, span), I32)
        for i in range(GROUP):
            limit = jnp.where(lane_tile == i, at[2, g * GROUP + i], limit)
        kept = jnp.where(own < limit, inner, 0.0).astype(BF16)
        outer = jnp.dot(kept, right, preferred_element_type=F32)
        for i in range(GROUP):
            to = at[dst_row, g * GROUP + i]
            acc[to] = acc[to] + outer[i * probes : (i + 1) * probes]
    half = mine.shape[0]
    mine[...] = acc[:half].astype(mine.dtype)
    send[...] = acc[half:].astype(send.dtype)


def tiles(pieces, src_row, dst_row, table, first, second, blocks, send_dtype, name):
    count, rank, width = first.shape
    probes = pieces[0].shape[1]
    rows = len(pieces) * pieces[0].shape[0]
    half = (blocks // 2, probes, width)

    def body(*refs):
        tiles_body(len(pieces), src_row, dst_row, *refs)

    return local(
        body,
        [shape(half, F32), shape(half, send_dtype)],
        table,
        *pieces,
        first,
        second,
        name=name,
        flops=4 * count * rank * width * probes * GROUP,
        scratch=(2 * rows + 4 * blocks) * probes * width,
        scratches=[
            pltpu.SMEM(table.shape, I32),
            pltpu.VMEM((rows, probes, width), BF16),
            pltpu.VMEM((blocks, probes, width), F32),
            pltpu.SemaphoreType.DMA,
        ],
    )


def place(relative, order):
    at = jnp.zeros_like(relative)
    for k, bit in enumerate(order):
        at = at + jnp.where((relative & bit) != 0, 1 << k, 0)
    return at


def plan(owners, weight, orders, splits, joins, cell_blocks, station_blocks, after):
    peers, count = owners[0].shape
    rows = weight.shape[0] // peers

    def body(*refs):
        far, weight_far, table, weight_near, near, sems = refs[:5], refs[5], refs[6], refs[7], refs[8:13], refs[13]
        me = lax.axis_index("tile")
        odd = (me & 1) != 0
        pairs = list(zip(far, near))
        for k in range(4):
            holder = me
            for bits in (0, 1):
                bit = jnp.where(odd, joins[1][bits], joins[0][bits])
                holder = (holder | bit) if (k >> bits) & 1 else (holder & ~bit)
            start = pl.multiple_of(holder * rows, rows)
            pairs.append((weight_far.at[pl.ds(start, rows)], weight_near.at[pl.ds(k * rows, rows)]))
        fetch(pairs, sems)
        col_owner, col_local, row_owner, row_local, rank = [ref[pl.ds(me, 1), :] for ref in near]
        span = peers // 2
        away = col_owner ^ me
        spot = jnp.where((col_owner & 1) != 0, place(away, orders[1]), place(away, orders[0]))
        table[0:1, :] = ((away & 1) * span + spot) * cell_blocks + col_local
        away = row_owner ^ me
        spots = []
        for q in (0, 1):
            spot = place(away, splits[q][::-1]) * 4 + place(row_owner, joins[q])
            spots.append(spot)
        spot = jnp.where((row_owner & 1) != 0, spots[1], spots[0])
        table[1:2, :] = ((away & 1) * span + spot) * station_blocks + row_local
        table[2:3, :] = rank

    return local(
        body,
        [shape((8, count), I32), shape((4 * rows, LANES), F32)],
        *owners,
        weight,
        name="plan",
        specs=[whole(pltpu.HBM)] * 6,
        scratches=[pltpu.VMEM((peers, count), I32)] * 5 + [pltpu.SemaphoreType.DMA((9,))],
        after=after,
    )


def shards(
    probes,
    level_set,
    unit_label,
    contrast,
    station_weight,
    u_factor,
    v_factor,
    col_owner,
    col_local,
    row_owner,
    row_local,
    tile_rank,
):
    peers = lax.axis_size("tile")
    tile_count, _, station_width = u_factor.shape
    cell_width = v_factor.shape[2]
    probe_count, cell_total = probes.shape
    cell_blocks = cell_total // cell_width
    station_blocks = station_weight.shape[0] // (peers * station_width)
    bits = [1 << k for k in range(1, peers.bit_length() - 1)]
    far = bits[:0:-1]
    orders = (bits[:1] + far, far + bits[:1])
    splits = (bits[:-2], bits[1:-1])
    joins = ((bits[-1], bits[-2]), (bits[0], bits[-1]))

    lanes = (cell_total // LANES, LANES)
    part, scaling = local(
        scale_body,
        [shape((cell_blocks, probe_count, cell_width), BF16), shape(lanes, F32)],
        contrast,
        level_set.reshape(lanes),
        unit_label.reshape(lanes),
        probes,
        name="scale",
        specs=[whole(pltpu.HBM)] * 4,
        scratches=[
            pltpu.SMEM(contrast.shape, F32),
            pltpu.VMEM(lanes, F32),
            pltpu.VMEM(lanes, I32),
            pltpu.VMEM(probes.shape, F32),
            pltpu.SemaphoreType.DMA((4,)),
        ],
    )
    steps = list(zip(*orders))
    for step, pair in enumerate(steps):
        got = swap(part, pair)
        if step == 0:
            table, weight = plan(
                [a.reshape(peers, tile_count) for a in (col_owner, col_local, row_owner, row_local, tile_rank)],
                station_weight.reshape(-1, LANES),
                orders,
                splits,
                joins,
                cell_blocks,
                station_blocks,
                (scaling,),
            )
            part = join(part, got, after=(table,))
        elif step == 1:
            v_here = load(v_factor, (part,), "load_v")
            u_here = load(u_factor, (part, v_here), "load_u")
            part = join(part, got, after=(u_here,))
        elif step < len(steps) - 1:
            part = join(part, got)
    pieces = [part, got]
    pieces = pieces + [swap(piece, (1, 1)) for piece in pieces]

    total, send = tiles(pieces, 0, 1, table, v_here, u_here, peers * station_blocks, F32, "forward")
    got = swap(send, (1, 1))
    for pair in zip(*splits):
        total, send = fold(total, got)
        got = swap(send, pair)
    for pair in zip(*joins):
        total, send = plus(total, got)
        got = swap(send, pair)
    pieces = [weigh(total, got, weight)]
    for pair in list(zip(*splits))[::-1] + [(1, 1)]:
        pieces = pieces + [swap(piece, pair) for piece in pieces]

    keep, send = tiles(pieces, 1, 0, table, u_here, v_here, peers * cell_blocks, BF16, "adjoint")
    got = swap(send, (1, 1))
    for pair in steps[::-1]:
        keep, send = fold(keep, got)
        got = swap(send, pair)
    return local(
        final_body,
        [shape((probe_count, cell_total), F32)],
        keep,
        got,
        scaling,
        name="final",
        far_out=True,
    )[0]


def solution(mesh):
    placed = (
        P(None, ("groups", "tile")),
        P(("groups", "tile")),
        P(("groups", "tile")),
        P("groups"),
        P("groups"),
        P(("groups", "tile"), None, None),
        P(("groups", "tile"), None, None),
        P("groups", None),
        P("groups"),
        P("groups", None),
        P("groups"),
        P("groups"),
    )
    return jax.shard_map(
        shards, mesh=mesh, in_specs=placed, out_specs=P(None, ("groups", "tile")), check_vma=False
    )
```

time: 105 us -> 97.4 us (0.928)
  the two profiles are of different devices: /device:TPU:0 before, /device:TPU:24 now
where the time goes in v4:
time: 97.4 us; the launch traced here: 97.1 us
  waiting for transfers between devices  70.1 us (72%)
  Pallas kernels  19.1 us (20%)
  starting transfers between devices  7.77 us (8%)
    ppermute x16, waiting for transfers between devices, swap(): lax.ppermute(array, 'tile', [(i, i ^ bits[i & 1]) for i in range(count)])  70.1 us
    pallas_call x16, Pallas kernels, local(): pl.pallas_call(run, out_shape=[a if far_out else pltpu.VMEM(a.shape, a.dt...  19.1 us
    ppermute x16, starting transfers between devices, swap(): lax.ppermute(array, 'tile', [(i, i ^ bits[i & 1]) for i in range(count)])  7.77 us
  transfers between devices with their start and end apart: 16, of which 14 were waited for; matrix products, arithmetic and copies ran while one was open for 0% of the time, Pallas kernels for 6%

profile of v4, /device:TPU:24, one launch (start us, length us, event | category | flops | bytes accessed | tf_op | source)
XLA Modules:
  0.0 97.1 jit_solution(12808179111508357942)
XLA Ops:
  0.0 1.1 %scale.1 = (bf16[16,8,512]{2,1,0:T(8,128)(2,1)S(1)}, f32[64,128]{1,0:T(8,128)S(1)}) custom-call(f32[4]{0:T(128)} %refs_0_.3, f32[64,128]{1,0:T(8,128)} %bitcast.9, s32[64,128]{1,0:T(8,128)} %bitcast.10, f32[8,8192]{1,0:T(8,128)} %refs_3_.1), custom_call_target="tpu_custom_call" | custom-call | bytes 491536 | tf_op jit(solution)/shard_map/scale/pallas_call | solution.py:44
  1.1 1.6 %collective-permute-start = (bf16[16,8,512]{2,1,0:T(8,128)(2,1)S(1)}, bf16[16,8,512]{2,1,0:T(8,128)(2,1)S(1)}, u32[]{:S(2)}, u32[]{:S(2)}) collective-permute-start(bf16[16,8,512]{2,1,0:T(8,128)(2,1)S(1)} %get-tuple-element.27.refs_0_), channel_id=1, source_target_pairs={{0,2},{1,9},{2,0},{3,11},{4,6},{5,13},{6,4},{7,15},{8,10},{9,1},{1... | collective-permute-start | bytes 393224 | tf_op jit(solution)/shard_map/ppermute | solution.py:32
  2.7 0.9 plan.1
  3.6 2.5 %collective-permute-done.refs_1_ = bf16[16,8,512]{2,1,0:T(8,128)(2,1)S(1)} collective-permute-done((bf16[16,8,512]{2,1,0:T(8,128)(2,1)S(1)}, bf16[16,8,512]{2,1,0:T(8,128)(2,1)S(1)}, u32[]{:S(2)}, u32[]{:S(2)}) %collective-permute-start) | collective-permute-done | bytes 131104 | tf_op jit(solution)/shard_map/ppermute | solution.py:32
  6.1 0.4 collective-permute-start.1
  6.5 2.2 %load_v.1.refs_2_.refs_5_.refs_6_ = bf16[128,32,512]{2,1,0:T(8,128)(2,1)S(1)} custom-call(bf16[128,32,512]{2,1,0:T(8,128)(2,1)} %refs_0_.4, bf16[32,8,512]{2,1,0:T(8,128)(2,1)S(1)} %join.2.refs_1_.refs_0_), custom_call_target="tpu_custom_call" | custom-call | bytes 8388608 | tf_op jit(solution)/shard_map/load_v/pallas_call | solution.py:44
  8.8 2.2 %load_u.1.refs_2_.refs_6_.refs_5_ = bf16[128,32,512]{2,1,0:T(8,128)(2,1)S(1)} custom-call(bf16[128,32,512]{2,1,0:T(8,128)(2,1)} %refs_0_.5, bf16[32,8,512]{2,1,0:T(8,128)(2,1)S(1)} %join.2.refs_1_.refs_0_, bf16[128,32,512]{2,1,0:T(8,128)(2,1)S(1)} %load_v.1.refs_2_.refs_5_.refs_6_), custom_call_target="tpu_custom_call" | custom-call | bytes 8388608 | tf_op jit(solution)/shard_map/load_u/pallas_call | solution.py:44
  11.0 5.3 %collective-permute-done.1.refs_1_ = bf16[32,8,512]{2,1,0:T(8,128)(2,1)S(1)} collective-permute-done((bf16[32,8,512]{2,1,0:T(8,128)(2,1)S(1)}, bf16[32,8,512]{2,1,0:T(8,128)(2,1)S(1)}, u32[]{:S(2)}, u32[]{:S(2)}) %collective-permute-start.1) | collective-permute-done | bytes 262176 | tf_op jit(solution)/shard_map/ppermute | solution.py:32
  16.3 0.1 collective-permute-start.2
  16.4 0.1 collective-permute-start.3
  16.5 9.1 %collective-permute-done.2.refs_2_ = bf16[64,8,512]{2,1,0:T(8,128)(2,1)S(1)} collective-permute-done((bf16[64,8,512]{2,1,0:T(8,128)(2,1)S(1)}, bf16[64,8,512]{2,1,0:T(8,128)(2,1)S(1)}, u32[]{:S(2)}, u32[]{:S(2)}) %collective-permute-start.2) | collective-permute-done | bytes 524320 | tf_op jit(solution)/shard_map/ppermute | solution.py:32
  25.5 0.0 collective-permute-start.4
  25.6 0.0 collective-permute-done.3.refs_3_
  25.6 1.9 %collective-permute-done.4.refs_4_ = bf16[64,8,512]{2,1,0:T(8,128)(2,1)S(1)} collective-permute-done((bf16[64,8,512]{2,1,0:T(8,128)(2,1)S(1)}, bf16[64,8,512]{2,1,0:T(8,128)(2,1)S(1)}, u32[]{:S(2)}, u32[]{:S(2)}) %collective-permute-start.4) | collective-permute-done | bytes 524320 | tf_op jit(solution)/shard_map/ppermute | solution.py:32
  27.5 5.6 %forward.1 = (f32[32,8,512]{2,1,0:T(8,128)S(1)}, f32[32,8,512]{2,1,0:T(8,128)S(1)}) custom-call(s32[8,128]{1,0:T(8,128)S(1)} %get-tuple-element.26.refs_2_.refs_0_, bf16[64,8,512]{2,1,0:T(8,128)(2,1)S(1)} %join.3.refs_1_, bf16[64,8,512]{2,1,0:T(8,128)(2,1)S(1)} %collective-permute-done.2.refs_2_, bf16[64,8,512]{2,1,0:T(8,128)(2,1)S(1)} %collective-permute-done.3.refs_3_, ...), custom_call_target="tpu_custom_call" | custom-call | flops 536870912 | bytes 11538432 | tf_op jit(solution)/shard_map/forward/pallas_call | solution.py:44
  33.0 0.2 collective-permute-start.5
  33.2 1.8 %collective-permute-done.5.refs_1_ = f32[32,8,512]{2,1,0:T(8,128)S(1)} collective-permute-done((f32[32,8,512]{2,1,0:T(8,128)S(1)}, f32[32,8,512]{2,1,0:T(8,128)S(1)}, u32[]{:S(2)}, u32[]{:S(2)}) %collective-permute-start.5) | collective-permute-done | bytes 524320 | tf_op jit(solution)/shard_map/ppermute | solution.py:32
  35.0 0.1 fold.4
  35.1 1.6 %collective-permute-start.6 = (bf16[16,8,512]{2,1,0:T(8,128)(2,1)S(1)}, bf16[16,8,512]{2,1,0:T(8,128)(2,1)S(1)}, u32[]{:S(2)}, u32[]{:S(2)}) collective-permute-start(bf16[16,8,512]{2,1,0:T(8,128)(2,1)S(1)} %get-tuple-element.31), channel_id=1, source_target_pairs={{0,2},{1,5},{2,0},{3,7},{4,6},{5,1},{6,4},{7,3},{8,10},{9,13},{10,... | collective-permute-start | bytes 393224 | tf_op jit(solution)/shard_map/ppermute | solution.py:32
  36.7 3.5 %collective-permute-done.6.refs_1_ = bf16[16,8,512]{2,1,0:T(8,128)(2,1)S(1)} collective-permute-done((bf16[16,8,512]{2,1,0:T(8,128)(2,1)S(1)}, bf16[16,8,512]{2,1,0:T(8,128)(2,1)S(1)}, u32[]{:S(2)}, u32[]{:S(2)}) %collective-permute-start.6) | collective-permute-done | bytes 131104 | tf_op jit(solution)/shard_map/ppermute | solution.py:32
  40.2 0.3 collective-permute-start.7
  40.4 8.0 %collective-permute-done.7.refs_1_ = bf16[16,8,512]{2,1,0:T(8,128)(2,1)S(1)} collective-permute-done((bf16[16,8,512]{2,1,0:T(8,128)(2,1)S(1)}, bf16[16,8,512]{2,1,0:T(8,128)(2,1)S(1)}, u32[]{:S(2)}, u32[]{:S(2)}) %collective-permute-start.7) | collective-permute-done | bytes 131104 | tf_op jit(solution)/shard_map/ppermute | solution.py:32
  48.5 0.1 collective-permute-start.8
  48.6 6.2 %collective-permute-done.8.refs_1_ = bf16[16,8,512]{2,1,0:T(8,128)(2,1)S(1)} collective-permute-done((bf16[16,8,512]{2,1,0:T(8,128)(2,1)S(1)}, bf16[16,8,512]{2,1,0:T(8,128)(2,1)S(1)}, u32[]{:S(2)}, u32[]{:S(2)}) %collective-permute-start.8) | collective-permute-done | bytes 131104 | tf_op jit(solution)/shard_map/ppermute | solution.py:32
  54.8 1.6 %collective-permute-start.9 = (bf16[16,8,512]{2,1,0:T(8,128)(2,1)S(1)}, bf16[16,8,512]{2,1,0:T(8,128)(2,1)S(1)}, u32[]{:S(2)}, u32[]{:S(2)}) collective-permute-start(bf16[16,8,512]{2,1,0:T(8,128)(2,1)S(1)} %weigh.1.refs_1_), channel_id=1, source_target_pairs={{0,2},{1,5},{2,0},{3,7},{4,6},{5,1},{6,4},{7,3},{8,10},{9,13},{10,... | collective-permute-start | bytes 393224 | tf_op jit(solution)/shard_map/ppermute | solution.py:32
  56.4 0.0 collective-permute-start.10
  56.4 3.5 %collective-permute-done.9.refs_2_ = bf16[16,8,512]{2,1,0:T(8,128)(2,1)S(1)} collective-permute-done((bf16[16,8,512]{2,1,0:T(8,128)(2,1)S(1)}, bf16[16,8,512]{2,1,0:T(8,128)(2,1)S(1)}, u32[]{:S(2)}, u32[]{:S(2)}) %collective-permute-start.9) | collective-permute-done | bytes 131104 | tf_op jit(solution)/shard_map/ppermute | solution.py:32
  59.9 0.0 collective-permute-start.11
  59.9 0.0 collective-permute-done.10.refs_3_
  59.9 1.3 %collective-permute-done.11.refs_4_ = bf16[16,8,512]{2,1,0:T(8,128)(2,1)S(1)} collective-permute-done((bf16[16,8,512]{2,1,0:T(8,128)(2,1)S(1)}, bf16[16,8,512]{2,1,0:T(8,128)(2,1)S(1)}, u32[]{:S(2)}, u32[]{:S(2)}) %collective-permute-start.11) | collective-permute-done | bytes 131104 | tf_op jit(solution)/shard_map/ppermute | solution.py:32
  61.2 5.7 %adjoint.1 = (f32[128,8,512]{2,1,0:T(8,128)S(1)}, bf16[128,8,512]{2,1,0:T(8,128)(2,1)S(1)}) custom-call(s32[8,128]{1,0:T(8,128)S(1)} %get-tuple-element.26.refs_2_.refs_0_, bf16[16,8,512]{2,1,0:T(8,128)(2,1)S(1)} %weigh.1.refs_1_, bf16[16,8,512]{2,1,0:T(8,128)(2,1)S(1)} %collective-permute-done.9.refs_2_, ...), custom_call_target="tpu_custom_call" | custom-call | flops 536870912 | bytes 12062720 | tf_op jit(solution)/shard_map/adjoint/pallas_call | solution.py:44
  67.0 0.2 collective-permute-start.12
  67.2 2.5 %collective-permute-done.12.refs_1_ = bf16[128,8,512]{2,1,0:T(8,128)(2,1)S(1)} collective-permute-done((bf16[128,8,512]{2,1,0:T(8,128)(2,1)S(1)}, bf16[128,8,512]{2,1,0:T(8,128)(2,1)S(1)}, u32[]{:S(2)}, u32[]{:S(2)}) %collective-permute-start.12) | collective-permute-done | bytes 1048608 | tf_op jit(solution)/shard_map/ppermute | solution.py:32
  69.7 0.2 fold.5
  69.9 0.1 collective-permute-start.13
  70.0 9.2 %collective-permute-done.13.refs_1_ = bf16[64,8,512]{2,1,0:T(8,128)(2,1)S(1)} collective-permute-done((bf16[64,8,512]{2,1,0:T(8,128)(2,1)S(1)}, bf16[64,8,512]{2,1,0:T(8,128)(2,1)S(1)}, u32[]{:S(2)}, u32[]{:S(2)}) %collective-permute-start.13) | collective-permute-done | bytes 524320 | tf_op jit(solution)/shard_map/ppermute | solution.py:32
  79.2 0.1 fold.6
  79.3 0.1 collective-permute-start.14
  79.3 11.9 %collective-permute-done.14.refs_1_ = bf16[32,8,512]{2,1,0:T(8,128)(2,1)S(1)} collective-permute-done((bf16[32,8,512]{2,1,0:T(8,128)(2,1)S(1)}, bf16[32,8,512]{2,1,0:T(8,128)(2,1)S(1)}, u32[]{:S(2)}, u32[]{:S(2)}) %collective-permute-start.14) | collective-permute-done | bytes 262176 | tf_op jit(solution)/shard_map/ppermute | solution.py:32
  91.3 1.6 %collective-permute-start.15 = (bf16[16,8,512]{2,1,0:T(8,128)(2,1)S(1)}, bf16[16,8,512]{2,1,0:T(8,128)(2,1)S(1)}, u32[]{:S(2)}, u32[]{:S(2)}) collective-permute-start(bf16[16,8,512]{2,1,0:T(8,128)(2,1)S(1)} %get-tuple-element.44), channel_id=1, source_target_pairs={{0,2},{1,9},{2,0},{3,11},{4,6},{5,13},{6,4},{7,15},{8,10},{9,1},{1... | collective-permute-start | bytes 393224 | tf_op jit(solution)/shard_map/ppermute | solution.py:32
  92.9 3.4 %collective-permute-done.15.refs_1_ = bf16[16,8,512]{2,1,0:T(8,128)(2,1)S(1)} collective-permute-done((bf16[16,8,512]{2,1,0:T(8,128)(2,1)S(1)}, bf16[16,8,512]{2,1,0:T(8,128)(2,1)S(1)}, u32[]{:S(2)}, u32[]{:S(2)}) %collective-permute-start.15) | collective-permute-done | bytes 131104 | tf_op jit(solution)/shard_map/ppermute | solution.py:32
  96.4 0.7 final.1
  (6 shorter events, 0.2 us)
Async XLA Ops:
  1.1 5.0 %collective-permute-start = (bf16[16,8,512]{2,1,0:T(8,128)(2,1)S(1)}, bf16[16,8,512]{2,1,0:T(8,128)(2,1)S(1)}, u32[]{:S(2)}, u32[]{:S(2)}) collective-permute-start(bf16[16,8,512]{2,1,0:T(8,128)(2,1)S(1)} %get-tuple-element.27.refs_0_), channel_id=1, source_target_pairs={{0,2},{1,9},{2,0},{3,11},{4,6},{5,13},{6,4},{7,15},{8,10},{9,1},{1... | collective-permute-start | bytes 393224 | tf_op jit(solution)/shard_map/ppermute | solution.py:32
  6.1 10.1 %collective-permute-start.1 = (bf16[32,8,512]{2,1,0:T(8,128)(2,1)S(1)}, bf16[32,8,512]{2,1,0:T(8,128)(2,1)S(1)}, u32[]{:S(2)}, u32[]{:S(2)}) collective-permute-start(bf16[32,8,512]{2,1,0:T(8,128)(2,1)S(1)} %join.2.refs_1_.refs_0_), channel_id=1, source_target_pairs={{0,8},{1,5},{2,10},{3,7},{4,12},{5,1},{6,14},{7,3},{8,0},{9,13},{1... | collective-permute-start | bytes 786440 | tf_op jit(solution)/shard_map/ppermute | solution.py:32
  16.3 9.2 %collective-permute-start.2 = (bf16[64,8,512]{2,1,0:T(8,128)(2,1)S(1)}, bf16[64,8,512]{2,1,0:T(8,128)(2,1)S(1)}, u32[]{:S(2)}, u32[]{:S(2)}) collective-permute-start(bf16[64,8,512]{2,1,0:T(8,128)(2,1)S(1)} %join.3.refs_1_), channel_id=1, source_target_pairs={{0,4},{1,3},{2,6},{3,1},{4,0},{5,7},{6,2},{7,5},{8,12},{9,11},{10,... | collective-permute-start | bytes 1572872 | tf_op jit(solution)/shard_map/ppermute | solution.py:32
  16.4 9.2 %collective-permute-start.3 = (bf16[64,8,512]{2,1,0:T(8,128)(2,1)S(1)}, bf16[64,8,512]{2,1,0:T(8,128)(2,1)S(1)}, u32[]{:S(2)}, u32[]{:S(2)}) collective-permute-start(bf16[64,8,512]{2,1,0:T(8,128)(2,1)S(1)} %join.3.refs_1_), channel_id=1, source_target_pairs={{0,1},{1,0},{2,3},{3,2},{4,5},{5,4},{6,7},{7,6},{8,9},{9,8},{10,11... | collective-permute-start | bytes 1572872 | tf_op jit(solution)/shard_map/ppermute | solution.py:32
  25.5 1.9 %collective-permute-start.4 = (bf16[64,8,512]{2,1,0:T(8,128)(2,1)S(1)}, bf16[64,8,512]{2,1,0:T(8,128)(2,1)S(1)}, u32[]{:S(2)}, u32[]{:S(2)}) collective-permute-start(bf16[64,8,512]{2,1,0:T(8,128)(2,1)S(1)} %collective-permute-done.2.refs_2_), channel_id=1, source_target_pairs={{0,1},{1,0},{2,3},{3,2},{4,5},{5,4},{6,7},{7,6},{8,9},{9,8},{10,11... | collective-permute-start | bytes 1572872 | tf_op jit(solution)/shard_map/ppermute | solution.py:32
  33.0 2.0 %collective-permute-start.5 = (f32[32,8,512]{2,1,0:T(8,128)S(1)}, f32[32,8,512]{2,1,0:T(8,128)S(1)}, u32[]{:S(2)}, u32[]{:S(2)}) collective-permute-start(f32[32,8,512]{2,1,0:T(8,128)S(1)} %get-tuple-element.29), channel_id=1, source_target_pairs={{0,1},{1,0},{2,3},{3,2},{4,5},{5,4},{6,7},{7,6},{8,9},{9,8},{10,11... | collective-permute-start | bytes 1572872 | tf_op jit(solution)/shard_map/ppermute | solution.py:32
  35.1 5.0 %collective-permute-start.6 = (bf16[16,8,512]{2,1,0:T(8,128)(2,1)S(1)}, bf16[16,8,512]{2,1,0:T(8,128)(2,1)S(1)}, u32[]{:S(2)}, u32[]{:S(2)}) collective-permute-start(bf16[16,8,512]{2,1,0:T(8,128)(2,1)S(1)} %get-tuple-element.31), channel_id=1, source_target_pairs={{0,2},{1,5},{2,0},{3,7},{4,6},{5,1},{6,4},{7,3},{8,10},{9,13},{10,... | collective-permute-start | bytes 393224 | tf_op jit(solution)/shard_map/ppermute | solution.py:32
  40.2 8.3 %collective-permute-start.7 = (bf16[16,8,512]{2,1,0:T(8,128)(2,1)S(1)}, bf16[16,8,512]{2,1,0:T(8,128)(2,1)S(1)}, u32[]{:S(2)}, u32[]{:S(2)}) collective-permute-start(bf16[16,8,512]{2,1,0:T(8,128)(2,1)S(1)} %get-tuple-element.33), channel_id=1, source_target_pairs={{0,8},{1,3},{2,10},{3,1},{4,12},{5,7},{6,14},{7,5},{8,0},{9,11},{1... | collective-permute-start | bytes 393224 | tf_op jit(solution)/shard_map/ppermute | solution.py:32
  48.5 6.3 %collective-permute-start.8 = (bf16[16,8,512]{2,1,0:T(8,128)(2,1)S(1)}, bf16[16,8,512]{2,1,0:T(8,128)(2,1)S(1)}, u32[]{:S(2)}, u32[]{:S(2)}) collective-permute-start(bf16[16,8,512]{2,1,0:T(8,128)(2,1)S(1)} %get-tuple-element.35), channel_id=1, source_target_pairs={{0,4},{1,9},{2,6},{3,11},{4,0},{5,13},{6,2},{7,15},{8,12},{9,1},{1... | collective-permute-start | bytes 393224 | tf_op jit(solution)/shard_map/ppermute | solution.py:32
  54.8 5.0 %collective-permute-start.9 = (bf16[16,8,512]{2,1,0:T(8,128)(2,1)S(1)}, bf16[16,8,512]{2,1,0:T(8,128)(2,1)S(1)}, u32[]{:S(2)}, u32[]{:S(2)}) collective-permute-start(bf16[16,8,512]{2,1,0:T(8,128)(2,1)S(1)} %weigh.1.refs_1_), channel_id=1, source_target_pairs={{0,2},{1,5},{2,0},{3,7},{4,6},{5,1},{6,4},{7,3},{8,10},{9,13},{10,... | collective-permute-start | bytes 393224 | tf_op jit(solution)/shard_map/ppermute | solution.py:32
  56.4 3.5 %collective-permute-start.10 = (bf16[16,8,512]{2,1,0:T(8,128)(2,1)S(1)}, bf16[16,8,512]{2,1,0:T(8,128)(2,1)S(1)}, u32[]{:S(2)}, u32[]{:S(2)}) collective-permute-start(bf16[16,8,512]{2,1,0:T(8,128)(2,1)S(1)} %weigh.1.refs_1_), channel_id=1, source_target_pairs={{0,1},{1,0},{2,3},{3,2},{4,5},{5,4},{6,7},{7,6},{8,9},{9,8},{10,11... | collective-permute-start | bytes 393224 | tf_op jit(solution)/shard_map/ppermute | solution.py:32
  59.9 1.3 %collective-permute-start.11 = (bf16[16,8,512]{2,1,0:T(8,128)(2,1)S(1)}, bf16[16,8,512]{2,1,0:T(8,128)(2,1)S(1)}, u32[]{:S(2)}, u32[]{:S(2)}) collective-permute-start(bf16[16,8,512]{2,1,0:T(8,128)(2,1)S(1)} %collective-permute-done.9.refs_2_), channel_id=1, source_target_pairs={{0,1},{1,0},{2,3},{3,2},{4,5},{5,4},{6,7},{7,6},{8,9},{9,8},{10,11... | collective-permute-start | bytes 393224 | tf_op jit(solution)/shard_map/ppermute | solution.py:32
  67.0 2.7 %collective-permute-start.12 = (bf16[128,8,512]{2,1,0:T(8,128)(2,1)S(1)}, bf16[128,8,512]{2,1,0:T(8,128)(2,1)S(1)}, u32[]{:S(2)}, u32[]{:S(2)}) collective-permute-start(bf16[128,8,512]{2,1,0:T(8,128)(2,1)S(1)} %get-tuple-element.38), channel_id=1, source_target_pairs={{0,1},{1,0},{2,3},{3,2},{4,5},{5,4},{6,7},{7,6},{8,9},{9,8},{10,11... | collective-permute-start | bytes 3145736 | tf_op jit(solution)/shard_map/ppermute | solution.py:32
  69.9 9.2 %collective-permute-start.13 = (bf16[64,8,512]{2,1,0:T(8,128)(2,1)S(1)}, bf16[64,8,512]{2,1,0:T(8,128)(2,1)S(1)}, u32[]{:S(2)}, u32[]{:S(2)}) collective-permute-start(bf16[64,8,512]{2,1,0:T(8,128)(2,1)S(1)} %get-tuple-element.40), channel_id=1, source_target_pairs={{0,4},{1,3},{2,6},{3,1},{4,0},{5,7},{6,2},{7,5},{8,12},{9,11},{10,... | collective-permute-start | bytes 1572872 | tf_op jit(solution)/shard_map/ppermute | solution.py:32
  79.3 12.0 %collective-permute-start.14 = (bf16[32,8,512]{2,1,0:T(8,128)(2,1)S(1)}, bf16[32,8,512]{2,1,0:T(8,128)(2,1)S(1)}, u32[]{:S(2)}, u32[]{:S(2)}) collective-permute-start(bf16[32,8,512]{2,1,0:T(8,128)(2,1)S(1)} %get-tuple-element.42), channel_id=1, source_target_pairs={{0,8},{1,5},{2,10},{3,7},{4,12},{5,1},{6,14},{7,3},{8,0},{9,13},{1... | collective-permute-start | bytes 786440 | tf_op jit(solution)/shard_map/ppermute | solution.py:32
  91.3 5.0 %collective-permute-start.15 = (bf16[16,8,512]{2,1,0:T(8,128)(2,1)S(1)}, bf16[16,8,512]{2,1,0:T(8,128)(2,1)S(1)}, u32[]{:S(2)}, u32[]{:S(2)}) collective-permute-start(bf16[16,8,512]{2,1,0:T(8,128)(2,1)S(1)} %get-tuple-element.44), channel_id=1, source_target_pairs={{0,2},{1,9},{2,0},{3,11},{4,6},{5,13},{6,4},{7,15},{8,10},{9,1},{1... | collective-permute-start | bytes 393224 | tf_op jit(solution)/shard_map/ppermute | solution.py:32

commit v5 on v4

v5 whole, which is shorter than its diff:
```python
import math

import jax
import jax.numpy as jnp
from jax import lax
from jax.experimental import pallas as pl
from jax.experimental.pallas import tpu as pltpu
from jax.sharding import PartitionSpec as P

BF16 = jnp.bfloat16
F32 = jnp.float32
I32 = jnp.int32
GROUP = 8
SKEW = 3
SQUARE = (6, 2, 4)
LANES = 128
MIB = 1024 * 1024


def whole(space=pltpu.VMEM):
    return pl.BlockSpec(memory_space=space)


def shape(dims, dtype):
    return jax.ShapeDtypeStruct(tuple(dims), dtype)


def size_of(array):
    return math.prod(array.shape) * jnp.dtype(array.dtype).itemsize


def swap(array, bits):
    count = lax.axis_size("tile")
    return lax.ppermute(array, "tile", [(i, i ^ bits) for i in range(count)])


def local(body, outs, *ins, name, scratch=0, scratches=(), specs=None, flops=0, far_out=False, after=()):
    nbytes = sum(size_of(a) for a in (*ins, *outs))
    specs = list(specs or [whole()] * len(ins)) + [whole()] * len(after)
    own = len(ins)
    ins = [pltpu.with_memory_space_constraint(a, s.memory_space) for a, s in zip((*ins, *after), specs)]

    def run(*refs):
        body(*refs[:own], *refs[len(ins) :])

    return pl.pallas_call(
        run,
        out_shape=[a if far_out else pltpu.VMEM(a.shape, a.dtype) for a in outs],
        in_specs=specs,
        out_specs=[whole()] * len(outs),
        scratch_shapes=list(scratches),
        compiler_params=pltpu.CompilerParams(vmem_limit_bytes=scratch + 8 * MIB),
        cost_estimate=pl.CostEstimate(flops=flops, bytes_accessed=nbytes, transcendentals=0),
        name=name,
    )(*ins)


def fetch(pairs, sems):
    copies = [pltpu.make_async_copy(a, b, sems.at[i]) for i, (a, b) in enumerate(pairs)]
    for copy in copies:
        copy.start()
    for copy in copies:
        copy.wait()


def load_body(source, out, sems):
    n = source.shape[0] // sems.shape[0]
    rows = [pl.ds(i * n, n) for i in range(sems.shape[0])]
    fetch([(source.at[r], out.at[r]) for r in rows], sems)


def load(array, after, name):
    return local(
        load_body,
        [shape(array.shape, array.dtype)],
        array,
        name=name,
        specs=[whole(pltpu.HBM)],
        scratches=[pltpu.SemaphoreType.DMA((8,))],
        after=after,
    )[0]


def scale_body(
    contrast, level, label, probes, part_p, part_q, scaling, contrast_near, level_near, label_near, probes_near, sems
):
    fetch(
        [(contrast, contrast_near), (level, level_near), (label, label_near), (probes, probes_near)],
        sems,
    )
    value = level_near[...]
    unit = label_near[...]
    factor = jnp.zeros_like(value)
    for k in range(contrast.shape[0]):
        factor = jnp.where(unit == k, contrast_near[k], factor)
    scaling[...] = factor / (1.0 + value * value)
    blocks, _, width = part_p.shape
    rows = width // LANES
    for half, part in enumerate((part_p, part_q)):
        for b in range(blocks):
            for c in range(rows):
                j = (half * blocks + b) * rows + c
                piece = probes_near[:, j * LANES : (j + 1) * LANES] * scaling[j : j + 1, :]
                part[b, :, c * LANES : (c + 1) * LANES] = piece.astype(BF16)


def final_body(keep_p, recv_p, keep_q, recv_q, scaling, out):
    blocks, _, width = keep_p.shape
    rows = width // LANES
    for half, (keep, recv) in enumerate(((keep_p, recv_p), (keep_q, recv_q))):
        for b in range(blocks):
            for c in range(rows):
                j = (half * blocks + b) * rows + c
                lanes = slice(c * LANES, (c + 1) * LANES)
                total = keep[b, :, lanes] + recv[b, :, lanes].astype(F32)
                out[:, j * LANES : (j + 1) * LANES] = total * scaling[j : j + 1, :]


def join_body(*refs):
    out, at = refs[-1], 0
    for ref in refs[:-1]:
        out[at : at + ref.shape[0]] = ref[...]
        at += ref.shape[0]


def join(*pieces, after=()):
    out = shape((sum(a.shape[0] for a in pieces),) + pieces[0].shape[1:], pieces[0].dtype)
    return local(join_body, [out], *pieces, name="join", after=after)[0]


def plus(total, *gots):
    def body(total, *refs):
        done = total[...]
        for ref in refs[:-2]:
            done = done + ref[...].astype(F32)
        refs[-2][...] = done
        refs[-1][...] = done.astype(BF16)

    return local(body, [shape(total.shape, F32), shape(total.shape, BF16)], total, *gots, name="plus")


def weigh(total, got, weight):
    def body(total, got, weight, out):
        blocks, _, width = out.shape
        rows = width // LANES
        for b in range(blocks):
            for c in range(rows):
                lanes = slice(c * LANES, (c + 1) * LANES)
                done = total[b, :, lanes] + got[b, :, lanes].astype(F32)
                j = b * rows + c
                out[b, :, lanes] = (done * weight[j : j + 1, :]).astype(BF16)

    return local(body, [shape(total.shape, BF16)], total, got, weight, name="weigh")[0]


def fold(keep, recv, dtypes=(F32, BF16)):
    n = keep.shape[0] // len(dtypes)

    def body(keep, recv, *outs):
        for i, out in enumerate(outs):
            at = slice(i * n, (i + 1) * n)
            out[...] = (keep[at] + recv[at].astype(F32)).astype(out.dtype)

    return local(body, [shape((n,) + keep.shape[1:], t) for t in dtypes], keep, recv, name="fold")


def tiles_body(piece_count, src_row, dst_row, table_near, *refs):
    pieces = refs[:piece_count]
    first, second, mine, send, at, table, acc, sem = refs[piece_count:]
    count, rank, width = first.shape
    groups = count // GROUP
    copy = pltpu.make_async_copy(table_near, at, sem)
    copy.start()
    acc[...] = jnp.zeros_like(acc)
    join_body(*pieces, table)
    probes = table.shape[1]
    span = GROUP * rank
    row_tile = lax.broadcasted_iota(I32, (GROUP * probes, span), 0) // probes
    col_tile = lax.broadcasted_iota(I32, (GROUP * probes, span), 1) // rank
    component = lax.broadcasted_iota(I32, (GROUP * probes, span), 1) % rank
    own = jnp.where(row_tile == col_tile, component, rank)
    lane_tile = lax.broadcasted_iota(I32, (1, span), 1) // rank
    copy.wait()

    def inner_of(g):
        taken = jnp.concatenate(
            [table[at[src_row, g * GROUP + i]].astype(F32) for i in range(GROUP)], axis=0
        ).astype(BF16)
        left = first[g * GROUP : (g + 1) * GROUP].reshape(span, width)
        inner = lax.dot_general(taken, left, (((1,), (1,)), ((), ())), preferred_element_type=F32)
        limit = jnp.zeros((1, span), I32)
        for i in range(GROUP):
            limit = jnp.where(lane_tile == i, at[2, g * GROUP + i], limit)
        return jnp.where(own < limit, inner, 0.0).astype(BF16)

    def outer_of(g, kept):
        right = second[g * GROUP : (g + 1) * GROUP].reshape(span, width)
        return jnp.dot(kept, right, preferred_element_type=F32)

    def add(g, outer):
        for i in range(GROUP):
            to = at[dst_row, g * GROUP + i]
            acc[to] = acc[to] + outer[i * probes : (i + 1) * probes]

    kept, outer = {}, {}
    for step in range(groups + 2 * SKEW):
        if step >= 2 * SKEW:
            add(step - 2 * SKEW, outer.pop(step - 2 * SKEW))
        if 0 <= step - SKEW < groups:
            outer[step - SKEW] = outer_of(step - SKEW, kept.pop(step - SKEW))
        if step < groups:
            kept[step] = inner_of(step)
    half = mine.shape[0]
    mine[...] = acc[:half].astype(mine.dtype)
    send[...] = acc[half:].astype(send.dtype)


def tiles(pieces, src_row, dst_row, table, first, second, blocks, send_dtype, name):
    count, rank, width = first.shape
    probes = pieces[0].shape[1]
    rows = sum(piece.shape[0] for piece in pieces)
    half = (blocks // 2, probes, width)

    def body(*refs):
        tiles_body(len(pieces), src_row, dst_row, *refs)

    return local(
        body,
        [shape(half, F32), shape(half, send_dtype)],
        table,
        *pieces,
        first,
        second,
        name=name,
        flops=4 * count * rank * width * probes * GROUP,
        scratch=(2 * rows + 4 * blocks) * probes * width,
        scratches=[
            pltpu.SMEM(table.shape, I32),
            pltpu.VMEM((rows, probes, width), BF16),
            pltpu.VMEM((blocks, probes, width), F32),
            pltpu.SemaphoreType.DMA,
        ],
    )


def place(relative, order):
    at = jnp.zeros_like(relative)
    for k, bit in enumerate(order):
        at = at + jnp.where((relative & bit) != 0, 1 << k, 0)
    return at


def plan(owners, weight, orders, cell_blocks, station_blocks, after):
    peers, count = owners[0].shape
    rows = weight.shape[0] // peers
    rest = peers // 8
    half = cell_blocks // 2

    def body(*refs):
        far, weight_far, table, weight_near, near, sems = refs[:5], refs[5], refs[6], refs[7], refs[8:13], refs[13]
        me = lax.axis_index("tile")
        pairs = list(zip(far, near))
        for k in range(rest):
            start = pl.multiple_of((k * 8 + (me & 7)) * rows, rows)
            pairs.append((weight_far.at[pl.ds(start, rows)], weight_near.at[pl.ds(k * rows, rows)]))
        fetch(pairs, sems)
        col_owner, col_local, row_owner, row_local, rank = [ref[pl.ds(me, 1), :] for ref in near]
        span = peers // 2
        away = col_owner ^ me
        is_q = col_local >= half
        spot = jnp.where(is_q, place(away, orders[1]) + (span - 1), place(away, orders[0]))
        table[0:1, :] = (away & 1) * (span * cell_blocks) + spot * half + col_local
        away = row_owner ^ me
        spot = (away & 1) * 4 + ((away & 4) // 2) + ((away & 2) // 2)
        table[1:2, :] = (spot * rest + row_owner // 8) * station_blocks + row_local
        table[2:3, :] = rank

    return local(
        body,
        [shape((8, count), I32), shape((rest * rows, LANES), F32)],
        *owners,
        weight,
        name="plan",
        specs=[whole(pltpu.HBM)] * 6,
        scratches=[pltpu.VMEM((peers, count), I32)] * 5 + [pltpu.SemaphoreType.DMA((5 + rest,))],
        after=after,
    )


def shards(
    probes,
    level_set,
    unit_label,
    contrast,
    station_weight,
    u_factor,
    v_factor,
    col_owner,
    col_local,
    row_owner,
    row_local,
    tile_rank,
):
    peers = lax.axis_size("tile")
    tile_count, _, station_width = u_factor.shape
    cell_width = v_factor.shape[2]
    probe_count, cell_total = probes.shape
    cell_blocks = cell_total // cell_width
    station_blocks = station_weight.shape[0] // (peers * station_width)
    bits = [1 << k for k in range(1, peers.bit_length() - 1)]
    far = bits[:0:-1]
    orders = (bits[:1] + far, far + bits[:1])

    lanes = (cell_total // LANES, LANES)
    half_dims = (cell_blocks // 2, probe_count, cell_width)
    part_p, part_q, scaling = local(
        scale_body,
        [shape(half_dims, BF16), shape(half_dims, BF16), shape(lanes, F32)],
        contrast,
        level_set.reshape(lanes),
        unit_label.reshape(lanes),
        probes,
        name="scale",
        specs=[whole(pltpu.HBM)] * 4,
        scratches=[
            pltpu.SMEM(contrast.shape, F32),
            pltpu.VMEM(lanes, F32),
            pltpu.VMEM(lanes, I32),
            pltpu.VMEM(probes.shape, F32),
            pltpu.SemaphoreType.DMA((4,)),
        ],
    )
    table, weight = plan(
        [a.reshape(peers, tile_count) for a in (col_owner, col_local, row_owner, row_local, tile_rank)],
        station_weight.reshape(-1, LANES),
        orders,
        cell_blocks,
        station_blocks,
        (scaling,),
    )
    steps = list(zip(*orders))
    after = (table,)
    for step, (bit_p, bit_q) in enumerate(steps):
        got_p = swap(part_p, bit_p)
        got_q = swap(part_q, bit_q)
        if step == 1:
            v_here = load(v_factor, (part_p, part_q), "load_v")
            u_here = load(u_factor, (part_p, part_q, v_here), "load_u")
            after = (u_here,)
        if step < len(steps) - 1:
            part_p = join(part_p, got_p, after=after)
            part_q = join(part_q, got_q)
            after = ()
    pieces = [part_p, got_p, part_q, got_q]
    pieces = pieces + [swap(piece, 1) for piece in pieces]

    total, send = tiles(pieces, 0, 1, table, v_here, u_here, peers * station_blocks, F32, "forward")
    got = swap(send, 1)
    total, send_y, send_z, send_yz = fold(total, got, (F32, BF16, BF16, BF16))
    sends = {2: send_y, 4: send_z, 6: send_yz}
    total, send = plus(total, *[swap(sends[k], k) for k in SQUARE])
    for bit in bits[2:-1]:
        total, send = plus(total, swap(send, bit))
    weighted = weigh(total, swap(send, bits[-1]), weight)
    gots = {k: swap(weighted, k) for k in SQUARE}
    around = join(gots[2], gots[4], gots[6])
    pieces = [weighted, around, swap(weighted, 1), swap(around, 1)]

    keep, send = tiles(pieces, 1, 0, table, u_here, v_here, peers * cell_blocks, BF16, "adjoint")
    got = swap(send, 1)
    keep_p, send_p, keep_q, send_q = fold(keep, got, (F32, BF16, F32, BF16))
    for step, (bit_p, bit_q) in enumerate(steps[::-1]):
        if step > 0:
            keep_p, send_p = fold(keep_p, got_p)
            keep_q, send_q = fold(keep_q, got_q)
        got_p = swap(send_p, bit_p)
        got_q = swap(send_q, bit_q)
    return local(
        final_body,
        [shape((probe_count, cell_total), F32)],
        keep_p,
        got_p,
        keep_q,
        got_q,
        scaling,
        name="final",
        far_out=True,
    )[0]


def solution(mesh):
    placed = (
        P(None, ("groups", "tile")),
        P(("groups", "tile")),
        P(("groups", "tile")),
        P("groups"),
        P("groups"),
        P(("groups", "tile"), None, None),
        P(("groups", "tile"), None, None),
        P("groups", None),
        P("groups"),
        P("groups", None),
        P("groups"),
        P("groups"),
    )
    return jax.shard_map(
        shards, mesh=mesh, in_specs=placed, out_specs=P(None, ("groups", "tile")), check_vma=False
    )
```

time: 97.4 us -> 83.9 us (0.86)
  the two profiles are of different devices: /device:TPU:24 before, /device:TPU:0 now
where the time goes in v5:
time: 83.9 us; the launch traced here: 83.7 us
  waiting for transfers between devices  42.9 us (51%)
  starting transfers between devices  27.2 us (32%)
  Pallas kernels  13.4 us (16%)
    ppermute x27, waiting for transfers between devices, swap(): return lax.ppermute(array, 'tile', [(i, i ^ bits) for i in range(count)])  42.9 us
    ppermute x27, starting transfers between devices, swap(): return lax.ppermute(array, 'tile', [(i, i ^ bits) for i in range(count)])  27.2 us
    pallas_call x20, Pallas kernels, local(): pl.pallas_call(run, out_shape=[a if far_out else pltpu.VMEM(a.shape, a.dt...  13.4 us
  transfers between devices with their start and end apart: 27, of which 19 were waited for; matrix products, arithmetic and copies ran while one was open for 0% of the time, Pallas kernels for 7%

profile of v5, /device:TPU:0, one launch (start us, length us, event | category | flops | bytes accessed | tf_op | source)
XLA Modules:
  0.0 83.7 jit_solution(17905927298043409805)
XLA Ops:
  0.0 1.1 %scale.1 = (bf16[8,8,512]{2,1,0:T(8,128)(2,1)S(1)}, bf16[8,8,512]{2,1,0:T(8,128)(2,1)S(1)}, f32[64,128]{1,0:T(8,128)S(1)}) custom-call(f32[4]{0:T(128)} %refs_0_.3, f32[64,128]{1,0:T(8,128)} %bitcast.9, s32[64,128]{1,0:T(8,128)} %bitcast.10, f32[8,8192]{1,0:T(8,128)} %refs_3_.1), custom_call_target="tpu_custom_call" | custom-call | bytes 491536 | tf_op jit(solution)/shard_map/scale/pallas_call | solution.py:46
  1.1 4.1 %collective-permute-start.2 = (bf16[8,8,512]{2,1,0:T(8,128)(2,1)S(1)}, bf16[8,8,512]{2,1,0:T(8,128)(2,1)S(1)}, u32[]{:S(2)}, u32[]{:S(2)}) collective-permute-start(bf16[8,8,512]{2,1,0:T(8,128)(2,1)S(1)} %get-tuple-element.35.refs_0_), channel_id=1, source_target_pairs={{0,8},{1,9},{2,10},{3,11},{4,12},{5,13},{6,14},{7,15},{8,0},{9,1},... | collective-permute-start | bytes 196616 | tf_op jit(solution)/shard_map/ppermute | solution.py:34
  5.2 1.5 %collective-permute-start = (bf16[8,8,512]{2,1,0:T(8,128)(2,1)S(1)}, bf16[8,8,512]{2,1,0:T(8,128)(2,1)S(1)}, u32[]{:S(2)}, u32[]{:S(2)}) collective-permute-start(bf16[8,8,512]{2,1,0:T(8,128)(2,1)S(1)} %get-tuple-element.34.refs_0_), channel_id=1, source_target_pairs={{0,2},{1,3},{2,0},{3,1},{4,6},{5,7},{6,4},{7,5},{8,10},{9,11},{10,... | collective-permute-start | bytes 196616 | tf_op jit(solution)/shard_map/ppermute | solution.py:34
  6.7 0.9 %plan.1 = (s32[8,128]{1,0:T(8,128)S(1)}, f32[32,128]{1,0:T(8,128)S(1)}) custom-call(s32[16,128]{1,0:T(8,128)} %bitcast.11, s32[16,128]{1,0:T(8,128)} %bitcast.12, s32[16,128]{1,0:T(8,128)} %bitcast.13, s32[16,128]{1,0:T(8,128)} %bitcast.14, s32[16,128]{1,0:T(8,128)} %bitcast.15, f32[256,128]{1,0:T(8,128)} %bitcast.8, ...), custom_call_target="tpu_custom_call" | custom-call | bytes 192512 | tf_op jit(solution)/shard_map/plan/pallas_call | solution.py:46
  7.6 1.2 %collective-permute-done.2.refs_1_ = bf16[8,8,512]{2,1,0:T(8,128)(2,1)S(1)} collective-permute-done((bf16[8,8,512]{2,1,0:T(8,128)(2,1)S(1)}, bf16[8,8,512]{2,1,0:T(8,128)(2,1)S(1)}, u32[]{:S(2)}, u32[]{:S(2)}) %collective-permute-start.2) | collective-permute-done | bytes 65568 | tf_op jit(solution)/shard_map/ppermute | solution.py:34
  8.8 0.6 collective-permute-start.4
  9.5 3.4 %collective-permute-start.1 = (bf16[16,8,512]{2,1,0:T(8,128)(2,1)S(1)}, bf16[16,8,512]{2,1,0:T(8,128)(2,1)S(1)}, u32[]{:S(2)}, u32[]{:S(2)}) collective-permute-start(bf16[16,8,512]{2,1,0:T(8,128)(2,1)S(1)} %join.5.refs_1_.refs_0_), channel_id=1, source_target_pairs={{0,8},{1,9},{2,10},{3,11},{4,12},{5,13},{6,14},{7,15},{8,0},{9,1},... | collective-permute-start | bytes 393224 | tf_op jit(solution)/shard_map/ppermute | solution.py:34
  12.9 2.2 %load_v.1.refs_3_.refs_9_.refs_6_ = bf16[128,32,512]{2,1,0:T(8,128)(2,1)S(1)} custom-call(bf16[128,32,512]{2,1,0:T(8,128)(2,1)} %refs_0_.4, bf16[16,8,512]{2,1,0:T(8,128)(2,1)S(1)} %join.5.refs_1_.refs_0_, bf16[16,8,512]{2,1,0:T(8,128)(2,1)S(1)} %join.6.refs_2_.refs_0_), custom_call_target="tpu_custom_call" | custom-call | bytes 8388608 | tf_op jit(solution)/shard_map/load_v/pallas_call | solution.py:46
  15.2 2.2 %load_u.1.refs_2_.refs_10_.refs_5_ = bf16[128,32,512]{2,1,0:T(8,128)(2,1)S(1)} custom-call(bf16[128,32,512]{2,1,0:T(8,128)(2,1)} %refs_0_.5, bf16[16,8,512]{2,1,0:T(8,128)(2,1)S(1)} %join.5.refs_1_.refs_0_, bf16[16,8,512]{2,1,0:T(8,128)(2,1)S(1)} %join.6.refs_2_.refs_0_, bf16[128,32,512]{2,1,0:T(8,128)(2,1)S(1)} %load_v.1.refs_3_.refs_9_.refs_6_), custom_call_target="tpu_custom_call" | custom-call | bytes 8388608 | tf_op jit(solution)/shard_map/load_u/pallas_call | solution.py:46
  17.4 1.6 %collective-permute-start.5 = (bf16[32,8,512]{2,1,0:T(8,128)(2,1)S(1)}, bf16[32,8,512]{2,1,0:T(8,128)(2,1)S(1)}, u32[]{:S(2)}, u32[]{:S(2)}) collective-permute-start(bf16[32,8,512]{2,1,0:T(8,128)(2,1)S(1)} %join.8.refs_3_), channel_id=1, source_target_pairs={{0,2},{1,3},{2,0},{3,1},{4,6},{5,7},{6,4},{7,5},{8,10},{9,11},{10,... | collective-permute-start | bytes 786440 | tf_op jit(solution)/shard_map/ppermute | solution.py:34
  19.2 0.5 collective-permute-start.6
  19.7 5.1 %collective-permute-done.5.refs_4_ = bf16[32,8,512]{2,1,0:T(8,128)(2,1)S(1)} collective-permute-done((bf16[32,8,512]{2,1,0:T(8,128)(2,1)S(1)}, bf16[32,8,512]{2,1,0:T(8,128)(2,1)S(1)}, u32[]{:S(2)}, u32[]{:S(2)}) %collective-permute-start.5) | collective-permute-done | bytes 262176 | tf_op jit(solution)/shard_map/ppermute | solution.py:34
  24.8 1.3 %collective-permute-done.3.refs_2_ = bf16[32,8,512]{2,1,0:T(8,128)(2,1)S(1)} collective-permute-done((bf16[32,8,512]{2,1,0:T(8,128)(2,1)S(1)}, bf16[32,8,512]{2,1,0:T(8,128)(2,1)S(1)}, u32[]{:S(2)}, u32[]{:S(2)}) %collective-permute-start.3) | collective-permute-done | bytes 262176 | tf_op jit(solution)/shard_map/ppermute | solution.py:34
  26.4 1.3 %collective-permute-done.7.refs_6_ = bf16[32,8,512]{2,1,0:T(8,128)(2,1)S(1)} collective-permute-done((bf16[32,8,512]{2,1,0:T(8,128)(2,1)S(1)}, bf16[32,8,512]{2,1,0:T(8,128)(2,1)S(1)}, u32[]{:S(2)}, u32[]{:S(2)}) %collective-permute-start.7) | collective-permute-done | bytes 262176 | tf_op jit(solution)/shard_map/ppermute | solution.py:34
  27.7 2.8 %forward.1 = (f32[32,8,512]{2,1,0:T(8,128)S(1)}, f32[32,8,512]{2,1,0:T(8,128)S(1)}) custom-call(s32[8,128]{1,0:T(8,128)S(1)} %get-tuple-element.33.refs_2_.refs_0_, bf16[32,8,512]{2,1,0:T(8,128)(2,1)S(1)} %join.7.refs_1_, bf16[32,8,512]{2,1,0:T(8,128)(2,1)S(1)} %collective-permute-done.3.refs_2_, bf16[32,8,512]{2,1,0:T(8,128)(2,1)S(1)} %join.8.refs_3_, ...), custom_call_target="tpu_custom_call" | custom-call | flops 536870912 | bytes 11538432 | tf_op jit(solution)/shard_map/forward/pallas_call | solution.py:46
  30.5 0.2 collective-permute-start.10
  30.7 1.8 %collective-permute-done.10.refs_1_ = f32[32,8,512]{2,1,0:T(8,128)S(1)} collective-permute-done((f32[32,8,512]{2,1,0:T(8,128)S(1)}, f32[32,8,512]{2,1,0:T(8,128)S(1)}, u32[]{:S(2)}, u32[]{:S(2)}) %collective-permute-start.10) | collective-permute-done | bytes 524320 | tf_op jit(solution)/shard_map/ppermute | solution.py:34
  32.5 1.3 %collective-permute-start.11 = (bf16[8,8,512]{2,1,0:T(8,128)(2,1)S(1)}, bf16[8,8,512]{2,1,0:T(8,128)(2,1)S(1)}, u32[]{:S(2)}, u32[]{:S(2)}) collective-permute-start(bf16[8,8,512]{2,1,0:T(8,128)(2,1)S(1)} %get-tuple-element.39), channel_id=1, source_target_pairs={{0,6},{1,7},{2,4},{3,5},{4,2},{5,3},{6,0},{7,1},{8,14},{9,15},{10,... | collective-permute-start | bytes 196616 | tf_op jit(solution)/shard_map/ppermute | solution.py:34
  33.8 0.6 collective-permute-start.12
  34.3 1.7 %collective-permute-start.13 = (bf16[8,8,512]{2,1,0:T(8,128)(2,1)S(1)}, bf16[8,8,512]{2,1,0:T(8,128)(2,1)S(1)}, u32[]{:S(2)}, u32[]{:S(2)}) collective-permute-start(bf16[8,8,512]{2,1,0:T(8,128)(2,1)S(1)} %get-tuple-element.41), channel_id=1, source_target_pairs={{0,4},{1,5},{2,6},{3,7},{4,0},{5,1},{6,2},{7,3},{8,12},{9,13},{10,... | collective-permute-start | bytes 196616 | tf_op jit(solution)/shard_map/ppermute | solution.py:34
  36.0 2.1 %collective-permute-done.11.refs_1_ = bf16[8,8,512]{2,1,0:T(8,128)(2,1)S(1)} collective-permute-done((bf16[8,8,512]{2,1,0:T(8,128)(2,1)S(1)}, bf16[8,8,512]{2,1,0:T(8,128)(2,1)S(1)}, u32[]{:S(2)}, u32[]{:S(2)}) %collective-permute-start.11) | collective-permute-done | bytes 65568 | tf_op jit(solution)/shard_map/ppermute | solution.py:34
  38.1 0.9 %collective-permute-done.12.refs_2_ = bf16[8,8,512]{2,1,0:T(8,128)(2,1)S(1)} collective-permute-done((bf16[8,8,512]{2,1,0:T(8,128)(2,1)S(1)}, bf16[8,8,512]{2,1,0:T(8,128)(2,1)S(1)}, u32[]{:S(2)}, u32[]{:S(2)}) %collective-permute-start.12) | collective-permute-done | bytes 65568 | tf_op jit(solution)/shard_map/ppermute | solution.py:34
  39.0 2.2 %collective-permute-start.14 = (bf16[8,8,512]{2,1,0:T(8,128)(2,1)S(1)}, bf16[8,8,512]{2,1,0:T(8,128)(2,1)S(1)}, u32[]{:S(2)}, u32[]{:S(2)}) collective-permute-start(bf16[8,8,512]{2,1,0:T(8,128)(2,1)S(1)} %get-tuple-element.43), channel_id=1, source_target_pairs={{0,8},{1,9},{2,10},{3,11},{4,12},{5,13},{6,14},{7,15},{8,0},{9,1},... | collective-permute-start | bytes 196616 | tf_op jit(solution)/shard_map/ppermute | solution.py:34
  41.2 3.1 %collective-permute-done.14.refs_1_ = bf16[8,8,512]{2,1,0:T(8,128)(2,1)S(1)} collective-permute-done((bf16[8,8,512]{2,1,0:T(8,128)(2,1)S(1)}, bf16[8,8,512]{2,1,0:T(8,128)(2,1)S(1)}, u32[]{:S(2)}, u32[]{:S(2)}) %collective-permute-start.14) | collective-permute-done | bytes 65568 | tf_op jit(solution)/shard_map/ppermute | solution.py:34
  44.3 1.6 %collective-permute-start.17 = (bf16[8,8,512]{2,1,0:T(8,128)(2,1)S(1)}, bf16[8,8,512]{2,1,0:T(8,128)(2,1)S(1)}, u32[]{:S(2)}, u32[]{:S(2)}) collective-permute-start(bf16[8,8,512]{2,1,0:T(8,128)(2,1)S(1)} %weigh.1.refs_1_), channel_id=1, source_target_pairs={{0,6},{1,7},{2,4},{3,5},{4,2},{5,3},{6,0},{7,1},{8,14},{9,15},{10,... | collective-permute-start | bytes 196616 | tf_op jit(solution)/shard_map/ppermute | solution.py:34
  45.9 1.7 %collective-permute-start.16 = (bf16[8,8,512]{2,1,0:T(8,128)(2,1)S(1)}, bf16[8,8,512]{2,1,0:T(8,128)(2,1)S(1)}, u32[]{:S(2)}, u32[]{:S(2)}) collective-permute-start(bf16[8,8,512]{2,1,0:T(8,128)(2,1)S(1)} %weigh.1.refs_1_), channel_id=1, source_target_pairs={{0,4},{1,5},{2,6},{3,7},{4,0},{5,1},{6,2},{7,3},{8,12},{9,13},{10,... | collective-permute-start | bytes 196616 | tf_op jit(solution)/shard_map/ppermute | solution.py:34
  47.6 0.3 collective-permute-start.15
  47.8 1.7 %collective-permute-done.17.refs_2_ = bf16[8,8,512]{2,1,0:T(8,128)(2,1)S(1)} collective-permute-done((bf16[8,8,512]{2,1,0:T(8,128)(2,1)S(1)}, bf16[8,8,512]{2,1,0:T(8,128)(2,1)S(1)}, u32[]{:S(2)}, u32[]{:S(2)}) %collective-permute-start.17) | collective-permute-done | bytes 65568 | tf_op jit(solution)/shard_map/ppermute | solution.py:34
  49.5 1.0 %collective-permute-done.16.refs_1_ = bf16[8,8,512]{2,1,0:T(8,128)(2,1)S(1)} collective-permute-done((bf16[8,8,512]{2,1,0:T(8,128)(2,1)S(1)}, bf16[8,8,512]{2,1,0:T(8,128)(2,1)S(1)}, u32[]{:S(2)}, u32[]{:S(2)}) %collective-permute-start.16) | collective-permute-done | bytes 65568 | tf_op jit(solution)/shard_map/ppermute | solution.py:34
  50.5 1.3 %collective-permute-done.15.refs_0_ = bf16[8,8,512]{2,1,0:T(8,128)(2,1)S(1)} collective-permute-done((bf16[8,8,512]{2,1,0:T(8,128)(2,1)S(1)}, bf16[8,8,512]{2,1,0:T(8,128)(2,1)S(1)}, u32[]{:S(2)}, u32[]{:S(2)}) %collective-permute-start.15) | collective-permute-done | bytes 65568 | tf_op jit(solution)/shard_map/ppermute | solution.py:34
  51.9 0.5 collective-permute-start.18
  52.4 1.0 %collective-permute-done.18.refs_3_ = bf16[8,8,512]{2,1,0:T(8,128)(2,1)S(1)} collective-permute-done((bf16[8,8,512]{2,1,0:T(8,128)(2,1)S(1)}, bf16[8,8,512]{2,1,0:T(8,128)(2,1)S(1)}, u32[]{:S(2)}, u32[]{:S(2)}) %collective-permute-start.18) | collective-permute-done | bytes 65568 | tf_op jit(solution)/shard_map/ppermute | solution.py:34
  53.5 2.9 %adjoint.1 = (f32[128,8,512]{2,1,0:T(8,128)S(1)}, bf16[128,8,512]{2,1,0:T(8,128)(2,1)S(1)}) custom-call(s32[8,128]{1,0:T(8,128)S(1)} %get-tuple-element.33.refs_2_.refs_0_, bf16[8,8,512]{2,1,0:T(8,128)(2,1)S(1)} %weigh.1.refs_1_, bf16[24,8,512]{2,1,0:T(8,128)(2,1)S(1)} %join.9.refs_2_, bf16[8,8,512]{2,1,0:T(8,128)(2,1)S(1)} %collective-permute-done.18.refs_3_, ...), custom_call_target="tpu_custom_call" | custom-call | flops 536870912 | bytes 12062720 | tf_op jit(solution)/shard_map/adjoint/pallas_call | solution.py:46
  56.4 0.3 collective-permute-start.20
  56.7 2.4 %collective-permute-done.20.refs_1_ = bf16[128,8,512]{2,1,0:T(8,128)(2,1)S(1)} collective-permute-done((bf16[128,8,512]{2,1,0:T(8,128)(2,1)S(1)}, bf16[128,8,512]{2,1,0:T(8,128)(2,1)S(1)}, u32[]{:S(2)}, u32[]{:S(2)}) %collective-permute-start.20) | collective-permute-done | bytes 1048608 | tf_op jit(solution)/shard_map/ppermute | solution.py:34
  59.1 0.2 fold.7
  59.4 0.4 collective-permute-start.21
  59.8 1.2 %collective-permute-start.24 = (bf16[32,8,512]{2,1,0:T(8,128)(2,1)S(1)}, bf16[32,8,512]{2,1,0:T(8,128)(2,1)S(1)}, u32[]{:S(2)}, u32[]{:S(2)}) collective-permute-start(bf16[32,8,512]{2,1,0:T(8,128)(2,1)S(1)} %get-tuple-element.54), channel_id=1, source_target_pairs={{0,2},{1,3},{2,0},{3,1},{4,6},{5,7},{6,4},{7,5},{8,10},{9,11},{10,... | collective-permute-start | bytes 786440 | tf_op jit(solution)/shard_map/ppermute | solution.py:34
  61.0 6.9 %collective-permute-done.21.refs_1_ = bf16[32,8,512]{2,1,0:T(8,128)(2,1)S(1)} collective-permute-done((bf16[32,8,512]{2,1,0:T(8,128)(2,1)S(1)}, bf16[32,8,512]{2,1,0:T(8,128)(2,1)S(1)}, u32[]{:S(2)}, u32[]{:S(2)}) %collective-permute-start.21) | collective-permute-done | bytes 262176 | tf_op jit(solution)/shard_map/ppermute | solution.py:34
  67.9 1.9 %collective-permute-start.22 = (bf16[16,8,512]{2,1,0:T(8,128)(2,1)S(1)}, bf16[16,8,512]{2,1,0:T(8,128)(2,1)S(1)}, u32[]{:S(2)}, u32[]{:S(2)}) collective-permute-start(bf16[16,8,512]{2,1,0:T(8,128)(2,1)S(1)} %get-tuple-element.50), channel_id=1, source_target_pairs={{0,8},{1,9},{2,10},{3,11},{4,12},{5,13},{6,14},{7,15},{8,0},{9,1},... | collective-permute-start | bytes 393224 | tf_op jit(solution)/shard_map/ppermute | solution.py:34
  69.9 0.4 collective-permute-start.25
  70.3 6.1 %collective-permute-done.22.refs_1_ = bf16[16,8,512]{2,1,0:T(8,128)(2,1)S(1)} collective-permute-done((bf16[16,8,512]{2,1,0:T(8,128)(2,1)S(1)}, bf16[16,8,512]{2,1,0:T(8,128)(2,1)S(1)}, u32[]{:S(2)}, u32[]{:S(2)}) %collective-permute-start.22) | collective-permute-done | bytes 131104 | tf_op jit(solution)/shard_map/ppermute | solution.py:34
  76.4 0.5 collective-permute-start.23
  76.9 0.3 collective-permute-done.25.refs_1_
  77.3 0.5 collective-permute-start.26
  77.7 3.0 %collective-permute-done.23.refs_1_ = bf16[8,8,512]{2,1,0:T(8,128)(2,1)S(1)} collective-permute-done((bf16[8,8,512]{2,1,0:T(8,128)(2,1)S(1)}, bf16[8,8,512]{2,1,0:T(8,128)(2,1)S(1)}, u32[]{:S(2)}, u32[]{:S(2)}) %collective-permute-start.23) | collective-permute-done | bytes 65568 | tf_op jit(solution)/shard_map/ppermute | solution.py:34
  80.7 2.2 %collective-permute-done.26.refs_3_ = bf16[8,8,512]{2,1,0:T(8,128)(2,1)S(1)} collective-permute-done((bf16[8,8,512]{2,1,0:T(8,128)(2,1)S(1)}, bf16[8,8,512]{2,1,0:T(8,128)(2,1)S(1)}, u32[]{:S(2)}, u32[]{:S(2)}) %collective-permute-start.26) | collective-permute-done | bytes 65568 | tf_op jit(solution)/shard_map/ppermute | solution.py:34
  82.9 0.7 final.1
  (26 shorter events, 0.8 us)
Async XLA Ops:
  1.1 7.8 %collective-permute-start.2 = (bf16[8,8,512]{2,1,0:T(8,128)(2,1)S(1)}, bf16[8,8,512]{2,1,0:T(8,128)(2,1)S(1)}, u32[]{:S(2)}, u32[]{:S(2)}) collective-permute-start(bf16[8,8,512]{2,1,0:T(8,128)(2,1)S(1)} %get-tuple-element.35.refs_0_), channel_id=1, source_target_pairs={{0,8},{1,9},{2,10},{3,11},{4,12},{5,13},{6,14},{7,15},{8,0},{9,1},... | collective-permute-start | bytes 196616 | tf_op jit(solution)/shard_map/ppermute | solution.py:34
  5.2 4.3 %collective-permute-start = (bf16[8,8,512]{2,1,0:T(8,128)(2,1)S(1)}, bf16[8,8,512]{2,1,0:T(8,128)(2,1)S(1)}, u32[]{:S(2)}, u32[]{:S(2)}) collective-permute-start(bf16[8,8,512]{2,1,0:T(8,128)(2,1)S(1)} %get-tuple-element.34.refs_0_), channel_id=1, source_target_pairs={{0,2},{1,3},{2,0},{3,1},{4,6},{5,7},{6,4},{7,5},{8,10},{9,11},{10,... | collective-permute-start | bytes 196616 | tf_op jit(solution)/shard_map/ppermute | solution.py:34
  8.8 8.5 %collective-permute-start.4 = (bf16[16,8,512]{2,1,0:T(8,128)(2,1)S(1)}, bf16[16,8,512]{2,1,0:T(8,128)(2,1)S(1)}, u32[]{:S(2)}, u32[]{:S(2)}) collective-permute-start(bf16[16,8,512]{2,1,0:T(8,128)(2,1)S(1)} %join.6.refs_2_.refs_0_), channel_id=1, source_target_pairs={{0,4},{1,5},{2,6},{3,7},{4,0},{5,1},{6,2},{7,3},{8,12},{9,13},{10,... | collective-permute-start | bytes 393224 | tf_op jit(solution)/shard_map/ppermute | solution.py:34
  9.5 9.5 %collective-permute-start.1 = (bf16[16,8,512]{2,1,0:T(8,128)(2,1)S(1)}, bf16[16,8,512]{2,1,0:T(8,128)(2,1)S(1)}, u32[]{:S(2)}, u32[]{:S(2)}) collective-permute-start(bf16[16,8,512]{2,1,0:T(8,128)(2,1)S(1)} %join.5.refs_1_.refs_0_), channel_id=1, source_target_pairs={{0,8},{1,9},{2,10},{3,11},{4,12},{5,13},{6,14},{7,15},{8,0},{9,1},... | collective-permute-start | bytes 393224 | tf_op jit(solution)/shard_map/ppermute | solution.py:34
  17.4 7.4 %collective-permute-start.5 = (bf16[32,8,512]{2,1,0:T(8,128)(2,1)S(1)}, bf16[32,8,512]{2,1,0:T(8,128)(2,1)S(1)}, u32[]{:S(2)}, u32[]{:S(2)}) collective-permute-start(bf16[32,8,512]{2,1,0:T(8,128)(2,1)S(1)} %join.8.refs_3_), channel_id=1, source_target_pairs={{0,2},{1,3},{2,0},{3,1},{4,6},{5,7},{6,4},{7,5},{8,10},{9,11},{10,... | collective-permute-start | bytes 786440 | tf_op jit(solution)/shard_map/ppermute | solution.py:34
  19.0 7.1 %collective-permute-start.3 = (bf16[32,8,512]{2,1,0:T(8,128)(2,1)S(1)}, bf16[32,8,512]{2,1,0:T(8,128)(2,1)S(1)}, u32[]{:S(2)}, u32[]{:S(2)}) collective-permute-start(bf16[32,8,512]{2,1,0:T(8,128)(2,1)S(1)} %join.7.refs_1_), channel_id=1, source_target_pairs={{0,4},{1,5},{2,6},{3,7},{4,0},{5,1},{6,2},{7,3},{8,12},{9,13},{10,... | collective-permute-start | bytes 786440 | tf_op jit(solution)/shard_map/ppermute | solution.py:34
  19.2 7.0 %collective-permute-start.8 = (bf16[32,8,512]{2,1,0:T(8,128)(2,1)S(1)}, bf16[32,8,512]{2,1,0:T(8,128)(2,1)S(1)}, u32[]{:S(2)}, u32[]{:S(2)}) collective-permute-start(bf16[32,8,512]{2,1,0:T(8,128)(2,1)S(1)} %join.8.refs_3_), channel_id=1, source_target_pairs={{0,1},{1,0},{2,3},{3,2},{4,5},{5,4},{6,7},{7,6},{8,9},{9,8},{10,11... | collective-permute-start | bytes 786440 | tf_op jit(solution)/shard_map/ppermute | solution.py:34
  19.2 7.0 %collective-permute-start.6 = (bf16[32,8,512]{2,1,0:T(8,128)(2,1)S(1)}, bf16[32,8,512]{2,1,0:T(8,128)(2,1)S(1)}, u32[]{:S(2)}, u32[]{:S(2)}) collective-permute-start(bf16[32,8,512]{2,1,0:T(8,128)(2,1)S(1)} %join.7.refs_1_), channel_id=1, source_target_pairs={{0,1},{1,0},{2,3},{3,2},{4,5},{5,4},{6,7},{7,6},{8,9},{9,8},{10,11... | collective-permute-start | bytes 786440 | tf_op jit(solution)/shard_map/ppermute | solution.py:34
  24.8 1.5 %collective-permute-start.9 = (bf16[32,8,512]{2,1,0:T(8,128)(2,1)S(1)}, bf16[32,8,512]{2,1,0:T(8,128)(2,1)S(1)}, u32[]{:S(2)}, u32[]{:S(2)}) collective-permute-start(bf16[32,8,512]{2,1,0:T(8,128)(2,1)S(1)} %collective-permute-done.5.refs_4_), channel_id=1, source_target_pairs={{0,1},{1,0},{2,3},{3,2},{4,5},{5,4},{6,7},{7,6},{8,9},{9,8},{10,11... | collective-permute-start | bytes 786440 | tf_op jit(solution)/shard_map/ppermute | solution.py:34
  26.1 1.5 %collective-permute-start.7 = (bf16[32,8,512]{2,1,0:T(8,128)(2,1)S(1)}, bf16[32,8,512]{2,1,0:T(8,128)(2,1)S(1)}, u32[]{:S(2)}, u32[]{:S(2)}) collective-permute-start(bf16[32,8,512]{2,1,0:T(8,128)(2,1)S(1)} %collective-permute-done.3.refs_2_), channel_id=1, source_target_pairs={{0,1},{1,0},{2,3},{3,2},{4,5},{5,4},{6,7},{7,6},{8,9},{9,8},{10,11... | collective-permute-start | bytes 786440 | tf_op jit(solution)/shard_map/ppermute | solution.py:34
  30.5 2.0 %collective-permute-start.10 = (f32[32,8,512]{2,1,0:T(8,128)S(1)}, f32[32,8,512]{2,1,0:T(8,128)S(1)}, u32[]{:S(2)}, u32[]{:S(2)}) collective-permute-start(f32[32,8,512]{2,1,0:T(8,128)S(1)} %get-tuple-element.37), channel_id=1, source_target_pairs={{0,1},{1,0},{2,3},{3,2},{4,5},{5,4},{6,7},{7,6},{8,9},{9,8},{10,11... | collective-permute-start | bytes 1572872 | tf_op jit(solution)/shard_map/ppermute | solution.py:34
  32.5 5.6 %collective-permute-start.11 = (bf16[8,8,512]{2,1,0:T(8,128)(2,1)S(1)}, bf16[8,8,512]{2,1,0:T(8,128)(2,1)S(1)}, u32[]{:S(2)}, u32[]{:S(2)}) collective-permute-start(bf16[8,8,512]{2,1,0:T(8,128)(2,1)S(1)} %get-tuple-element.39), channel_id=1, source_target_pairs={{0,6},{1,7},{2,4},{3,5},{4,2},{5,3},{6,0},{7,1},{8,14},{9,15},{10,... | collective-permute-start | bytes 196616 | tf_op jit(solution)/shard_map/ppermute | solution.py:34
  33.8 5.2 %collective-permute-start.12 = (bf16[8,8,512]{2,1,0:T(8,128)(2,1)S(1)}, bf16[8,8,512]{2,1,0:T(8,128)(2,1)S(1)}, u32[]{:S(2)}, u32[]{:S(2)}) collective-permute-start(bf16[8,8,512]{2,1,0:T(8,128)(2,1)S(1)} %get-tuple-element.40), channel_id=1, source_target_pairs={{0,2},{1,3},{2,0},{3,1},{4,6},{5,7},{6,4},{7,5},{8,10},{9,11},{10,... | collective-permute-start | bytes 196616 | tf_op jit(solution)/shard_map/ppermute | solution.py:34
  34.3 4.7 %collective-permute-start.13 = (bf16[8,8,512]{2,1,0:T(8,128)(2,1)S(1)}, bf16[8,8,512]{2,1,0:T(8,128)(2,1)S(1)}, u32[]{:S(2)}, u32[]{:S(2)}) collective-permute-start(bf16[8,8,512]{2,1,0:T(8,128)(2,1)S(1)} %get-tuple-element.41), channel_id=1, source_target_pairs={{0,4},{1,5},{2,6},{3,7},{4,0},{5,1},{6,2},{7,3},{8,12},{9,13},{10,... | collective-permute-start | bytes 196616 | tf_op jit(solution)/shard_map/ppermute | solution.py:34
  39.0 5.2 %collective-permute-start.14 = (bf16[8,8,512]{2,1,0:T(8,128)(2,1)S(1)}, bf16[8,8,512]{2,1,0:T(8,128)(2,1)S(1)}, u32[]{:S(2)}, u32[]{:S(2)}) collective-permute-start(bf16[8,8,512]{2,1,0:T(8,128)(2,1)S(1)} %get-tuple-element.43), channel_id=1, source_target_pairs={{0,8},{1,9},{2,10},{3,11},{4,12},{5,13},{6,14},{7,15},{8,0},{9,1},... | collective-permute-start | bytes 196616 | tf_op jit(solution)/shard_map/ppermute | solution.py:34
  44.3 5.2 %collective-permute-start.17 = (bf16[8,8,512]{2,1,0:T(8,128)(2,1)S(1)}, bf16[8,8,512]{2,1,0:T(8,128)(2,1)S(1)}, u32[]{:S(2)}, u32[]{:S(2)}) collective-permute-start(bf16[8,8,512]{2,1,0:T(8,128)(2,1)S(1)} %weigh.1.refs_1_), channel_id=1, source_target_pairs={{0,6},{1,7},{2,4},{3,5},{4,2},{5,3},{6,0},{7,1},{8,14},{9,15},{10,... | collective-permute-start | bytes 196616 | tf_op jit(solution)/shard_map/ppermute | solution.py:34
  45.9 4.6 %collective-permute-start.16 = (bf16[8,8,512]{2,1,0:T(8,128)(2,1)S(1)}, bf16[8,8,512]{2,1,0:T(8,128)(2,1)S(1)}, u32[]{:S(2)}, u32[]{:S(2)}) collective-permute-start(bf16[8,8,512]{2,1,0:T(8,128)(2,1)S(1)} %weigh.1.refs_1_), channel_id=1, source_target_pairs={{0,4},{1,5},{2,6},{3,7},{4,0},{5,1},{6,2},{7,3},{8,12},{9,13},{10,... | collective-permute-start | bytes 196616 | tf_op jit(solution)/shard_map/ppermute | solution.py:34
  47.6 4.3 %collective-permute-start.15 = (bf16[8,8,512]{2,1,0:T(8,128)(2,1)S(1)}, bf16[8,8,512]{2,1,0:T(8,128)(2,1)S(1)}, u32[]{:S(2)}, u32[]{:S(2)}) collective-permute-start(bf16[8,8,512]{2,1,0:T(8,128)(2,1)S(1)} %weigh.1.refs_1_), channel_id=1, source_target_pairs={{0,2},{1,3},{2,0},{3,1},{4,6},{5,7},{6,4},{7,5},{8,10},{9,11},{10,... | collective-permute-start | bytes 196616 | tf_op jit(solution)/shard_map/ppermute | solution.py:34
  51.9 1.6 %collective-permute-start.19 = (bf16[24,8,512]{2,1,0:T(8,128)(2,1)S(1)}, bf16[24,8,512]{2,1,0:T(8,128)(2,1)S(1)}, u32[]{:S(2)}, u32[]{:S(2)}) collective-permute-start(bf16[24,8,512]{2,1,0:T(8,128)(2,1)S(1)} %join.9.refs_2_), channel_id=1, source_target_pairs={{0,1},{1,0},{2,3},{3,2},{4,5},{5,4},{6,7},{7,6},{8,9},{9,8},{10,11... | collective-permute-start | bytes 589832 | tf_op jit(solution)/shard_map/ppermute | solution.py:34
  51.9 1.5 %collective-permute-start.18 = (bf16[8,8,512]{2,1,0:T(8,128)(2,1)S(1)}, bf16[8,8,512]{2,1,0:T(8,128)(2,1)S(1)}, u32[]{:S(2)}, u32[]{:S(2)}) collective-permute-start(bf16[8,8,512]{2,1,0:T(8,128)(2,1)S(1)} %weigh.1.refs_1_), channel_id=1, source_target_pairs={{0,1},{1,0},{2,3},{3,2},{4,5},{5,4},{6,7},{7,6},{8,9},{9,8},{10,11... | collective-permute-start | bytes 196616 | tf_op jit(solution)/shard_map/ppermute | solution.py:34
  56.4 2.7 %collective-permute-start.20 = (bf16[128,8,512]{2,1,0:T(8,128)(2,1)S(1)}, bf16[128,8,512]{2,1,0:T(8,128)(2,1)S(1)}, u32[]{:S(2)}, u32[]{:S(2)}) collective-permute-start(bf16[128,8,512]{2,1,0:T(8,128)(2,1)S(1)} %get-tuple-element.46), channel_id=1, source_target_pairs={{0,1},{1,0},{2,3},{3,2},{4,5},{5,4},{6,7},{7,6},{8,9},{9,8},{10,11... | collective-permute-start | bytes 3145736 | tf_op jit(solution)/shard_map/ppermute | solution.py:34
  59.4 8.5 %collective-permute-start.21 = (bf16[32,8,512]{2,1,0:T(8,128)(2,1)S(1)}, bf16[32,8,512]{2,1,0:T(8,128)(2,1)S(1)}, u32[]{:S(2)}, u32[]{:S(2)}) collective-permute-start(bf16[32,8,512]{2,1,0:T(8,128)(2,1)S(1)} %get-tuple-element.48), channel_id=1, source_target_pairs={{0,4},{1,5},{2,6},{3,7},{4,0},{5,1},{6,2},{7,3},{8,12},{9,13},{10,... | collective-permute-start | bytes 786440 | tf_op jit(solution)/shard_map/ppermute | solution.py:34
  59.8 10.1 %collective-permute-start.24 = (bf16[32,8,512]{2,1,0:T(8,128)(2,1)S(1)}, bf16[32,8,512]{2,1,0:T(8,128)(2,1)S(1)}, u32[]{:S(2)}, u32[]{:S(2)}) collective-permute-start(bf16[32,8,512]{2,1,0:T(8,128)(2,1)S(1)} %get-tuple-element.54), channel_id=1, source_target_pairs={{0,2},{1,3},{2,0},{3,1},{4,6},{5,7},{6,4},{7,5},{8,10},{9,11},{10,... | collective-permute-start | bytes 786440 | tf_op jit(solution)/shard_map/ppermute | solution.py:34
  67.9 8.4 %collective-permute-start.22 = (bf16[16,8,512]{2,1,0:T(8,128)(2,1)S(1)}, bf16[16,8,512]{2,1,0:T(8,128)(2,1)S(1)}, u32[]{:S(2)}, u32[]{:S(2)}) collective-permute-start(bf16[16,8,512]{2,1,0:T(8,128)(2,1)S(1)} %get-tuple-element.50), channel_id=1, source_target_pairs={{0,8},{1,9},{2,10},{3,11},{4,12},{5,13},{6,14},{7,15},{8,0},{9,1},... | collective-permute-start | bytes 393224 | tf_op jit(solution)/shard_map/ppermute | solution.py:34
  69.9 7.3 %collective-permute-start.25 = (bf16[16,8,512]{2,1,0:T(8,128)(2,1)S(1)}, bf16[16,8,512]{2,1,0:T(8,128)(2,1)S(1)}, u32[]{:S(2)}, u32[]{:S(2)}) collective-permute-start(bf16[16,8,512]{2,1,0:T(8,128)(2,1)S(1)} %get-tuple-element.56), channel_id=1, source_target_pairs={{0,4},{1,5},{2,6},{3,7},{4,0},{5,1},{6,2},{7,3},{8,12},{9,13},{10,... | collective-permute-start | bytes 393224 | tf_op jit(solution)/shard_map/ppermute | solution.py:34
  76.4 4.3 %collective-permute-start.23 = (bf16[8,8,512]{2,1,0:T(8,128)(2,1)S(1)}, bf16[8,8,512]{2,1,0:T(8,128)(2,1)S(1)}, u32[]{:S(2)}, u32[]{:S(2)}) collective-permute-start(bf16[8,8,512]{2,1,0:T(8,128)(2,1)S(1)} %get-tuple-element.52), channel_id=1, source_target_pairs={{0,2},{1,3},{2,0},{3,1},{4,6},{5,7},{6,4},{7,5},{8,10},{9,11},{10,... | collective-permute-start | bytes 196616 | tf_op jit(solution)/shard_map/ppermute | solution.py:34
  77.3 5.7 %collective-permute-start.26 = (bf16[8,8,512]{2,1,0:T(8,128)(2,1)S(1)}, bf16[8,8,512]{2,1,0:T(8,128)(2,1)S(1)}, u32[]{:S(2)}, u32[]{:S(2)}) collective-permute-start(bf16[8,8,512]{2,1,0:T(8,128)(2,1)S(1)} %get-tuple-element.58), channel_id=1, source_target_pairs={{0,8},{1,9},{2,10},{3,11},{4,12},{5,13},{6,14},{7,15},{8,0},{9,1},... | collective-permute-start | bytes 196616 | tf_op jit(solution)/shard_map/ppermute | solution.py:34

commit v6 on v5

--- a/solution.py
+++ b/solution.py
@@ -34,9 +34,12 @@
     return lax.ppermute(array, "tile", [(i, i ^ bits) for i in range(count)])
 
 
-def local(body, outs, *ins, name, scratch=0, scratches=(), specs=None, flops=0, far_out=False, after=()):
+def local(
+    body, outs, *ins, name, scratch=0, scratches=(), specs=None, out_specs=None, flops=0, after=(), aliases=None
+):
     nbytes = sum(size_of(a) for a in (*ins, *outs))
     specs = list(specs or [whole()] * len(ins)) + [whole()] * len(after)
+    out_specs = list(out_specs or [whole()] * len(outs))
     own = len(ins)
     ins = [pltpu.with_memory_space_constraint(a, s.memory_space) for a, s in zip((*ins, *after), specs)]
 
@@ -45,9 +48,10 @@
 
     return pl.pallas_call(
         run,
-        out_shape=[a if far_out else pltpu.VMEM(a.shape, a.dtype) for a in outs],
+        out_shape=[a if s.memory_space is None else s.memory_space(a.shape, a.dtype) for a, s in zip(outs, out_specs)],
         in_specs=specs,
-        out_specs=[whole()] * len(outs),
+        out_specs=[whole() if s.memory_space is None else s for s in out_specs],
+        input_output_aliases=aliases or {},
         scratch_shapes=list(scratches),
         compiler_params=pltpu.CompilerParams(vmem_limit_bytes=scratch + 8 * MIB),
         cost_estimate=pl.CostEstimate(flops=flops, bytes_accessed=nbytes, transcendentals=0),
@@ -153,25 +157,29 @@
     return local(body, [shape(total.shape, BF16)], total, got, weight, name="weigh")[0]
 
 
-def fold(keep, recv, dtypes=(F32, BF16)):
-    n = keep.shape[0] // len(dtypes)
+def fold(keep, recv, dtypes=(F32, BF16), base=0):
+    n = recv.shape[0] // len(dtypes)
 
     def body(keep, recv, *outs):
         for i, out in enumerate(outs):
-            at = slice(i * n, (i + 1) * n)
-            out[...] = (keep[at] + recv[at].astype(F32)).astype(out.dtype)
+            mine = keep[base + i * n : base + (i + 1) * n]
+            out[...] = (mine + recv[i * n : (i + 1) * n].astype(F32)).astype(out.dtype)
 
     return local(body, [shape((n,) + keep.shape[1:], t) for t in dtypes], keep, recv, name="fold")
 
 
-def tiles_body(piece_count, src_row, dst_row, table_near, *refs):
+def zeros(dims, after):
+    def body(out):
+        out[...] = jnp.zeros_like(out)
+
+    return local(body, [shape(dims, F32)], name="zeros", after=after)[0]
+
+
+def tiles_body(piece_count, src_row, dst_row, at, _, *refs):
     pieces = refs[:piece_count]
-    first, second, mine, send, at, table, acc, sem = refs[piece_count:]
+    first, second, acc, *sends, table = refs[piece_count:]
     count, rank, width = first.shape
     groups = count // GROUP
-    copy = pltpu.make_async_copy(table_near, at, sem)
-    copy.start()
-    acc[...] = jnp.zeros_like(acc)
     join_body(*pieces, table)
     probes = table.shape[1]
     span = GROUP * rank
@@ -180,7 +188,6 @@
     component = lax.broadcasted_iota(I32, (GROUP * probes, span), 1) % rank
     own = jnp.where(row_tile == col_tile, component, rank)
     lane_tile = lax.broadcasted_iota(I32, (1, span), 1) // rank
-    copy.wait()
 
     def inner_of(g):
         taken = jnp.concatenate(
@@ -210,36 +217,34 @@
             outer[step - SKEW] = outer_of(step - SKEW, kept.pop(step - SKEW))
         if step < groups:
             kept[step] = inner_of(step)
-    half = mine.shape[0]
-    mine[...] = acc[:half].astype(mine.dtype)
-    send[...] = acc[half:].astype(send.dtype)
-
-
-def tiles(pieces, src_row, dst_row, table, first, second, blocks, send_dtype, name):
+    base = acc.shape[0] // 2
+    for send in sends:
+        send[...] = acc[base : base + send.shape[0]].astype(send.dtype)
+        base += send.shape[0]
+
+
+def tiles(pieces, src_row, dst_row, table, first, second, acc, parts, send_dtype, name):
     count, rank, width = first.shape
-    probes = pieces[0].shape[1]
+    blocks, probes, _ = acc.shape
     rows = sum(piece.shape[0] for piece in pieces)
-    half = (blocks // 2, probes, width)
 
     def body(*refs):
         tiles_body(len(pieces), src_row, dst_row, *refs)
 
     return local(
         body,
-        [shape(half, F32), shape(half, send_dtype)],
+        [shape(acc.shape, F32)] + [shape((blocks // 2 // parts, probes, width), send_dtype)] * parts,
         table,
+        acc,
         *pieces,
         first,
         second,
         name=name,
+        specs=[whole(pltpu.SMEM)] + [whole()] * (len(pieces) + 3),
+        aliases={1: 0},
         flops=4 * count * rank * width * probes * GROUP,
-        scratch=(2 * rows + 4 * blocks) * probes * width,
-        scratches=[
-            pltpu.SMEM(table.shape, I32),
-            pltpu.VMEM((rows, probes, width), BF16),
-            pltpu.VMEM((blocks, probes, width), F32),
-            pltpu.SemaphoreType.DMA,
-        ],
+        scratch=2 * rows * probes * width,
+        scratches=[pltpu.VMEM((rows, probes, width), BF16)],
     )
 
 
@@ -257,7 +262,8 @@
     half = cell_blocks // 2
 
     def body(*refs):
-        far, weight_far, table, weight_near, near, sems = refs[:5], refs[5], refs[6], refs[7], refs[8:13], refs[13]
+        far, weight_far, table_out, weight_near = refs[:5], refs[5], refs[6], refs[7]
+        near, table, sems = refs[8:13], refs[13], refs[14]
         me = lax.axis_index("tile")
         pairs = list(zip(far, near))
         for k in range(rest):
@@ -274,6 +280,7 @@
         spot = (away & 1) * 4 + ((away & 4) // 2) + ((away & 2) // 2)
         table[1:2, :] = (spot * rest + row_owner // 8) * station_blocks + row_local
         table[2:3, :] = rank
+        fetch([(table, table_out)], sems)
 
     return local(
         body,
@@ -282,7 +289,9 @@
         weight,
         name="plan",
         specs=[whole(pltpu.HBM)] * 6,
-        scratches=[pltpu.VMEM((peers, count), I32)] * 5 + [pltpu.SemaphoreType.DMA((5 + rest,))],
+        out_specs=[whole(pltpu.SMEM), whole()],
+        scratches=[pltpu.VMEM((peers, count), I32)] * 5
+        + [pltpu.VMEM((8, count), I32), pltpu.SemaphoreType.DMA((5 + rest,))],
         after=after,
     )
 
@@ -339,7 +348,7 @@
         (scaling,),
     )
     steps = list(zip(*orders))
-    after = (table,)
+    after = (weight,)
     for step, (bit_p, bit_q) in enumerate(steps):
         got_p = swap(part_p, bit_p)
         got_q = swap(part_q, bit_q)
@@ -354,11 +363,13 @@
     pieces = [part_p, got_p, part_q, got_q]
     pieces = pieces + [swap(piece, 1) for piece in pieces]
 
-    total, send = tiles(pieces, 0, 1, table, v_here, u_here, peers * station_blocks, F32, "forward")
-    got = swap(send, 1)
-    total, send_y, send_z, send_yz = fold(total, got, (F32, BF16, BF16, BF16))
-    sends = {2: send_y, 4: send_z, 6: send_yz}
-    total, send = plus(total, *[swap(sends[k], k) for k in SQUARE])
+    acc = zeros((peers * station_blocks, probe_count, station_width), (part_p, part_q))
+    total, *sends = tiles(pieces, 0, 1, table, v_here, u_here, acc, 4, F32, "forward")
+    quarters = [0] * 4
+    for k in SQUARE + (0,):
+        kept = F32 if k == 0 else BF16
+        quarters[k // 2] = fold(total, swap(sends[k // 2], 1), (kept,), base=k // 2 * sends[0].shape[0])[0]
+    total, send = plus(quarters[0], *[swap(quarters[k // 2], k) for k in SQUARE])
     for bit in bits[2:-1]:
         total, send = plus(total, swap(send, bit))
     weighted = weigh(total, swap(send, bits[-1]), weight)
@@ -366,9 +377,10 @@
     around = join(gots[2], gots[4], gots[6])
     pieces = [weighted, around, swap(weighted, 1), swap(around, 1)]
 
-    keep, send = tiles(pieces, 1, 0, table, u_here, v_here, peers * cell_blocks, BF16, "adjoint")
-    got = swap(send, 1)
-    keep_p, send_p, keep_q, send_q = fold(keep, got, (F32, BF16, F32, BF16))
+    acc = zeros((peers * cell_blocks, probe_count, cell_width), (total,))
+    total, send_p, send_q = tiles(pieces, 1, 0, table, u_here, v_here, acc, 2, BF16, "adjoint")
+    keep_p, send_p = fold(total, swap(send_p, 1))
+    keep_q, send_q = fold(total, swap(send_q, 1), base=total.shape[0] // 4)
     for step, (bit_p, bit_q) in enumerate(steps[::-1]):
         if step > 0:
             keep_p, send_p = fold(keep_p, got_p)
@@ -384,7 +396,7 @@
         got_q,
         scaling,
         name="final",
-        far_out=True,
+        out_specs=[whole(None)],
     )[0]
 
 

time: 83.9 us -> 81.3 us (0.969)
  waiting for transfers between devices: 42.9 us -> 39.5 us
  starting transfers between devices: 27.2 us -> 28.4 us
    ppermute x27 -> x31, waiting for transfers between devices: 42.9 us -> 39.5 us  [swap(): return lax.ppermute(array, 'tile', [(i, i ^ bits) for i in range(count)])]
    ppermute x27 -> x31, starting transfers between devices: 27.2 us -> 28.4 us  [swap(): return lax.ppermute(array, 'tile', [(i, i ^ bits) for i in range(count)])]
    pallas_call x20 -> x26, Pallas kernels: 13.4 us -> 12.9 us  [local(): pl.pallas_call(run, out_shape=[a if s.memory_space is None else s.memory_...]
  transfers between devices with their start and end apart: 27 -> 31, of which waited for: 19 -> 20; matrix products, arithmetic and copies ran while one was open for 0% -> 0% of each run, Pallas kernels for 7% -> 8%
where the time goes in v6:
time: 81.3 us; the launch traced here: 81 us
  waiting for transfers between devices  39.5 us (49%)
  starting transfers between devices  28.4 us (35%)
  Pallas kernels  12.9 us (16%)
    ppermute x31, waiting for transfers between devices, swap(): return lax.ppermute(array, 'tile', [(i, i ^ bits) for i in range(count)])  39.5 us
    ppermute x31, starting transfers between devices, swap(): return lax.ppermute(array, 'tile', [(i, i ^ bits) for i in range(count)])  28.4 us
    pallas_call x26, Pallas kernels, local(): pl.pallas_call(run, out_shape=[a if s.memory_space is None else s.memory_...  12.9 us
  transfers between devices with their start and end apart: 31, of which 20 were waited for; matrix products, arithmetic and copies ran while one was open for 0% of the time, Pallas kernels for 8%

profile of v6, /device:TPU:0, one launch (start us, length us, event | category | flops | bytes accessed | tf_op | source)
XLA Modules:
  0.0 81.0 jit_solution(11197375325282635494)
XLA Ops:
  0.0 1.1 %scale.1 = (bf16[8,8,512]{2,1,0:T(8,128)(2,1)S(1)}, bf16[8,8,512]{2,1,0:T(8,128)(2,1)S(1)}, f32[64,128]{1,0:T(8,128)S(1)}) custom-call(f32[4]{0:T(128)} %refs_0_.3, f32[64,128]{1,0:T(8,128)} %bitcast.9, s32[64,128]{1,0:T(8,128)} %bitcast.10, f32[8,8192]{1,0:T(8,128)} %refs_3_.1), custom_call_target="tpu_custom_call" | custom-call | bytes 491536 | tf_op jit(solution)/shard_map/scale/pallas_call | solution.py:49
  1.1 4.1 %collective-permute-start.2 = (bf16[8,8,512]{2,1,0:T(8,128)(2,1)S(1)}, bf16[8,8,512]{2,1,0:T(8,128)(2,1)S(1)}, u32[]{:S(2)}, u32[]{:S(2)}) collective-permute-start(bf16[8,8,512]{2,1,0:T(8,128)(2,1)S(1)} %get-tuple-element.36.refs_0_), channel_id=1, source_target_pairs={{0,8},{1,9},{2,10},{3,11},{4,12},{5,13},{6,14},{7,15},{8,0},{9,1},... | collective-permute-start | bytes 196616 | tf_op jit(solution)/shard_map/ppermute | solution.py:34
  5.2 1.5 %collective-permute-start = (bf16[8,8,512]{2,1,0:T(8,128)(2,1)S(1)}, bf16[8,8,512]{2,1,0:T(8,128)(2,1)S(1)}, u32[]{:S(2)}, u32[]{:S(2)}) collective-permute-start(bf16[8,8,512]{2,1,0:T(8,128)(2,1)S(1)} %get-tuple-element.34.refs_0_), channel_id=1, source_target_pairs={{0,2},{1,3},{2,0},{3,1},{4,6},{5,7},{6,4},{7,5},{8,10},{9,11},{10,... | collective-permute-start | bytes 196616 | tf_op jit(solution)/shard_map/ppermute | solution.py:34
  6.7 1.5 %plan.1 = (s32[8,128]{1,0:T(8,128)S(4)}, f32[32,128]{1,0:T(8,128)S(1)}) custom-call(s32[16,128]{1,0:T(8,128)} %bitcast.11, s32[16,128]{1,0:T(8,128)} %bitcast.12, s32[16,128]{1,0:T(8,128)} %bitcast.13, s32[16,128]{1,0:T(8,128)} %bitcast.14, s32[16,128]{1,0:T(8,128)} %bitcast.15, f32[256,128]{1,0:T(8,128)} %bitcast.8, ...), custom_call_target="tpu_custom_call" | custom-call | bytes 192512 | tf_op jit(solution)/shard_map/plan/pallas_call | solution.py:49
  8.2 0.7 collective-permute-done.2.refs_1_
  8.8 1.0 %collective-permute-start.3 = (bf16[16,8,512]{2,1,0:T(8,128)(2,1)S(1)}, bf16[16,8,512]{2,1,0:T(8,128)(2,1)S(1)}, u32[]{:S(2)}, u32[]{:S(2)}) collective-permute-start(bf16[16,8,512]{2,1,0:T(8,128)(2,1)S(1)} %join.6.refs_2_.refs_0_), channel_id=1, source_target_pairs={{0,4},{1,5},{2,6},{3,7},{4,0},{5,1},{6,2},{7,3},{8,12},{9,13},{10,... | collective-permute-start | bytes 393224 | tf_op jit(solution)/shard_map/ppermute | solution.py:34
  9.9 3.1 %collective-permute-start.1 = (bf16[16,8,512]{2,1,0:T(8,128)(2,1)S(1)}, bf16[16,8,512]{2,1,0:T(8,128)(2,1)S(1)}, u32[]{:S(2)}, u32[]{:S(2)}) collective-permute-start(bf16[16,8,512]{2,1,0:T(8,128)(2,1)S(1)} %join.5.refs_1_.refs_0_), channel_id=1, source_target_pairs={{0,8},{1,9},{2,10},{3,11},{4,12},{5,13},{6,14},{7,15},{8,0},{9,1},... | collective-permute-start | bytes 393224 | tf_op jit(solution)/shard_map/ppermute | solution.py:34
  12.9 2.2 %load_v.1.refs_3_.refs_10_.refs_7_ = bf16[128,32,512]{2,1,0:T(8,128)(2,1)S(1)} custom-call(bf16[128,32,512]{2,1,0:T(8,128)(2,1)} %refs_0_.4, bf16[16,8,512]{2,1,0:T(8,128)(2,1)S(1)} %join.5.refs_1_.refs_0_, bf16[16,8,512]{2,1,0:T(8,128)(2,1)S(1)} %join.6.refs_2_.refs_0_), custom_call_target="tpu_custom_call" | custom-call | bytes 8388608 | tf_op jit(solution)/shard_map/load_v/pallas_call | solution.py:49
  15.2 2.2 %load_u.1.refs_2_.refs_11_.refs_6_ = bf16[128,32,512]{2,1,0:T(8,128)(2,1)S(1)} custom-call(bf16[128,32,512]{2,1,0:T(8,128)(2,1)} %refs_0_.5, bf16[16,8,512]{2,1,0:T(8,128)(2,1)S(1)} %join.5.refs_1_.refs_0_, bf16[16,8,512]{2,1,0:T(8,128)(2,1)S(1)} %join.6.refs_2_.refs_0_, bf16[128,32,512]{2,1,0:T(8,128)(2,1)S(1)} %load_v.1.refs_3_.refs_10_.refs_7_), custom_call_target="tpu_custom_call" | custom-call | bytes 8388608 | tf_op jit(solution)/shard_map/load_u/pallas_call | solution.py:49
  17.4 1.6 %collective-permute-start.5 = (bf16[32,8,512]{2,1,0:T(8,128)(2,1)S(1)}, bf16[32,8,512]{2,1,0:T(8,128)(2,1)S(1)}, u32[]{:S(2)}, u32[]{:S(2)}) collective-permute-start(bf16[32,8,512]{2,1,0:T(8,128)(2,1)S(1)} %join.8.refs_1_.refs_4_), channel_id=1, source_target_pairs={{0,2},{1,3},{2,0},{3,1},{4,6},{5,7},{6,4},{7,5},{8,10},{9,11},{10,... | collective-permute-start | bytes 786440 | tf_op jit(solution)/shard_map/ppermute | solution.py:34
  19.2 0.5 collective-permute-start.6
  19.7 5.1 %collective-permute-done.5.refs_5_ = bf16[32,8,512]{2,1,0:T(8,128)(2,1)S(1)} collective-permute-done((bf16[32,8,512]{2,1,0:T(8,128)(2,1)S(1)}, bf16[32,8,512]{2,1,0:T(8,128)(2,1)S(1)}, u32[]{:S(2)}, u32[]{:S(2)}) %collective-permute-start.5) | collective-permute-done | bytes 262176 | tf_op jit(solution)/shard_map/ppermute | solution.py:34
  24.8 1.3 %collective-permute-done.4.refs_3_ = bf16[32,8,512]{2,1,0:T(8,128)(2,1)S(1)} collective-permute-done((bf16[32,8,512]{2,1,0:T(8,128)(2,1)S(1)}, bf16[32,8,512]{2,1,0:T(8,128)(2,1)S(1)}, u32[]{:S(2)}, u32[]{:S(2)}) %collective-permute-start.4) | collective-permute-done | bytes 262176 | tf_op jit(solution)/shard_map/ppermute | solution.py:34
  26.3 1.3 %collective-permute-done.7.refs_7_ = bf16[32,8,512]{2,1,0:T(8,128)(2,1)S(1)} collective-permute-done((bf16[32,8,512]{2,1,0:T(8,128)(2,1)S(1)}, bf16[32,8,512]{2,1,0:T(8,128)(2,1)S(1)}, u32[]{:S(2)}, u32[]{:S(2)}) %collective-permute-start.7) | collective-permute-done | bytes 262176 | tf_op jit(solution)/shard_map/ppermute | solution.py:34
  27.7 2.2 %forward.1 = (f32[64,8,512]{2,1,0:T(8,128)S(1)}, f32[8,8,512]{2,1,0:T(8,128)S(1)}, f32[8,8,512]{2,1,0:T(8,128)S(1)}, f32[8,8,512]{2,1,0:T(8,128)S(1)}, f32[8,8,512]{2,1,0:T(8,128)S(1)}) custom-call(s32[8,128]{1,0:T(8,128)S(4)} %get-tuple-element.33.refs_0_, f32[64,8,512]{2,1,0:T(8,128)S(1)} %zeros.2.refs_1_, ...), custom_call_target="tpu_custom_call", output_to_operand_aliasing={{0}: (1, {})} | custom-call | flops 536870912 | bytes 13111296 | tf_op jit(solution)/shard_map/forward/pallas_call | solution.py:49
  30.1 0.4 collective-permute-start.13
  30.6 0.4 collective-permute-start.10
  31.0 0.3 collective-permute-done.11.refs_1_
  31.3 1.3 %collective-permute-start.12 = (bf16[8,8,512]{2,1,0:T(8,128)(2,1)S(1)}, bf16[8,8,512]{2,1,0:T(8,128)(2,1)S(1)}, u32[]{:S(2)}, u32[]{:S(2)}) collective-permute-start(bf16[8,8,512]{2,1,0:T(8,128)(2,1)S(1)} %fold.11), channel_id=1, source_target_pairs={{0,6},{1,7},{2,4},{3,5},{4,2},{5,3},{6,0},{7,1},{8,14},{9,15},{10,... | collective-permute-start | bytes 196616 | tf_op jit(solution)/shard_map/ppermute | solution.py:34
  32.6 0.6 collective-permute-start.14
  33.2 1.8 %collective-permute-start.16 = (bf16[8,8,512]{2,1,0:T(8,128)(2,1)S(1)}, bf16[8,8,512]{2,1,0:T(8,128)(2,1)S(1)}, u32[]{:S(2)}, u32[]{:S(2)}) collective-permute-start(bf16[8,8,512]{2,1,0:T(8,128)(2,1)S(1)} %fold.13), channel_id=1, source_target_pairs={{0,4},{1,5},{2,6},{3,7},{4,0},{5,1},{6,2},{7,3},{8,12},{9,13},{10,... | collective-permute-start | bytes 196616 | tf_op jit(solution)/shard_map/ppermute | solution.py:34
  35.1 1.7 %collective-permute-done.12.refs_1_ = bf16[8,8,512]{2,1,0:T(8,128)(2,1)S(1)} collective-permute-done((bf16[8,8,512]{2,1,0:T(8,128)(2,1)S(1)}, bf16[8,8,512]{2,1,0:T(8,128)(2,1)S(1)}, u32[]{:S(2)}, u32[]{:S(2)}) %collective-permute-start.12) | collective-permute-done | bytes 65568 | tf_op jit(solution)/shard_map/ppermute | solution.py:34
  36.8 1.1 %collective-permute-done.14.refs_2_ = bf16[8,8,512]{2,1,0:T(8,128)(2,1)S(1)} collective-permute-done((bf16[8,8,512]{2,1,0:T(8,128)(2,1)S(1)}, bf16[8,8,512]{2,1,0:T(8,128)(2,1)S(1)}, u32[]{:S(2)}, u32[]{:S(2)}) %collective-permute-start.14) | collective-permute-done | bytes 65568 | tf_op jit(solution)/shard_map/ppermute | solution.py:34
  37.9 2.3 %collective-permute-start.17 = (bf16[8,8,512]{2,1,0:T(8,128)(2,1)S(1)}, bf16[8,8,512]{2,1,0:T(8,128)(2,1)S(1)}, u32[]{:S(2)}, u32[]{:S(2)}) collective-permute-start(bf16[8,8,512]{2,1,0:T(8,128)(2,1)S(1)} %get-tuple-element.43), channel_id=1, source_target_pairs={{0,8},{1,9},{2,10},{3,11},{4,12},{5,13},{6,14},{7,15},{8,0},{9,1},... | collective-permute-start | bytes 196616 | tf_op jit(solution)/shard_map/ppermute | solution.py:34
  40.2 3.0 %collective-permute-done.17.refs_1_ = bf16[8,8,512]{2,1,0:T(8,128)(2,1)S(1)} collective-permute-done((bf16[8,8,512]{2,1,0:T(8,128)(2,1)S(1)}, bf16[8,8,512]{2,1,0:T(8,128)(2,1)S(1)}, u32[]{:S(2)}, u32[]{:S(2)}) %collective-permute-start.17) | collective-permute-done | bytes 65568 | tf_op jit(solution)/shard_map/ppermute | solution.py:34
  43.2 1.7 %collective-permute-start.20 = (bf16[8,8,512]{2,1,0:T(8,128)(2,1)S(1)}, bf16[8,8,512]{2,1,0:T(8,128)(2,1)S(1)}, u32[]{:S(2)}, u32[]{:S(2)}) collective-permute-start(bf16[8,8,512]{2,1,0:T(8,128)(2,1)S(1)} %weigh.1.refs_2_), channel_id=1, source_target_pairs={{0,6},{1,7},{2,4},{3,5},{4,2},{5,3},{6,0},{7,1},{8,14},{9,15},{10,... | collective-permute-start | bytes 196616 | tf_op jit(solution)/shard_map/ppermute | solution.py:34
  44.9 1.7 %collective-permute-start.19 = (bf16[8,8,512]{2,1,0:T(8,128)(2,1)S(1)}, bf16[8,8,512]{2,1,0:T(8,128)(2,1)S(1)}, u32[]{:S(2)}, u32[]{:S(2)}) collective-permute-start(bf16[8,8,512]{2,1,0:T(8,128)(2,1)S(1)} %weigh.1.refs_2_), channel_id=1, source_target_pairs={{0,4},{1,5},{2,6},{3,7},{4,0},{5,1},{6,2},{7,3},{8,12},{9,13},{10,... | collective-permute-start | bytes 196616 | tf_op jit(solution)/shard_map/ppermute | solution.py:34
  46.8 1.7 %collective-permute-done.20.refs_2_ = bf16[8,8,512]{2,1,0:T(8,128)(2,1)S(1)} collective-permute-done((bf16[8,8,512]{2,1,0:T(8,128)(2,1)S(1)}, bf16[8,8,512]{2,1,0:T(8,128)(2,1)S(1)}, u32[]{:S(2)}, u32[]{:S(2)}) %collective-permute-start.20) | collective-permute-done | bytes 65568 | tf_op jit(solution)/shard_map/ppermute | solution.py:34
  48.4 1.1 %collective-permute-done.19.refs_1_ = bf16[8,8,512]{2,1,0:T(8,128)(2,1)S(1)} collective-permute-done((bf16[8,8,512]{2,1,0:T(8,128)(2,1)S(1)}, bf16[8,8,512]{2,1,0:T(8,128)(2,1)S(1)}, u32[]{:S(2)}, u32[]{:S(2)}) %collective-permute-start.19) | collective-permute-done | bytes 65568 | tf_op jit(solution)/shard_map/ppermute | solution.py:34
  49.5 1.3 %collective-permute-done.18.refs_0_ = bf16[8,8,512]{2,1,0:T(8,128)(2,1)S(1)} collective-permute-done((bf16[8,8,512]{2,1,0:T(8,128)(2,1)S(1)}, bf16[8,8,512]{2,1,0:T(8,128)(2,1)S(1)}, u32[]{:S(2)}, u32[]{:S(2)}) %collective-permute-start.18) | collective-permute-done | bytes 65568 | tf_op jit(solution)/shard_map/ppermute | solution.py:34
  50.9 0.5 collective-permute-start.21
  51.7 0.7 collective-permute-done.21.refs_4_
  52.4 2.2 %adjoint.1 = (f32[256,8,512]{2,1,0:T(8,128)S(1)}, bf16[64,8,512]{2,1,0:T(8,128)(2,1)S(1)}, bf16[64,8,512]{2,1,0:T(8,128)(2,1)S(1)}) custom-call(s32[8,128]{1,0:T(8,128)S(4)} %get-tuple-element.33.refs_0_, f32[256,8,512]{2,1,0:T(8,128)S(1)} %zeros.3.refs_1_, bf16[8,8,512]{2,1,0:T(8,128)(2,1)S(1)} %weigh.1.refs_2_, ...), custom_call_target="tpu_custom_call", output_to_operand_aliasing={{0}: (1, {})} | custom-call | flops 536870912 | bytes 18354176 | tf_op jit(solution)/shard_map/adjoint/pallas_call | solution.py:49
  54.6 0.3 collective-permute-start.23
  54.9 0.3 collective-permute-start.27
  55.2 1.4 %collective-permute-done.23.refs_1_ = bf16[64,8,512]{2,1,0:T(8,128)(2,1)S(1)} collective-permute-done((bf16[64,8,512]{2,1,0:T(8,128)(2,1)S(1)}, bf16[64,8,512]{2,1,0:T(8,128)(2,1)S(1)}, u32[]{:S(2)}, u32[]{:S(2)}) %collective-permute-start.23) | collective-permute-done | bytes 524320 | tf_op jit(solution)/shard_map/ppermute | solution.py:34
  56.7 0.4 collective-permute-start.24
  57.4 1.1 %collective-permute-start.28 = (bf16[32,8,512]{2,1,0:T(8,128)(2,1)S(1)}, bf16[32,8,512]{2,1,0:T(8,128)(2,1)S(1)}, u32[]{:S(2)}, u32[]{:S(2)}) collective-permute-start(bf16[32,8,512]{2,1,0:T(8,128)(2,1)S(1)} %get-tuple-element.54), channel_id=1, source_target_pairs={{0,2},{1,3},{2,0},{3,1},{4,6},{5,7},{6,4},{7,5},{8,10},{9,11},{10,... | collective-permute-start | bytes 786440 | tf_op jit(solution)/shard_map/ppermute | solution.py:34
  58.5 6.7 %collective-permute-done.24.refs_1_ = bf16[32,8,512]{2,1,0:T(8,128)(2,1)S(1)} collective-permute-done((bf16[32,8,512]{2,1,0:T(8,128)(2,1)S(1)}, bf16[32,8,512]{2,1,0:T(8,128)(2,1)S(1)}, u32[]{:S(2)}, u32[]{:S(2)}) %collective-permute-start.24) | collective-permute-done | bytes 262176 | tf_op jit(solution)/shard_map/ppermute | solution.py:34
  65.3 1.9 %collective-permute-start.25 = (bf16[16,8,512]{2,1,0:T(8,128)(2,1)S(1)}, bf16[16,8,512]{2,1,0:T(8,128)(2,1)S(1)}, u32[]{:S(2)}, u32[]{:S(2)}) collective-permute-start(bf16[16,8,512]{2,1,0:T(8,128)(2,1)S(1)} %get-tuple-element.49), channel_id=1, source_target_pairs={{0,8},{1,9},{2,10},{3,11},{4,12},{5,13},{6,14},{7,15},{8,0},{9,1},... | collective-permute-start | bytes 393224 | tf_op jit(solution)/shard_map/ppermute | solution.py:34
  67.2 0.4 collective-permute-start.29
  67.6 6.1 %collective-permute-done.25.refs_1_ = bf16[16,8,512]{2,1,0:T(8,128)(2,1)S(1)} collective-permute-done((bf16[16,8,512]{2,1,0:T(8,128)(2,1)S(1)}, bf16[16,8,512]{2,1,0:T(8,128)(2,1)S(1)}, u32[]{:S(2)}, u32[]{:S(2)}) %collective-permute-start.25) | collective-permute-done | bytes 131104 | tf_op jit(solution)/shard_map/ppermute | solution.py:34
  73.7 0.5 collective-permute-start.26
  74.2 0.4 collective-permute-done.29.refs_1_
  74.6 0.5 collective-permute-start.30
  75.0 3.0 %collective-permute-done.26.refs_1_ = bf16[8,8,512]{2,1,0:T(8,128)(2,1)S(1)} collective-permute-done((bf16[8,8,512]{2,1,0:T(8,128)(2,1)S(1)}, bf16[8,8,512]{2,1,0:T(8,128)(2,1)S(1)}, u32[]{:S(2)}, u32[]{:S(2)}) %collective-permute-start.26) | collective-permute-done | bytes 65568 | tf_op jit(solution)/shard_map/ppermute | solution.py:34
  78.0 2.2 %collective-permute-done.30.refs_3_ = bf16[8,8,512]{2,1,0:T(8,128)(2,1)S(1)} collective-permute-done((bf16[8,8,512]{2,1,0:T(8,128)(2,1)S(1)}, bf16[8,8,512]{2,1,0:T(8,128)(2,1)S(1)}, u32[]{:S(2)}, u32[]{:S(2)}) %collective-permute-start.30) | collective-permute-done | bytes 65568 | tf_op jit(solution)/shard_map/ppermute | solution.py:34
  80.2 0.7 final.1
  (40 shorter events, 2.0 us)
Async XLA Ops:
  1.1 7.8 %collective-permute-start.2 = (bf16[8,8,512]{2,1,0:T(8,128)(2,1)S(1)}, bf16[8,8,512]{2,1,0:T(8,128)(2,1)S(1)}, u32[]{:S(2)}, u32[]{:S(2)}) collective-permute-start(bf16[8,8,512]{2,1,0:T(8,128)(2,1)S(1)} %get-tuple-element.36.refs_0_), channel_id=1, source_target_pairs={{0,8},{1,9},{2,10},{3,11},{4,12},{5,13},{6,14},{7,15},{8,0},{9,1},... | collective-permute-start | bytes 196616 | tf_op jit(solution)/shard_map/ppermute | solution.py:34
  5.2 4.7 %collective-permute-start = (bf16[8,8,512]{2,1,0:T(8,128)(2,1)S(1)}, bf16[8,8,512]{2,1,0:T(8,128)(2,1)S(1)}, u32[]{:S(2)}, u32[]{:S(2)}) collective-permute-start(bf16[8,8,512]{2,1,0:T(8,128)(2,1)S(1)} %get-tuple-element.34.refs_0_), channel_id=1, source_target_pairs={{0,2},{1,3},{2,0},{3,1},{4,6},{5,7},{6,4},{7,5},{8,10},{9,11},{10,... | collective-permute-start | bytes 196616 | tf_op jit(solution)/shard_map/ppermute | solution.py:34
  8.8 8.5 %collective-permute-start.3 = (bf16[16,8,512]{2,1,0:T(8,128)(2,1)S(1)}, bf16[16,8,512]{2,1,0:T(8,128)(2,1)S(1)}, u32[]{:S(2)}, u32[]{:S(2)}) collective-permute-start(bf16[16,8,512]{2,1,0:T(8,128)(2,1)S(1)} %join.6.refs_2_.refs_0_), channel_id=1, source_target_pairs={{0,4},{1,5},{2,6},{3,7},{4,0},{5,1},{6,2},{7,3},{8,12},{9,13},{10,... | collective-permute-start | bytes 393224 | tf_op jit(solution)/shard_map/ppermute | solution.py:34
  9.9 9.1 %collective-permute-start.1 = (bf16[16,8,512]{2,1,0:T(8,128)(2,1)S(1)}, bf16[16,8,512]{2,1,0:T(8,128)(2,1)S(1)}, u32[]{:S(2)}, u32[]{:S(2)}) collective-permute-start(bf16[16,8,512]{2,1,0:T(8,128)(2,1)S(1)} %join.5.refs_1_.refs_0_), channel_id=1, source_target_pairs={{0,8},{1,9},{2,10},{3,11},{4,12},{5,13},{6,14},{7,15},{8,0},{9,1},... | collective-permute-start | bytes 393224 | tf_op jit(solution)/shard_map/ppermute | solution.py:34
  17.4 7.4 %collective-permute-start.5 = (bf16[32,8,512]{2,1,0:T(8,128)(2,1)S(1)}, bf16[32,8,512]{2,1,0:T(8,128)(2,1)S(1)}, u32[]{:S(2)}, u32[]{:S(2)}) collective-permute-start(bf16[32,8,512]{2,1,0:T(8,128)(2,1)S(1)} %join.8.refs_1_.refs_4_), channel_id=1, source_target_pairs={{0,2},{1,3},{2,0},{3,1},{4,6},{5,7},{6,4},{7,5},{8,10},{9,11},{10,... | collective-permute-start | bytes 786440 | tf_op jit(solution)/shard_map/ppermute | solution.py:34
  19.0 7.1 %collective-permute-start.4 = (bf16[32,8,512]{2,1,0:T(8,128)(2,1)S(1)}, bf16[32,8,512]{2,1,0:T(8,128)(2,1)S(1)}, u32[]{:S(2)}, u32[]{:S(2)}) collective-permute-start(bf16[32,8,512]{2,1,0:T(8,128)(2,1)S(1)} %join.7.refs_0_.refs_2_), channel_id=1, source_target_pairs={{0,4},{1,5},{2,6},{3,7},{4,0},{5,1},{6,2},{7,3},{8,12},{9,13},{10,... | collective-permute-start | bytes 786440 | tf_op jit(solution)/shard_map/ppermute | solution.py:34
  19.2 7.0 %collective-permute-start.8 = (bf16[32,8,512]{2,1,0:T(8,128)(2,1)S(1)}, bf16[32,8,512]{2,1,0:T(8,128)(2,1)S(1)}, u32[]{:S(2)}, u32[]{:S(2)}) collective-permute-start(bf16[32,8,512]{2,1,0:T(8,128)(2,1)S(1)} %join.8.refs_1_.refs_4_), channel_id=1, source_target_pairs={{0,1},{1,0},{2,3},{3,2},{4,5},{5,4},{6,7},{7,6},{8,9},{9,8},{10,11... | collective-permute-start | bytes 786440 | tf_op jit(solution)/shard_map/ppermute | solution.py:34
  19.2 7.0 %collective-permute-start.6 = (bf16[32,8,512]{2,1,0:T(8,128)(2,1)S(1)}, bf16[32,8,512]{2,1,0:T(8,128)(2,1)S(1)}, u32[]{:S(2)}, u32[]{:S(2)}) collective-permute-start(bf16[32,8,512]{2,1,0:T(8,128)(2,1)S(1)} %join.7.refs_0_.refs_2_), channel_id=1, source_target_pairs={{0,1},{1,0},{2,3},{3,2},{4,5},{5,4},{6,7},{7,6},{8,9},{9,8},{10,11... | collective-permute-start | bytes 786440 | tf_op jit(solution)/shard_map/ppermute | solution.py:34
  24.8 1.5 %collective-permute-start.9 = (bf16[32,8,512]{2,1,0:T(8,128)(2,1)S(1)}, bf16[32,8,512]{2,1,0:T(8,128)(2,1)S(1)}, u32[]{:S(2)}, u32[]{:S(2)}) collective-permute-start(bf16[32,8,512]{2,1,0:T(8,128)(2,1)S(1)} %collective-permute-done.5.refs_5_), channel_id=1, source_target_pairs={{0,1},{1,0},{2,3},{3,2},{4,5},{5,4},{6,7},{7,6},{8,9},{9,8},{10,11... | collective-permute-start | bytes 786440 | tf_op jit(solution)/shard_map/ppermute | solution.py:34
  26.1 1.5 %collective-permute-start.7 = (bf16[32,8,512]{2,1,0:T(8,128)(2,1)S(1)}, bf16[32,8,512]{2,1,0:T(8,128)(2,1)S(1)}, u32[]{:S(2)}, u32[]{:S(2)}) collective-permute-start(bf16[32,8,512]{2,1,0:T(8,128)(2,1)S(1)} %collective-permute-done.4.refs_3_), channel_id=1, source_target_pairs={{0,1},{1,0},{2,3},{3,2},{4,5},{5,4},{6,7},{7,6},{8,9},{9,8},{10,11... | collective-permute-start | bytes 786440 | tf_op jit(solution)/shard_map/ppermute | solution.py:34
  29.9 1.4 %collective-permute-start.11 = (f32[8,8,512]{2,1,0:T(8,128)S(1)}, f32[8,8,512]{2,1,0:T(8,128)S(1)}, u32[]{:S(2)}, u32[]{:S(2)}) collective-permute-start(f32[8,8,512]{2,1,0:T(8,128)S(1)} %get-tuple-element.39), channel_id=1, source_target_pairs={{0,1},{1,0},{2,3},{3,2},{4,5},{5,4},{6,7},{7,6},{8,9},{9,8},{10,11... | collective-permute-start | bytes 393224 | tf_op jit(solution)/shard_map/ppermute | solution.py:34
  30.1 2.5 %collective-permute-start.13 = (f32[8,8,512]{2,1,0:T(8,128)S(1)}, f32[8,8,512]{2,1,0:T(8,128)S(1)}, u32[]{:S(2)}, u32[]{:S(2)}) collective-permute-start(f32[8,8,512]{2,1,0:T(8,128)S(1)} %get-tuple-element.40), channel_id=1, source_target_pairs={{0,1},{1,0},{2,3},{3,2},{4,5},{5,4},{6,7},{7,6},{8,9},{9,8},{10,11... | collective-permute-start | bytes 393224 | tf_op jit(solution)/shard_map/ppermute | solution.py:34
  30.4 2.8 %collective-permute-start.15 = (f32[8,8,512]{2,1,0:T(8,128)S(1)}, f32[8,8,512]{2,1,0:T(8,128)S(1)}, u32[]{:S(2)}, u32[]{:S(2)}) collective-permute-start(f32[8,8,512]{2,1,0:T(8,128)S(1)} %get-tuple-element.41), channel_id=1, source_target_pairs={{0,1},{1,0},{2,3},{3,2},{4,5},{5,4},{6,7},{7,6},{8,9},{9,8},{10,11... | collective-permute-start | bytes 393224 | tf_op jit(solution)/shard_map/ppermute | solution.py:34
  30.6 4.5 %collective-permute-start.10 = (f32[8,8,512]{2,1,0:T(8,128)S(1)}, f32[8,8,512]{2,1,0:T(8,128)S(1)}, u32[]{:S(2)}, u32[]{:S(2)}) collective-permute-start(f32[8,8,512]{2,1,0:T(8,128)S(1)} %get-tuple-element.38), channel_id=1, source_target_pairs={{0,1},{1,0},{2,3},{3,2},{4,5},{5,4},{6,7},{7,6},{8,9},{9,8},{10,11... | collective-permute-start | bytes 393224 | tf_op jit(solution)/shard_map/ppermute | solution.py:34
  31.3 5.4 %collective-permute-start.12 = (bf16[8,8,512]{2,1,0:T(8,128)(2,1)S(1)}, bf16[8,8,512]{2,1,0:T(8,128)(2,1)S(1)}, u32[]{:S(2)}, u32[]{:S(2)}) collective-permute-start(bf16[8,8,512]{2,1,0:T(8,128)(2,1)S(1)} %fold.11), channel_id=1, source_target_pairs={{0,6},{1,7},{2,4},{3,5},{4,2},{5,3},{6,0},{7,1},{8,14},{9,15},{10,... | collective-permute-start | bytes 196616 | tf_op jit(solution)/shard_map/ppermute | solution.py:34
  32.6 5.2 %collective-permute-start.14 = (bf16[8,8,512]{2,1,0:T(8,128)(2,1)S(1)}, bf16[8,8,512]{2,1,0:T(8,128)(2,1)S(1)}, u32[]{:S(2)}, u32[]{:S(2)}) collective-permute-start(bf16[8,8,512]{2,1,0:T(8,128)(2,1)S(1)} %fold.12), channel_id=1, source_target_pairs={{0,2},{1,3},{2,0},{3,1},{4,6},{5,7},{6,4},{7,5},{8,10},{9,11},{10,... | collective-permute-start | bytes 196616 | tf_op jit(solution)/shard_map/ppermute | solution.py:34
  33.2 4.6 %collective-permute-start.16 = (bf16[8,8,512]{2,1,0:T(8,128)(2,1)S(1)}, bf16[8,8,512]{2,1,0:T(8,128)(2,1)S(1)}, u32[]{:S(2)}, u32[]{:S(2)}) collective-permute-start(bf16[8,8,512]{2,1,0:T(8,128)(2,1)S(1)} %fold.13), channel_id=1, source_target_pairs={{0,4},{1,5},{2,6},{3,7},{4,0},{5,1},{6,2},{7,3},{8,12},{9,13},{10,... | collective-permute-start | bytes 196616 | tf_op jit(solution)/shard_map/ppermute | solution.py:34
  37.9 5.3 %collective-permute-start.17 = (bf16[8,8,512]{2,1,0:T(8,128)(2,1)S(1)}, bf16[8,8,512]{2,1,0:T(8,128)(2,1)S(1)}, u32[]{:S(2)}, u32[]{:S(2)}) collective-permute-start(bf16[8,8,512]{2,1,0:T(8,128)(2,1)S(1)} %get-tuple-element.43), channel_id=1, source_target_pairs={{0,8},{1,9},{2,10},{3,11},{4,12},{5,13},{6,14},{7,15},{8,0},{9,1},... | collective-permute-start | bytes 196616 | tf_op jit(solution)/shard_map/ppermute | solution.py:34
  43.2 5.2 %collective-permute-start.20 = (bf16[8,8,512]{2,1,0:T(8,128)(2,1)S(1)}, bf16[8,8,512]{2,1,0:T(8,128)(2,1)S(1)}, u32[]{:S(2)}, u32[]{:S(2)}) collective-permute-start(bf16[8,8,512]{2,1,0:T(8,128)(2,1)S(1)} %weigh.1.refs_2_), channel_id=1, source_target_pairs={{0,6},{1,7},{2,4},{3,5},{4,2},{5,3},{6,0},{7,1},{8,14},{9,15},{10,... | collective-permute-start | bytes 196616 | tf_op jit(solution)/shard_map/ppermute | solution.py:34
  44.9 4.6 %collective-permute-start.19 = (bf16[8,8,512]{2,1,0:T(8,128)(2,1)S(1)}, bf16[8,8,512]{2,1,0:T(8,128)(2,1)S(1)}, u32[]{:S(2)}, u32[]{:S(2)}) collective-permute-start(bf16[8,8,512]{2,1,0:T(8,128)(2,1)S(1)} %weigh.1.refs_2_), channel_id=1, source_target_pairs={{0,4},{1,5},{2,6},{3,7},{4,0},{5,1},{6,2},{7,3},{8,12},{9,13},{10,... | collective-permute-start | bytes 196616 | tf_op jit(solution)/shard_map/ppermute | solution.py:34
  46.6 4.3 %collective-permute-start.18 = (bf16[8,8,512]{2,1,0:T(8,128)(2,1)S(1)}, bf16[8,8,512]{2,1,0:T(8,128)(2,1)S(1)}, u32[]{:S(2)}, u32[]{:S(2)}) collective-permute-start(bf16[8,8,512]{2,1,0:T(8,128)(2,1)S(1)} %weigh.1.refs_2_), channel_id=1, source_target_pairs={{0,2},{1,3},{2,0},{3,1},{4,6},{5,7},{6,4},{7,5},{8,10},{9,11},{10,... | collective-permute-start | bytes 196616 | tf_op jit(solution)/shard_map/ppermute | solution.py:34
  50.8 1.6 %collective-permute-start.22 = (bf16[24,8,512]{2,1,0:T(8,128)(2,1)S(1)}, bf16[24,8,512]{2,1,0:T(8,128)(2,1)S(1)}, u32[]{:S(2)}, u32[]{:S(2)}) collective-permute-start(bf16[24,8,512]{2,1,0:T(8,128)(2,1)S(1)} %join.9.refs_3_), channel_id=1, source_target_pairs={{0,1},{1,0},{2,3},{3,2},{4,5},{5,4},{6,7},{7,6},{8,9},{9,8},{10,11... | collective-permute-start | bytes 589832 | tf_op jit(solution)/shard_map/ppermute | solution.py:34
  50.9 1.5 %collective-permute-start.21 = (bf16[8,8,512]{2,1,0:T(8,128)(2,1)S(1)}, bf16[8,8,512]{2,1,0:T(8,128)(2,1)S(1)}, u32[]{:S(2)}, u32[]{:S(2)}) collective-permute-start(bf16[8,8,512]{2,1,0:T(8,128)(2,1)S(1)} %weigh.1.refs_2_), channel_id=1, source_target_pairs={{0,1},{1,0},{2,3},{3,2},{4,5},{5,4},{6,7},{7,6},{8,9},{9,8},{10,11... | collective-permute-start | bytes 196616 | tf_op jit(solution)/shard_map/ppermute | solution.py:34
  54.6 2.0 %collective-permute-start.23 = (bf16[64,8,512]{2,1,0:T(8,128)(2,1)S(1)}, bf16[64,8,512]{2,1,0:T(8,128)(2,1)S(1)}, u32[]{:S(2)}, u32[]{:S(2)}) collective-permute-start(bf16[64,8,512]{2,1,0:T(8,128)(2,1)S(1)} %get-tuple-element.45), channel_id=1, source_target_pairs={{0,1},{1,0},{2,3},{3,2},{4,5},{5,4},{6,7},{7,6},{8,9},{9,8},{10,11... | collective-permute-start | bytes 1572872 | tf_op jit(solution)/shard_map/ppermute | solution.py:34
  54.9 2.4 %collective-permute-start.27 = (bf16[64,8,512]{2,1,0:T(8,128)(2,1)S(1)}, bf16[64,8,512]{2,1,0:T(8,128)(2,1)S(1)}, u32[]{:S(2)}, u32[]{:S(2)}) collective-permute-start(bf16[64,8,512]{2,1,0:T(8,128)(2,1)S(1)} %get-tuple-element.52), channel_id=1, source_target_pairs={{0,1},{1,0},{2,3},{3,2},{4,5},{5,4},{6,7},{7,6},{8,9},{9,8},{10,11... | collective-permute-start | bytes 1572872 | tf_op jit(solution)/shard_map/ppermute | solution.py:34
  56.7 8.5 %collective-permute-start.24 = (bf16[32,8,512]{2,1,0:T(8,128)(2,1)S(1)}, bf16[32,8,512]{2,1,0:T(8,128)(2,1)S(1)}, u32[]{:S(2)}, u32[]{:S(2)}) collective-permute-start(bf16[32,8,512]{2,1,0:T(8,128)(2,1)S(1)} %get-tuple-element.47), channel_id=1, source_target_pairs={{0,4},{1,5},{2,6},{3,7},{4,0},{5,1},{6,2},{7,3},{8,12},{9,13},{10,... | collective-permute-start | bytes 786440 | tf_op jit(solution)/shard_map/ppermute | solution.py:34
  57.4 9.7 %collective-permute-start.28 = (bf16[32,8,512]{2,1,0:T(8,128)(2,1)S(1)}, bf16[32,8,512]{2,1,0:T(8,128)(2,1)S(1)}, u32[]{:S(2)}, u32[]{:S(2)}) collective-permute-start(bf16[32,8,512]{2,1,0:T(8,128)(2,1)S(1)} %get-tuple-element.54), channel_id=1, source_target_pairs={{0,2},{1,3},{2,0},{3,1},{4,6},{5,7},{6,4},{7,5},{8,10},{9,11},{10,... | collective-permute-start | bytes 786440 | tf_op jit(solution)/shard_map/ppermute | solution.py:34
  65.3 8.4 %collective-permute-start.25 = (bf16[16,8,512]{2,1,0:T(8,128)(2,1)S(1)}, bf16[16,8,512]{2,1,0:T(8,128)(2,1)S(1)}, u32[]{:S(2)}, u32[]{:S(2)}) collective-permute-start(bf16[16,8,512]{2,1,0:T(8,128)(2,1)S(1)} %get-tuple-element.49), channel_id=1, source_target_pairs={{0,8},{1,9},{2,10},{3,11},{4,12},{5,13},{6,14},{7,15},{8,0},{9,1},... | collective-permute-start | bytes 393224 | tf_op jit(solution)/shard_map/ppermute | solution.py:34
  67.2 7.3 %collective-permute-start.29 = (bf16[16,8,512]{2,1,0:T(8,128)(2,1)S(1)}, bf16[16,8,512]{2,1,0:T(8,128)(2,1)S(1)}, u32[]{:S(2)}, u32[]{:S(2)}) collective-permute-start(bf16[16,8,512]{2,1,0:T(8,128)(2,1)S(1)} %get-tuple-element.56), channel_id=1, source_target_pairs={{0,4},{1,5},{2,6},{3,7},{4,0},{5,1},{6,2},{7,3},{8,12},{9,13},{10,... | collective-permute-start | bytes 393224 | tf_op jit(solution)/shard_map/ppermute | solution.py:34
  73.7 4.3 %collective-permute-start.26 = (bf16[8,8,512]{2,1,0:T(8,128)(2,1)S(1)}, bf16[8,8,512]{2,1,0:T(8,128)(2,1)S(1)}, u32[]{:S(2)}, u32[]{:S(2)}) collective-permute-start(bf16[8,8,512]{2,1,0:T(8,128)(2,1)S(1)} %get-tuple-element.51), channel_id=1, source_target_pairs={{0,2},{1,3},{2,0},{3,1},{4,6},{5,7},{6,4},{7,5},{8,10},{9,11},{10,... | collective-permute-start | bytes 196616 | tf_op jit(solution)/shard_map/ppermute | solution.py:34
  74.6 5.6 %collective-permute-start.30 = (bf16[8,8,512]{2,1,0:T(8,128)(2,1)S(1)}, bf16[8,8,512]{2,1,0:T(8,128)(2,1)S(1)}, u32[]{:S(2)}, u32[]{:S(2)}) collective-permute-start(bf16[8,8,512]{2,1,0:T(8,128)(2,1)S(1)} %get-tuple-element.58), channel_id=1, source_target_pairs={{0,8},{1,9},{2,10},{3,11},{4,12},{5,13},{6,14},{7,15},{8,0},{9,1},... | collective-permute-start | bytes 196616 | tf_op jit(solution)/shard_map/ppermute | solution.py:34

commit v7 on v6

--- a/solution.py
+++ b/solution.py
@@ -13,6 +13,7 @@
 GROUP = 8
 SKEW = 3
 SQUARE = (6, 2, 4)
+MORE = 1
 LANES = 128
 MIB = 1024 * 1024
 
@@ -98,23 +99,21 @@
     for k in range(contrast.shape[0]):
         factor = jnp.where(unit == k, contrast_near[k], factor)
     scaling[...] = factor / (1.0 + value * value)
-    blocks, _, width = part_p.shape
-    rows = width // LANES
-    for half, part in enumerate((part_p, part_q)):
-        for b in range(blocks):
+    rows = part_p.shape[2] // LANES
+    for first, part in ((0, part_p), (part_p.shape[0], part_q)):
+        for b in range(part.shape[0]):
             for c in range(rows):
-                j = (half * blocks + b) * rows + c
+                j = (first + b) * rows + c
                 piece = probes_near[:, j * LANES : (j + 1) * LANES] * scaling[j : j + 1, :]
                 part[b, :, c * LANES : (c + 1) * LANES] = piece.astype(BF16)
 
 
 def final_body(keep_p, recv_p, keep_q, recv_q, scaling, out):
-    blocks, _, width = keep_p.shape
-    rows = width // LANES
-    for half, (keep, recv) in enumerate(((keep_p, recv_p), (keep_q, recv_q))):
-        for b in range(blocks):
+    rows = keep_p.shape[2] // LANES
+    for first, keep, recv in ((0, keep_p, recv_p), (keep_p.shape[0], keep_q, recv_q)):
+        for b in range(keep.shape[0]):
             for c in range(rows):
-                j = (half * blocks + b) * rows + c
+                j = (first + b) * rows + c
                 lanes = slice(c * LANES, (c + 1) * LANES)
                 total = keep[b, :, lanes] + recv[b, :, lanes].astype(F32)
                 out[:, j * LANES : (j + 1) * LANES] = total * scaling[j : j + 1, :]
@@ -225,7 +224,7 @@
 
 def tiles(pieces, src_row, dst_row, table, first, second, acc, parts, send_dtype, name):
     count, rank, width = first.shape
-    blocks, probes, _ = acc.shape
+    probes = acc.shape[1]
     rows = sum(piece.shape[0] for piece in pieces)
 
     def body(*refs):
@@ -233,7 +232,7 @@
 
     return local(
         body,
-        [shape(acc.shape, F32)] + [shape((blocks // 2 // parts, probes, width), send_dtype)] * parts,
+        [shape(acc.shape, F32)] + [shape((n, probes, width), send_dtype) for n in parts],
         table,
         acc,
         *pieces,
@@ -259,7 +258,7 @@
     peers, count = owners[0].shape
     rows = weight.shape[0] // peers
     rest = peers // 8
-    half = cell_blocks // 2
+    ahead = cell_blocks // 2 + MORE
 
     def body(*refs):
         far, weight_far, table_out, weight_near = refs[:5], refs[5], refs[6], refs[7]
@@ -273,9 +272,9 @@
         col_owner, col_local, row_owner, row_local, rank = [ref[pl.ds(me, 1), :] for ref in near]
         span = peers // 2
         away = col_owner ^ me
-        is_q = col_local >= half
-        spot = jnp.where(is_q, place(away, orders[1]) + (span - 1), place(away, orders[0]))
-        table[0:1, :] = (away & 1) * (span * cell_blocks) + spot * half + col_local
+        in_p = place(away, orders[0]) * ahead + col_local
+        in_q = place(away, orders[1]) * (cell_blocks - ahead) + (col_local + (span - 1) * ahead)
+        table[0:1, :] = (away & 1) * (span * cell_blocks) + jnp.where(col_local >= ahead, in_q, in_p)
         away = row_owner ^ me
         spot = (away & 1) * 4 + ((away & 4) // 2) + ((away & 2) // 2)
         table[1:2, :] = (spot * rest + row_owner // 8) * station_blocks + row_local
@@ -321,10 +320,11 @@
     orders = (bits[:1] + far, far + bits[:1])
 
     lanes = (cell_total // LANES, LANES)
-    half_dims = (cell_blocks // 2, probe_count, cell_width)
+    ahead = cell_blocks // 2 + MORE
+    behind = cell_blocks - ahead
     part_p, part_q, scaling = local(
         scale_body,
-        [shape(half_dims, BF16), shape(half_dims, BF16), shape(lanes, F32)],
+        [shape((n, probe_count, cell_width), BF16) for n in (ahead, behind)] + [shape(lanes, F32)],
         contrast,
         level_set.reshape(lanes),
         unit_label.reshape(lanes),
@@ -363,24 +363,25 @@
     pieces = [part_p, got_p, part_q, got_q]
     pieces = pieces + [swap(piece, 1) for piece in pieces]
 
+    len_quarter = peers * station_blocks // 8
     acc = zeros((peers * station_blocks, probe_count, station_width), (part_p, part_q))
-    total, *sends = tiles(pieces, 0, 1, table, v_here, u_here, acc, 4, F32, "forward")
+    total, *sends = tiles(pieces, 0, 1, table, v_here, u_here, acc, [len_quarter] * 4, F32, "forward")
     quarters = [0] * 4
     for k in SQUARE + (0,):
         kept = F32 if k == 0 else BF16
-        quarters[k // 2] = fold(total, swap(sends[k // 2], 1), (kept,), base=k // 2 * sends[0].shape[0])[0]
+        quarters[k // 2] = fold(total, swap(sends[k // 2], 1), (kept,), base=k // 2 * len_quarter)[0]
     total, send = plus(quarters[0], *[swap(quarters[k // 2], k) for k in SQUARE])
     for bit in bits[2:-1]:
         total, send = plus(total, swap(send, bit))
     weighted = weigh(total, swap(send, bits[-1]), weight)
     gots = {k: swap(weighted, k) for k in SQUARE}
-    around = join(gots[2], gots[4], gots[6])
-    pieces = [weighted, around, swap(weighted, 1), swap(around, 1)]
+    pieces = [weighted, gots[2], gots[4], gots[6]]
+    pieces = pieces + [swap(piece, 1) for piece in pieces]
 
     acc = zeros((peers * cell_blocks, probe_count, cell_width), (total,))
-    total, send_p, send_q = tiles(pieces, 1, 0, table, u_here, v_here, acc, 2, BF16, "adjoint")
+    total, send_p, send_q = tiles(pieces, 1, 0, table, u_here, v_here, acc, [n * peers // 2 for n in (ahead, behind)], BF16, "adjoint")
     keep_p, send_p = fold(total, swap(send_p, 1))
-    keep_q, send_q = fold(total, swap(send_q, 1), base=total.shape[0] // 4)
+    keep_q, send_q = fold(total, swap(send_q, 1), base=ahead * peers // 2)
     for step, (bit_p, bit_q) in enumerate(steps[::-1]):
         if step > 0:
             keep_p, send_p = fold(keep_p, got_p)

time: 81.3 us -> 97.1 us (1.19)
  waiting for transfers between devices: 39.5 us -> 56 us
    ppermute x31 -> x33, waiting for transfers between devices: 39.5 us -> 56 us  [swap(): return lax.ppermute(array, 'tile', [(i, i ^ bits) for i in range(count)])]
    ppermute x31 -> x33, starting transfers between devices: 28.4 us -> 27.8 us  [swap(): return lax.ppermute(array, 'tile', [(i, i ^ bits) for i in range(count)])]
    pallas_call x26 -> x25, Pallas kernels: 12.9 us -> 12.9 us  [local(): pl.pallas_call(run, out_shape=[a if s.memory_space is None else s.memory_...]
  transfers between devices with their start and end apart: 31 -> 33, of which waited for: 20 -> 19; matrix products, arithmetic and copies ran while one was open for 0% -> 0% of each run, Pallas kernels for 8% -> 7%
where the time goes in v7:
time: 97.1 us; the launch traced here: 96.9 us
  waiting for transfers between devices  56 us (58%)
  starting transfers between devices  27.8 us (29%)
  Pallas kernels  12.9 us (13%)
    ppermute x33, waiting for transfers between devices, swap(): return lax.ppermute(array, 'tile', [(i, i ^ bits) for i in range(count)])  56 us
    ppermute x33, starting transfers between devices, swap(): return lax.ppermute(array, 'tile', [(i, i ^ bits) for i in range(count)])  27.8 us
    pallas_call x25, Pallas kernels, local(): pl.pallas_call(run, out_shape=[a if s.memory_space is None else s.memory_...  12.9 us
  transfers between devices with their start and end apart: 33, of which 19 were waited for; matrix products, arithmetic and copies ran while one was open for 0% of the time, Pallas kernels for 7%

profile of v7, /device:TPU:0, one launch (start us, length us, event | category | flops | bytes accessed | tf_op | source)
XLA Modules:
  0.0 96.9 jit_solution(13419266890159354987)
XLA Ops:
  0.0 1.1 %scale.1 = (bf16[9,8,512]{2,1,0:T(8,128)(2,1)S(1)}, bf16[7,8,512]{2,1,0:T(8,128)(2,1)S(1)}, f32[64,128]{1,0:T(8,128)S(1)}) custom-call(f32[4]{0:T(128)} %refs_0_.3, f32[64,128]{1,0:T(8,128)} %bitcast.9, s32[64,128]{1,0:T(8,128)} %bitcast.10, f32[8,8192]{1,0:T(8,128)} %refs_3_.1), custom_call_target="tpu_custom_call" | custom-call | bytes 491536 | tf_op jit(solution)/shard_map/scale/pallas_call | solution.py:50
  1.1 3.0 %collective-permute-start = (bf16[9,8,512]{2,1,0:T(8,128)(2,1)S(1)}, bf16[9,8,512]{2,1,0:T(8,128)(2,1)S(1)}, u32[]{:S(2)}, u32[]{:S(2)}) collective-permute-start(bf16[9,8,512]{2,1,0:T(8,128)(2,1)S(1)} %get-tuple-element.34.refs_0_), channel_id=1, source_target_pairs={{0,2},{1,3},{2,0},{3,1},{4,6},{5,7},{6,4},{7,5},{8,10},{9,11},{10,... | collective-permute-start | bytes 221192 | tf_op jit(solution)/shard_map/ppermute | solution.py:35
  4.1 1.5 %plan.1 = (s32[8,128]{1,0:T(8,128)S(4)}, f32[32,128]{1,0:T(8,128)S(1)}) custom-call(s32[16,128]{1,0:T(8,128)} %bitcast.11, s32[16,128]{1,0:T(8,128)} %bitcast.12, s32[16,128]{1,0:T(8,128)} %bitcast.13, s32[16,128]{1,0:T(8,128)} %bitcast.14, s32[16,128]{1,0:T(8,128)} %bitcast.15, f32[256,128]{1,0:T(8,128)} %bitcast.8, ...), custom_call_target="tpu_custom_call" | custom-call | bytes 192512 | tf_op jit(solution)/shard_map/plan/pallas_call | solution.py:50
  5.6 0.9 collective-permute-done.refs_1_
  6.5 3.2 %collective-permute-start.1 = (bf16[18,8,512]{2,1,0:T(8,128)(2,1)S(1)}, bf16[18,8,512]{2,1,0:T(8,128)(2,1)S(1)}, u32[]{:S(2)}, u32[]{:S(2)}) collective-permute-start(bf16[18,8,512]{2,1,0:T(8,128)(2,1)S(1)} %join.4.refs_1_.refs_0_), channel_id=1, source_target_pairs={{0,8},{1,9},{2,10},{3,11},{4,12},{5,13},{6,14},{7,15},{8,0},{9,1},... | collective-permute-start | bytes 442376 | tf_op jit(solution)/shard_map/ppermute | solution.py:35
  9.7 8.2 %collective-permute-done.2.refs_1_ = bf16[7,8,512]{2,1,0:T(8,128)(2,1)S(1)} collective-permute-done((bf16[7,8,512]{2,1,0:T(8,128)(2,1)S(1)}, bf16[7,8,512]{2,1,0:T(8,128)(2,1)S(1)}, u32[]{:S(2)}, u32[]{:S(2)}) %collective-permute-start.2) | collective-permute-done | bytes 57376 | tf_op jit(solution)/shard_map/ppermute | solution.py:35
  17.9 2.2 %load_v.1.refs_3_.refs_10_.refs_11_ = bf16[128,32,512]{2,1,0:T(8,128)(2,1)S(1)} custom-call(bf16[128,32,512]{2,1,0:T(8,128)(2,1)} %refs_0_.4, bf16[18,8,512]{2,1,0:T(8,128)(2,1)S(1)} %join.4.refs_1_.refs_0_, bf16[14,8,512]{2,1,0:T(8,128)(2,1)S(1)} %join.5.refs_2_.refs_0_), custom_call_target="tpu_custom_call" | custom-call | bytes 8388608 | tf_op jit(solution)/shard_map/load_v/pallas_call | solution.py:50
  20.2 2.2 %load_u.1.refs_2_.refs_11_.refs_10_ = bf16[128,32,512]{2,1,0:T(8,128)(2,1)S(1)} custom-call(bf16[128,32,512]{2,1,0:T(8,128)(2,1)} %refs_0_.5, bf16[18,8,512]{2,1,0:T(8,128)(2,1)S(1)} %join.4.refs_1_.refs_0_, bf16[14,8,512]{2,1,0:T(8,128)(2,1)S(1)} %join.5.refs_2_.refs_0_, bf16[128,32,512]{2,1,0:T(8,128)(2,1)S(1)} %load_v.1.refs_3_.refs_10_.refs_11_), custom_call_target="tpu_custom_call" | custom-call | bytes 8388608 | tf_op jit(solution)/shard_map/load_u/pallas_call | solution.py:50
  22.4 0.8 collective-permute-start.4
  23.2 1.3 %collective-permute-start.3 = (bf16[14,8,512]{2,1,0:T(8,128)(2,1)S(1)}, bf16[14,8,512]{2,1,0:T(8,128)(2,1)S(1)}, u32[]{:S(2)}, u32[]{:S(2)}) collective-permute-start(bf16[14,8,512]{2,1,0:T(8,128)(2,1)S(1)} %join.5.refs_2_.refs_0_), channel_id=1, source_target_pairs={{0,4},{1,5},{2,6},{3,7},{4,0},{5,1},{6,2},{7,3},{8,12},{9,13},{10,... | collective-permute-start | bytes 344072 | tf_op jit(solution)/shard_map/ppermute | solution.py:35
  24.5 8.3 %collective-permute-done.3.refs_1_ = bf16[14,8,512]{2,1,0:T(8,128)(2,1)S(1)} collective-permute-done((bf16[14,8,512]{2,1,0:T(8,128)(2,1)S(1)}, bf16[14,8,512]{2,1,0:T(8,128)(2,1)S(1)}, u32[]{:S(2)}, u32[]{:S(2)}) %collective-permute-start.3) | collective-permute-done | bytes 114720 | tf_op jit(solution)/shard_map/ppermute | solution.py:35
  32.9 1.6 %collective-permute-start.5 = (bf16[28,8,512]{2,1,0:T(8,128)(2,1)S(1)}, bf16[28,8,512]{2,1,0:T(8,128)(2,1)S(1)}, u32[]{:S(2)}, u32[]{:S(2)}) collective-permute-start(bf16[28,8,512]{2,1,0:T(8,128)(2,1)S(1)} %join.7.refs_1_.refs_4_), channel_id=1, source_target_pairs={{0,2},{1,3},{2,0},{3,1},{4,6},{5,7},{6,4},{7,5},{8,10},{9,11},{10,... | collective-permute-start | bytes 688136 | tf_op jit(solution)/shard_map/ppermute | solution.py:35
  34.5 0.5 collective-permute-start.7
  35.0 4.0 %collective-permute-done.5.refs_5_ = bf16[28,8,512]{2,1,0:T(8,128)(2,1)S(1)} collective-permute-done((bf16[28,8,512]{2,1,0:T(8,128)(2,1)S(1)}, bf16[28,8,512]{2,1,0:T(8,128)(2,1)S(1)}, u32[]{:S(2)}, u32[]{:S(2)}) %collective-permute-start.5) | collective-permute-done | bytes 229408 | tf_op jit(solution)/shard_map/ppermute | solution.py:35
  39.1 1.4 %collective-permute-done.9.refs_9_ = bf16[28,8,512]{2,1,0:T(8,128)(2,1)S(1)} collective-permute-done((bf16[28,8,512]{2,1,0:T(8,128)(2,1)S(1)}, bf16[28,8,512]{2,1,0:T(8,128)(2,1)S(1)}, u32[]{:S(2)}, u32[]{:S(2)}) %collective-permute-start.9) | collective-permute-done | bytes 229408 | tf_op jit(solution)/shard_map/ppermute | solution.py:35
  40.5 2.2 %forward.1 = (f32[64,8,512]{2,1,0:T(8,128)S(1)}, f32[8,8,512]{2,1,0:T(8,128)S(1)}, f32[8,8,512]{2,1,0:T(8,128)S(1)}, f32[8,8,512]{2,1,0:T(8,128)S(1)}, f32[8,8,512]{2,1,0:T(8,128)S(1)}) custom-call(s32[8,128]{1,0:T(8,128)S(4)} %get-tuple-element.33.refs_0_, f32[64,8,512]{2,1,0:T(8,128)S(1)} %zeros.2.refs_1_, ...), custom_call_target="tpu_custom_call", output_to_operand_aliasing={{0}: (1, {})} | custom-call | flops 536870912 | bytes 13111296 | tf_op jit(solution)/shard_map/forward/pallas_call | solution.py:50
  42.9 0.4 collective-permute-start.13
  43.4 0.4 collective-permute-start.10
  43.8 0.3 collective-permute-done.11.refs_1_
  44.1 3.4 %collective-permute-start.12 = (bf16[8,8,512]{2,1,0:T(8,128)(2,1)S(1)}, bf16[8,8,512]{2,1,0:T(8,128)(2,1)S(1)}, u32[]{:S(2)}, u32[]{:S(2)}) collective-permute-start(bf16[8,8,512]{2,1,0:T(8,128)(2,1)S(1)} %fold.11), channel_id=1, source_target_pairs={{0,6},{1,7},{2,4},{3,5},{4,2},{5,3},{6,0},{7,1},{8,14},{9,15},{10,... | collective-permute-start | bytes 196616 | tf_op jit(solution)/shard_map/ppermute | solution.py:35
  47.5 0.6 collective-permute-start.14
  48.4 1.5 %collective-permute-done.12.refs_1_ = bf16[8,8,512]{2,1,0:T(8,128)(2,1)S(1)} collective-permute-done((bf16[8,8,512]{2,1,0:T(8,128)(2,1)S(1)}, bf16[8,8,512]{2,1,0:T(8,128)(2,1)S(1)}, u32[]{:S(2)}, u32[]{:S(2)}) %collective-permute-start.12) | collective-permute-done | bytes 65568 | tf_op jit(solution)/shard_map/ppermute | solution.py:35
  49.9 1.9 %collective-permute-done.14.refs_2_ = bf16[8,8,512]{2,1,0:T(8,128)(2,1)S(1)} collective-permute-done((bf16[8,8,512]{2,1,0:T(8,128)(2,1)S(1)}, bf16[8,8,512]{2,1,0:T(8,128)(2,1)S(1)}, u32[]{:S(2)}, u32[]{:S(2)}) %collective-permute-start.14) | collective-permute-done | bytes 65568 | tf_op jit(solution)/shard_map/ppermute | solution.py:35
  51.9 0.6 collective-permute-done.16.refs_3_
  52.5 3.4 %collective-permute-start.17 = (bf16[8,8,512]{2,1,0:T(8,128)(2,1)S(1)}, bf16[8,8,512]{2,1,0:T(8,128)(2,1)S(1)}, u32[]{:S(2)}, u32[]{:S(2)}) collective-permute-start(bf16[8,8,512]{2,1,0:T(8,128)(2,1)S(1)} %get-tuple-element.43), channel_id=1, source_target_pairs={{0,8},{1,9},{2,10},{3,11},{4,12},{5,13},{6,14},{7,15},{8,0},{9,1},... | collective-permute-start | bytes 196616 | tf_op jit(solution)/shard_map/ppermute | solution.py:35
  55.9 2.9 %collective-permute-done.17.refs_1_ = bf16[8,8,512]{2,1,0:T(8,128)(2,1)S(1)} collective-permute-done((bf16[8,8,512]{2,1,0:T(8,128)(2,1)S(1)}, bf16[8,8,512]{2,1,0:T(8,128)(2,1)S(1)}, u32[]{:S(2)}, u32[]{:S(2)}) %collective-permute-start.17) | collective-permute-done | bytes 65568 | tf_op jit(solution)/shard_map/ppermute | solution.py:35
  58.9 1.0 %collective-permute-start.20 = (bf16[8,8,512]{2,1,0:T(8,128)(2,1)S(1)}, bf16[8,8,512]{2,1,0:T(8,128)(2,1)S(1)}, u32[]{:S(2)}, u32[]{:S(2)}) collective-permute-start(bf16[8,8,512]{2,1,0:T(8,128)(2,1)S(1)} %weigh.1.refs_2_), channel_id=1, source_target_pairs={{0,6},{1,7},{2,4},{3,5},{4,2},{5,3},{6,0},{7,1},{8,14},{9,15},{10,... | collective-permute-start | bytes 196616 | tf_op jit(solution)/shard_map/ppermute | solution.py:35
  59.9 2.1 %collective-permute-start.19 = (bf16[8,8,512]{2,1,0:T(8,128)(2,1)S(1)}, bf16[8,8,512]{2,1,0:T(8,128)(2,1)S(1)}, u32[]{:S(2)}, u32[]{:S(2)}) collective-permute-start(bf16[8,8,512]{2,1,0:T(8,128)(2,1)S(1)} %weigh.1.refs_2_), channel_id=1, source_target_pairs={{0,4},{1,5},{2,6},{3,7},{4,0},{5,1},{6,2},{7,3},{8,12},{9,13},{10,... | collective-permute-start | bytes 196616 | tf_op jit(solution)/shard_map/ppermute | solution.py:35
  62.0 0.5 collective-permute-start.18
  62.5 1.7 %collective-permute-done.20.refs_5_ = bf16[8,8,512]{2,1,0:T(8,128)(2,1)S(1)} collective-permute-done((bf16[8,8,512]{2,1,0:T(8,128)(2,1)S(1)}, bf16[8,8,512]{2,1,0:T(8,128)(2,1)S(1)}, u32[]{:S(2)}, u32[]{:S(2)}) %collective-permute-start.20) | collective-permute-done | bytes 65568 | tf_op jit(solution)/shard_map/ppermute | solution.py:35
  64.2 0.8 collective-permute-done.19.refs_4_
  65.0 1.3 %collective-permute-done.18.refs_3_ = bf16[8,8,512]{2,1,0:T(8,128)(2,1)S(1)} collective-permute-done((bf16[8,8,512]{2,1,0:T(8,128)(2,1)S(1)}, bf16[8,8,512]{2,1,0:T(8,128)(2,1)S(1)}, u32[]{:S(2)}, u32[]{:S(2)}) %collective-permute-start.18) | collective-permute-done | bytes 65568 | tf_op jit(solution)/shard_map/ppermute | solution.py:35
  66.3 0.3 zeros.3.refs_1_
  66.6 0.9 collective-permute-done.22.refs_7_
  67.5 2.2 %adjoint.1 = (f32[256,8,512]{2,1,0:T(8,128)S(1)}, bf16[72,8,512]{2,1,0:T(8,128)(2,1)S(1)}, bf16[56,8,512]{2,1,0:T(8,128)(2,1)S(1)}) custom-call(s32[8,128]{1,0:T(8,128)S(4)} %get-tuple-element.33.refs_0_, f32[256,8,512]{2,1,0:T(8,128)S(1)} %zeros.3.refs_1_, bf16[8,8,512]{2,1,0:T(8,128)(2,1)S(1)} %weigh.1.refs_2_, ...), custom_call_target="tpu_custom_call", output_to_operand_aliasing={{0}: (1, {})} | custom-call | flops 536870912 | bytes 18354176 | tf_op jit(solution)/shard_map/adjoint/pallas_call | solution.py:50
  69.9 0.4 collective-permute-start.29
  70.3 1.5 %collective-permute-done.25.refs_1_ = bf16[72,8,512]{2,1,0:T(8,128)(2,1)S(1)} collective-permute-done((bf16[72,8,512]{2,1,0:T(8,128)(2,1)S(1)}, bf16[72,8,512]{2,1,0:T(8,128)(2,1)S(1)}, u32[]{:S(2)}, u32[]{:S(2)}) %collective-permute-start.25) | collective-permute-done | bytes 589856 | tf_op jit(solution)/shard_map/ppermute | solution.py:35
  71.9 0.2 collective-permute-start.26
  72.1 0.3 collective-permute-done.29.refs_1_
  72.5 0.5 collective-permute-start.30
  73.0 8.0 %collective-permute-done.26.refs_1_ = bf16[36,8,512]{2,1,0:T(8,128)(2,1)S(1)} collective-permute-done((bf16[36,8,512]{2,1,0:T(8,128)(2,1)S(1)}, bf16[36,8,512]{2,1,0:T(8,128)(2,1)S(1)}, u32[]{:S(2)}, u32[]{:S(2)}) %collective-permute-start.26) | collective-permute-done | bytes 294944 | tf_op jit(solution)/shard_map/ppermute | solution.py:35
  81.1 2.2 %collective-permute-start.27 = (bf16[18,8,512]{2,1,0:T(8,128)(2,1)S(1)}, bf16[18,8,512]{2,1,0:T(8,128)(2,1)S(1)}, u32[]{:S(2)}, u32[]{:S(2)}) collective-permute-start(bf16[18,8,512]{2,1,0:T(8,128)(2,1)S(1)} %get-tuple-element.49), channel_id=1, source_target_pairs={{0,8},{1,9},{2,10},{3,11},{4,12},{5,13},{6,14},{7,15},{8,0},{9,1},... | collective-permute-start | bytes 442376 | tf_op jit(solution)/shard_map/ppermute | solution.py:35
  83.4 0.7 collective-permute-start.31
  84.0 6.4 %collective-permute-done.27.refs_1_ = bf16[18,8,512]{2,1,0:T(8,128)(2,1)S(1)} collective-permute-done((bf16[18,8,512]{2,1,0:T(8,128)(2,1)S(1)}, bf16[18,8,512]{2,1,0:T(8,128)(2,1)S(1)}, u32[]{:S(2)}, u32[]{:S(2)}) %collective-permute-start.27) | collective-permute-done | bytes 147488 | tf_op jit(solution)/shard_map/ppermute | solution.py:35
  90.4 0.5 collective-permute-start.28
  91.0 0.3 collective-permute-start.32
  91.3 4.8 %collective-permute-done.32.refs_3_ = bf16[7,8,512]{2,1,0:T(8,128)(2,1)S(1)} collective-permute-done((bf16[7,8,512]{2,1,0:T(8,128)(2,1)S(1)}, bf16[7,8,512]{2,1,0:T(8,128)(2,1)S(1)}, u32[]{:S(2)}, u32[]{:S(2)}) %collective-permute-start.32) | collective-permute-done | bytes 57376 | tf_op jit(solution)/shard_map/ppermute | solution.py:35
  96.1 0.7 final.1
  (43 shorter events, 1.5 us)
Async XLA Ops:
  1.1 5.4 %collective-permute-start = (bf16[9,8,512]{2,1,0:T(8,128)(2,1)S(1)}, bf16[9,8,512]{2,1,0:T(8,128)(2,1)S(1)}, u32[]{:S(2)}, u32[]{:S(2)}) collective-permute-start(bf16[9,8,512]{2,1,0:T(8,128)(2,1)S(1)} %get-tuple-element.34.refs_0_), channel_id=1, source_target_pairs={{0,2},{1,3},{2,0},{3,1},{4,6},{5,7},{6,4},{7,5},{8,10},{9,11},{10,... | collective-permute-start | bytes 221192 | tf_op jit(solution)/shard_map/ppermute | solution.py:35
  6.5 15.9 %collective-permute-start.1 = (bf16[18,8,512]{2,1,0:T(8,128)(2,1)S(1)}, bf16[18,8,512]{2,1,0:T(8,128)(2,1)S(1)}, u32[]{:S(2)}, u32[]{:S(2)}) collective-permute-start(bf16[18,8,512]{2,1,0:T(8,128)(2,1)S(1)} %join.4.refs_1_.refs_0_), channel_id=1, source_target_pairs={{0,8},{1,9},{2,10},{3,11},{4,12},{5,13},{6,14},{7,15},{8,0},{9,1},... | collective-permute-start | bytes 442376 | tf_op jit(solution)/shard_map/ppermute | solution.py:35
  9.6 8.3 %collective-permute-start.2 = (bf16[7,8,512]{2,1,0:T(8,128)(2,1)S(1)}, bf16[7,8,512]{2,1,0:T(8,128)(2,1)S(1)}, u32[]{:S(2)}, u32[]{:S(2)}) collective-permute-start(bf16[7,8,512]{2,1,0:T(8,128)(2,1)S(1)} %get-tuple-element.36.refs_0_), channel_id=1, source_target_pairs={{0,8},{1,9},{2,10},{3,11},{4,12},{5,13},{6,14},{7,15},{8,0},{9,1},... | collective-permute-start | bytes 172040 | tf_op jit(solution)/shard_map/ppermute | solution.py:35
  22.4 12.0 %collective-permute-start.4 = (bf16[36,8,512]{2,1,0:T(8,128)(2,1)S(1)}, bf16[36,8,512]{2,1,0:T(8,128)(2,1)S(1)}, u32[]{:S(2)}, u32[]{:S(2)}) collective-permute-start(bf16[36,8,512]{2,1,0:T(8,128)(2,1)S(1)} %join.6.refs_0_.refs_2_), channel_id=1, source_target_pairs={{0,4},{1,5},{2,6},{3,7},{4,0},{5,1},{6,2},{7,3},{8,12},{9,13},{10,... | collective-permute-start | bytes 884744 | tf_op jit(solution)/shard_map/ppermute | solution.py:35
  23.2 9.6 %collective-permute-start.3 = (bf16[14,8,512]{2,1,0:T(8,128)(2,1)S(1)}, bf16[14,8,512]{2,1,0:T(8,128)(2,1)S(1)}, u32[]{:S(2)}, u32[]{:S(2)}) collective-permute-start(bf16[14,8,512]{2,1,0:T(8,128)(2,1)S(1)} %join.5.refs_2_.refs_0_), channel_id=1, source_target_pairs={{0,4},{1,5},{2,6},{3,7},{4,0},{5,1},{6,2},{7,3},{8,12},{9,13},{10,... | collective-permute-start | bytes 344072 | tf_op jit(solution)/shard_map/ppermute | solution.py:35
  32.9 6.1 %collective-permute-start.5 = (bf16[28,8,512]{2,1,0:T(8,128)(2,1)S(1)}, bf16[28,8,512]{2,1,0:T(8,128)(2,1)S(1)}, u32[]{:S(2)}, u32[]{:S(2)}) collective-permute-start(bf16[28,8,512]{2,1,0:T(8,128)(2,1)S(1)} %join.7.refs_1_.refs_4_), channel_id=1, source_target_pairs={{0,2},{1,3},{2,0},{3,1},{4,6},{5,7},{6,4},{7,5},{8,10},{9,11},{10,... | collective-permute-start | bytes 688136 | tf_op jit(solution)/shard_map/ppermute | solution.py:35
  34.5 4.6 %collective-permute-start.6 = (bf16[36,8,512]{2,1,0:T(8,128)(2,1)S(1)}, bf16[36,8,512]{2,1,0:T(8,128)(2,1)S(1)}, u32[]{:S(2)}, u32[]{:S(2)}) collective-permute-start(bf16[36,8,512]{2,1,0:T(8,128)(2,1)S(1)} %join.6.refs_0_.refs_2_), channel_id=1, source_target_pairs={{0,1},{1,0},{2,3},{3,2},{4,5},{5,4},{6,7},{7,6},{8,9},{9,8},{10,11... | collective-permute-start | bytes 884744 | tf_op jit(solution)/shard_map/ppermute | solution.py:35
  34.5 6.0 %collective-permute-start.7 = (bf16[36,8,512]{2,1,0:T(8,128)(2,1)S(1)}, bf16[36,8,512]{2,1,0:T(8,128)(2,1)S(1)}, u32[]{:S(2)}, u32[]{:S(2)}) collective-permute-start(bf16[36,8,512]{2,1,0:T(8,128)(2,1)S(1)} %collective-permute-done.4.refs_3_), channel_id=1, source_target_pairs={{0,1},{1,0},{2,3},{3,2},{4,5},{5,4},{6,7},{7,6},{8,9},{9,8},{10,11... | collective-permute-start | bytes 884744 | tf_op jit(solution)/shard_map/ppermute | solution.py:35
  35.0 4.1 %collective-permute-start.8 = (bf16[28,8,512]{2,1,0:T(8,128)(2,1)S(1)}, bf16[28,8,512]{2,1,0:T(8,128)(2,1)S(1)}, u32[]{:S(2)}, u32[]{:S(2)}) collective-permute-start(bf16[28,8,512]{2,1,0:T(8,128)(2,1)S(1)} %join.7.refs_1_.refs_4_), channel_id=1, source_target_pairs={{0,1},{1,0},{2,3},{3,2},{4,5},{5,4},{6,7},{7,6},{8,9},{9,8},{10,11... | collective-permute-start | bytes 688136 | tf_op jit(solution)/shard_map/ppermute | solution.py:35
  39.0 1.5 %collective-permute-start.9 = (bf16[28,8,512]{2,1,0:T(8,128)(2,1)S(1)}, bf16[28,8,512]{2,1,0:T(8,128)(2,1)S(1)}, u32[]{:S(2)}, u32[]{:S(2)}) collective-permute-start(bf16[28,8,512]{2,1,0:T(8,128)(2,1)S(1)} %collective-permute-done.5.refs_5_), channel_id=1, source_target_pairs={{0,1},{1,0},{2,3},{3,2},{4,5},{5,4},{6,7},{7,6},{8,9},{9,8},{10,11... | collective-permute-start | bytes 688136 | tf_op jit(solution)/shard_map/ppermute | solution.py:35
  42.7 1.4 %collective-permute-start.11 = (f32[8,8,512]{2,1,0:T(8,128)S(1)}, f32[8,8,512]{2,1,0:T(8,128)S(1)}, u32[]{:S(2)}, u32[]{:S(2)}) collective-permute-start(f32[8,8,512]{2,1,0:T(8,128)S(1)} %get-tuple-element.39), channel_id=1, source_target_pairs={{0,1},{1,0},{2,3},{3,2},{4,5},{5,4},{6,7},{7,6},{8,9},{9,8},{10,11... | collective-permute-start | bytes 393224 | tf_op jit(solution)/shard_map/ppermute | solution.py:35
  42.9 4.7 %collective-permute-start.13 = (f32[8,8,512]{2,1,0:T(8,128)S(1)}, f32[8,8,512]{2,1,0:T(8,128)S(1)}, u32[]{:S(2)}, u32[]{:S(2)}) collective-permute-start(f32[8,8,512]{2,1,0:T(8,128)S(1)} %get-tuple-element.40), channel_id=1, source_target_pairs={{0,1},{1,0},{2,3},{3,2},{4,5},{5,4},{6,7},{7,6},{8,9},{9,8},{10,11... | collective-permute-start | bytes 393224 | tf_op jit(solution)/shard_map/ppermute | solution.py:35
  43.2 4.9 %collective-permute-start.15 = (f32[8,8,512]{2,1,0:T(8,128)S(1)}, f32[8,8,512]{2,1,0:T(8,128)S(1)}, u32[]{:S(2)}, u32[]{:S(2)}) collective-permute-start(f32[8,8,512]{2,1,0:T(8,128)S(1)} %get-tuple-element.41), channel_id=1, source_target_pairs={{0,1},{1,0},{2,3},{3,2},{4,5},{5,4},{6,7},{7,6},{8,9},{9,8},{10,11... | collective-permute-start | bytes 393224 | tf_op jit(solution)/shard_map/ppermute | solution.py:35
  43.4 5.0 %collective-permute-start.10 = (f32[8,8,512]{2,1,0:T(8,128)S(1)}, f32[8,8,512]{2,1,0:T(8,128)S(1)}, u32[]{:S(2)}, u32[]{:S(2)}) collective-permute-start(f32[8,8,512]{2,1,0:T(8,128)S(1)} %get-tuple-element.38), channel_id=1, source_target_pairs={{0,1},{1,0},{2,3},{3,2},{4,5},{5,4},{6,7},{7,6},{8,9},{9,8},{10,11... | collective-permute-start | bytes 393224 | tf_op jit(solution)/shard_map/ppermute | solution.py:35
  44.1 5.8 %collective-permute-start.12 = (bf16[8,8,512]{2,1,0:T(8,128)(2,1)S(1)}, bf16[8,8,512]{2,1,0:T(8,128)(2,1)S(1)}, u32[]{:S(2)}, u32[]{:S(2)}) collective-permute-start(bf16[8,8,512]{2,1,0:T(8,128)(2,1)S(1)} %fold.11), channel_id=1, source_target_pairs={{0,6},{1,7},{2,4},{3,5},{4,2},{5,3},{6,0},{7,1},{8,14},{9,15},{10,... | collective-permute-start | bytes 196616 | tf_op jit(solution)/shard_map/ppermute | solution.py:35
  47.5 4.3 %collective-permute-start.14 = (bf16[8,8,512]{2,1,0:T(8,128)(2,1)S(1)}, bf16[8,8,512]{2,1,0:T(8,128)(2,1)S(1)}, u32[]{:S(2)}, u32[]{:S(2)}) collective-permute-start(bf16[8,8,512]{2,1,0:T(8,128)(2,1)S(1)} %fold.12), channel_id=1, source_target_pairs={{0,2},{1,3},{2,0},{3,1},{4,6},{5,7},{6,4},{7,5},{8,10},{9,11},{10,... | collective-permute-start | bytes 196616 | tf_op jit(solution)/shard_map/ppermute | solution.py:35
  48.1 4.3 %collective-permute-start.16 = (bf16[8,8,512]{2,1,0:T(8,128)(2,1)S(1)}, bf16[8,8,512]{2,1,0:T(8,128)(2,1)S(1)}, u32[]{:S(2)}, u32[]{:S(2)}) collective-permute-start(bf16[8,8,512]{2,1,0:T(8,128)(2,1)S(1)} %fold.13), channel_id=1, source_target_pairs={{0,4},{1,5},{2,6},{3,7},{4,0},{5,1},{6,2},{7,3},{8,12},{9,13},{10,... | collective-permute-start | bytes 196616 | tf_op jit(solution)/shard_map/ppermute | solution.py:35
  52.5 6.4 %collective-permute-start.17 = (bf16[8,8,512]{2,1,0:T(8,128)(2,1)S(1)}, bf16[8,8,512]{2,1,0:T(8,128)(2,1)S(1)}, u32[]{:S(2)}, u32[]{:S(2)}) collective-permute-start(bf16[8,8,512]{2,1,0:T(8,128)(2,1)S(1)} %get-tuple-element.43), channel_id=1, source_target_pairs={{0,8},{1,9},{2,10},{3,11},{4,12},{5,13},{6,14},{7,15},{8,0},{9,1},... | collective-permute-start | bytes 196616 | tf_op jit(solution)/shard_map/ppermute | solution.py:35
  58.9 5.2 %collective-permute-start.20 = (bf16[8,8,512]{2,1,0:T(8,128)(2,1)S(1)}, bf16[8,8,512]{2,1,0:T(8,128)(2,1)S(1)}, u32[]{:S(2)}, u32[]{:S(2)}) collective-permute-start(bf16[8,8,512]{2,1,0:T(8,128)(2,1)S(1)} %weigh.1.refs_2_), channel_id=1, source_target_pairs={{0,6},{1,7},{2,4},{3,5},{4,2},{5,3},{6,0},{7,1},{8,14},{9,15},{10,... | collective-permute-start | bytes 196616 | tf_op jit(solution)/shard_map/ppermute | solution.py:35
  59.9 5.0 %collective-permute-start.19 = (bf16[8,8,512]{2,1,0:T(8,128)(2,1)S(1)}, bf16[8,8,512]{2,1,0:T(8,128)(2,1)S(1)}, u32[]{:S(2)}, u32[]{:S(2)}) collective-permute-start(bf16[8,8,512]{2,1,0:T(8,128)(2,1)S(1)} %weigh.1.refs_2_), channel_id=1, source_target_pairs={{0,4},{1,5},{2,6},{3,7},{4,0},{5,1},{6,2},{7,3},{8,12},{9,13},{10,... | collective-permute-start | bytes 196616 | tf_op jit(solution)/shard_map/ppermute | solution.py:35
  62.0 4.3 %collective-permute-start.18 = (bf16[8,8,512]{2,1,0:T(8,128)(2,1)S(1)}, bf16[8,8,512]{2,1,0:T(8,128)(2,1)S(1)}, u32[]{:S(2)}, u32[]{:S(2)}) collective-permute-start(bf16[8,8,512]{2,1,0:T(8,128)(2,1)S(1)} %weigh.1.refs_2_), channel_id=1, source_target_pairs={{0,2},{1,3},{2,0},{3,1},{4,6},{5,7},{6,4},{7,5},{8,10},{9,11},{10,... | collective-permute-start | bytes 196616 | tf_op jit(solution)/shard_map/ppermute | solution.py:35
  62.5 4.1 %collective-permute-start.21 = (bf16[8,8,512]{2,1,0:T(8,128)(2,1)S(1)}, bf16[8,8,512]{2,1,0:T(8,128)(2,1)S(1)}, u32[]{:S(2)}, u32[]{:S(2)}) collective-permute-start(bf16[8,8,512]{2,1,0:T(8,128)(2,1)S(1)} %weigh.1.refs_2_), channel_id=1, source_target_pairs={{0,1},{1,0},{2,3},{3,2},{4,5},{5,4},{6,7},{7,6},{8,9},{9,8},{10,11... | collective-permute-start | bytes 196616 | tf_op jit(solution)/shard_map/ppermute | solution.py:35
  64.1 2.4 %collective-permute-start.24 = (bf16[8,8,512]{2,1,0:T(8,128)(2,1)S(1)}, bf16[8,8,512]{2,1,0:T(8,128)(2,1)S(1)}, u32[]{:S(2)}, u32[]{:S(2)}) collective-permute-start(bf16[8,8,512]{2,1,0:T(8,128)(2,1)S(1)} %collective-permute-done.20.refs_5_), channel_id=1, source_target_pairs={{0,1},{1,0},{2,3},{3,2},{4,5},{5,4},{6,7},{7,6},{8,9},{9,8},{10,11... | collective-permute-start | bytes 196616 | tf_op jit(solution)/shard_map/ppermute | solution.py:35
  65.0 1.6 %collective-permute-start.23 = (bf16[8,8,512]{2,1,0:T(8,128)(2,1)S(1)}, bf16[8,8,512]{2,1,0:T(8,128)(2,1)S(1)}, u32[]{:S(2)}, u32[]{:S(2)}) collective-permute-start(bf16[8,8,512]{2,1,0:T(8,128)(2,1)S(1)} %collective-permute-done.19.refs_4_), channel_id=1, source_target_pairs={{0,1},{1,0},{2,3},{3,2},{4,5},{5,4},{6,7},{7,6},{8,9},{9,8},{10,11... | collective-permute-start | bytes 196616 | tf_op jit(solution)/shard_map/ppermute | solution.py:35
  66.3 1.3 %collective-permute-start.22 = (bf16[8,8,512]{2,1,0:T(8,128)(2,1)S(1)}, bf16[8,8,512]{2,1,0:T(8,128)(2,1)S(1)}, u32[]{:S(2)}, u32[]{:S(2)}) collective-permute-start(bf16[8,8,512]{2,1,0:T(8,128)(2,1)S(1)} %collective-permute-done.18.refs_3_), channel_id=1, source_target_pairs={{0,1},{1,0},{2,3},{3,2},{4,5},{5,4},{6,7},{7,6},{8,9},{9,8},{10,11... | collective-permute-start | bytes 196616 | tf_op jit(solution)/shard_map/ppermute | solution.py:35
  69.7 2.1 %collective-permute-start.25 = (bf16[72,8,512]{2,1,0:T(8,128)(2,1)S(1)}, bf16[72,8,512]{2,1,0:T(8,128)(2,1)S(1)}, u32[]{:S(2)}, u32[]{:S(2)}) collective-permute-start(bf16[72,8,512]{2,1,0:T(8,128)(2,1)S(1)} %get-tuple-element.45), channel_id=1, source_target_pairs={{0,1},{1,0},{2,3},{3,2},{4,5},{5,4},{6,7},{7,6},{8,9},{9,8},{10,11... | collective-permute-start | bytes 1769480 | tf_op jit(solution)/shard_map/ppermute | solution.py:35
  69.9 2.5 %collective-permute-start.29 = (bf16[56,8,512]{2,1,0:T(8,128)(2,1)S(1)}, bf16[56,8,512]{2,1,0:T(8,128)(2,1)S(1)}, u32[]{:S(2)}, u32[]{:S(2)}) collective-permute-start(bf16[56,8,512]{2,1,0:T(8,128)(2,1)S(1)} %get-tuple-element.52), channel_id=1, source_target_pairs={{0,1},{1,0},{2,3},{3,2},{4,5},{5,4},{6,7},{7,6},{8,9},{9,8},{10,11... | collective-permute-start | bytes 1376264 | tf_op jit(solution)/shard_map/ppermute | solution.py:35
  71.9 9.1 %collective-permute-start.26 = (bf16[36,8,512]{2,1,0:T(8,128)(2,1)S(1)}, bf16[36,8,512]{2,1,0:T(8,128)(2,1)S(1)}, u32[]{:S(2)}, u32[]{:S(2)}) collective-permute-start(bf16[36,8,512]{2,1,0:T(8,128)(2,1)S(1)} %get-tuple-element.47), channel_id=1, source_target_pairs={{0,4},{1,5},{2,6},{3,7},{4,0},{5,1},{6,2},{7,3},{8,12},{9,13},{10,... | collective-permute-start | bytes 884744 | tf_op jit(solution)/shard_map/ppermute | solution.py:35
  72.5 10.8 %collective-permute-start.30 = (bf16[28,8,512]{2,1,0:T(8,128)(2,1)S(1)}, bf16[28,8,512]{2,1,0:T(8,128)(2,1)S(1)}, u32[]{:S(2)}, u32[]{:S(2)}) collective-permute-start(bf16[28,8,512]{2,1,0:T(8,128)(2,1)S(1)} %get-tuple-element.54), channel_id=1, source_target_pairs={{0,2},{1,3},{2,0},{3,1},{4,6},{5,7},{6,4},{7,5},{8,10},{9,11},{10,... | collective-permute-start | bytes 688136 | tf_op jit(solution)/shard_map/ppermute | solution.py:35
  81.1 9.3 %collective-permute-start.27 = (bf16[18,8,512]{2,1,0:T(8,128)(2,1)S(1)}, bf16[18,8,512]{2,1,0:T(8,128)(2,1)S(1)}, u32[]{:S(2)}, u32[]{:S(2)}) collective-permute-start(bf16[18,8,512]{2,1,0:T(8,128)(2,1)S(1)} %get-tuple-element.49), channel_id=1, source_target_pairs={{0,8},{1,9},{2,10},{3,11},{4,12},{5,13},{6,14},{7,15},{8,0},{9,1},... | collective-permute-start | bytes 442376 | tf_op jit(solution)/shard_map/ppermute | solution.py:35
  83.4 7.6 %collective-permute-start.31 = (bf16[14,8,512]{2,1,0:T(8,128)(2,1)S(1)}, bf16[14,8,512]{2,1,0:T(8,128)(2,1)S(1)}, u32[]{:S(2)}, u32[]{:S(2)}) collective-permute-start(bf16[14,8,512]{2,1,0:T(8,128)(2,1)S(1)} %get-tuple-element.56), channel_id=1, source_target_pairs={{0,4},{1,5},{2,6},{3,7},{4,0},{5,1},{6,2},{7,3},{8,12},{9,13},{10,... | collective-permute-start | bytes 344072 | tf_op jit(solution)/shard_map/ppermute | solution.py:35
  90.4 5.7 %collective-permute-start.28 = (bf16[9,8,512]{2,1,0:T(8,128)(2,1)S(1)}, bf16[9,8,512]{2,1,0:T(8,128)(2,1)S(1)}, u32[]{:S(2)}, u32[]{:S(2)}) collective-permute-start(bf16[9,8,512]{2,1,0:T(8,128)(2,1)S(1)} %get-tuple-element.51), channel_id=1, source_target_pairs={{0,2},{1,3},{2,0},{3,1},{4,6},{5,7},{6,4},{7,5},{8,10},{9,11},{10,... | collective-permute-start | bytes 221192 | tf_op jit(solution)/shard_map/ppermute | solution.py:35
  91.0 5.2 %collective-permute-start.32 = (bf16[7,8,512]{2,1,0:T(8,128)(2,1)S(1)}, bf16[7,8,512]{2,1,0:T(8,128)(2,1)S(1)}, u32[]{:S(2)}, u32[]{:S(2)}) collective-permute-start(bf16[7,8,512]{2,1,0:T(8,128)(2,1)S(1)} %get-tuple-element.58), channel_id=1, source_target_pairs={{0,8},{1,9},{2,10},{3,11},{4,12},{5,13},{6,14},{7,15},{8,0},{9,1},... | collective-permute-start | bytes 172040 | tf_op jit(solution)/shard_map/ppermute | solution.py:35

commit v8 on v6

v8 whole, which is shorter than its diff:
```python
import math

import jax
import jax.numpy as jnp
from jax import lax
from jax.experimental import pallas as pl
from jax.experimental.pallas import tpu as pltpu
from jax.sharding import PartitionSpec as P

BF16 = jnp.bfloat16
F32 = jnp.float32
I32 = jnp.int32
GROUP = 8
SKEW = 3
SQUARE = (6, 2, 4)
LANES = 128
MIB = 1024 * 1024


def whole(space=pltpu.VMEM):
    return pl.BlockSpec(memory_space=space)


def shape(dims, dtype):
    return jax.ShapeDtypeStruct(tuple(dims), dtype)


def size_of(array):
    return math.prod(array.shape) * jnp.dtype(array.dtype).itemsize


def swap(array, bits):
    count = lax.axis_size("tile")
    return lax.ppermute(array, "tile", [(i, i ^ bits) for i in range(count)])


def local(
    body, outs, *ins, name, scratch=0, scratches=(), specs=None, out_specs=None, flops=0, after=(), aliases=None
):
    nbytes = sum(size_of(a) for a in (*ins, *outs))
    specs = list(specs or [whole()] * len(ins)) + [whole()] * len(after)
    out_specs = list(out_specs or [whole()] * len(outs))
    own = len(ins)
    ins = [pltpu.with_memory_space_constraint(a, s.memory_space) for a, s in zip((*ins, *after), specs)]

    def run(*refs):
        body(*refs[:own], *refs[len(ins) :])

    return pl.pallas_call(
        run,
        out_shape=[a if s.memory_space is None else s.memory_space(a.shape, a.dtype) for a, s in zip(outs, out_specs)],
        in_specs=specs,
        out_specs=[whole() if s.memory_space is None else s for s in out_specs],
        input_output_aliases=aliases or {},
        scratch_shapes=list(scratches),
        compiler_params=pltpu.CompilerParams(vmem_limit_bytes=scratch + 8 * MIB),
        cost_estimate=pl.CostEstimate(flops=flops, bytes_accessed=nbytes, transcendentals=0),
        name=name,
    )(*ins)


def fetch(pairs, sems):
    copies = [pltpu.make_async_copy(a, b, sems.at[i]) for i, (a, b) in enumerate(pairs)]
    for copy in copies:
        copy.start()
    for copy in copies:
        copy.wait()


def load(array, after, name):
    count, rank, width = array.shape
    half = width // 2
    pieces = 4
    n = count // pieces

    def body(source, mine, other, sems):
        core = lax.axis_index("tile") & 1
        pairs = []
        for out, which in ((other, 1 - core), (mine, core)):
            lanes = pl.ds(pl.multiple_of(which * half, half), half)
            for i in range(pieces):
                rows = pl.ds(i * n, n)
                pairs.append((source.at[rows, :, lanes], out.at[rows]))
        fetch(pairs, sems)

    return local(
        body,
        [shape((count, rank, half), array.dtype)] * 2,
        array,
        name=name,
        specs=[whole(pltpu.HBM)],
        scratches=[pltpu.SemaphoreType.DMA((2 * pieces,))],
        after=after,
    )


def scale_body(contrast, level, label, probes, mine, other, scaling, contrast_near, level_near, label_near, probes_near, sems):
    fetch(
        [(contrast, contrast_near), (level, level_near), (label, label_near), (probes, probes_near)],
        sems,
    )
    odd = (lax.axis_index("tile") & 1) != 0
    value = level_near[...]
    unit = label_near[...]
    factor = jnp.zeros_like(value)
    for k in range(contrast.shape[0]):
        factor = jnp.where(unit == k, contrast_near[k], factor)
    scaling[...] = factor / (1.0 + value * value)
    blocks, _, half = mine.shape
    rows = half // LANES
    for b in range(blocks):
        for c in range(rows):
            low, high = [
                probes_near[:, j * LANES : (j + 1) * LANES] * scaling[j : j + 1, :]
                for j in (2 * b * rows + c, (2 * b + 1) * rows + c)
            ]
            lanes = slice(c * LANES, (c + 1) * LANES)
            mine[b, :, lanes] = jnp.where(odd, high, low).astype(BF16)
            other[b, :, lanes] = jnp.where(odd, low, high).astype(BF16)


def final_body(keep, recv, other, scaling, out):
    odd = (lax.axis_index("tile") & 1) != 0
    blocks, _, half = other.shape
    rows = half // LANES
    for b in range(blocks):
        for c in range(rows):
            lanes = slice(c * LANES, (c + 1) * LANES)
            own = keep[b, :, lanes] + recv[b, :, lanes].astype(F32)
            got = other[b, :, lanes]
            for j, total in (
                (2 * b * rows + c, jnp.where(odd, got, own)),
                ((2 * b + 1) * rows + c, jnp.where(odd, own, got)),
            ):
                out[:, j * LANES : (j + 1) * LANES] = total * scaling[j : j + 1, :]


def join_body(*refs):
    out, at = refs[-1], 0
    for ref in refs[:-1]:
        out[at : at + ref.shape[0]] = ref[...]
        at += ref.shape[0]


def join(*pieces, after=()):
    out = shape((sum(a.shape[0] for a in pieces),) + pieces[0].shape[1:], pieces[0].dtype)
    return local(join_body, [out], *pieces, name="join", after=after)[0]


def plus(total, *gots):
    dims = gots[0].shape

    def body(total, *refs):
        done = total[: dims[0]]
        for ref in refs[:-2]:
            done = done + ref[...].astype(F32)
        refs[-2][...] = done
        refs[-1][...] = done.astype(BF16)

    return local(body, [shape(dims, F32), shape(dims, BF16)], total, *gots, name="plus")


def weigh(total, got, weight):
    def body(total, got, weight, out):
        core = lax.axis_index("tile") & 1
        blocks, _, half = out.shape
        rows = half // LANES
        for b in range(blocks):
            for c in range(rows):
                lanes = slice(c * LANES, (c + 1) * LANES)
                done = total[b, :, lanes] + got[b, :, lanes].astype(F32)
                row = weight[pl.ds((2 * b + core) * rows + c, 1), :]
                out[b, :, lanes] = (done * row).astype(BF16)

    return local(body, [shape(total.shape, BF16)], total, got, weight, name="weigh")[0]


def fold(keep, recv, dtypes=(F32, BF16), base=0):
    n = recv.shape[0] // len(dtypes)
    outs = [shape((n,) + keep.shape[1:], t) for t in dtypes]

    def body(keep, recv, *outs):
        for i, out in enumerate(outs):
            mine = keep[base + i * n : base + (i + 1) * n]
            out[...] = (mine + recv[i * n : (i + 1) * n].astype(F32)).astype(out.dtype)

    return local(body, outs, keep, recv, name="fold")


def zeros(dims, after):
    def body(out):
        out[...] = jnp.zeros_like(out)

    return local(body, [shape(dims, F32)], name="zeros", after=after)[0]


def own_mask(rank, probes):
    dims = (GROUP * probes, GROUP * rank)
    rows = lax.broadcasted_iota(I32, dims, 0) // probes
    columns = lax.broadcasted_iota(I32, dims, 1)
    return jnp.where(rows == columns // rank, columns % rank, rank)


def skewed(groups, *stages):
    held = {}
    last = SKEW * (len(stages) - 1)
    for step in range(groups + last):
        for k in range(len(stages) - 1, -1, -1):
            g = step - k * SKEW
            if 0 <= g < groups:
                held[g] = stages[k](g, held.get(g))
                if k == len(stages) - 1:
                    del held[g]


def shrink(pieces, at_rows, table, factors, name):
    count, rank, half = factors[0].shape
    probes = pieces[0].shape[1]
    groups = count // GROUP
    span = GROUP * rank
    rows = sum(piece.shape[0] for piece in pieces)

    def body(at, *refs):
        mine, other, out, near = refs[len(pieces) :]
        join_body(*refs[: len(pieces)], near)
        own = own_mask(rank, probes)
        lane_tile = lax.broadcasted_iota(I32, (1, span), 1) // rank

        def dots(g, _):
            row, first = at_rows[g // groups], (g % groups) * GROUP
            taken = jnp.concatenate([near[at[row, first + i]].astype(F32) for i in range(GROUP)], axis=0)
            factor = (mine, other)[g // groups][first : first + GROUP].reshape(span, half)
            return lax.dot_general(
                taken.astype(BF16), factor, (((1,), (1,)), ((), ())), preferred_element_type=F32
            )

        def store(g, inner):
            row, first = 4 + g // groups, (g % groups) * GROUP
            limit = jnp.zeros((1, span), I32)
            for i in range(GROUP):
                limit = jnp.where(lane_tile == i, at[row, first + i], limit)
            inner = jnp.where(own < limit, inner, 0.0)
            out[g] = sum(inner[i * probes : (i + 1) * probes] for i in range(GROUP))

        skewed(2 * groups, dots, store)

    return local(
        body,
        [shape((2 * groups, probes, span), F32)],
        table,
        *pieces,
        *factors,
        name=name,
        specs=[whole(pltpu.SMEM)] + [whole()] * (len(pieces) + 2),
        flops=4 * count * rank * half * probes * GROUP,
        scratch=2 * rows * probes * half,
        scratches=[pltpu.VMEM((rows, probes, half), BF16)],
    )[0]


def expand(mine_sum, other_sum, at_rows, table, factors, acc, sends, name):
    count, rank, half = factors[0].shape
    probes = acc.shape[1]
    groups = count // GROUP
    span = GROUP * rank

    def body(at, _, sums, got, mine, other, out, *parts):
        own = own_mask(rank, probes) < rank

        def dots(g, _):
            total = sums[g] + got[(g + groups) % (2 * groups)]
            total = jnp.concatenate([total.astype(BF16).astype(F32)] * GROUP, axis=0)
            total = jnp.where(own, total, 0.0).astype(BF16)
            first = (g % groups) * GROUP
            factor = (mine, other)[g // groups][first : first + GROUP].reshape(span, half)
            return jnp.dot(total, factor, preferred_element_type=F32)

        def add(g, outer):
            row, first = at_rows[g // groups], (g % groups) * GROUP
            for i in range(GROUP):
                to = at[row, first + i]
                out[to] = out[to] + outer[i * probes : (i + 1) * probes]

        skewed(2 * groups, dots, add)
        for part, (start, size) in zip(parts, sends):
            part[...] = out[start : start + size].astype(BF16)

    return local(
        body,
        [shape(acc.shape, F32)] + [shape((size, probes, half), BF16) for _, size in sends],
        table,
        acc,
        mine_sum,
        other_sum,
        *factors,
        name=name,
        specs=[whole(pltpu.SMEM)] + [whole()] * 5,
        aliases={1: 0},
        flops=4 * count * rank * half * probes * GROUP,
    )


def place(relative, order):
    at = jnp.zeros_like(relative)
    for k, bit in enumerate(order):
        at = at + jnp.where((relative & bit) != 0, 1 << k, 0)
    return at


def plan(owners, weight, orders, cell_blocks, station_blocks, after):
    peers, count = owners[0].shape
    rows = 2 * (weight.shape[0] // peers)
    rest = peers // 8

    def body(*refs):
        far, weight_far, table_out, weight_near = refs[:5], refs[5], refs[6], refs[7]
        near, table, sems = refs[8:13], refs[13], refs[14]
        me = lax.axis_index("tile")
        pairs = list(zip(far, near))
        for k in range(rest):
            start = pl.multiple_of((k * 4 + (me & 6) // 2) * rows, rows)
            pairs.append((weight_far.at[pl.ds(start, rows)], weight_near.at[pl.ds(k * rows, rows)]))
        fetch(pairs, sems)
        span = peers // 2
        for k, holder in enumerate((me, me ^ 1)):
            col_owner, col_local, row_owner, row_local, rank = [ref[pl.ds(holder, 1), :] for ref in near]
            away = col_owner ^ me
            spot = jnp.where((away & 1) != 0, span + place(away, orders[1]), place(away, orders[0]))
            table[k : k + 1, :] = spot * cell_blocks + col_local
            away = row_owner ^ me
            spot = (((away & 6) // 2) * rest + row_owner // 8) * 2 + (row_owner & 1)
            table[k + 2 : k + 3, :] = spot * station_blocks + row_local
            table[k + 4 : k + 5, :] = rank
        fetch([(table, table_out)], sems)

    return local(
        body,
        [shape((8, count), I32), shape((rest * rows, LANES), F32)],
        *owners,
        weight,
        name="plan",
        specs=[whole(pltpu.HBM)] * 6,
        out_specs=[whole(pltpu.SMEM), whole()],
        scratches=[pltpu.VMEM((peers, count), I32)] * 5
        + [pltpu.VMEM((8, count), I32), pltpu.SemaphoreType.DMA((5 + rest,))],
        after=after,
    )


def shards(
    probes,
    level_set,
    unit_label,
    contrast,
    station_weight,
    u_factor,
    v_factor,
    col_owner,
    col_local,
    row_owner,
    row_local,
    tile_rank,
):
    peers = lax.axis_size("tile")
    tile_count, _, station_width = u_factor.shape
    cell_width = v_factor.shape[2]
    probe_count, cell_total = probes.shape
    cell_blocks = cell_total // cell_width
    station_blocks = station_weight.shape[0] // (peers * station_width)
    bits = [1 << k for k in range(1, peers.bit_length() - 1)]
    far = bits[:0:-1]
    orders = (far + bits[:1], bits[:1] + far)

    lanes = (cell_total // LANES, LANES)
    half_dims = (cell_blocks, probe_count, cell_width // 2)
    part_p, send, scaling = local(
        scale_body,
        [shape(half_dims, BF16), shape(half_dims, BF16), shape(lanes, F32)],
        contrast,
        level_set.reshape(lanes),
        unit_label.reshape(lanes),
        probes,
        name="scale",
        specs=[whole(pltpu.HBM)] * 4,
        scratches=[
            pltpu.SMEM(contrast.shape, F32),
            pltpu.VMEM(lanes, F32),
            pltpu.VMEM(lanes, I32),
            pltpu.VMEM(probes.shape, F32),
            pltpu.SemaphoreType.DMA((4,)),
        ],
    )
    part_q = swap(send, 1)
    table, weight = plan(
        [a.reshape(peers, tile_count) for a in (col_owner, col_local, row_owner, row_local, tile_rank)],
        station_weight.reshape(-1, LANES),
        orders,
        cell_blocks,
        station_blocks,
        (scaling,),
    )
    steps = list(zip(*orders))
    after = (weight,)
    for step, (bit_p, bit_q) in enumerate(steps):
        got_p = swap(part_p, bit_p)
        got_q = swap(part_q, bit_q)
        if step == 1:
            v_here, v_send = load(v_factor, (part_p, part_q), "load_v")
            u_here, u_send = load(u_factor, (part_p, part_q, v_here), "load_u")
            after = (u_here,)
        if step < len(steps) - 1:
            part_p = join(part_p, got_p, after=after)
            part_q = join(part_q, got_q)
            after = ()
    v_both = (v_here, swap(v_send, 1))
    u_both = (u_here, swap(u_send, 1))

    stations = peers * station_blocks
    acc = zeros((stations, probe_count, station_width // 2), (part_p, part_q))
    coeff = shrink([part_p, got_p, part_q, got_q], (0, 1), table, v_both, "coeff")
    quarter = stations // 4
    total, *sends = expand(
        coeff,
        swap(coeff, 1),
        (2, 3),
        table,
        u_both,
        acc,
        [(k // 2 * quarter, quarter) for k in SQUARE],
        "partial",
    )
    total, send = plus(total, *[swap(send, k) for k, send in zip(SQUARE, sends)])
    for bit in bits[2:-1]:
        total, send = plus(total, swap(send, bit))
    weighted = weigh(total, swap(send, bits[-1]), weight)
    gots = {k: swap(weighted, k) for k in SQUARE}

    cells = peers * cell_blocks
    acc = zeros((cells, probe_count, cell_width // 2), (total,))
    back = shrink([weighted, gots[2], gots[4], gots[6]], (2, 3), table, u_both, "back")
    total, send_p, send_q = expand(
        back,
        swap(back, 1),
        (0, 1),
        table,
        v_both,
        acc,
        [(cells // 4, cells // 4), (3 * cells // 4, cells // 4)],
        "spread",
    )
    keep_p, keep_q, base = total, total, cells // 2
    for step, (bit_p, bit_q) in enumerate(steps[::-1]):
        got_p = swap(send_p, bit_p)
        got_q = swap(send_q, bit_q)
        if step < len(steps) - 1:
            keep_p, send_p = fold(keep_p, got_p)
            keep_q, send_q = fold(keep_q, got_q, base=base)
            base = 0
    other = fold(keep_q, got_q, (F32,))[0]
    return local(
        final_body,
        [shape((probe_count, cell_total), F32)],
        keep_p,
        got_p,
        swap(other, 1),
        scaling,
        name="final",
        out_specs=[whole(None)],
    )[0]


def solution(mesh):
    placed = (
        P(None, ("groups", "tile")),
        P(("groups", "tile")),
        P(("groups", "tile")),
        P("groups"),
        P("groups"),
        P(("groups", "tile"), None, None),
        P(("groups", "tile"), None, None),
        P("groups", None),
        P("groups"),
        P("groups", None),
        P("groups"),
        P("groups"),
    )
    return jax.shard_map(
        shards, mesh=mesh, in_specs=placed, out_specs=P(None, ("groups", "tile")), check_vma=False
    )
```

time: 81.3 us -> 89.5 us (1.10)
  waiting for transfers between devices: 39.5 us -> 49.7 us
  starting transfers between devices: 28.4 us -> 25.2 us
  Pallas kernels: 12.9 us -> 14.1 us
    ppermute x31 -> x25, waiting for transfers between devices: 39.5 us -> 49.7 us  [swap(): return lax.ppermute(array, 'tile', [(i, i ^ bits) for i in range(count)])]
    ppermute x31 -> x25, starting transfers between devices: 28.4 us -> 25.2 us  [swap(): return lax.ppermute(array, 'tile', [(i, i ^ bits) for i in range(count)])]
    pallas_call x26 -> x22, Pallas kernels: 12.9 us -> 14.1 us  [local(): pl.pallas_call(run, out_shape=[a if s.memory_space is None else s.memory_...]
  transfers between devices with their start and end apart: 31 -> 25, of which waited for: 20 -> 19; matrix products, arithmetic and copies ran while one was open for 0% -> 0% of each run, Pallas kernels for 8% -> 6%
where the time goes in v8:
time: 89.5 us; the launch traced here: 89.2 us
  waiting for transfers between devices  49.7 us (56%)
  starting transfers between devices  25.2 us (28%)
  Pallas kernels  14.1 us (16%)
    ppermute x25, waiting for transfers between devices, swap(): return lax.ppermute(array, 'tile', [(i, i ^ bits) for i in range(count)])  49.7 us
    ppermute x25, starting transfers between devices, swap(): return lax.ppermute(array, 'tile', [(i, i ^ bits) for i in range(count)])  25.2 us
    pallas_call x22, Pallas kernels, local(): pl.pallas_call(run, out_shape=[a if s.memory_space is None else s.memory_...  14.1 us
  transfers between devices with their start and end apart: 25, of which 19 were waited for; matrix products, arithmetic and copies ran while one was open for 0% of the time, Pallas kernels for 6%

profile of v8, /device:TPU:0, one launch (start us, length us, event | category | flops | bytes accessed | tf_op | source)
XLA Modules:
  0.0 89.2 jit_solution(18177933001929584863)
XLA Ops:
  0.0 1.1 %scale.1 = (bf16[16,8,256]{2,1,0:T(8,128)(2,1)S(1)}, bf16[16,8,256]{2,1,0:T(8,128)(2,1)S(1)}, f32[64,128]{1,0:T(8,128)S(1)}) custom-call(f32[4]{0:T(128)} %refs_0_.3, f32[64,128]{1,0:T(8,128)} %bitcast.9, s32[64,128]{1,0:T(8,128)} %bitcast.10, f32[8,8192]{1,0:T(8,128)} %refs_3_.1), custom_call_target="tpu_custom_call" | custom-call | bytes 491536 | tf_op jit(solution)/shard_map/scale/pallas_call | solution.py:49
  1.1 0.5 collective-permute-start.2
  1.6 3.7 %collective-permute-start = (bf16[16,8,256]{2,1,0:T(8,128)(2,1)S(1)}, bf16[16,8,256]{2,1,0:T(8,128)(2,1)S(1)}, u32[]{:S(2)}, u32[]{:S(2)}) collective-permute-start(bf16[16,8,256]{2,1,0:T(8,128)(2,1)S(1)} %get-tuple-element.33.refs_0_), channel_id=1, source_target_pairs={{0,8},{1,9},{2,10},{3,11},{4,12},{5,13},{6,14},{7,15},{8,0},{9,1},... | collective-permute-start | bytes 196616 | tf_op jit(solution)/shard_map/ppermute | solution.py:34
  5.3 1.5 %collective-permute-start.3 = (bf16[16,8,256]{2,1,0:T(8,128)(2,1)S(1)}, bf16[16,8,256]{2,1,0:T(8,128)(2,1)S(1)}, u32[]{:S(2)}, u32[]{:S(2)}) collective-permute-start(bf16[16,8,256]{2,1,0:T(8,128)(2,1)S(1)} %collective-permute-done.2.refs_0_), channel_id=1, source_target_pairs={{0,2},{1,3},{2,0},{3,1},{4,6},{5,7},{6,4},{7,5},{8,10},{9,11},{10,... | collective-permute-start | bytes 196616 | tf_op jit(solution)/shard_map/ppermute | solution.py:34
  6.8 1.5 %plan.1 = (s32[8,128]{1,0:T(8,128)S(4)}, f32[64,128]{1,0:T(8,128)S(1)}) custom-call(s32[16,128]{1,0:T(8,128)} %bitcast.11, s32[16,128]{1,0:T(8,128)} %bitcast.12, s32[16,128]{1,0:T(8,128)} %bitcast.13, s32[16,128]{1,0:T(8,128)} %bitcast.14, s32[16,128]{1,0:T(8,128)} %bitcast.15, f32[256,128]{1,0:T(8,128)} %bitcast.8, ...), custom_call_target="tpu_custom_call" | custom-call | bytes 208896 | tf_op jit(solution)/shard_map/plan/pallas_call | solution.py:49
  8.3 1.1 %collective-permute-done.refs_1_ = bf16[16,8,256]{2,1,0:T(8,128)(2,1)S(1)} collective-permute-done((bf16[16,8,256]{2,1,0:T(8,128)(2,1)S(1)}, bf16[16,8,256]{2,1,0:T(8,128)(2,1)S(1)}, u32[]{:S(2)}, u32[]{:S(2)}) %collective-permute-start) | collective-permute-done | bytes 65568 | tf_op jit(solution)/shard_map/ppermute | solution.py:34
  9.4 0.2 collective-permute-done.3.refs_1_
  9.5 2.2 %load_v.1 = (bf16[128,32,256]{2,1,0:T(8,128)(2,1)S(1)}, bf16[128,32,256]{2,1,0:T(8,128)(2,1)S(1)}) custom-call(bf16[128,32,512]{2,1,0:T(8,128)(2,1)} %refs_0_.4, bf16[32,8,256]{2,1,0:T(8,128)(2,1)S(1)} %join.4.refs_1_.refs_0_, bf16[32,8,256]{2,1,0:T(8,128)(2,1)S(1)} %join.5.refs_2_.refs_0_), custom_call_target="tpu_custom_call" | custom-call | bytes 8388608 | tf_op jit(solution)/shard_map/load_v/pallas_call | solution.py:49
  11.9 2.2 %load_u.1 = (bf16[128,32,256]{2,1,0:T(8,128)(2,1)S(1)}, bf16[128,32,256]{2,1,0:T(8,128)(2,1)S(1)}) custom-call(bf16[128,32,512]{2,1,0:T(8,128)(2,1)} %refs_0_.5, bf16[32,8,256]{2,1,0:T(8,128)(2,1)S(1)} %join.4.refs_1_.refs_0_, bf16[32,8,256]{2,1,0:T(8,128)(2,1)S(1)} %join.5.refs_2_.refs_0_, bf16[128,32,256]{2,1,0:T(8,128)(2,1)S(1)} %get-tuple-element.36.refs_3_.refs_5_.refs_4_), custom_call_target="tpu_custom_call" | custom-call | bytes 8388608 | tf_op jit(solution)/shard_map/load_u/pallas_call | solution.py:49
  14.1 0.5 collective-permute-start.9
  14.6 1.6 %collective-permute-start.1 = (bf16[32,8,256]{2,1,0:T(8,128)(2,1)S(1)}, bf16[32,8,256]{2,1,0:T(8,128)(2,1)S(1)}, u32[]{:S(2)}, u32[]{:S(2)}) collective-permute-start(bf16[32,8,256]{2,1,0:T(8,128)(2,1)S(1)} %join.4.refs_1_.refs_0_), channel_id=1, source_target_pairs={{0,4},{1,5},{2,6},{3,7},{4,0},{5,1},{6,2},{7,3},{8,12},{9,13},{10,... | collective-permute-start | bytes 393224 | tf_op jit(solution)/shard_map/ppermute | solution.py:34
  16.2 2.4 %collective-permute-start.4 = (bf16[32,8,256]{2,1,0:T(8,128)(2,1)S(1)}, bf16[32,8,256]{2,1,0:T(8,128)(2,1)S(1)}, u32[]{:S(2)}, u32[]{:S(2)}) collective-permute-start(bf16[32,8,256]{2,1,0:T(8,128)(2,1)S(1)} %join.5.refs_2_.refs_0_), channel_id=1, source_target_pairs={{0,8},{1,9},{2,10},{3,11},{4,12},{5,13},{6,14},{7,15},{8,0},{9,1},... | collective-permute-start | bytes 393224 | tf_op jit(solution)/shard_map/ppermute | solution.py:34
  18.6 3.8 %collective-permute-done.1.refs_1_ = bf16[32,8,256]{2,1,0:T(8,128)(2,1)S(1)} collective-permute-done((bf16[32,8,256]{2,1,0:T(8,128)(2,1)S(1)}, bf16[32,8,256]{2,1,0:T(8,128)(2,1)S(1)}, u32[]{:S(2)}, u32[]{:S(2)}) %collective-permute-start.1) | collective-permute-done | bytes 131104 | tf_op jit(solution)/shard_map/ppermute | solution.py:34
  22.4 1.6 %collective-permute-start.5 = (bf16[64,8,256]{2,1,0:T(8,128)(2,1)S(1)}, bf16[64,8,256]{2,1,0:T(8,128)(2,1)S(1)}, u32[]{:S(2)}, u32[]{:S(2)}) collective-permute-start(bf16[64,8,256]{2,1,0:T(8,128)(2,1)S(1)} %join.6.refs_0_.refs_1_), channel_id=1, source_target_pairs={{0,2},{1,3},{2,0},{3,1},{4,6},{5,7},{6,4},{7,5},{8,10},{9,11},{10,... | collective-permute-start | bytes 786440 | tf_op jit(solution)/shard_map/ppermute | solution.py:34
  24.0 1.2 %collective-permute-done.4.refs_1_ = bf16[32,8,256]{2,1,0:T(8,128)(2,1)S(1)} collective-permute-done((bf16[32,8,256]{2,1,0:T(8,128)(2,1)S(1)}, bf16[32,8,256]{2,1,0:T(8,128)(2,1)S(1)}, u32[]{:S(2)}, u32[]{:S(2)}) %collective-permute-start.4) | collective-permute-done | bytes 131104 | tf_op jit(solution)/shard_map/ppermute | solution.py:34
  25.2 0.2 collective-permute-start.6
  25.4 3.5 %collective-permute-done.5.refs_2_ = bf16[64,8,256]{2,1,0:T(8,128)(2,1)S(1)} collective-permute-done((bf16[64,8,256]{2,1,0:T(8,128)(2,1)S(1)}, bf16[64,8,256]{2,1,0:T(8,128)(2,1)S(1)}, u32[]{:S(2)}, u32[]{:S(2)}) %collective-permute-start.5) | collective-permute-done | bytes 262176 | tf_op jit(solution)/shard_map/ppermute | solution.py:34
  28.9 2.8 %collective-permute-done.6.refs_4_ = bf16[64,8,256]{2,1,0:T(8,128)(2,1)S(1)} collective-permute-done((bf16[64,8,256]{2,1,0:T(8,128)(2,1)S(1)}, bf16[64,8,256]{2,1,0:T(8,128)(2,1)S(1)}, u32[]{:S(2)}, u32[]{:S(2)}) %collective-permute-start.6) | collective-permute-done | bytes 262176 | tf_op jit(solution)/shard_map/ppermute | solution.py:34
  31.6 1.4 %coeff.1.refs_2_ = f32[32,8,256]{2,1,0:T(8,128)S(1)} custom-call(s32[8,128]{1,0:T(8,128)S(4)} %get-tuple-element.32.refs_0_, bf16[64,8,256]{2,1,0:T(8,128)(2,1)S(1)} %join.6.refs_0_.refs_1_, bf16[64,8,256]{2,1,0:T(8,128)(2,1)S(1)} %collective-permute-done.5.refs_2_, bf16[64,8,256]{2,1,0:T(8,128)(2,1)S(1)} %join.7.refs_1_.refs_3_, ...), custom_call_target="tpu_custom_call" | custom-call | flops 268435456 | bytes 5509120 | tf_op jit(solution)/shard_map/coeff/pallas_call | solution.py:49
  33.2 1.5 %collective-permute-done.8.refs_3_ = f32[32,8,256]{2,1,0:T(8,128)S(1)} collective-permute-done((f32[32,8,256]{2,1,0:T(8,128)S(1)}, f32[32,8,256]{2,1,0:T(8,128)S(1)}, u32[]{:S(2)}, u32[]{:S(2)}) %collective-permute-start.8) | collective-permute-done | bytes 262176 | tf_op jit(solution)/shard_map/ppermute | solution.py:34
  34.7 1.5 %partial.1 = (f32[64,8,256]{2,1,0:T(8,128)S(1)}, bf16[16,8,256]{2,1,0:T(8,128)(2,1)S(1)}, bf16[16,8,256]{2,1,0:T(8,128)(2,1)S(1)}, bf16[16,8,256]{2,1,0:T(8,128)(2,1)S(1)}) custom-call(s32[8,128]{1,0:T(8,128)S(4)} %get-tuple-element.32.refs_0_, f32[64,8,256]{2,1,0:T(8,128)S(1)} %zeros.2.refs_1_, ...), custom_call_target="tpu_custom_call", output_to_operand_aliasing={{0}: (1, {})} | custom-call | flops 268435456 | bytes 5967872 | tf_op jit(solution)/shard_map/partial/pallas_call | solution.py:49
  36.2 2.5 %collective-permute-start.10 = (bf16[16,8,256]{2,1,0:T(8,128)(2,1)S(1)}, bf16[16,8,256]{2,1,0:T(8,128)(2,1)S(1)}, u32[]{:S(2)}, u32[]{:S(2)}) collective-permute-start(bf16[16,8,256]{2,1,0:T(8,128)(2,1)S(1)} %get-tuple-element.41), channel_id=1, source_target_pairs={{0,6},{1,7},{2,4},{3,5},{4,2},{5,3},{6,0},{7,1},{8,14},{9,15},{10,... | collective-permute-start | bytes 196616 | tf_op jit(solution)/shard_map/ppermute | solution.py:34
  38.6 0.5 collective-permute-start.11
  39.2 0.6 collective-permute-start.12
  39.7 1.7 %collective-permute-done.10.refs_1_ = bf16[16,8,256]{2,1,0:T(8,128)(2,1)S(1)} collective-permute-done((bf16[16,8,256]{2,1,0:T(8,128)(2,1)S(1)}, bf16[16,8,256]{2,1,0:T(8,128)(2,1)S(1)}, u32[]{:S(2)}, u32[]{:S(2)}) %collective-permute-start.10) | collective-permute-done | bytes 65568 | tf_op jit(solution)/shard_map/ppermute | solution.py:34
  41.5 1.5 %collective-permute-done.11.refs_2_ = bf16[16,8,256]{2,1,0:T(8,128)(2,1)S(1)} collective-permute-done((bf16[16,8,256]{2,1,0:T(8,128)(2,1)S(1)}, bf16[16,8,256]{2,1,0:T(8,128)(2,1)S(1)}, u32[]{:S(2)}, u32[]{:S(2)}) %collective-permute-start.11) | collective-permute-done | bytes 65568 | tf_op jit(solution)/shard_map/ppermute | solution.py:34
  42.9 0.5 collective-permute-done.12.refs_3_
  43.5 2.5 %collective-permute-start.13 = (bf16[16,8,256]{2,1,0:T(8,128)(2,1)S(1)}, bf16[16,8,256]{2,1,0:T(8,128)(2,1)S(1)}, u32[]{:S(2)}, u32[]{:S(2)}) collective-permute-start(bf16[16,8,256]{2,1,0:T(8,128)(2,1)S(1)} %get-tuple-element.45), channel_id=1, source_target_pairs={{0,8},{1,9},{2,10},{3,11},{4,12},{5,13},{6,14},{7,15},{8,0},{9,1},... | collective-permute-start | bytes 196616 | tf_op jit(solution)/shard_map/ppermute | solution.py:34
  46.0 3.4 %collective-permute-done.13.refs_1_ = bf16[16,8,256]{2,1,0:T(8,128)(2,1)S(1)} collective-permute-done((bf16[16,8,256]{2,1,0:T(8,128)(2,1)S(1)}, bf16[16,8,256]{2,1,0:T(8,128)(2,1)S(1)}, u32[]{:S(2)}, u32[]{:S(2)}) %collective-permute-start.13) | collective-permute-done | bytes 65568 | tf_op jit(solution)/shard_map/ppermute | solution.py:34
  49.4 1.0 %collective-permute-start.16 = (bf16[16,8,256]{2,1,0:T(8,128)(2,1)S(1)}, bf16[16,8,256]{2,1,0:T(8,128)(2,1)S(1)}, u32[]{:S(2)}, u32[]{:S(2)}) collective-permute-start(bf16[16,8,256]{2,1,0:T(8,128)(2,1)S(1)} %weigh.1.refs_1_), channel_id=1, source_target_pairs={{0,6},{1,7},{2,4},{3,5},{4,2},{5,3},{6,0},{7,1},{8,14},{9,15},{10,... | collective-permute-start | bytes 196616 | tf_op jit(solution)/shard_map/ppermute | solution.py:34
  50.4 2.1 %collective-permute-start.15 = (bf16[16,8,256]{2,1,0:T(8,128)(2,1)S(1)}, bf16[16,8,256]{2,1,0:T(8,128)(2,1)S(1)}, u32[]{:S(2)}, u32[]{:S(2)}) collective-permute-start(bf16[16,8,256]{2,1,0:T(8,128)(2,1)S(1)} %weigh.1.refs_1_), channel_id=1, source_target_pairs={{0,4},{1,5},{2,6},{3,7},{4,0},{5,1},{6,2},{7,3},{8,12},{9,13},{10,... | collective-permute-start | bytes 196616 | tf_op jit(solution)/shard_map/ppermute | solution.py:34
  52.6 0.4 collective-permute-start.14
  53.0 1.7 %collective-permute-done.16.refs_4_ = bf16[16,8,256]{2,1,0:T(8,128)(2,1)S(1)} collective-permute-done((bf16[16,8,256]{2,1,0:T(8,128)(2,1)S(1)}, bf16[16,8,256]{2,1,0:T(8,128)(2,1)S(1)}, u32[]{:S(2)}, u32[]{:S(2)}) %collective-permute-start.16) | collective-permute-done | bytes 65568 | tf_op jit(solution)/shard_map/ppermute | solution.py:34
  54.6 0.9 collective-permute-done.15.refs_3_
  55.5 1.3 %collective-permute-done.14.refs_2_ = bf16[16,8,256]{2,1,0:T(8,128)(2,1)S(1)} collective-permute-done((bf16[16,8,256]{2,1,0:T(8,128)(2,1)S(1)}, bf16[16,8,256]{2,1,0:T(8,128)(2,1)S(1)}, u32[]{:S(2)}, u32[]{:S(2)}) %collective-permute-start.14) | collective-permute-done | bytes 65568 | tf_op jit(solution)/shard_map/ppermute | solution.py:34
  56.8 1.4 %back.1.refs_2_ = f32[32,8,256]{2,1,0:T(8,128)S(1)} custom-call(s32[8,128]{1,0:T(8,128)S(4)} %get-tuple-element.32.refs_0_, bf16[16,8,256]{2,1,0:T(8,128)(2,1)S(1)} %weigh.1.refs_1_, bf16[16,8,256]{2,1,0:T(8,128)(2,1)S(1)} %collective-permute-done.14.refs_2_, bf16[16,8,256]{2,1,0:T(8,128)(2,1)S(1)} %collective-permute-done.15.refs_3_, ...), custom_call_target="tpu_custom_call" | custom-call | flops 268435456 | bytes 4722688 | tf_op jit(solution)/shard_map/back/pallas_call | solution.py:49
  58.5 1.4 %collective-permute-done.17.refs_3_ = f32[32,8,256]{2,1,0:T(8,128)S(1)} collective-permute-done((f32[32,8,256]{2,1,0:T(8,128)S(1)}, f32[32,8,256]{2,1,0:T(8,128)S(1)}, u32[]{:S(2)}, u32[]{:S(2)}) %collective-permute-start.17) | collective-permute-done | bytes 262176 | tf_op jit(solution)/shard_map/ppermute | solution.py:34
  59.8 1.5 %spread.1 = (f32[256,8,256]{2,1,0:T(8,128)S(1)}, bf16[64,8,256]{2,1,0:T(8,128)(2,1)S(1)}, bf16[64,8,256]{2,1,0:T(8,128)(2,1)S(1)}) custom-call(s32[8,128]{1,0:T(8,128)S(4)} %get-tuple-element.32.refs_0_, f32[256,8,256]{2,1,0:T(8,128)S(1)} %zeros.3.refs_1_, f32[32,8,256]{2,1,0:T(8,128)S(1)} %back.1.refs_2_, ...), custom_call_target="tpu_custom_call", output_to_operand_aliasing={{0}: (1, {})} | custom-call | flops 268435456 | bytes 9441280 | tf_op jit(solution)/shard_map/spread/pallas_call | solution.py:49
  61.4 0.6 collective-permute-start.18
  62.1 7.7 %collective-permute-done.21.refs_1_ = bf16[64,8,256]{2,1,0:T(8,128)(2,1)S(1)} collective-permute-done((bf16[64,8,256]{2,1,0:T(8,128)(2,1)S(1)}, bf16[64,8,256]{2,1,0:T(8,128)(2,1)S(1)}, u32[]{:S(2)}, u32[]{:S(2)}) %collective-permute-start.21) | collective-permute-done | bytes 262176 | tf_op jit(solution)/shard_map/ppermute | solution.py:34
  69.8 1.8 %collective-permute-start.22 = (bf16[32,8,256]{2,1,0:T(8,128)(2,1)S(1)}, bf16[32,8,256]{2,1,0:T(8,128)(2,1)S(1)}, u32[]{:S(2)}, u32[]{:S(2)}) collective-permute-start(bf16[32,8,256]{2,1,0:T(8,128)(2,1)S(1)} %get-tuple-element.54), channel_id=1, source_target_pairs={{0,8},{1,9},{2,10},{3,11},{4,12},{5,13},{6,14},{7,15},{8,0},{9,1},... | collective-permute-start | bytes 393224 | tf_op jit(solution)/shard_map/ppermute | solution.py:34
  71.6 0.4 collective-permute-start.19
  72.0 6.4 %collective-permute-done.22.refs_1_ = bf16[32,8,256]{2,1,0:T(8,128)(2,1)S(1)} collective-permute-done((bf16[32,8,256]{2,1,0:T(8,128)(2,1)S(1)}, bf16[32,8,256]{2,1,0:T(8,128)(2,1)S(1)}, u32[]{:S(2)}, u32[]{:S(2)}) %collective-permute-start.22) | collective-permute-done | bytes 131104 | tf_op jit(solution)/shard_map/ppermute | solution.py:34
  78.4 0.2 collective-permute-start.23
  78.7 4.1 %collective-permute-done.23.refs_1_ = bf16[16,8,256]{2,1,0:T(8,128)(2,1)S(1)} collective-permute-done((bf16[16,8,256]{2,1,0:T(8,128)(2,1)S(1)}, bf16[16,8,256]{2,1,0:T(8,128)(2,1)S(1)}, u32[]{:S(2)}, u32[]{:S(2)}) %collective-permute-start.23) | collective-permute-done | bytes 65568 | tf_op jit(solution)/shard_map/ppermute | solution.py:34
  82.9 0.3 collective-permute-start.20
  83.2 5.2 %collective-permute-done.20.refs_1_ = bf16[16,8,256]{2,1,0:T(8,128)(2,1)S(1)} collective-permute-done((bf16[16,8,256]{2,1,0:T(8,128)(2,1)S(1)}, bf16[16,8,256]{2,1,0:T(8,128)(2,1)S(1)}, u32[]{:S(2)}, u32[]{:S(2)}) %collective-permute-start.20) | collective-permute-done | bytes 65568 | tf_op jit(solution)/shard_map/ppermute | solution.py:34
  88.4 0.7 final.1
  (24 shorter events, 0.8 us)
Async XLA Ops:
  1.1 4.2 %collective-permute-start.2 = (bf16[16,8,256]{2,1,0:T(8,128)(2,1)S(1)}, bf16[16,8,256]{2,1,0:T(8,128)(2,1)S(1)}, u32[]{:S(2)}, u32[]{:S(2)}) collective-permute-start(bf16[16,8,256]{2,1,0:T(8,128)(2,1)S(1)} %get-tuple-element.35), channel_id=1, source_target_pairs={{0,1},{1,0},{2,3},{3,2},{4,5},{5,4},{6,7},{7,6},{8,9},{9,8},{10,11... | collective-permute-start | bytes 196616 | tf_op jit(solution)/shard_map/ppermute | solution.py:34
  1.6 7.8 %collective-permute-start = (bf16[16,8,256]{2,1,0:T(8,128)(2,1)S(1)}, bf16[16,8,256]{2,1,0:T(8,128)(2,1)S(1)}, u32[]{:S(2)}, u32[]{:S(2)}) collective-permute-start(bf16[16,8,256]{2,1,0:T(8,128)(2,1)S(1)} %get-tuple-element.33.refs_0_), channel_id=1, source_target_pairs={{0,8},{1,9},{2,10},{3,11},{4,12},{5,13},{6,14},{7,15},{8,0},{9,1},... | collective-permute-start | bytes 196616 | tf_op jit(solution)/shard_map/ppermute | solution.py:34
  5.3 4.3 %collective-permute-start.3 = (bf16[16,8,256]{2,1,0:T(8,128)(2,1)S(1)}, bf16[16,8,256]{2,1,0:T(8,128)(2,1)S(1)}, u32[]{:S(2)}, u32[]{:S(2)}) collective-permute-start(bf16[16,8,256]{2,1,0:T(8,128)(2,1)S(1)} %collective-permute-done.2.refs_0_), channel_id=1, source_target_pairs={{0,2},{1,3},{2,0},{3,1},{4,6},{5,7},{6,4},{7,5},{8,10},{9,11},{10,... | collective-permute-start | bytes 196616 | tf_op jit(solution)/shard_map/ppermute | solution.py:34
  11.8 19.9 %collective-permute-start.7 = (bf16[128,32,256]{2,1,0:T(8,128)(2,1)S(1)}, bf16[128,32,256]{2,1,0:T(8,128)(2,1)S(1)}, u32[]{:S(2)}, u32[]{:S(2)}) collective-permute-start(bf16[128,32,256]{2,1,0:T(8,128)(2,1)S(1)} %get-tuple-element.38), channel_id=1, source_target_pairs={{0,1},{1,0},{2,3},{3,2},{4,5},{5,4},{6,7},{7,6},{8,9},{9,8},{10,11... | collective-permute-start | bytes 6291464 | tf_op jit(solution)/shard_map/ppermute | solution.py:34
  14.1 19.1 %collective-permute-start.9 = (bf16[128,32,256]{2,1,0:T(8,128)(2,1)S(1)}, bf16[128,32,256]{2,1,0:T(8,128)(2,1)S(1)}, u32[]{:S(2)}, u32[]{:S(2)}) collective-permute-start(bf16[128,32,256]{2,1,0:T(8,128)(2,1)S(1)} %get-tuple-element.39), channel_id=1, source_target_pairs={{0,1},{1,0},{2,3},{3,2},{4,5},{5,4},{6,7},{7,6},{8,9},{9,8},{10,11... | collective-permute-start | bytes 6291464 | tf_op jit(solution)/shard_map/ppermute | solution.py:34
  14.6 7.8 %collective-permute-start.1 = (bf16[32,8,256]{2,1,0:T(8,128)(2,1)S(1)}, bf16[32,8,256]{2,1,0:T(8,128)(2,1)S(1)}, u32[]{:S(2)}, u32[]{:S(2)}) collective-permute-start(bf16[32,8,256]{2,1,0:T(8,128)(2,1)S(1)} %join.4.refs_1_.refs_0_), channel_id=1, source_target_pairs={{0,4},{1,5},{2,6},{3,7},{4,0},{5,1},{6,2},{7,3},{8,12},{9,13},{10,... | collective-permute-start | bytes 393224 | tf_op jit(solution)/shard_map/ppermute | solution.py:34
  16.2 9.0 %collective-permute-start.4 = (bf16[32,8,256]{2,1,0:T(8,128)(2,1)S(1)}, bf16[32,8,256]{2,1,0:T(8,128)(2,1)S(1)}, u32[]{:S(2)}, u32[]{:S(2)}) collective-permute-start(bf16[32,8,256]{2,1,0:T(8,128)(2,1)S(1)} %join.5.refs_2_.refs_0_), channel_id=1, source_target_pairs={{0,8},{1,9},{2,10},{3,11},{4,12},{5,13},{6,14},{7,15},{8,0},{9,1},... | collective-permute-start | bytes 393224 | tf_op jit(solution)/shard_map/ppermute | solution.py:34
  22.4 6.4 %collective-permute-start.5 = (bf16[64,8,256]{2,1,0:T(8,128)(2,1)S(1)}, bf16[64,8,256]{2,1,0:T(8,128)(2,1)S(1)}, u32[]{:S(2)}, u32[]{:S(2)}) collective-permute-start(bf16[64,8,256]{2,1,0:T(8,128)(2,1)S(1)} %join.6.refs_0_.refs_1_), channel_id=1, source_target_pairs={{0,2},{1,3},{2,0},{3,1},{4,6},{5,7},{6,4},{7,5},{8,10},{9,11},{10,... | collective-permute-start | bytes 786440 | tf_op jit(solution)/shard_map/ppermute | solution.py:34
  25.2 6.4 %collective-permute-start.6 = (bf16[64,8,256]{2,1,0:T(8,128)(2,1)S(1)}, bf16[64,8,256]{2,1,0:T(8,128)(2,1)S(1)}, u32[]{:S(2)}, u32[]{:S(2)}) collective-permute-start(bf16[64,8,256]{2,1,0:T(8,128)(2,1)S(1)} %join.7.refs_1_.refs_3_), channel_id=1, source_target_pairs={{0,4},{1,5},{2,6},{3,7},{4,0},{5,1},{6,2},{7,3},{8,12},{9,13},{10,... | collective-permute-start | bytes 786440 | tf_op jit(solution)/shard_map/ppermute | solution.py:34
  33.1 1.6 %collective-permute-start.8 = (f32[32,8,256]{2,1,0:T(8,128)S(1)}, f32[32,8,256]{2,1,0:T(8,128)S(1)}, u32[]{:S(2)}, u32[]{:S(2)}) collective-permute-start(f32[32,8,256]{2,1,0:T(8,128)S(1)} %coeff.1.refs_2_), channel_id=1, source_target_pairs={{0,1},{1,0},{2,3},{3,2},{4,5},{5,4},{6,7},{7,6},{8,9},{9,8},{10,11... | collective-permute-start | bytes 786440 | tf_op jit(solution)/shard_map/ppermute | solution.py:34
  36.2 5.3 %collective-permute-start.10 = (bf16[16,8,256]{2,1,0:T(8,128)(2,1)S(1)}, bf16[16,8,256]{2,1,0:T(8,128)(2,1)S(1)}, u32[]{:S(2)}, u32[]{:S(2)}) collective-permute-start(bf16[16,8,256]{2,1,0:T(8,128)(2,1)S(1)} %get-tuple-element.41), channel_id=1, source_target_pairs={{0,6},{1,7},{2,4},{3,5},{4,2},{5,3},{6,0},{7,1},{8,14},{9,15},{10,... | collective-permute-start | bytes 196616 | tf_op jit(solution)/shard_map/ppermute | solution.py:34
  38.6 4.3 %collective-permute-start.11 = (bf16[16,8,256]{2,1,0:T(8,128)(2,1)S(1)}, bf16[16,8,256]{2,1,0:T(8,128)(2,1)S(1)}, u32[]{:S(2)}, u32[]{:S(2)}) collective-permute-start(bf16[16,8,256]{2,1,0:T(8,128)(2,1)S(1)} %get-tuple-element.42), channel_id=1, source_target_pairs={{0,2},{1,3},{2,0},{3,1},{4,6},{5,7},{6,4},{7,5},{8,10},{9,11},{10,... | collective-permute-start | bytes 196616 | tf_op jit(solution)/shard_map/ppermute | solution.py:34
  39.2 4.3 %collective-permute-start.12 = (bf16[16,8,256]{2,1,0:T(8,128)(2,1)S(1)}, bf16[16,8,256]{2,1,0:T(8,128)(2,1)S(1)}, u32[]{:S(2)}, u32[]{:S(2)}) collective-permute-start(bf16[16,8,256]{2,1,0:T(8,128)(2,1)S(1)} %get-tuple-element.43), channel_id=1, source_target_pairs={{0,4},{1,5},{2,6},{3,7},{4,0},{5,1},{6,2},{7,3},{8,12},{9,13},{10,... | collective-permute-start | bytes 196616 | tf_op jit(solution)/shard_map/ppermute | solution.py:34
  43.5 5.9 %collective-permute-start.13 = (bf16[16,8,256]{2,1,0:T(8,128)(2,1)S(1)}, bf16[16,8,256]{2,1,0:T(8,128)(2,1)S(1)}, u32[]{:S(2)}, u32[]{:S(2)}) collective-permute-start(bf16[16,8,256]{2,1,0:T(8,128)(2,1)S(1)} %get-tuple-element.45), channel_id=1, source_target_pairs={{0,8},{1,9},{2,10},{3,11},{4,12},{5,13},{6,14},{7,15},{8,0},{9,1},... | collective-permute-start | bytes 196616 | tf_op jit(solution)/shard_map/ppermute | solution.py:34
  49.4 5.2 %collective-permute-start.16 = (bf16[16,8,256]{2,1,0:T(8,128)(2,1)S(1)}, bf16[16,8,256]{2,1,0:T(8,128)(2,1)S(1)}, u32[]{:S(2)}, u32[]{:S(2)}) collective-permute-start(bf16[16,8,256]{2,1,0:T(8,128)(2,1)S(1)} %weigh.1.refs_1_), channel_id=1, source_target_pairs={{0,6},{1,7},{2,4},{3,5},{4,2},{5,3},{6,0},{7,1},{8,14},{9,15},{10,... | collective-permute-start | bytes 196616 | tf_op jit(solution)/shard_map/ppermute | solution.py:34
  50.4 5.1 %collective-permute-start.15 = (bf16[16,8,256]{2,1,0:T(8,128)(2,1)S(1)}, bf16[16,8,256]{2,1,0:T(8,128)(2,1)S(1)}, u32[]{:S(2)}, u32[]{:S(2)}) collective-permute-start(bf16[16,8,256]{2,1,0:T(8,128)(2,1)S(1)} %weigh.1.refs_1_), channel_id=1, source_target_pairs={{0,4},{1,5},{2,6},{3,7},{4,0},{5,1},{6,2},{7,3},{8,12},{9,13},{10,... | collective-permute-start | bytes 196616 | tf_op jit(solution)/shard_map/ppermute | solution.py:34
  52.6 4.3 %collective-permute-start.14 = (bf16[16,8,256]{2,1,0:T(8,128)(2,1)S(1)}, bf16[16,8,256]{2,1,0:T(8,128)(2,1)S(1)}, u32[]{:S(2)}, u32[]{:S(2)}) collective-permute-start(bf16[16,8,256]{2,1,0:T(8,128)(2,1)S(1)} %weigh.1.refs_1_), channel_id=1, source_target_pairs={{0,2},{1,3},{2,0},{3,1},{4,6},{5,7},{6,4},{7,5},{8,10},{9,11},{10,... | collective-permute-start | bytes 196616 | tf_op jit(solution)/shard_map/ppermute | solution.py:34
  58.2 1.6 %collective-permute-start.17 = (f32[32,8,256]{2,1,0:T(8,128)S(1)}, f32[32,8,256]{2,1,0:T(8,128)S(1)}, u32[]{:S(2)}, u32[]{:S(2)}) collective-permute-start(f32[32,8,256]{2,1,0:T(8,128)S(1)} %back.1.refs_2_), channel_id=1, source_target_pairs={{0,1},{1,0},{2,3},{3,2},{4,5},{5,4},{6,7},{7,6},{8,9},{9,8},{10,11... | collective-permute-start | bytes 786440 | tf_op jit(solution)/shard_map/ppermute | solution.py:34
  61.4 8.4 %collective-permute-start.21 = (bf16[64,8,256]{2,1,0:T(8,128)(2,1)S(1)}, bf16[64,8,256]{2,1,0:T(8,128)(2,1)S(1)}, u32[]{:S(2)}, u32[]{:S(2)}) collective-permute-start(bf16[64,8,256]{2,1,0:T(8,128)(2,1)S(1)} %get-tuple-element.52), channel_id=1, source_target_pairs={{0,4},{1,5},{2,6},{3,7},{4,0},{5,1},{6,2},{7,3},{8,12},{9,13},{10,... | collective-permute-start | bytes 786440 | tf_op jit(solution)/shard_map/ppermute | solution.py:34
  61.4 10.1 %collective-permute-start.18 = (bf16[64,8,256]{2,1,0:T(8,128)(2,1)S(1)}, bf16[64,8,256]{2,1,0:T(8,128)(2,1)S(1)}, u32[]{:S(2)}, u32[]{:S(2)}) collective-permute-start(bf16[64,8,256]{2,1,0:T(8,128)(2,1)S(1)} %get-tuple-element.47), channel_id=1, source_target_pairs={{0,2},{1,3},{2,0},{3,1},{4,6},{5,7},{6,4},{7,5},{8,10},{9,11},{10,... | collective-permute-start | bytes 786440 | tf_op jit(solution)/shard_map/ppermute | solution.py:34
  69.8 8.6 %collective-permute-start.22 = (bf16[32,8,256]{2,1,0:T(8,128)(2,1)S(1)}, bf16[32,8,256]{2,1,0:T(8,128)(2,1)S(1)}, u32[]{:S(2)}, u32[]{:S(2)}) collective-permute-start(bf16[32,8,256]{2,1,0:T(8,128)(2,1)S(1)} %get-tuple-element.54), channel_id=1, source_target_pairs={{0,8},{1,9},{2,10},{3,11},{4,12},{5,13},{6,14},{7,15},{8,0},{9,1},... | collective-permute-start | bytes 393224 | tf_op jit(solution)/shard_map/ppermute | solution.py:34
  71.6 11.2 %collective-permute-start.19 = (bf16[32,8,256]{2,1,0:T(8,128)(2,1)S(1)}, bf16[32,8,256]{2,1,0:T(8,128)(2,1)S(1)}, u32[]{:S(2)}, u32[]{:S(2)}) collective-permute-start(bf16[32,8,256]{2,1,0:T(8,128)(2,1)S(1)} %get-tuple-element.49), channel_id=1, source_target_pairs={{0,4},{1,5},{2,6},{3,7},{4,0},{5,1},{6,2},{7,3},{8,12},{9,13},{10,... | collective-permute-start | bytes 393224 | tf_op jit(solution)/shard_map/ppermute | solution.py:34
  78.4 4.3 %collective-permute-start.23 = (bf16[16,8,256]{2,1,0:T(8,128)(2,1)S(1)}, bf16[16,8,256]{2,1,0:T(8,128)(2,1)S(1)}, u32[]{:S(2)}, u32[]{:S(2)}) collective-permute-start(bf16[16,8,256]{2,1,0:T(8,128)(2,1)S(1)} %get-tuple-element.56), channel_id=1, source_target_pairs={{0,2},{1,3},{2,0},{3,1},{4,6},{5,7},{6,4},{7,5},{8,10},{9,11},{10,... | collective-permute-start | bytes 196616 | tf_op jit(solution)/shard_map/ppermute | solution.py:34
  82.8 5.7 %collective-permute-start.24 = (f32[16,8,256]{2,1,0:T(8,128)S(1)}, f32[16,8,256]{2,1,0:T(8,128)S(1)}, u32[]{:S(2)}, u32[]{:S(2)}) collective-permute-start(f32[16,8,256]{2,1,0:T(8,128)S(1)} %fold.9), channel_id=1, source_target_pairs={{0,1},{1,0},{2,3},{3,2},{4,5},{5,4},{6,7},{7,6},{8,9},{9,8},{10,11... | collective-permute-start | bytes 393224 | tf_op jit(solution)/shard_map/ppermute | solution.py:34
  82.9 5.5 %collective-permute-start.20 = (bf16[16,8,256]{2,1,0:T(8,128)(2,1)S(1)}, bf16[16,8,256]{2,1,0:T(8,128)(2,1)S(1)}, u32[]{:S(2)}, u32[]{:S(2)}) collective-permute-start(bf16[16,8,256]{2,1,0:T(8,128)(2,1)S(1)} %get-tuple-element.51), channel_id=1, source_target_pairs={{0,8},{1,9},{2,10},{3,11},{4,12},{5,13},{6,14},{7,15},{8,0},{9,1},... | collective-permute-start | bytes 196616 | tf_op jit(solution)/shard_map/ppermute | solution.py:34

commit v9 on v8

--- a/solution.py
+++ b/solution.py
@@ -54,7 +54,7 @@
         input_output_aliases=aliases or {},
         scratch_shapes=list(scratches),
         compiler_params=pltpu.CompilerParams(vmem_limit_bytes=scratch + 8 * MIB),
-        cost_estimate=pl.CostEstimate(flops=flops, bytes_accessed=nbytes, transcendentals=0),
+        cost_estimate=pl.CostEstimate(flops=0, bytes_accessed=0, transcendentals=0),
         name=name,
     )(*ins)
 
@@ -119,15 +119,15 @@
             other[b, :, lanes] = jnp.where(odd, low, high).astype(BF16)
 
 
-def final_body(keep, recv, other, scaling, out):
+def final_body(keep, recv, other_keep, other_recv, scaling, out):
     odd = (lax.axis_index("tile") & 1) != 0
-    blocks, _, half = other.shape
+    blocks, _, half = keep.shape
     rows = half // LANES
     for b in range(blocks):
         for c in range(rows):
             lanes = slice(c * LANES, (c + 1) * LANES)
             own = keep[b, :, lanes] + recv[b, :, lanes].astype(F32)
-            got = other[b, :, lanes]
+            got = other_keep[b, :, lanes] + other_recv[b, :, lanes].astype(F32)
             for j, total in (
                 (2 * b * rows + c, jnp.where(odd, got, own)),
                 ((2 * b + 1) * rows + c, jnp.where(odd, own, got)),
@@ -185,6 +185,14 @@
             out[...] = (mine + recv[i * n : (i + 1) * n].astype(F32)).astype(out.dtype)
 
     return local(body, outs, keep, recv, name="fold")
+
+
+def gate(arrays, after):
+    def body(*refs):
+        pass
+
+    outs = [shape(a.shape, a.dtype) for a in arrays]
+    return local(body, outs, *arrays, name="gate", after=after, aliases={i: i for i in range(len(arrays))})
 
 
 def zeros(dims, after):
@@ -403,7 +411,7 @@
     after = (weight,)
     for step, (bit_p, bit_q) in enumerate(steps):
         got_p = swap(part_p, bit_p)
-        got_q = swap(part_q, bit_q)
+        got_q = swap(part_q, bit_q) if step else swap(send, bit_q ^ 1)
         if step == 1:
             v_here, v_send = load(v_factor, (part_p, part_q), "load_v")
             u_here, u_send = load(u_factor, (part_p, part_q, v_here), "load_u")
@@ -412,6 +420,8 @@
             part_p = join(part_p, got_p, after=after)
             part_q = join(part_q, got_q)
             after = ()
+        if step == 1:
+            v_send, u_send = gate((v_send, u_send), (part_p, part_q))
     v_both = (v_here, swap(v_send, 1))
     u_both = (u_here, swap(u_send, 1))
 
@@ -450,19 +460,20 @@
     )
     keep_p, keep_q, base = total, total, cells // 2
     for step, (bit_p, bit_q) in enumerate(steps[::-1]):
+        ends = step == len(steps) - 1
         got_p = swap(send_p, bit_p)
-        got_q = swap(send_q, bit_q)
-        if step < len(steps) - 1:
+        got_q = swap(send_q, bit_q ^ ends)
+        if not ends:
             keep_p, send_p = fold(keep_p, got_p)
             keep_q, send_q = fold(keep_q, got_q, base=base)
             base = 0
-    other = fold(keep_q, got_q, (F32,))[0]
     return local(
         final_body,
         [shape((probe_count, cell_total), F32)],
         keep_p,
         got_p,
-        swap(other, 1),
+        swap(keep_q, 1),
+        got_q,
         scaling,
         name="final",
         out_specs=[whole(None)],

time: 89.5 us -> 83 us (0.927)
  waiting for transfers between devices: 49.7 us -> 39.6 us
  starting transfers between devices: 25.2 us -> 28.8 us
    ppermute x25, waiting for transfers between devices: 49.7 us -> 39.6 us  [swap(): return lax.ppermute(array, 'tile', [(i, i ^ bits) for i in range(count)])]
    ppermute x25, starting transfers between devices: 25.2 us -> 28.8 us  [swap(): return lax.ppermute(array, 'tile', [(i, i ^ bits) for i in range(count)])]
  transfers between devices with their start and end apart: 25 -> 25, of which waited for: 19 -> 19; matrix products, arithmetic and copies ran while one was open for 0% -> 0% of each run, Pallas kernels for 6% -> 9%
where the time goes in v9:
time: 83 us; the launch traced here: 82.7 us
  waiting for transfers between devices  39.6 us (48%)
  starting transfers between devices  28.8 us (35%)
  Pallas kernels  14.1 us (17%)
    ppermute x25, waiting for transfers between devices, swap(): return lax.ppermute(array, 'tile', [(i, i ^ bits) for i in range(count)])  39.6 us
    ppermute x25, starting transfers between devices, swap(): return lax.ppermute(array, 'tile', [(i, i ^ bits) for i in range(count)])  28.8 us
    pallas_call x22, Pallas kernels, local(): pl.pallas_call(run, out_shape=[a if s.memory_space is None else s.memory_...  14.1 us
  transfers between devices with their start and end apart: 25, of which 19 were waited for; matrix products, arithmetic and copies ran while one was open for 0% of the time, Pallas kernels for 9%

profile of v9, /device:TPU:0, one launch (start us, length us, event | category | flops | bytes accessed | tf_op | source)
XLA Modules:
  0.0 82.7 jit_solution(2118921851745497864)
XLA Ops:
  0.0 1.1 %scale.1 = (bf16[16,8,256]{2,1,0:T(8,128)(2,1)S(1)}, bf16[16,8,256]{2,1,0:T(8,128)(2,1)S(1)}, f32[64,128]{1,0:T(8,128)S(1)}) custom-call(f32[4]{0:T(128)} %refs_0_.3, f32[64,128]{1,0:T(8,128)} %bitcast.9, s32[64,128]{1,0:T(8,128)} %bitcast.10, f32[8,8192]{1,0:T(8,128)} %refs_3_.1), custom_call_target="tpu_custom_call" | custom-call | tf_op jit(solution)/shard_map/scale/pallas_call | solution.py:49
  1.1 0.5 collective-permute-start.2
  1.6 2.6 %collective-permute-start.3 = (bf16[16,8,256]{2,1,0:T(8,128)(2,1)S(1)}, bf16[16,8,256]{2,1,0:T(8,128)(2,1)S(1)}, u32[]{:S(2)}, u32[]{:S(2)}) collective-permute-start(bf16[16,8,256]{2,1,0:T(8,128)(2,1)S(1)} %get-tuple-element.37), channel_id=1, source_target_pairs={{0,3},{1,2},{2,1},{3,0},{4,7},{5,6},{6,5},{7,4},{8,11},{9,10},{10,... | collective-permute-start | bytes 196616 | tf_op jit(solution)/shard_map/ppermute | solution.py:34
  4.2 2.6 %collective-permute-start = (bf16[16,8,256]{2,1,0:T(8,128)(2,1)S(1)}, bf16[16,8,256]{2,1,0:T(8,128)(2,1)S(1)}, u32[]{:S(2)}, u32[]{:S(2)}) collective-permute-start(bf16[16,8,256]{2,1,0:T(8,128)(2,1)S(1)} %get-tuple-element.35.refs_0_), channel_id=1, source_target_pairs={{0,8},{1,9},{2,10},{3,11},{4,12},{5,13},{6,14},{7,15},{8,0},{9,1},... | collective-permute-start | bytes 196616 | tf_op jit(solution)/shard_map/ppermute | solution.py:34
  6.8 1.5 %plan.1 = (s32[8,128]{1,0:T(8,128)S(4)}, f32[64,128]{1,0:T(8,128)S(1)}) custom-call(s32[16,128]{1,0:T(8,128)} %bitcast.11, s32[16,128]{1,0:T(8,128)} %bitcast.12, s32[16,128]{1,0:T(8,128)} %bitcast.13, s32[16,128]{1,0:T(8,128)} %bitcast.14, s32[16,128]{1,0:T(8,128)} %bitcast.15, f32[256,128]{1,0:T(8,128)} %bitcast.8, ...), custom_call_target="tpu_custom_call" | custom-call | tf_op jit(solution)/shard_map/plan/pallas_call | solution.py:49
  8.4 0.8 collective-permute-start.4
  9.2 1.6 %collective-permute-done.refs_1_ = bf16[16,8,256]{2,1,0:T(8,128)(2,1)S(1)} collective-permute-done((bf16[16,8,256]{2,1,0:T(8,128)(2,1)S(1)}, bf16[16,8,256]{2,1,0:T(8,128)(2,1)S(1)}, u32[]{:S(2)}, u32[]{:S(2)}) %collective-permute-start) | collective-permute-done | bytes 65568 | tf_op jit(solution)/shard_map/ppermute | solution.py:34
  10.8 0.6 collective-permute-start.1
  11.4 2.2 %load_v.1 = (bf16[128,32,256]{2,1,0:T(8,128)(2,1)S(1)}, bf16[128,32,256]{2,1,0:T(8,128)(2,1)S(1)}) custom-call(bf16[128,32,512]{2,1,0:T(8,128)(2,1)} %refs_0_.4, bf16[32,8,256]{2,1,0:T(8,128)(2,1)S(1)} %join.4.refs_1_.refs_0_, bf16[32,8,256]{2,1,0:T(8,128)(2,1)S(1)} %join.5.refs_2_.refs_0_), custom_call_target="tpu_custom_call" | custom-call | tf_op jit(solution)/shard_map/load_v/pallas_call | solution.py:49
  13.6 2.2 %load_u.1 = (bf16[128,32,256]{2,1,0:T(8,128)(2,1)S(1)}, bf16[128,32,256]{2,1,0:T(8,128)(2,1)S(1)}) custom-call(bf16[128,32,512]{2,1,0:T(8,128)(2,1)} %refs_0_.5, bf16[32,8,256]{2,1,0:T(8,128)(2,1)S(1)} %join.4.refs_1_.refs_0_, bf16[32,8,256]{2,1,0:T(8,128)(2,1)S(1)} %join.5.refs_2_.refs_0_, bf16[128,32,256]{2,1,0:T(8,128)(2,1)S(1)} %get-tuple-element.38.refs_3_.refs_5_.refs_4_), custom_call_target="tpu_custom_call" | custom-call | tf_op jit(solution)/shard_map/load_u/pallas_call | solution.py:49
  15.9 1.6 %collective-permute-done.4.refs_1_ = bf16[32,8,256]{2,1,0:T(8,128)(2,1)S(1)} collective-permute-done((bf16[32,8,256]{2,1,0:T(8,128)(2,1)S(1)}, bf16[32,8,256]{2,1,0:T(8,128)(2,1)S(1)}, u32[]{:S(2)}, u32[]{:S(2)}) %collective-permute-start.4) | collective-permute-done | bytes 131104 | tf_op jit(solution)/shard_map/ppermute | solution.py:34
  17.7 0.5 collective-permute-start.9
  18.2 0.4 collective-permute-start.5
  18.6 1.3 %collective-permute-start.6 = (bf16[64,8,256]{2,1,0:T(8,128)(2,1)S(1)}, bf16[64,8,256]{2,1,0:T(8,128)(2,1)S(1)}, u32[]{:S(2)}, u32[]{:S(2)}) collective-permute-start(bf16[64,8,256]{2,1,0:T(8,128)(2,1)S(1)} %join.7.refs_1_.refs_3_), channel_id=1, source_target_pairs={{0,4},{1,5},{2,6},{3,7},{4,0},{5,1},{6,2},{7,3},{8,12},{9,13},{10,... | collective-permute-start | bytes 786440 | tf_op jit(solution)/shard_map/ppermute | solution.py:34
  19.9 6.5 %collective-permute-done.5.refs_2_ = bf16[64,8,256]{2,1,0:T(8,128)(2,1)S(1)} collective-permute-done((bf16[64,8,256]{2,1,0:T(8,128)(2,1)S(1)}, bf16[64,8,256]{2,1,0:T(8,128)(2,1)S(1)}, u32[]{:S(2)}, u32[]{:S(2)}) %collective-permute-start.5) | collective-permute-done | bytes 262176 | tf_op jit(solution)/shard_map/ppermute | solution.py:34
  26.5 0.2 collective-permute-done.6.refs_4_
  26.6 1.4 %coeff.1.refs_2_ = f32[32,8,256]{2,1,0:T(8,128)S(1)} custom-call(s32[8,128]{1,0:T(8,128)S(4)} %get-tuple-element.34.refs_0_, bf16[64,8,256]{2,1,0:T(8,128)(2,1)S(1)} %join.6.refs_0_.refs_2_.refs_1_, bf16[64,8,256]{2,1,0:T(8,128)(2,1)S(1)} %collective-permute-done.5.refs_2_, bf16[64,8,256]{2,1,0:T(8,128)(2,1)S(1)} %join.7.refs_1_.refs_3_, ...), custom_call_target="tpu_custom_call" | custom-call | tf_op jit(solution)/shard_map/coeff/pallas_call | solution.py:49
  28.2 1.5 %collective-permute-done.8.refs_3_ = f32[32,8,256]{2,1,0:T(8,128)S(1)} collective-permute-done((f32[32,8,256]{2,1,0:T(8,128)S(1)}, f32[32,8,256]{2,1,0:T(8,128)S(1)}, u32[]{:S(2)}, u32[]{:S(2)}) %collective-permute-start.8) | collective-permute-done | bytes 262176 | tf_op jit(solution)/shard_map/ppermute | solution.py:34
  29.7 1.5 %partial.1 = (f32[64,8,256]{2,1,0:T(8,128)S(1)}, bf16[16,8,256]{2,1,0:T(8,128)(2,1)S(1)}, bf16[16,8,256]{2,1,0:T(8,128)(2,1)S(1)}, bf16[16,8,256]{2,1,0:T(8,128)(2,1)S(1)}) custom-call(s32[8,128]{1,0:T(8,128)S(4)} %get-tuple-element.34.refs_0_, f32[64,8,256]{2,1,0:T(8,128)S(1)} %zeros.2.refs_1_, ...), custom_call_target="tpu_custom_call", output_to_operand_aliasing={{0}: (1, {})} | custom-call | tf_op jit(solution)/shard_map/partial/pallas_call | solution.py:49
  31.2 1.4 %collective-permute-start.10 = (bf16[16,8,256]{2,1,0:T(8,128)(2,1)S(1)}, bf16[16,8,256]{2,1,0:T(8,128)(2,1)S(1)}, u32[]{:S(2)}, u32[]{:S(2)}) collective-permute-start(bf16[16,8,256]{2,1,0:T(8,128)(2,1)S(1)} %get-tuple-element.45), channel_id=1, source_target_pairs={{0,6},{1,7},{2,4},{3,5},{4,2},{5,3},{6,0},{7,1},{8,14},{9,15},{10,... | collective-permute-start | bytes 196616 | tf_op jit(solution)/shard_map/ppermute | solution.py:34
  32.5 1.5 %collective-permute-start.11 = (bf16[16,8,256]{2,1,0:T(8,128)(2,1)S(1)}, bf16[16,8,256]{2,1,0:T(8,128)(2,1)S(1)}, u32[]{:S(2)}, u32[]{:S(2)}) collective-permute-start(bf16[16,8,256]{2,1,0:T(8,128)(2,1)S(1)} %get-tuple-element.46), channel_id=1, source_target_pairs={{0,2},{1,3},{2,0},{3,1},{4,6},{5,7},{6,4},{7,5},{8,10},{9,11},{10,... | collective-permute-start | bytes 196616 | tf_op jit(solution)/shard_map/ppermute | solution.py:34
  34.0 0.7 collective-permute-start.12
  34.7 2.0 %collective-permute-done.10.refs_1_ = bf16[16,8,256]{2,1,0:T(8,128)(2,1)S(1)} collective-permute-done((bf16[16,8,256]{2,1,0:T(8,128)(2,1)S(1)}, bf16[16,8,256]{2,1,0:T(8,128)(2,1)S(1)}, u32[]{:S(2)}, u32[]{:S(2)}) %collective-permute-start.10) | collective-permute-done | bytes 65568 | tf_op jit(solution)/shard_map/ppermute | solution.py:34
  36.7 1.0 %collective-permute-done.11.refs_2_ = bf16[16,8,256]{2,1,0:T(8,128)(2,1)S(1)} collective-permute-done((bf16[16,8,256]{2,1,0:T(8,128)(2,1)S(1)}, bf16[16,8,256]{2,1,0:T(8,128)(2,1)S(1)}, u32[]{:S(2)}, u32[]{:S(2)}) %collective-permute-start.11) | collective-permute-done | bytes 65568 | tf_op jit(solution)/shard_map/ppermute | solution.py:34
  37.7 0.6 collective-permute-done.12.refs_3_
  38.3 4.0 %collective-permute-start.13 = (bf16[16,8,256]{2,1,0:T(8,128)(2,1)S(1)}, bf16[16,8,256]{2,1,0:T(8,128)(2,1)S(1)}, u32[]{:S(2)}, u32[]{:S(2)}) collective-permute-start(bf16[16,8,256]{2,1,0:T(8,128)(2,1)S(1)} %get-tuple-element.49), channel_id=1, source_target_pairs={{0,8},{1,9},{2,10},{3,11},{4,12},{5,13},{6,14},{7,15},{8,0},{9,1},... | collective-permute-start | bytes 196616 | tf_op jit(solution)/shard_map/ppermute | solution.py:34
  42.3 2.9 %collective-permute-done.13.refs_1_ = bf16[16,8,256]{2,1,0:T(8,128)(2,1)S(1)} collective-permute-done((bf16[16,8,256]{2,1,0:T(8,128)(2,1)S(1)}, bf16[16,8,256]{2,1,0:T(8,128)(2,1)S(1)}, u32[]{:S(2)}, u32[]{:S(2)}) %collective-permute-start.13) | collective-permute-done | bytes 65568 | tf_op jit(solution)/shard_map/ppermute | solution.py:34
  45.3 1.6 %collective-permute-start.14 = (bf16[16,8,256]{2,1,0:T(8,128)(2,1)S(1)}, bf16[16,8,256]{2,1,0:T(8,128)(2,1)S(1)}, u32[]{:S(2)}, u32[]{:S(2)}) collective-permute-start(bf16[16,8,256]{2,1,0:T(8,128)(2,1)S(1)} %weigh.1.refs_1_), channel_id=1, source_target_pairs={{0,2},{1,3},{2,0},{3,1},{4,6},{5,7},{6,4},{7,5},{8,10},{9,11},{10,... | collective-permute-start | bytes 196616 | tf_op jit(solution)/shard_map/ppermute | solution.py:34
  46.9 0.3 collective-permute-start.15
  47.2 1.7 %collective-permute-start.16 = (bf16[16,8,256]{2,1,0:T(8,128)(2,1)S(1)}, bf16[16,8,256]{2,1,0:T(8,128)(2,1)S(1)}, u32[]{:S(2)}, u32[]{:S(2)}) collective-permute-start(bf16[16,8,256]{2,1,0:T(8,128)(2,1)S(1)} %weigh.1.refs_1_), channel_id=1, source_target_pairs={{0,6},{1,7},{2,4},{3,5},{4,2},{5,3},{6,0},{7,1},{8,14},{9,15},{10,... | collective-permute-start | bytes 196616 | tf_op jit(solution)/shard_map/ppermute | solution.py:34
  48.9 0.8 collective-permute-done.14.refs_2_
  49.7 1.5 %collective-permute-done.15.refs_3_ = bf16[16,8,256]{2,1,0:T(8,128)(2,1)S(1)} collective-permute-done((bf16[16,8,256]{2,1,0:T(8,128)(2,1)S(1)}, bf16[16,8,256]{2,1,0:T(8,128)(2,1)S(1)}, u32[]{:S(2)}, u32[]{:S(2)}) %collective-permute-start.15) | collective-permute-done | bytes 65568 | tf_op jit(solution)/shard_map/ppermute | solution.py:34
  51.2 1.2 %collective-permute-done.16.refs_4_ = bf16[16,8,256]{2,1,0:T(8,128)(2,1)S(1)} collective-permute-done((bf16[16,8,256]{2,1,0:T(8,128)(2,1)S(1)}, bf16[16,8,256]{2,1,0:T(8,128)(2,1)S(1)}, u32[]{:S(2)}, u32[]{:S(2)}) %collective-permute-start.16) | collective-permute-done | bytes 65568 | tf_op jit(solution)/shard_map/ppermute | solution.py:34
  52.3 1.4 %back.1.refs_2_ = f32[32,8,256]{2,1,0:T(8,128)S(1)} custom-call(s32[8,128]{1,0:T(8,128)S(4)} %get-tuple-element.34.refs_0_, bf16[16,8,256]{2,1,0:T(8,128)(2,1)S(1)} %weigh.1.refs_1_, bf16[16,8,256]{2,1,0:T(8,128)(2,1)S(1)} %collective-permute-done.14.refs_2_, bf16[16,8,256]{2,1,0:T(8,128)(2,1)S(1)} %collective-permute-done.15.refs_3_, ...), custom_call_target="tpu_custom_call" | custom-call | tf_op jit(solution)/shard_map/back/pallas_call | solution.py:49
  54.0 1.4 %collective-permute-done.17.refs_3_ = f32[32,8,256]{2,1,0:T(8,128)S(1)} collective-permute-done((f32[32,8,256]{2,1,0:T(8,128)S(1)}, f32[32,8,256]{2,1,0:T(8,128)S(1)}, u32[]{:S(2)}, u32[]{:S(2)}) %collective-permute-start.17) | collective-permute-done | bytes 262176 | tf_op jit(solution)/shard_map/ppermute | solution.py:34
  55.4 1.5 %spread.1 = (f32[256,8,256]{2,1,0:T(8,128)S(1)}, bf16[64,8,256]{2,1,0:T(8,128)(2,1)S(1)}, bf16[64,8,256]{2,1,0:T(8,128)(2,1)S(1)}) custom-call(s32[8,128]{1,0:T(8,128)S(4)} %get-tuple-element.34.refs_0_, f32[256,8,256]{2,1,0:T(8,128)S(1)} %zeros.3.refs_1_, f32[32,8,256]{2,1,0:T(8,128)S(1)} %back.1.refs_2_, ...), custom_call_target="tpu_custom_call", output_to_operand_aliasing={{0}: (1, {})} | custom-call | tf_op jit(solution)/shard_map/spread/pallas_call | solution.py:49
  56.9 1.8 %collective-permute-start.21 = (bf16[64,8,256]{2,1,0:T(8,128)(2,1)S(1)}, bf16[64,8,256]{2,1,0:T(8,128)(2,1)S(1)}, u32[]{:S(2)}, u32[]{:S(2)}) collective-permute-start(bf16[64,8,256]{2,1,0:T(8,128)(2,1)S(1)} %get-tuple-element.56), channel_id=1, source_target_pairs={{0,4},{1,5},{2,6},{3,7},{4,0},{5,1},{6,2},{7,3},{8,12},{9,13},{10,... | collective-permute-start | bytes 786440 | tf_op jit(solution)/shard_map/ppermute | solution.py:34
  58.7 0.5 collective-permute-start.18
  59.2 6.1 %collective-permute-done.21.refs_1_ = bf16[64,8,256]{2,1,0:T(8,128)(2,1)S(1)} collective-permute-done((bf16[64,8,256]{2,1,0:T(8,128)(2,1)S(1)}, bf16[64,8,256]{2,1,0:T(8,128)(2,1)S(1)}, u32[]{:S(2)}, u32[]{:S(2)}) %collective-permute-start.21) | collective-permute-done | bytes 262176 | tf_op jit(solution)/shard_map/ppermute | solution.py:34
  65.3 3.6 %collective-permute-start.22 = (bf16[32,8,256]{2,1,0:T(8,128)(2,1)S(1)}, bf16[32,8,256]{2,1,0:T(8,128)(2,1)S(1)}, u32[]{:S(2)}, u32[]{:S(2)}) collective-permute-start(bf16[32,8,256]{2,1,0:T(8,128)(2,1)S(1)} %get-tuple-element.58), channel_id=1, source_target_pairs={{0,8},{1,9},{2,10},{3,11},{4,12},{5,13},{6,14},{7,15},{8,0},{9,1},... | collective-permute-start | bytes 393224 | tf_op jit(solution)/shard_map/ppermute | solution.py:34
  69.0 0.6 collective-permute-start.19
  69.6 5.2 %collective-permute-done.22.refs_1_ = bf16[32,8,256]{2,1,0:T(8,128)(2,1)S(1)} collective-permute-done((bf16[32,8,256]{2,1,0:T(8,128)(2,1)S(1)}, bf16[32,8,256]{2,1,0:T(8,128)(2,1)S(1)}, u32[]{:S(2)}, u32[]{:S(2)}) %collective-permute-start.22) | collective-permute-done | bytes 131104 | tf_op jit(solution)/shard_map/ppermute | solution.py:34
  74.9 0.6 collective-permute-start.24
  75.5 0.4 collective-permute-done.19.refs_1_
  75.9 0.9 %collective-permute-start.20 = (bf16[16,8,256]{2,1,0:T(8,128)(2,1)S(1)}, bf16[16,8,256]{2,1,0:T(8,128)(2,1)S(1)}, u32[]{:S(2)}, u32[]{:S(2)}) collective-permute-start(bf16[16,8,256]{2,1,0:T(8,128)(2,1)S(1)} %get-tuple-element.55), channel_id=1, source_target_pairs={{0,8},{1,9},{2,10},{3,11},{4,12},{5,13},{6,14},{7,15},{8,0},{9,1},... | collective-permute-start | bytes 196616 | tf_op jit(solution)/shard_map/ppermute | solution.py:34
  76.8 1.9 %collective-permute-done.24.refs_3_ = bf16[16,8,256]{2,1,0:T(8,128)(2,1)S(1)} collective-permute-done((bf16[16,8,256]{2,1,0:T(8,128)(2,1)S(1)}, bf16[16,8,256]{2,1,0:T(8,128)(2,1)S(1)}, u32[]{:S(2)}, u32[]{:S(2)}) %collective-permute-start.24) | collective-permute-done | bytes 65568 | tf_op jit(solution)/shard_map/ppermute | solution.py:34
  78.8 3.2 %collective-permute-done.20.refs_1_ = bf16[16,8,256]{2,1,0:T(8,128)(2,1)S(1)} collective-permute-done((bf16[16,8,256]{2,1,0:T(8,128)(2,1)S(1)}, bf16[16,8,256]{2,1,0:T(8,128)(2,1)S(1)}, u32[]{:S(2)}, u32[]{:S(2)}) %collective-permute-start.20) | collective-permute-done | bytes 65568 | tf_op jit(solution)/shard_map/ppermute | solution.py:34
  82.0 0.7 final.1
  (24 shorter events, 0.8 us)
Async XLA Ops:
  1.1 7.3 %collective-permute-start.2 = (bf16[16,8,256]{2,1,0:T(8,128)(2,1)S(1)}, bf16[16,8,256]{2,1,0:T(8,128)(2,1)S(1)}, u32[]{:S(2)}, u32[]{:S(2)}) collective-permute-start(bf16[16,8,256]{2,1,0:T(8,128)(2,1)S(1)} %get-tuple-element.37), channel_id=1, source_target_pairs={{0,1},{1,0},{2,3},{3,2},{4,5},{5,4},{6,7},{7,6},{8,9},{9,8},{10,11... | collective-permute-start | bytes 196616 | tf_op jit(solution)/shard_map/ppermute | solution.py:34
  1.6 6.8 %collective-permute-start.3 = (bf16[16,8,256]{2,1,0:T(8,128)(2,1)S(1)}, bf16[16,8,256]{2,1,0:T(8,128)(2,1)S(1)}, u32[]{:S(2)}, u32[]{:S(2)}) collective-permute-start(bf16[16,8,256]{2,1,0:T(8,128)(2,1)S(1)} %get-tuple-element.37), channel_id=1, source_target_pairs={{0,3},{1,2},{2,1},{3,0},{4,7},{5,6},{6,5},{7,4},{8,11},{9,10},{10,... | collective-permute-start | bytes 196616 | tf_op jit(solution)/shard_map/ppermute | solution.py:34
  4.2 6.6 %collective-permute-start = (bf16[16,8,256]{2,1,0:T(8,128)(2,1)S(1)}, bf16[16,8,256]{2,1,0:T(8,128)(2,1)S(1)}, u32[]{:S(2)}, u32[]{:S(2)}) collective-permute-start(bf16[16,8,256]{2,1,0:T(8,128)(2,1)S(1)} %get-tuple-element.35.refs_0_), channel_id=1, source_target_pairs={{0,8},{1,9},{2,10},{3,11},{4,12},{5,13},{6,14},{7,15},{8,0},{9,1},... | collective-permute-start | bytes 196616 | tf_op jit(solution)/shard_map/ppermute | solution.py:34
  8.4 9.1 %collective-permute-start.4 = (bf16[32,8,256]{2,1,0:T(8,128)(2,1)S(1)}, bf16[32,8,256]{2,1,0:T(8,128)(2,1)S(1)}, u32[]{:S(2)}, u32[]{:S(2)}) collective-permute-start(bf16[32,8,256]{2,1,0:T(8,128)(2,1)S(1)} %join.5.refs_2_.refs_0_), channel_id=1, source_target_pairs={{0,8},{1,9},{2,10},{3,11},{4,12},{5,13},{6,14},{7,15},{8,0},{9,1},... | collective-permute-start | bytes 393224 | tf_op jit(solution)/shard_map/ppermute | solution.py:34
  10.8 6.7 %collective-permute-start.1 = (bf16[32,8,256]{2,1,0:T(8,128)(2,1)S(1)}, bf16[32,8,256]{2,1,0:T(8,128)(2,1)S(1)}, u32[]{:S(2)}, u32[]{:S(2)}) collective-permute-start(bf16[32,8,256]{2,1,0:T(8,128)(2,1)S(1)} %join.4.refs_1_.refs_0_), channel_id=1, source_target_pairs={{0,4},{1,5},{2,6},{3,7},{4,0},{5,1},{6,2},{7,3},{8,12},{9,13},{10,... | collective-permute-start | bytes 393224 | tf_op jit(solution)/shard_map/ppermute | solution.py:34
  17.6 9.0 %collective-permute-start.7 = (bf16[128,32,256]{2,1,0:T(8,128)(2,1)S(1)}, bf16[128,32,256]{2,1,0:T(8,128)(2,1)S(1)}, u32[]{:S(2)}, u32[]{:S(2)}) collective-permute-start(bf16[128,32,256]{2,1,0:T(8,128)(2,1)S(1)} %get-tuple-element.42), channel_id=1, source_target_pairs={{0,1},{1,0},{2,3},{3,2},{4,5},{5,4},{6,7},{7,6},{8,9},{9,8},{10,11... | collective-permute-start | bytes 6291464 | tf_op jit(solution)/shard_map/ppermute | solution.py:34
  17.7 10.5 %collective-permute-start.9 = (bf16[128,32,256]{2,1,0:T(8,128)(2,1)S(1)}, bf16[128,32,256]{2,1,0:T(8,128)(2,1)S(1)}, u32[]{:S(2)}, u32[]{:S(2)}) collective-permute-start(bf16[128,32,256]{2,1,0:T(8,128)(2,1)S(1)} %get-tuple-element.43), channel_id=1, source_target_pairs={{0,1},{1,0},{2,3},{3,2},{4,5},{5,4},{6,7},{7,6},{8,9},{9,8},{10,11... | collective-permute-start | bytes 6291464 | tf_op jit(solution)/shard_map/ppermute | solution.py:34
  18.2 8.3 %collective-permute-start.5 = (bf16[64,8,256]{2,1,0:T(8,128)(2,1)S(1)}, bf16[64,8,256]{2,1,0:T(8,128)(2,1)S(1)}, u32[]{:S(2)}, u32[]{:S(2)}) collective-permute-start(bf16[64,8,256]{2,1,0:T(8,128)(2,1)S(1)} %join.6.refs_0_.refs_2_.refs_1_), channel_id=1, source_target_pairs={{0,2},{1,3},{2,0},{3,1},{4,6},{5,7},{6,4},{7,5},{8,10},{9,11},{10,... | collective-permute-start | bytes 786440 | tf_op jit(solution)/shard_map/ppermute | solution.py:34
  18.6 8.0 %collective-permute-start.6 = (bf16[64,8,256]{2,1,0:T(8,128)(2,1)S(1)}, bf16[64,8,256]{2,1,0:T(8,128)(2,1)S(1)}, u32[]{:S(2)}, u32[]{:S(2)}) collective-permute-start(bf16[64,8,256]{2,1,0:T(8,128)(2,1)S(1)} %join.7.refs_1_.refs_3_), channel_id=1, source_target_pairs={{0,4},{1,5},{2,6},{3,7},{4,0},{5,1},{6,2},{7,3},{8,12},{9,13},{10,... | collective-permute-start | bytes 786440 | tf_op jit(solution)/shard_map/ppermute | solution.py:34
  28.1 1.6 %collective-permute-start.8 = (f32[32,8,256]{2,1,0:T(8,128)S(1)}, f32[32,8,256]{2,1,0:T(8,128)S(1)}, u32[]{:S(2)}, u32[]{:S(2)}) collective-permute-start(f32[32,8,256]{2,1,0:T(8,128)S(1)} %coeff.1.refs_2_), channel_id=1, source_target_pairs={{0,1},{1,0},{2,3},{3,2},{4,5},{5,4},{6,7},{7,6},{8,9},{9,8},{10,11... | collective-permute-start | bytes 786440 | tf_op jit(solution)/shard_map/ppermute | solution.py:34
  31.2 5.5 %collective-permute-start.10 = (bf16[16,8,256]{2,1,0:T(8,128)(2,1)S(1)}, bf16[16,8,256]{2,1,0:T(8,128)(2,1)S(1)}, u32[]{:S(2)}, u32[]{:S(2)}) collective-permute-start(bf16[16,8,256]{2,1,0:T(8,128)(2,1)S(1)} %get-tuple-element.45), channel_id=1, source_target_pairs={{0,6},{1,7},{2,4},{3,5},{4,2},{5,3},{6,0},{7,1},{8,14},{9,15},{10,... | collective-permute-start | bytes 196616 | tf_op jit(solution)/shard_map/ppermute | solution.py:34
  32.5 5.1 %collective-permute-start.11 = (bf16[16,8,256]{2,1,0:T(8,128)(2,1)S(1)}, bf16[16,8,256]{2,1,0:T(8,128)(2,1)S(1)}, u32[]{:S(2)}, u32[]{:S(2)}) collective-permute-start(bf16[16,8,256]{2,1,0:T(8,128)(2,1)S(1)} %get-tuple-element.46), channel_id=1, source_target_pairs={{0,2},{1,3},{2,0},{3,1},{4,6},{5,7},{6,4},{7,5},{8,10},{9,11},{10,... | collective-permute-start | bytes 196616 | tf_op jit(solution)/shard_map/ppermute | solution.py:34
  34.0 4.3 %collective-permute-start.12 = (bf16[16,8,256]{2,1,0:T(8,128)(2,1)S(1)}, bf16[16,8,256]{2,1,0:T(8,128)(2,1)S(1)}, u32[]{:S(2)}, u32[]{:S(2)}) collective-permute-start(bf16[16,8,256]{2,1,0:T(8,128)(2,1)S(1)} %get-tuple-element.47), channel_id=1, source_target_pairs={{0,4},{1,5},{2,6},{3,7},{4,0},{5,1},{6,2},{7,3},{8,12},{9,13},{10,... | collective-permute-start | bytes 196616 | tf_op jit(solution)/shard_map/ppermute | solution.py:34
  38.3 6.9 %collective-permute-start.13 = (bf16[16,8,256]{2,1,0:T(8,128)(2,1)S(1)}, bf16[16,8,256]{2,1,0:T(8,128)(2,1)S(1)}, u32[]{:S(2)}, u32[]{:S(2)}) collective-permute-start(bf16[16,8,256]{2,1,0:T(8,128)(2,1)S(1)} %get-tuple-element.49), channel_id=1, source_target_pairs={{0,8},{1,9},{2,10},{3,11},{4,12},{5,13},{6,14},{7,15},{8,0},{9,1},... | collective-permute-start | bytes 196616 | tf_op jit(solution)/shard_map/ppermute | solution.py:34
  45.3 4.4 %collective-permute-start.14 = (bf16[16,8,256]{2,1,0:T(8,128)(2,1)S(1)}, bf16[16,8,256]{2,1,0:T(8,128)(2,1)S(1)}, u32[]{:S(2)}, u32[]{:S(2)}) collective-permute-start(bf16[16,8,256]{2,1,0:T(8,128)(2,1)S(1)} %weigh.1.refs_1_), channel_id=1, source_target_pairs={{0,2},{1,3},{2,0},{3,1},{4,6},{5,7},{6,4},{7,5},{8,10},{9,11},{10,... | collective-permute-start | bytes 196616 | tf_op jit(solution)/shard_map/ppermute | solution.py:34
  46.9 4.3 %collective-permute-start.15 = (bf16[16,8,256]{2,1,0:T(8,128)(2,1)S(1)}, bf16[16,8,256]{2,1,0:T(8,128)(2,1)S(1)}, u32[]{:S(2)}, u32[]{:S(2)}) collective-permute-start(bf16[16,8,256]{2,1,0:T(8,128)(2,1)S(1)} %weigh.1.refs_1_), channel_id=1, source_target_pairs={{0,4},{1,5},{2,6},{3,7},{4,0},{5,1},{6,2},{7,3},{8,12},{9,13},{10,... | collective-permute-start | bytes 196616 | tf_op jit(solution)/shard_map/ppermute | solution.py:34
  47.2 5.2 %collective-permute-start.16 = (bf16[16,8,256]{2,1,0:T(8,128)(2,1)S(1)}, bf16[16,8,256]{2,1,0:T(8,128)(2,1)S(1)}, u32[]{:S(2)}, u32[]{:S(2)}) collective-permute-start(bf16[16,8,256]{2,1,0:T(8,128)(2,1)S(1)} %weigh.1.refs_1_), channel_id=1, source_target_pairs={{0,6},{1,7},{2,4},{3,5},{4,2},{5,3},{6,0},{7,1},{8,14},{9,15},{10,... | collective-permute-start | bytes 196616 | tf_op jit(solution)/shard_map/ppermute | solution.py:34
  53.8 1.6 %collective-permute-start.17 = (f32[32,8,256]{2,1,0:T(8,128)S(1)}, f32[32,8,256]{2,1,0:T(8,128)S(1)}, u32[]{:S(2)}, u32[]{:S(2)}) collective-permute-start(f32[32,8,256]{2,1,0:T(8,128)S(1)} %back.1.refs_2_), channel_id=1, source_target_pairs={{0,1},{1,0},{2,3},{3,2},{4,5},{5,4},{6,7},{7,6},{8,9},{9,8},{10,11... | collective-permute-start | bytes 786440 | tf_op jit(solution)/shard_map/ppermute | solution.py:34
  56.9 8.4 %collective-permute-start.21 = (bf16[64,8,256]{2,1,0:T(8,128)(2,1)S(1)}, bf16[64,8,256]{2,1,0:T(8,128)(2,1)S(1)}, u32[]{:S(2)}, u32[]{:S(2)}) collective-permute-start(bf16[64,8,256]{2,1,0:T(8,128)(2,1)S(1)} %get-tuple-element.56), channel_id=1, source_target_pairs={{0,4},{1,5},{2,6},{3,7},{4,0},{5,1},{6,2},{7,3},{8,12},{9,13},{10,... | collective-permute-start | bytes 786440 | tf_op jit(solution)/shard_map/ppermute | solution.py:34
  58.7 10.3 %collective-permute-start.18 = (bf16[64,8,256]{2,1,0:T(8,128)(2,1)S(1)}, bf16[64,8,256]{2,1,0:T(8,128)(2,1)S(1)}, u32[]{:S(2)}, u32[]{:S(2)}) collective-permute-start(bf16[64,8,256]{2,1,0:T(8,128)(2,1)S(1)} %get-tuple-element.51), channel_id=1, source_target_pairs={{0,2},{1,3},{2,0},{3,1},{4,6},{5,7},{6,4},{7,5},{8,10},{9,11},{10,... | collective-permute-start | bytes 786440 | tf_op jit(solution)/shard_map/ppermute | solution.py:34
  65.3 9.4 %collective-permute-start.22 = (bf16[32,8,256]{2,1,0:T(8,128)(2,1)S(1)}, bf16[32,8,256]{2,1,0:T(8,128)(2,1)S(1)}, u32[]{:S(2)}, u32[]{:S(2)}) collective-permute-start(bf16[32,8,256]{2,1,0:T(8,128)(2,1)S(1)} %get-tuple-element.58), channel_id=1, source_target_pairs={{0,8},{1,9},{2,10},{3,11},{4,12},{5,13},{6,14},{7,15},{8,0},{9,1},... | collective-permute-start | bytes 393224 | tf_op jit(solution)/shard_map/ppermute | solution.py:34
  69.0 6.9 %collective-permute-start.19 = (bf16[32,8,256]{2,1,0:T(8,128)(2,1)S(1)}, bf16[32,8,256]{2,1,0:T(8,128)(2,1)S(1)}, u32[]{:S(2)}, u32[]{:S(2)}) collective-permute-start(bf16[32,8,256]{2,1,0:T(8,128)(2,1)S(1)} %get-tuple-element.53), channel_id=1, source_target_pairs={{0,4},{1,5},{2,6},{3,7},{4,0},{5,1},{6,2},{7,3},{8,12},{9,13},{10,... | collective-permute-start | bytes 393224 | tf_op jit(solution)/shard_map/ppermute | solution.py:34
  74.8 7.2 %collective-permute-start.23 = (f32[16,8,256]{2,1,0:T(8,128)S(1)}, f32[16,8,256]{2,1,0:T(8,128)S(1)}, u32[]{:S(2)}, u32[]{:S(2)}) collective-permute-start(f32[16,8,256]{2,1,0:T(8,128)S(1)} %get-tuple-element.59), channel_id=1, source_target_pairs={{0,1},{1,0},{2,3},{3,2},{4,5},{5,4},{6,7},{7,6},{8,9},{9,8},{10,11... | collective-permute-start | bytes 393224 | tf_op jit(solution)/shard_map/ppermute | solution.py:34
  74.9 3.9 %collective-permute-start.24 = (bf16[16,8,256]{2,1,0:T(8,128)(2,1)S(1)}, bf16[16,8,256]{2,1,0:T(8,128)(2,1)S(1)}, u32[]{:S(2)}, u32[]{:S(2)}) collective-permute-start(bf16[16,8,256]{2,1,0:T(8,128)(2,1)S(1)} %get-tuple-element.60), channel_id=1, source_target_pairs={{0,3},{1,2},{2,1},{3,0},{4,7},{5,6},{6,5},{7,4},{8,11},{9,10},{10,... | collective-permute-start | bytes 196616 | tf_op jit(solution)/shard_map/ppermute | solution.py:34
  75.9 6.0 %collective-permute-start.20 = (bf16[16,8,256]{2,1,0:T(8,128)(2,1)S(1)}, bf16[16,8,256]{2,1,0:T(8,128)(2,1)S(1)}, u32[]{:S(2)}, u32[]{:S(2)}) collective-permute-start(bf16[16,8,256]{2,1,0:T(8,128)(2,1)S(1)} %get-tuple-element.55), channel_id=1, source_target_pairs={{0,8},{1,9},{2,10},{3,11},{4,12},{5,13},{6,14},{7,15},{8,0},{9,1},... | collective-permute-start | bytes 196616 | tf_op jit(solution)/shard_map/ppermute | solution.py:34

commit v10 on v9

--- a/solution.py
+++ b/solution.py
@@ -67,29 +67,30 @@
         copy.wait()
 
 
-def load(array, after, name):
-    count, rank, width = array.shape
+def load(arrays, after):
+    count, rank, width = arrays[0].shape
     half = width // 2
-    pieces = 4
-    n = count // pieces
-
-    def body(source, mine, other, sems):
+    parts = 4
+    n = count // parts
+
+    def body(*refs):
+        sources, mine, other, sems = refs[:2], refs[2:4], refs[4], refs[5]
         core = lax.axis_index("tile") & 1
         pairs = []
-        for out, which in ((other, 1 - core), (mine, core)):
-            lanes = pl.ds(pl.multiple_of(which * half, half), half)
-            for i in range(pieces):
-                rows = pl.ds(i * n, n)
-                pairs.append((source.at[rows, :, lanes], out.at[rows]))
+        for k, source in enumerate(sources):
+            for which, out, base in ((1 - core, other, k * count), (core, mine[k], 0)):
+                lanes = pl.ds(pl.multiple_of(which * half, half), half)
+                for i in range(parts):
+                    pairs.append((source.at[pl.ds(i * n, n), :, lanes], out.at[pl.ds(base + i * n, n)]))
         fetch(pairs, sems)
 
     return local(
         body,
-        [shape((count, rank, half), array.dtype)] * 2,
-        array,
-        name=name,
-        specs=[whole(pltpu.HBM)],
-        scratches=[pltpu.SemaphoreType.DMA((2 * pieces,))],
+        [shape((k * count, rank, half), arrays[0].dtype) for k in (1, 1, 2)],
+        *arrays,
+        name="load",
+        specs=[whole(pltpu.HBM)] * 2,
+        scratches=[pltpu.SemaphoreType.DMA((4 * parts,))],
         after=after,
     )
 
@@ -237,6 +238,8 @@
         def dots(g, _):
             row, first = at_rows[g // groups], (g % groups) * GROUP
             taken = jnp.concatenate([near[at[row, first + i]].astype(F32) for i in range(GROUP)], axis=0)
+            if g >= groups:
+                first += factors[2] * count
             factor = (mine, other)[g // groups][first : first + GROUP].reshape(span, half)
             return lax.dot_general(
                 taken.astype(BF16), factor, (((1,), (1,)), ((), ())), preferred_element_type=F32
@@ -257,7 +260,7 @@
         [shape((2 * groups, probes, span), F32)],
         table,
         *pieces,
-        *factors,
+        *factors[:2],
         name=name,
         specs=[whole(pltpu.SMEM)] + [whole()] * (len(pieces) + 2),
         flops=4 * count * rank * half * probes * GROUP,
@@ -280,6 +283,8 @@
             total = jnp.concatenate([total.astype(BF16).astype(F32)] * GROUP, axis=0)
             total = jnp.where(own, total, 0.0).astype(BF16)
             first = (g % groups) * GROUP
+            if g >= groups:
+                first += factors[2] * count
             factor = (mine, other)[g // groups][first : first + GROUP].reshape(span, half)
             return jnp.dot(total, factor, preferred_element_type=F32)
 
@@ -300,7 +305,7 @@
         acc,
         mine_sum,
         other_sum,
-        *factors,
+        *factors[:2],
         name=name,
         specs=[whole(pltpu.SMEM)] + [whole()] * 5,
         aliases={1: 0},
@@ -336,7 +341,10 @@
             spot = jnp.where((away & 1) != 0, span + place(away, orders[1]), place(away, orders[0]))
             table[k : k + 1, :] = spot * cell_blocks + col_local
             away = row_owner ^ me
-            spot = (((away & 6) // 2) * rest + row_owner // 8) * 2 + (row_owner & 1)
+            quarter = jnp.zeros_like(away)
+            for j, bit in enumerate(SQUARE):
+                quarter = jnp.where((away & 6) == bit, 1 + j, quarter)
+            spot = (quarter * rest + row_owner // 8) * 2 + (row_owner & 1)
             table[k + 2 : k + 3, :] = spot * station_blocks + row_local
             table[k + 4 : k + 5, :] = rank
         fetch([(table, table_out)], sems)
@@ -413,47 +421,46 @@
         got_p = swap(part_p, bit_p)
         got_q = swap(part_q, bit_q) if step else swap(send, bit_q ^ 1)
         if step == 1:
-            v_here, v_send = load(v_factor, (part_p, part_q), "load_v")
-            u_here, u_send = load(u_factor, (part_p, part_q, v_here), "load_u")
+            v_here, u_here, halves = load((v_factor, u_factor), (part_p, part_q))
             after = (u_here,)
         if step < len(steps) - 1:
             part_p = join(part_p, got_p, after=after)
             part_q = join(part_q, got_q)
             after = ()
         if step == 1:
-            v_send, u_send = gate((v_send, u_send), (part_p, part_q))
-    v_both = (v_here, swap(v_send, 1))
-    u_both = (u_here, swap(u_send, 1))
+            halves = gate((halves,), (part_p, part_q))[0]
+    halves = swap(halves, 1)
 
     stations = peers * station_blocks
     acc = zeros((stations, probe_count, station_width // 2), (part_p, part_q))
-    coeff = shrink([part_p, got_p, part_q, got_q], (0, 1), table, v_both, "coeff")
+    coeff = shrink([part_p, got_p, part_q, got_q], (0, 1), table, (v_here, halves, 0), "coeff")
     quarter = stations // 4
     total, *sends = expand(
         coeff,
         swap(coeff, 1),
         (2, 3),
         table,
-        u_both,
+        (u_here, halves, 1),
         acc,
-        [(k // 2 * quarter, quarter) for k in SQUARE],
+        [((1 + j) * quarter, quarter) for j in range(len(SQUARE))],
         "partial",
     )
-    total, send = plus(total, *[swap(send, k) for k, send in zip(SQUARE, sends)])
+    sends = dict(zip(SQUARE, sends))
+    total, send = plus(total, *[swap(sends[k], k) for k in (4, 6, 2)])
     for bit in bits[2:-1]:
         total, send = plus(total, swap(send, bit))
     weighted = weigh(total, swap(send, bits[-1]), weight)
-    gots = {k: swap(weighted, k) for k in SQUARE}
+    pieces = [weighted] + [swap(weighted, k) for k in SQUARE]
 
     cells = peers * cell_blocks
     acc = zeros((cells, probe_count, cell_width // 2), (total,))
-    back = shrink([weighted, gots[2], gots[4], gots[6]], (2, 3), table, u_both, "back")
+    back = shrink(pieces, (2, 3), table, (u_here, halves, 1), "back")
     total, send_p, send_q = expand(
         back,
         swap(back, 1),
         (0, 1),
         table,
-        v_both,
+        (v_here, halves, 0),
         acc,
         [(cells // 4, cells // 4), (3 * cells // 4, cells // 4)],
         "spread",

time: 83 us -> 82.1 us (0.989)
  Pallas kernels: 14.1 us -> 13.1 us
  starting transfers between devices: 28.8 us -> 29.8 us
    ppermute x25 -> x24, starting transfers between devices: 28.8 us -> 29.8 us  [swap(): return lax.ppermute(array, 'tile', [(i, i ^ bits) for i in range(count)])]
    pallas_call x22 -> x21, Pallas kernels: 14.1 us -> 13.1 us  [local(): pl.pallas_call(run, out_shape=[a if s.memory_space is None else s.memory_...]
    ppermute x25 -> x24, waiting for transfers between devices: 39.6 us -> 38.8 us  [swap(): return lax.ppermute(array, 'tile', [(i, i ^ bits) for i in range(count)])]
  transfers between devices with their start and end apart: 25 -> 24, of which waited for: 19 -> 18; matrix products, arithmetic and copies ran while one was open for 0% -> 0% of each run, Pallas kernels for 9% -> 7%
where the time goes in v10:
time: 82.1 us; the launch traced here: 81.9 us
  waiting for transfers between devices  38.8 us (47%)
  starting transfers between devices  29.8 us (36%)
  Pallas kernels  13.1 us (16%)
    ppermute x24, waiting for transfers between devices, swap(): return lax.ppermute(array, 'tile', [(i, i ^ bits) for i in range(count)])  38.8 us
    ppermute x24, starting transfers between devices, swap(): return lax.ppermute(array, 'tile', [(i, i ^ bits) for i in range(count)])  29.8 us
    pallas_call x21, Pallas kernels, local(): pl.pallas_call(run, out_shape=[a if s.memory_space is None else s.memory_...  13.1 us
  transfers between devices with their start and end apart: 24, of which 18 were waited for; matrix products, arithmetic and copies ran while one was open for 0% of the time, Pallas kernels for 7%

profile of v10, /device:TPU:0, one launch (start us, length us, event | category | flops | bytes accessed | tf_op | source)
XLA Modules:
  0.0 81.9 jit_solution(8916571529121423416)
XLA Ops:
  0.0 1.1 %scale.1 = (bf16[16,8,256]{2,1,0:T(8,128)(2,1)S(1)}, bf16[16,8,256]{2,1,0:T(8,128)(2,1)S(1)}, f32[64,128]{1,0:T(8,128)S(1)}) custom-call(f32[4]{0:T(128)} %refs_0_.2, f32[64,128]{1,0:T(8,128)} %bitcast.9, s32[64,128]{1,0:T(8,128)} %bitcast.10, f32[8,8192]{1,0:T(8,128)} %refs_3_.1), custom_call_target="tpu_custom_call" | custom-call | tf_op jit(solution)/shard_map/scale/pallas_call | solution.py:49
  1.1 0.5 collective-permute-start.2
  1.6 2.6 %collective-permute-start.3 = (bf16[16,8,256]{2,1,0:T(8,128)(2,1)S(1)}, bf16[16,8,256]{2,1,0:T(8,128)(2,1)S(1)}, u32[]{:S(2)}, u32[]{:S(2)}) collective-permute-start(bf16[16,8,256]{2,1,0:T(8,128)(2,1)S(1)} %get-tuple-element.34), channel_id=1, source_target_pairs={{0,3},{1,2},{2,1},{3,0},{4,7},{5,6},{6,5},{7,4},{8,11},{9,10},{10,... | collective-permute-start | bytes 196616 | tf_op jit(solution)/shard_map/ppermute | solution.py:34
  4.2 2.6 %collective-permute-start = (bf16[16,8,256]{2,1,0:T(8,128)(2,1)S(1)}, bf16[16,8,256]{2,1,0:T(8,128)(2,1)S(1)}, u32[]{:S(2)}, u32[]{:S(2)}) collective-permute-start(bf16[16,8,256]{2,1,0:T(8,128)(2,1)S(1)} %get-tuple-element.32.refs_0_), channel_id=1, source_target_pairs={{0,8},{1,9},{2,10},{3,11},{4,12},{5,13},{6,14},{7,15},{8,0},{9,1},... | collective-permute-start | bytes 196616 | tf_op jit(solution)/shard_map/ppermute | solution.py:34
  6.8 1.5 %plan.1 = (s32[8,128]{1,0:T(8,128)S(4)}, f32[64,128]{1,0:T(8,128)S(1)}) custom-call(s32[16,128]{1,0:T(8,128)} %bitcast.11, s32[16,128]{1,0:T(8,128)} %bitcast.12, s32[16,128]{1,0:T(8,128)} %bitcast.13, s32[16,128]{1,0:T(8,128)} %bitcast.14, s32[16,128]{1,0:T(8,128)} %bitcast.15, f32[256,128]{1,0:T(8,128)} %bitcast.8, ...), custom_call_target="tpu_custom_call" | custom-call | tf_op jit(solution)/shard_map/plan/pallas_call | solution.py:49
  8.4 0.8 collective-permute-start.4
  9.2 1.6 %collective-permute-done.refs_1_ = bf16[16,8,256]{2,1,0:T(8,128)(2,1)S(1)} collective-permute-done((bf16[16,8,256]{2,1,0:T(8,128)(2,1)S(1)}, bf16[16,8,256]{2,1,0:T(8,128)(2,1)S(1)}, u32[]{:S(2)}, u32[]{:S(2)}) %collective-permute-start) | collective-permute-done | bytes 65568 | tf_op jit(solution)/shard_map/ppermute | solution.py:34
  10.8 0.6 collective-permute-start.1
  11.4 3.5 %load.1 = (bf16[128,32,256]{2,1,0:T(8,128)(2,1)S(1)}, bf16[128,32,256]{2,1,0:T(8,128)(2,1)S(1)}, bf16[256,32,256]{2,1,0:T(8,128)(2,1)S(1)}) custom-call(bf16[128,32,512]{2,1,0:T(8,128)(2,1)} %refs_0_.3, bf16[128,32,512]{2,1,0:T(8,128)(2,1)} %refs_1_.1, bf16[32,8,256]{2,1,0:T(8,128)(2,1)S(1)} %join.4.refs_2_.refs_0_, bf16[32,8,256]{2,1,0:T(8,128)(2,1)S(1)} %join.5.refs_3_.refs_0_), custom_call_target="tpu_custom_call" | custom-call | tf_op jit(solution)/shard_map/load/pallas_call | solution.py:49
  14.9 2.5 %collective-permute-done.4.refs_1_ = bf16[32,8,256]{2,1,0:T(8,128)(2,1)S(1)} collective-permute-done((bf16[32,8,256]{2,1,0:T(8,128)(2,1)S(1)}, bf16[32,8,256]{2,1,0:T(8,128)(2,1)S(1)}, u32[]{:S(2)}, u32[]{:S(2)}) %collective-permute-start.4) | collective-permute-done | bytes 131104 | tf_op jit(solution)/shard_map/ppermute | solution.py:34
  17.5 0.1 collective-permute-done.1.refs_1_
  17.6 0.1 collective-permute-start.7
  17.7 0.5 collective-permute-start.5
  18.2 1.3 %collective-permute-start.6 = (bf16[64,8,256]{2,1,0:T(8,128)(2,1)S(1)}, bf16[64,8,256]{2,1,0:T(8,128)(2,1)S(1)}, u32[]{:S(2)}, u32[]{:S(2)}) collective-permute-start(bf16[64,8,256]{2,1,0:T(8,128)(2,1)S(1)} %join.7.refs_1_.refs_2_.refs_3_), channel_id=1, source_target_pairs={{0,4},{1,5},{2,6},{3,7},{4,0},{5,1},{6,2},{7,3},{8,12},{9,13},{10,... | collective-permute-start | bytes 786440 | tf_op jit(solution)/shard_map/ppermute | solution.py:34
  19.5 6.9 %collective-permute-done.5.refs_2_ = bf16[64,8,256]{2,1,0:T(8,128)(2,1)S(1)} collective-permute-done((bf16[64,8,256]{2,1,0:T(8,128)(2,1)S(1)}, bf16[64,8,256]{2,1,0:T(8,128)(2,1)S(1)}, u32[]{:S(2)}, u32[]{:S(2)}) %collective-permute-start.5) | collective-permute-done | bytes 262176 | tf_op jit(solution)/shard_map/ppermute | solution.py:34
  26.4 0.2 collective-permute-done.6.refs_4_
  26.5 1.4 %coeff.1.refs_2_ = f32[32,8,256]{2,1,0:T(8,128)S(1)} custom-call(s32[8,128]{1,0:T(8,128)S(4)} %get-tuple-element.31.refs_0_, bf16[64,8,256]{2,1,0:T(8,128)(2,1)S(1)} %join.6.refs_0_.refs_1_, bf16[64,8,256]{2,1,0:T(8,128)(2,1)S(1)} %collective-permute-done.5.refs_2_, bf16[64,8,256]{2,1,0:T(8,128)(2,1)S(1)} %join.7.refs_1_.refs_2_.refs_3_, ...), custom_call_target="tpu_custom_call" | custom-call | tf_op jit(solution)/shard_map/coeff/pallas_call | solution.py:49
  28.1 1.5 %collective-permute-done.8.refs_3_ = f32[32,8,256]{2,1,0:T(8,128)S(1)} collective-permute-done((f32[32,8,256]{2,1,0:T(8,128)S(1)}, f32[32,8,256]{2,1,0:T(8,128)S(1)}, u32[]{:S(2)}, u32[]{:S(2)}) %collective-permute-start.8) | collective-permute-done | bytes 262176 | tf_op jit(solution)/shard_map/ppermute | solution.py:34
  29.6 1.5 %partial.1 = (f32[64,8,256]{2,1,0:T(8,128)S(1)}, bf16[16,8,256]{2,1,0:T(8,128)(2,1)S(1)}, bf16[16,8,256]{2,1,0:T(8,128)(2,1)S(1)}, bf16[16,8,256]{2,1,0:T(8,128)(2,1)S(1)}) custom-call(s32[8,128]{1,0:T(8,128)S(4)} %get-tuple-element.31.refs_0_, f32[64,8,256]{2,1,0:T(8,128)S(1)} %zeros.2.refs_1_, ...), custom_call_target="tpu_custom_call", output_to_operand_aliasing={{0}: (1, {})} | custom-call | tf_op jit(solution)/shard_map/partial/pallas_call | solution.py:49
  31.1 1.4 %collective-permute-start.10 = (bf16[16,8,256]{2,1,0:T(8,128)(2,1)S(1)}, bf16[16,8,256]{2,1,0:T(8,128)(2,1)S(1)}, u32[]{:S(2)}, u32[]{:S(2)}) collective-permute-start(bf16[16,8,256]{2,1,0:T(8,128)(2,1)S(1)} %get-tuple-element.40), channel_id=1, source_target_pairs={{0,6},{1,7},{2,4},{3,5},{4,2},{5,3},{6,0},{7,1},{8,14},{9,15},{10,... | collective-permute-start | bytes 196616 | tf_op jit(solution)/shard_map/ppermute | solution.py:34
  32.5 1.5 %collective-permute-start.11 = (bf16[16,8,256]{2,1,0:T(8,128)(2,1)S(1)}, bf16[16,8,256]{2,1,0:T(8,128)(2,1)S(1)}, u32[]{:S(2)}, u32[]{:S(2)}) collective-permute-start(bf16[16,8,256]{2,1,0:T(8,128)(2,1)S(1)} %get-tuple-element.41), channel_id=1, source_target_pairs={{0,2},{1,3},{2,0},{3,1},{4,6},{5,7},{6,4},{7,5},{8,10},{9,11},{10,... | collective-permute-start | bytes 196616 | tf_op jit(solution)/shard_map/ppermute | solution.py:34
  34.0 0.7 collective-permute-start.9
  34.7 2.0 %collective-permute-done.10.refs_2_ = bf16[16,8,256]{2,1,0:T(8,128)(2,1)S(1)} collective-permute-done((bf16[16,8,256]{2,1,0:T(8,128)(2,1)S(1)}, bf16[16,8,256]{2,1,0:T(8,128)(2,1)S(1)}, u32[]{:S(2)}, u32[]{:S(2)}) %collective-permute-start.10) | collective-permute-done | bytes 65568 | tf_op jit(solution)/shard_map/ppermute | solution.py:34
  36.6 1.0 %collective-permute-done.11.refs_3_ = bf16[16,8,256]{2,1,0:T(8,128)(2,1)S(1)} collective-permute-done((bf16[16,8,256]{2,1,0:T(8,128)(2,1)S(1)}, bf16[16,8,256]{2,1,0:T(8,128)(2,1)S(1)}, u32[]{:S(2)}, u32[]{:S(2)}) %collective-permute-start.11) | collective-permute-done | bytes 65568 | tf_op jit(solution)/shard_map/ppermute | solution.py:34
  37.6 0.6 collective-permute-done.9.refs_1_
  38.3 4.0 %collective-permute-start.12 = (bf16[16,8,256]{2,1,0:T(8,128)(2,1)S(1)}, bf16[16,8,256]{2,1,0:T(8,128)(2,1)S(1)}, u32[]{:S(2)}, u32[]{:S(2)}) collective-permute-start(bf16[16,8,256]{2,1,0:T(8,128)(2,1)S(1)} %get-tuple-element.43), channel_id=1, source_target_pairs={{0,8},{1,9},{2,10},{3,11},{4,12},{5,13},{6,14},{7,15},{8,0},{9,1},... | collective-permute-start | bytes 196616 | tf_op jit(solution)/shard_map/ppermute | solution.py:34
  42.3 3.1 %collective-permute-done.12.refs_1_ = bf16[16,8,256]{2,1,0:T(8,128)(2,1)S(1)} collective-permute-done((bf16[16,8,256]{2,1,0:T(8,128)(2,1)S(1)}, bf16[16,8,256]{2,1,0:T(8,128)(2,1)S(1)}, u32[]{:S(2)}, u32[]{:S(2)}) %collective-permute-start.12) | collective-permute-done | bytes 65568 | tf_op jit(solution)/shard_map/ppermute | solution.py:34
  45.4 0.5 collective-permute-start.13
  45.9 1.0 %collective-permute-start.14 = (bf16[16,8,256]{2,1,0:T(8,128)(2,1)S(1)}, bf16[16,8,256]{2,1,0:T(8,128)(2,1)S(1)}, u32[]{:S(2)}, u32[]{:S(2)}) collective-permute-start(bf16[16,8,256]{2,1,0:T(8,128)(2,1)S(1)} %weigh.1.refs_1_), channel_id=1, source_target_pairs={{0,2},{1,3},{2,0},{3,1},{4,6},{5,7},{6,4},{7,5},{8,10},{9,11},{10,... | collective-permute-start | bytes 196616 | tf_op jit(solution)/shard_map/ppermute | solution.py:34
  46.8 2.1 %collective-permute-start.15 = (bf16[16,8,256]{2,1,0:T(8,128)(2,1)S(1)}, bf16[16,8,256]{2,1,0:T(8,128)(2,1)S(1)}, u32[]{:S(2)}, u32[]{:S(2)}) collective-permute-start(bf16[16,8,256]{2,1,0:T(8,128)(2,1)S(1)} %weigh.1.refs_1_), channel_id=1, source_target_pairs={{0,4},{1,5},{2,6},{3,7},{4,0},{5,1},{6,2},{7,3},{8,12},{9,13},{10,... | collective-permute-start | bytes 196616 | tf_op jit(solution)/shard_map/ppermute | solution.py:34
  48.9 1.8 %collective-permute-done.13.refs_2_ = bf16[16,8,256]{2,1,0:T(8,128)(2,1)S(1)} collective-permute-done((bf16[16,8,256]{2,1,0:T(8,128)(2,1)S(1)}, bf16[16,8,256]{2,1,0:T(8,128)(2,1)S(1)}, u32[]{:S(2)}, u32[]{:S(2)}) %collective-permute-start.13) | collective-permute-done | bytes 65568 | tf_op jit(solution)/shard_map/ppermute | solution.py:34
  50.7 0.2 collective-permute-done.14.refs_3_
  50.9 0.3 collective-permute-done.15.refs_4_
  51.2 1.4 %back.1.refs_2_ = f32[32,8,256]{2,1,0:T(8,128)S(1)} custom-call(s32[8,128]{1,0:T(8,128)S(4)} %get-tuple-element.31.refs_0_, bf16[16,8,256]{2,1,0:T(8,128)(2,1)S(1)} %weigh.1.refs_1_, bf16[16,8,256]{2,1,0:T(8,128)(2,1)S(1)} %collective-permute-done.13.refs_2_, bf16[16,8,256]{2,1,0:T(8,128)(2,1)S(1)} %collective-permute-done.14.refs_3_, ...), custom_call_target="tpu_custom_call" | custom-call | tf_op jit(solution)/shard_map/back/pallas_call | solution.py:49
  52.6 0.1 zeros.3.refs_1_
  52.8 1.4 %collective-permute-done.16.refs_3_ = f32[32,8,256]{2,1,0:T(8,128)S(1)} collective-permute-done((f32[32,8,256]{2,1,0:T(8,128)S(1)}, f32[32,8,256]{2,1,0:T(8,128)S(1)}, u32[]{:S(2)}, u32[]{:S(2)}) %collective-permute-start.16) | collective-permute-done | bytes 262176 | tf_op jit(solution)/shard_map/ppermute | solution.py:34
  54.2 1.5 %spread.1 = (f32[256,8,256]{2,1,0:T(8,128)S(1)}, bf16[64,8,256]{2,1,0:T(8,128)(2,1)S(1)}, bf16[64,8,256]{2,1,0:T(8,128)(2,1)S(1)}) custom-call(s32[8,128]{1,0:T(8,128)S(4)} %get-tuple-element.31.refs_0_, f32[256,8,256]{2,1,0:T(8,128)S(1)} %zeros.3.refs_1_, f32[32,8,256]{2,1,0:T(8,128)S(1)} %back.1.refs_2_, ...), custom_call_target="tpu_custom_call", output_to_operand_aliasing={{0}: (1, {})} | custom-call | tf_op jit(solution)/shard_map/spread/pallas_call | solution.py:49
  55.7 2.1 %collective-permute-start.20 = (bf16[64,8,256]{2,1,0:T(8,128)(2,1)S(1)}, bf16[64,8,256]{2,1,0:T(8,128)(2,1)S(1)}, u32[]{:S(2)}, u32[]{:S(2)}) collective-permute-start(bf16[64,8,256]{2,1,0:T(8,128)(2,1)S(1)} %get-tuple-element.50), channel_id=1, source_target_pairs={{0,4},{1,5},{2,6},{3,7},{4,0},{5,1},{6,2},{7,3},{8,12},{9,13},{10,... | collective-permute-start | bytes 786440 | tf_op jit(solution)/shard_map/ppermute | solution.py:34
  57.8 1.1 %collective-permute-start.17 = (bf16[64,8,256]{2,1,0:T(8,128)(2,1)S(1)}, bf16[64,8,256]{2,1,0:T(8,128)(2,1)S(1)}, u32[]{:S(2)}, u32[]{:S(2)}) collective-permute-start(bf16[64,8,256]{2,1,0:T(8,128)(2,1)S(1)} %get-tuple-element.45), channel_id=1, source_target_pairs={{0,2},{1,3},{2,0},{3,1},{4,6},{5,7},{6,4},{7,5},{8,10},{9,11},{10,... | collective-permute-start | bytes 786440 | tf_op jit(solution)/shard_map/ppermute | solution.py:34
  58.9 5.5 %collective-permute-done.20.refs_1_ = bf16[64,8,256]{2,1,0:T(8,128)(2,1)S(1)} collective-permute-done((bf16[64,8,256]{2,1,0:T(8,128)(2,1)S(1)}, bf16[64,8,256]{2,1,0:T(8,128)(2,1)S(1)}, u32[]{:S(2)}, u32[]{:S(2)}) %collective-permute-start.20) | collective-permute-done | bytes 262176 | tf_op jit(solution)/shard_map/ppermute | solution.py:34
  64.4 2.7 %collective-permute-start.21 = (bf16[32,8,256]{2,1,0:T(8,128)(2,1)S(1)}, bf16[32,8,256]{2,1,0:T(8,128)(2,1)S(1)}, u32[]{:S(2)}, u32[]{:S(2)}) collective-permute-start(bf16[32,8,256]{2,1,0:T(8,128)(2,1)S(1)} %get-tuple-element.52), channel_id=1, source_target_pairs={{0,8},{1,9},{2,10},{3,11},{4,12},{5,13},{6,14},{7,15},{8,0},{9,1},... | collective-permute-start | bytes 393224 | tf_op jit(solution)/shard_map/ppermute | solution.py:34
  67.1 1.3 %collective-permute-start.18 = (bf16[32,8,256]{2,1,0:T(8,128)(2,1)S(1)}, bf16[32,8,256]{2,1,0:T(8,128)(2,1)S(1)}, u32[]{:S(2)}, u32[]{:S(2)}) collective-permute-start(bf16[32,8,256]{2,1,0:T(8,128)(2,1)S(1)} %get-tuple-element.47), channel_id=1, source_target_pairs={{0,4},{1,5},{2,6},{3,7},{4,0},{5,1},{6,2},{7,3},{8,12},{9,13},{10,... | collective-permute-start | bytes 393224 | tf_op jit(solution)/shard_map/ppermute | solution.py:34
  68.5 4.8 %collective-permute-done.21.refs_1_ = bf16[32,8,256]{2,1,0:T(8,128)(2,1)S(1)} collective-permute-done((bf16[32,8,256]{2,1,0:T(8,128)(2,1)S(1)}, bf16[32,8,256]{2,1,0:T(8,128)(2,1)S(1)}, u32[]{:S(2)}, u32[]{:S(2)}) %collective-permute-start.21) | collective-permute-done | bytes 131104 | tf_op jit(solution)/shard_map/ppermute | solution.py:34
  73.4 1.3 %collective-permute-start.23 = (bf16[16,8,256]{2,1,0:T(8,128)(2,1)S(1)}, bf16[16,8,256]{2,1,0:T(8,128)(2,1)S(1)}, u32[]{:S(2)}, u32[]{:S(2)}) collective-permute-start(bf16[16,8,256]{2,1,0:T(8,128)(2,1)S(1)} %get-tuple-element.54), channel_id=1, source_target_pairs={{0,3},{1,2},{2,1},{3,0},{4,7},{5,6},{6,5},{7,4},{8,11},{9,10},{10,... | collective-permute-start | bytes 196616 | tf_op jit(solution)/shard_map/ppermute | solution.py:34
  74.7 0.9 %collective-permute-start.19 = (bf16[16,8,256]{2,1,0:T(8,128)(2,1)S(1)}, bf16[16,8,256]{2,1,0:T(8,128)(2,1)S(1)}, u32[]{:S(2)}, u32[]{:S(2)}) collective-permute-start(bf16[16,8,256]{2,1,0:T(8,128)(2,1)S(1)} %get-tuple-element.49), channel_id=1, source_target_pairs={{0,8},{1,9},{2,10},{3,11},{4,12},{5,13},{6,14},{7,15},{8,0},{9,1},... | collective-permute-start | bytes 196616 | tf_op jit(solution)/shard_map/ppermute | solution.py:34
  75.6 1.6 %collective-permute-done.23.refs_3_ = bf16[16,8,256]{2,1,0:T(8,128)(2,1)S(1)} collective-permute-done((bf16[16,8,256]{2,1,0:T(8,128)(2,1)S(1)}, bf16[16,8,256]{2,1,0:T(8,128)(2,1)S(1)}, u32[]{:S(2)}, u32[]{:S(2)}) %collective-permute-start.23) | collective-permute-done | bytes 65568 | tf_op jit(solution)/shard_map/ppermute | solution.py:34
  77.3 3.8 %collective-permute-done.19.refs_1_ = bf16[16,8,256]{2,1,0:T(8,128)(2,1)S(1)} collective-permute-done((bf16[16,8,256]{2,1,0:T(8,128)(2,1)S(1)}, bf16[16,8,256]{2,1,0:T(8,128)(2,1)S(1)}, u32[]{:S(2)}, u32[]{:S(2)}) %collective-permute-start.19) | collective-permute-done | bytes 65568 | tf_op jit(solution)/shard_map/ppermute | solution.py:34
  81.1 0.7 final.1
  (21 shorter events, 0.5 us)
Async XLA Ops:
  1.1 7.3 %collective-permute-start.2 = (bf16[16,8,256]{2,1,0:T(8,128)(2,1)S(1)}, bf16[16,8,256]{2,1,0:T(8,128)(2,1)S(1)}, u32[]{:S(2)}, u32[]{:S(2)}) collective-permute-start(bf16[16,8,256]{2,1,0:T(8,128)(2,1)S(1)} %get-tuple-element.34), channel_id=1, source_target_pairs={{0,1},{1,0},{2,3},{3,2},{4,5},{5,4},{6,7},{7,6},{8,9},{9,8},{10,11... | collective-permute-start | bytes 196616 | tf_op jit(solution)/shard_map/ppermute | solution.py:34
  1.6 6.8 %collective-permute-start.3 = (bf16[16,8,256]{2,1,0:T(8,128)(2,1)S(1)}, bf16[16,8,256]{2,1,0:T(8,128)(2,1)S(1)}, u32[]{:S(2)}, u32[]{:S(2)}) collective-permute-start(bf16[16,8,256]{2,1,0:T(8,128)(2,1)S(1)} %get-tuple-element.34), channel_id=1, source_target_pairs={{0,3},{1,2},{2,1},{3,0},{4,7},{5,6},{6,5},{7,4},{8,11},{9,10},{10,... | collective-permute-start | bytes 196616 | tf_op jit(solution)/shard_map/ppermute | solution.py:34
  4.2 6.6 %collective-permute-start = (bf16[16,8,256]{2,1,0:T(8,128)(2,1)S(1)}, bf16[16,8,256]{2,1,0:T(8,128)(2,1)S(1)}, u32[]{:S(2)}, u32[]{:S(2)}) collective-permute-start(bf16[16,8,256]{2,1,0:T(8,128)(2,1)S(1)} %get-tuple-element.32.refs_0_), channel_id=1, source_target_pairs={{0,8},{1,9},{2,10},{3,11},{4,12},{5,13},{6,14},{7,15},{8,0},{9,1},... | collective-permute-start | bytes 196616 | tf_op jit(solution)/shard_map/ppermute | solution.py:34
  8.4 9.1 %collective-permute-start.4 = (bf16[32,8,256]{2,1,0:T(8,128)(2,1)S(1)}, bf16[32,8,256]{2,1,0:T(8,128)(2,1)S(1)}, u32[]{:S(2)}, u32[]{:S(2)}) collective-permute-start(bf16[32,8,256]{2,1,0:T(8,128)(2,1)S(1)} %join.5.refs_3_.refs_0_), channel_id=1, source_target_pairs={{0,8},{1,9},{2,10},{3,11},{4,12},{5,13},{6,14},{7,15},{8,0},{9,1},... | collective-permute-start | bytes 393224 | tf_op jit(solution)/shard_map/ppermute | solution.py:34
  10.8 6.7 %collective-permute-start.1 = (bf16[32,8,256]{2,1,0:T(8,128)(2,1)S(1)}, bf16[32,8,256]{2,1,0:T(8,128)(2,1)S(1)}, u32[]{:S(2)}, u32[]{:S(2)}) collective-permute-start(bf16[32,8,256]{2,1,0:T(8,128)(2,1)S(1)} %join.4.refs_2_.refs_0_), channel_id=1, source_target_pairs={{0,4},{1,5},{2,6},{3,7},{4,0},{5,1},{6,2},{7,3},{8,12},{9,13},{10,... | collective-permute-start | bytes 393224 | tf_op jit(solution)/shard_map/ppermute | solution.py:34
  17.6 9.0 %collective-permute-start.7 = (bf16[256,32,256]{2,1,0:T(8,128)(2,1)S(1)}, bf16[256,32,256]{2,1,0:T(8,128)(2,1)S(1)}, u32[]{:S(2)}, u32[]{:S(2)}) collective-permute-start(bf16[256,32,256]{2,1,0:T(8,128)(2,1)S(1)} %gate.1), channel_id=1, source_target_pairs={{0,1},{1,0},{2,3},{3,2},{4,5},{5,4},{6,7},{7,6},{8,9},{9,8},{10,11... | collective-permute-start | bytes 12582920 | tf_op jit(solution)/shard_map/ppermute | solution.py:34
  17.7 8.7 %collective-permute-start.5 = (bf16[64,8,256]{2,1,0:T(8,128)(2,1)S(1)}, bf16[64,8,256]{2,1,0:T(8,128)(2,1)S(1)}, u32[]{:S(2)}, u32[]{:S(2)}) collective-permute-start(bf16[64,8,256]{2,1,0:T(8,128)(2,1)S(1)} %join.6.refs_0_.refs_1_), channel_id=1, source_target_pairs={{0,2},{1,3},{2,0},{3,1},{4,6},{5,7},{6,4},{7,5},{8,10},{9,11},{10,... | collective-permute-start | bytes 786440 | tf_op jit(solution)/shard_map/ppermute | solution.py:34
  18.2 8.4 %collective-permute-start.6 = (bf16[64,8,256]{2,1,0:T(8,128)(2,1)S(1)}, bf16[64,8,256]{2,1,0:T(8,128)(2,1)S(1)}, u32[]{:S(2)}, u32[]{:S(2)}) collective-permute-start(bf16[64,8,256]{2,1,0:T(8,128)(2,1)S(1)} %join.7.refs_1_.refs_2_.refs_3_), channel_id=1, source_target_pairs={{0,4},{1,5},{2,6},{3,7},{4,0},{5,1},{6,2},{7,3},{8,12},{9,13},{10,... | collective-permute-start | bytes 786440 | tf_op jit(solution)/shard_map/ppermute | solution.py:34
  28.0 1.6 %collective-permute-start.8 = (f32[32,8,256]{2,1,0:T(8,128)S(1)}, f32[32,8,256]{2,1,0:T(8,128)S(1)}, u32[]{:S(2)}, u32[]{:S(2)}) collective-permute-start(f32[32,8,256]{2,1,0:T(8,128)S(1)} %coeff.1.refs_2_), channel_id=1, source_target_pairs={{0,1},{1,0},{2,3},{3,2},{4,5},{5,4},{6,7},{7,6},{8,9},{9,8},{10,11... | collective-permute-start | bytes 786440 | tf_op jit(solution)/shard_map/ppermute | solution.py:34
  31.1 5.5 %collective-permute-start.10 = (bf16[16,8,256]{2,1,0:T(8,128)(2,1)S(1)}, bf16[16,8,256]{2,1,0:T(8,128)(2,1)S(1)}, u32[]{:S(2)}, u32[]{:S(2)}) collective-permute-start(bf16[16,8,256]{2,1,0:T(8,128)(2,1)S(1)} %get-tuple-element.40), channel_id=1, source_target_pairs={{0,6},{1,7},{2,4},{3,5},{4,2},{5,3},{6,0},{7,1},{8,14},{9,15},{10,... | collective-permute-start | bytes 196616 | tf_op jit(solution)/shard_map/ppermute | solution.py:34
  32.5 5.1 %collective-permute-start.11 = (bf16[16,8,256]{2,1,0:T(8,128)(2,1)S(1)}, bf16[16,8,256]{2,1,0:T(8,128)(2,1)S(1)}, u32[]{:S(2)}, u32[]{:S(2)}) collective-permute-start(bf16[16,8,256]{2,1,0:T(8,128)(2,1)S(1)} %get-tuple-element.41), channel_id=1, source_target_pairs={{0,2},{1,3},{2,0},{3,1},{4,6},{5,7},{6,4},{7,5},{8,10},{9,11},{10,... | collective-permute-start | bytes 196616 | tf_op jit(solution)/shard_map/ppermute | solution.py:34
  34.0 4.3 %collective-permute-start.9 = (bf16[16,8,256]{2,1,0:T(8,128)(2,1)S(1)}, bf16[16,8,256]{2,1,0:T(8,128)(2,1)S(1)}, u32[]{:S(2)}, u32[]{:S(2)}) collective-permute-start(bf16[16,8,256]{2,1,0:T(8,128)(2,1)S(1)} %get-tuple-element.39), channel_id=1, source_target_pairs={{0,4},{1,5},{2,6},{3,7},{4,0},{5,1},{6,2},{7,3},{8,12},{9,13},{10,... | collective-permute-start | bytes 196616 | tf_op jit(solution)/shard_map/ppermute | solution.py:34
  38.3 7.0 %collective-permute-start.12 = (bf16[16,8,256]{2,1,0:T(8,128)(2,1)S(1)}, bf16[16,8,256]{2,1,0:T(8,128)(2,1)S(1)}, u32[]{:S(2)}, u32[]{:S(2)}) collective-permute-start(bf16[16,8,256]{2,1,0:T(8,128)(2,1)S(1)} %get-tuple-element.43), channel_id=1, source_target_pairs={{0,8},{1,9},{2,10},{3,11},{4,12},{5,13},{6,14},{7,15},{8,0},{9,1},... | collective-permute-start | bytes 196616 | tf_op jit(solution)/shard_map/ppermute | solution.py:34
  45.4 5.3 %collective-permute-start.13 = (bf16[16,8,256]{2,1,0:T(8,128)(2,1)S(1)}, bf16[16,8,256]{2,1,0:T(8,128)(2,1)S(1)}, u32[]{:S(2)}, u32[]{:S(2)}) collective-permute-start(bf16[16,8,256]{2,1,0:T(8,128)(2,1)S(1)} %weigh.1.refs_1_), channel_id=1, source_target_pairs={{0,6},{1,7},{2,4},{3,5},{4,2},{5,3},{6,0},{7,1},{8,14},{9,15},{10,... | collective-permute-start | bytes 196616 | tf_op jit(solution)/shard_map/ppermute | solution.py:34
  45.9 5.0 %collective-permute-start.14 = (bf16[16,8,256]{2,1,0:T(8,128)(2,1)S(1)}, bf16[16,8,256]{2,1,0:T(8,128)(2,1)S(1)}, u32[]{:S(2)}, u32[]{:S(2)}) collective-permute-start(bf16[16,8,256]{2,1,0:T(8,128)(2,1)S(1)} %weigh.1.refs_1_), channel_id=1, source_target_pairs={{0,2},{1,3},{2,0},{3,1},{4,6},{5,7},{6,4},{7,5},{8,10},{9,11},{10,... | collective-permute-start | bytes 196616 | tf_op jit(solution)/shard_map/ppermute | solution.py:34
  46.8 4.3 %collective-permute-start.15 = (bf16[16,8,256]{2,1,0:T(8,128)(2,1)S(1)}, bf16[16,8,256]{2,1,0:T(8,128)(2,1)S(1)}, u32[]{:S(2)}, u32[]{:S(2)}) collective-permute-start(bf16[16,8,256]{2,1,0:T(8,128)(2,1)S(1)} %weigh.1.refs_1_), channel_id=1, source_target_pairs={{0,4},{1,5},{2,6},{3,7},{4,0},{5,1},{6,2},{7,3},{8,12},{9,13},{10,... | collective-permute-start | bytes 196616 | tf_op jit(solution)/shard_map/ppermute | solution.py:34
  52.6 1.6 %collective-permute-start.16 = (f32[32,8,256]{2,1,0:T(8,128)S(1)}, f32[32,8,256]{2,1,0:T(8,128)S(1)}, u32[]{:S(2)}, u32[]{:S(2)}) collective-permute-start(f32[32,8,256]{2,1,0:T(8,128)S(1)} %back.1.refs_2_), channel_id=1, source_target_pairs={{0,1},{1,0},{2,3},{3,2},{4,5},{5,4},{6,7},{7,6},{8,9},{9,8},{10,11... | collective-permute-start | bytes 786440 | tf_op jit(solution)/shard_map/ppermute | solution.py:34
  55.7 8.7 %collective-permute-start.20 = (bf16[64,8,256]{2,1,0:T(8,128)(2,1)S(1)}, bf16[64,8,256]{2,1,0:T(8,128)(2,1)S(1)}, u32[]{:S(2)}, u32[]{:S(2)}) collective-permute-start(bf16[64,8,256]{2,1,0:T(8,128)(2,1)S(1)} %get-tuple-element.50), channel_id=1, source_target_pairs={{0,4},{1,5},{2,6},{3,7},{4,0},{5,1},{6,2},{7,3},{8,12},{9,13},{10,... | collective-permute-start | bytes 786440 | tf_op jit(solution)/shard_map/ppermute | solution.py:34
  57.8 9.3 %collective-permute-start.17 = (bf16[64,8,256]{2,1,0:T(8,128)(2,1)S(1)}, bf16[64,8,256]{2,1,0:T(8,128)(2,1)S(1)}, u32[]{:S(2)}, u32[]{:S(2)}) collective-permute-start(bf16[64,8,256]{2,1,0:T(8,128)(2,1)S(1)} %get-tuple-element.45), channel_id=1, source_target_pairs={{0,2},{1,3},{2,0},{3,1},{4,6},{5,7},{6,4},{7,5},{8,10},{9,11},{10,... | collective-permute-start | bytes 786440 | tf_op jit(solution)/shard_map/ppermute | solution.py:34
  64.4 8.9 %collective-permute-start.21 = (bf16[32,8,256]{2,1,0:T(8,128)(2,1)S(1)}, bf16[32,8,256]{2,1,0:T(8,128)(2,1)S(1)}, u32[]{:S(2)}, u32[]{:S(2)}) collective-permute-start(bf16[32,8,256]{2,1,0:T(8,128)(2,1)S(1)} %get-tuple-element.52), channel_id=1, source_target_pairs={{0,8},{1,9},{2,10},{3,11},{4,12},{5,13},{6,14},{7,15},{8,0},{9,1},... | collective-permute-start | bytes 393224 | tf_op jit(solution)/shard_map/ppermute | solution.py:34
  67.1 7.5 %collective-permute-start.18 = (bf16[32,8,256]{2,1,0:T(8,128)(2,1)S(1)}, bf16[32,8,256]{2,1,0:T(8,128)(2,1)S(1)}, u32[]{:S(2)}, u32[]{:S(2)}) collective-permute-start(bf16[32,8,256]{2,1,0:T(8,128)(2,1)S(1)} %get-tuple-element.47), channel_id=1, source_target_pairs={{0,4},{1,5},{2,6},{3,7},{4,0},{5,1},{6,2},{7,3},{8,12},{9,13},{10,... | collective-permute-start | bytes 393224 | tf_op jit(solution)/shard_map/ppermute | solution.py:34
  73.3 7.8 %collective-permute-start.22 = (f32[16,8,256]{2,1,0:T(8,128)S(1)}, f32[16,8,256]{2,1,0:T(8,128)S(1)}, u32[]{:S(2)}, u32[]{:S(2)}) collective-permute-start(f32[16,8,256]{2,1,0:T(8,128)S(1)} %get-tuple-element.53), channel_id=1, source_target_pairs={{0,1},{1,0},{2,3},{3,2},{4,5},{5,4},{6,7},{7,6},{8,9},{9,8},{10,11... | collective-permute-start | bytes 393224 | tf_op jit(solution)/shard_map/ppermute | solution.py:34
  73.4 3.9 %collective-permute-start.23 = (bf16[16,8,256]{2,1,0:T(8,128)(2,1)S(1)}, bf16[16,8,256]{2,1,0:T(8,128)(2,1)S(1)}, u32[]{:S(2)}, u32[]{:S(2)}) collective-permute-start(bf16[16,8,256]{2,1,0:T(8,128)(2,1)S(1)} %get-tuple-element.54), channel_id=1, source_target_pairs={{0,3},{1,2},{2,1},{3,0},{4,7},{5,6},{6,5},{7,4},{8,11},{9,10},{10,... | collective-permute-start | bytes 196616 | tf_op jit(solution)/shard_map/ppermute | solution.py:34
  74.7 6.4 %collective-permute-start.19 = (bf16[16,8,256]{2,1,0:T(8,128)(2,1)S(1)}, bf16[16,8,256]{2,1,0:T(8,128)(2,1)S(1)}, u32[]{:S(2)}, u32[]{:S(2)}) collective-permute-start(bf16[16,8,256]{2,1,0:T(8,128)(2,1)S(1)} %get-tuple-element.49), channel_id=1, source_target_pairs={{0,8},{1,9},{2,10},{3,11},{4,12},{5,13},{6,14},{7,15},{8,0},{9,1},... | collective-permute-start | bytes 196616 | tf_op jit(solution)/shard_map/ppermute | solution.py:34

commit v11 on v6

--- a/solution.py
+++ b/solution.py
@@ -67,22 +67,26 @@
         copy.wait()
 
 
-def load_body(source, out, sems):
-    n = source.shape[0] // sems.shape[0]
-    rows = [pl.ds(i * n, n) for i in range(sems.shape[0])]
-    fetch([(source.at[r], out.at[r]) for r in rows], sems)
-
-
-def load(array, after, name):
+def load(arrays, after):
+    parts = 4
+
+    def body(*refs):
+        count = len(refs) // 2
+        pairs = []
+        for source, out in zip(refs[:count], refs[count:-1]):
+            n = source.shape[0] // parts
+            pairs += [(source.at[pl.ds(i * n, n)], out.at[pl.ds(i * n, n)]) for i in range(parts)]
+        fetch(pairs, refs[-1])
+
     return local(
-        load_body,
-        [shape(array.shape, array.dtype)],
-        array,
-        name=name,
-        specs=[whole(pltpu.HBM)],
-        scratches=[pltpu.SemaphoreType.DMA((8,))],
+        body,
+        [shape(a.shape, a.dtype) for a in arrays],
+        *arrays,
+        name="load",
+        specs=[whole(pltpu.HBM)] * len(arrays),
+        scratches=[pltpu.SemaphoreType.DMA((parts * len(arrays),))],
         after=after,
-    )[0]
+    )
 
 
 def scale_body(
@@ -108,7 +112,7 @@
                 part[b, :, c * LANES : (c + 1) * LANES] = piece.astype(BF16)
 
 
-def final_body(keep_p, recv_p, keep_q, recv_q, scaling, out):
+def final_body(keep_q, recv_q, keep_p, recv_p, scaling, out):
     blocks, _, width = keep_p.shape
     rows = width // LANES
     for half, (keep, recv) in enumerate(((keep_p, recv_p), (keep_q, recv_q))):
@@ -353,8 +357,7 @@
         got_p = swap(part_p, bit_p)
         got_q = swap(part_q, bit_q)
         if step == 1:
-            v_here = load(v_factor, (part_p, part_q), "load_v")
-            u_here = load(u_factor, (part_p, part_q, v_here), "load_u")
+            v_here, u_here = load((v_factor, u_factor), (part_p, part_q))
             after = (u_here,)
         if step < len(steps) - 1:
             part_p = join(part_p, got_p, after=after)
@@ -379,21 +382,21 @@
 
     acc = zeros((peers * cell_blocks, probe_count, cell_width), (total,))
     total, send_p, send_q = tiles(pieces, 1, 0, table, u_here, v_here, acc, 2, BF16, "adjoint")
+    keep_q, send_q = fold(total, swap(send_q, 1), base=total.shape[0] // 4)
     keep_p, send_p = fold(total, swap(send_p, 1))
-    keep_q, send_q = fold(total, swap(send_q, 1), base=total.shape[0] // 4)
     for step, (bit_p, bit_q) in enumerate(steps[::-1]):
         if step > 0:
+            keep_q, send_q = fold(keep_q, got_q)
             keep_p, send_p = fold(keep_p, got_p)
-            keep_q, send_q = fold(keep_q, got_q)
+        got_q = swap(send_q, bit_q)
         got_p = swap(send_p, bit_p)
-        got_q = swap(send_q, bit_q)
     return local(
         final_body,
         [shape((probe_count, cell_total), F32)],
+        keep_q,
+        got_q,
         keep_p,
         got_p,
-        keep_q,
-        got_q,
         scaling,
         name="final",
         out_specs=[whole(None)],

time: 81.3 us -> 82.1 us (level)
  starting transfers between devices: 28.4 us -> 29.8 us
  Pallas kernels: 12.9 us -> 12 us
    ppermute x31, starting transfers between devices: 28.4 us -> 29.8 us  [swap(): return lax.ppermute(array, 'tile', [(i, i ^ bits) for i in range(count)])]
    pallas_call x26 -> x25, Pallas kernels: 12.9 us -> 12 us  [local(): pl.pallas_call(run, out_shape=[a if s.memory_space is None else s.memory_...]
  transfers between devices with their start and end apart: 31 -> 31, of which waited for: 20 -> 21; matrix products, arithmetic and copies ran while one was open for 0% -> 0% of each run, Pallas kernels for 8% -> 7%
where the time goes in v11:
time: 82.1 us; the launch traced here: 81.8 us
  waiting for transfers between devices  39.9 us (49%)
  starting transfers between devices  29.8 us (36%)
  Pallas kernels  12 us (15%)
    ppermute x31, waiting for transfers between devices, swap(): return lax.ppermute(array, 'tile', [(i, i ^ bits) for i in range(count)])  39.9 us
    ppermute x31, starting transfers between devices, swap(): return lax.ppermute(array, 'tile', [(i, i ^ bits) for i in range(count)])  29.8 us
    pallas_call x25, Pallas kernels, local(): pl.pallas_call(run, out_shape=[a if s.memory_space is None else s.memory_...  12 us
  transfers between devices with their start and end apart: 31, of which 21 were waited for; matrix products, arithmetic and copies ran while one was open for 0% of the time, Pallas kernels for 7%

profile of v11, /device:TPU:0, one launch (start us, length us, event | category | flops | bytes accessed | tf_op | source)
XLA Modules:
  0.0 81.8 jit_solution(3727205914751073231)
XLA Ops:
  0.0 1.1 %scale.1 = (bf16[8,8,512]{2,1,0:T(8,128)(2,1)S(1)}, bf16[8,8,512]{2,1,0:T(8,128)(2,1)S(1)}, f32[64,128]{1,0:T(8,128)S(1)}) custom-call(f32[4]{0:T(128)} %refs_0_.2, f32[64,128]{1,0:T(8,128)} %bitcast.9, s32[64,128]{1,0:T(8,128)} %bitcast.10, f32[8,8192]{1,0:T(8,128)} %refs_3_.1), custom_call_target="tpu_custom_call" | custom-call | bytes 491536 | tf_op jit(solution)/shard_map/scale/pallas_call | solution.py:49
  1.1 4.1 %collective-permute-start.2 = (bf16[8,8,512]{2,1,0:T(8,128)(2,1)S(1)}, bf16[8,8,512]{2,1,0:T(8,128)(2,1)S(1)}, u32[]{:S(2)}, u32[]{:S(2)}) collective-permute-start(bf16[8,8,512]{2,1,0:T(8,128)(2,1)S(1)} %get-tuple-element.38.refs_0_), channel_id=1, source_target_pairs={{0,8},{1,9},{2,10},{3,11},{4,12},{5,13},{6,14},{7,15},{8,0},{9,1},... | collective-permute-start | bytes 196616 | tf_op jit(solution)/shard_map/ppermute | solution.py:34
  5.2 1.5 %collective-permute-start = (bf16[8,8,512]{2,1,0:T(8,128)(2,1)S(1)}, bf16[8,8,512]{2,1,0:T(8,128)(2,1)S(1)}, u32[]{:S(2)}, u32[]{:S(2)}) collective-permute-start(bf16[8,8,512]{2,1,0:T(8,128)(2,1)S(1)} %get-tuple-element.36.refs_0_), channel_id=1, source_target_pairs={{0,2},{1,3},{2,0},{3,1},{4,6},{5,7},{6,4},{7,5},{8,10},{9,11},{10,... | collective-permute-start | bytes 196616 | tf_op jit(solution)/shard_map/ppermute | solution.py:34
  6.7 1.5 %plan.1 = (s32[8,128]{1,0:T(8,128)S(4)}, f32[32,128]{1,0:T(8,128)S(1)}) custom-call(s32[16,128]{1,0:T(8,128)} %bitcast.11, s32[16,128]{1,0:T(8,128)} %bitcast.12, s32[16,128]{1,0:T(8,128)} %bitcast.13, s32[16,128]{1,0:T(8,128)} %bitcast.14, s32[16,128]{1,0:T(8,128)} %bitcast.15, f32[256,128]{1,0:T(8,128)} %bitcast.8, ...), custom_call_target="tpu_custom_call" | custom-call | bytes 192512 | tf_op jit(solution)/shard_map/plan/pallas_call | solution.py:49
  8.2 0.7 collective-permute-done.2.refs_1_
  8.8 1.0 %collective-permute-start.3 = (bf16[16,8,512]{2,1,0:T(8,128)(2,1)S(1)}, bf16[16,8,512]{2,1,0:T(8,128)(2,1)S(1)}, u32[]{:S(2)}, u32[]{:S(2)}) collective-permute-start(bf16[16,8,512]{2,1,0:T(8,128)(2,1)S(1)} %join.6.refs_3_.refs_0_), channel_id=1, source_target_pairs={{0,4},{1,5},{2,6},{3,7},{4,0},{5,1},{6,2},{7,3},{8,12},{9,13},{10,... | collective-permute-start | bytes 393224 | tf_op jit(solution)/shard_map/ppermute | solution.py:34
  9.9 3.1 %collective-permute-start.1 = (bf16[16,8,512]{2,1,0:T(8,128)(2,1)S(1)}, bf16[16,8,512]{2,1,0:T(8,128)(2,1)S(1)}, u32[]{:S(2)}, u32[]{:S(2)}) collective-permute-start(bf16[16,8,512]{2,1,0:T(8,128)(2,1)S(1)} %join.5.refs_2_.refs_0_), channel_id=1, source_target_pairs={{0,8},{1,9},{2,10},{3,11},{4,12},{5,13},{6,14},{7,15},{8,0},{9,1},... | collective-permute-start | bytes 393224 | tf_op jit(solution)/shard_map/ppermute | solution.py:34
  12.9 3.5 %load.1 = (bf16[128,32,512]{2,1,0:T(8,128)(2,1)S(1)}, bf16[128,32,512]{2,1,0:T(8,128)(2,1)S(1)}) custom-call(bf16[128,32,512]{2,1,0:T(8,128)(2,1)} %refs_0_.3, bf16[128,32,512]{2,1,0:T(8,128)(2,1)} %refs_1_.1, bf16[16,8,512]{2,1,0:T(8,128)(2,1)S(1)} %join.5.refs_2_.refs_0_, bf16[16,8,512]{2,1,0:T(8,128)(2,1)S(1)} %join.6.refs_3_.refs_0_), custom_call_target="tpu_custom_call" | custom-call | bytes 16777216 | tf_op jit(solution)/shard_map/load/pallas_call | solution.py:49
  16.5 1.6 %collective-permute-start.5 = (bf16[32,8,512]{2,1,0:T(8,128)(2,1)S(1)}, bf16[32,8,512]{2,1,0:T(8,128)(2,1)S(1)}, u32[]{:S(2)}, u32[]{:S(2)}) collective-permute-start(bf16[32,8,512]{2,1,0:T(8,128)(2,1)S(1)} %join.8.refs_1_.refs_4_), channel_id=1, source_target_pairs={{0,2},{1,3},{2,0},{3,1},{4,6},{5,7},{6,4},{7,5},{8,10},{9,11},{10,... | collective-permute-start | bytes 786440 | tf_op jit(solution)/shard_map/ppermute | solution.py:34
  18.0 0.8 collective-permute-done.1.refs_1_
  18.9 0.3 collective-permute-start.4
  19.2 0.5 collective-permute-start.6
  19.7 4.1 %collective-permute-done.5.refs_5_ = bf16[32,8,512]{2,1,0:T(8,128)(2,1)S(1)} collective-permute-done((bf16[32,8,512]{2,1,0:T(8,128)(2,1)S(1)}, bf16[32,8,512]{2,1,0:T(8,128)(2,1)S(1)}, u32[]{:S(2)}, u32[]{:S(2)}) %collective-permute-start.5) | collective-permute-done | bytes 262176 | tf_op jit(solution)/shard_map/ppermute | solution.py:34
  23.8 1.5 %collective-permute-done.4.refs_3_ = bf16[32,8,512]{2,1,0:T(8,128)(2,1)S(1)} collective-permute-done((bf16[32,8,512]{2,1,0:T(8,128)(2,1)S(1)}, bf16[32,8,512]{2,1,0:T(8,128)(2,1)S(1)}, u32[]{:S(2)}, u32[]{:S(2)}) %collective-permute-start.4) | collective-permute-done | bytes 262176 | tf_op jit(solution)/shard_map/ppermute | solution.py:34
  25.4 1.4 %collective-permute-done.7.refs_7_ = bf16[32,8,512]{2,1,0:T(8,128)(2,1)S(1)} collective-permute-done((bf16[32,8,512]{2,1,0:T(8,128)(2,1)S(1)}, bf16[32,8,512]{2,1,0:T(8,128)(2,1)S(1)}, u32[]{:S(2)}, u32[]{:S(2)}) %collective-permute-start.7) | collective-permute-done | bytes 262176 | tf_op jit(solution)/shard_map/ppermute | solution.py:34
  26.8 2.2 %forward.1 = (f32[64,8,512]{2,1,0:T(8,128)S(1)}, f32[8,8,512]{2,1,0:T(8,128)S(1)}, f32[8,8,512]{2,1,0:T(8,128)S(1)}, f32[8,8,512]{2,1,0:T(8,128)S(1)}, f32[8,8,512]{2,1,0:T(8,128)S(1)}) custom-call(s32[8,128]{1,0:T(8,128)S(4)} %get-tuple-element.35.refs_0_, f32[64,8,512]{2,1,0:T(8,128)S(1)} %zeros.2.refs_1_, ...), custom_call_target="tpu_custom_call", output_to_operand_aliasing={{0}: (1, {})} | custom-call | flops 536870912 | bytes 13111296 | tf_op jit(solution)/shard_map/forward/pallas_call | solution.py:49
  29.2 0.4 collective-permute-start.13
  29.7 0.4 collective-permute-start.10
  30.1 0.3 collective-permute-done.11.refs_1_
  30.5 2.1 %collective-permute-start.12 = (bf16[8,8,512]{2,1,0:T(8,128)(2,1)S(1)}, bf16[8,8,512]{2,1,0:T(8,128)(2,1)S(1)}, u32[]{:S(2)}, u32[]{:S(2)}) collective-permute-start(bf16[8,8,512]{2,1,0:T(8,128)(2,1)S(1)} %fold.11), channel_id=1, source_target_pairs={{0,6},{1,7},{2,4},{3,5},{4,2},{5,3},{6,0},{7,1},{8,14},{9,15},{10,... | collective-permute-start | bytes 196616 | tf_op jit(solution)/shard_map/ppermute | solution.py:34
  32.6 0.6 collective-permute-start.14
  33.2 1.0 %collective-permute-start.16 = (bf16[8,8,512]{2,1,0:T(8,128)(2,1)S(1)}, bf16[8,8,512]{2,1,0:T(8,128)(2,1)S(1)}, u32[]{:S(2)}, u32[]{:S(2)}) collective-permute-start(bf16[8,8,512]{2,1,0:T(8,128)(2,1)S(1)} %fold.13), channel_id=1, source_target_pairs={{0,4},{1,5},{2,6},{3,7},{4,0},{5,1},{6,2},{7,3},{8,12},{9,13},{10,... | collective-permute-start | bytes 196616 | tf_op jit(solution)/shard_map/ppermute | solution.py:34
  34.2 1.5 %collective-permute-done.12.refs_1_ = bf16[8,8,512]{2,1,0:T(8,128)(2,1)S(1)} collective-permute-done((bf16[8,8,512]{2,1,0:T(8,128)(2,1)S(1)}, bf16[8,8,512]{2,1,0:T(8,128)(2,1)S(1)}, u32[]{:S(2)}, u32[]{:S(2)}) %collective-permute-start.12) | collective-permute-done | bytes 65568 | tf_op jit(solution)/shard_map/ppermute | solution.py:34
  35.8 1.3 %collective-permute-done.14.refs_2_ = bf16[8,8,512]{2,1,0:T(8,128)(2,1)S(1)} collective-permute-done((bf16[8,8,512]{2,1,0:T(8,128)(2,1)S(1)}, bf16[8,8,512]{2,1,0:T(8,128)(2,1)S(1)}, u32[]{:S(2)}, u32[]{:S(2)}) %collective-permute-start.14) | collective-permute-done | bytes 65568 | tf_op jit(solution)/shard_map/ppermute | solution.py:34
  37.1 0.4 collective-permute-done.16.refs_3_
  37.5 2.6 %collective-permute-start.17 = (bf16[8,8,512]{2,1,0:T(8,128)(2,1)S(1)}, bf16[8,8,512]{2,1,0:T(8,128)(2,1)S(1)}, u32[]{:S(2)}, u32[]{:S(2)}) collective-permute-start(bf16[8,8,512]{2,1,0:T(8,128)(2,1)S(1)} %get-tuple-element.47), channel_id=1, source_target_pairs={{0,8},{1,9},{2,10},{3,11},{4,12},{5,13},{6,14},{7,15},{8,0},{9,1},... | collective-permute-start | bytes 196616 | tf_op jit(solution)/shard_map/ppermute | solution.py:34
  40.2 3.3 %collective-permute-done.17.refs_1_ = bf16[8,8,512]{2,1,0:T(8,128)(2,1)S(1)} collective-permute-done((bf16[8,8,512]{2,1,0:T(8,128)(2,1)S(1)}, bf16[8,8,512]{2,1,0:T(8,128)(2,1)S(1)}, u32[]{:S(2)}, u32[]{:S(2)}) %collective-permute-start.17) | collective-permute-done | bytes 65568 | tf_op jit(solution)/shard_map/ppermute | solution.py:34
  43.5 1.4 %collective-permute-start.20 = (bf16[8,8,512]{2,1,0:T(8,128)(2,1)S(1)}, bf16[8,8,512]{2,1,0:T(8,128)(2,1)S(1)}, u32[]{:S(2)}, u32[]{:S(2)}) collective-permute-start(bf16[8,8,512]{2,1,0:T(8,128)(2,1)S(1)} %weigh.1.refs_2_), channel_id=1, source_target_pairs={{0,6},{1,7},{2,4},{3,5},{4,2},{5,3},{6,0},{7,1},{8,14},{9,15},{10,... | collective-permute-start | bytes 196616 | tf_op jit(solution)/shard_map/ppermute | solution.py:34
  44.9 1.7 %collective-permute-start.19 = (bf16[8,8,512]{2,1,0:T(8,128)(2,1)S(1)}, bf16[8,8,512]{2,1,0:T(8,128)(2,1)S(1)}, u32[]{:S(2)}, u32[]{:S(2)}) collective-permute-start(bf16[8,8,512]{2,1,0:T(8,128)(2,1)S(1)} %weigh.1.refs_2_), channel_id=1, source_target_pairs={{0,4},{1,5},{2,6},{3,7},{4,0},{5,1},{6,2},{7,3},{8,12},{9,13},{10,... | collective-permute-start | bytes 196616 | tf_op jit(solution)/shard_map/ppermute | solution.py:34
  46.6 0.5 collective-permute-start.18
  47.1 1.7 %collective-permute-done.20.refs_2_ = bf16[8,8,512]{2,1,0:T(8,128)(2,1)S(1)} collective-permute-done((bf16[8,8,512]{2,1,0:T(8,128)(2,1)S(1)}, bf16[8,8,512]{2,1,0:T(8,128)(2,1)S(1)}, u32[]{:S(2)}, u32[]{:S(2)}) %collective-permute-start.20) | collective-permute-done | bytes 65568 | tf_op jit(solution)/shard_map/ppermute | solution.py:34
  48.7 0.8 collective-permute-done.19.refs_1_
  49.5 1.3 %collective-permute-done.18.refs_0_ = bf16[8,8,512]{2,1,0:T(8,128)(2,1)S(1)} collective-permute-done((bf16[8,8,512]{2,1,0:T(8,128)(2,1)S(1)}, bf16[8,8,512]{2,1,0:T(8,128)(2,1)S(1)}, u32[]{:S(2)}, u32[]{:S(2)}) %collective-permute-start.18) | collective-permute-done | bytes 65568 | tf_op jit(solution)/shard_map/ppermute | solution.py:34
  50.9 0.5 collective-permute-start.21
  51.7 0.7 collective-permute-done.21.refs_4_
  52.4 2.2 %adjoint.1 = (f32[256,8,512]{2,1,0:T(8,128)S(1)}, bf16[64,8,512]{2,1,0:T(8,128)(2,1)S(1)}, bf16[64,8,512]{2,1,0:T(8,128)(2,1)S(1)}) custom-call(s32[8,128]{1,0:T(8,128)S(4)} %get-tuple-element.35.refs_0_, f32[256,8,512]{2,1,0:T(8,128)S(1)} %zeros.3.refs_1_, bf16[8,8,512]{2,1,0:T(8,128)(2,1)S(1)} %weigh.1.refs_2_, ...), custom_call_target="tpu_custom_call", output_to_operand_aliasing={{0}: (1, {})} | custom-call | flops 536870912 | bytes 18354176 | tf_op jit(solution)/shard_map/adjoint/pallas_call | solution.py:49
  55.2 1.4 %collective-permute-done.23.refs_1_ = bf16[64,8,512]{2,1,0:T(8,128)(2,1)S(1)} collective-permute-done((bf16[64,8,512]{2,1,0:T(8,128)(2,1)S(1)}, bf16[64,8,512]{2,1,0:T(8,128)(2,1)S(1)}, u32[]{:S(2)}, u32[]{:S(2)}) %collective-permute-start.23) | collective-permute-done | bytes 524320 | tf_op jit(solution)/shard_map/ppermute | solution.py:34
  56.7 0.6 collective-permute-start.24
  57.4 0.4 collective-permute-start.28
  57.9 7.3 %collective-permute-done.24.refs_1_ = bf16[32,8,512]{2,1,0:T(8,128)(2,1)S(1)} collective-permute-done((bf16[32,8,512]{2,1,0:T(8,128)(2,1)S(1)}, bf16[32,8,512]{2,1,0:T(8,128)(2,1)S(1)}, u32[]{:S(2)}, u32[]{:S(2)}) %collective-permute-start.24) | collective-permute-done | bytes 262176 | tf_op jit(solution)/shard_map/ppermute | solution.py:34
  65.2 0.4 collective-permute-start.25
  66.0 1.9 %collective-permute-start.29 = (bf16[16,8,512]{2,1,0:T(8,128)(2,1)S(1)}, bf16[16,8,512]{2,1,0:T(8,128)(2,1)S(1)}, u32[]{:S(2)}, u32[]{:S(2)}) collective-permute-start(bf16[16,8,512]{2,1,0:T(8,128)(2,1)S(1)} %get-tuple-element.60), channel_id=1, source_target_pairs={{0,8},{1,9},{2,10},{3,11},{4,12},{5,13},{6,14},{7,15},{8,0},{9,1},... | collective-permute-start | bytes 393224 | tf_op jit(solution)/shard_map/ppermute | solution.py:34
  67.9 4.4 %collective-permute-done.25.refs_1_ = bf16[16,8,512]{2,1,0:T(8,128)(2,1)S(1)} collective-permute-done((bf16[16,8,512]{2,1,0:T(8,128)(2,1)S(1)}, bf16[16,8,512]{2,1,0:T(8,128)(2,1)S(1)}, u32[]{:S(2)}, u32[]{:S(2)}) %collective-permute-start.25) | collective-permute-done | bytes 131104 | tf_op jit(solution)/shard_map/ppermute | solution.py:34
  72.4 1.3 %collective-permute-start.26 = (bf16[8,8,512]{2,1,0:T(8,128)(2,1)S(1)}, bf16[8,8,512]{2,1,0:T(8,128)(2,1)S(1)}, u32[]{:S(2)}, u32[]{:S(2)}) collective-permute-start(bf16[8,8,512]{2,1,0:T(8,128)(2,1)S(1)} %get-tuple-element.55), channel_id=1, source_target_pairs={{0,8},{1,9},{2,10},{3,11},{4,12},{5,13},{6,14},{7,15},{8,0},{9,1},... | collective-permute-start | bytes 196616 | tf_op jit(solution)/shard_map/ppermute | solution.py:34
  73.7 3.0 %collective-permute-done.29.refs_1_ = bf16[16,8,512]{2,1,0:T(8,128)(2,1)S(1)} collective-permute-done((bf16[16,8,512]{2,1,0:T(8,128)(2,1)S(1)}, bf16[16,8,512]{2,1,0:T(8,128)(2,1)S(1)}, u32[]{:S(2)}, u32[]{:S(2)}) %collective-permute-start.29) | collective-permute-done | bytes 131104 | tf_op jit(solution)/shard_map/ppermute | solution.py:34
  76.8 0.9 %collective-permute-start.30 = (bf16[8,8,512]{2,1,0:T(8,128)(2,1)S(1)}, bf16[8,8,512]{2,1,0:T(8,128)(2,1)S(1)}, u32[]{:S(2)}, u32[]{:S(2)}) collective-permute-start(bf16[8,8,512]{2,1,0:T(8,128)(2,1)S(1)} %get-tuple-element.62), channel_id=1, source_target_pairs={{0,2},{1,3},{2,0},{3,1},{4,6},{5,7},{6,4},{7,5},{8,10},{9,11},{10,... | collective-permute-start | bytes 196616 | tf_op jit(solution)/shard_map/ppermute | solution.py:34
  77.6 3.5 %collective-permute-done.30.refs_3_ = bf16[8,8,512]{2,1,0:T(8,128)(2,1)S(1)} collective-permute-done((bf16[8,8,512]{2,1,0:T(8,128)(2,1)S(1)}, bf16[8,8,512]{2,1,0:T(8,128)(2,1)S(1)}, u32[]{:S(2)}, u32[]{:S(2)}) %collective-permute-start.30) | collective-permute-done | bytes 65568 | tf_op jit(solution)/shard_map/ppermute | solution.py:34
  81.1 0.7 final.1
  (39 shorter events, 2.2 us)
Async XLA Ops:
  1.1 7.8 %collective-permute-start.2 = (bf16[8,8,512]{2,1,0:T(8,128)(2,1)S(1)}, bf16[8,8,512]{2,1,0:T(8,128)(2,1)S(1)}, u32[]{:S(2)}, u32[]{:S(2)}) collective-permute-start(bf16[8,8,512]{2,1,0:T(8,128)(2,1)S(1)} %get-tuple-element.38.refs_0_), channel_id=1, source_target_pairs={{0,8},{1,9},{2,10},{3,11},{4,12},{5,13},{6,14},{7,15},{8,0},{9,1},... | collective-permute-start | bytes 196616 | tf_op jit(solution)/shard_map/ppermute | solution.py:34
  5.2 4.7 %collective-permute-start = (bf16[8,8,512]{2,1,0:T(8,128)(2,1)S(1)}, bf16[8,8,512]{2,1,0:T(8,128)(2,1)S(1)}, u32[]{:S(2)}, u32[]{:S(2)}) collective-permute-start(bf16[8,8,512]{2,1,0:T(8,128)(2,1)S(1)} %get-tuple-element.36.refs_0_), channel_id=1, source_target_pairs={{0,2},{1,3},{2,0},{3,1},{4,6},{5,7},{6,4},{7,5},{8,10},{9,11},{10,... | collective-permute-start | bytes 196616 | tf_op jit(solution)/shard_map/ppermute | solution.py:34
  8.8 7.6 %collective-permute-start.3 = (bf16[16,8,512]{2,1,0:T(8,128)(2,1)S(1)}, bf16[16,8,512]{2,1,0:T(8,128)(2,1)S(1)}, u32[]{:S(2)}, u32[]{:S(2)}) collective-permute-start(bf16[16,8,512]{2,1,0:T(8,128)(2,1)S(1)} %join.6.refs_3_.refs_0_), channel_id=1, source_target_pairs={{0,4},{1,5},{2,6},{3,7},{4,0},{5,1},{6,2},{7,3},{8,12},{9,13},{10,... | collective-permute-start | bytes 393224 | tf_op jit(solution)/shard_map/ppermute | solution.py:34
  9.9 9.0 %collective-permute-start.1 = (bf16[16,8,512]{2,1,0:T(8,128)(2,1)S(1)}, bf16[16,8,512]{2,1,0:T(8,128)(2,1)S(1)}, u32[]{:S(2)}, u32[]{:S(2)}) collective-permute-start(bf16[16,8,512]{2,1,0:T(8,128)(2,1)S(1)} %join.5.refs_2_.refs_0_), channel_id=1, source_target_pairs={{0,8},{1,9},{2,10},{3,11},{4,12},{5,13},{6,14},{7,15},{8,0},{9,1},... | collective-permute-start | bytes 393224 | tf_op jit(solution)/shard_map/ppermute | solution.py:34
  16.5 7.4 %collective-permute-start.5 = (bf16[32,8,512]{2,1,0:T(8,128)(2,1)S(1)}, bf16[32,8,512]{2,1,0:T(8,128)(2,1)S(1)}, u32[]{:S(2)}, u32[]{:S(2)}) collective-permute-start(bf16[32,8,512]{2,1,0:T(8,128)(2,1)S(1)} %join.8.refs_1_.refs_4_), channel_id=1, source_target_pairs={{0,2},{1,3},{2,0},{3,1},{4,6},{5,7},{6,4},{7,5},{8,10},{9,11},{10,... | collective-permute-start | bytes 786440 | tf_op jit(solution)/shard_map/ppermute | solution.py:34
  18.9 6.4 %collective-permute-start.4 = (bf16[32,8,512]{2,1,0:T(8,128)(2,1)S(1)}, bf16[32,8,512]{2,1,0:T(8,128)(2,1)S(1)}, u32[]{:S(2)}, u32[]{:S(2)}) collective-permute-start(bf16[32,8,512]{2,1,0:T(8,128)(2,1)S(1)} %join.7.refs_0_.refs_2_), channel_id=1, source_target_pairs={{0,4},{1,5},{2,6},{3,7},{4,0},{5,1},{6,2},{7,3},{8,12},{9,13},{10,... | collective-permute-start | bytes 786440 | tf_op jit(solution)/shard_map/ppermute | solution.py:34
  19.2 6.2 %collective-permute-start.8 = (bf16[32,8,512]{2,1,0:T(8,128)(2,1)S(1)}, bf16[32,8,512]{2,1,0:T(8,128)(2,1)S(1)}, u32[]{:S(2)}, u32[]{:S(2)}) collective-permute-start(bf16[32,8,512]{2,1,0:T(8,128)(2,1)S(1)} %join.8.refs_1_.refs_4_), channel_id=1, source_target_pairs={{0,1},{1,0},{2,3},{3,2},{4,5},{5,4},{6,7},{7,6},{8,9},{9,8},{10,11... | collective-permute-start | bytes 786440 | tf_op jit(solution)/shard_map/ppermute | solution.py:34
  19.2 6.2 %collective-permute-start.6 = (bf16[32,8,512]{2,1,0:T(8,128)(2,1)S(1)}, bf16[32,8,512]{2,1,0:T(8,128)(2,1)S(1)}, u32[]{:S(2)}, u32[]{:S(2)}) collective-permute-start(bf16[32,8,512]{2,1,0:T(8,128)(2,1)S(1)} %join.7.refs_0_.refs_2_), channel_id=1, source_target_pairs={{0,1},{1,0},{2,3},{3,2},{4,5},{5,4},{6,7},{7,6},{8,9},{9,8},{10,11... | collective-permute-start | bytes 786440 | tf_op jit(solution)/shard_map/ppermute | solution.py:34
  23.8 1.6 %collective-permute-start.9 = (bf16[32,8,512]{2,1,0:T(8,128)(2,1)S(1)}, bf16[32,8,512]{2,1,0:T(8,128)(2,1)S(1)}, u32[]{:S(2)}, u32[]{:S(2)}) collective-permute-start(bf16[32,8,512]{2,1,0:T(8,128)(2,1)S(1)} %collective-permute-done.5.refs_5_), channel_id=1, source_target_pairs={{0,1},{1,0},{2,3},{3,2},{4,5},{5,4},{6,7},{7,6},{8,9},{9,8},{10,11... | collective-permute-start | bytes 786440 | tf_op jit(solution)/shard_map/ppermute | solution.py:34
  25.3 1.5 %collective-permute-start.7 = (bf16[32,8,512]{2,1,0:T(8,128)(2,1)S(1)}, bf16[32,8,512]{2,1,0:T(8,128)(2,1)S(1)}, u32[]{:S(2)}, u32[]{:S(2)}) collective-permute-start(bf16[32,8,512]{2,1,0:T(8,128)(2,1)S(1)} %collective-permute-done.4.refs_3_), channel_id=1, source_target_pairs={{0,1},{1,0},{2,3},{3,2},{4,5},{5,4},{6,7},{7,6},{8,9},{9,8},{10,11... | collective-permute-start | bytes 786440 | tf_op jit(solution)/shard_map/ppermute | solution.py:34
  29.0 1.4 %collective-permute-start.11 = (f32[8,8,512]{2,1,0:T(8,128)S(1)}, f32[8,8,512]{2,1,0:T(8,128)S(1)}, u32[]{:S(2)}, u32[]{:S(2)}) collective-permute-start(f32[8,8,512]{2,1,0:T(8,128)S(1)} %get-tuple-element.43), channel_id=1, source_target_pairs={{0,1},{1,0},{2,3},{3,2},{4,5},{5,4},{6,7},{7,6},{8,9},{9,8},{10,11... | collective-permute-start | bytes 393224 | tf_op jit(solution)/shard_map/ppermute | solution.py:34
  29.2 3.3 %collective-permute-start.13 = (f32[8,8,512]{2,1,0:T(8,128)S(1)}, f32[8,8,512]{2,1,0:T(8,128)S(1)}, u32[]{:S(2)}, u32[]{:S(2)}) collective-permute-start(f32[8,8,512]{2,1,0:T(8,128)S(1)} %get-tuple-element.44), channel_id=1, source_target_pairs={{0,1},{1,0},{2,3},{3,2},{4,5},{5,4},{6,7},{7,6},{8,9},{9,8},{10,11... | collective-permute-start | bytes 393224 | tf_op jit(solution)/shard_map/ppermute | solution.py:34
  29.6 3.6 %collective-permute-start.15 = (f32[8,8,512]{2,1,0:T(8,128)S(1)}, f32[8,8,512]{2,1,0:T(8,128)S(1)}, u32[]{:S(2)}, u32[]{:S(2)}) collective-permute-start(f32[8,8,512]{2,1,0:T(8,128)S(1)} %get-tuple-element.45), channel_id=1, source_target_pairs={{0,1},{1,0},{2,3},{3,2},{4,5},{5,4},{6,7},{7,6},{8,9},{9,8},{10,11... | collective-permute-start | bytes 393224 | tf_op jit(solution)/shard_map/ppermute | solution.py:34
  29.7 4.5 %collective-permute-start.10 = (f32[8,8,512]{2,1,0:T(8,128)S(1)}, f32[8,8,512]{2,1,0:T(8,128)S(1)}, u32[]{:S(2)}, u32[]{:S(2)}) collective-permute-start(f32[8,8,512]{2,1,0:T(8,128)S(1)} %get-tuple-element.42), channel_id=1, source_target_pairs={{0,1},{1,0},{2,3},{3,2},{4,5},{5,4},{6,7},{7,6},{8,9},{9,8},{10,11... | collective-permute-start | bytes 393224 | tf_op jit(solution)/shard_map/ppermute | solution.py:34
  30.5 5.3 %collective-permute-start.12 = (bf16[8,8,512]{2,1,0:T(8,128)(2,1)S(1)}, bf16[8,8,512]{2,1,0:T(8,128)(2,1)S(1)}, u32[]{:S(2)}, u32[]{:S(2)}) collective-permute-start(bf16[8,8,512]{2,1,0:T(8,128)(2,1)S(1)} %fold.11), channel_id=1, source_target_pairs={{0,6},{1,7},{2,4},{3,5},{4,2},{5,3},{6,0},{7,1},{8,14},{9,15},{10,... | collective-permute-start | bytes 196616 | tf_op jit(solution)/shard_map/ppermute | solution.py:34
  32.6 4.5 %collective-permute-start.14 = (bf16[8,8,512]{2,1,0:T(8,128)(2,1)S(1)}, bf16[8,8,512]{2,1,0:T(8,128)(2,1)S(1)}, u32[]{:S(2)}, u32[]{:S(2)}) collective-permute-start(bf16[8,8,512]{2,1,0:T(8,128)(2,1)S(1)} %fold.12), channel_id=1, source_target_pairs={{0,2},{1,3},{2,0},{3,1},{4,6},{5,7},{6,4},{7,5},{8,10},{9,11},{10,... | collective-permute-start | bytes 196616 | tf_op jit(solution)/shard_map/ppermute | solution.py:34
  33.2 4.3 %collective-permute-start.16 = (bf16[8,8,512]{2,1,0:T(8,128)(2,1)S(1)}, bf16[8,8,512]{2,1,0:T(8,128)(2,1)S(1)}, u32[]{:S(2)}, u32[]{:S(2)}) collective-permute-start(bf16[8,8,512]{2,1,0:T(8,128)(2,1)S(1)} %fold.13), channel_id=1, source_target_pairs={{0,4},{1,5},{2,6},{3,7},{4,0},{5,1},{6,2},{7,3},{8,12},{9,13},{10,... | collective-permute-start | bytes 196616 | tf_op jit(solution)/shard_map/ppermute | solution.py:34
  37.5 5.9 %collective-permute-start.17 = (bf16[8,8,512]{2,1,0:T(8,128)(2,1)S(1)}, bf16[8,8,512]{2,1,0:T(8,128)(2,1)S(1)}, u32[]{:S(2)}, u32[]{:S(2)}) collective-permute-start(bf16[8,8,512]{2,1,0:T(8,128)(2,1)S(1)} %get-tuple-element.47), channel_id=1, source_target_pairs={{0,8},{1,9},{2,10},{3,11},{4,12},{5,13},{6,14},{7,15},{8,0},{9,1},... | collective-permute-start | bytes 196616 | tf_op jit(solution)/shard_map/ppermute | solution.py:34
  43.5 5.2 %collective-permute-start.20 = (bf16[8,8,512]{2,1,0:T(8,128)(2,1)S(1)}, bf16[8,8,512]{2,1,0:T(8,128)(2,1)S(1)}, u32[]{:S(2)}, u32[]{:S(2)}) collective-permute-start(bf16[8,8,512]{2,1,0:T(8,128)(2,1)S(1)} %weigh.1.refs_2_), channel_id=1, source_target_pairs={{0,6},{1,7},{2,4},{3,5},{4,2},{5,3},{6,0},{7,1},{8,14},{9,15},{10,... | collective-permute-start | bytes 196616 | tf_op jit(solution)/shard_map/ppermute | solution.py:34
  44.9 4.6 %collective-permute-start.19 = (bf16[8,8,512]{2,1,0:T(8,128)(2,1)S(1)}, bf16[8,8,512]{2,1,0:T(8,128)(2,1)S(1)}, u32[]{:S(2)}, u32[]{:S(2)}) collective-permute-start(bf16[8,8,512]{2,1,0:T(8,128)(2,1)S(1)} %weigh.1.refs_2_), channel_id=1, source_target_pairs={{0,4},{1,5},{2,6},{3,7},{4,0},{5,1},{6,2},{7,3},{8,12},{9,13},{10,... | collective-permute-start | bytes 196616 | tf_op jit(solution)/shard_map/ppermute | solution.py:34
  46.6 4.3 %collective-permute-start.18 = (bf16[8,8,512]{2,1,0:T(8,128)(2,1)S(1)}, bf16[8,8,512]{2,1,0:T(8,128)(2,1)S(1)}, u32[]{:S(2)}, u32[]{:S(2)}) collective-permute-start(bf16[8,8,512]{2,1,0:T(8,128)(2,1)S(1)} %weigh.1.refs_2_), channel_id=1, source_target_pairs={{0,2},{1,3},{2,0},{3,1},{4,6},{5,7},{6,4},{7,5},{8,10},{9,11},{10,... | collective-permute-start | bytes 196616 | tf_op jit(solution)/shard_map/ppermute | solution.py:34
  50.8 1.6 %collective-permute-start.22 = (bf16[24,8,512]{2,1,0:T(8,128)(2,1)S(1)}, bf16[24,8,512]{2,1,0:T(8,128)(2,1)S(1)}, u32[]{:S(2)}, u32[]{:S(2)}) collective-permute-start(bf16[24,8,512]{2,1,0:T(8,128)(2,1)S(1)} %join.9.refs_3_), channel_id=1, source_target_pairs={{0,1},{1,0},{2,3},{3,2},{4,5},{5,4},{6,7},{7,6},{8,9},{9,8},{10,11... | collective-permute-start | bytes 589832 | tf_op jit(solution)/shard_map/ppermute | solution.py:34
  50.9 1.5 %collective-permute-start.21 = (bf16[8,8,512]{2,1,0:T(8,128)(2,1)S(1)}, bf16[8,8,512]{2,1,0:T(8,128)(2,1)S(1)}, u32[]{:S(2)}, u32[]{:S(2)}) collective-permute-start(bf16[8,8,512]{2,1,0:T(8,128)(2,1)S(1)} %weigh.1.refs_2_), channel_id=1, source_target_pairs={{0,1},{1,0},{2,3},{3,2},{4,5},{5,4},{6,7},{7,6},{8,9},{9,8},{10,11... | collective-permute-start | bytes 196616 | tf_op jit(solution)/shard_map/ppermute | solution.py:34
  54.6 2.0 %collective-permute-start.23 = (bf16[64,8,512]{2,1,0:T(8,128)(2,1)S(1)}, bf16[64,8,512]{2,1,0:T(8,128)(2,1)S(1)}, u32[]{:S(2)}, u32[]{:S(2)}) collective-permute-start(bf16[64,8,512]{2,1,0:T(8,128)(2,1)S(1)} %get-tuple-element.49), channel_id=1, source_target_pairs={{0,1},{1,0},{2,3},{3,2},{4,5},{5,4},{6,7},{7,6},{8,9},{9,8},{10,11... | collective-permute-start | bytes 1572872 | tf_op jit(solution)/shard_map/ppermute | solution.py:34
  54.9 2.4 %collective-permute-start.27 = (bf16[64,8,512]{2,1,0:T(8,128)(2,1)S(1)}, bf16[64,8,512]{2,1,0:T(8,128)(2,1)S(1)}, u32[]{:S(2)}, u32[]{:S(2)}) collective-permute-start(bf16[64,8,512]{2,1,0:T(8,128)(2,1)S(1)} %get-tuple-element.56), channel_id=1, source_target_pairs={{0,1},{1,0},{2,3},{3,2},{4,5},{5,4},{6,7},{7,6},{8,9},{9,8},{10,11... | collective-permute-start | bytes 1572872 | tf_op jit(solution)/shard_map/ppermute | solution.py:34
  56.7 8.5 %collective-permute-start.24 = (bf16[32,8,512]{2,1,0:T(8,128)(2,1)S(1)}, bf16[32,8,512]{2,1,0:T(8,128)(2,1)S(1)}, u32[]{:S(2)}, u32[]{:S(2)}) collective-permute-start(bf16[32,8,512]{2,1,0:T(8,128)(2,1)S(1)} %get-tuple-element.51), channel_id=1, source_target_pairs={{0,2},{1,3},{2,0},{3,1},{4,6},{5,7},{6,4},{7,5},{8,10},{9,11},{10,... | collective-permute-start | bytes 786440 | tf_op jit(solution)/shard_map/ppermute | solution.py:34
  57.4 8.5 %collective-permute-start.28 = (bf16[32,8,512]{2,1,0:T(8,128)(2,1)S(1)}, bf16[32,8,512]{2,1,0:T(8,128)(2,1)S(1)}, u32[]{:S(2)}, u32[]{:S(2)}) collective-permute-start(bf16[32,8,512]{2,1,0:T(8,128)(2,1)S(1)} %get-tuple-element.58), channel_id=1, source_target_pairs={{0,4},{1,5},{2,6},{3,7},{4,0},{5,1},{6,2},{7,3},{8,12},{9,13},{10,... | collective-permute-start | bytes 786440 | tf_op jit(solution)/shard_map/ppermute | solution.py:34
  65.2 7.1 %collective-permute-start.25 = (bf16[16,8,512]{2,1,0:T(8,128)(2,1)S(1)}, bf16[16,8,512]{2,1,0:T(8,128)(2,1)S(1)}, u32[]{:S(2)}, u32[]{:S(2)}) collective-permute-start(bf16[16,8,512]{2,1,0:T(8,128)(2,1)S(1)} %get-tuple-element.53), channel_id=1, source_target_pairs={{0,4},{1,5},{2,6},{3,7},{4,0},{5,1},{6,2},{7,3},{8,12},{9,13},{10,... | collective-permute-start | bytes 393224 | tf_op jit(solution)/shard_map/ppermute | solution.py:34
  66.0 10.7 %collective-permute-start.29 = (bf16[16,8,512]{2,1,0:T(8,128)(2,1)S(1)}, bf16[16,8,512]{2,1,0:T(8,128)(2,1)S(1)}, u32[]{:S(2)}, u32[]{:S(2)}) collective-permute-start(bf16[16,8,512]{2,1,0:T(8,128)(2,1)S(1)} %get-tuple-element.60), channel_id=1, source_target_pairs={{0,8},{1,9},{2,10},{3,11},{4,12},{5,13},{6,14},{7,15},{8,0},{9,1},... | collective-permute-start | bytes 393224 | tf_op jit(solution)/shard_map/ppermute | solution.py:34
  72.4 5.3 %collective-permute-start.26 = (bf16[8,8,512]{2,1,0:T(8,128)(2,1)S(1)}, bf16[8,8,512]{2,1,0:T(8,128)(2,1)S(1)}, u32[]{:S(2)}, u32[]{:S(2)}) collective-permute-start(bf16[8,8,512]{2,1,0:T(8,128)(2,1)S(1)} %get-tuple-element.55), channel_id=1, source_target_pairs={{0,8},{1,9},{2,10},{3,11},{4,12},{5,13},{6,14},{7,15},{8,0},{9,1},... | collective-permute-start | bytes 196616 | tf_op jit(solution)/shard_map/ppermute | solution.py:34
  76.8 4.3 %collective-permute-start.30 = (bf16[8,8,512]{2,1,0:T(8,128)(2,1)S(1)}, bf16[8,8,512]{2,1,0:T(8,128)(2,1)S(1)}, u32[]{:S(2)}, u32[]{:S(2)}) collective-permute-start(bf16[8,8,512]{2,1,0:T(8,128)(2,1)S(1)} %get-tuple-element.62), channel_id=1, source_target_pairs={{0,2},{1,3},{2,0},{3,1},{4,6},{5,7},{6,4},{7,5},{8,10},{9,11},{10,... | collective-permute-start | bytes 196616 | tf_op jit(solution)/shard_map/ppermute | solution.py:34

commit v12 on v11

--- a/solution.py
+++ b/solution.py
@@ -352,17 +352,21 @@
         (scaling,),
     )
     steps = list(zip(*orders))
-    after = (weight,)
+    early = swap(part_p, steps[1][0])
     for step, (bit_p, bit_q) in enumerate(steps):
-        got_p = swap(part_p, bit_p)
         got_q = swap(part_q, bit_q)
         if step == 1:
-            v_here, u_here = load((v_factor, u_factor), (part_p, part_q))
-            after = (u_here,)
-        if step < len(steps) - 1:
-            part_p = join(part_p, got_p, after=after)
+            parts_p = (part_p, got_p, early, swap(got_p, bit_p))
+            v_here, u_here = load((v_factor, u_factor), (part_q,))
+            part_p = join(*parts_p, after=(u_here,))
+        else:
+            got_p = swap(part_p, bit_p)
+        if step == 0:
+            part_q = join(part_q, got_q, after=(weight,))
+        elif step < len(steps) - 1:
             part_q = join(part_q, got_q)
-            after = ()
+            if step > 1:
+                part_p = join(part_p, got_p)
     pieces = [part_p, got_p, part_q, got_q]
     pieces = pieces + [swap(piece, 1) for piece in pieces]
 

time: 82.1 us -> 84.7 us (1.032)
  waiting for transfers between devices: 39.9 us -> 46.8 us
  starting transfers between devices: 29.8 us -> 25.5 us
    ppermute x31 -> x32, waiting for transfers between devices: 39.9 us -> 46.8 us  [swap(): return lax.ppermute(array, 'tile', [(i, i ^ bits) for i in range(count)])]
    ppermute x31 -> x32, starting transfers between devices: 29.8 us -> 25.5 us  [swap(): return lax.ppermute(array, 'tile', [(i, i ^ bits) for i in range(count)])]
    pallas_call x25 -> x24, Pallas kernels: 12 us -> 11.9 us  [local(): pl.pallas_call(run, out_shape=[a if s.memory_space is None else s.memory_...]
  transfers between devices with their start and end apart: 31 -> 32, of which waited for: 21 -> 22; matrix products, arithmetic and copies ran while one was open for 0% -> 0% of each run, Pallas kernels for 7% -> 7%
where the time goes in v12:
time: 84.7 us; the launch traced here: 84.4 us
  waiting for transfers between devices  46.8 us (55%)
  starting transfers between devices  25.5 us (30%)
  Pallas kernels  11.9 us (14%)
    ppermute x32, waiting for transfers between devices, swap(): return lax.ppermute(array, 'tile', [(i, i ^ bits) for i in range(count)])  46.8 us
    ppermute x32, starting transfers between devices, swap(): return lax.ppermute(array, 'tile', [(i, i ^ bits) for i in range(count)])  25.5 us
    pallas_call x24, Pallas kernels, local(): pl.pallas_call(run, out_shape=[a if s.memory_space is None else s.memory_...  11.9 us
  transfers between devices with their start and end apart: 32, of which 22 were waited for; matrix products, arithmetic and copies ran while one was open for 0% of the time, Pallas kernels for 7%

profile of v12, /device:TPU:0, one launch (start us, length us, event | category | flops | bytes accessed | tf_op | source)
XLA Modules:
  0.0 84.4 jit_solution(403718342708476022)
XLA Ops:
  0.0 1.1 %scale.1 = (bf16[8,8,512]{2,1,0:T(8,128)(2,1)S(1)}, bf16[8,8,512]{2,1,0:T(8,128)(2,1)S(1)}, f32[64,128]{1,0:T(8,128)S(1)}) custom-call(f32[4]{0:T(128)} %refs_0_.2, f32[64,128]{1,0:T(8,128)} %bitcast.9, s32[64,128]{1,0:T(8,128)} %bitcast.10, f32[8,8192]{1,0:T(8,128)} %refs_3_.1), custom_call_target="tpu_custom_call" | custom-call | bytes 491536 | tf_op jit(solution)/shard_map/scale/pallas_call | solution.py:49
  1.1 4.1 %collective-permute-start.3 = (bf16[8,8,512]{2,1,0:T(8,128)(2,1)S(1)}, bf16[8,8,512]{2,1,0:T(8,128)(2,1)S(1)}, u32[]{:S(2)}, u32[]{:S(2)}) collective-permute-start(bf16[8,8,512]{2,1,0:T(8,128)(2,1)S(1)} %get-tuple-element.37.refs_0_), channel_id=1, source_target_pairs={{0,8},{1,9},{2,10},{3,11},{4,12},{5,13},{6,14},{7,15},{8,0},{9,1},... | collective-permute-start | bytes 196616 | tf_op jit(solution)/shard_map/ppermute | solution.py:34
  5.2 1.5 %collective-permute-start = (bf16[8,8,512]{2,1,0:T(8,128)(2,1)S(1)}, bf16[8,8,512]{2,1,0:T(8,128)(2,1)S(1)}, u32[]{:S(2)}, u32[]{:S(2)}) collective-permute-start(bf16[8,8,512]{2,1,0:T(8,128)(2,1)S(1)} %get-tuple-element.36.refs_0_), channel_id=1, source_target_pairs={{0,2},{1,3},{2,0},{3,1},{4,6},{5,7},{6,4},{7,5},{8,10},{9,11},{10,... | collective-permute-start | bytes 196616 | tf_op jit(solution)/shard_map/ppermute | solution.py:34
  6.7 1.5 %plan.1 = (s32[8,128]{1,0:T(8,128)S(4)}, f32[32,128]{1,0:T(8,128)S(1)}) custom-call(s32[16,128]{1,0:T(8,128)} %bitcast.11, s32[16,128]{1,0:T(8,128)} %bitcast.12, s32[16,128]{1,0:T(8,128)} %bitcast.13, s32[16,128]{1,0:T(8,128)} %bitcast.14, s32[16,128]{1,0:T(8,128)} %bitcast.15, f32[256,128]{1,0:T(8,128)} %bitcast.8, ...), custom_call_target="tpu_custom_call" | custom-call | bytes 192512 | tf_op jit(solution)/shard_map/plan/pallas_call | solution.py:49
  8.2 0.7 collective-permute-done.3.refs_1_
  8.8 1.0 %collective-permute-start.4 = (bf16[16,8,512]{2,1,0:T(8,128)(2,1)S(1)}, bf16[16,8,512]{2,1,0:T(8,128)(2,1)S(1)}, u32[]{:S(2)}, u32[]{:S(2)}) collective-permute-start(bf16[16,8,512]{2,1,0:T(8,128)(2,1)S(1)} %join.4.refs_2_.refs_0_), channel_id=1, source_target_pairs={{0,4},{1,5},{2,6},{3,7},{4,0},{5,1},{6,2},{7,3},{8,12},{9,13},{10,... | collective-permute-start | bytes 393224 | tf_op jit(solution)/shard_map/ppermute | solution.py:34
  9.9 3.0 %collective-permute-start.1 = (bf16[8,8,512]{2,1,0:T(8,128)(2,1)S(1)}, bf16[8,8,512]{2,1,0:T(8,128)(2,1)S(1)}, u32[]{:S(2)}, u32[]{:S(2)}) collective-permute-start(bf16[8,8,512]{2,1,0:T(8,128)(2,1)S(1)} %get-tuple-element.36.refs_0_), channel_id=1, source_target_pairs={{0,8},{1,9},{2,10},{3,11},{4,12},{5,13},{6,14},{7,15},{8,0},{9,1},... | collective-permute-start | bytes 196616 | tf_op jit(solution)/shard_map/ppermute | solution.py:34
  12.9 3.5 %load.1 = (bf16[128,32,512]{2,1,0:T(8,128)(2,1)S(1)}, bf16[128,32,512]{2,1,0:T(8,128)(2,1)S(1)}) custom-call(bf16[128,32,512]{2,1,0:T(8,128)(2,1)} %refs_0_.3, bf16[128,32,512]{2,1,0:T(8,128)(2,1)} %refs_1_.1, bf16[16,8,512]{2,1,0:T(8,128)(2,1)S(1)} %join.4.refs_2_.refs_0_), custom_call_target="tpu_custom_call" | custom-call | bytes 16777216 | tf_op jit(solution)/shard_map/load/pallas_call | solution.py:49
  16.4 2.9 %collective-permute-done.2.refs_3_ = bf16[8,8,512]{2,1,0:T(8,128)(2,1)S(1)} collective-permute-done((bf16[8,8,512]{2,1,0:T(8,128)(2,1)S(1)}, bf16[8,8,512]{2,1,0:T(8,128)(2,1)S(1)}, u32[]{:S(2)}, u32[]{:S(2)}) %collective-permute-start.2) | collective-permute-done | bytes 65568 | tf_op jit(solution)/shard_map/ppermute | solution.py:34
  19.5 1.6 %collective-permute-start.6 = (bf16[32,8,512]{2,1,0:T(8,128)(2,1)S(1)}, bf16[32,8,512]{2,1,0:T(8,128)(2,1)S(1)}, u32[]{:S(2)}, u32[]{:S(2)}) collective-permute-start(bf16[32,8,512]{2,1,0:T(8,128)(2,1)S(1)} %join.6.refs_1_.refs_4_), channel_id=1, source_target_pairs={{0,2},{1,3},{2,0},{3,1},{4,6},{5,7},{6,4},{7,5},{8,10},{9,11},{10,... | collective-permute-start | bytes 786440 | tf_op jit(solution)/shard_map/ppermute | solution.py:34
  21.0 0.5 collective-permute-start.9
  21.5 5.5 %collective-permute-done.5.refs_3_ = bf16[32,8,512]{2,1,0:T(8,128)(2,1)S(1)} collective-permute-done((bf16[32,8,512]{2,1,0:T(8,128)(2,1)S(1)}, bf16[32,8,512]{2,1,0:T(8,128)(2,1)S(1)}, u32[]{:S(2)}, u32[]{:S(2)}) %collective-permute-start.5) | collective-permute-done | bytes 262176 | tf_op jit(solution)/shard_map/ppermute | solution.py:34
  27.2 0.4 collective-permute-start.10
  27.6 0.9 %collective-permute-done.8.refs_7_ = bf16[32,8,512]{2,1,0:T(8,128)(2,1)S(1)} collective-permute-done((bf16[32,8,512]{2,1,0:T(8,128)(2,1)S(1)}, bf16[32,8,512]{2,1,0:T(8,128)(2,1)S(1)}, u32[]{:S(2)}, u32[]{:S(2)}) %collective-permute-start.8) | collective-permute-done | bytes 262176 | tf_op jit(solution)/shard_map/ppermute | solution.py:34
  28.6 0.4 collective-permute-done.10.refs_9_
  28.9 2.2 %forward.1 = (f32[64,8,512]{2,1,0:T(8,128)S(1)}, f32[8,8,512]{2,1,0:T(8,128)S(1)}, f32[8,8,512]{2,1,0:T(8,128)S(1)}, f32[8,8,512]{2,1,0:T(8,128)S(1)}, f32[8,8,512]{2,1,0:T(8,128)S(1)}) custom-call(s32[8,128]{1,0:T(8,128)S(4)} %get-tuple-element.35.refs_0_, f32[64,8,512]{2,1,0:T(8,128)S(1)} %zeros.2.refs_1_, ...), custom_call_target="tpu_custom_call", output_to_operand_aliasing={{0}: (1, {})} | custom-call | flops 536870912 | bytes 13111296 | tf_op jit(solution)/shard_map/forward/pallas_call | solution.py:49
  31.3 0.4 collective-permute-start.14
  31.9 0.4 collective-permute-start.11
  32.2 0.3 collective-permute-done.12.refs_1_
  32.6 2.5 %collective-permute-start.13 = (bf16[8,8,512]{2,1,0:T(8,128)(2,1)S(1)}, bf16[8,8,512]{2,1,0:T(8,128)(2,1)S(1)}, u32[]{:S(2)}, u32[]{:S(2)}) collective-permute-start(bf16[8,8,512]{2,1,0:T(8,128)(2,1)S(1)} %fold.11), channel_id=1, source_target_pairs={{0,6},{1,7},{2,4},{3,5},{4,2},{5,3},{6,0},{7,1},{8,14},{9,15},{10,... | collective-permute-start | bytes 196616 | tf_op jit(solution)/shard_map/ppermute | solution.py:34
  35.1 0.6 collective-permute-start.15
  35.7 0.6 collective-permute-start.17
  36.3 1.5 %collective-permute-done.13.refs_1_ = bf16[8,8,512]{2,1,0:T(8,128)(2,1)S(1)} collective-permute-done((bf16[8,8,512]{2,1,0:T(8,128)(2,1)S(1)}, bf16[8,8,512]{2,1,0:T(8,128)(2,1)S(1)}, u32[]{:S(2)}, u32[]{:S(2)}) %collective-permute-start.13) | collective-permute-done | bytes 65568 | tf_op jit(solution)/shard_map/ppermute | solution.py:34
  37.8 1.6 %collective-permute-done.15.refs_2_ = bf16[8,8,512]{2,1,0:T(8,128)(2,1)S(1)} collective-permute-done((bf16[8,8,512]{2,1,0:T(8,128)(2,1)S(1)}, bf16[8,8,512]{2,1,0:T(8,128)(2,1)S(1)}, u32[]{:S(2)}, u32[]{:S(2)}) %collective-permute-start.15) | collective-permute-done | bytes 65568 | tf_op jit(solution)/shard_map/ppermute | solution.py:34
  39.4 0.6 collective-permute-done.17.refs_3_
  40.0 0.6 collective-permute-start.18
  40.7 5.3 %collective-permute-done.18.refs_1_ = bf16[8,8,512]{2,1,0:T(8,128)(2,1)S(1)} collective-permute-done((bf16[8,8,512]{2,1,0:T(8,128)(2,1)S(1)}, bf16[8,8,512]{2,1,0:T(8,128)(2,1)S(1)}, u32[]{:S(2)}, u32[]{:S(2)}) %collective-permute-start.18) | collective-permute-done | bytes 65568 | tf_op jit(solution)/shard_map/ppermute | solution.py:34
  46.0 0.9 %collective-permute-start.21 = (bf16[8,8,512]{2,1,0:T(8,128)(2,1)S(1)}, bf16[8,8,512]{2,1,0:T(8,128)(2,1)S(1)}, u32[]{:S(2)}, u32[]{:S(2)}) collective-permute-start(bf16[8,8,512]{2,1,0:T(8,128)(2,1)S(1)} %weigh.1.refs_2_), channel_id=1, source_target_pairs={{0,6},{1,7},{2,4},{3,5},{4,2},{5,3},{6,0},{7,1},{8,14},{9,15},{10,... | collective-permute-start | bytes 196616 | tf_op jit(solution)/shard_map/ppermute | solution.py:34
  46.9 2.2 %collective-permute-start.20 = (bf16[8,8,512]{2,1,0:T(8,128)(2,1)S(1)}, bf16[8,8,512]{2,1,0:T(8,128)(2,1)S(1)}, u32[]{:S(2)}, u32[]{:S(2)}) collective-permute-start(bf16[8,8,512]{2,1,0:T(8,128)(2,1)S(1)} %weigh.1.refs_2_), channel_id=1, source_target_pairs={{0,4},{1,5},{2,6},{3,7},{4,0},{5,1},{6,2},{7,3},{8,12},{9,13},{10,... | collective-permute-start | bytes 196616 | tf_op jit(solution)/shard_map/ppermute | solution.py:34
  49.1 0.4 collective-permute-start.19
  49.6 1.7 %collective-permute-done.21.refs_2_ = bf16[8,8,512]{2,1,0:T(8,128)(2,1)S(1)} collective-permute-done((bf16[8,8,512]{2,1,0:T(8,128)(2,1)S(1)}, bf16[8,8,512]{2,1,0:T(8,128)(2,1)S(1)}, u32[]{:S(2)}, u32[]{:S(2)}) %collective-permute-start.21) | collective-permute-done | bytes 65568 | tf_op jit(solution)/shard_map/ppermute | solution.py:34
  51.2 0.9 %collective-permute-done.20.refs_1_ = bf16[8,8,512]{2,1,0:T(8,128)(2,1)S(1)} collective-permute-done((bf16[8,8,512]{2,1,0:T(8,128)(2,1)S(1)}, bf16[8,8,512]{2,1,0:T(8,128)(2,1)S(1)}, u32[]{:S(2)}, u32[]{:S(2)}) %collective-permute-start.20) | collective-permute-done | bytes 65568 | tf_op jit(solution)/shard_map/ppermute | solution.py:34
  52.1 1.3 %collective-permute-done.19.refs_0_ = bf16[8,8,512]{2,1,0:T(8,128)(2,1)S(1)} collective-permute-done((bf16[8,8,512]{2,1,0:T(8,128)(2,1)S(1)}, bf16[8,8,512]{2,1,0:T(8,128)(2,1)S(1)}, u32[]{:S(2)}, u32[]{:S(2)}) %collective-permute-start.19) | collective-permute-done | bytes 65568 | tf_op jit(solution)/shard_map/ppermute | solution.py:34
  53.5 0.5 collective-permute-start.22
  54.3 0.7 collective-permute-done.22.refs_4_
  55.0 2.2 %adjoint.1 = (f32[256,8,512]{2,1,0:T(8,128)S(1)}, bf16[64,8,512]{2,1,0:T(8,128)(2,1)S(1)}, bf16[64,8,512]{2,1,0:T(8,128)(2,1)S(1)}) custom-call(s32[8,128]{1,0:T(8,128)S(4)} %get-tuple-element.35.refs_0_, f32[256,8,512]{2,1,0:T(8,128)S(1)} %zeros.3.refs_1_, bf16[8,8,512]{2,1,0:T(8,128)(2,1)S(1)} %weigh.1.refs_2_, ...), custom_call_target="tpu_custom_call", output_to_operand_aliasing={{0}: (1, {})} | custom-call | flops 536870912 | bytes 18354176 | tf_op jit(solution)/shard_map/adjoint/pallas_call | solution.py:49
  57.2 0.3 collective-permute-start.24
  57.8 1.4 %collective-permute-done.24.refs_1_ = bf16[64,8,512]{2,1,0:T(8,128)(2,1)S(1)} collective-permute-done((bf16[64,8,512]{2,1,0:T(8,128)(2,1)S(1)}, bf16[64,8,512]{2,1,0:T(8,128)(2,1)S(1)}, u32[]{:S(2)}, u32[]{:S(2)}) %collective-permute-start.24) | collective-permute-done | bytes 524320 | tf_op jit(solution)/shard_map/ppermute | solution.py:34
  59.3 0.5 collective-permute-start.25
  60.1 7.6 %collective-permute-done.25.refs_1_ = bf16[32,8,512]{2,1,0:T(8,128)(2,1)S(1)} collective-permute-done((bf16[32,8,512]{2,1,0:T(8,128)(2,1)S(1)}, bf16[32,8,512]{2,1,0:T(8,128)(2,1)S(1)}, u32[]{:S(2)}, u32[]{:S(2)}) %collective-permute-start.25) | collective-permute-done | bytes 262176 | tf_op jit(solution)/shard_map/ppermute | solution.py:34
  67.9 0.6 collective-permute-done.29.refs_1_
  68.6 1.3 %collective-permute-start.30 = (bf16[16,8,512]{2,1,0:T(8,128)(2,1)S(1)}, bf16[16,8,512]{2,1,0:T(8,128)(2,1)S(1)}, u32[]{:S(2)}, u32[]{:S(2)}) collective-permute-start(bf16[16,8,512]{2,1,0:T(8,128)(2,1)S(1)} %get-tuple-element.60), channel_id=1, source_target_pairs={{0,8},{1,9},{2,10},{3,11},{4,12},{5,13},{6,14},{7,15},{8,0},{9,1},... | collective-permute-start | bytes 393224 | tf_op jit(solution)/shard_map/ppermute | solution.py:34
  69.9 3.8 %collective-permute-done.26.refs_1_ = bf16[16,8,512]{2,1,0:T(8,128)(2,1)S(1)} collective-permute-done((bf16[16,8,512]{2,1,0:T(8,128)(2,1)S(1)}, bf16[16,8,512]{2,1,0:T(8,128)(2,1)S(1)}, u32[]{:S(2)}, u32[]{:S(2)}) %collective-permute-start.26) | collective-permute-done | bytes 131104 | tf_op jit(solution)/shard_map/ppermute | solution.py:34
  73.7 0.4 collective-permute-start.27
  74.1 5.1 %collective-permute-done.30.refs_1_ = bf16[16,8,512]{2,1,0:T(8,128)(2,1)S(1)} collective-permute-done((bf16[16,8,512]{2,1,0:T(8,128)(2,1)S(1)}, bf16[16,8,512]{2,1,0:T(8,128)(2,1)S(1)}, u32[]{:S(2)}, u32[]{:S(2)}) %collective-permute-start.30) | collective-permute-done | bytes 131104 | tf_op jit(solution)/shard_map/ppermute | solution.py:34
  79.3 0.8 collective-permute-start.31
  80.1 3.6 %collective-permute-done.31.refs_3_ = bf16[8,8,512]{2,1,0:T(8,128)(2,1)S(1)} collective-permute-done((bf16[8,8,512]{2,1,0:T(8,128)(2,1)S(1)}, bf16[8,8,512]{2,1,0:T(8,128)(2,1)S(1)}, u32[]{:S(2)}, u32[]{:S(2)}) %collective-permute-start.31) | collective-permute-done | bytes 65568 | tf_op jit(solution)/shard_map/ppermute | solution.py:34
  83.6 0.7 final.1
  (40 shorter events, 2.1 us)
Async XLA Ops:
  1.1 7.8 %collective-permute-start.3 = (bf16[8,8,512]{2,1,0:T(8,128)(2,1)S(1)}, bf16[8,8,512]{2,1,0:T(8,128)(2,1)S(1)}, u32[]{:S(2)}, u32[]{:S(2)}) collective-permute-start(bf16[8,8,512]{2,1,0:T(8,128)(2,1)S(1)} %get-tuple-element.37.refs_0_), channel_id=1, source_target_pairs={{0,8},{1,9},{2,10},{3,11},{4,12},{5,13},{6,14},{7,15},{8,0},{9,1},... | collective-permute-start | bytes 196616 | tf_op jit(solution)/shard_map/ppermute | solution.py:34
  5.2 7.7 %collective-permute-start = (bf16[8,8,512]{2,1,0:T(8,128)(2,1)S(1)}, bf16[8,8,512]{2,1,0:T(8,128)(2,1)S(1)}, u32[]{:S(2)}, u32[]{:S(2)}) collective-permute-start(bf16[8,8,512]{2,1,0:T(8,128)(2,1)S(1)} %get-tuple-element.36.refs_0_), channel_id=1, source_target_pairs={{0,2},{1,3},{2,0},{3,1},{4,6},{5,7},{6,4},{7,5},{8,10},{9,11},{10,... | collective-permute-start | bytes 196616 | tf_op jit(solution)/shard_map/ppermute | solution.py:34
  8.8 10.6 %collective-permute-start.4 = (bf16[16,8,512]{2,1,0:T(8,128)(2,1)S(1)}, bf16[16,8,512]{2,1,0:T(8,128)(2,1)S(1)}, u32[]{:S(2)}, u32[]{:S(2)}) collective-permute-start(bf16[16,8,512]{2,1,0:T(8,128)(2,1)S(1)} %join.4.refs_2_.refs_0_), channel_id=1, source_target_pairs={{0,4},{1,5},{2,6},{3,7},{4,0},{5,1},{6,2},{7,3},{8,12},{9,13},{10,... | collective-permute-start | bytes 393224 | tf_op jit(solution)/shard_map/ppermute | solution.py:34
  9.9 6.5 %collective-permute-start.1 = (bf16[8,8,512]{2,1,0:T(8,128)(2,1)S(1)}, bf16[8,8,512]{2,1,0:T(8,128)(2,1)S(1)}, u32[]{:S(2)}, u32[]{:S(2)}) collective-permute-start(bf16[8,8,512]{2,1,0:T(8,128)(2,1)S(1)} %get-tuple-element.36.refs_0_), channel_id=1, source_target_pairs={{0,8},{1,9},{2,10},{3,11},{4,12},{5,13},{6,14},{7,15},{8,0},{9,1},... | collective-permute-start | bytes 196616 | tf_op jit(solution)/shard_map/ppermute | solution.py:34
  12.9 6.5 %collective-permute-start.2 = (bf16[8,8,512]{2,1,0:T(8,128)(2,1)S(1)}, bf16[8,8,512]{2,1,0:T(8,128)(2,1)S(1)}, u32[]{:S(2)}, u32[]{:S(2)}) collective-permute-start(bf16[8,8,512]{2,1,0:T(8,128)(2,1)S(1)} %collective-permute-done.refs_1_), channel_id=1, source_target_pairs={{0,8},{1,9},{2,10},{3,11},{4,12},{5,13},{6,14},{7,15},{8,0},{9,1},... | collective-permute-start | bytes 196616 | tf_op jit(solution)/shard_map/ppermute | solution.py:34
  19.3 7.7 %collective-permute-start.5 = (bf16[32,8,512]{2,1,0:T(8,128)(2,1)S(1)}, bf16[32,8,512]{2,1,0:T(8,128)(2,1)S(1)}, u32[]{:S(2)}, u32[]{:S(2)}) collective-permute-start(bf16[32,8,512]{2,1,0:T(8,128)(2,1)S(1)} %join.5.refs_0_.refs_2_), channel_id=1, source_target_pairs={{0,4},{1,5},{2,6},{3,7},{4,0},{5,1},{6,2},{7,3},{8,12},{9,13},{10,... | collective-permute-start | bytes 786440 | tf_op jit(solution)/shard_map/ppermute | solution.py:34
  19.5 7.7 %collective-permute-start.6 = (bf16[32,8,512]{2,1,0:T(8,128)(2,1)S(1)}, bf16[32,8,512]{2,1,0:T(8,128)(2,1)S(1)}, u32[]{:S(2)}, u32[]{:S(2)}) collective-permute-start(bf16[32,8,512]{2,1,0:T(8,128)(2,1)S(1)} %join.6.refs_1_.refs_4_), channel_id=1, source_target_pairs={{0,2},{1,3},{2,0},{3,1},{4,6},{5,7},{6,4},{7,5},{8,10},{9,11},{10,... | collective-permute-start | bytes 786440 | tf_op jit(solution)/shard_map/ppermute | solution.py:34
  21.0 6.6 %collective-permute-start.7 = (bf16[32,8,512]{2,1,0:T(8,128)(2,1)S(1)}, bf16[32,8,512]{2,1,0:T(8,128)(2,1)S(1)}, u32[]{:S(2)}, u32[]{:S(2)}) collective-permute-start(bf16[32,8,512]{2,1,0:T(8,128)(2,1)S(1)} %join.5.refs_0_.refs_2_), channel_id=1, source_target_pairs={{0,1},{1,0},{2,3},{3,2},{4,5},{5,4},{6,7},{7,6},{8,9},{9,8},{10,11... | collective-permute-start | bytes 786440 | tf_op jit(solution)/shard_map/ppermute | solution.py:34
  21.0 6.6 %collective-permute-start.9 = (bf16[32,8,512]{2,1,0:T(8,128)(2,1)S(1)}, bf16[32,8,512]{2,1,0:T(8,128)(2,1)S(1)}, u32[]{:S(2)}, u32[]{:S(2)}) collective-permute-start(bf16[32,8,512]{2,1,0:T(8,128)(2,1)S(1)} %join.6.refs_1_.refs_4_), channel_id=1, source_target_pairs={{0,1},{1,0},{2,3},{3,2},{4,5},{5,4},{6,7},{7,6},{8,9},{9,8},{10,11... | collective-permute-start | bytes 786440 | tf_op jit(solution)/shard_map/ppermute | solution.py:34
  27.0 1.5 %collective-permute-start.8 = (bf16[32,8,512]{2,1,0:T(8,128)(2,1)S(1)}, bf16[32,8,512]{2,1,0:T(8,128)(2,1)S(1)}, u32[]{:S(2)}, u32[]{:S(2)}) collective-permute-start(bf16[32,8,512]{2,1,0:T(8,128)(2,1)S(1)} %collective-permute-done.5.refs_3_), channel_id=1, source_target_pairs={{0,1},{1,0},{2,3},{3,2},{4,5},{5,4},{6,7},{7,6},{8,9},{9,8},{10,11... | collective-permute-start | bytes 786440 | tf_op jit(solution)/shard_map/ppermute | solution.py:34
  27.2 1.8 %collective-permute-start.10 = (bf16[32,8,512]{2,1,0:T(8,128)(2,1)S(1)}, bf16[32,8,512]{2,1,0:T(8,128)(2,1)S(1)}, u32[]{:S(2)}, u32[]{:S(2)}) collective-permute-start(bf16[32,8,512]{2,1,0:T(8,128)(2,1)S(1)} %collective-permute-done.6.refs_5_), channel_id=1, source_target_pairs={{0,1},{1,0},{2,3},{3,2},{4,5},{5,4},{6,7},{7,6},{8,9},{9,8},{10,11... | collective-permute-start | bytes 786440 | tf_op jit(solution)/shard_map/ppermute | solution.py:34
  31.1 1.4 %collective-permute-start.12 = (f32[8,8,512]{2,1,0:T(8,128)S(1)}, f32[8,8,512]{2,1,0:T(8,128)S(1)}, u32[]{:S(2)}, u32[]{:S(2)}) collective-permute-start(f32[8,8,512]{2,1,0:T(8,128)S(1)} %get-tuple-element.43), channel_id=1, source_target_pairs={{0,1},{1,0},{2,3},{3,2},{4,5},{5,4},{6,7},{7,6},{8,9},{9,8},{10,11... | collective-permute-start | bytes 393224 | tf_op jit(solution)/shard_map/ppermute | solution.py:34
  31.3 3.7 %collective-permute-start.14 = (f32[8,8,512]{2,1,0:T(8,128)S(1)}, f32[8,8,512]{2,1,0:T(8,128)S(1)}, u32[]{:S(2)}, u32[]{:S(2)}) collective-permute-start(f32[8,8,512]{2,1,0:T(8,128)S(1)} %get-tuple-element.44), channel_id=1, source_target_pairs={{0,1},{1,0},{2,3},{3,2},{4,5},{5,4},{6,7},{7,6},{8,9},{9,8},{10,11... | collective-permute-start | bytes 393224 | tf_op jit(solution)/shard_map/ppermute | solution.py:34
  31.7 3.9 %collective-permute-start.16 = (f32[8,8,512]{2,1,0:T(8,128)S(1)}, f32[8,8,512]{2,1,0:T(8,128)S(1)}, u32[]{:S(2)}, u32[]{:S(2)}) collective-permute-start(f32[8,8,512]{2,1,0:T(8,128)S(1)} %get-tuple-element.45), channel_id=1, source_target_pairs={{0,1},{1,0},{2,3},{3,2},{4,5},{5,4},{6,7},{7,6},{8,9},{9,8},{10,11... | collective-permute-start | bytes 393224 | tf_op jit(solution)/shard_map/ppermute | solution.py:34
  31.9 4.4 %collective-permute-start.11 = (f32[8,8,512]{2,1,0:T(8,128)S(1)}, f32[8,8,512]{2,1,0:T(8,128)S(1)}, u32[]{:S(2)}, u32[]{:S(2)}) collective-permute-start(f32[8,8,512]{2,1,0:T(8,128)S(1)} %get-tuple-element.42), channel_id=1, source_target_pairs={{0,1},{1,0},{2,3},{3,2},{4,5},{5,4},{6,7},{7,6},{8,9},{9,8},{10,11... | collective-permute-start | bytes 393224 | tf_op jit(solution)/shard_map/ppermute | solution.py:34
  32.6 5.2 %collective-permute-start.13 = (bf16[8,8,512]{2,1,0:T(8,128)(2,1)S(1)}, bf16[8,8,512]{2,1,0:T(8,128)(2,1)S(1)}, u32[]{:S(2)}, u32[]{:S(2)}) collective-permute-start(bf16[8,8,512]{2,1,0:T(8,128)(2,1)S(1)} %fold.11), channel_id=1, source_target_pairs={{0,6},{1,7},{2,4},{3,5},{4,2},{5,3},{6,0},{7,1},{8,14},{9,15},{10,... | collective-permute-start | bytes 196616 | tf_op jit(solution)/shard_map/ppermute | solution.py:34
  35.1 4.3 %collective-permute-start.15 = (bf16[8,8,512]{2,1,0:T(8,128)(2,1)S(1)}, bf16[8,8,512]{2,1,0:T(8,128)(2,1)S(1)}, u32[]{:S(2)}, u32[]{:S(2)}) collective-permute-start(bf16[8,8,512]{2,1,0:T(8,128)(2,1)S(1)} %fold.12), channel_id=1, source_target_pairs={{0,2},{1,3},{2,0},{3,1},{4,6},{5,7},{6,4},{7,5},{8,10},{9,11},{10,... | collective-permute-start | bytes 196616 | tf_op jit(solution)/shard_map/ppermute | solution.py:34
  35.7 4.3 %collective-permute-start.17 = (bf16[8,8,512]{2,1,0:T(8,128)(2,1)S(1)}, bf16[8,8,512]{2,1,0:T(8,128)(2,1)S(1)}, u32[]{:S(2)}, u32[]{:S(2)}) collective-permute-start(bf16[8,8,512]{2,1,0:T(8,128)(2,1)S(1)} %fold.13), channel_id=1, source_target_pairs={{0,4},{1,5},{2,6},{3,7},{4,0},{5,1},{6,2},{7,3},{8,12},{9,13},{10,... | collective-permute-start | bytes 196616 | tf_op jit(solution)/shard_map/ppermute | solution.py:34
  40.0 5.9 %collective-permute-start.18 = (bf16[8,8,512]{2,1,0:T(8,128)(2,1)S(1)}, bf16[8,8,512]{2,1,0:T(8,128)(2,1)S(1)}, u32[]{:S(2)}, u32[]{:S(2)}) collective-permute-start(bf16[8,8,512]{2,1,0:T(8,128)(2,1)S(1)} %get-tuple-element.47), channel_id=1, source_target_pairs={{0,8},{1,9},{2,10},{3,11},{4,12},{5,13},{6,14},{7,15},{8,0},{9,1},... | collective-permute-start | bytes 196616 | tf_op jit(solution)/shard_map/ppermute | solution.py:34
  46.0 5.2 %collective-permute-start.21 = (bf16[8,8,512]{2,1,0:T(8,128)(2,1)S(1)}, bf16[8,8,512]{2,1,0:T(8,128)(2,1)S(1)}, u32[]{:S(2)}, u32[]{:S(2)}) collective-permute-start(bf16[8,8,512]{2,1,0:T(8,128)(2,1)S(1)} %weigh.1.refs_2_), channel_id=1, source_target_pairs={{0,6},{1,7},{2,4},{3,5},{4,2},{5,3},{6,0},{7,1},{8,14},{9,15},{10,... | collective-permute-start | bytes 196616 | tf_op jit(solution)/shard_map/ppermute | solution.py:34
  46.9 5.1 %collective-permute-start.20 = (bf16[8,8,512]{2,1,0:T(8,128)(2,1)S(1)}, bf16[8,8,512]{2,1,0:T(8,128)(2,1)S(1)}, u32[]{:S(2)}, u32[]{:S(2)}) collective-permute-start(bf16[8,8,512]{2,1,0:T(8,128)(2,1)S(1)} %weigh.1.refs_2_), channel_id=1, source_target_pairs={{0,4},{1,5},{2,6},{3,7},{4,0},{5,1},{6,2},{7,3},{8,12},{9,13},{10,... | collective-permute-start | bytes 196616 | tf_op jit(solution)/shard_map/ppermute | solution.py:34
  49.1 4.3 %collective-permute-start.19 = (bf16[8,8,512]{2,1,0:T(8,128)(2,1)S(1)}, bf16[8,8,512]{2,1,0:T(8,128)(2,1)S(1)}, u32[]{:S(2)}, u32[]{:S(2)}) collective-permute-start(bf16[8,8,512]{2,1,0:T(8,128)(2,1)S(1)} %weigh.1.refs_2_), channel_id=1, source_target_pairs={{0,2},{1,3},{2,0},{3,1},{4,6},{5,7},{6,4},{7,5},{8,10},{9,11},{10,... | collective-permute-start | bytes 196616 | tf_op jit(solution)/shard_map/ppermute | solution.py:34
  53.4 1.6 %collective-permute-start.23 = (bf16[24,8,512]{2,1,0:T(8,128)(2,1)S(1)}, bf16[24,8,512]{2,1,0:T(8,128)(2,1)S(1)}, u32[]{:S(2)}, u32[]{:S(2)}) collective-permute-start(bf16[24,8,512]{2,1,0:T(8,128)(2,1)S(1)} %join.7.refs_3_), channel_id=1, source_target_pairs={{0,1},{1,0},{2,3},{3,2},{4,5},{5,4},{6,7},{7,6},{8,9},{9,8},{10,11... | collective-permute-start | bytes 589832 | tf_op jit(solution)/shard_map/ppermute | solution.py:34
  53.5 1.5 %collective-permute-start.22 = (bf16[8,8,512]{2,1,0:T(8,128)(2,1)S(1)}, bf16[8,8,512]{2,1,0:T(8,128)(2,1)S(1)}, u32[]{:S(2)}, u32[]{:S(2)}) collective-permute-start(bf16[8,8,512]{2,1,0:T(8,128)(2,1)S(1)} %weigh.1.refs_2_), channel_id=1, source_target_pairs={{0,1},{1,0},{2,3},{3,2},{4,5},{5,4},{6,7},{7,6},{8,9},{9,8},{10,11... | collective-permute-start | bytes 196616 | tf_op jit(solution)/shard_map/ppermute | solution.py:34
  57.2 2.0 %collective-permute-start.24 = (bf16[64,8,512]{2,1,0:T(8,128)(2,1)S(1)}, bf16[64,8,512]{2,1,0:T(8,128)(2,1)S(1)}, u32[]{:S(2)}, u32[]{:S(2)}) collective-permute-start(bf16[64,8,512]{2,1,0:T(8,128)(2,1)S(1)} %get-tuple-element.49), channel_id=1, source_target_pairs={{0,1},{1,0},{2,3},{3,2},{4,5},{5,4},{6,7},{7,6},{8,9},{9,8},{10,11... | collective-permute-start | bytes 1572872 | tf_op jit(solution)/shard_map/ppermute | solution.py:34
  57.5 2.4 %collective-permute-start.28 = (bf16[64,8,512]{2,1,0:T(8,128)(2,1)S(1)}, bf16[64,8,512]{2,1,0:T(8,128)(2,1)S(1)}, u32[]{:S(2)}, u32[]{:S(2)}) collective-permute-start(bf16[64,8,512]{2,1,0:T(8,128)(2,1)S(1)} %get-tuple-element.56), channel_id=1, source_target_pairs={{0,1},{1,0},{2,3},{3,2},{4,5},{5,4},{6,7},{7,6},{8,9},{9,8},{10,11... | collective-permute-start | bytes 1572872 | tf_op jit(solution)/shard_map/ppermute | solution.py:34
  59.3 8.5 %collective-permute-start.25 = (bf16[32,8,512]{2,1,0:T(8,128)(2,1)S(1)}, bf16[32,8,512]{2,1,0:T(8,128)(2,1)S(1)}, u32[]{:S(2)}, u32[]{:S(2)}) collective-permute-start(bf16[32,8,512]{2,1,0:T(8,128)(2,1)S(1)} %get-tuple-element.51), channel_id=1, source_target_pairs={{0,2},{1,3},{2,0},{3,1},{4,6},{5,7},{6,4},{7,5},{8,10},{9,11},{10,... | collective-permute-start | bytes 786440 | tf_op jit(solution)/shard_map/ppermute | solution.py:34
  60.0 8.5 %collective-permute-start.29 = (bf16[32,8,512]{2,1,0:T(8,128)(2,1)S(1)}, bf16[32,8,512]{2,1,0:T(8,128)(2,1)S(1)}, u32[]{:S(2)}, u32[]{:S(2)}) collective-permute-start(bf16[32,8,512]{2,1,0:T(8,128)(2,1)S(1)} %get-tuple-element.58), channel_id=1, source_target_pairs={{0,4},{1,5},{2,6},{3,7},{4,0},{5,1},{6,2},{7,3},{8,12},{9,13},{10,... | collective-permute-start | bytes 786440 | tf_op jit(solution)/shard_map/ppermute | solution.py:34
  67.8 5.9 %collective-permute-start.26 = (bf16[16,8,512]{2,1,0:T(8,128)(2,1)S(1)}, bf16[16,8,512]{2,1,0:T(8,128)(2,1)S(1)}, u32[]{:S(2)}, u32[]{:S(2)}) collective-permute-start(bf16[16,8,512]{2,1,0:T(8,128)(2,1)S(1)} %get-tuple-element.53), channel_id=1, source_target_pairs={{0,4},{1,5},{2,6},{3,7},{4,0},{5,1},{6,2},{7,3},{8,12},{9,13},{10,... | collective-permute-start | bytes 393224 | tf_op jit(solution)/shard_map/ppermute | solution.py:34
  68.6 10.7 %collective-permute-start.30 = (bf16[16,8,512]{2,1,0:T(8,128)(2,1)S(1)}, bf16[16,8,512]{2,1,0:T(8,128)(2,1)S(1)}, u32[]{:S(2)}, u32[]{:S(2)}) collective-permute-start(bf16[16,8,512]{2,1,0:T(8,128)(2,1)S(1)} %get-tuple-element.60), channel_id=1, source_target_pairs={{0,8},{1,9},{2,10},{3,11},{4,12},{5,13},{6,14},{7,15},{8,0},{9,1},... | collective-permute-start | bytes 393224 | tf_op jit(solution)/shard_map/ppermute | solution.py:34
  73.7 6.3 %collective-permute-start.27 = (bf16[8,8,512]{2,1,0:T(8,128)(2,1)S(1)}, bf16[8,8,512]{2,1,0:T(8,128)(2,1)S(1)}, u32[]{:S(2)}, u32[]{:S(2)}) collective-permute-start(bf16[8,8,512]{2,1,0:T(8,128)(2,1)S(1)} %get-tuple-element.55), channel_id=1, source_target_pairs={{0,8},{1,9},{2,10},{3,11},{4,12},{5,13},{6,14},{7,15},{8,0},{9,1},... | collective-permute-start | bytes 196616 | tf_op jit(solution)/shard_map/ppermute | solution.py:34
  79.3 4.3 %collective-permute-start.31 = (bf16[8,8,512]{2,1,0:T(8,128)(2,1)S(1)}, bf16[8,8,512]{2,1,0:T(8,128)(2,1)S(1)}, u32[]{:S(2)}, u32[]{:S(2)}) collective-permute-start(bf16[8,8,512]{2,1,0:T(8,128)(2,1)S(1)} %get-tuple-element.62), channel_id=1, source_target_pairs={{0,2},{1,3},{2,0},{3,1},{4,6},{5,7},{6,4},{7,5},{8,10},{9,11},{10,... | collective-permute-start | bytes 196616 | tf_op jit(solution)/shard_map/ppermute | solution.py:34

commit v13 on v6

--- a/solution.py
+++ b/solution.py
@@ -318,7 +318,7 @@
     station_blocks = station_weight.shape[0] // (peers * station_width)
     bits = [1 << k for k in range(1, peers.bit_length() - 1)]
     far = bits[:0:-1]
-    orders = (bits[:1] + far, far + bits[:1])
+    orders = (far[:1] + bits[:1] + far[1:], far + bits[:1])
 
     lanes = (cell_total // LANES, LANES)
     half_dims = (cell_blocks // 2, probe_count, cell_width)

time: 81.3 us -> 80.2 us (0.986)
  waiting for transfers between devices: 39.5 us -> 37.2 us
  starting transfers between devices: 28.4 us -> 29.6 us
    ppermute x31, waiting for transfers between devices: 39.5 us -> 37.2 us  [swap(): return lax.ppermute(array, 'tile', [(i, i ^ bits) for i in range(count)])]
    ppermute x31, starting transfers between devices: 28.4 us -> 29.6 us  [swap(): return lax.ppermute(array, 'tile', [(i, i ^ bits) for i in range(count)])]
  transfers between devices with their start and end apart: 31 -> 31, of which waited for: 20 -> 21; matrix products, arithmetic and copies ran while one was open for 0% -> 0% of each run, Pallas kernels for 8% -> 8%
where the time goes in v13:
time: 80.2 us; the launch traced here: 79.9 us
  waiting for transfers between devices  37.2 us (46%)
  starting transfers between devices  29.6 us (37%)
  Pallas kernels  12.9 us (16%)
    ppermute x31, waiting for transfers between devices, swap(): return lax.ppermute(array, 'tile', [(i, i ^ bits) for i in range(count)])  37.2 us
    ppermute x31, starting transfers between devices, swap(): return lax.ppermute(array, 'tile', [(i, i ^ bits) for i in range(count)])  29.6 us
    pallas_call x26, Pallas kernels, local(): pl.pallas_call(run, out_shape=[a if s.memory_space is None else s.memory_...  12.9 us
  transfers between devices with their start and end apart: 31, of which 21 were waited for; matrix products, arithmetic and copies ran while one was open for 0% of the time, Pallas kernels for 8%

profile of v13, /device:TPU:0, one launch (start us, length us, event | category | flops | bytes accessed | tf_op | source)
XLA Modules:
  0.0 79.9 jit_solution(3053478937140816092)
XLA Ops:
  0.0 1.1 %scale.1 = (bf16[8,8,512]{2,1,0:T(8,128)(2,1)S(1)}, bf16[8,8,512]{2,1,0:T(8,128)(2,1)S(1)}, f32[64,128]{1,0:T(8,128)S(1)}) custom-call(f32[4]{0:T(128)} %refs_0_.3, f32[64,128]{1,0:T(8,128)} %bitcast.9, s32[64,128]{1,0:T(8,128)} %bitcast.10, f32[8,8192]{1,0:T(8,128)} %refs_3_.1), custom_call_target="tpu_custom_call" | custom-call | bytes 491536 | tf_op jit(solution)/shard_map/scale/pallas_call | solution.py:49
  1.1 4.1 %collective-permute-start.2 = (bf16[8,8,512]{2,1,0:T(8,128)(2,1)S(1)}, bf16[8,8,512]{2,1,0:T(8,128)(2,1)S(1)}, u32[]{:S(2)}, u32[]{:S(2)}) collective-permute-start(bf16[8,8,512]{2,1,0:T(8,128)(2,1)S(1)} %get-tuple-element.36.refs_0_), channel_id=1, source_target_pairs={{0,8},{1,9},{2,10},{3,11},{4,12},{5,13},{6,14},{7,15},{8,0},{9,1},... | collective-permute-start | bytes 196616 | tf_op jit(solution)/shard_map/ppermute | solution.py:34
  5.3 1.5 %plan.1 = (s32[8,128]{1,0:T(8,128)S(4)}, f32[32,128]{1,0:T(8,128)S(1)}) custom-call(s32[16,128]{1,0:T(8,128)} %bitcast.11, s32[16,128]{1,0:T(8,128)} %bitcast.12, s32[16,128]{1,0:T(8,128)} %bitcast.13, s32[16,128]{1,0:T(8,128)} %bitcast.14, s32[16,128]{1,0:T(8,128)} %bitcast.15, f32[256,128]{1,0:T(8,128)} %bitcast.8, ...), custom_call_target="tpu_custom_call" | custom-call | bytes 192512 | tf_op jit(solution)/shard_map/plan/pallas_call | solution.py:49
  6.7 2.1 %collective-permute-done.2.refs_1_ = bf16[8,8,512]{2,1,0:T(8,128)(2,1)S(1)} collective-permute-done((bf16[8,8,512]{2,1,0:T(8,128)(2,1)S(1)}, bf16[8,8,512]{2,1,0:T(8,128)(2,1)S(1)}, u32[]{:S(2)}, u32[]{:S(2)}) %collective-permute-start.2) | collective-permute-done | bytes 65568 | tf_op jit(solution)/shard_map/ppermute | solution.py:34
  8.8 2.1 %collective-permute-start.3 = (bf16[16,8,512]{2,1,0:T(8,128)(2,1)S(1)}, bf16[16,8,512]{2,1,0:T(8,128)(2,1)S(1)}, u32[]{:S(2)}, u32[]{:S(2)}) collective-permute-start(bf16[16,8,512]{2,1,0:T(8,128)(2,1)S(1)} %join.6.refs_2_.refs_0_), channel_id=1, source_target_pairs={{0,4},{1,5},{2,6},{3,7},{4,0},{5,1},{6,2},{7,3},{8,12},{9,13},{10,... | collective-permute-start | bytes 393224 | tf_op jit(solution)/shard_map/ppermute | solution.py:34
  11.0 0.7 collective-permute-done.refs_1_
  11.7 1.8 %collective-permute-start.1 = (bf16[16,8,512]{2,1,0:T(8,128)(2,1)S(1)}, bf16[16,8,512]{2,1,0:T(8,128)(2,1)S(1)}, u32[]{:S(2)}, u32[]{:S(2)}) collective-permute-start(bf16[16,8,512]{2,1,0:T(8,128)(2,1)S(1)} %join.5.refs_1_.refs_0_), channel_id=1, source_target_pairs={{0,2},{1,3},{2,0},{3,1},{4,6},{5,7},{6,4},{7,5},{8,10},{9,11},{10,... | collective-permute-start | bytes 393224 | tf_op jit(solution)/shard_map/ppermute | solution.py:34
  13.4 2.2 %load_v.1.refs_3_.refs_10_.refs_7_ = bf16[128,32,512]{2,1,0:T(8,128)(2,1)S(1)} custom-call(bf16[128,32,512]{2,1,0:T(8,128)(2,1)} %refs_0_.4, bf16[16,8,512]{2,1,0:T(8,128)(2,1)S(1)} %join.5.refs_1_.refs_0_, bf16[16,8,512]{2,1,0:T(8,128)(2,1)S(1)} %join.6.refs_2_.refs_0_), custom_call_target="tpu_custom_call" | custom-call | bytes 8388608 | tf_op jit(solution)/shard_map/load_v/pallas_call | solution.py:49
  15.7 2.2 %load_u.1.refs_2_.refs_11_.refs_6_ = bf16[128,32,512]{2,1,0:T(8,128)(2,1)S(1)} custom-call(bf16[128,32,512]{2,1,0:T(8,128)(2,1)} %refs_0_.5, bf16[16,8,512]{2,1,0:T(8,128)(2,1)S(1)} %join.5.refs_1_.refs_0_, bf16[16,8,512]{2,1,0:T(8,128)(2,1)S(1)} %join.6.refs_2_.refs_0_, bf16[128,32,512]{2,1,0:T(8,128)(2,1)S(1)} %load_v.1.refs_3_.refs_10_.refs_7_), custom_call_target="tpu_custom_call" | custom-call | bytes 8388608 | tf_op jit(solution)/shard_map/load_u/pallas_call | solution.py:49
  17.9 0.4 collective-permute-start.5
  18.3 0.6 collective-permute-start.4
  19.0 0.5 collective-permute-start.6
  19.5 6.3 %collective-permute-done.5.refs_5_ = bf16[32,8,512]{2,1,0:T(8,128)(2,1)S(1)} collective-permute-done((bf16[32,8,512]{2,1,0:T(8,128)(2,1)S(1)}, bf16[32,8,512]{2,1,0:T(8,128)(2,1)S(1)}, u32[]{:S(2)}, u32[]{:S(2)}) %collective-permute-start.5) | collective-permute-done | bytes 262176 | tf_op jit(solution)/shard_map/ppermute | solution.py:34
  25.9 0.4 collective-permute-start.7
  26.4 0.9 %collective-permute-done.9.refs_9_ = bf16[32,8,512]{2,1,0:T(8,128)(2,1)S(1)} collective-permute-done((bf16[32,8,512]{2,1,0:T(8,128)(2,1)S(1)}, bf16[32,8,512]{2,1,0:T(8,128)(2,1)S(1)}, u32[]{:S(2)}, u32[]{:S(2)}) %collective-permute-start.9) | collective-permute-done | bytes 262176 | tf_op jit(solution)/shard_map/ppermute | solution.py:34
  27.3 0.4 collective-permute-done.7.refs_7_
  27.7 2.2 %forward.1 = (f32[64,8,512]{2,1,0:T(8,128)S(1)}, f32[8,8,512]{2,1,0:T(8,128)S(1)}, f32[8,8,512]{2,1,0:T(8,128)S(1)}, f32[8,8,512]{2,1,0:T(8,128)S(1)}, f32[8,8,512]{2,1,0:T(8,128)S(1)}) custom-call(s32[8,128]{1,0:T(8,128)S(4)} %get-tuple-element.33.refs_0_, f32[64,8,512]{2,1,0:T(8,128)S(1)} %zeros.2.refs_1_, ...), custom_call_target="tpu_custom_call", output_to_operand_aliasing={{0}: (1, {})} | custom-call | flops 536870912 | bytes 13111296 | tf_op jit(solution)/shard_map/forward/pallas_call | solution.py:49
  30.0 0.4 collective-permute-start.13
  30.6 0.4 collective-permute-start.10
  30.9 0.3 collective-permute-done.11.refs_1_
  31.3 1.5 %collective-permute-start.12 = (bf16[8,8,512]{2,1,0:T(8,128)(2,1)S(1)}, bf16[8,8,512]{2,1,0:T(8,128)(2,1)S(1)}, u32[]{:S(2)}, u32[]{:S(2)}) collective-permute-start(bf16[8,8,512]{2,1,0:T(8,128)(2,1)S(1)} %fold.11), channel_id=1, source_target_pairs={{0,6},{1,7},{2,4},{3,5},{4,2},{5,3},{6,0},{7,1},{8,14},{9,15},{10,... | collective-permute-start | bytes 196616 | tf_op jit(solution)/shard_map/ppermute | solution.py:34
  32.8 0.6 collective-permute-start.14
  33.5 1.5 %collective-permute-start.16 = (bf16[8,8,512]{2,1,0:T(8,128)(2,1)S(1)}, bf16[8,8,512]{2,1,0:T(8,128)(2,1)S(1)}, u32[]{:S(2)}, u32[]{:S(2)}) collective-permute-start(bf16[8,8,512]{2,1,0:T(8,128)(2,1)S(1)} %fold.13), channel_id=1, source_target_pairs={{0,4},{1,5},{2,6},{3,7},{4,0},{5,1},{6,2},{7,3},{8,12},{9,13},{10,... | collective-permute-start | bytes 196616 | tf_op jit(solution)/shard_map/ppermute | solution.py:34
  35.0 1.5 %collective-permute-done.12.refs_1_ = bf16[8,8,512]{2,1,0:T(8,128)(2,1)S(1)} collective-permute-done((bf16[8,8,512]{2,1,0:T(8,128)(2,1)S(1)}, bf16[8,8,512]{2,1,0:T(8,128)(2,1)S(1)}, u32[]{:S(2)}, u32[]{:S(2)}) %collective-permute-start.12) | collective-permute-done | bytes 65568 | tf_op jit(solution)/shard_map/ppermute | solution.py:34
  36.6 1.2 %collective-permute-done.14.refs_2_ = bf16[8,8,512]{2,1,0:T(8,128)(2,1)S(1)} collective-permute-done((bf16[8,8,512]{2,1,0:T(8,128)(2,1)S(1)}, bf16[8,8,512]{2,1,0:T(8,128)(2,1)S(1)}, u32[]{:S(2)}, u32[]{:S(2)}) %collective-permute-start.14) | collective-permute-done | bytes 65568 | tf_op jit(solution)/shard_map/ppermute | solution.py:34
  37.9 3.4 %collective-permute-start.17 = (bf16[8,8,512]{2,1,0:T(8,128)(2,1)S(1)}, bf16[8,8,512]{2,1,0:T(8,128)(2,1)S(1)}, u32[]{:S(2)}, u32[]{:S(2)}) collective-permute-start(bf16[8,8,512]{2,1,0:T(8,128)(2,1)S(1)} %get-tuple-element.43), channel_id=1, source_target_pairs={{0,8},{1,9},{2,10},{3,11},{4,12},{5,13},{6,14},{7,15},{8,0},{9,1},... | collective-permute-start | bytes 196616 | tf_op jit(solution)/shard_map/ppermute | solution.py:34
  41.3 2.9 %collective-permute-done.17.refs_1_ = bf16[8,8,512]{2,1,0:T(8,128)(2,1)S(1)} collective-permute-done((bf16[8,8,512]{2,1,0:T(8,128)(2,1)S(1)}, bf16[8,8,512]{2,1,0:T(8,128)(2,1)S(1)}, u32[]{:S(2)}, u32[]{:S(2)}) %collective-permute-start.17) | collective-permute-done | bytes 65568 | tf_op jit(solution)/shard_map/ppermute | solution.py:34
  44.3 1.4 %collective-permute-start.20 = (bf16[8,8,512]{2,1,0:T(8,128)(2,1)S(1)}, bf16[8,8,512]{2,1,0:T(8,128)(2,1)S(1)}, u32[]{:S(2)}, u32[]{:S(2)}) collective-permute-start(bf16[8,8,512]{2,1,0:T(8,128)(2,1)S(1)} %weigh.1.refs_2_), channel_id=1, source_target_pairs={{0,6},{1,7},{2,4},{3,5},{4,2},{5,3},{6,0},{7,1},{8,14},{9,15},{10,... | collective-permute-start | bytes 196616 | tf_op jit(solution)/shard_map/ppermute | solution.py:34
  45.6 1.6 %collective-permute-start.19 = (bf16[8,8,512]{2,1,0:T(8,128)(2,1)S(1)}, bf16[8,8,512]{2,1,0:T(8,128)(2,1)S(1)}, u32[]{:S(2)}, u32[]{:S(2)}) collective-permute-start(bf16[8,8,512]{2,1,0:T(8,128)(2,1)S(1)} %weigh.1.refs_2_), channel_id=1, source_target_pairs={{0,4},{1,5},{2,6},{3,7},{4,0},{5,1},{6,2},{7,3},{8,12},{9,13},{10,... | collective-permute-start | bytes 196616 | tf_op jit(solution)/shard_map/ppermute | solution.py:34
  47.2 0.6 collective-permute-start.18
  47.8 1.7 %collective-permute-done.20.refs_2_ = bf16[8,8,512]{2,1,0:T(8,128)(2,1)S(1)} collective-permute-done((bf16[8,8,512]{2,1,0:T(8,128)(2,1)S(1)}, bf16[8,8,512]{2,1,0:T(8,128)(2,1)S(1)}, u32[]{:S(2)}, u32[]{:S(2)}) %collective-permute-start.20) | collective-permute-done | bytes 65568 | tf_op jit(solution)/shard_map/ppermute | solution.py:34
  49.5 0.7 collective-permute-done.19.refs_1_
  50.2 1.3 %collective-permute-done.18.refs_0_ = bf16[8,8,512]{2,1,0:T(8,128)(2,1)S(1)} collective-permute-done((bf16[8,8,512]{2,1,0:T(8,128)(2,1)S(1)}, bf16[8,8,512]{2,1,0:T(8,128)(2,1)S(1)}, u32[]{:S(2)}, u32[]{:S(2)}) %collective-permute-start.18) | collective-permute-done | bytes 65568 | tf_op jit(solution)/shard_map/ppermute | solution.py:34
  51.6 0.5 collective-permute-start.21
  52.4 0.7 collective-permute-done.21.refs_4_
  53.1 2.2 %adjoint.1 = (f32[256,8,512]{2,1,0:T(8,128)S(1)}, bf16[64,8,512]{2,1,0:T(8,128)(2,1)S(1)}, bf16[64,8,512]{2,1,0:T(8,128)(2,1)S(1)}) custom-call(s32[8,128]{1,0:T(8,128)S(4)} %get-tuple-element.33.refs_0_, f32[256,8,512]{2,1,0:T(8,128)S(1)} %zeros.3.refs_1_, bf16[8,8,512]{2,1,0:T(8,128)(2,1)S(1)} %weigh.1.refs_2_, ...), custom_call_target="tpu_custom_call", output_to_operand_aliasing={{0}: (1, {})} | custom-call | flops 536870912 | bytes 18354176 | tf_op jit(solution)/shard_map/adjoint/pallas_call | solution.py:49
  55.9 1.4 %collective-permute-done.23.refs_1_ = bf16[64,8,512]{2,1,0:T(8,128)(2,1)S(1)} collective-permute-done((bf16[64,8,512]{2,1,0:T(8,128)(2,1)S(1)}, bf16[64,8,512]{2,1,0:T(8,128)(2,1)S(1)}, u32[]{:S(2)}, u32[]{:S(2)}) %collective-permute-start.23) | collective-permute-done | bytes 524320 | tf_op jit(solution)/shard_map/ppermute | solution.py:34
  57.4 0.5 collective-permute-start.24
  58.1 0.6 collective-permute-start.28
  58.8 7.1 %collective-permute-done.24.refs_1_ = bf16[32,8,512]{2,1,0:T(8,128)(2,1)S(1)} collective-permute-done((bf16[32,8,512]{2,1,0:T(8,128)(2,1)S(1)}, bf16[32,8,512]{2,1,0:T(8,128)(2,1)S(1)}, u32[]{:S(2)}, u32[]{:S(2)}) %collective-permute-start.24) | collective-permute-done | bytes 262176 | tf_op jit(solution)/shard_map/ppermute | solution.py:34
  65.9 0.6 collective-permute-start.25
  66.7 1.2 %collective-permute-start.29 = (bf16[16,8,512]{2,1,0:T(8,128)(2,1)S(1)}, bf16[16,8,512]{2,1,0:T(8,128)(2,1)S(1)}, u32[]{:S(2)}, u32[]{:S(2)}) collective-permute-start(bf16[16,8,512]{2,1,0:T(8,128)(2,1)S(1)} %get-tuple-element.56), channel_id=1, source_target_pairs={{0,4},{1,5},{2,6},{3,7},{4,0},{5,1},{6,2},{7,3},{8,12},{9,13},{10,... | collective-permute-start | bytes 393224 | tf_op jit(solution)/shard_map/ppermute | solution.py:34
  67.9 3.1 %collective-permute-done.25.refs_1_ = bf16[16,8,512]{2,1,0:T(8,128)(2,1)S(1)} collective-permute-done((bf16[16,8,512]{2,1,0:T(8,128)(2,1)S(1)}, bf16[16,8,512]{2,1,0:T(8,128)(2,1)S(1)}, u32[]{:S(2)}, u32[]{:S(2)}) %collective-permute-start.25) | collective-permute-done | bytes 131104 | tf_op jit(solution)/shard_map/ppermute | solution.py:34
  71.0 2.3 %collective-permute-start.26 = (bf16[8,8,512]{2,1,0:T(8,128)(2,1)S(1)}, bf16[8,8,512]{2,1,0:T(8,128)(2,1)S(1)}, u32[]{:S(2)}, u32[]{:S(2)}) collective-permute-start(bf16[8,8,512]{2,1,0:T(8,128)(2,1)S(1)} %get-tuple-element.51), channel_id=1, source_target_pairs={{0,8},{1,9},{2,10},{3,11},{4,12},{5,13},{6,14},{7,15},{8,0},{9,1},... | collective-permute-start | bytes 196616 | tf_op jit(solution)/shard_map/ppermute | solution.py:34
  73.3 1.4 %collective-permute-start.30 = (bf16[8,8,512]{2,1,0:T(8,128)(2,1)S(1)}, bf16[8,8,512]{2,1,0:T(8,128)(2,1)S(1)}, u32[]{:S(2)}, u32[]{:S(2)}) collective-permute-start(bf16[8,8,512]{2,1,0:T(8,128)(2,1)S(1)} %get-tuple-element.58), channel_id=1, source_target_pairs={{0,8},{1,9},{2,10},{3,11},{4,12},{5,13},{6,14},{7,15},{8,0},{9,1},... | collective-permute-start | bytes 196616 | tf_op jit(solution)/shard_map/ppermute | solution.py:34
  74.7 2.8 %collective-permute-done.26.refs_1_ = bf16[8,8,512]{2,1,0:T(8,128)(2,1)S(1)} collective-permute-done((bf16[8,8,512]{2,1,0:T(8,128)(2,1)S(1)}, bf16[8,8,512]{2,1,0:T(8,128)(2,1)S(1)}, u32[]{:S(2)}, u32[]{:S(2)}) %collective-permute-start.26) | collective-permute-done | bytes 65568 | tf_op jit(solution)/shard_map/ppermute | solution.py:34
  77.5 1.6 %collective-permute-done.30.refs_3_ = bf16[8,8,512]{2,1,0:T(8,128)(2,1)S(1)} collective-permute-done((bf16[8,8,512]{2,1,0:T(8,128)(2,1)S(1)}, bf16[8,8,512]{2,1,0:T(8,128)(2,1)S(1)}, u32[]{:S(2)}, u32[]{:S(2)}) %collective-permute-start.30) | collective-permute-done | bytes 65568 | tf_op jit(solution)/shard_map/ppermute | solution.py:34
  79.1 0.7 final.1
  (40 shorter events, 2.3 us)
Async XLA Ops:
  1.1 7.8 %collective-permute-start.2 = (bf16[8,8,512]{2,1,0:T(8,128)(2,1)S(1)}, bf16[8,8,512]{2,1,0:T(8,128)(2,1)S(1)}, u32[]{:S(2)}, u32[]{:S(2)}) collective-permute-start(bf16[8,8,512]{2,1,0:T(8,128)(2,1)S(1)} %get-tuple-element.36.refs_0_), channel_id=1, source_target_pairs={{0,8},{1,9},{2,10},{3,11},{4,12},{5,13},{6,14},{7,15},{8,0},{9,1},... | collective-permute-start | bytes 196616 | tf_op jit(solution)/shard_map/ppermute | solution.py:34
  5.2 6.5 %collective-permute-start = (bf16[8,8,512]{2,1,0:T(8,128)(2,1)S(1)}, bf16[8,8,512]{2,1,0:T(8,128)(2,1)S(1)}, u32[]{:S(2)}, u32[]{:S(2)}) collective-permute-start(bf16[8,8,512]{2,1,0:T(8,128)(2,1)S(1)} %get-tuple-element.34.refs_0_), channel_id=1, source_target_pairs={{0,8},{1,9},{2,10},{3,11},{4,12},{5,13},{6,14},{7,15},{8,0},{9,1},... | collective-permute-start | bytes 196616 | tf_op jit(solution)/shard_map/ppermute | solution.py:34
  8.8 9.1 %collective-permute-start.3 = (bf16[16,8,512]{2,1,0:T(8,128)(2,1)S(1)}, bf16[16,8,512]{2,1,0:T(8,128)(2,1)S(1)}, u32[]{:S(2)}, u32[]{:S(2)}) collective-permute-start(bf16[16,8,512]{2,1,0:T(8,128)(2,1)S(1)} %join.6.refs_2_.refs_0_), channel_id=1, source_target_pairs={{0,4},{1,5},{2,6},{3,7},{4,0},{5,1},{6,2},{7,3},{8,12},{9,13},{10,... | collective-permute-start | bytes 393224 | tf_op jit(solution)/shard_map/ppermute | solution.py:34
  11.7 6.6 %collective-permute-start.1 = (bf16[16,8,512]{2,1,0:T(8,128)(2,1)S(1)}, bf16[16,8,512]{2,1,0:T(8,128)(2,1)S(1)}, u32[]{:S(2)}, u32[]{:S(2)}) collective-permute-start(bf16[16,8,512]{2,1,0:T(8,128)(2,1)S(1)} %join.5.refs_1_.refs_0_), channel_id=1, source_target_pairs={{0,2},{1,3},{2,0},{3,1},{4,6},{5,7},{6,4},{7,5},{8,10},{9,11},{10,... | collective-permute-start | bytes 393224 | tf_op jit(solution)/shard_map/ppermute | solution.py:34
  17.9 7.8 %collective-permute-start.5 = (bf16[32,8,512]{2,1,0:T(8,128)(2,1)S(1)}, bf16[32,8,512]{2,1,0:T(8,128)(2,1)S(1)}, u32[]{:S(2)}, u32[]{:S(2)}) collective-permute-start(bf16[32,8,512]{2,1,0:T(8,128)(2,1)S(1)} %join.8.refs_1_.refs_4_), channel_id=1, source_target_pairs={{0,2},{1,3},{2,0},{3,1},{4,6},{5,7},{6,4},{7,5},{8,10},{9,11},{10,... | collective-permute-start | bytes 786440 | tf_op jit(solution)/shard_map/ppermute | solution.py:34
  18.3 7.5 %collective-permute-start.4 = (bf16[32,8,512]{2,1,0:T(8,128)(2,1)S(1)}, bf16[32,8,512]{2,1,0:T(8,128)(2,1)S(1)}, u32[]{:S(2)}, u32[]{:S(2)}) collective-permute-start(bf16[32,8,512]{2,1,0:T(8,128)(2,1)S(1)} %join.7.refs_0_.refs_2_), channel_id=1, source_target_pairs={{0,4},{1,5},{2,6},{3,7},{4,0},{5,1},{6,2},{7,3},{8,12},{9,13},{10,... | collective-permute-start | bytes 786440 | tf_op jit(solution)/shard_map/ppermute | solution.py:34
  19.0 7.4 %collective-permute-start.8 = (bf16[32,8,512]{2,1,0:T(8,128)(2,1)S(1)}, bf16[32,8,512]{2,1,0:T(8,128)(2,1)S(1)}, u32[]{:S(2)}, u32[]{:S(2)}) collective-permute-start(bf16[32,8,512]{2,1,0:T(8,128)(2,1)S(1)} %join.8.refs_1_.refs_4_), channel_id=1, source_target_pairs={{0,1},{1,0},{2,3},{3,2},{4,5},{5,4},{6,7},{7,6},{8,9},{9,8},{10,11... | collective-permute-start | bytes 786440 | tf_op jit(solution)/shard_map/ppermute | solution.py:34
  19.0 7.4 %collective-permute-start.6 = (bf16[32,8,512]{2,1,0:T(8,128)(2,1)S(1)}, bf16[32,8,512]{2,1,0:T(8,128)(2,1)S(1)}, u32[]{:S(2)}, u32[]{:S(2)}) collective-permute-start(bf16[32,8,512]{2,1,0:T(8,128)(2,1)S(1)} %join.7.refs_0_.refs_2_), channel_id=1, source_target_pairs={{0,1},{1,0},{2,3},{3,2},{4,5},{5,4},{6,7},{7,6},{8,9},{9,8},{10,11... | collective-permute-start | bytes 786440 | tf_op jit(solution)/shard_map/ppermute | solution.py:34
  25.7 1.5 %collective-permute-start.9 = (bf16[32,8,512]{2,1,0:T(8,128)(2,1)S(1)}, bf16[32,8,512]{2,1,0:T(8,128)(2,1)S(1)}, u32[]{:S(2)}, u32[]{:S(2)}) collective-permute-start(bf16[32,8,512]{2,1,0:T(8,128)(2,1)S(1)} %collective-permute-done.5.refs_5_), channel_id=1, source_target_pairs={{0,1},{1,0},{2,3},{3,2},{4,5},{5,4},{6,7},{7,6},{8,9},{9,8},{10,11... | collective-permute-start | bytes 786440 | tf_op jit(solution)/shard_map/ppermute | solution.py:34
  25.9 1.8 %collective-permute-start.7 = (bf16[32,8,512]{2,1,0:T(8,128)(2,1)S(1)}, bf16[32,8,512]{2,1,0:T(8,128)(2,1)S(1)}, u32[]{:S(2)}, u32[]{:S(2)}) collective-permute-start(bf16[32,8,512]{2,1,0:T(8,128)(2,1)S(1)} %collective-permute-done.4.refs_3_), channel_id=1, source_target_pairs={{0,1},{1,0},{2,3},{3,2},{4,5},{5,4},{6,7},{7,6},{8,9},{9,8},{10,11... | collective-permute-start | bytes 786440 | tf_op jit(solution)/shard_map/ppermute | solution.py:34
  29.9 1.4 %collective-permute-start.11 = (f32[8,8,512]{2,1,0:T(8,128)S(1)}, f32[8,8,512]{2,1,0:T(8,128)S(1)}, u32[]{:S(2)}, u32[]{:S(2)}) collective-permute-start(f32[8,8,512]{2,1,0:T(8,128)S(1)} %get-tuple-element.39), channel_id=1, source_target_pairs={{0,1},{1,0},{2,3},{3,2},{4,5},{5,4},{6,7},{7,6},{8,9},{9,8},{10,11... | collective-permute-start | bytes 393224 | tf_op jit(solution)/shard_map/ppermute | solution.py:34
  30.0 2.8 %collective-permute-start.13 = (f32[8,8,512]{2,1,0:T(8,128)S(1)}, f32[8,8,512]{2,1,0:T(8,128)S(1)}, u32[]{:S(2)}, u32[]{:S(2)}) collective-permute-start(f32[8,8,512]{2,1,0:T(8,128)S(1)} %get-tuple-element.40), channel_id=1, source_target_pairs={{0,1},{1,0},{2,3},{3,2},{4,5},{5,4},{6,7},{7,6},{8,9},{9,8},{10,11... | collective-permute-start | bytes 393224 | tf_op jit(solution)/shard_map/ppermute | solution.py:34
  30.4 3.0 %collective-permute-start.15 = (f32[8,8,512]{2,1,0:T(8,128)S(1)}, f32[8,8,512]{2,1,0:T(8,128)S(1)}, u32[]{:S(2)}, u32[]{:S(2)}) collective-permute-start(f32[8,8,512]{2,1,0:T(8,128)S(1)} %get-tuple-element.41), channel_id=1, source_target_pairs={{0,1},{1,0},{2,3},{3,2},{4,5},{5,4},{6,7},{7,6},{8,9},{9,8},{10,11... | collective-permute-start | bytes 393224 | tf_op jit(solution)/shard_map/ppermute | solution.py:34
  30.6 4.5 %collective-permute-start.10 = (f32[8,8,512]{2,1,0:T(8,128)S(1)}, f32[8,8,512]{2,1,0:T(8,128)S(1)}, u32[]{:S(2)}, u32[]{:S(2)}) collective-permute-start(f32[8,8,512]{2,1,0:T(8,128)S(1)} %get-tuple-element.38), channel_id=1, source_target_pairs={{0,1},{1,0},{2,3},{3,2},{4,5},{5,4},{6,7},{7,6},{8,9},{9,8},{10,11... | collective-permute-start | bytes 393224 | tf_op jit(solution)/shard_map/ppermute | solution.py:34
  31.3 5.3 %collective-permute-start.12 = (bf16[8,8,512]{2,1,0:T(8,128)(2,1)S(1)}, bf16[8,8,512]{2,1,0:T(8,128)(2,1)S(1)}, u32[]{:S(2)}, u32[]{:S(2)}) collective-permute-start(bf16[8,8,512]{2,1,0:T(8,128)(2,1)S(1)} %fold.11), channel_id=1, source_target_pairs={{0,6},{1,7},{2,4},{3,5},{4,2},{5,3},{6,0},{7,1},{8,14},{9,15},{10,... | collective-permute-start | bytes 196616 | tf_op jit(solution)/shard_map/ppermute | solution.py:34
  32.8 5.0 %collective-permute-start.14 = (bf16[8,8,512]{2,1,0:T(8,128)(2,1)S(1)}, bf16[8,8,512]{2,1,0:T(8,128)(2,1)S(1)}, u32[]{:S(2)}, u32[]{:S(2)}) collective-permute-start(bf16[8,8,512]{2,1,0:T(8,128)(2,1)S(1)} %fold.12), channel_id=1, source_target_pairs={{0,2},{1,3},{2,0},{3,1},{4,6},{5,7},{6,4},{7,5},{8,10},{9,11},{10,... | collective-permute-start | bytes 196616 | tf_op jit(solution)/shard_map/ppermute | solution.py:34
  33.5 4.4 %collective-permute-start.16 = (bf16[8,8,512]{2,1,0:T(8,128)(2,1)S(1)}, bf16[8,8,512]{2,1,0:T(8,128)(2,1)S(1)}, u32[]{:S(2)}, u32[]{:S(2)}) collective-permute-start(bf16[8,8,512]{2,1,0:T(8,128)(2,1)S(1)} %fold.13), channel_id=1, source_target_pairs={{0,4},{1,5},{2,6},{3,7},{4,0},{5,1},{6,2},{7,3},{8,12},{9,13},{10,... | collective-permute-start | bytes 196616 | tf_op jit(solution)/shard_map/ppermute | solution.py:34
  37.9 6.4 %collective-permute-start.17 = (bf16[8,8,512]{2,1,0:T(8,128)(2,1)S(1)}, bf16[8,8,512]{2,1,0:T(8,128)(2,1)S(1)}, u32[]{:S(2)}, u32[]{:S(2)}) collective-permute-start(bf16[8,8,512]{2,1,0:T(8,128)(2,1)S(1)} %get-tuple-element.43), channel_id=1, source_target_pairs={{0,8},{1,9},{2,10},{3,11},{4,12},{5,13},{6,14},{7,15},{8,0},{9,1},... | collective-permute-start | bytes 196616 | tf_op jit(solution)/shard_map/ppermute | solution.py:34
  44.3 5.2 %collective-permute-start.20 = (bf16[8,8,512]{2,1,0:T(8,128)(2,1)S(1)}, bf16[8,8,512]{2,1,0:T(8,128)(2,1)S(1)}, u32[]{:S(2)}, u32[]{:S(2)}) collective-permute-start(bf16[8,8,512]{2,1,0:T(8,128)(2,1)S(1)} %weigh.1.refs_2_), channel_id=1, source_target_pairs={{0,6},{1,7},{2,4},{3,5},{4,2},{5,3},{6,0},{7,1},{8,14},{9,15},{10,... | collective-permute-start | bytes 196616 | tf_op jit(solution)/shard_map/ppermute | solution.py:34
  45.6 4.6 %collective-permute-start.19 = (bf16[8,8,512]{2,1,0:T(8,128)(2,1)S(1)}, bf16[8,8,512]{2,1,0:T(8,128)(2,1)S(1)}, u32[]{:S(2)}, u32[]{:S(2)}) collective-permute-start(bf16[8,8,512]{2,1,0:T(8,128)(2,1)S(1)} %weigh.1.refs_2_), channel_id=1, source_target_pairs={{0,4},{1,5},{2,6},{3,7},{4,0},{5,1},{6,2},{7,3},{8,12},{9,13},{10,... | collective-permute-start | bytes 196616 | tf_op jit(solution)/shard_map/ppermute | solution.py:34
  47.2 4.3 %collective-permute-start.18 = (bf16[8,8,512]{2,1,0:T(8,128)(2,1)S(1)}, bf16[8,8,512]{2,1,0:T(8,128)(2,1)S(1)}, u32[]{:S(2)}, u32[]{:S(2)}) collective-permute-start(bf16[8,8,512]{2,1,0:T(8,128)(2,1)S(1)} %weigh.1.refs_2_), channel_id=1, source_target_pairs={{0,2},{1,3},{2,0},{3,1},{4,6},{5,7},{6,4},{7,5},{8,10},{9,11},{10,... | collective-permute-start | bytes 196616 | tf_op jit(solution)/shard_map/ppermute | solution.py:34
  51.5 1.6 %collective-permute-start.22 = (bf16[24,8,512]{2,1,0:T(8,128)(2,1)S(1)}, bf16[24,8,512]{2,1,0:T(8,128)(2,1)S(1)}, u32[]{:S(2)}, u32[]{:S(2)}) collective-permute-start(bf16[24,8,512]{2,1,0:T(8,128)(2,1)S(1)} %join.9.refs_3_), channel_id=1, source_target_pairs={{0,1},{1,0},{2,3},{3,2},{4,5},{5,4},{6,7},{7,6},{8,9},{9,8},{10,11... | collective-permute-start | bytes 589832 | tf_op jit(solution)/shard_map/ppermute | solution.py:34
  51.6 1.5 %collective-permute-start.21 = (bf16[8,8,512]{2,1,0:T(8,128)(2,1)S(1)}, bf16[8,8,512]{2,1,0:T(8,128)(2,1)S(1)}, u32[]{:S(2)}, u32[]{:S(2)}) collective-permute-start(bf16[8,8,512]{2,1,0:T(8,128)(2,1)S(1)} %weigh.1.refs_2_), channel_id=1, source_target_pairs={{0,1},{1,0},{2,3},{3,2},{4,5},{5,4},{6,7},{7,6},{8,9},{9,8},{10,11... | collective-permute-start | bytes 196616 | tf_op jit(solution)/shard_map/ppermute | solution.py:34
  55.3 2.0 %collective-permute-start.23 = (bf16[64,8,512]{2,1,0:T(8,128)(2,1)S(1)}, bf16[64,8,512]{2,1,0:T(8,128)(2,1)S(1)}, u32[]{:S(2)}, u32[]{:S(2)}) collective-permute-start(bf16[64,8,512]{2,1,0:T(8,128)(2,1)S(1)} %get-tuple-element.45), channel_id=1, source_target_pairs={{0,1},{1,0},{2,3},{3,2},{4,5},{5,4},{6,7},{7,6},{8,9},{9,8},{10,11... | collective-permute-start | bytes 1572872 | tf_op jit(solution)/shard_map/ppermute | solution.py:34
  55.6 2.4 %collective-permute-start.27 = (bf16[64,8,512]{2,1,0:T(8,128)(2,1)S(1)}, bf16[64,8,512]{2,1,0:T(8,128)(2,1)S(1)}, u32[]{:S(2)}, u32[]{:S(2)}) collective-permute-start(bf16[64,8,512]{2,1,0:T(8,128)(2,1)S(1)} %get-tuple-element.52), channel_id=1, source_target_pairs={{0,1},{1,0},{2,3},{3,2},{4,5},{5,4},{6,7},{7,6},{8,9},{9,8},{10,11... | collective-permute-start | bytes 1572872 | tf_op jit(solution)/shard_map/ppermute | solution.py:34
  57.4 8.5 %collective-permute-start.24 = (bf16[32,8,512]{2,1,0:T(8,128)(2,1)S(1)}, bf16[32,8,512]{2,1,0:T(8,128)(2,1)S(1)}, u32[]{:S(2)}, u32[]{:S(2)}) collective-permute-start(bf16[32,8,512]{2,1,0:T(8,128)(2,1)S(1)} %get-tuple-element.47), channel_id=1, source_target_pairs={{0,4},{1,5},{2,6},{3,7},{4,0},{5,1},{6,2},{7,3},{8,12},{9,13},{10,... | collective-permute-start | bytes 786440 | tf_op jit(solution)/shard_map/ppermute | solution.py:34
  58.1 8.5 %collective-permute-start.28 = (bf16[32,8,512]{2,1,0:T(8,128)(2,1)S(1)}, bf16[32,8,512]{2,1,0:T(8,128)(2,1)S(1)}, u32[]{:S(2)}, u32[]{:S(2)}) collective-permute-start(bf16[32,8,512]{2,1,0:T(8,128)(2,1)S(1)} %get-tuple-element.54), channel_id=1, source_target_pairs={{0,2},{1,3},{2,0},{3,1},{4,6},{5,7},{6,4},{7,5},{8,10},{9,11},{10,... | collective-permute-start | bytes 786440 | tf_op jit(solution)/shard_map/ppermute | solution.py:34
  65.9 5.0 %collective-permute-start.25 = (bf16[16,8,512]{2,1,0:T(8,128)(2,1)S(1)}, bf16[16,8,512]{2,1,0:T(8,128)(2,1)S(1)}, u32[]{:S(2)}, u32[]{:S(2)}) collective-permute-start(bf16[16,8,512]{2,1,0:T(8,128)(2,1)S(1)} %get-tuple-element.49), channel_id=1, source_target_pairs={{0,2},{1,3},{2,0},{3,1},{4,6},{5,7},{6,4},{7,5},{8,10},{9,11},{10,... | collective-permute-start | bytes 393224 | tf_op jit(solution)/shard_map/ppermute | solution.py:34
  66.7 6.6 %collective-permute-start.29 = (bf16[16,8,512]{2,1,0:T(8,128)(2,1)S(1)}, bf16[16,8,512]{2,1,0:T(8,128)(2,1)S(1)}, u32[]{:S(2)}, u32[]{:S(2)}) collective-permute-start(bf16[16,8,512]{2,1,0:T(8,128)(2,1)S(1)} %get-tuple-element.56), channel_id=1, source_target_pairs={{0,4},{1,5},{2,6},{3,7},{4,0},{5,1},{6,2},{7,3},{8,12},{9,13},{10,... | collective-permute-start | bytes 393224 | tf_op jit(solution)/shard_map/ppermute | solution.py:34
  71.0 6.5 %collective-permute-start.26 = (bf16[8,8,512]{2,1,0:T(8,128)(2,1)S(1)}, bf16[8,8,512]{2,1,0:T(8,128)(2,1)S(1)}, u32[]{:S(2)}, u32[]{:S(2)}) collective-permute-start(bf16[8,8,512]{2,1,0:T(8,128)(2,1)S(1)} %get-tuple-element.51), channel_id=1, source_target_pairs={{0,8},{1,9},{2,10},{3,11},{4,12},{5,13},{6,14},{7,15},{8,0},{9,1},... | collective-permute-start | bytes 196616 | tf_op jit(solution)/shard_map/ppermute | solution.py:34
  73.3 5.8 %collective-permute-start.30 = (bf16[8,8,512]{2,1,0:T(8,128)(2,1)S(1)}, bf16[8,8,512]{2,1,0:T(8,128)(2,1)S(1)}, u32[]{:S(2)}, u32[]{:S(2)}) collective-permute-start(bf16[8,8,512]{2,1,0:T(8,128)(2,1)S(1)} %get-tuple-element.58), channel_id=1, source_target_pairs={{0,8},{1,9},{2,10},{3,11},{4,12},{5,13},{6,14},{7,15},{8,0},{9,1},... | collective-permute-start | bytes 196616 | tf_op jit(solution)/shard_map/ppermute | solution.py:34

commit v14 on v13

--- a/solution.py
+++ b/solution.py
@@ -274,8 +274,9 @@
         span = peers // 2
         away = col_owner ^ me
         is_q = col_local >= half
-        spot = jnp.where(is_q, place(away, orders[1]) + (span - 1), place(away, orders[0]))
-        table[0:1, :] = (away & 1) * (span * cell_blocks) + spot * half + col_local
+        for row, (order_p, order_q) in zip((0, 3), orders):
+            spot = jnp.where(is_q, place(away, order_q) + (span - 1), place(away, order_p))
+            table[row : row + 1, :] = (away & 1) * (span * cell_blocks) + spot * half + col_local
         away = row_owner ^ me
         spot = (away & 1) * 4 + ((away & 4) // 2) + ((away & 2) // 2)
         table[1:2, :] = (spot * rest + row_owner // 8) * station_blocks + row_local
@@ -318,7 +319,8 @@
     station_blocks = station_weight.shape[0] // (peers * station_width)
     bits = [1 << k for k in range(1, peers.bit_length() - 1)]
     far = bits[:0:-1]
-    orders = (far[:1] + bits[:1] + far[1:], far + bits[:1])
+    gather = (bits[:1] + far, far + bits[:1])
+    scatter = (far[:1] + bits[:1] + far[1:], far + bits[:1])
 
     lanes = (cell_total // LANES, LANES)
     half_dims = (cell_blocks // 2, probe_count, cell_width)
@@ -342,12 +344,12 @@
     table, weight = plan(
         [a.reshape(peers, tile_count) for a in (col_owner, col_local, row_owner, row_local, tile_rank)],
         station_weight.reshape(-1, LANES),
-        orders,
+        (gather, scatter),
         cell_blocks,
         station_blocks,
         (scaling,),
     )
-    steps = list(zip(*orders))
+    steps = list(zip(*gather))
     after = (weight,)
     for step, (bit_p, bit_q) in enumerate(steps):
         got_p = swap(part_p, bit_p)
@@ -378,10 +380,10 @@
     pieces = [weighted, around, swap(weighted, 1), swap(around, 1)]
 
     acc = zeros((peers * cell_blocks, probe_count, cell_width), (total,))
-    total, send_p, send_q = tiles(pieces, 1, 0, table, u_here, v_here, acc, 2, BF16, "adjoint")
+    total, send_p, send_q = tiles(pieces, 1, 3, table, u_here, v_here, acc, 2, BF16, "adjoint")
     keep_p, send_p = fold(total, swap(send_p, 1))
     keep_q, send_q = fold(total, swap(send_q, 1), base=total.shape[0] // 4)
-    for step, (bit_p, bit_q) in enumerate(steps[::-1]):
+    for step, (bit_p, bit_q) in enumerate(list(zip(*scatter))[::-1]):
         if step > 0:
             keep_p, send_p = fold(keep_p, got_p)
             keep_q, send_q = fold(keep_q, got_q)

time: 80.2 us -> 79 us (0.985)
  waiting for transfers between devices: 37.2 us -> 35.8 us
    ppermute x31, waiting for transfers between devices: 37.2 us -> 35.8 us  [swap(): return lax.ppermute(array, 'tile', [(i, i ^ bits) for i in range(count)])]
  transfers between devices with their start and end apart: 31 -> 31, of which waited for: 21 -> 20; matrix products, arithmetic and copies ran while one was open for 0% -> 0% of each run, Pallas kernels for 8% -> 8%
where the time goes in v14:
time: 79 us; the launch traced here: 78.7 us
  waiting for transfers between devices  35.8 us (45%)
  starting transfers between devices  29.8 us (38%)
  Pallas kernels  12.9 us (16%)
    ppermute x31, waiting for transfers between devices, swap(): return lax.ppermute(array, 'tile', [(i, i ^ bits) for i in range(count)])  35.8 us
    ppermute x31, starting transfers between devices, swap(): return lax.ppermute(array, 'tile', [(i, i ^ bits) for i in range(count)])  29.8 us
    pallas_call x26, Pallas kernels, local(): pl.pallas_call(run, out_shape=[a if s.memory_space is None else s.memory_...  12.9 us
  transfers between devices with their start and end apart: 31, of which 20 were waited for; matrix products, arithmetic and copies ran while one was open for 0% of the time, Pallas kernels for 8%

profile of v14, /device:TPU:0, one launch (start us, length us, event | category | flops | bytes accessed | tf_op | source)
XLA Modules:
  0.0 78.7 jit_solution(16560726528698865764)
XLA Ops:
  0.0 1.1 %scale.1 = (bf16[8,8,512]{2,1,0:T(8,128)(2,1)S(1)}, bf16[8,8,512]{2,1,0:T(8,128)(2,1)S(1)}, f32[64,128]{1,0:T(8,128)S(1)}) custom-call(f32[4]{0:T(128)} %refs_0_.3, f32[64,128]{1,0:T(8,128)} %bitcast.9, s32[64,128]{1,0:T(8,128)} %bitcast.10, f32[8,8192]{1,0:T(8,128)} %refs_3_.1), custom_call_target="tpu_custom_call" | custom-call | bytes 491536 | tf_op jit(solution)/shard_map/scale/pallas_call | solution.py:49
  1.1 4.1 %collective-permute-start.2 = (bf16[8,8,512]{2,1,0:T(8,128)(2,1)S(1)}, bf16[8,8,512]{2,1,0:T(8,128)(2,1)S(1)}, u32[]{:S(2)}, u32[]{:S(2)}) collective-permute-start(bf16[8,8,512]{2,1,0:T(8,128)(2,1)S(1)} %get-tuple-element.36.refs_0_), channel_id=1, source_target_pairs={{0,8},{1,9},{2,10},{3,11},{4,12},{5,13},{6,14},{7,15},{8,0},{9,1},... | collective-permute-start | bytes 196616 | tf_op jit(solution)/shard_map/ppermute | solution.py:34
  5.2 1.5 %collective-permute-start = (bf16[8,8,512]{2,1,0:T(8,128)(2,1)S(1)}, bf16[8,8,512]{2,1,0:T(8,128)(2,1)S(1)}, u32[]{:S(2)}, u32[]{:S(2)}) collective-permute-start(bf16[8,8,512]{2,1,0:T(8,128)(2,1)S(1)} %get-tuple-element.34.refs_0_), channel_id=1, source_target_pairs={{0,2},{1,3},{2,0},{3,1},{4,6},{5,7},{6,4},{7,5},{8,10},{9,11},{10,... | collective-permute-start | bytes 196616 | tf_op jit(solution)/shard_map/ppermute | solution.py:34
  6.7 1.5 %plan.1 = (s32[8,128]{1,0:T(8,128)S(4)}, f32[32,128]{1,0:T(8,128)S(1)}) custom-call(s32[16,128]{1,0:T(8,128)} %bitcast.11, s32[16,128]{1,0:T(8,128)} %bitcast.12, s32[16,128]{1,0:T(8,128)} %bitcast.13, s32[16,128]{1,0:T(8,128)} %bitcast.14, s32[16,128]{1,0:T(8,128)} %bitcast.15, f32[256,128]{1,0:T(8,128)} %bitcast.8, ...), custom_call_target="tpu_custom_call" | custom-call | bytes 192512 | tf_op jit(solution)/shard_map/plan/pallas_call | solution.py:49
  8.2 0.6 collective-permute-done.2.refs_1_
  8.8 1.0 %collective-permute-start.3 = (bf16[16,8,512]{2,1,0:T(8,128)(2,1)S(1)}, bf16[16,8,512]{2,1,0:T(8,128)(2,1)S(1)}, u32[]{:S(2)}, u32[]{:S(2)}) collective-permute-start(bf16[16,8,512]{2,1,0:T(8,128)(2,1)S(1)} %join.6.refs_2_.refs_0_), channel_id=1, source_target_pairs={{0,4},{1,5},{2,6},{3,7},{4,0},{5,1},{6,2},{7,3},{8,12},{9,13},{10,... | collective-permute-start | bytes 393224 | tf_op jit(solution)/shard_map/ppermute | solution.py:34
  9.9 3.1 %collective-permute-start.1 = (bf16[16,8,512]{2,1,0:T(8,128)(2,1)S(1)}, bf16[16,8,512]{2,1,0:T(8,128)(2,1)S(1)}, u32[]{:S(2)}, u32[]{:S(2)}) collective-permute-start(bf16[16,8,512]{2,1,0:T(8,128)(2,1)S(1)} %join.5.refs_1_.refs_0_), channel_id=1, source_target_pairs={{0,8},{1,9},{2,10},{3,11},{4,12},{5,13},{6,14},{7,15},{8,0},{9,1},... | collective-permute-start | bytes 393224 | tf_op jit(solution)/shard_map/ppermute | solution.py:34
  12.9 2.2 %load_v.1.refs_3_.refs_10_.refs_7_ = bf16[128,32,512]{2,1,0:T(8,128)(2,1)S(1)} custom-call(bf16[128,32,512]{2,1,0:T(8,128)(2,1)} %refs_0_.4, bf16[16,8,512]{2,1,0:T(8,128)(2,1)S(1)} %join.5.refs_1_.refs_0_, bf16[16,8,512]{2,1,0:T(8,128)(2,1)S(1)} %join.6.refs_2_.refs_0_), custom_call_target="tpu_custom_call" | custom-call | bytes 8388608 | tf_op jit(solution)/shard_map/load_v/pallas_call | solution.py:49
  15.2 2.2 %load_u.1.refs_2_.refs_11_.refs_6_ = bf16[128,32,512]{2,1,0:T(8,128)(2,1)S(1)} custom-call(bf16[128,32,512]{2,1,0:T(8,128)(2,1)} %refs_0_.5, bf16[16,8,512]{2,1,0:T(8,128)(2,1)S(1)} %join.5.refs_1_.refs_0_, bf16[16,8,512]{2,1,0:T(8,128)(2,1)S(1)} %join.6.refs_2_.refs_0_, bf16[128,32,512]{2,1,0:T(8,128)(2,1)S(1)} %load_v.1.refs_3_.refs_10_.refs_7_), custom_call_target="tpu_custom_call" | custom-call | bytes 8388608 | tf_op jit(solution)/shard_map/load_u/pallas_call | solution.py:49
  17.4 1.6 %collective-permute-start.5 = (bf16[32,8,512]{2,1,0:T(8,128)(2,1)S(1)}, bf16[32,8,512]{2,1,0:T(8,128)(2,1)S(1)}, u32[]{:S(2)}, u32[]{:S(2)}) collective-permute-start(bf16[32,8,512]{2,1,0:T(8,128)(2,1)S(1)} %join.8.refs_1_.refs_4_), channel_id=1, source_target_pairs={{0,2},{1,3},{2,0},{3,1},{4,6},{5,7},{6,4},{7,5},{8,10},{9,11},{10,... | collective-permute-start | bytes 786440 | tf_op jit(solution)/shard_map/ppermute | solution.py:34
  19.2 0.5 collective-permute-start.6
  19.7 5.1 %collective-permute-done.5.refs_5_ = bf16[32,8,512]{2,1,0:T(8,128)(2,1)S(1)} collective-permute-done((bf16[32,8,512]{2,1,0:T(8,128)(2,1)S(1)}, bf16[32,8,512]{2,1,0:T(8,128)(2,1)S(1)}, u32[]{:S(2)}, u32[]{:S(2)}) %collective-permute-start.5) | collective-permute-done | bytes 262176 | tf_op jit(solution)/shard_map/ppermute | solution.py:34
  24.8 1.3 %collective-permute-done.4.refs_3_ = bf16[32,8,512]{2,1,0:T(8,128)(2,1)S(1)} collective-permute-done((bf16[32,8,512]{2,1,0:T(8,128)(2,1)S(1)}, bf16[32,8,512]{2,1,0:T(8,128)(2,1)S(1)}, u32[]{:S(2)}, u32[]{:S(2)}) %collective-permute-start.4) | collective-permute-done | bytes 262176 | tf_op jit(solution)/shard_map/ppermute | solution.py:34
  26.3 1.3 %collective-permute-done.7.refs_7_ = bf16[32,8,512]{2,1,0:T(8,128)(2,1)S(1)} collective-permute-done((bf16[32,8,512]{2,1,0:T(8,128)(2,1)S(1)}, bf16[32,8,512]{2,1,0:T(8,128)(2,1)S(1)}, u32[]{:S(2)}, u32[]{:S(2)}) %collective-permute-start.7) | collective-permute-done | bytes 262176 | tf_op jit(solution)/shard_map/ppermute | solution.py:34
  27.7 2.2 %forward.1 = (f32[64,8,512]{2,1,0:T(8,128)S(1)}, f32[8,8,512]{2,1,0:T(8,128)S(1)}, f32[8,8,512]{2,1,0:T(8,128)S(1)}, f32[8,8,512]{2,1,0:T(8,128)S(1)}, f32[8,8,512]{2,1,0:T(8,128)S(1)}) custom-call(s32[8,128]{1,0:T(8,128)S(4)} %get-tuple-element.33.refs_0_, f32[64,8,512]{2,1,0:T(8,128)S(1)} %zeros.2.refs_1_, ...), custom_call_target="tpu_custom_call", output_to_operand_aliasing={{0}: (1, {})} | custom-call | flops 536870912 | bytes 13111296 | tf_op jit(solution)/shard_map/forward/pallas_call | solution.py:49
  30.1 0.4 collective-permute-start.13
  30.6 0.4 collective-permute-start.10
  31.0 0.3 collective-permute-done.11.refs_1_
  31.3 1.3 %collective-permute-start.12 = (bf16[8,8,512]{2,1,0:T(8,128)(2,1)S(1)}, bf16[8,8,512]{2,1,0:T(8,128)(2,1)S(1)}, u32[]{:S(2)}, u32[]{:S(2)}) collective-permute-start(bf16[8,8,512]{2,1,0:T(8,128)(2,1)S(1)} %fold.11), channel_id=1, source_target_pairs={{0,6},{1,7},{2,4},{3,5},{4,2},{5,3},{6,0},{7,1},{8,14},{9,15},{10,... | collective-permute-start | bytes 196616 | tf_op jit(solution)/shard_map/ppermute | solution.py:34
  32.6 0.6 collective-permute-start.14
  33.2 1.8 %collective-permute-start.16 = (bf16[8,8,512]{2,1,0:T(8,128)(2,1)S(1)}, bf16[8,8,512]{2,1,0:T(8,128)(2,1)S(1)}, u32[]{:S(2)}, u32[]{:S(2)}) collective-permute-start(bf16[8,8,512]{2,1,0:T(8,128)(2,1)S(1)} %fold.13), channel_id=1, source_target_pairs={{0,4},{1,5},{2,6},{3,7},{4,0},{5,1},{6,2},{7,3},{8,12},{9,13},{10,... | collective-permute-start | bytes 196616 | tf_op jit(solution)/shard_map/ppermute | solution.py:34
  35.1 1.7 %collective-permute-done.12.refs_1_ = bf16[8,8,512]{2,1,0:T(8,128)(2,1)S(1)} collective-permute-done((bf16[8,8,512]{2,1,0:T(8,128)(2,1)S(1)}, bf16[8,8,512]{2,1,0:T(8,128)(2,1)S(1)}, u32[]{:S(2)}, u32[]{:S(2)}) %collective-permute-start.12) | collective-permute-done | bytes 65568 | tf_op jit(solution)/shard_map/ppermute | solution.py:34
  36.8 1.1 %collective-permute-done.14.refs_2_ = bf16[8,8,512]{2,1,0:T(8,128)(2,1)S(1)} collective-permute-done((bf16[8,8,512]{2,1,0:T(8,128)(2,1)S(1)}, bf16[8,8,512]{2,1,0:T(8,128)(2,1)S(1)}, u32[]{:S(2)}, u32[]{:S(2)}) %collective-permute-start.14) | collective-permute-done | bytes 65568 | tf_op jit(solution)/shard_map/ppermute | solution.py:34
  37.9 2.3 %collective-permute-start.17 = (bf16[8,8,512]{2,1,0:T(8,128)(2,1)S(1)}, bf16[8,8,512]{2,1,0:T(8,128)(2,1)S(1)}, u32[]{:S(2)}, u32[]{:S(2)}) collective-permute-start(bf16[8,8,512]{2,1,0:T(8,128)(2,1)S(1)} %get-tuple-element.43), channel_id=1, source_target_pairs={{0,8},{1,9},{2,10},{3,11},{4,12},{5,13},{6,14},{7,15},{8,0},{9,1},... | collective-permute-start | bytes 196616 | tf_op jit(solution)/shard_map/ppermute | solution.py:34
  40.2 3.0 %collective-permute-done.17.refs_1_ = bf16[8,8,512]{2,1,0:T(8,128)(2,1)S(1)} collective-permute-done((bf16[8,8,512]{2,1,0:T(8,128)(2,1)S(1)}, bf16[8,8,512]{2,1,0:T(8,128)(2,1)S(1)}, u32[]{:S(2)}, u32[]{:S(2)}) %collective-permute-start.17) | collective-permute-done | bytes 65568 | tf_op jit(solution)/shard_map/ppermute | solution.py:34
  43.2 1.7 %collective-permute-start.20 = (bf16[8,8,512]{2,1,0:T(8,128)(2,1)S(1)}, bf16[8,8,512]{2,1,0:T(8,128)(2,1)S(1)}, u32[]{:S(2)}, u32[]{:S(2)}) collective-permute-start(bf16[8,8,512]{2,1,0:T(8,128)(2,1)S(1)} %weigh.1.refs_2_), channel_id=1, source_target_pairs={{0,6},{1,7},{2,4},{3,5},{4,2},{5,3},{6,0},{7,1},{8,14},{9,15},{10,... | collective-permute-start | bytes 196616 | tf_op jit(solution)/shard_map/ppermute | solution.py:34
  44.9 1.7 %collective-permute-start.19 = (bf16[8,8,512]{2,1,0:T(8,128)(2,1)S(1)}, bf16[8,8,512]{2,1,0:T(8,128)(2,1)S(1)}, u32[]{:S(2)}, u32[]{:S(2)}) collective-permute-start(bf16[8,8,512]{2,1,0:T(8,128)(2,1)S(1)} %weigh.1.refs_2_), channel_id=1, source_target_pairs={{0,4},{1,5},{2,6},{3,7},{4,0},{5,1},{6,2},{7,3},{8,12},{9,13},{10,... | collective-permute-start | bytes 196616 | tf_op jit(solution)/shard_map/ppermute | solution.py:34
  46.8 1.7 %collective-permute-done.20.refs_2_ = bf16[8,8,512]{2,1,0:T(8,128)(2,1)S(1)} collective-permute-done((bf16[8,8,512]{2,1,0:T(8,128)(2,1)S(1)}, bf16[8,8,512]{2,1,0:T(8,128)(2,1)S(1)}, u32[]{:S(2)}, u32[]{:S(2)}) %collective-permute-start.20) | collective-permute-done | bytes 65568 | tf_op jit(solution)/shard_map/ppermute | solution.py:34
  48.4 1.1 %collective-permute-done.19.refs_1_ = bf16[8,8,512]{2,1,0:T(8,128)(2,1)S(1)} collective-permute-done((bf16[8,8,512]{2,1,0:T(8,128)(2,1)S(1)}, bf16[8,8,512]{2,1,0:T(8,128)(2,1)S(1)}, u32[]{:S(2)}, u32[]{:S(2)}) %collective-permute-start.19) | collective-permute-done | bytes 65568 | tf_op jit(solution)/shard_map/ppermute | solution.py:34
  49.5 1.3 %collective-permute-done.18.refs_0_ = bf16[8,8,512]{2,1,0:T(8,128)(2,1)S(1)} collective-permute-done((bf16[8,8,512]{2,1,0:T(8,128)(2,1)S(1)}, bf16[8,8,512]{2,1,0:T(8,128)(2,1)S(1)}, u32[]{:S(2)}, u32[]{:S(2)}) %collective-permute-start.18) | collective-permute-done | bytes 65568 | tf_op jit(solution)/shard_map/ppermute | solution.py:34
  50.9 0.5 collective-permute-start.21
  51.4 0.3 zeros.3.refs_1_
  51.7 0.7 collective-permute-done.21.refs_4_
  52.4 2.2 %adjoint.1 = (f32[256,8,512]{2,1,0:T(8,128)S(1)}, bf16[64,8,512]{2,1,0:T(8,128)(2,1)S(1)}, bf16[64,8,512]{2,1,0:T(8,128)(2,1)S(1)}) custom-call(s32[8,128]{1,0:T(8,128)S(4)} %get-tuple-element.33.refs_0_, f32[256,8,512]{2,1,0:T(8,128)S(1)} %zeros.3.refs_1_, bf16[8,8,512]{2,1,0:T(8,128)(2,1)S(1)} %weigh.1.refs_2_, ...), custom_call_target="tpu_custom_call", output_to_operand_aliasing={{0}: (1, {})} | custom-call | flops 536870912 | bytes 18354176 | tf_op jit(solution)/shard_map/adjoint/pallas_call | solution.py:49
  54.6 0.3 collective-permute-start.23
  54.9 0.3 collective-permute-start.27
  55.2 1.4 %collective-permute-done.23.refs_1_ = bf16[64,8,512]{2,1,0:T(8,128)(2,1)S(1)} collective-permute-done((bf16[64,8,512]{2,1,0:T(8,128)(2,1)S(1)}, bf16[64,8,512]{2,1,0:T(8,128)(2,1)S(1)}, u32[]{:S(2)}, u32[]{:S(2)}) %collective-permute-start.23) | collective-permute-done | bytes 524320 | tf_op jit(solution)/shard_map/ppermute | solution.py:34
  56.7 0.4 collective-permute-start.24
  57.4 1.1 %collective-permute-start.28 = (bf16[32,8,512]{2,1,0:T(8,128)(2,1)S(1)}, bf16[32,8,512]{2,1,0:T(8,128)(2,1)S(1)}, u32[]{:S(2)}, u32[]{:S(2)}) collective-permute-start(bf16[32,8,512]{2,1,0:T(8,128)(2,1)S(1)} %get-tuple-element.54), channel_id=1, source_target_pairs={{0,2},{1,3},{2,0},{3,1},{4,6},{5,7},{6,4},{7,5},{8,10},{9,11},{10,... | collective-permute-start | bytes 786440 | tf_op jit(solution)/shard_map/ppermute | solution.py:34
  58.5 6.7 %collective-permute-done.24.refs_1_ = bf16[32,8,512]{2,1,0:T(8,128)(2,1)S(1)} collective-permute-done((bf16[32,8,512]{2,1,0:T(8,128)(2,1)S(1)}, bf16[32,8,512]{2,1,0:T(8,128)(2,1)S(1)}, u32[]{:S(2)}, u32[]{:S(2)}) %collective-permute-start.24) | collective-permute-done | bytes 262176 | tf_op jit(solution)/shard_map/ppermute | solution.py:34
  65.5 0.4 collective-permute-done.28.refs_1_
  66.0 1.2 %collective-permute-start.29 = (bf16[16,8,512]{2,1,0:T(8,128)(2,1)S(1)}, bf16[16,8,512]{2,1,0:T(8,128)(2,1)S(1)}, u32[]{:S(2)}, u32[]{:S(2)}) collective-permute-start(bf16[16,8,512]{2,1,0:T(8,128)(2,1)S(1)} %get-tuple-element.56), channel_id=1, source_target_pairs={{0,4},{1,5},{2,6},{3,7},{4,0},{5,1},{6,2},{7,3},{8,12},{9,13},{10,... | collective-permute-start | bytes 393224 | tf_op jit(solution)/shard_map/ppermute | solution.py:34
  67.2 3.1 %collective-permute-done.25.refs_1_ = bf16[16,8,512]{2,1,0:T(8,128)(2,1)S(1)} collective-permute-done((bf16[16,8,512]{2,1,0:T(8,128)(2,1)S(1)}, bf16[16,8,512]{2,1,0:T(8,128)(2,1)S(1)}, u32[]{:S(2)}, u32[]{:S(2)}) %collective-permute-start.25) | collective-permute-done | bytes 131104 | tf_op jit(solution)/shard_map/ppermute | solution.py:34
  70.3 1.9 %collective-permute-start.26 = (bf16[8,8,512]{2,1,0:T(8,128)(2,1)S(1)}, bf16[8,8,512]{2,1,0:T(8,128)(2,1)S(1)}, u32[]{:S(2)}, u32[]{:S(2)}) collective-permute-start(bf16[8,8,512]{2,1,0:T(8,128)(2,1)S(1)} %get-tuple-element.51), channel_id=1, source_target_pairs={{0,8},{1,9},{2,10},{3,11},{4,12},{5,13},{6,14},{7,15},{8,0},{9,1},... | collective-permute-start | bytes 196616 | tf_op jit(solution)/shard_map/ppermute | solution.py:34
  72.3 1.1 %collective-permute-start.30 = (bf16[8,8,512]{2,1,0:T(8,128)(2,1)S(1)}, bf16[8,8,512]{2,1,0:T(8,128)(2,1)S(1)}, u32[]{:S(2)}, u32[]{:S(2)}) collective-permute-start(bf16[8,8,512]{2,1,0:T(8,128)(2,1)S(1)} %get-tuple-element.58), channel_id=1, source_target_pairs={{0,8},{1,9},{2,10},{3,11},{4,12},{5,13},{6,14},{7,15},{8,0},{9,1},... | collective-permute-start | bytes 196616 | tf_op jit(solution)/shard_map/ppermute | solution.py:34
  73.4 2.9 %collective-permute-done.26.refs_1_ = bf16[8,8,512]{2,1,0:T(8,128)(2,1)S(1)} collective-permute-done((bf16[8,8,512]{2,1,0:T(8,128)(2,1)S(1)}, bf16[8,8,512]{2,1,0:T(8,128)(2,1)S(1)}, u32[]{:S(2)}, u32[]{:S(2)}) %collective-permute-start.26) | collective-permute-done | bytes 65568 | tf_op jit(solution)/shard_map/ppermute | solution.py:34
  76.4 1.6 %collective-permute-done.30.refs_3_ = bf16[8,8,512]{2,1,0:T(8,128)(2,1)S(1)} collective-permute-done((bf16[8,8,512]{2,1,0:T(8,128)(2,1)S(1)}, bf16[8,8,512]{2,1,0:T(8,128)(2,1)S(1)}, u32[]{:S(2)}, u32[]{:S(2)}) %collective-permute-start.30) | collective-permute-done | bytes 65568 | tf_op jit(solution)/shard_map/ppermute | solution.py:34
  77.9 0.7 final.1
  (40 shorter events, 2.0 us)
Async XLA Ops:
  1.1 7.8 %collective-permute-start.2 = (bf16[8,8,512]{2,1,0:T(8,128)(2,1)S(1)}, bf16[8,8,512]{2,1,0:T(8,128)(2,1)S(1)}, u32[]{:S(2)}, u32[]{:S(2)}) collective-permute-start(bf16[8,8,512]{2,1,0:T(8,128)(2,1)S(1)} %get-tuple-element.36.refs_0_), channel_id=1, source_target_pairs={{0,8},{1,9},{2,10},{3,11},{4,12},{5,13},{6,14},{7,15},{8,0},{9,1},... | collective-permute-start | bytes 196616 | tf_op jit(solution)/shard_map/ppermute | solution.py:34
  5.2 4.7 %collective-permute-start = (bf16[8,8,512]{2,1,0:T(8,128)(2,1)S(1)}, bf16[8,8,512]{2,1,0:T(8,128)(2,1)S(1)}, u32[]{:S(2)}, u32[]{:S(2)}) collective-permute-start(bf16[8,8,512]{2,1,0:T(8,128)(2,1)S(1)} %get-tuple-element.34.refs_0_), channel_id=1, source_target_pairs={{0,2},{1,3},{2,0},{3,1},{4,6},{5,7},{6,4},{7,5},{8,10},{9,11},{10,... | collective-permute-start | bytes 196616 | tf_op jit(solution)/shard_map/ppermute | solution.py:34
  8.8 8.5 %collective-permute-start.3 = (bf16[16,8,512]{2,1,0:T(8,128)(2,1)S(1)}, bf16[16,8,512]{2,1,0:T(8,128)(2,1)S(1)}, u32[]{:S(2)}, u32[]{:S(2)}) collective-permute-start(bf16[16,8,512]{2,1,0:T(8,128)(2,1)S(1)} %join.6.refs_2_.refs_0_), channel_id=1, source_target_pairs={{0,4},{1,5},{2,6},{3,7},{4,0},{5,1},{6,2},{7,3},{8,12},{9,13},{10,... | collective-permute-start | bytes 393224 | tf_op jit(solution)/shard_map/ppermute | solution.py:34
  9.9 9.1 %collective-permute-start.1 = (bf16[16,8,512]{2,1,0:T(8,128)(2,1)S(1)}, bf16[16,8,512]{2,1,0:T(8,128)(2,1)S(1)}, u32[]{:S(2)}, u32[]{:S(2)}) collective-permute-start(bf16[16,8,512]{2,1,0:T(8,128)(2,1)S(1)} %join.5.refs_1_.refs_0_), channel_id=1, source_target_pairs={{0,8},{1,9},{2,10},{3,11},{4,12},{5,13},{6,14},{7,15},{8,0},{9,1},... | collective-permute-start | bytes 393224 | tf_op jit(solution)/shard_map/ppermute | solution.py:34
  17.4 7.4 %collective-permute-start.5 = (bf16[32,8,512]{2,1,0:T(8,128)(2,1)S(1)}, bf16[32,8,512]{2,1,0:T(8,128)(2,1)S(1)}, u32[]{:S(2)}, u32[]{:S(2)}) collective-permute-start(bf16[32,8,512]{2,1,0:T(8,128)(2,1)S(1)} %join.8.refs_1_.refs_4_), channel_id=1, source_target_pairs={{0,2},{1,3},{2,0},{3,1},{4,6},{5,7},{6,4},{7,5},{8,10},{9,11},{10,... | collective-permute-start | bytes 786440 | tf_op jit(solution)/shard_map/ppermute | solution.py:34
  19.0 7.1 %collective-permute-start.4 = (bf16[32,8,512]{2,1,0:T(8,128)(2,1)S(1)}, bf16[32,8,512]{2,1,0:T(8,128)(2,1)S(1)}, u32[]{:S(2)}, u32[]{:S(2)}) collective-permute-start(bf16[32,8,512]{2,1,0:T(8,128)(2,1)S(1)} %join.7.refs_0_.refs_2_), channel_id=1, source_target_pairs={{0,4},{1,5},{2,6},{3,7},{4,0},{5,1},{6,2},{7,3},{8,12},{9,13},{10,... | collective-permute-start | bytes 786440 | tf_op jit(solution)/shard_map/ppermute | solution.py:34
  19.2 7.0 %collective-permute-start.8 = (bf16[32,8,512]{2,1,0:T(8,128)(2,1)S(1)}, bf16[32,8,512]{2,1,0:T(8,128)(2,1)S(1)}, u32[]{:S(2)}, u32[]{:S(2)}) collective-permute-start(bf16[32,8,512]{2,1,0:T(8,128)(2,1)S(1)} %join.8.refs_1_.refs_4_), channel_id=1, source_target_pairs={{0,1},{1,0},{2,3},{3,2},{4,5},{5,4},{6,7},{7,6},{8,9},{9,8},{10,11... | collective-permute-start | bytes 786440 | tf_op jit(solution)/shard_map/ppermute | solution.py:34
  19.2 7.0 %collective-permute-start.6 = (bf16[32,8,512]{2,1,0:T(8,128)(2,1)S(1)}, bf16[32,8,512]{2,1,0:T(8,128)(2,1)S(1)}, u32[]{:S(2)}, u32[]{:S(2)}) collective-permute-start(bf16[32,8,512]{2,1,0:T(8,128)(2,1)S(1)} %join.7.refs_0_.refs_2_), channel_id=1, source_target_pairs={{0,1},{1,0},{2,3},{3,2},{4,5},{5,4},{6,7},{7,6},{8,9},{9,8},{10,11... | collective-permute-start | bytes 786440 | tf_op jit(solution)/shard_map/ppermute | solution.py:34
  24.8 1.5 %collective-permute-start.9 = (bf16[32,8,512]{2,1,0:T(8,128)(2,1)S(1)}, bf16[32,8,512]{2,1,0:T(8,128)(2,1)S(1)}, u32[]{:S(2)}, u32[]{:S(2)}) collective-permute-start(bf16[32,8,512]{2,1,0:T(8,128)(2,1)S(1)} %collective-permute-done.5.refs_5_), channel_id=1, source_target_pairs={{0,1},{1,0},{2,3},{3,2},{4,5},{5,4},{6,7},{7,6},{8,9},{9,8},{10,11... | collective-permute-start | bytes 786440 | tf_op jit(solution)/shard_map/ppermute | solution.py:34
  26.1 1.5 %collective-permute-start.7 = (bf16[32,8,512]{2,1,0:T(8,128)(2,1)S(1)}, bf16[32,8,512]{2,1,0:T(8,128)(2,1)S(1)}, u32[]{:S(2)}, u32[]{:S(2)}) collective-permute-start(bf16[32,8,512]{2,1,0:T(8,128)(2,1)S(1)} %collective-permute-done.4.refs_3_), channel_id=1, source_target_pairs={{0,1},{1,0},{2,3},{3,2},{4,5},{5,4},{6,7},{7,6},{8,9},{9,8},{10,11... | collective-permute-start | bytes 786440 | tf_op jit(solution)/shard_map/ppermute | solution.py:34
  29.9 1.4 %collective-permute-start.11 = (f32[8,8,512]{2,1,0:T(8,128)S(1)}, f32[8,8,512]{2,1,0:T(8,128)S(1)}, u32[]{:S(2)}, u32[]{:S(2)}) collective-permute-start(f32[8,8,512]{2,1,0:T(8,128)S(1)} %get-tuple-element.39), channel_id=1, source_target_pairs={{0,1},{1,0},{2,3},{3,2},{4,5},{5,4},{6,7},{7,6},{8,9},{9,8},{10,11... | collective-permute-start | bytes 393224 | tf_op jit(solution)/shard_map/ppermute | solution.py:34
  30.1 2.5 %collective-permute-start.13 = (f32[8,8,512]{2,1,0:T(8,128)S(1)}, f32[8,8,512]{2,1,0:T(8,128)S(1)}, u32[]{:S(2)}, u32[]{:S(2)}) collective-permute-start(f32[8,8,512]{2,1,0:T(8,128)S(1)} %get-tuple-element.40), channel_id=1, source_target_pairs={{0,1},{1,0},{2,3},{3,2},{4,5},{5,4},{6,7},{7,6},{8,9},{9,8},{10,11... | collective-permute-start | bytes 393224 | tf_op jit(solution)/shard_map/ppermute | solution.py:34
  30.4 2.8 %collective-permute-start.15 = (f32[8,8,512]{2,1,0:T(8,128)S(1)}, f32[8,8,512]{2,1,0:T(8,128)S(1)}, u32[]{:S(2)}, u32[]{:S(2)}) collective-permute-start(f32[8,8,512]{2,1,0:T(8,128)S(1)} %get-tuple-element.41), channel_id=1, source_target_pairs={{0,1},{1,0},{2,3},{3,2},{4,5},{5,4},{6,7},{7,6},{8,9},{9,8},{10,11... | collective-permute-start | bytes 393224 | tf_op jit(solution)/shard_map/ppermute | solution.py:34
  30.6 4.5 %collective-permute-start.10 = (f32[8,8,512]{2,1,0:T(8,128)S(1)}, f32[8,8,512]{2,1,0:T(8,128)S(1)}, u32[]{:S(2)}, u32[]{:S(2)}) collective-permute-start(f32[8,8,512]{2,1,0:T(8,128)S(1)} %get-tuple-element.38), channel_id=1, source_target_pairs={{0,1},{1,0},{2,3},{3,2},{4,5},{5,4},{6,7},{7,6},{8,9},{9,8},{10,11... | collective-permute-start | bytes 393224 | tf_op jit(solution)/shard_map/ppermute | solution.py:34
  31.3 5.4 %collective-permute-start.12 = (bf16[8,8,512]{2,1,0:T(8,128)(2,1)S(1)}, bf16[8,8,512]{2,1,0:T(8,128)(2,1)S(1)}, u32[]{:S(2)}, u32[]{:S(2)}) collective-permute-start(bf16[8,8,512]{2,1,0:T(8,128)(2,1)S(1)} %fold.11), channel_id=1, source_target_pairs={{0,6},{1,7},{2,4},{3,5},{4,2},{5,3},{6,0},{7,1},{8,14},{9,15},{10,... | collective-permute-start | bytes 196616 | tf_op jit(solution)/shard_map/ppermute | solution.py:34
  32.6 5.2 %collective-permute-start.14 = (bf16[8,8,512]{2,1,0:T(8,128)(2,1)S(1)}, bf16[8,8,512]{2,1,0:T(8,128)(2,1)S(1)}, u32[]{:S(2)}, u32[]{:S(2)}) collective-permute-start(bf16[8,8,512]{2,1,0:T(8,128)(2,1)S(1)} %fold.12), channel_id=1, source_target_pairs={{0,2},{1,3},{2,0},{3,1},{4,6},{5,7},{6,4},{7,5},{8,10},{9,11},{10,... | collective-permute-start | bytes 196616 | tf_op jit(solution)/shard_map/ppermute | solution.py:34
  33.2 4.6 %collective-permute-start.16 = (bf16[8,8,512]{2,1,0:T(8,128)(2,1)S(1)}, bf16[8,8,512]{2,1,0:T(8,128)(2,1)S(1)}, u32[]{:S(2)}, u32[]{:S(2)}) collective-permute-start(bf16[8,8,512]{2,1,0:T(8,128)(2,1)S(1)} %fold.13), channel_id=1, source_target_pairs={{0,4},{1,5},{2,6},{3,7},{4,0},{5,1},{6,2},{7,3},{8,12},{9,13},{10,... | collective-permute-start | bytes 196616 | tf_op jit(solution)/shard_map/ppermute | solution.py:34
  37.9 5.3 %collective-permute-start.17 = (bf16[8,8,512]{2,1,0:T(8,128)(2,1)S(1)}, bf16[8,8,512]{2,1,0:T(8,128)(2,1)S(1)}, u32[]{:S(2)}, u32[]{:S(2)}) collective-permute-start(bf16[8,8,512]{2,1,0:T(8,128)(2,1)S(1)} %get-tuple-element.43), channel_id=1, source_target_pairs={{0,8},{1,9},{2,10},{3,11},{4,12},{5,13},{6,14},{7,15},{8,0},{9,1},... | collective-permute-start | bytes 196616 | tf_op jit(solution)/shard_map/ppermute | solution.py:34
  43.2 5.2 %collective-permute-start.20 = (bf16[8,8,512]{2,1,0:T(8,128)(2,1)S(1)}, bf16[8,8,512]{2,1,0:T(8,128)(2,1)S(1)}, u32[]{:S(2)}, u32[]{:S(2)}) collective-permute-start(bf16[8,8,512]{2,1,0:T(8,128)(2,1)S(1)} %weigh.1.refs_2_), channel_id=1, source_target_pairs={{0,6},{1,7},{2,4},{3,5},{4,2},{5,3},{6,0},{7,1},{8,14},{9,15},{10,... | collective-permute-start | bytes 196616 | tf_op jit(solution)/shard_map/ppermute | solution.py:34
  44.9 4.6 %collective-permute-start.19 = (bf16[8,8,512]{2,1,0:T(8,128)(2,1)S(1)}, bf16[8,8,512]{2,1,0:T(8,128)(2,1)S(1)}, u32[]{:S(2)}, u32[]{:S(2)}) collective-permute-start(bf16[8,8,512]{2,1,0:T(8,128)(2,1)S(1)} %weigh.1.refs_2_), channel_id=1, source_target_pairs={{0,4},{1,5},{2,6},{3,7},{4,0},{5,1},{6,2},{7,3},{8,12},{9,13},{10,... | collective-permute-start | bytes 196616 | tf_op jit(solution)/shard_map/ppermute | solution.py:34
  46.6 4.3 %collective-permute-start.18 = (bf16[8,8,512]{2,1,0:T(8,128)(2,1)S(1)}, bf16[8,8,512]{2,1,0:T(8,128)(2,1)S(1)}, u32[]{:S(2)}, u32[]{:S(2)}) collective-permute-start(bf16[8,8,512]{2,1,0:T(8,128)(2,1)S(1)} %weigh.1.refs_2_), channel_id=1, source_target_pairs={{0,2},{1,3},{2,0},{3,1},{4,6},{5,7},{6,4},{7,5},{8,10},{9,11},{10,... | collective-permute-start | bytes 196616 | tf_op jit(solution)/shard_map/ppermute | solution.py:34
  50.8 1.6 %collective-permute-start.22 = (bf16[24,8,512]{2,1,0:T(8,128)(2,1)S(1)}, bf16[24,8,512]{2,1,0:T(8,128)(2,1)S(1)}, u32[]{:S(2)}, u32[]{:S(2)}) collective-permute-start(bf16[24,8,512]{2,1,0:T(8,128)(2,1)S(1)} %join.9.refs_3_), channel_id=1, source_target_pairs={{0,1},{1,0},{2,3},{3,2},{4,5},{5,4},{6,7},{7,6},{8,9},{9,8},{10,11... | collective-permute-start | bytes 589832 | tf_op jit(solution)/shard_map/ppermute | solution.py:34
  50.9 1.5 %collective-permute-start.21 = (bf16[8,8,512]{2,1,0:T(8,128)(2,1)S(1)}, bf16[8,8,512]{2,1,0:T(8,128)(2,1)S(1)}, u32[]{:S(2)}, u32[]{:S(2)}) collective-permute-start(bf16[8,8,512]{2,1,0:T(8,128)(2,1)S(1)} %weigh.1.refs_2_), channel_id=1, source_target_pairs={{0,1},{1,0},{2,3},{3,2},{4,5},{5,4},{6,7},{7,6},{8,9},{9,8},{10,11... | collective-permute-start | bytes 196616 | tf_op jit(solution)/shard_map/ppermute | solution.py:34
  54.6 2.0 %collective-permute-start.23 = (bf16[64,8,512]{2,1,0:T(8,128)(2,1)S(1)}, bf16[64,8,512]{2,1,0:T(8,128)(2,1)S(1)}, u32[]{:S(2)}, u32[]{:S(2)}) collective-permute-start(bf16[64,8,512]{2,1,0:T(8,128)(2,1)S(1)} %get-tuple-element.45), channel_id=1, source_target_pairs={{0,1},{1,0},{2,3},{3,2},{4,5},{5,4},{6,7},{7,6},{8,9},{9,8},{10,11... | collective-permute-start | bytes 1572872 | tf_op jit(solution)/shard_map/ppermute | solution.py:34
  54.9 2.4 %collective-permute-start.27 = (bf16[64,8,512]{2,1,0:T(8,128)(2,1)S(1)}, bf16[64,8,512]{2,1,0:T(8,128)(2,1)S(1)}, u32[]{:S(2)}, u32[]{:S(2)}) collective-permute-start(bf16[64,8,512]{2,1,0:T(8,128)(2,1)S(1)} %get-tuple-element.52), channel_id=1, source_target_pairs={{0,1},{1,0},{2,3},{3,2},{4,5},{5,4},{6,7},{7,6},{8,9},{9,8},{10,11... | collective-permute-start | bytes 1572872 | tf_op jit(solution)/shard_map/ppermute | solution.py:34
  56.7 8.5 %collective-permute-start.24 = (bf16[32,8,512]{2,1,0:T(8,128)(2,1)S(1)}, bf16[32,8,512]{2,1,0:T(8,128)(2,1)S(1)}, u32[]{:S(2)}, u32[]{:S(2)}) collective-permute-start(bf16[32,8,512]{2,1,0:T(8,128)(2,1)S(1)} %get-tuple-element.47), channel_id=1, source_target_pairs={{0,4},{1,5},{2,6},{3,7},{4,0},{5,1},{6,2},{7,3},{8,12},{9,13},{10,... | collective-permute-start | bytes 786440 | tf_op jit(solution)/shard_map/ppermute | solution.py:34
  57.4 8.5 %collective-permute-start.28 = (bf16[32,8,512]{2,1,0:T(8,128)(2,1)S(1)}, bf16[32,8,512]{2,1,0:T(8,128)(2,1)S(1)}, u32[]{:S(2)}, u32[]{:S(2)}) collective-permute-start(bf16[32,8,512]{2,1,0:T(8,128)(2,1)S(1)} %get-tuple-element.54), channel_id=1, source_target_pairs={{0,2},{1,3},{2,0},{3,1},{4,6},{5,7},{6,4},{7,5},{8,10},{9,11},{10,... | collective-permute-start | bytes 786440 | tf_op jit(solution)/shard_map/ppermute | solution.py:34
  65.3 5.0 %collective-permute-start.25 = (bf16[16,8,512]{2,1,0:T(8,128)(2,1)S(1)}, bf16[16,8,512]{2,1,0:T(8,128)(2,1)S(1)}, u32[]{:S(2)}, u32[]{:S(2)}) collective-permute-start(bf16[16,8,512]{2,1,0:T(8,128)(2,1)S(1)} %get-tuple-element.49), channel_id=1, source_target_pairs={{0,2},{1,3},{2,0},{3,1},{4,6},{5,7},{6,4},{7,5},{8,10},{9,11},{10,... | collective-permute-start | bytes 393224 | tf_op jit(solution)/shard_map/ppermute | solution.py:34
  66.0 6.2 %collective-permute-start.29 = (bf16[16,8,512]{2,1,0:T(8,128)(2,1)S(1)}, bf16[16,8,512]{2,1,0:T(8,128)(2,1)S(1)}, u32[]{:S(2)}, u32[]{:S(2)}) collective-permute-start(bf16[16,8,512]{2,1,0:T(8,128)(2,1)S(1)} %get-tuple-element.56), channel_id=1, source_target_pairs={{0,4},{1,5},{2,6},{3,7},{4,0},{5,1},{6,2},{7,3},{8,12},{9,13},{10,... | collective-permute-start | bytes 393224 | tf_op jit(solution)/shard_map/ppermute | solution.py:34
  70.3 6.0 %collective-permute-start.26 = (bf16[8,8,512]{2,1,0:T(8,128)(2,1)S(1)}, bf16[8,8,512]{2,1,0:T(8,128)(2,1)S(1)}, u32[]{:S(2)}, u32[]{:S(2)}) collective-permute-start(bf16[8,8,512]{2,1,0:T(8,128)(2,1)S(1)} %get-tuple-element.51), channel_id=1, source_target_pairs={{0,8},{1,9},{2,10},{3,11},{4,12},{5,13},{6,14},{7,15},{8,0},{9,1},... | collective-permute-start | bytes 196616 | tf_op jit(solution)/shard_map/ppermute | solution.py:34
  72.3 5.7 %collective-permute-start.30 = (bf16[8,8,512]{2,1,0:T(8,128)(2,1)S(1)}, bf16[8,8,512]{2,1,0:T(8,128)(2,1)S(1)}, u32[]{:S(2)}, u32[]{:S(2)}) collective-permute-start(bf16[8,8,512]{2,1,0:T(8,128)(2,1)S(1)} %get-tuple-element.58), channel_id=1, source_target_pairs={{0,8},{1,9},{2,10},{3,11},{4,12},{5,13},{6,14},{7,15},{8,0},{9,1},... | collective-permute-start | bytes 196616 | tf_op jit(solution)/shard_map/ppermute | solution.py:34

commit v15 on v14

--- a/solution.py
+++ b/solution.py
@@ -376,8 +376,8 @@
         total, send = plus(total, swap(send, bit))
     weighted = weigh(total, swap(send, bits[-1]), weight)
     gots = {k: swap(weighted, k) for k in SQUARE}
-    around = join(gots[2], gots[4], gots[6])
-    pieces = [weighted, around, swap(weighted, 1), swap(around, 1)]
+    around = join(weighted, gots[2], gots[4], gots[6])
+    pieces = [around, swap(around, 1)]
 
     acc = zeros((peers * cell_blocks, probe_count, cell_width), (total,))
     total, send_p, send_q = tiles(pieces, 1, 3, table, u_here, v_here, acc, 2, BF16, "adjoint")

time: 79 us -> 78.9 us (level)
    ppermute x31 -> x30, starting transfers between devices: 29.8 us -> 29.4 us  [swap(): return lax.ppermute(array, 'tile', [(i, i ^ bits) for i in range(count)])]
    ppermute x31 -> x30, waiting for transfers between devices: 35.8 us -> 36.1 us  [swap(): return lax.ppermute(array, 'tile', [(i, i ^ bits) for i in range(count)])]
  transfers between devices with their start and end apart: 31 -> 30, of which waited for: 20 -> 20; matrix products, arithmetic and copies ran while one was open for 0% -> 0% of each run, Pallas kernels for 8% -> 9%
where the time goes in v15:
time: 78.9 us; the launch traced here: 78.6 us
  waiting for transfers between devices  36.1 us (46%)
  starting transfers between devices  29.4 us (37%)
  Pallas kernels  12.9 us (16%)
    ppermute x30, waiting for transfers between devices, swap(): return lax.ppermute(array, 'tile', [(i, i ^ bits) for i in range(count)])  36.1 us
    ppermute x30, starting transfers between devices, swap(): return lax.ppermute(array, 'tile', [(i, i ^ bits) for i in range(count)])  29.4 us
    pallas_call x26, Pallas kernels, local(): pl.pallas_call(run, out_shape=[a if s.memory_space is None else s.memory_...  12.9 us
  transfers between devices with their start and end apart: 30, of which 20 were waited for; matrix products, arithmetic and copies ran while one was open for 0% of the time, Pallas kernels for 9%

profile of v15, /device:TPU:0, one launch (start us, length us, event | category | flops | bytes accessed | tf_op | source)
XLA Modules:
  0.0 78.6 jit_solution(14798258438397929825)
XLA Ops:
  0.0 1.1 %scale.1 = (bf16[8,8,512]{2,1,0:T(8,128)(2,1)S(1)}, bf16[8,8,512]{2,1,0:T(8,128)(2,1)S(1)}, f32[64,128]{1,0:T(8,128)S(1)}) custom-call(f32[4]{0:T(128)} %refs_0_.3, f32[64,128]{1,0:T(8,128)} %bitcast.9, s32[64,128]{1,0:T(8,128)} %bitcast.10, f32[8,8192]{1,0:T(8,128)} %refs_3_.1), custom_call_target="tpu_custom_call" | custom-call | bytes 491536 | tf_op jit(solution)/shard_map/scale/pallas_call | solution.py:49
  1.1 4.1 %collective-permute-start.2 = (bf16[8,8,512]{2,1,0:T(8,128)(2,1)S(1)}, bf16[8,8,512]{2,1,0:T(8,128)(2,1)S(1)}, u32[]{:S(2)}, u32[]{:S(2)}) collective-permute-start(bf16[8,8,512]{2,1,0:T(8,128)(2,1)S(1)} %get-tuple-element.36.refs_0_), channel_id=1, source_target_pairs={{0,8},{1,9},{2,10},{3,11},{4,12},{5,13},{6,14},{7,15},{8,0},{9,1},... | collective-permute-start | bytes 196616 | tf_op jit(solution)/shard_map/ppermute | solution.py:34
  5.2 1.5 %collective-permute-start = (bf16[8,8,512]{2,1,0:T(8,128)(2,1)S(1)}, bf16[8,8,512]{2,1,0:T(8,128)(2,1)S(1)}, u32[]{:S(2)}, u32[]{:S(2)}) collective-permute-start(bf16[8,8,512]{2,1,0:T(8,128)(2,1)S(1)} %get-tuple-element.34.refs_0_), channel_id=1, source_target_pairs={{0,2},{1,3},{2,0},{3,1},{4,6},{5,7},{6,4},{7,5},{8,10},{9,11},{10,... | collective-permute-start | bytes 196616 | tf_op jit(solution)/shard_map/ppermute | solution.py:34
  6.7 1.5 %plan.1 = (s32[8,128]{1,0:T(8,128)S(4)}, f32[32,128]{1,0:T(8,128)S(1)}) custom-call(s32[16,128]{1,0:T(8,128)} %bitcast.11, s32[16,128]{1,0:T(8,128)} %bitcast.12, s32[16,128]{1,0:T(8,128)} %bitcast.13, s32[16,128]{1,0:T(8,128)} %bitcast.14, s32[16,128]{1,0:T(8,128)} %bitcast.15, f32[256,128]{1,0:T(8,128)} %bitcast.8, ...), custom_call_target="tpu_custom_call" | custom-call | bytes 192512 | tf_op jit(solution)/shard_map/plan/pallas_call | solution.py:49
  8.2 0.6 collective-permute-done.2.refs_1_
  8.8 1.0 %collective-permute-start.3 = (bf16[16,8,512]{2,1,0:T(8,128)(2,1)S(1)}, bf16[16,8,512]{2,1,0:T(8,128)(2,1)S(1)}, u32[]{:S(2)}, u32[]{:S(2)}) collective-permute-start(bf16[16,8,512]{2,1,0:T(8,128)(2,1)S(1)} %join.6.refs_2_.refs_0_), channel_id=1, source_target_pairs={{0,4},{1,5},{2,6},{3,7},{4,0},{5,1},{6,2},{7,3},{8,12},{9,13},{10,... | collective-permute-start | bytes 393224 | tf_op jit(solution)/shard_map/ppermute | solution.py:34
  9.9 3.1 %collective-permute-start.1 = (bf16[16,8,512]{2,1,0:T(8,128)(2,1)S(1)}, bf16[16,8,512]{2,1,0:T(8,128)(2,1)S(1)}, u32[]{:S(2)}, u32[]{:S(2)}) collective-permute-start(bf16[16,8,512]{2,1,0:T(8,128)(2,1)S(1)} %join.5.refs_1_.refs_0_), channel_id=1, source_target_pairs={{0,8},{1,9},{2,10},{3,11},{4,12},{5,13},{6,14},{7,15},{8,0},{9,1},... | collective-permute-start | bytes 393224 | tf_op jit(solution)/shard_map/ppermute | solution.py:34
  12.9 2.2 %load_v.1.refs_3_.refs_10_.refs_5_ = bf16[128,32,512]{2,1,0:T(8,128)(2,1)S(1)} custom-call(bf16[128,32,512]{2,1,0:T(8,128)(2,1)} %refs_0_.4, bf16[16,8,512]{2,1,0:T(8,128)(2,1)S(1)} %join.5.refs_1_.refs_0_, bf16[16,8,512]{2,1,0:T(8,128)(2,1)S(1)} %join.6.refs_2_.refs_0_), custom_call_target="tpu_custom_call" | custom-call | bytes 8388608 | tf_op jit(solution)/shard_map/load_v/pallas_call | solution.py:49
  15.2 2.2 %load_u.1.refs_2_.refs_11_.refs_4_ = bf16[128,32,512]{2,1,0:T(8,128)(2,1)S(1)} custom-call(bf16[128,32,512]{2,1,0:T(8,128)(2,1)} %refs_0_.5, bf16[16,8,512]{2,1,0:T(8,128)(2,1)S(1)} %join.5.refs_1_.refs_0_, bf16[16,8,512]{2,1,0:T(8,128)(2,1)S(1)} %join.6.refs_2_.refs_0_, bf16[128,32,512]{2,1,0:T(8,128)(2,1)S(1)} %load_v.1.refs_3_.refs_10_.refs_5_), custom_call_target="tpu_custom_call" | custom-call | bytes 8388608 | tf_op jit(solution)/shard_map/load_u/pallas_call | solution.py:49
  17.4 1.6 %collective-permute-start.5 = (bf16[32,8,512]{2,1,0:T(8,128)(2,1)S(1)}, bf16[32,8,512]{2,1,0:T(8,128)(2,1)S(1)}, u32[]{:S(2)}, u32[]{:S(2)}) collective-permute-start(bf16[32,8,512]{2,1,0:T(8,128)(2,1)S(1)} %join.8.refs_1_.refs_4_), channel_id=1, source_target_pairs={{0,2},{1,3},{2,0},{3,1},{4,6},{5,7},{6,4},{7,5},{8,10},{9,11},{10,... | collective-permute-start | bytes 786440 | tf_op jit(solution)/shard_map/ppermute | solution.py:34
  19.2 0.5 collective-permute-start.6
  19.7 5.1 %collective-permute-done.5.refs_5_ = bf16[32,8,512]{2,1,0:T(8,128)(2,1)S(1)} collective-permute-done((bf16[32,8,512]{2,1,0:T(8,128)(2,1)S(1)}, bf16[32,8,512]{2,1,0:T(8,128)(2,1)S(1)}, u32[]{:S(2)}, u32[]{:S(2)}) %collective-permute-start.5) | collective-permute-done | bytes 262176 | tf_op jit(solution)/shard_map/ppermute | solution.py:34
  24.8 1.3 %collective-permute-done.4.refs_3_ = bf16[32,8,512]{2,1,0:T(8,128)(2,1)S(1)} collective-permute-done((bf16[32,8,512]{2,1,0:T(8,128)(2,1)S(1)}, bf16[32,8,512]{2,1,0:T(8,128)(2,1)S(1)}, u32[]{:S(2)}, u32[]{:S(2)}) %collective-permute-start.4) | collective-permute-done | bytes 262176 | tf_op jit(solution)/shard_map/ppermute | solution.py:34
  26.3 1.3 %collective-permute-done.7.refs_7_ = bf16[32,8,512]{2,1,0:T(8,128)(2,1)S(1)} collective-permute-done((bf16[32,8,512]{2,1,0:T(8,128)(2,1)S(1)}, bf16[32,8,512]{2,1,0:T(8,128)(2,1)S(1)}, u32[]{:S(2)}, u32[]{:S(2)}) %collective-permute-start.7) | collective-permute-done | bytes 262176 | tf_op jit(solution)/shard_map/ppermute | solution.py:34
  27.7 2.2 %forward.1 = (f32[64,8,512]{2,1,0:T(8,128)S(1)}, f32[8,8,512]{2,1,0:T(8,128)S(1)}, f32[8,8,512]{2,1,0:T(8,128)S(1)}, f32[8,8,512]{2,1,0:T(8,128)S(1)}, f32[8,8,512]{2,1,0:T(8,128)S(1)}) custom-call(s32[8,128]{1,0:T(8,128)S(4)} %get-tuple-element.33.refs_0_, f32[64,8,512]{2,1,0:T(8,128)S(1)} %zeros.2.refs_1_, ...), custom_call_target="tpu_custom_call", output_to_operand_aliasing={{0}: (1, {})} | custom-call | flops 536870912 | bytes 13111296 | tf_op jit(solution)/shard_map/forward/pallas_call | solution.py:49
  30.1 0.4 collective-permute-start.13
  30.6 0.4 collective-permute-start.10
  31.0 0.3 collective-permute-done.11.refs_1_
  31.3 1.3 %collective-permute-start.12 = (bf16[8,8,512]{2,1,0:T(8,128)(2,1)S(1)}, bf16[8,8,512]{2,1,0:T(8,128)(2,1)S(1)}, u32[]{:S(2)}, u32[]{:S(2)}) collective-permute-start(bf16[8,8,512]{2,1,0:T(8,128)(2,1)S(1)} %fold.11), channel_id=1, source_target_pairs={{0,6},{1,7},{2,4},{3,5},{4,2},{5,3},{6,0},{7,1},{8,14},{9,15},{10,... | collective-permute-start | bytes 196616 | tf_op jit(solution)/shard_map/ppermute | solution.py:34
  32.6 0.6 collective-permute-start.14
  33.2 1.8 %collective-permute-start.16 = (bf16[8,8,512]{2,1,0:T(8,128)(2,1)S(1)}, bf16[8,8,512]{2,1,0:T(8,128)(2,1)S(1)}, u32[]{:S(2)}, u32[]{:S(2)}) collective-permute-start(bf16[8,8,512]{2,1,0:T(8,128)(2,1)S(1)} %fold.13), channel_id=1, source_target_pairs={{0,4},{1,5},{2,6},{3,7},{4,0},{5,1},{6,2},{7,3},{8,12},{9,13},{10,... | collective-permute-start | bytes 196616 | tf_op jit(solution)/shard_map/ppermute | solution.py:34
  35.1 1.7 %collective-permute-done.12.refs_1_ = bf16[8,8,512]{2,1,0:T(8,128)(2,1)S(1)} collective-permute-done((bf16[8,8,512]{2,1,0:T(8,128)(2,1)S(1)}, bf16[8,8,512]{2,1,0:T(8,128)(2,1)S(1)}, u32[]{:S(2)}, u32[]{:S(2)}) %collective-permute-start.12) | collective-permute-done | bytes 65568 | tf_op jit(solution)/shard_map/ppermute | solution.py:34
  36.7 1.1 %collective-permute-done.14.refs_2_ = bf16[8,8,512]{2,1,0:T(8,128)(2,1)S(1)} collective-permute-done((bf16[8,8,512]{2,1,0:T(8,128)(2,1)S(1)}, bf16[8,8,512]{2,1,0:T(8,128)(2,1)S(1)}, u32[]{:S(2)}, u32[]{:S(2)}) %collective-permute-start.14) | collective-permute-done | bytes 65568 | tf_op jit(solution)/shard_map/ppermute | solution.py:34
  37.9 2.3 %collective-permute-start.17 = (bf16[8,8,512]{2,1,0:T(8,128)(2,1)S(1)}, bf16[8,8,512]{2,1,0:T(8,128)(2,1)S(1)}, u32[]{:S(2)}, u32[]{:S(2)}) collective-permute-start(bf16[8,8,512]{2,1,0:T(8,128)(2,1)S(1)} %get-tuple-element.43), channel_id=1, source_target_pairs={{0,8},{1,9},{2,10},{3,11},{4,12},{5,13},{6,14},{7,15},{8,0},{9,1},... | collective-permute-start | bytes 196616 | tf_op jit(solution)/shard_map/ppermute | solution.py:34
  40.2 3.0 %collective-permute-done.17.refs_1_ = bf16[8,8,512]{2,1,0:T(8,128)(2,1)S(1)} collective-permute-done((bf16[8,8,512]{2,1,0:T(8,128)(2,1)S(1)}, bf16[8,8,512]{2,1,0:T(8,128)(2,1)S(1)}, u32[]{:S(2)}, u32[]{:S(2)}) %collective-permute-start.17) | collective-permute-done | bytes 65568 | tf_op jit(solution)/shard_map/ppermute | solution.py:34
  43.2 1.7 %collective-permute-start.20 = (bf16[8,8,512]{2,1,0:T(8,128)(2,1)S(1)}, bf16[8,8,512]{2,1,0:T(8,128)(2,1)S(1)}, u32[]{:S(2)}, u32[]{:S(2)}) collective-permute-start(bf16[8,8,512]{2,1,0:T(8,128)(2,1)S(1)} %weigh.1.refs_0_), channel_id=1, source_target_pairs={{0,6},{1,7},{2,4},{3,5},{4,2},{5,3},{6,0},{7,1},{8,14},{9,15},{10,... | collective-permute-start | bytes 196616 | tf_op jit(solution)/shard_map/ppermute | solution.py:34
  44.9 1.7 %collective-permute-start.19 = (bf16[8,8,512]{2,1,0:T(8,128)(2,1)S(1)}, bf16[8,8,512]{2,1,0:T(8,128)(2,1)S(1)}, u32[]{:S(2)}, u32[]{:S(2)}) collective-permute-start(bf16[8,8,512]{2,1,0:T(8,128)(2,1)S(1)} %weigh.1.refs_0_), channel_id=1, source_target_pairs={{0,4},{1,5},{2,6},{3,7},{4,0},{5,1},{6,2},{7,3},{8,12},{9,13},{10,... | collective-permute-start | bytes 196616 | tf_op jit(solution)/shard_map/ppermute | solution.py:34
  46.7 1.7 %collective-permute-done.20.refs_3_ = bf16[8,8,512]{2,1,0:T(8,128)(2,1)S(1)} collective-permute-done((bf16[8,8,512]{2,1,0:T(8,128)(2,1)S(1)}, bf16[8,8,512]{2,1,0:T(8,128)(2,1)S(1)}, u32[]{:S(2)}, u32[]{:S(2)}) %collective-permute-start.20) | collective-permute-done | bytes 65568 | tf_op jit(solution)/shard_map/ppermute | solution.py:34
  48.4 1.1 %collective-permute-done.19.refs_2_ = bf16[8,8,512]{2,1,0:T(8,128)(2,1)S(1)} collective-permute-done((bf16[8,8,512]{2,1,0:T(8,128)(2,1)S(1)}, bf16[8,8,512]{2,1,0:T(8,128)(2,1)S(1)}, u32[]{:S(2)}, u32[]{:S(2)}) %collective-permute-start.19) | collective-permute-done | bytes 65568 | tf_op jit(solution)/shard_map/ppermute | solution.py:34
  49.5 1.3 %collective-permute-done.18.refs_1_ = bf16[8,8,512]{2,1,0:T(8,128)(2,1)S(1)} collective-permute-done((bf16[8,8,512]{2,1,0:T(8,128)(2,1)S(1)}, bf16[8,8,512]{2,1,0:T(8,128)(2,1)S(1)}, u32[]{:S(2)}, u32[]{:S(2)}) %collective-permute-start.18) | collective-permute-done | bytes 65568 | tf_op jit(solution)/shard_map/ppermute | solution.py:34
  50.9 0.3 zeros.3.refs_1_
  51.2 1.2 %collective-permute-done.21.refs_3_ = bf16[32,8,512]{2,1,0:T(8,128)(2,1)S(1)} collective-permute-done((bf16[32,8,512]{2,1,0:T(8,128)(2,1)S(1)}, bf16[32,8,512]{2,1,0:T(8,128)(2,1)S(1)}, u32[]{:S(2)}, u32[]{:S(2)}) %collective-permute-start.21) | collective-permute-done | bytes 262176 | tf_op jit(solution)/shard_map/ppermute | solution.py:34
  52.4 2.2 %adjoint.1 = (f32[256,8,512]{2,1,0:T(8,128)S(1)}, bf16[64,8,512]{2,1,0:T(8,128)(2,1)S(1)}, bf16[64,8,512]{2,1,0:T(8,128)(2,1)S(1)}) custom-call(s32[8,128]{1,0:T(8,128)S(4)} %get-tuple-element.33.refs_0_, f32[256,8,512]{2,1,0:T(8,128)S(1)} %zeros.3.refs_1_, bf16[32,8,512]{2,1,0:T(8,128)(2,1)S(1)} %join.9.refs_2_, ...), custom_call_target="tpu_custom_call", output_to_operand_aliasing={{0}: (1, {})} | custom-call | flops 536870912 | bytes 18354176 | tf_op jit(solution)/shard_map/adjoint/pallas_call | solution.py:49
  54.8 0.4 collective-permute-start.26
  55.2 1.4 %collective-permute-done.22.refs_1_ = bf16[64,8,512]{2,1,0:T(8,128)(2,1)S(1)} collective-permute-done((bf16[64,8,512]{2,1,0:T(8,128)(2,1)S(1)}, bf16[64,8,512]{2,1,0:T(8,128)(2,1)S(1)}, u32[]{:S(2)}, u32[]{:S(2)}) %collective-permute-start.22) | collective-permute-done | bytes 524320 | tf_op jit(solution)/shard_map/ppermute | solution.py:34
  56.7 0.4 collective-permute-start.23
  57.1 0.3 collective-permute-done.26.refs_1_
  57.4 1.1 %collective-permute-start.27 = (bf16[32,8,512]{2,1,0:T(8,128)(2,1)S(1)}, bf16[32,8,512]{2,1,0:T(8,128)(2,1)S(1)}, u32[]{:S(2)}, u32[]{:S(2)}) collective-permute-start(bf16[32,8,512]{2,1,0:T(8,128)(2,1)S(1)} %get-tuple-element.54), channel_id=1, source_target_pairs={{0,2},{1,3},{2,0},{3,1},{4,6},{5,7},{6,4},{7,5},{8,10},{9,11},{10,... | collective-permute-start | bytes 786440 | tf_op jit(solution)/shard_map/ppermute | solution.py:34
  58.5 6.6 %collective-permute-done.23.refs_1_ = bf16[32,8,512]{2,1,0:T(8,128)(2,1)S(1)} collective-permute-done((bf16[32,8,512]{2,1,0:T(8,128)(2,1)S(1)}, bf16[32,8,512]{2,1,0:T(8,128)(2,1)S(1)}, u32[]{:S(2)}, u32[]{:S(2)}) %collective-permute-start.23) | collective-permute-done | bytes 262176 | tf_op jit(solution)/shard_map/ppermute | solution.py:34
  65.2 0.3 collective-permute-start.24
  65.4 0.4 collective-permute-done.27.refs_1_
  65.9 1.2 %collective-permute-start.28 = (bf16[16,8,512]{2,1,0:T(8,128)(2,1)S(1)}, bf16[16,8,512]{2,1,0:T(8,128)(2,1)S(1)}, u32[]{:S(2)}, u32[]{:S(2)}) collective-permute-start(bf16[16,8,512]{2,1,0:T(8,128)(2,1)S(1)} %get-tuple-element.56), channel_id=1, source_target_pairs={{0,4},{1,5},{2,6},{3,7},{4,0},{5,1},{6,2},{7,3},{8,12},{9,13},{10,... | collective-permute-start | bytes 393224 | tf_op jit(solution)/shard_map/ppermute | solution.py:34
  67.1 3.1 %collective-permute-done.24.refs_1_ = bf16[16,8,512]{2,1,0:T(8,128)(2,1)S(1)} collective-permute-done((bf16[16,8,512]{2,1,0:T(8,128)(2,1)S(1)}, bf16[16,8,512]{2,1,0:T(8,128)(2,1)S(1)}, u32[]{:S(2)}, u32[]{:S(2)}) %collective-permute-start.24) | collective-permute-done | bytes 131104 | tf_op jit(solution)/shard_map/ppermute | solution.py:34
  70.2 1.9 %collective-permute-start.25 = (bf16[8,8,512]{2,1,0:T(8,128)(2,1)S(1)}, bf16[8,8,512]{2,1,0:T(8,128)(2,1)S(1)}, u32[]{:S(2)}, u32[]{:S(2)}) collective-permute-start(bf16[8,8,512]{2,1,0:T(8,128)(2,1)S(1)} %get-tuple-element.51), channel_id=1, source_target_pairs={{0,8},{1,9},{2,10},{3,11},{4,12},{5,13},{6,14},{7,15},{8,0},{9,1},... | collective-permute-start | bytes 196616 | tf_op jit(solution)/shard_map/ppermute | solution.py:34
  72.2 1.3 %collective-permute-start.29 = (bf16[8,8,512]{2,1,0:T(8,128)(2,1)S(1)}, bf16[8,8,512]{2,1,0:T(8,128)(2,1)S(1)}, u32[]{:S(2)}, u32[]{:S(2)}) collective-permute-start(bf16[8,8,512]{2,1,0:T(8,128)(2,1)S(1)} %get-tuple-element.58), channel_id=1, source_target_pairs={{0,8},{1,9},{2,10},{3,11},{4,12},{5,13},{6,14},{7,15},{8,0},{9,1},... | collective-permute-start | bytes 196616 | tf_op jit(solution)/shard_map/ppermute | solution.py:34
  73.4 2.7 %collective-permute-done.25.refs_1_ = bf16[8,8,512]{2,1,0:T(8,128)(2,1)S(1)} collective-permute-done((bf16[8,8,512]{2,1,0:T(8,128)(2,1)S(1)}, bf16[8,8,512]{2,1,0:T(8,128)(2,1)S(1)}, u32[]{:S(2)}, u32[]{:S(2)}) %collective-permute-start.25) | collective-permute-done | bytes 65568 | tf_op jit(solution)/shard_map/ppermute | solution.py:34
  76.2 1.7 %collective-permute-done.29.refs_3_ = bf16[8,8,512]{2,1,0:T(8,128)(2,1)S(1)} collective-permute-done((bf16[8,8,512]{2,1,0:T(8,128)(2,1)S(1)}, bf16[8,8,512]{2,1,0:T(8,128)(2,1)S(1)}, u32[]{:S(2)}, u32[]{:S(2)}) %collective-permute-start.29) | collective-permute-done | bytes 65568 | tf_op jit(solution)/shard_map/ppermute | solution.py:34
  77.8 0.7 final.1
  (38 shorter events, 1.7 us)
Async XLA Ops:
  1.1 7.8 %collective-permute-start.2 = (bf16[8,8,512]{2,1,0:T(8,128)(2,1)S(1)}, bf16[8,8,512]{2,1,0:T(8,128)(2,1)S(1)}, u32[]{:S(2)}, u32[]{:S(2)}) collective-permute-start(bf16[8,8,512]{2,1,0:T(8,128)(2,1)S(1)} %get-tuple-element.36.refs_0_), channel_id=1, source_target_pairs={{0,8},{1,9},{2,10},{3,11},{4,12},{5,13},{6,14},{7,15},{8,0},{9,1},... | collective-permute-start | bytes 196616 | tf_op jit(solution)/shard_map/ppermute | solution.py:34
  5.2 4.7 %collective-permute-start = (bf16[8,8,512]{2,1,0:T(8,128)(2,1)S(1)}, bf16[8,8,512]{2,1,0:T(8,128)(2,1)S(1)}, u32[]{:S(2)}, u32[]{:S(2)}) collective-permute-start(bf16[8,8,512]{2,1,0:T(8,128)(2,1)S(1)} %get-tuple-element.34.refs_0_), channel_id=1, source_target_pairs={{0,2},{1,3},{2,0},{3,1},{4,6},{5,7},{6,4},{7,5},{8,10},{9,11},{10,... | collective-permute-start | bytes 196616 | tf_op jit(solution)/shard_map/ppermute | solution.py:34
  8.8 8.5 %collective-permute-start.3 = (bf16[16,8,512]{2,1,0:T(8,128)(2,1)S(1)}, bf16[16,8,512]{2,1,0:T(8,128)(2,1)S(1)}, u32[]{:S(2)}, u32[]{:S(2)}) collective-permute-start(bf16[16,8,512]{2,1,0:T(8,128)(2,1)S(1)} %join.6.refs_2_.refs_0_), channel_id=1, source_target_pairs={{0,4},{1,5},{2,6},{3,7},{4,0},{5,1},{6,2},{7,3},{8,12},{9,13},{10,... | collective-permute-start | bytes 393224 | tf_op jit(solution)/shard_map/ppermute | solution.py:34
  9.9 9.1 %collective-permute-start.1 = (bf16[16,8,512]{2,1,0:T(8,128)(2,1)S(1)}, bf16[16,8,512]{2,1,0:T(8,128)(2,1)S(1)}, u32[]{:S(2)}, u32[]{:S(2)}) collective-permute-start(bf16[16,8,512]{2,1,0:T(8,128)(2,1)S(1)} %join.5.refs_1_.refs_0_), channel_id=1, source_target_pairs={{0,8},{1,9},{2,10},{3,11},{4,12},{5,13},{6,14},{7,15},{8,0},{9,1},... | collective-permute-start | bytes 393224 | tf_op jit(solution)/shard_map/ppermute | solution.py:34
  17.4 7.4 %collective-permute-start.5 = (bf16[32,8,512]{2,1,0:T(8,128)(2,1)S(1)}, bf16[32,8,512]{2,1,0:T(8,128)(2,1)S(1)}, u32[]{:S(2)}, u32[]{:S(2)}) collective-permute-start(bf16[32,8,512]{2,1,0:T(8,128)(2,1)S(1)} %join.8.refs_1_.refs_4_), channel_id=1, source_target_pairs={{0,2},{1,3},{2,0},{3,1},{4,6},{5,7},{6,4},{7,5},{8,10},{9,11},{10,... | collective-permute-start | bytes 786440 | tf_op jit(solution)/shard_map/ppermute | solution.py:34
  19.0 7.1 %collective-permute-start.4 = (bf16[32,8,512]{2,1,0:T(8,128)(2,1)S(1)}, bf16[32,8,512]{2,1,0:T(8,128)(2,1)S(1)}, u32[]{:S(2)}, u32[]{:S(2)}) collective-permute-start(bf16[32,8,512]{2,1,0:T(8,128)(2,1)S(1)} %join.7.refs_0_.refs_2_), channel_id=1, source_target_pairs={{0,4},{1,5},{2,6},{3,7},{4,0},{5,1},{6,2},{7,3},{8,12},{9,13},{10,... | collective-permute-start | bytes 786440 | tf_op jit(solution)/shard_map/ppermute | solution.py:34
  19.2 7.0 %collective-permute-start.8 = (bf16[32,8,512]{2,1,0:T(8,128)(2,1)S(1)}, bf16[32,8,512]{2,1,0:T(8,128)(2,1)S(1)}, u32[]{:S(2)}, u32[]{:S(2)}) collective-permute-start(bf16[32,8,512]{2,1,0:T(8,128)(2,1)S(1)} %join.8.refs_1_.refs_4_), channel_id=1, source_target_pairs={{0,1},{1,0},{2,3},{3,2},{4,5},{5,4},{6,7},{7,6},{8,9},{9,8},{10,11... | collective-permute-start | bytes 786440 | tf_op jit(solution)/shard_map/ppermute | solution.py:34
  19.2 7.0 %collective-permute-start.6 = (bf16[32,8,512]{2,1,0:T(8,128)(2,1)S(1)}, bf16[32,8,512]{2,1,0:T(8,128)(2,1)S(1)}, u32[]{:S(2)}, u32[]{:S(2)}) collective-permute-start(bf16[32,8,512]{2,1,0:T(8,128)(2,1)S(1)} %join.7.refs_0_.refs_2_), channel_id=1, source_target_pairs={{0,1},{1,0},{2,3},{3,2},{4,5},{5,4},{6,7},{7,6},{8,9},{9,8},{10,11... | collective-permute-start | bytes 786440 | tf_op jit(solution)/shard_map/ppermute | solution.py:34
  24.8 1.5 %collective-permute-start.9 = (bf16[32,8,512]{2,1,0:T(8,128)(2,1)S(1)}, bf16[32,8,512]{2,1,0:T(8,128)(2,1)S(1)}, u32[]{:S(2)}, u32[]{:S(2)}) collective-permute-start(bf16[32,8,512]{2,1,0:T(8,128)(2,1)S(1)} %collective-permute-done.5.refs_5_), channel_id=1, source_target_pairs={{0,1},{1,0},{2,3},{3,2},{4,5},{5,4},{6,7},{7,6},{8,9},{9,8},{10,11... | collective-permute-start | bytes 786440 | tf_op jit(solution)/shard_map/ppermute | solution.py:34
  26.1 1.5 %collective-permute-start.7 = (bf16[32,8,512]{2,1,0:T(8,128)(2,1)S(1)}, bf16[32,8,512]{2,1,0:T(8,128)(2,1)S(1)}, u32[]{:S(2)}, u32[]{:S(2)}) collective-permute-start(bf16[32,8,512]{2,1,0:T(8,128)(2,1)S(1)} %collective-permute-done.4.refs_3_), channel_id=1, source_target_pairs={{0,1},{1,0},{2,3},{3,2},{4,5},{5,4},{6,7},{7,6},{8,9},{9,8},{10,11... | collective-permute-start | bytes 786440 | tf_op jit(solution)/shard_map/ppermute | solution.py:34
  29.9 1.4 %collective-permute-start.11 = (f32[8,8,512]{2,1,0:T(8,128)S(1)}, f32[8,8,512]{2,1,0:T(8,128)S(1)}, u32[]{:S(2)}, u32[]{:S(2)}) collective-permute-start(f32[8,8,512]{2,1,0:T(8,128)S(1)} %get-tuple-element.39), channel_id=1, source_target_pairs={{0,1},{1,0},{2,3},{3,2},{4,5},{5,4},{6,7},{7,6},{8,9},{9,8},{10,11... | collective-permute-start | bytes 393224 | tf_op jit(solution)/shard_map/ppermute | solution.py:34
  30.1 2.5 %collective-permute-start.13 = (f32[8,8,512]{2,1,0:T(8,128)S(1)}, f32[8,8,512]{2,1,0:T(8,128)S(1)}, u32[]{:S(2)}, u32[]{:S(2)}) collective-permute-start(f32[8,8,512]{2,1,0:T(8,128)S(1)} %get-tuple-element.40), channel_id=1, source_target_pairs={{0,1},{1,0},{2,3},{3,2},{4,5},{5,4},{6,7},{7,6},{8,9},{9,8},{10,11... | collective-permute-start | bytes 393224 | tf_op jit(solution)/shard_map/ppermute | solution.py:34
  30.4 2.8 %collective-permute-start.15 = (f32[8,8,512]{2,1,0:T(8,128)S(1)}, f32[8,8,512]{2,1,0:T(8,128)S(1)}, u32[]{:S(2)}, u32[]{:S(2)}) collective-permute-start(f32[8,8,512]{2,1,0:T(8,128)S(1)} %get-tuple-element.41), channel_id=1, source_target_pairs={{0,1},{1,0},{2,3},{3,2},{4,5},{5,4},{6,7},{7,6},{8,9},{9,8},{10,11... | collective-permute-start | bytes 393224 | tf_op jit(solution)/shard_map/ppermute | solution.py:34
  30.6 4.5 %collective-permute-start.10 = (f32[8,8,512]{2,1,0:T(8,128)S(1)}, f32[8,8,512]{2,1,0:T(8,128)S(1)}, u32[]{:S(2)}, u32[]{:S(2)}) collective-permute-start(f32[8,8,512]{2,1,0:T(8,128)S(1)} %get-tuple-element.38), channel_id=1, source_target_pairs={{0,1},{1,0},{2,3},{3,2},{4,5},{5,4},{6,7},{7,6},{8,9},{9,8},{10,11... | collective-permute-start | bytes 393224 | tf_op jit(solution)/shard_map/ppermute | solution.py:34
  31.3 5.4 %collective-permute-start.12 = (bf16[8,8,512]{2,1,0:T(8,128)(2,1)S(1)}, bf16[8,8,512]{2,1,0:T(8,128)(2,1)S(1)}, u32[]{:S(2)}, u32[]{:S(2)}) collective-permute-start(bf16[8,8,512]{2,1,0:T(8,128)(2,1)S(1)} %fold.11), channel_id=1, source_target_pairs={{0,6},{1,7},{2,4},{3,5},{4,2},{5,3},{6,0},{7,1},{8,14},{9,15},{10,... | collective-permute-start | bytes 196616 | tf_op jit(solution)/shard_map/ppermute | solution.py:34
  32.6 5.2 %collective-permute-start.14 = (bf16[8,8,512]{2,1,0:T(8,128)(2,1)S(1)}, bf16[8,8,512]{2,1,0:T(8,128)(2,1)S(1)}, u32[]{:S(2)}, u32[]{:S(2)}) collective-permute-start(bf16[8,8,512]{2,1,0:T(8,128)(2,1)S(1)} %fold.12), channel_id=1, source_target_pairs={{0,2},{1,3},{2,0},{3,1},{4,6},{5,7},{6,4},{7,5},{8,10},{9,11},{10,... | collective-permute-start | bytes 196616 | tf_op jit(solution)/shard_map/ppermute | solution.py:34
  33.2 4.6 %collective-permute-start.16 = (bf16[8,8,512]{2,1,0:T(8,128)(2,1)S(1)}, bf16[8,8,512]{2,1,0:T(8,128)(2,1)S(1)}, u32[]{:S(2)}, u32[]{:S(2)}) collective-permute-start(bf16[8,8,512]{2,1,0:T(8,128)(2,1)S(1)} %fold.13), channel_id=1, source_target_pairs={{0,4},{1,5},{2,6},{3,7},{4,0},{5,1},{6,2},{7,3},{8,12},{9,13},{10,... | collective-permute-start | bytes 196616 | tf_op jit(solution)/shard_map/ppermute | solution.py:34
  37.9 5.3 %collective-permute-start.17 = (bf16[8,8,512]{2,1,0:T(8,128)(2,1)S(1)}, bf16[8,8,512]{2,1,0:T(8,128)(2,1)S(1)}, u32[]{:S(2)}, u32[]{:S(2)}) collective-permute-start(bf16[8,8,512]{2,1,0:T(8,128)(2,1)S(1)} %get-tuple-element.43), channel_id=1, source_target_pairs={{0,8},{1,9},{2,10},{3,11},{4,12},{5,13},{6,14},{7,15},{8,0},{9,1},... | collective-permute-start | bytes 196616 | tf_op jit(solution)/shard_map/ppermute | solution.py:34
  43.2 5.2 %collective-permute-start.20 = (bf16[8,8,512]{2,1,0:T(8,128)(2,1)S(1)}, bf16[8,8,512]{2,1,0:T(8,128)(2,1)S(1)}, u32[]{:S(2)}, u32[]{:S(2)}) collective-permute-start(bf16[8,8,512]{2,1,0:T(8,128)(2,1)S(1)} %weigh.1.refs_0_), channel_id=1, source_target_pairs={{0,6},{1,7},{2,4},{3,5},{4,2},{5,3},{6,0},{7,1},{8,14},{9,15},{10,... | collective-permute-start | bytes 196616 | tf_op jit(solution)/shard_map/ppermute | solution.py:34
  44.9 4.6 %collective-permute-start.19 = (bf16[8,8,512]{2,1,0:T(8,128)(2,1)S(1)}, bf16[8,8,512]{2,1,0:T(8,128)(2,1)S(1)}, u32[]{:S(2)}, u32[]{:S(2)}) collective-permute-start(bf16[8,8,512]{2,1,0:T(8,128)(2,1)S(1)} %weigh.1.refs_0_), channel_id=1, source_target_pairs={{0,4},{1,5},{2,6},{3,7},{4,0},{5,1},{6,2},{7,3},{8,12},{9,13},{10,... | collective-permute-start | bytes 196616 | tf_op jit(solution)/shard_map/ppermute | solution.py:34
  46.6 4.3 %collective-permute-start.18 = (bf16[8,8,512]{2,1,0:T(8,128)(2,1)S(1)}, bf16[8,8,512]{2,1,0:T(8,128)(2,1)S(1)}, u32[]{:S(2)}, u32[]{:S(2)}) collective-permute-start(bf16[8,8,512]{2,1,0:T(8,128)(2,1)S(1)} %weigh.1.refs_0_), channel_id=1, source_target_pairs={{0,2},{1,3},{2,0},{3,1},{4,6},{5,7},{6,4},{7,5},{8,10},{9,11},{10,... | collective-permute-start | bytes 196616 | tf_op jit(solution)/shard_map/ppermute | solution.py:34
  50.8 1.6 %collective-permute-start.21 = (bf16[32,8,512]{2,1,0:T(8,128)(2,1)S(1)}, bf16[32,8,512]{2,1,0:T(8,128)(2,1)S(1)}, u32[]{:S(2)}, u32[]{:S(2)}) collective-permute-start(bf16[32,8,512]{2,1,0:T(8,128)(2,1)S(1)} %join.9.refs_2_), channel_id=1, source_target_pairs={{0,1},{1,0},{2,3},{3,2},{4,5},{5,4},{6,7},{7,6},{8,9},{9,8},{10,11... | collective-permute-start | bytes 786440 | tf_op jit(solution)/shard_map/ppermute | solution.py:34
  54.6 2.0 %collective-permute-start.22 = (bf16[64,8,512]{2,1,0:T(8,128)(2,1)S(1)}, bf16[64,8,512]{2,1,0:T(8,128)(2,1)S(1)}, u32[]{:S(2)}, u32[]{:S(2)}) collective-permute-start(bf16[64,8,512]{2,1,0:T(8,128)(2,1)S(1)} %get-tuple-element.45), channel_id=1, source_target_pairs={{0,1},{1,0},{2,3},{3,2},{4,5},{5,4},{6,7},{7,6},{8,9},{9,8},{10,11... | collective-permute-start | bytes 1572872 | tf_op jit(solution)/shard_map/ppermute | solution.py:34
  54.8 2.5 %collective-permute-start.26 = (bf16[64,8,512]{2,1,0:T(8,128)(2,1)S(1)}, bf16[64,8,512]{2,1,0:T(8,128)(2,1)S(1)}, u32[]{:S(2)}, u32[]{:S(2)}) collective-permute-start(bf16[64,8,512]{2,1,0:T(8,128)(2,1)S(1)} %get-tuple-element.52), channel_id=1, source_target_pairs={{0,1},{1,0},{2,3},{3,2},{4,5},{5,4},{6,7},{7,6},{8,9},{9,8},{10,11... | collective-permute-start | bytes 1572872 | tf_op jit(solution)/shard_map/ppermute | solution.py:34
  56.7 8.4 %collective-permute-start.23 = (bf16[32,8,512]{2,1,0:T(8,128)(2,1)S(1)}, bf16[32,8,512]{2,1,0:T(8,128)(2,1)S(1)}, u32[]{:S(2)}, u32[]{:S(2)}) collective-permute-start(bf16[32,8,512]{2,1,0:T(8,128)(2,1)S(1)} %get-tuple-element.47), channel_id=1, source_target_pairs={{0,4},{1,5},{2,6},{3,7},{4,0},{5,1},{6,2},{7,3},{8,12},{9,13},{10,... | collective-permute-start | bytes 786440 | tf_op jit(solution)/shard_map/ppermute | solution.py:34
  57.4 8.4 %collective-permute-start.27 = (bf16[32,8,512]{2,1,0:T(8,128)(2,1)S(1)}, bf16[32,8,512]{2,1,0:T(8,128)(2,1)S(1)}, u32[]{:S(2)}, u32[]{:S(2)}) collective-permute-start(bf16[32,8,512]{2,1,0:T(8,128)(2,1)S(1)} %get-tuple-element.54), channel_id=1, source_target_pairs={{0,2},{1,3},{2,0},{3,1},{4,6},{5,7},{6,4},{7,5},{8,10},{9,11},{10,... | collective-permute-start | bytes 786440 | tf_op jit(solution)/shard_map/ppermute | solution.py:34
  65.2 5.0 %collective-permute-start.24 = (bf16[16,8,512]{2,1,0:T(8,128)(2,1)S(1)}, bf16[16,8,512]{2,1,0:T(8,128)(2,1)S(1)}, u32[]{:S(2)}, u32[]{:S(2)}) collective-permute-start(bf16[16,8,512]{2,1,0:T(8,128)(2,1)S(1)} %get-tuple-element.49), channel_id=1, source_target_pairs={{0,2},{1,3},{2,0},{3,1},{4,6},{5,7},{6,4},{7,5},{8,10},{9,11},{10,... | collective-permute-start | bytes 393224 | tf_op jit(solution)/shard_map/ppermute | solution.py:34
  65.9 6.2 %collective-permute-start.28 = (bf16[16,8,512]{2,1,0:T(8,128)(2,1)S(1)}, bf16[16,8,512]{2,1,0:T(8,128)(2,1)S(1)}, u32[]{:S(2)}, u32[]{:S(2)}) collective-permute-start(bf16[16,8,512]{2,1,0:T(8,128)(2,1)S(1)} %get-tuple-element.56), channel_id=1, source_target_pairs={{0,4},{1,5},{2,6},{3,7},{4,0},{5,1},{6,2},{7,3},{8,12},{9,13},{10,... | collective-permute-start | bytes 393224 | tf_op jit(solution)/shard_map/ppermute | solution.py:34
  70.2 5.9 %collective-permute-start.25 = (bf16[8,8,512]{2,1,0:T(8,128)(2,1)S(1)}, bf16[8,8,512]{2,1,0:T(8,128)(2,1)S(1)}, u32[]{:S(2)}, u32[]{:S(2)}) collective-permute-start(bf16[8,8,512]{2,1,0:T(8,128)(2,1)S(1)} %get-tuple-element.51), channel_id=1, source_target_pairs={{0,8},{1,9},{2,10},{3,11},{4,12},{5,13},{6,14},{7,15},{8,0},{9,1},... | collective-permute-start | bytes 196616 | tf_op jit(solution)/shard_map/ppermute | solution.py:34
  72.2 5.7 %collective-permute-start.29 = (bf16[8,8,512]{2,1,0:T(8,128)(2,1)S(1)}, bf16[8,8,512]{2,1,0:T(8,128)(2,1)S(1)}, u32[]{:S(2)}, u32[]{:S(2)}) collective-permute-start(bf16[8,8,512]{2,1,0:T(8,128)(2,1)S(1)} %get-tuple-element.58), channel_id=1, source_target_pairs={{0,8},{1,9},{2,10},{3,11},{4,12},{5,13},{6,14},{7,15},{8,0},{9,1},... | collective-permute-start | bytes 196616 | tf_op jit(solution)/shard_map/ppermute | solution.py:34

commit v16 on v15

--- a/solution.py
+++ b/solution.py
@@ -67,22 +67,26 @@
         copy.wait()
 
 
-def load_body(source, out, sems):
-    n = source.shape[0] // sems.shape[0]
-    rows = [pl.ds(i * n, n) for i in range(sems.shape[0])]
-    fetch([(source.at[r], out.at[r]) for r in rows], sems)
-
-
-def load(array, after, name):
+def load(arrays, after):
+    parts = 4
+
+    def body(*refs):
+        count = len(refs) // 2
+        pairs = []
+        for source, out in zip(refs[:count], refs[count:-1]):
+            n = source.shape[0] // parts
+            pairs += [(source.at[pl.ds(i * n, n)], out.at[pl.ds(i * n, n)]) for i in range(parts)]
+        fetch(pairs, refs[-1])
+
     return local(
-        load_body,
-        [shape(array.shape, array.dtype)],
-        array,
-        name=name,
-        specs=[whole(pltpu.HBM)],
-        scratches=[pltpu.SemaphoreType.DMA((8,))],
+        body,
+        [shape(a.shape, a.dtype) for a in arrays],
+        *arrays,
+        name="load",
+        specs=[whole(pltpu.HBM)] * len(arrays),
+        scratches=[pltpu.SemaphoreType.DMA((parts * len(arrays),))],
         after=after,
-    )[0]
+    )
 
 
 def scale_body(
@@ -355,8 +359,7 @@
         got_p = swap(part_p, bit_p)
         got_q = swap(part_q, bit_q)
         if step == 1:
-            v_here = load(v_factor, (part_p, part_q), "load_v")
-            u_here = load(u_factor, (part_p, part_q, v_here), "load_u")
+            v_here, u_here = load((v_factor, u_factor), (part_p, part_q))
             after = (u_here,)
         if step < len(steps) - 1:
             part_p = join(part_p, got_p, after=after)

time: 78.9 us -> 78.9 us (level)
  Pallas kernels: 12.9 us -> 12 us
    pallas_call x26 -> x25, Pallas kernels: 12.9 us -> 12 us  [local(): pl.pallas_call(run, out_shape=[a if s.memory_space is None else s.memory_...]
  transfers between devices with their start and end apart: 30 -> 30, of which waited for: 20 -> 21; matrix products, arithmetic and copies ran while one was open for 0% -> 0% of each run, Pallas kernels for 9% -> 7%
where the time goes in v16:
time: 78.9 us; the launch traced here: 78.6 us
  waiting for transfers between devices  36.8 us (47%)
  starting transfers between devices  29.7 us (38%)
  Pallas kernels  12 us (15%)
    ppermute x30, waiting for transfers between devices, swap(): return lax.ppermute(array, 'tile', [(i, i ^ bits) for i in range(count)])  36.8 us
    ppermute x30, starting transfers between devices, swap(): return lax.ppermute(array, 'tile', [(i, i ^ bits) for i in range(count)])  29.7 us
    pallas_call x25, Pallas kernels, local(): pl.pallas_call(run, out_shape=[a if s.memory_space is None else s.memory_...  12 us
  transfers between devices with their start and end apart: 30, of which 21 were waited for; matrix products, arithmetic and copies ran while one was open for 0% of the time, Pallas kernels for 7%

profile of v16, /device:TPU:0, one launch (start us, length us, event | category | flops | bytes accessed | tf_op | source)
XLA Modules:
  0.0 78.6 jit_solution(14708662900160757103)
XLA Ops:
  0.0 1.1 %scale.1 = (bf16[8,8,512]{2,1,0:T(8,128)(2,1)S(1)}, bf16[8,8,512]{2,1,0:T(8,128)(2,1)S(1)}, f32[64,128]{1,0:T(8,128)S(1)}) custom-call(f32[4]{0:T(128)} %refs_0_.2, f32[64,128]{1,0:T(8,128)} %bitcast.9, s32[64,128]{1,0:T(8,128)} %bitcast.10, f32[8,8192]{1,0:T(8,128)} %refs_3_.1), custom_call_target="tpu_custom_call" | custom-call | bytes 491536 | tf_op jit(solution)/shard_map/scale/pallas_call | solution.py:49
  1.1 4.1 %collective-permute-start.2 = (bf16[8,8,512]{2,1,0:T(8,128)(2,1)S(1)}, bf16[8,8,512]{2,1,0:T(8,128)(2,1)S(1)}, u32[]{:S(2)}, u32[]{:S(2)}) collective-permute-start(bf16[8,8,512]{2,1,0:T(8,128)(2,1)S(1)} %get-tuple-element.38.refs_0_), channel_id=1, source_target_pairs={{0,8},{1,9},{2,10},{3,11},{4,12},{5,13},{6,14},{7,15},{8,0},{9,1},... | collective-permute-start | bytes 196616 | tf_op jit(solution)/shard_map/ppermute | solution.py:34
  5.2 1.5 %collective-permute-start = (bf16[8,8,512]{2,1,0:T(8,128)(2,1)S(1)}, bf16[8,8,512]{2,1,0:T(8,128)(2,1)S(1)}, u32[]{:S(2)}, u32[]{:S(2)}) collective-permute-start(bf16[8,8,512]{2,1,0:T(8,128)(2,1)S(1)} %get-tuple-element.36.refs_0_), channel_id=1, source_target_pairs={{0,2},{1,3},{2,0},{3,1},{4,6},{5,7},{6,4},{7,5},{8,10},{9,11},{10,... | collective-permute-start | bytes 196616 | tf_op jit(solution)/shard_map/ppermute | solution.py:34
  6.7 1.5 %plan.1 = (s32[8,128]{1,0:T(8,128)S(4)}, f32[32,128]{1,0:T(8,128)S(1)}) custom-call(s32[16,128]{1,0:T(8,128)} %bitcast.11, s32[16,128]{1,0:T(8,128)} %bitcast.12, s32[16,128]{1,0:T(8,128)} %bitcast.13, s32[16,128]{1,0:T(8,128)} %bitcast.14, s32[16,128]{1,0:T(8,128)} %bitcast.15, f32[256,128]{1,0:T(8,128)} %bitcast.8, ...), custom_call_target="tpu_custom_call" | custom-call | bytes 192512 | tf_op jit(solution)/shard_map/plan/pallas_call | solution.py:49
  8.2 0.6 collective-permute-done.2.refs_1_
  8.8 1.0 %collective-permute-start.3 = (bf16[16,8,512]{2,1,0:T(8,128)(2,1)S(1)}, bf16[16,8,512]{2,1,0:T(8,128)(2,1)S(1)}, u32[]{:S(2)}, u32[]{:S(2)}) collective-permute-start(bf16[16,8,512]{2,1,0:T(8,128)(2,1)S(1)} %join.6.refs_3_.refs_0_), channel_id=1, source_target_pairs={{0,4},{1,5},{2,6},{3,7},{4,0},{5,1},{6,2},{7,3},{8,12},{9,13},{10,... | collective-permute-start | bytes 393224 | tf_op jit(solution)/shard_map/ppermute | solution.py:34
  9.9 3.1 %collective-permute-start.1 = (bf16[16,8,512]{2,1,0:T(8,128)(2,1)S(1)}, bf16[16,8,512]{2,1,0:T(8,128)(2,1)S(1)}, u32[]{:S(2)}, u32[]{:S(2)}) collective-permute-start(bf16[16,8,512]{2,1,0:T(8,128)(2,1)S(1)} %join.5.refs_2_.refs_0_), channel_id=1, source_target_pairs={{0,8},{1,9},{2,10},{3,11},{4,12},{5,13},{6,14},{7,15},{8,0},{9,1},... | collective-permute-start | bytes 393224 | tf_op jit(solution)/shard_map/ppermute | solution.py:34
  12.9 3.5 %load.1 = (bf16[128,32,512]{2,1,0:T(8,128)(2,1)S(1)}, bf16[128,32,512]{2,1,0:T(8,128)(2,1)S(1)}) custom-call(bf16[128,32,512]{2,1,0:T(8,128)(2,1)} %refs_0_.3, bf16[128,32,512]{2,1,0:T(8,128)(2,1)} %refs_1_.1, bf16[16,8,512]{2,1,0:T(8,128)(2,1)S(1)} %join.5.refs_2_.refs_0_, bf16[16,8,512]{2,1,0:T(8,128)(2,1)S(1)} %join.6.refs_3_.refs_0_), custom_call_target="tpu_custom_call" | custom-call | bytes 16777216 | tf_op jit(solution)/shard_map/load/pallas_call | solution.py:49
  16.5 1.6 %collective-permute-start.5 = (bf16[32,8,512]{2,1,0:T(8,128)(2,1)S(1)}, bf16[32,8,512]{2,1,0:T(8,128)(2,1)S(1)}, u32[]{:S(2)}, u32[]{:S(2)}) collective-permute-start(bf16[32,8,512]{2,1,0:T(8,128)(2,1)S(1)} %join.8.refs_1_.refs_4_), channel_id=1, source_target_pairs={{0,2},{1,3},{2,0},{3,1},{4,6},{5,7},{6,4},{7,5},{8,10},{9,11},{10,... | collective-permute-start | bytes 786440 | tf_op jit(solution)/shard_map/ppermute | solution.py:34
  18.0 0.8 %collective-permute-done.1.refs_1_ = bf16[16,8,512]{2,1,0:T(8,128)(2,1)S(1)} collective-permute-done((bf16[16,8,512]{2,1,0:T(8,128)(2,1)S(1)}, bf16[16,8,512]{2,1,0:T(8,128)(2,1)S(1)}, u32[]{:S(2)}, u32[]{:S(2)}) %collective-permute-start.1) | collective-permute-done | bytes 131104 | tf_op jit(solution)/shard_map/ppermute | solution.py:34
  18.9 0.3 collective-permute-start.4
  19.2 0.5 collective-permute-start.6
  19.7 4.1 %collective-permute-done.5.refs_5_ = bf16[32,8,512]{2,1,0:T(8,128)(2,1)S(1)} collective-permute-done((bf16[32,8,512]{2,1,0:T(8,128)(2,1)S(1)}, bf16[32,8,512]{2,1,0:T(8,128)(2,1)S(1)}, u32[]{:S(2)}, u32[]{:S(2)}) %collective-permute-start.5) | collective-permute-done | bytes 262176 | tf_op jit(solution)/shard_map/ppermute | solution.py:34
  23.8 1.5 %collective-permute-done.4.refs_3_ = bf16[32,8,512]{2,1,0:T(8,128)(2,1)S(1)} collective-permute-done((bf16[32,8,512]{2,1,0:T(8,128)(2,1)S(1)}, bf16[32,8,512]{2,1,0:T(8,128)(2,1)S(1)}, u32[]{:S(2)}, u32[]{:S(2)}) %collective-permute-start.4) | collective-permute-done | bytes 262176 | tf_op jit(solution)/shard_map/ppermute | solution.py:34
  25.4 1.4 %collective-permute-done.7.refs_7_ = bf16[32,8,512]{2,1,0:T(8,128)(2,1)S(1)} collective-permute-done((bf16[32,8,512]{2,1,0:T(8,128)(2,1)S(1)}, bf16[32,8,512]{2,1,0:T(8,128)(2,1)S(1)}, u32[]{:S(2)}, u32[]{:S(2)}) %collective-permute-start.7) | collective-permute-done | bytes 262176 | tf_op jit(solution)/shard_map/ppermute | solution.py:34
  26.8 2.2 %forward.1 = (f32[64,8,512]{2,1,0:T(8,128)S(1)}, f32[8,8,512]{2,1,0:T(8,128)S(1)}, f32[8,8,512]{2,1,0:T(8,128)S(1)}, f32[8,8,512]{2,1,0:T(8,128)S(1)}, f32[8,8,512]{2,1,0:T(8,128)S(1)}) custom-call(s32[8,128]{1,0:T(8,128)S(4)} %get-tuple-element.35.refs_0_, f32[64,8,512]{2,1,0:T(8,128)S(1)} %zeros.2.refs_1_, ...), custom_call_target="tpu_custom_call", output_to_operand_aliasing={{0}: (1, {})} | custom-call | flops 536870912 | bytes 13111296 | tf_op jit(solution)/shard_map/forward/pallas_call | solution.py:49
  29.2 0.4 collective-permute-start.13
  29.7 0.4 collective-permute-start.10
  30.1 0.3 collective-permute-done.11.refs_1_
  30.5 2.1 %collective-permute-start.12 = (bf16[8,8,512]{2,1,0:T(8,128)(2,1)S(1)}, bf16[8,8,512]{2,1,0:T(8,128)(2,1)S(1)}, u32[]{:S(2)}, u32[]{:S(2)}) collective-permute-start(bf16[8,8,512]{2,1,0:T(8,128)(2,1)S(1)} %fold.11), channel_id=1, source_target_pairs={{0,6},{1,7},{2,4},{3,5},{4,2},{5,3},{6,0},{7,1},{8,14},{9,15},{10,... | collective-permute-start | bytes 196616 | tf_op jit(solution)/shard_map/ppermute | solution.py:34
  32.6 0.6 collective-permute-start.14
  33.2 1.0 %collective-permute-start.16 = (bf16[8,8,512]{2,1,0:T(8,128)(2,1)S(1)}, bf16[8,8,512]{2,1,0:T(8,128)(2,1)S(1)}, u32[]{:S(2)}, u32[]{:S(2)}) collective-permute-start(bf16[8,8,512]{2,1,0:T(8,128)(2,1)S(1)} %fold.13), channel_id=1, source_target_pairs={{0,4},{1,5},{2,6},{3,7},{4,0},{5,1},{6,2},{7,3},{8,12},{9,13},{10,... | collective-permute-start | bytes 196616 | tf_op jit(solution)/shard_map/ppermute | solution.py:34
  34.2 1.5 %collective-permute-done.12.refs_1_ = bf16[8,8,512]{2,1,0:T(8,128)(2,1)S(1)} collective-permute-done((bf16[8,8,512]{2,1,0:T(8,128)(2,1)S(1)}, bf16[8,8,512]{2,1,0:T(8,128)(2,1)S(1)}, u32[]{:S(2)}, u32[]{:S(2)}) %collective-permute-start.12) | collective-permute-done | bytes 65568 | tf_op jit(solution)/shard_map/ppermute | solution.py:34
  35.8 1.3 %collective-permute-done.14.refs_2_ = bf16[8,8,512]{2,1,0:T(8,128)(2,1)S(1)} collective-permute-done((bf16[8,8,512]{2,1,0:T(8,128)(2,1)S(1)}, bf16[8,8,512]{2,1,0:T(8,128)(2,1)S(1)}, u32[]{:S(2)}, u32[]{:S(2)}) %collective-permute-start.14) | collective-permute-done | bytes 65568 | tf_op jit(solution)/shard_map/ppermute | solution.py:34
  37.1 0.4 collective-permute-done.16.refs_3_
  37.5 2.6 %collective-permute-start.17 = (bf16[8,8,512]{2,1,0:T(8,128)(2,1)S(1)}, bf16[8,8,512]{2,1,0:T(8,128)(2,1)S(1)}, u32[]{:S(2)}, u32[]{:S(2)}) collective-permute-start(bf16[8,8,512]{2,1,0:T(8,128)(2,1)S(1)} %get-tuple-element.47), channel_id=1, source_target_pairs={{0,8},{1,9},{2,10},{3,11},{4,12},{5,13},{6,14},{7,15},{8,0},{9,1},... | collective-permute-start | bytes 196616 | tf_op jit(solution)/shard_map/ppermute | solution.py:34
  40.2 3.3 %collective-permute-done.17.refs_1_ = bf16[8,8,512]{2,1,0:T(8,128)(2,1)S(1)} collective-permute-done((bf16[8,8,512]{2,1,0:T(8,128)(2,1)S(1)}, bf16[8,8,512]{2,1,0:T(8,128)(2,1)S(1)}, u32[]{:S(2)}, u32[]{:S(2)}) %collective-permute-start.17) | collective-permute-done | bytes 65568 | tf_op jit(solution)/shard_map/ppermute | solution.py:34
  43.5 1.4 %collective-permute-start.20 = (bf16[8,8,512]{2,1,0:T(8,128)(2,1)S(1)}, bf16[8,8,512]{2,1,0:T(8,128)(2,1)S(1)}, u32[]{:S(2)}, u32[]{:S(2)}) collective-permute-start(bf16[8,8,512]{2,1,0:T(8,128)(2,1)S(1)} %weigh.1.refs_0_), channel_id=1, source_target_pairs={{0,6},{1,7},{2,4},{3,5},{4,2},{5,3},{6,0},{7,1},{8,14},{9,15},{10,... | collective-permute-start | bytes 196616 | tf_op jit(solution)/shard_map/ppermute | solution.py:34
  44.9 1.7 %collective-permute-start.19 = (bf16[8,8,512]{2,1,0:T(8,128)(2,1)S(1)}, bf16[8,8,512]{2,1,0:T(8,128)(2,1)S(1)}, u32[]{:S(2)}, u32[]{:S(2)}) collective-permute-start(bf16[8,8,512]{2,1,0:T(8,128)(2,1)S(1)} %weigh.1.refs_0_), channel_id=1, source_target_pairs={{0,4},{1,5},{2,6},{3,7},{4,0},{5,1},{6,2},{7,3},{8,12},{9,13},{10,... | collective-permute-start | bytes 196616 | tf_op jit(solution)/shard_map/ppermute | solution.py:34
  46.6 0.5 collective-permute-start.18
  47.1 1.7 %collective-permute-done.20.refs_3_ = bf16[8,8,512]{2,1,0:T(8,128)(2,1)S(1)} collective-permute-done((bf16[8,8,512]{2,1,0:T(8,128)(2,1)S(1)}, bf16[8,8,512]{2,1,0:T(8,128)(2,1)S(1)}, u32[]{:S(2)}, u32[]{:S(2)}) %collective-permute-start.20) | collective-permute-done | bytes 65568 | tf_op jit(solution)/shard_map/ppermute | solution.py:34
  48.7 0.8 collective-permute-done.19.refs_2_
  49.5 1.3 %collective-permute-done.18.refs_1_ = bf16[8,8,512]{2,1,0:T(8,128)(2,1)S(1)} collective-permute-done((bf16[8,8,512]{2,1,0:T(8,128)(2,1)S(1)}, bf16[8,8,512]{2,1,0:T(8,128)(2,1)S(1)}, u32[]{:S(2)}, u32[]{:S(2)}) %collective-permute-start.18) | collective-permute-done | bytes 65568 | tf_op jit(solution)/shard_map/ppermute | solution.py:34
  51.2 1.2 %collective-permute-done.21.refs_3_ = bf16[32,8,512]{2,1,0:T(8,128)(2,1)S(1)} collective-permute-done((bf16[32,8,512]{2,1,0:T(8,128)(2,1)S(1)}, bf16[32,8,512]{2,1,0:T(8,128)(2,1)S(1)}, u32[]{:S(2)}, u32[]{:S(2)}) %collective-permute-start.21) | collective-permute-done | bytes 262176 | tf_op jit(solution)/shard_map/ppermute | solution.py:34
  52.4 2.2 %adjoint.1 = (f32[256,8,512]{2,1,0:T(8,128)S(1)}, bf16[64,8,512]{2,1,0:T(8,128)(2,1)S(1)}, bf16[64,8,512]{2,1,0:T(8,128)(2,1)S(1)}) custom-call(s32[8,128]{1,0:T(8,128)S(4)} %get-tuple-element.35.refs_0_, f32[256,8,512]{2,1,0:T(8,128)S(1)} %zeros.3.refs_1_, bf16[32,8,512]{2,1,0:T(8,128)(2,1)S(1)} %join.9.refs_2_, ...), custom_call_target="tpu_custom_call", output_to_operand_aliasing={{0}: (1, {})} | custom-call | flops 536870912 | bytes 18354176 | tf_op jit(solution)/shard_map/adjoint/pallas_call | solution.py:49
  54.8 0.4 collective-permute-start.26
  55.2 1.4 %collective-permute-done.22.refs_1_ = bf16[64,8,512]{2,1,0:T(8,128)(2,1)S(1)} collective-permute-done((bf16[64,8,512]{2,1,0:T(8,128)(2,1)S(1)}, bf16[64,8,512]{2,1,0:T(8,128)(2,1)S(1)}, u32[]{:S(2)}, u32[]{:S(2)}) %collective-permute-start.22) | collective-permute-done | bytes 524320 | tf_op jit(solution)/shard_map/ppermute | solution.py:34
  56.7 0.4 collective-permute-start.23
  57.4 0.6 collective-permute-start.27
  58.0 7.1 %collective-permute-done.23.refs_1_ = bf16[32,8,512]{2,1,0:T(8,128)(2,1)S(1)} collective-permute-done((bf16[32,8,512]{2,1,0:T(8,128)(2,1)S(1)}, bf16[32,8,512]{2,1,0:T(8,128)(2,1)S(1)}, u32[]{:S(2)}, u32[]{:S(2)}) %collective-permute-start.23) | collective-permute-done | bytes 262176 | tf_op jit(solution)/shard_map/ppermute | solution.py:34
  65.2 0.6 collective-permute-start.24
  65.9 1.2 %collective-permute-start.28 = (bf16[16,8,512]{2,1,0:T(8,128)(2,1)S(1)}, bf16[16,8,512]{2,1,0:T(8,128)(2,1)S(1)}, u32[]{:S(2)}, u32[]{:S(2)}) collective-permute-start(bf16[16,8,512]{2,1,0:T(8,128)(2,1)S(1)} %get-tuple-element.60), channel_id=1, source_target_pairs={{0,4},{1,5},{2,6},{3,7},{4,0},{5,1},{6,2},{7,3},{8,12},{9,13},{10,... | collective-permute-start | bytes 393224 | tf_op jit(solution)/shard_map/ppermute | solution.py:34
  67.1 3.1 %collective-permute-done.24.refs_1_ = bf16[16,8,512]{2,1,0:T(8,128)(2,1)S(1)} collective-permute-done((bf16[16,8,512]{2,1,0:T(8,128)(2,1)S(1)}, bf16[16,8,512]{2,1,0:T(8,128)(2,1)S(1)}, u32[]{:S(2)}, u32[]{:S(2)}) %collective-permute-start.24) | collective-permute-done | bytes 131104 | tf_op jit(solution)/shard_map/ppermute | solution.py:34
  70.2 1.9 %collective-permute-start.25 = (bf16[8,8,512]{2,1,0:T(8,128)(2,1)S(1)}, bf16[8,8,512]{2,1,0:T(8,128)(2,1)S(1)}, u32[]{:S(2)}, u32[]{:S(2)}) collective-permute-start(bf16[8,8,512]{2,1,0:T(8,128)(2,1)S(1)} %get-tuple-element.55), channel_id=1, source_target_pairs={{0,8},{1,9},{2,10},{3,11},{4,12},{5,13},{6,14},{7,15},{8,0},{9,1},... | collective-permute-start | bytes 196616 | tf_op jit(solution)/shard_map/ppermute | solution.py:34
  72.2 1.2 %collective-permute-start.29 = (bf16[8,8,512]{2,1,0:T(8,128)(2,1)S(1)}, bf16[8,8,512]{2,1,0:T(8,128)(2,1)S(1)}, u32[]{:S(2)}, u32[]{:S(2)}) collective-permute-start(bf16[8,8,512]{2,1,0:T(8,128)(2,1)S(1)} %get-tuple-element.62), channel_id=1, source_target_pairs={{0,8},{1,9},{2,10},{3,11},{4,12},{5,13},{6,14},{7,15},{8,0},{9,1},... | collective-permute-start | bytes 196616 | tf_op jit(solution)/shard_map/ppermute | solution.py:34
  73.4 2.7 %collective-permute-done.25.refs_1_ = bf16[8,8,512]{2,1,0:T(8,128)(2,1)S(1)} collective-permute-done((bf16[8,8,512]{2,1,0:T(8,128)(2,1)S(1)}, bf16[8,8,512]{2,1,0:T(8,128)(2,1)S(1)}, u32[]{:S(2)}, u32[]{:S(2)}) %collective-permute-start.25) | collective-permute-done | bytes 65568 | tf_op jit(solution)/shard_map/ppermute | solution.py:34
  76.1 1.7 %collective-permute-done.29.refs_3_ = bf16[8,8,512]{2,1,0:T(8,128)(2,1)S(1)} collective-permute-done((bf16[8,8,512]{2,1,0:T(8,128)(2,1)S(1)}, bf16[8,8,512]{2,1,0:T(8,128)(2,1)S(1)}, u32[]{:S(2)}, u32[]{:S(2)}) %collective-permute-start.29) | collective-permute-done | bytes 65568 | tf_op jit(solution)/shard_map/ppermute | solution.py:34
  77.8 0.7 final.1
  (37 shorter events, 1.9 us)
Async XLA Ops:
  1.1 7.8 %collective-permute-start.2 = (bf16[8,8,512]{2,1,0:T(8,128)(2,1)S(1)}, bf16[8,8,512]{2,1,0:T(8,128)(2,1)S(1)}, u32[]{:S(2)}, u32[]{:S(2)}) collective-permute-start(bf16[8,8,512]{2,1,0:T(8,128)(2,1)S(1)} %get-tuple-element.38.refs_0_), channel_id=1, source_target_pairs={{0,8},{1,9},{2,10},{3,11},{4,12},{5,13},{6,14},{7,15},{8,0},{9,1},... | collective-permute-start | bytes 196616 | tf_op jit(solution)/shard_map/ppermute | solution.py:34
  5.2 4.7 %collective-permute-start = (bf16[8,8,512]{2,1,0:T(8,128)(2,1)S(1)}, bf16[8,8,512]{2,1,0:T(8,128)(2,1)S(1)}, u32[]{:S(2)}, u32[]{:S(2)}) collective-permute-start(bf16[8,8,512]{2,1,0:T(8,128)(2,1)S(1)} %get-tuple-element.36.refs_0_), channel_id=1, source_target_pairs={{0,2},{1,3},{2,0},{3,1},{4,6},{5,7},{6,4},{7,5},{8,10},{9,11},{10,... | collective-permute-start | bytes 196616 | tf_op jit(solution)/shard_map/ppermute | solution.py:34
  8.8 7.6 %collective-permute-start.3 = (bf16[16,8,512]{2,1,0:T(8,128)(2,1)S(1)}, bf16[16,8,512]{2,1,0:T(8,128)(2,1)S(1)}, u32[]{:S(2)}, u32[]{:S(2)}) collective-permute-start(bf16[16,8,512]{2,1,0:T(8,128)(2,1)S(1)} %join.6.refs_3_.refs_0_), channel_id=1, source_target_pairs={{0,4},{1,5},{2,6},{3,7},{4,0},{5,1},{6,2},{7,3},{8,12},{9,13},{10,... | collective-permute-start | bytes 393224 | tf_op jit(solution)/shard_map/ppermute | solution.py:34
  9.9 9.0 %collective-permute-start.1 = (bf16[16,8,512]{2,1,0:T(8,128)(2,1)S(1)}, bf16[16,8,512]{2,1,0:T(8,128)(2,1)S(1)}, u32[]{:S(2)}, u32[]{:S(2)}) collective-permute-start(bf16[16,8,512]{2,1,0:T(8,128)(2,1)S(1)} %join.5.refs_2_.refs_0_), channel_id=1, source_target_pairs={{0,8},{1,9},{2,10},{3,11},{4,12},{5,13},{6,14},{7,15},{8,0},{9,1},... | collective-permute-start | bytes 393224 | tf_op jit(solution)/shard_map/ppermute | solution.py:34
  16.5 7.4 %collective-permute-start.5 = (bf16[32,8,512]{2,1,0:T(8,128)(2,1)S(1)}, bf16[32,8,512]{2,1,0:T(8,128)(2,1)S(1)}, u32[]{:S(2)}, u32[]{:S(2)}) collective-permute-start(bf16[32,8,512]{2,1,0:T(8,128)(2,1)S(1)} %join.8.refs_1_.refs_4_), channel_id=1, source_target_pairs={{0,2},{1,3},{2,0},{3,1},{4,6},{5,7},{6,4},{7,5},{8,10},{9,11},{10,... | collective-permute-start | bytes 786440 | tf_op jit(solution)/shard_map/ppermute | solution.py:34
  18.9 6.4 %collective-permute-start.4 = (bf16[32,8,512]{2,1,0:T(8,128)(2,1)S(1)}, bf16[32,8,512]{2,1,0:T(8,128)(2,1)S(1)}, u32[]{:S(2)}, u32[]{:S(2)}) collective-permute-start(bf16[32,8,512]{2,1,0:T(8,128)(2,1)S(1)} %join.7.refs_0_.refs_2_), channel_id=1, source_target_pairs={{0,4},{1,5},{2,6},{3,7},{4,0},{5,1},{6,2},{7,3},{8,12},{9,13},{10,... | collective-permute-start | bytes 786440 | tf_op jit(solution)/shard_map/ppermute | solution.py:34
  19.2 6.2 %collective-permute-start.8 = (bf16[32,8,512]{2,1,0:T(8,128)(2,1)S(1)}, bf16[32,8,512]{2,1,0:T(8,128)(2,1)S(1)}, u32[]{:S(2)}, u32[]{:S(2)}) collective-permute-start(bf16[32,8,512]{2,1,0:T(8,128)(2,1)S(1)} %join.8.refs_1_.refs_4_), channel_id=1, source_target_pairs={{0,1},{1,0},{2,3},{3,2},{4,5},{5,4},{6,7},{7,6},{8,9},{9,8},{10,11... | collective-permute-start | bytes 786440 | tf_op jit(solution)/shard_map/ppermute | solution.py:34
  19.2 6.2 %collective-permute-start.6 = (bf16[32,8,512]{2,1,0:T(8,128)(2,1)S(1)}, bf16[32,8,512]{2,1,0:T(8,128)(2,1)S(1)}, u32[]{:S(2)}, u32[]{:S(2)}) collective-permute-start(bf16[32,8,512]{2,1,0:T(8,128)(2,1)S(1)} %join.7.refs_0_.refs_2_), channel_id=1, source_target_pairs={{0,1},{1,0},{2,3},{3,2},{4,5},{5,4},{6,7},{7,6},{8,9},{9,8},{10,11... | collective-permute-start | bytes 786440 | tf_op jit(solution)/shard_map/ppermute | solution.py:34
  23.8 1.6 %collective-permute-start.9 = (bf16[32,8,512]{2,1,0:T(8,128)(2,1)S(1)}, bf16[32,8,512]{2,1,0:T(8,128)(2,1)S(1)}, u32[]{:S(2)}, u32[]{:S(2)}) collective-permute-start(bf16[32,8,512]{2,1,0:T(8,128)(2,1)S(1)} %collective-permute-done.5.refs_5_), channel_id=1, source_target_pairs={{0,1},{1,0},{2,3},{3,2},{4,5},{5,4},{6,7},{7,6},{8,9},{9,8},{10,11... | collective-permute-start | bytes 786440 | tf_op jit(solution)/shard_map/ppermute | solution.py:34
  25.3 1.5 %collective-permute-start.7 = (bf16[32,8,512]{2,1,0:T(8,128)(2,1)S(1)}, bf16[32,8,512]{2,1,0:T(8,128)(2,1)S(1)}, u32[]{:S(2)}, u32[]{:S(2)}) collective-permute-start(bf16[32,8,512]{2,1,0:T(8,128)(2,1)S(1)} %collective-permute-done.4.refs_3_), channel_id=1, source_target_pairs={{0,1},{1,0},{2,3},{3,2},{4,5},{5,4},{6,7},{7,6},{8,9},{9,8},{10,11... | collective-permute-start | bytes 786440 | tf_op jit(solution)/shard_map/ppermute | solution.py:34
  29.0 1.4 %collective-permute-start.11 = (f32[8,8,512]{2,1,0:T(8,128)S(1)}, f32[8,8,512]{2,1,0:T(8,128)S(1)}, u32[]{:S(2)}, u32[]{:S(2)}) collective-permute-start(f32[8,8,512]{2,1,0:T(8,128)S(1)} %get-tuple-element.43), channel_id=1, source_target_pairs={{0,1},{1,0},{2,3},{3,2},{4,5},{5,4},{6,7},{7,6},{8,9},{9,8},{10,11... | collective-permute-start | bytes 393224 | tf_op jit(solution)/shard_map/ppermute | solution.py:34
  29.2 3.3 %collective-permute-start.13 = (f32[8,8,512]{2,1,0:T(8,128)S(1)}, f32[8,8,512]{2,1,0:T(8,128)S(1)}, u32[]{:S(2)}, u32[]{:S(2)}) collective-permute-start(f32[8,8,512]{2,1,0:T(8,128)S(1)} %get-tuple-element.44), channel_id=1, source_target_pairs={{0,1},{1,0},{2,3},{3,2},{4,5},{5,4},{6,7},{7,6},{8,9},{9,8},{10,11... | collective-permute-start | bytes 393224 | tf_op jit(solution)/shard_map/ppermute | solution.py:34
  29.6 3.5 %collective-permute-start.15 = (f32[8,8,512]{2,1,0:T(8,128)S(1)}, f32[8,8,512]{2,1,0:T(8,128)S(1)}, u32[]{:S(2)}, u32[]{:S(2)}) collective-permute-start(f32[8,8,512]{2,1,0:T(8,128)S(1)} %get-tuple-element.45), channel_id=1, source_target_pairs={{0,1},{1,0},{2,3},{3,2},{4,5},{5,4},{6,7},{7,6},{8,9},{9,8},{10,11... | collective-permute-start | bytes 393224 | tf_op jit(solution)/shard_map/ppermute | solution.py:34
  29.7 4.5 %collective-permute-start.10 = (f32[8,8,512]{2,1,0:T(8,128)S(1)}, f32[8,8,512]{2,1,0:T(8,128)S(1)}, u32[]{:S(2)}, u32[]{:S(2)}) collective-permute-start(f32[8,8,512]{2,1,0:T(8,128)S(1)} %get-tuple-element.42), channel_id=1, source_target_pairs={{0,1},{1,0},{2,3},{3,2},{4,5},{5,4},{6,7},{7,6},{8,9},{9,8},{10,11... | collective-permute-start | bytes 393224 | tf_op jit(solution)/shard_map/ppermute | solution.py:34
  30.5 5.3 %collective-permute-start.12 = (bf16[8,8,512]{2,1,0:T(8,128)(2,1)S(1)}, bf16[8,8,512]{2,1,0:T(8,128)(2,1)S(1)}, u32[]{:S(2)}, u32[]{:S(2)}) collective-permute-start(bf16[8,8,512]{2,1,0:T(8,128)(2,1)S(1)} %fold.11), channel_id=1, source_target_pairs={{0,6},{1,7},{2,4},{3,5},{4,2},{5,3},{6,0},{7,1},{8,14},{9,15},{10,... | collective-permute-start | bytes 196616 | tf_op jit(solution)/shard_map/ppermute | solution.py:34
  32.6 4.5 %collective-permute-start.14 = (bf16[8,8,512]{2,1,0:T(8,128)(2,1)S(1)}, bf16[8,8,512]{2,1,0:T(8,128)(2,1)S(1)}, u32[]{:S(2)}, u32[]{:S(2)}) collective-permute-start(bf16[8,8,512]{2,1,0:T(8,128)(2,1)S(1)} %fold.12), channel_id=1, source_target_pairs={{0,2},{1,3},{2,0},{3,1},{4,6},{5,7},{6,4},{7,5},{8,10},{9,11},{10,... | collective-permute-start | bytes 196616 | tf_op jit(solution)/shard_map/ppermute | solution.py:34
  33.2 4.3 %collective-permute-start.16 = (bf16[8,8,512]{2,1,0:T(8,128)(2,1)S(1)}, bf16[8,8,512]{2,1,0:T(8,128)(2,1)S(1)}, u32[]{:S(2)}, u32[]{:S(2)}) collective-permute-start(bf16[8,8,512]{2,1,0:T(8,128)(2,1)S(1)} %fold.13), channel_id=1, source_target_pairs={{0,4},{1,5},{2,6},{3,7},{4,0},{5,1},{6,2},{7,3},{8,12},{9,13},{10,... | collective-permute-start | bytes 196616 | tf_op jit(solution)/shard_map/ppermute | solution.py:34
  37.5 5.9 %collective-permute-start.17 = (bf16[8,8,512]{2,1,0:T(8,128)(2,1)S(1)}, bf16[8,8,512]{2,1,0:T(8,128)(2,1)S(1)}, u32[]{:S(2)}, u32[]{:S(2)}) collective-permute-start(bf16[8,8,512]{2,1,0:T(8,128)(2,1)S(1)} %get-tuple-element.47), channel_id=1, source_target_pairs={{0,8},{1,9},{2,10},{3,11},{4,12},{5,13},{6,14},{7,15},{8,0},{9,1},... | collective-permute-start | bytes 196616 | tf_op jit(solution)/shard_map/ppermute | solution.py:34
  43.5 5.2 %collective-permute-start.20 = (bf16[8,8,512]{2,1,0:T(8,128)(2,1)S(1)}, bf16[8,8,512]{2,1,0:T(8,128)(2,1)S(1)}, u32[]{:S(2)}, u32[]{:S(2)}) collective-permute-start(bf16[8,8,512]{2,1,0:T(8,128)(2,1)S(1)} %weigh.1.refs_0_), channel_id=1, source_target_pairs={{0,6},{1,7},{2,4},{3,5},{4,2},{5,3},{6,0},{7,1},{8,14},{9,15},{10,... | collective-permute-start | bytes 196616 | tf_op jit(solution)/shard_map/ppermute | solution.py:34
  44.9 4.6 %collective-permute-start.19 = (bf16[8,8,512]{2,1,0:T(8,128)(2,1)S(1)}, bf16[8,8,512]{2,1,0:T(8,128)(2,1)S(1)}, u32[]{:S(2)}, u32[]{:S(2)}) collective-permute-start(bf16[8,8,512]{2,1,0:T(8,128)(2,1)S(1)} %weigh.1.refs_0_), channel_id=1, source_target_pairs={{0,4},{1,5},{2,6},{3,7},{4,0},{5,1},{6,2},{7,3},{8,12},{9,13},{10,... | collective-permute-start | bytes 196616 | tf_op jit(solution)/shard_map/ppermute | solution.py:34
  46.6 4.3 %collective-permute-start.18 = (bf16[8,8,512]{2,1,0:T(8,128)(2,1)S(1)}, bf16[8,8,512]{2,1,0:T(8,128)(2,1)S(1)}, u32[]{:S(2)}, u32[]{:S(2)}) collective-permute-start(bf16[8,8,512]{2,1,0:T(8,128)(2,1)S(1)} %weigh.1.refs_0_), channel_id=1, source_target_pairs={{0,2},{1,3},{2,0},{3,1},{4,6},{5,7},{6,4},{7,5},{8,10},{9,11},{10,... | collective-permute-start | bytes 196616 | tf_op jit(solution)/shard_map/ppermute | solution.py:34
  50.8 1.6 %collective-permute-start.21 = (bf16[32,8,512]{2,1,0:T(8,128)(2,1)S(1)}, bf16[32,8,512]{2,1,0:T(8,128)(2,1)S(1)}, u32[]{:S(2)}, u32[]{:S(2)}) collective-permute-start(bf16[32,8,512]{2,1,0:T(8,128)(2,1)S(1)} %join.9.refs_2_), channel_id=1, source_target_pairs={{0,1},{1,0},{2,3},{3,2},{4,5},{5,4},{6,7},{7,6},{8,9},{9,8},{10,11... | collective-permute-start | bytes 786440 | tf_op jit(solution)/shard_map/ppermute | solution.py:34
  54.6 2.0 %collective-permute-start.22 = (bf16[64,8,512]{2,1,0:T(8,128)(2,1)S(1)}, bf16[64,8,512]{2,1,0:T(8,128)(2,1)S(1)}, u32[]{:S(2)}, u32[]{:S(2)}) collective-permute-start(bf16[64,8,512]{2,1,0:T(8,128)(2,1)S(1)} %get-tuple-element.49), channel_id=1, source_target_pairs={{0,1},{1,0},{2,3},{3,2},{4,5},{5,4},{6,7},{7,6},{8,9},{9,8},{10,11... | collective-permute-start | bytes 1572872 | tf_op jit(solution)/shard_map/ppermute | solution.py:34
  54.8 2.5 %collective-permute-start.26 = (bf16[64,8,512]{2,1,0:T(8,128)(2,1)S(1)}, bf16[64,8,512]{2,1,0:T(8,128)(2,1)S(1)}, u32[]{:S(2)}, u32[]{:S(2)}) collective-permute-start(bf16[64,8,512]{2,1,0:T(8,128)(2,1)S(1)} %get-tuple-element.56), channel_id=1, source_target_pairs={{0,1},{1,0},{2,3},{3,2},{4,5},{5,4},{6,7},{7,6},{8,9},{9,8},{10,11... | collective-permute-start | bytes 1572872 | tf_op jit(solution)/shard_map/ppermute | solution.py:34
  56.7 8.4 %collective-permute-start.23 = (bf16[32,8,512]{2,1,0:T(8,128)(2,1)S(1)}, bf16[32,8,512]{2,1,0:T(8,128)(2,1)S(1)}, u32[]{:S(2)}, u32[]{:S(2)}) collective-permute-start(bf16[32,8,512]{2,1,0:T(8,128)(2,1)S(1)} %get-tuple-element.51), channel_id=1, source_target_pairs={{0,4},{1,5},{2,6},{3,7},{4,0},{5,1},{6,2},{7,3},{8,12},{9,13},{10,... | collective-permute-start | bytes 786440 | tf_op jit(solution)/shard_map/ppermute | solution.py:34
  57.4 8.4 %collective-permute-start.27 = (bf16[32,8,512]{2,1,0:T(8,128)(2,1)S(1)}, bf16[32,8,512]{2,1,0:T(8,128)(2,1)S(1)}, u32[]{:S(2)}, u32[]{:S(2)}) collective-permute-start(bf16[32,8,512]{2,1,0:T(8,128)(2,1)S(1)} %get-tuple-element.58), channel_id=1, source_target_pairs={{0,2},{1,3},{2,0},{3,1},{4,6},{5,7},{6,4},{7,5},{8,10},{9,11},{10,... | collective-permute-start | bytes 786440 | tf_op jit(solution)/shard_map/ppermute | solution.py:34
  65.2 5.0 %collective-permute-start.24 = (bf16[16,8,512]{2,1,0:T(8,128)(2,1)S(1)}, bf16[16,8,512]{2,1,0:T(8,128)(2,1)S(1)}, u32[]{:S(2)}, u32[]{:S(2)}) collective-permute-start(bf16[16,8,512]{2,1,0:T(8,128)(2,1)S(1)} %get-tuple-element.53), channel_id=1, source_target_pairs={{0,2},{1,3},{2,0},{3,1},{4,6},{5,7},{6,4},{7,5},{8,10},{9,11},{10,... | collective-permute-start | bytes 393224 | tf_op jit(solution)/shard_map/ppermute | solution.py:34
  65.9 6.2 %collective-permute-start.28 = (bf16[16,8,512]{2,1,0:T(8,128)(2,1)S(1)}, bf16[16,8,512]{2,1,0:T(8,128)(2,1)S(1)}, u32[]{:S(2)}, u32[]{:S(2)}) collective-permute-start(bf16[16,8,512]{2,1,0:T(8,128)(2,1)S(1)} %get-tuple-element.60), channel_id=1, source_target_pairs={{0,4},{1,5},{2,6},{3,7},{4,0},{5,1},{6,2},{7,3},{8,12},{9,13},{10,... | collective-permute-start | bytes 393224 | tf_op jit(solution)/shard_map/ppermute | solution.py:34
  70.2 5.9 %collective-permute-start.25 = (bf16[8,8,512]{2,1,0:T(8,128)(2,1)S(1)}, bf16[8,8,512]{2,1,0:T(8,128)(2,1)S(1)}, u32[]{:S(2)}, u32[]{:S(2)}) collective-permute-start(bf16[8,8,512]{2,1,0:T(8,128)(2,1)S(1)} %get-tuple-element.55), channel_id=1, source_target_pairs={{0,8},{1,9},{2,10},{3,11},{4,12},{5,13},{6,14},{7,15},{8,0},{9,1},... | collective-permute-start | bytes 196616 | tf_op jit(solution)/shard_map/ppermute | solution.py:34
  72.2 5.7 %collective-permute-start.29 = (bf16[8,8,512]{2,1,0:T(8,128)(2,1)S(1)}, bf16[8,8,512]{2,1,0:T(8,128)(2,1)S(1)}, u32[]{:S(2)}, u32[]{:S(2)}) collective-permute-start(bf16[8,8,512]{2,1,0:T(8,128)(2,1)S(1)} %get-tuple-element.62), channel_id=1, source_target_pairs={{0,8},{1,9},{2,10},{3,11},{4,12},{5,13},{6,14},{7,15},{8,0},{9,1},... | collective-permute-start | bytes 196616 | tf_op jit(solution)/shard_map/ppermute | solution.py:34

commit v17 on v15

--- a/solution.py
+++ b/solution.py
@@ -366,7 +366,7 @@
     pieces = pieces + [swap(piece, 1) for piece in pieces]
 
     acc = zeros((peers * station_blocks, probe_count, station_width), (part_p, part_q))
-    total, *sends = tiles(pieces, 0, 1, table, v_here, u_here, acc, 4, F32, "forward")
+    total, *sends = tiles(pieces, 0, 1, table, v_here, u_here, acc, 4, BF16, "forward")
     quarters = [0] * 4
     for k in SQUARE + (0,):
         kept = F32 if k == 0 else BF16

time: 78.9 us -> 78.8 us (level)
  no operation moved by 1% of the time
where the time goes in v17:
time: 78.8 us; the launch traced here: 78.5 us
  waiting for transfers between devices  36 us (46%)
  starting transfers between devices  29.4 us (37%)
  Pallas kernels  12.9 us (16%)
    ppermute x30, waiting for transfers between devices, swap(): return lax.ppermute(array, 'tile', [(i, i ^ bits) for i in range(count)])  36 us
    ppermute x30, starting transfers between devices, swap(): return lax.ppermute(array, 'tile', [(i, i ^ bits) for i in range(count)])  29.4 us
    pallas_call x26, Pallas kernels, local(): pl.pallas_call(run, out_shape=[a if s.memory_space is None else s.memory_...  12.9 us
  transfers between devices with their start and end apart: 30, of which 20 were waited for; matrix products, arithmetic and copies ran while one was open for 0% of the time, Pallas kernels for 9%

profile of v17, /device:TPU:0, one launch (start us, length us, event | category | flops | bytes accessed | tf_op | source)
XLA Modules:
  0.0 78.5 jit_solution(18407878837005889647)
XLA Ops:
  0.0 1.1 %scale.1 = (bf16[8,8,512]{2,1,0:T(8,128)(2,1)S(1)}, bf16[8,8,512]{2,1,0:T(8,128)(2,1)S(1)}, f32[64,128]{1,0:T(8,128)S(1)}) custom-call(f32[4]{0:T(128)} %refs_0_.3, f32[64,128]{1,0:T(8,128)} %bitcast.9, s32[64,128]{1,0:T(8,128)} %bitcast.10, f32[8,8192]{1,0:T(8,128)} %refs_3_.1), custom_call_target="tpu_custom_call" | custom-call | bytes 491536 | tf_op jit(solution)/shard_map/scale/pallas_call | solution.py:49
  1.1 4.1 %collective-permute-start.2 = (bf16[8,8,512]{2,1,0:T(8,128)(2,1)S(1)}, bf16[8,8,512]{2,1,0:T(8,128)(2,1)S(1)}, u32[]{:S(2)}, u32[]{:S(2)}) collective-permute-start(bf16[8,8,512]{2,1,0:T(8,128)(2,1)S(1)} %get-tuple-element.36.refs_0_), channel_id=1, source_target_pairs={{0,8},{1,9},{2,10},{3,11},{4,12},{5,13},{6,14},{7,15},{8,0},{9,1},... | collective-permute-start | bytes 196616 | tf_op jit(solution)/shard_map/ppermute | solution.py:34
  5.2 1.5 %collective-permute-start = (bf16[8,8,512]{2,1,0:T(8,128)(2,1)S(1)}, bf16[8,8,512]{2,1,0:T(8,128)(2,1)S(1)}, u32[]{:S(2)}, u32[]{:S(2)}) collective-permute-start(bf16[8,8,512]{2,1,0:T(8,128)(2,1)S(1)} %get-tuple-element.34.refs_0_), channel_id=1, source_target_pairs={{0,2},{1,3},{2,0},{3,1},{4,6},{5,7},{6,4},{7,5},{8,10},{9,11},{10,... | collective-permute-start | bytes 196616 | tf_op jit(solution)/shard_map/ppermute | solution.py:34
  6.7 1.5 %plan.1 = (s32[8,128]{1,0:T(8,128)S(4)}, f32[32,128]{1,0:T(8,128)S(1)}) custom-call(s32[16,128]{1,0:T(8,128)} %bitcast.11, s32[16,128]{1,0:T(8,128)} %bitcast.12, s32[16,128]{1,0:T(8,128)} %bitcast.13, s32[16,128]{1,0:T(8,128)} %bitcast.14, s32[16,128]{1,0:T(8,128)} %bitcast.15, f32[256,128]{1,0:T(8,128)} %bitcast.8, ...), custom_call_target="tpu_custom_call" | custom-call | bytes 192512 | tf_op jit(solution)/shard_map/plan/pallas_call | solution.py:49
  8.2 0.6 collective-permute-done.2.refs_1_
  8.8 1.0 %collective-permute-start.3 = (bf16[16,8,512]{2,1,0:T(8,128)(2,1)S(1)}, bf16[16,8,512]{2,1,0:T(8,128)(2,1)S(1)}, u32[]{:S(2)}, u32[]{:S(2)}) collective-permute-start(bf16[16,8,512]{2,1,0:T(8,128)(2,1)S(1)} %join.6.refs_2_.refs_0_), channel_id=1, source_target_pairs={{0,4},{1,5},{2,6},{3,7},{4,0},{5,1},{6,2},{7,3},{8,12},{9,13},{10,... | collective-permute-start | bytes 393224 | tf_op jit(solution)/shard_map/ppermute | solution.py:34
  9.9 3.1 %collective-permute-start.1 = (bf16[16,8,512]{2,1,0:T(8,128)(2,1)S(1)}, bf16[16,8,512]{2,1,0:T(8,128)(2,1)S(1)}, u32[]{:S(2)}, u32[]{:S(2)}) collective-permute-start(bf16[16,8,512]{2,1,0:T(8,128)(2,1)S(1)} %join.5.refs_1_.refs_0_), channel_id=1, source_target_pairs={{0,8},{1,9},{2,10},{3,11},{4,12},{5,13},{6,14},{7,15},{8,0},{9,1},... | collective-permute-start | bytes 393224 | tf_op jit(solution)/shard_map/ppermute | solution.py:34
  12.9 2.2 %load_v.1.refs_3_.refs_10_.refs_5_ = bf16[128,32,512]{2,1,0:T(8,128)(2,1)S(1)} custom-call(bf16[128,32,512]{2,1,0:T(8,128)(2,1)} %refs_0_.4, bf16[16,8,512]{2,1,0:T(8,128)(2,1)S(1)} %join.5.refs_1_.refs_0_, bf16[16,8,512]{2,1,0:T(8,128)(2,1)S(1)} %join.6.refs_2_.refs_0_), custom_call_target="tpu_custom_call" | custom-call | bytes 8388608 | tf_op jit(solution)/shard_map/load_v/pallas_call | solution.py:49
  15.2 2.2 %load_u.1.refs_2_.refs_11_.refs_4_ = bf16[128,32,512]{2,1,0:T(8,128)(2,1)S(1)} custom-call(bf16[128,32,512]{2,1,0:T(8,128)(2,1)} %refs_0_.5, bf16[16,8,512]{2,1,0:T(8,128)(2,1)S(1)} %join.5.refs_1_.refs_0_, bf16[16,8,512]{2,1,0:T(8,128)(2,1)S(1)} %join.6.refs_2_.refs_0_, bf16[128,32,512]{2,1,0:T(8,128)(2,1)S(1)} %load_v.1.refs_3_.refs_10_.refs_5_), custom_call_target="tpu_custom_call" | custom-call | bytes 8388608 | tf_op jit(solution)/shard_map/load_u/pallas_call | solution.py:49
  17.4 1.6 %collective-permute-start.5 = (bf16[32,8,512]{2,1,0:T(8,128)(2,1)S(1)}, bf16[32,8,512]{2,1,0:T(8,128)(2,1)S(1)}, u32[]{:S(2)}, u32[]{:S(2)}) collective-permute-start(bf16[32,8,512]{2,1,0:T(8,128)(2,1)S(1)} %join.8.refs_1_.refs_4_), channel_id=1, source_target_pairs={{0,2},{1,3},{2,0},{3,1},{4,6},{5,7},{6,4},{7,5},{8,10},{9,11},{10,... | collective-permute-start | bytes 786440 | tf_op jit(solution)/shard_map/ppermute | solution.py:34
  19.2 0.5 collective-permute-start.6
  19.7 5.1 %collective-permute-done.5.refs_5_ = bf16[32,8,512]{2,1,0:T(8,128)(2,1)S(1)} collective-permute-done((bf16[32,8,512]{2,1,0:T(8,128)(2,1)S(1)}, bf16[32,8,512]{2,1,0:T(8,128)(2,1)S(1)}, u32[]{:S(2)}, u32[]{:S(2)}) %collective-permute-start.5) | collective-permute-done | bytes 262176 | tf_op jit(solution)/shard_map/ppermute | solution.py:34
  24.8 1.3 %collective-permute-done.4.refs_3_ = bf16[32,8,512]{2,1,0:T(8,128)(2,1)S(1)} collective-permute-done((bf16[32,8,512]{2,1,0:T(8,128)(2,1)S(1)}, bf16[32,8,512]{2,1,0:T(8,128)(2,1)S(1)}, u32[]{:S(2)}, u32[]{:S(2)}) %collective-permute-start.4) | collective-permute-done | bytes 262176 | tf_op jit(solution)/shard_map/ppermute | solution.py:34
  26.3 1.3 %collective-permute-done.7.refs_7_ = bf16[32,8,512]{2,1,0:T(8,128)(2,1)S(1)} collective-permute-done((bf16[32,8,512]{2,1,0:T(8,128)(2,1)S(1)}, bf16[32,8,512]{2,1,0:T(8,128)(2,1)S(1)}, u32[]{:S(2)}, u32[]{:S(2)}) %collective-permute-start.7) | collective-permute-done | bytes 262176 | tf_op jit(solution)/shard_map/ppermute | solution.py:34
  27.7 2.2 %forward.1 = (f32[64,8,512]{2,1,0:T(8,128)S(1)}, bf16[8,8,512]{2,1,0:T(8,128)(2,1)S(1)}, bf16[8,8,512]{2,1,0:T(8,128)(2,1)S(1)}, bf16[8,8,512]{2,1,0:T(8,128)(2,1)S(1)}, bf16[8,8,512]{2,1,0:T(8,128)(2,1)S(1)}) custom-call(s32[8,128]{1,0:T(8,128)S(4)} %get-tuple-element.33.refs_0_, f32[64,8,512]{2,1,0:T(8,128)S(1)} %zeros.2.refs_1_, ...), custom_call_target="tpu_custom_call", output_to_operand_aliasing={{0}: (1, {})} | custom-call | flops 536870912 | bytes 12849152 | tf_op jit(solution)/shard_map/forward/pallas_call | solution.py:49
  30.1 0.4 collective-permute-start.13
  30.6 0.4 collective-permute-start.10
  31.0 0.2 collective-permute-done.11.refs_1_
  31.2 1.3 %collective-permute-start.12 = (bf16[8,8,512]{2,1,0:T(8,128)(2,1)S(1)}, bf16[8,8,512]{2,1,0:T(8,128)(2,1)S(1)}, u32[]{:S(2)}, u32[]{:S(2)}) collective-permute-start(bf16[8,8,512]{2,1,0:T(8,128)(2,1)S(1)} %fold.11), channel_id=1, source_target_pairs={{0,6},{1,7},{2,4},{3,5},{4,2},{5,3},{6,0},{7,1},{8,14},{9,15},{10,... | collective-permute-start | bytes 196616 | tf_op jit(solution)/shard_map/ppermute | solution.py:34
  32.5 0.6 collective-permute-start.14
  33.1 1.8 %collective-permute-start.16 = (bf16[8,8,512]{2,1,0:T(8,128)(2,1)S(1)}, bf16[8,8,512]{2,1,0:T(8,128)(2,1)S(1)}, u32[]{:S(2)}, u32[]{:S(2)}) collective-permute-start(bf16[8,8,512]{2,1,0:T(8,128)(2,1)S(1)} %fold.13), channel_id=1, source_target_pairs={{0,4},{1,5},{2,6},{3,7},{4,0},{5,1},{6,2},{7,3},{8,12},{9,13},{10,... | collective-permute-start | bytes 196616 | tf_op jit(solution)/shard_map/ppermute | solution.py:34
  35.0 1.7 %collective-permute-done.12.refs_1_ = bf16[8,8,512]{2,1,0:T(8,128)(2,1)S(1)} collective-permute-done((bf16[8,8,512]{2,1,0:T(8,128)(2,1)S(1)}, bf16[8,8,512]{2,1,0:T(8,128)(2,1)S(1)}, u32[]{:S(2)}, u32[]{:S(2)}) %collective-permute-start.12) | collective-permute-done | bytes 65568 | tf_op jit(solution)/shard_map/ppermute | solution.py:34
  36.6 1.1 %collective-permute-done.14.refs_2_ = bf16[8,8,512]{2,1,0:T(8,128)(2,1)S(1)} collective-permute-done((bf16[8,8,512]{2,1,0:T(8,128)(2,1)S(1)}, bf16[8,8,512]{2,1,0:T(8,128)(2,1)S(1)}, u32[]{:S(2)}, u32[]{:S(2)}) %collective-permute-start.14) | collective-permute-done | bytes 65568 | tf_op jit(solution)/shard_map/ppermute | solution.py:34
  37.8 2.3 %collective-permute-start.17 = (bf16[8,8,512]{2,1,0:T(8,128)(2,1)S(1)}, bf16[8,8,512]{2,1,0:T(8,128)(2,1)S(1)}, u32[]{:S(2)}, u32[]{:S(2)}) collective-permute-start(bf16[8,8,512]{2,1,0:T(8,128)(2,1)S(1)} %get-tuple-element.43), channel_id=1, source_target_pairs={{0,8},{1,9},{2,10},{3,11},{4,12},{5,13},{6,14},{7,15},{8,0},{9,1},... | collective-permute-start | bytes 196616 | tf_op jit(solution)/shard_map/ppermute | solution.py:34
  40.1 3.0 %collective-permute-done.17.refs_1_ = bf16[8,8,512]{2,1,0:T(8,128)(2,1)S(1)} collective-permute-done((bf16[8,8,512]{2,1,0:T(8,128)(2,1)S(1)}, bf16[8,8,512]{2,1,0:T(8,128)(2,1)S(1)}, u32[]{:S(2)}, u32[]{:S(2)}) %collective-permute-start.17) | collective-permute-done | bytes 65568 | tf_op jit(solution)/shard_map/ppermute | solution.py:34
  43.1 1.7 %collective-permute-start.20 = (bf16[8,8,512]{2,1,0:T(8,128)(2,1)S(1)}, bf16[8,8,512]{2,1,0:T(8,128)(2,1)S(1)}, u32[]{:S(2)}, u32[]{:S(2)}) collective-permute-start(bf16[8,8,512]{2,1,0:T(8,128)(2,1)S(1)} %weigh.1.refs_0_), channel_id=1, source_target_pairs={{0,6},{1,7},{2,4},{3,5},{4,2},{5,3},{6,0},{7,1},{8,14},{9,15},{10,... | collective-permute-start | bytes 196616 | tf_op jit(solution)/shard_map/ppermute | solution.py:34
  44.8 1.7 %collective-permute-start.19 = (bf16[8,8,512]{2,1,0:T(8,128)(2,1)S(1)}, bf16[8,8,512]{2,1,0:T(8,128)(2,1)S(1)}, u32[]{:S(2)}, u32[]{:S(2)}) collective-permute-start(bf16[8,8,512]{2,1,0:T(8,128)(2,1)S(1)} %weigh.1.refs_0_), channel_id=1, source_target_pairs={{0,4},{1,5},{2,6},{3,7},{4,0},{5,1},{6,2},{7,3},{8,12},{9,13},{10,... | collective-permute-start | bytes 196616 | tf_op jit(solution)/shard_map/ppermute | solution.py:34
  46.7 1.7 %collective-permute-done.20.refs_3_ = bf16[8,8,512]{2,1,0:T(8,128)(2,1)S(1)} collective-permute-done((bf16[8,8,512]{2,1,0:T(8,128)(2,1)S(1)}, bf16[8,8,512]{2,1,0:T(8,128)(2,1)S(1)}, u32[]{:S(2)}, u32[]{:S(2)}) %collective-permute-start.20) | collective-permute-done | bytes 65568 | tf_op jit(solution)/shard_map/ppermute | solution.py:34
  48.3 1.1 %collective-permute-done.19.refs_2_ = bf16[8,8,512]{2,1,0:T(8,128)(2,1)S(1)} collective-permute-done((bf16[8,8,512]{2,1,0:T(8,128)(2,1)S(1)}, bf16[8,8,512]{2,1,0:T(8,128)(2,1)S(1)}, u32[]{:S(2)}, u32[]{:S(2)}) %collective-permute-start.19) | collective-permute-done | bytes 65568 | tf_op jit(solution)/shard_map/ppermute | solution.py:34
  49.4 1.3 %collective-permute-done.18.refs_1_ = bf16[8,8,512]{2,1,0:T(8,128)(2,1)S(1)} collective-permute-done((bf16[8,8,512]{2,1,0:T(8,128)(2,1)S(1)}, bf16[8,8,512]{2,1,0:T(8,128)(2,1)S(1)}, u32[]{:S(2)}, u32[]{:S(2)}) %collective-permute-start.18) | collective-permute-done | bytes 65568 | tf_op jit(solution)/shard_map/ppermute | solution.py:34
  50.8 0.3 zeros.3.refs_1_
  51.1 1.2 %collective-permute-done.21.refs_3_ = bf16[32,8,512]{2,1,0:T(8,128)(2,1)S(1)} collective-permute-done((bf16[32,8,512]{2,1,0:T(8,128)(2,1)S(1)}, bf16[32,8,512]{2,1,0:T(8,128)(2,1)S(1)}, u32[]{:S(2)}, u32[]{:S(2)}) %collective-permute-start.21) | collective-permute-done | bytes 262176 | tf_op jit(solution)/shard_map/ppermute | solution.py:34
  52.3 2.2 %adjoint.1 = (f32[256,8,512]{2,1,0:T(8,128)S(1)}, bf16[64,8,512]{2,1,0:T(8,128)(2,1)S(1)}, bf16[64,8,512]{2,1,0:T(8,128)(2,1)S(1)}) custom-call(s32[8,128]{1,0:T(8,128)S(4)} %get-tuple-element.33.refs_0_, f32[256,8,512]{2,1,0:T(8,128)S(1)} %zeros.3.refs_1_, bf16[32,8,512]{2,1,0:T(8,128)(2,1)S(1)} %join.9.refs_2_, ...), custom_call_target="tpu_custom_call", output_to_operand_aliasing={{0}: (1, {})} | custom-call | flops 536870912 | bytes 18354176 | tf_op jit(solution)/shard_map/adjoint/pallas_call | solution.py:49
  54.7 0.4 collective-permute-start.26
  55.1 1.4 %collective-permute-done.22.refs_1_ = bf16[64,8,512]{2,1,0:T(8,128)(2,1)S(1)} collective-permute-done((bf16[64,8,512]{2,1,0:T(8,128)(2,1)S(1)}, bf16[64,8,512]{2,1,0:T(8,128)(2,1)S(1)}, u32[]{:S(2)}, u32[]{:S(2)}) %collective-permute-start.22) | collective-permute-done | bytes 524320 | tf_op jit(solution)/shard_map/ppermute | solution.py:34
  56.6 0.4 collective-permute-start.23
  57.0 0.2 collective-permute-done.26.refs_1_
  57.3 1.1 %collective-permute-start.27 = (bf16[32,8,512]{2,1,0:T(8,128)(2,1)S(1)}, bf16[32,8,512]{2,1,0:T(8,128)(2,1)S(1)}, u32[]{:S(2)}, u32[]{:S(2)}) collective-permute-start(bf16[32,8,512]{2,1,0:T(8,128)(2,1)S(1)} %get-tuple-element.54), channel_id=1, source_target_pairs={{0,2},{1,3},{2,0},{3,1},{4,6},{5,7},{6,4},{7,5},{8,10},{9,11},{10,... | collective-permute-start | bytes 786440 | tf_op jit(solution)/shard_map/ppermute | solution.py:34
  58.4 6.6 %collective-permute-done.23.refs_1_ = bf16[32,8,512]{2,1,0:T(8,128)(2,1)S(1)} collective-permute-done((bf16[32,8,512]{2,1,0:T(8,128)(2,1)S(1)}, bf16[32,8,512]{2,1,0:T(8,128)(2,1)S(1)}, u32[]{:S(2)}, u32[]{:S(2)}) %collective-permute-start.23) | collective-permute-done | bytes 262176 | tf_op jit(solution)/shard_map/ppermute | solution.py:34
  65.1 0.3 collective-permute-start.24
  65.3 0.4 collective-permute-done.27.refs_1_
  65.8 1.2 %collective-permute-start.28 = (bf16[16,8,512]{2,1,0:T(8,128)(2,1)S(1)}, bf16[16,8,512]{2,1,0:T(8,128)(2,1)S(1)}, u32[]{:S(2)}, u32[]{:S(2)}) collective-permute-start(bf16[16,8,512]{2,1,0:T(8,128)(2,1)S(1)} %get-tuple-element.56), channel_id=1, source_target_pairs={{0,4},{1,5},{2,6},{3,7},{4,0},{5,1},{6,2},{7,3},{8,12},{9,13},{10,... | collective-permute-start | bytes 393224 | tf_op jit(solution)/shard_map/ppermute | solution.py:34
  67.0 3.1 %collective-permute-done.24.refs_1_ = bf16[16,8,512]{2,1,0:T(8,128)(2,1)S(1)} collective-permute-done((bf16[16,8,512]{2,1,0:T(8,128)(2,1)S(1)}, bf16[16,8,512]{2,1,0:T(8,128)(2,1)S(1)}, u32[]{:S(2)}, u32[]{:S(2)}) %collective-permute-start.24) | collective-permute-done | bytes 131104 | tf_op jit(solution)/shard_map/ppermute | solution.py:34
  70.1 1.9 %collective-permute-start.25 = (bf16[8,8,512]{2,1,0:T(8,128)(2,1)S(1)}, bf16[8,8,512]{2,1,0:T(8,128)(2,1)S(1)}, u32[]{:S(2)}, u32[]{:S(2)}) collective-permute-start(bf16[8,8,512]{2,1,0:T(8,128)(2,1)S(1)} %get-tuple-element.51), channel_id=1, source_target_pairs={{0,8},{1,9},{2,10},{3,11},{4,12},{5,13},{6,14},{7,15},{8,0},{9,1},... | collective-permute-start | bytes 196616 | tf_op jit(solution)/shard_map/ppermute | solution.py:34
  72.1 1.3 %collective-permute-start.29 = (bf16[8,8,512]{2,1,0:T(8,128)(2,1)S(1)}, bf16[8,8,512]{2,1,0:T(8,128)(2,1)S(1)}, u32[]{:S(2)}, u32[]{:S(2)}) collective-permute-start(bf16[8,8,512]{2,1,0:T(8,128)(2,1)S(1)} %get-tuple-element.58), channel_id=1, source_target_pairs={{0,8},{1,9},{2,10},{3,11},{4,12},{5,13},{6,14},{7,15},{8,0},{9,1},... | collective-permute-start | bytes 196616 | tf_op jit(solution)/shard_map/ppermute | solution.py:34
  73.3 2.7 %collective-permute-done.25.refs_1_ = bf16[8,8,512]{2,1,0:T(8,128)(2,1)S(1)} collective-permute-done((bf16[8,8,512]{2,1,0:T(8,128)(2,1)S(1)}, bf16[8,8,512]{2,1,0:T(8,128)(2,1)S(1)}, u32[]{:S(2)}, u32[]{:S(2)}) %collective-permute-start.25) | collective-permute-done | bytes 65568 | tf_op jit(solution)/shard_map/ppermute | solution.py:34
  76.1 1.7 %collective-permute-done.29.refs_3_ = bf16[8,8,512]{2,1,0:T(8,128)(2,1)S(1)} collective-permute-done((bf16[8,8,512]{2,1,0:T(8,128)(2,1)S(1)}, bf16[8,8,512]{2,1,0:T(8,128)(2,1)S(1)}, u32[]{:S(2)}, u32[]{:S(2)}) %collective-permute-start.29) | collective-permute-done | bytes 65568 | tf_op jit(solution)/shard_map/ppermute | solution.py:34
  77.7 0.7 final.1
  (38 shorter events, 1.7 us)
Async XLA Ops:
  1.1 7.8 %collective-permute-start.2 = (bf16[8,8,512]{2,1,0:T(8,128)(2,1)S(1)}, bf16[8,8,512]{2,1,0:T(8,128)(2,1)S(1)}, u32[]{:S(2)}, u32[]{:S(2)}) collective-permute-start(bf16[8,8,512]{2,1,0:T(8,128)(2,1)S(1)} %get-tuple-element.36.refs_0_), channel_id=1, source_target_pairs={{0,8},{1,9},{2,10},{3,11},{4,12},{5,13},{6,14},{7,15},{8,0},{9,1},... | collective-permute-start | bytes 196616 | tf_op jit(solution)/shard_map/ppermute | solution.py:34
  5.2 4.7 %collective-permute-start = (bf16[8,8,512]{2,1,0:T(8,128)(2,1)S(1)}, bf16[8,8,512]{2,1,0:T(8,128)(2,1)S(1)}, u32[]{:S(2)}, u32[]{:S(2)}) collective-permute-start(bf16[8,8,512]{2,1,0:T(8,128)(2,1)S(1)} %get-tuple-element.34.refs_0_), channel_id=1, source_target_pairs={{0,2},{1,3},{2,0},{3,1},{4,6},{5,7},{6,4},{7,5},{8,10},{9,11},{10,... | collective-permute-start | bytes 196616 | tf_op jit(solution)/shard_map/ppermute | solution.py:34
  8.8 8.5 %collective-permute-start.3 = (bf16[16,8,512]{2,1,0:T(8,128)(2,1)S(1)}, bf16[16,8,512]{2,1,0:T(8,128)(2,1)S(1)}, u32[]{:S(2)}, u32[]{:S(2)}) collective-permute-start(bf16[16,8,512]{2,1,0:T(8,128)(2,1)S(1)} %join.6.refs_2_.refs_0_), channel_id=1, source_target_pairs={{0,4},{1,5},{2,6},{3,7},{4,0},{5,1},{6,2},{7,3},{8,12},{9,13},{10,... | collective-permute-start | bytes 393224 | tf_op jit(solution)/shard_map/ppermute | solution.py:34
  9.9 9.1 %collective-permute-start.1 = (bf16[16,8,512]{2,1,0:T(8,128)(2,1)S(1)}, bf16[16,8,512]{2,1,0:T(8,128)(2,1)S(1)}, u32[]{:S(2)}, u32[]{:S(2)}) collective-permute-start(bf16[16,8,512]{2,1,0:T(8,128)(2,1)S(1)} %join.5.refs_1_.refs_0_), channel_id=1, source_target_pairs={{0,8},{1,9},{2,10},{3,11},{4,12},{5,13},{6,14},{7,15},{8,0},{9,1},... | collective-permute-start | bytes 393224 | tf_op jit(solution)/shard_map/ppermute | solution.py:34
  17.4 7.4 %collective-permute-start.5 = (bf16[32,8,512]{2,1,0:T(8,128)(2,1)S(1)}, bf16[32,8,512]{2,1,0:T(8,128)(2,1)S(1)}, u32[]{:S(2)}, u32[]{:S(2)}) collective-permute-start(bf16[32,8,512]{2,1,0:T(8,128)(2,1)S(1)} %join.8.refs_1_.refs_4_), channel_id=1, source_target_pairs={{0,2},{1,3},{2,0},{3,1},{4,6},{5,7},{6,4},{7,5},{8,10},{9,11},{10,... | collective-permute-start | bytes 786440 | tf_op jit(solution)/shard_map/ppermute | solution.py:34
  19.0 7.1 %collective-permute-start.4 = (bf16[32,8,512]{2,1,0:T(8,128)(2,1)S(1)}, bf16[32,8,512]{2,1,0:T(8,128)(2,1)S(1)}, u32[]{:S(2)}, u32[]{:S(2)}) collective-permute-start(bf16[32,8,512]{2,1,0:T(8,128)(2,1)S(1)} %join.7.refs_0_.refs_2_), channel_id=1, source_target_pairs={{0,4},{1,5},{2,6},{3,7},{4,0},{5,1},{6,2},{7,3},{8,12},{9,13},{10,... | collective-permute-start | bytes 786440 | tf_op jit(solution)/shard_map/ppermute | solution.py:34
  19.2 7.0 %collective-permute-start.8 = (bf16[32,8,512]{2,1,0:T(8,128)(2,1)S(1)}, bf16[32,8,512]{2,1,0:T(8,128)(2,1)S(1)}, u32[]{:S(2)}, u32[]{:S(2)}) collective-permute-start(bf16[32,8,512]{2,1,0:T(8,128)(2,1)S(1)} %join.8.refs_1_.refs_4_), channel_id=1, source_target_pairs={{0,1},{1,0},{2,3},{3,2},{4,5},{5,4},{6,7},{7,6},{8,9},{9,8},{10,11... | collective-permute-start | bytes 786440 | tf_op jit(solution)/shard_map/ppermute | solution.py:34
  19.2 7.0 %collective-permute-start.6 = (bf16[32,8,512]{2,1,0:T(8,128)(2,1)S(1)}, bf16[32,8,512]{2,1,0:T(8,128)(2,1)S(1)}, u32[]{:S(2)}, u32[]{:S(2)}) collective-permute-start(bf16[32,8,512]{2,1,0:T(8,128)(2,1)S(1)} %join.7.refs_0_.refs_2_), channel_id=1, source_target_pairs={{0,1},{1,0},{2,3},{3,2},{4,5},{5,4},{6,7},{7,6},{8,9},{9,8},{10,11... | collective-permute-start | bytes 786440 | tf_op jit(solution)/shard_map/ppermute | solution.py:34
  24.8 1.5 %collective-permute-start.9 = (bf16[32,8,512]{2,1,0:T(8,128)(2,1)S(1)}, bf16[32,8,512]{2,1,0:T(8,128)(2,1)S(1)}, u32[]{:S(2)}, u32[]{:S(2)}) collective-permute-start(bf16[32,8,512]{2,1,0:T(8,128)(2,1)S(1)} %collective-permute-done.5.refs_5_), channel_id=1, source_target_pairs={{0,1},{1,0},{2,3},{3,2},{4,5},{5,4},{6,7},{7,6},{8,9},{9,8},{10,11... | collective-permute-start | bytes 786440 | tf_op jit(solution)/shard_map/ppermute | solution.py:34
  26.1 1.5 %collective-permute-start.7 = (bf16[32,8,512]{2,1,0:T(8,128)(2,1)S(1)}, bf16[32,8,512]{2,1,0:T(8,128)(2,1)S(1)}, u32[]{:S(2)}, u32[]{:S(2)}) collective-permute-start(bf16[32,8,512]{2,1,0:T(8,128)(2,1)S(1)} %collective-permute-done.4.refs_3_), channel_id=1, source_target_pairs={{0,1},{1,0},{2,3},{3,2},{4,5},{5,4},{6,7},{7,6},{8,9},{9,8},{10,11... | collective-permute-start | bytes 786440 | tf_op jit(solution)/shard_map/ppermute | solution.py:34
  29.9 1.3 %collective-permute-start.11 = (bf16[8,8,512]{2,1,0:T(8,128)(2,1)S(1)}, bf16[8,8,512]{2,1,0:T(8,128)(2,1)S(1)}, u32[]{:S(2)}, u32[]{:S(2)}) collective-permute-start(bf16[8,8,512]{2,1,0:T(8,128)(2,1)S(1)} %get-tuple-element.39), channel_id=1, source_target_pairs={{0,1},{1,0},{2,3},{3,2},{4,5},{5,4},{6,7},{7,6},{8,9},{9,8},{10,11... | collective-permute-start | bytes 196616 | tf_op jit(solution)/shard_map/ppermute | solution.py:34
  30.1 2.4 %collective-permute-start.13 = (bf16[8,8,512]{2,1,0:T(8,128)(2,1)S(1)}, bf16[8,8,512]{2,1,0:T(8,128)(2,1)S(1)}, u32[]{:S(2)}, u32[]{:S(2)}) collective-permute-start(bf16[8,8,512]{2,1,0:T(8,128)(2,1)S(1)} %get-tuple-element.40), channel_id=1, source_target_pairs={{0,1},{1,0},{2,3},{3,2},{4,5},{5,4},{6,7},{7,6},{8,9},{9,8},{10,11... | collective-permute-start | bytes 196616 | tf_op jit(solution)/shard_map/ppermute | solution.py:34
  30.4 2.7 %collective-permute-start.15 = (bf16[8,8,512]{2,1,0:T(8,128)(2,1)S(1)}, bf16[8,8,512]{2,1,0:T(8,128)(2,1)S(1)}, u32[]{:S(2)}, u32[]{:S(2)}) collective-permute-start(bf16[8,8,512]{2,1,0:T(8,128)(2,1)S(1)} %get-tuple-element.41), channel_id=1, source_target_pairs={{0,1},{1,0},{2,3},{3,2},{4,5},{5,4},{6,7},{7,6},{8,9},{9,8},{10,11... | collective-permute-start | bytes 196616 | tf_op jit(solution)/shard_map/ppermute | solution.py:34
  30.6 4.4 %collective-permute-start.10 = (bf16[8,8,512]{2,1,0:T(8,128)(2,1)S(1)}, bf16[8,8,512]{2,1,0:T(8,128)(2,1)S(1)}, u32[]{:S(2)}, u32[]{:S(2)}) collective-permute-start(bf16[8,8,512]{2,1,0:T(8,128)(2,1)S(1)} %get-tuple-element.38), channel_id=1, source_target_pairs={{0,1},{1,0},{2,3},{3,2},{4,5},{5,4},{6,7},{7,6},{8,9},{9,8},{10,11... | collective-permute-start | bytes 196616 | tf_op jit(solution)/shard_map/ppermute | solution.py:34
  31.2 5.4 %collective-permute-start.12 = (bf16[8,8,512]{2,1,0:T(8,128)(2,1)S(1)}, bf16[8,8,512]{2,1,0:T(8,128)(2,1)S(1)}, u32[]{:S(2)}, u32[]{:S(2)}) collective-permute-start(bf16[8,8,512]{2,1,0:T(8,128)(2,1)S(1)} %fold.11), channel_id=1, source_target_pairs={{0,6},{1,7},{2,4},{3,5},{4,2},{5,3},{6,0},{7,1},{8,14},{9,15},{10,... | collective-permute-start | bytes 196616 | tf_op jit(solution)/shard_map/ppermute | solution.py:34
  32.5 5.2 %collective-permute-start.14 = (bf16[8,8,512]{2,1,0:T(8,128)(2,1)S(1)}, bf16[8,8,512]{2,1,0:T(8,128)(2,1)S(1)}, u32[]{:S(2)}, u32[]{:S(2)}) collective-permute-start(bf16[8,8,512]{2,1,0:T(8,128)(2,1)S(1)} %fold.12), channel_id=1, source_target_pairs={{0,2},{1,3},{2,0},{3,1},{4,6},{5,7},{6,4},{7,5},{8,10},{9,11},{10,... | collective-permute-start | bytes 196616 | tf_op jit(solution)/shard_map/ppermute | solution.py:34
  33.1 4.6 %collective-permute-start.16 = (bf16[8,8,512]{2,1,0:T(8,128)(2,1)S(1)}, bf16[8,8,512]{2,1,0:T(8,128)(2,1)S(1)}, u32[]{:S(2)}, u32[]{:S(2)}) collective-permute-start(bf16[8,8,512]{2,1,0:T(8,128)(2,1)S(1)} %fold.13), channel_id=1, source_target_pairs={{0,4},{1,5},{2,6},{3,7},{4,0},{5,1},{6,2},{7,3},{8,12},{9,13},{10,... | collective-permute-start | bytes 196616 | tf_op jit(solution)/shard_map/ppermute | solution.py:34
  37.8 5.3 %collective-permute-start.17 = (bf16[8,8,512]{2,1,0:T(8,128)(2,1)S(1)}, bf16[8,8,512]{2,1,0:T(8,128)(2,1)S(1)}, u32[]{:S(2)}, u32[]{:S(2)}) collective-permute-start(bf16[8,8,512]{2,1,0:T(8,128)(2,1)S(1)} %get-tuple-element.43), channel_id=1, source_target_pairs={{0,8},{1,9},{2,10},{3,11},{4,12},{5,13},{6,14},{7,15},{8,0},{9,1},... | collective-permute-start | bytes 196616 | tf_op jit(solution)/shard_map/ppermute | solution.py:34
  43.1 5.2 %collective-permute-start.20 = (bf16[8,8,512]{2,1,0:T(8,128)(2,1)S(1)}, bf16[8,8,512]{2,1,0:T(8,128)(2,1)S(1)}, u32[]{:S(2)}, u32[]{:S(2)}) collective-permute-start(bf16[8,8,512]{2,1,0:T(8,128)(2,1)S(1)} %weigh.1.refs_0_), channel_id=1, source_target_pairs={{0,6},{1,7},{2,4},{3,5},{4,2},{5,3},{6,0},{7,1},{8,14},{9,15},{10,... | collective-permute-start | bytes 196616 | tf_op jit(solution)/shard_map/ppermute | solution.py:34
  44.8 4.6 %collective-permute-start.19 = (bf16[8,8,512]{2,1,0:T(8,128)(2,1)S(1)}, bf16[8,8,512]{2,1,0:T(8,128)(2,1)S(1)}, u32[]{:S(2)}, u32[]{:S(2)}) collective-permute-start(bf16[8,8,512]{2,1,0:T(8,128)(2,1)S(1)} %weigh.1.refs_0_), channel_id=1, source_target_pairs={{0,4},{1,5},{2,6},{3,7},{4,0},{5,1},{6,2},{7,3},{8,12},{9,13},{10,... | collective-permute-start | bytes 196616 | tf_op jit(solution)/shard_map/ppermute | solution.py:34
  46.4 4.3 %collective-permute-start.18 = (bf16[8,8,512]{2,1,0:T(8,128)(2,1)S(1)}, bf16[8,8,512]{2,1,0:T(8,128)(2,1)S(1)}, u32[]{:S(2)}, u32[]{:S(2)}) collective-permute-start(bf16[8,8,512]{2,1,0:T(8,128)(2,1)S(1)} %weigh.1.refs_0_), channel_id=1, source_target_pairs={{0,2},{1,3},{2,0},{3,1},{4,6},{5,7},{6,4},{7,5},{8,10},{9,11},{10,... | collective-permute-start | bytes 196616 | tf_op jit(solution)/shard_map/ppermute | solution.py:34
  50.7 1.6 %collective-permute-start.21 = (bf16[32,8,512]{2,1,0:T(8,128)(2,1)S(1)}, bf16[32,8,512]{2,1,0:T(8,128)(2,1)S(1)}, u32[]{:S(2)}, u32[]{:S(2)}) collective-permute-start(bf16[32,8,512]{2,1,0:T(8,128)(2,1)S(1)} %join.9.refs_2_), channel_id=1, source_target_pairs={{0,1},{1,0},{2,3},{3,2},{4,5},{5,4},{6,7},{7,6},{8,9},{9,8},{10,11... | collective-permute-start | bytes 786440 | tf_op jit(solution)/shard_map/ppermute | solution.py:34
  54.5 2.0 %collective-permute-start.22 = (bf16[64,8,512]{2,1,0:T(8,128)(2,1)S(1)}, bf16[64,8,512]{2,1,0:T(8,128)(2,1)S(1)}, u32[]{:S(2)}, u32[]{:S(2)}) collective-permute-start(bf16[64,8,512]{2,1,0:T(8,128)(2,1)S(1)} %get-tuple-element.45), channel_id=1, source_target_pairs={{0,1},{1,0},{2,3},{3,2},{4,5},{5,4},{6,7},{7,6},{8,9},{9,8},{10,11... | collective-permute-start | bytes 1572872 | tf_op jit(solution)/shard_map/ppermute | solution.py:34
  54.7 2.5 %collective-permute-start.26 = (bf16[64,8,512]{2,1,0:T(8,128)(2,1)S(1)}, bf16[64,8,512]{2,1,0:T(8,128)(2,1)S(1)}, u32[]{:S(2)}, u32[]{:S(2)}) collective-permute-start(bf16[64,8,512]{2,1,0:T(8,128)(2,1)S(1)} %get-tuple-element.52), channel_id=1, source_target_pairs={{0,1},{1,0},{2,3},{3,2},{4,5},{5,4},{6,7},{7,6},{8,9},{9,8},{10,11... | collective-permute-start | bytes 1572872 | tf_op jit(solution)/shard_map/ppermute | solution.py:34
  56.6 8.4 %collective-permute-start.23 = (bf16[32,8,512]{2,1,0:T(8,128)(2,1)S(1)}, bf16[32,8,512]{2,1,0:T(8,128)(2,1)S(1)}, u32[]{:S(2)}, u32[]{:S(2)}) collective-permute-start(bf16[32,8,512]{2,1,0:T(8,128)(2,1)S(1)} %get-tuple-element.47), channel_id=1, source_target_pairs={{0,4},{1,5},{2,6},{3,7},{4,0},{5,1},{6,2},{7,3},{8,12},{9,13},{10,... | collective-permute-start | bytes 786440 | tf_op jit(solution)/shard_map/ppermute | solution.py:34
  57.3 8.4 %collective-permute-start.27 = (bf16[32,8,512]{2,1,0:T(8,128)(2,1)S(1)}, bf16[32,8,512]{2,1,0:T(8,128)(2,1)S(1)}, u32[]{:S(2)}, u32[]{:S(2)}) collective-permute-start(bf16[32,8,512]{2,1,0:T(8,128)(2,1)S(1)} %get-tuple-element.54), channel_id=1, source_target_pairs={{0,2},{1,3},{2,0},{3,1},{4,6},{5,7},{6,4},{7,5},{8,10},{9,11},{10,... | collective-permute-start | bytes 786440 | tf_op jit(solution)/shard_map/ppermute | solution.py:34
  65.1 5.0 %collective-permute-start.24 = (bf16[16,8,512]{2,1,0:T(8,128)(2,1)S(1)}, bf16[16,8,512]{2,1,0:T(8,128)(2,1)S(1)}, u32[]{:S(2)}, u32[]{:S(2)}) collective-permute-start(bf16[16,8,512]{2,1,0:T(8,128)(2,1)S(1)} %get-tuple-element.49), channel_id=1, source_target_pairs={{0,2},{1,3},{2,0},{3,1},{4,6},{5,7},{6,4},{7,5},{8,10},{9,11},{10,... | collective-permute-start | bytes 393224 | tf_op jit(solution)/shard_map/ppermute | solution.py:34
  65.8 6.2 %collective-permute-start.28 = (bf16[16,8,512]{2,1,0:T(8,128)(2,1)S(1)}, bf16[16,8,512]{2,1,0:T(8,128)(2,1)S(1)}, u32[]{:S(2)}, u32[]{:S(2)}) collective-permute-start(bf16[16,8,512]{2,1,0:T(8,128)(2,1)S(1)} %get-tuple-element.56), channel_id=1, source_target_pairs={{0,4},{1,5},{2,6},{3,7},{4,0},{5,1},{6,2},{7,3},{8,12},{9,13},{10,... | collective-permute-start | bytes 393224 | tf_op jit(solution)/shard_map/ppermute | solution.py:34
  70.1 5.9 %collective-permute-start.25 = (bf16[8,8,512]{2,1,0:T(8,128)(2,1)S(1)}, bf16[8,8,512]{2,1,0:T(8,128)(2,1)S(1)}, u32[]{:S(2)}, u32[]{:S(2)}) collective-permute-start(bf16[8,8,512]{2,1,0:T(8,128)(2,1)S(1)} %get-tuple-element.51), channel_id=1, source_target_pairs={{0,8},{1,9},{2,10},{3,11},{4,12},{5,13},{6,14},{7,15},{8,0},{9,1},... | collective-permute-start | bytes 196616 | tf_op jit(solution)/shard_map/ppermute | solution.py:34
  72.1 5.7 %collective-permute-start.29 = (bf16[8,8,512]{2,1,0:T(8,128)(2,1)S(1)}, bf16[8,8,512]{2,1,0:T(8,128)(2,1)S(1)}, u32[]{:S(2)}, u32[]{:S(2)}) collective-permute-start(bf16[8,8,512]{2,1,0:T(8,128)(2,1)S(1)} %get-tuple-element.58), channel_id=1, source_target_pairs={{0,8},{1,9},{2,10},{3,11},{4,12},{5,13},{6,14},{7,15},{8,0},{9,1},... | collective-permute-start | bytes 196616 | tf_op jit(solution)/shard_map/ppermute | solution.py:34

commit v18 on v15

--- a/solution.py
+++ b/solution.py
@@ -12,7 +12,7 @@
 I32 = jnp.int32
 GROUP = 8
 SKEW = 3
-SQUARE = (6, 2, 4)
+SQUARE = (6, 4, 2)
 LANES = 128
 MIB = 1024 * 1024
 

time: 78.9 us -> 78.1 us (0.990)
  transfers between devices with their start and end apart: 30 -> 30, of which waited for: 20 -> 19; matrix products, arithmetic and copies ran while one was open for 0% -> 0% of each run, Pallas kernels for 9% -> 9%
where the time goes in v18:
time: 78.1 us; the launch traced here: 77.8 us
  waiting for transfers between devices  35.8 us (46%)
  starting transfers between devices  28.9 us (37%)
  Pallas kernels  12.9 us (17%)
    ppermute x30, waiting for transfers between devices, swap(): return lax.ppermute(array, 'tile', [(i, i ^ bits) for i in range(count)])  35.8 us
    ppermute x30, starting transfers between devices, swap(): return lax.ppermute(array, 'tile', [(i, i ^ bits) for i in range(count)])  28.9 us
    pallas_call x26, Pallas kernels, local(): pl.pallas_call(run, out_shape=[a if s.memory_space is None else s.memory_...  12.9 us
  transfers between devices with their start and end apart: 30, of which 19 were waited for; matrix products, arithmetic and copies ran while one was open for 0% of the time, Pallas kernels for 9%

profile of v18, /device:TPU:0, one launch (start us, length us, event | category | flops | bytes accessed | tf_op | source)
XLA Modules:
  0.0 77.8 jit_solution(3116046790572017031)
XLA Ops:
  0.0 1.1 %scale.1 = (bf16[8,8,512]{2,1,0:T(8,128)(2,1)S(1)}, bf16[8,8,512]{2,1,0:T(8,128)(2,1)S(1)}, f32[64,128]{1,0:T(8,128)S(1)}) custom-call(f32[4]{0:T(128)} %refs_0_.3, f32[64,128]{1,0:T(8,128)} %bitcast.9, s32[64,128]{1,0:T(8,128)} %bitcast.10, f32[8,8192]{1,0:T(8,128)} %refs_3_.1), custom_call_target="tpu_custom_call" | custom-call | bytes 491536 | tf_op jit(solution)/shard_map/scale/pallas_call | solution.py:49
  1.1 4.1 %collective-permute-start.2 = (bf16[8,8,512]{2,1,0:T(8,128)(2,1)S(1)}, bf16[8,8,512]{2,1,0:T(8,128)(2,1)S(1)}, u32[]{:S(2)}, u32[]{:S(2)}) collective-permute-start(bf16[8,8,512]{2,1,0:T(8,128)(2,1)S(1)} %get-tuple-element.36.refs_0_), channel_id=1, source_target_pairs={{0,8},{1,9},{2,10},{3,11},{4,12},{5,13},{6,14},{7,15},{8,0},{9,1},... | collective-permute-start | bytes 196616 | tf_op jit(solution)/shard_map/ppermute | solution.py:34
  5.2 1.5 %collective-permute-start = (bf16[8,8,512]{2,1,0:T(8,128)(2,1)S(1)}, bf16[8,8,512]{2,1,0:T(8,128)(2,1)S(1)}, u32[]{:S(2)}, u32[]{:S(2)}) collective-permute-start(bf16[8,8,512]{2,1,0:T(8,128)(2,1)S(1)} %get-tuple-element.34.refs_0_), channel_id=1, source_target_pairs={{0,2},{1,3},{2,0},{3,1},{4,6},{5,7},{6,4},{7,5},{8,10},{9,11},{10,... | collective-permute-start | bytes 196616 | tf_op jit(solution)/shard_map/ppermute | solution.py:34
  6.7 1.5 %plan.1 = (s32[8,128]{1,0:T(8,128)S(4)}, f32[32,128]{1,0:T(8,128)S(1)}) custom-call(s32[16,128]{1,0:T(8,128)} %bitcast.11, s32[16,128]{1,0:T(8,128)} %bitcast.12, s32[16,128]{1,0:T(8,128)} %bitcast.13, s32[16,128]{1,0:T(8,128)} %bitcast.14, s32[16,128]{1,0:T(8,128)} %bitcast.15, f32[256,128]{1,0:T(8,128)} %bitcast.8, ...), custom_call_target="tpu_custom_call" | custom-call | bytes 192512 | tf_op jit(solution)/shard_map/plan/pallas_call | solution.py:49
  8.2 0.6 collective-permute-done.2.refs_1_
  8.8 1.0 %collective-permute-start.3 = (bf16[16,8,512]{2,1,0:T(8,128)(2,1)S(1)}, bf16[16,8,512]{2,1,0:T(8,128)(2,1)S(1)}, u32[]{:S(2)}, u32[]{:S(2)}) collective-permute-start(bf16[16,8,512]{2,1,0:T(8,128)(2,1)S(1)} %join.6.refs_2_.refs_0_), channel_id=1, source_target_pairs={{0,4},{1,5},{2,6},{3,7},{4,0},{5,1},{6,2},{7,3},{8,12},{9,13},{10,... | collective-permute-start | bytes 393224 | tf_op jit(solution)/shard_map/ppermute | solution.py:34
  9.9 3.1 %collective-permute-start.1 = (bf16[16,8,512]{2,1,0:T(8,128)(2,1)S(1)}, bf16[16,8,512]{2,1,0:T(8,128)(2,1)S(1)}, u32[]{:S(2)}, u32[]{:S(2)}) collective-permute-start(bf16[16,8,512]{2,1,0:T(8,128)(2,1)S(1)} %join.5.refs_1_.refs_0_), channel_id=1, source_target_pairs={{0,8},{1,9},{2,10},{3,11},{4,12},{5,13},{6,14},{7,15},{8,0},{9,1},... | collective-permute-start | bytes 393224 | tf_op jit(solution)/shard_map/ppermute | solution.py:34
  12.9 2.2 %load_v.1.refs_3_.refs_10_.refs_5_ = bf16[128,32,512]{2,1,0:T(8,128)(2,1)S(1)} custom-call(bf16[128,32,512]{2,1,0:T(8,128)(2,1)} %refs_0_.4, bf16[16,8,512]{2,1,0:T(8,128)(2,1)S(1)} %join.5.refs_1_.refs_0_, bf16[16,8,512]{2,1,0:T(8,128)(2,1)S(1)} %join.6.refs_2_.refs_0_), custom_call_target="tpu_custom_call" | custom-call | bytes 8388608 | tf_op jit(solution)/shard_map/load_v/pallas_call | solution.py:49
  15.2 2.2 %load_u.1.refs_2_.refs_11_.refs_4_ = bf16[128,32,512]{2,1,0:T(8,128)(2,1)S(1)} custom-call(bf16[128,32,512]{2,1,0:T(8,128)(2,1)} %refs_0_.5, bf16[16,8,512]{2,1,0:T(8,128)(2,1)S(1)} %join.5.refs_1_.refs_0_, bf16[16,8,512]{2,1,0:T(8,128)(2,1)S(1)} %join.6.refs_2_.refs_0_, bf16[128,32,512]{2,1,0:T(8,128)(2,1)S(1)} %load_v.1.refs_3_.refs_10_.refs_5_), custom_call_target="tpu_custom_call" | custom-call | bytes 8388608 | tf_op jit(solution)/shard_map/load_u/pallas_call | solution.py:49
  17.4 1.6 %collective-permute-start.5 = (bf16[32,8,512]{2,1,0:T(8,128)(2,1)S(1)}, bf16[32,8,512]{2,1,0:T(8,128)(2,1)S(1)}, u32[]{:S(2)}, u32[]{:S(2)}) collective-permute-start(bf16[32,8,512]{2,1,0:T(8,128)(2,1)S(1)} %join.8.refs_1_.refs_4_), channel_id=1, source_target_pairs={{0,2},{1,3},{2,0},{3,1},{4,6},{5,7},{6,4},{7,5},{8,10},{9,11},{10,... | collective-permute-start | bytes 786440 | tf_op jit(solution)/shard_map/ppermute | solution.py:34
  19.2 0.5 collective-permute-start.6
  19.7 5.1 %collective-permute-done.5.refs_5_ = bf16[32,8,512]{2,1,0:T(8,128)(2,1)S(1)} collective-permute-done((bf16[32,8,512]{2,1,0:T(8,128)(2,1)S(1)}, bf16[32,8,512]{2,1,0:T(8,128)(2,1)S(1)}, u32[]{:S(2)}, u32[]{:S(2)}) %collective-permute-start.5) | collective-permute-done | bytes 262176 | tf_op jit(solution)/shard_map/ppermute | solution.py:34
  24.8 1.3 %collective-permute-done.4.refs_3_ = bf16[32,8,512]{2,1,0:T(8,128)(2,1)S(1)} collective-permute-done((bf16[32,8,512]{2,1,0:T(8,128)(2,1)S(1)}, bf16[32,8,512]{2,1,0:T(8,128)(2,1)S(1)}, u32[]{:S(2)}, u32[]{:S(2)}) %collective-permute-start.4) | collective-permute-done | bytes 262176 | tf_op jit(solution)/shard_map/ppermute | solution.py:34
  26.3 1.3 %collective-permute-done.7.refs_7_ = bf16[32,8,512]{2,1,0:T(8,128)(2,1)S(1)} collective-permute-done((bf16[32,8,512]{2,1,0:T(8,128)(2,1)S(1)}, bf16[32,8,512]{2,1,0:T(8,128)(2,1)S(1)}, u32[]{:S(2)}, u32[]{:S(2)}) %collective-permute-start.7) | collective-permute-done | bytes 262176 | tf_op jit(solution)/shard_map/ppermute | solution.py:34
  27.7 2.2 %forward.1 = (f32[64,8,512]{2,1,0:T(8,128)S(1)}, f32[8,8,512]{2,1,0:T(8,128)S(1)}, f32[8,8,512]{2,1,0:T(8,128)S(1)}, f32[8,8,512]{2,1,0:T(8,128)S(1)}, f32[8,8,512]{2,1,0:T(8,128)S(1)}) custom-call(s32[8,128]{1,0:T(8,128)S(4)} %get-tuple-element.33.refs_0_, f32[64,8,512]{2,1,0:T(8,128)S(1)} %zeros.2.refs_1_, ...), custom_call_target="tpu_custom_call", output_to_operand_aliasing={{0}: (1, {})} | custom-call | flops 536870912 | bytes 13111296 | tf_op jit(solution)/shard_map/forward/pallas_call | solution.py:49
  30.1 0.4 collective-permute-start.13
  30.6 0.4 collective-permute-start.10
  31.0 0.3 collective-permute-done.11.refs_1_
  31.3 1.3 %collective-permute-start.12 = (bf16[8,8,512]{2,1,0:T(8,128)(2,1)S(1)}, bf16[8,8,512]{2,1,0:T(8,128)(2,1)S(1)}, u32[]{:S(2)}, u32[]{:S(2)}) collective-permute-start(bf16[8,8,512]{2,1,0:T(8,128)(2,1)S(1)} %fold.11), channel_id=1, source_target_pairs={{0,6},{1,7},{2,4},{3,5},{4,2},{5,3},{6,0},{7,1},{8,14},{9,15},{10,... | collective-permute-start | bytes 196616 | tf_op jit(solution)/shard_map/ppermute | solution.py:34
  32.6 1.0 %collective-permute-start.14 = (bf16[8,8,512]{2,1,0:T(8,128)(2,1)S(1)}, bf16[8,8,512]{2,1,0:T(8,128)(2,1)S(1)}, u32[]{:S(2)}, u32[]{:S(2)}) collective-permute-start(bf16[8,8,512]{2,1,0:T(8,128)(2,1)S(1)} %fold.12), channel_id=1, source_target_pairs={{0,4},{1,5},{2,6},{3,7},{4,0},{5,1},{6,2},{7,3},{8,12},{9,13},{10,... | collective-permute-start | bytes 196616 | tf_op jit(solution)/shard_map/ppermute | solution.py:34
  33.6 1.4 %collective-permute-start.16 = (bf16[8,8,512]{2,1,0:T(8,128)(2,1)S(1)}, bf16[8,8,512]{2,1,0:T(8,128)(2,1)S(1)}, u32[]{:S(2)}, u32[]{:S(2)}) collective-permute-start(bf16[8,8,512]{2,1,0:T(8,128)(2,1)S(1)} %fold.13), channel_id=1, source_target_pairs={{0,2},{1,3},{2,0},{3,1},{4,6},{5,7},{6,4},{7,5},{8,10},{9,11},{10,... | collective-permute-start | bytes 196616 | tf_op jit(solution)/shard_map/ppermute | solution.py:34
  35.1 2.2 %collective-permute-done.12.refs_1_ = bf16[8,8,512]{2,1,0:T(8,128)(2,1)S(1)} collective-permute-done((bf16[8,8,512]{2,1,0:T(8,128)(2,1)S(1)}, bf16[8,8,512]{2,1,0:T(8,128)(2,1)S(1)}, u32[]{:S(2)}, u32[]{:S(2)}) %collective-permute-start.12) | collective-permute-done | bytes 65568 | tf_op jit(solution)/shard_map/ppermute | solution.py:34
  37.2 0.7 collective-permute-done.16.refs_3_
  38.0 2.0 %collective-permute-start.17 = (bf16[8,8,512]{2,1,0:T(8,128)(2,1)S(1)}, bf16[8,8,512]{2,1,0:T(8,128)(2,1)S(1)}, u32[]{:S(2)}, u32[]{:S(2)}) collective-permute-start(bf16[8,8,512]{2,1,0:T(8,128)(2,1)S(1)} %get-tuple-element.43), channel_id=1, source_target_pairs={{0,8},{1,9},{2,10},{3,11},{4,12},{5,13},{6,14},{7,15},{8,0},{9,1},... | collective-permute-start | bytes 196616 | tf_op jit(solution)/shard_map/ppermute | solution.py:34
  40.0 4.0 %collective-permute-done.17.refs_1_ = bf16[8,8,512]{2,1,0:T(8,128)(2,1)S(1)} collective-permute-done((bf16[8,8,512]{2,1,0:T(8,128)(2,1)S(1)}, bf16[8,8,512]{2,1,0:T(8,128)(2,1)S(1)}, u32[]{:S(2)}, u32[]{:S(2)}) %collective-permute-start.17) | collective-permute-done | bytes 65568 | tf_op jit(solution)/shard_map/ppermute | solution.py:34
  43.9 0.5 collective-permute-start.20
  44.5 2.1 %collective-permute-start.19 = (bf16[8,8,512]{2,1,0:T(8,128)(2,1)S(1)}, bf16[8,8,512]{2,1,0:T(8,128)(2,1)S(1)}, u32[]{:S(2)}, u32[]{:S(2)}) collective-permute-start(bf16[8,8,512]{2,1,0:T(8,128)(2,1)S(1)} %weigh.1.refs_0_), channel_id=1, source_target_pairs={{0,4},{1,5},{2,6},{3,7},{4,0},{5,1},{6,2},{7,3},{8,12},{9,13},{10,... | collective-permute-start | bytes 196616 | tf_op jit(solution)/shard_map/ppermute | solution.py:34
  46.6 0.9 %collective-permute-start.18 = (bf16[8,8,512]{2,1,0:T(8,128)(2,1)S(1)}, bf16[8,8,512]{2,1,0:T(8,128)(2,1)S(1)}, u32[]{:S(2)}, u32[]{:S(2)}) collective-permute-start(bf16[8,8,512]{2,1,0:T(8,128)(2,1)S(1)} %weigh.1.refs_0_), channel_id=1, source_target_pairs={{0,2},{1,3},{2,0},{3,1},{4,6},{5,7},{6,4},{7,5},{8,10},{9,11},{10,... | collective-permute-start | bytes 196616 | tf_op jit(solution)/shard_map/ppermute | solution.py:34
  47.5 1.7 %collective-permute-done.20.refs_3_ = bf16[8,8,512]{2,1,0:T(8,128)(2,1)S(1)} collective-permute-done((bf16[8,8,512]{2,1,0:T(8,128)(2,1)S(1)}, bf16[8,8,512]{2,1,0:T(8,128)(2,1)S(1)}, u32[]{:S(2)}, u32[]{:S(2)}) %collective-permute-start.20) | collective-permute-done | bytes 65568 | tf_op jit(solution)/shard_map/ppermute | solution.py:34
  49.2 0.4 collective-permute-done.19.refs_2_
  49.5 1.3 %collective-permute-done.18.refs_1_ = bf16[8,8,512]{2,1,0:T(8,128)(2,1)S(1)} collective-permute-done((bf16[8,8,512]{2,1,0:T(8,128)(2,1)S(1)}, bf16[8,8,512]{2,1,0:T(8,128)(2,1)S(1)}, u32[]{:S(2)}, u32[]{:S(2)}) %collective-permute-start.18) | collective-permute-done | bytes 65568 | tf_op jit(solution)/shard_map/ppermute | solution.py:34
  51.0 0.3 zeros.3.refs_1_
  51.2 1.2 %collective-permute-done.21.refs_3_ = bf16[32,8,512]{2,1,0:T(8,128)(2,1)S(1)} collective-permute-done((bf16[32,8,512]{2,1,0:T(8,128)(2,1)S(1)}, bf16[32,8,512]{2,1,0:T(8,128)(2,1)S(1)}, u32[]{:S(2)}, u32[]{:S(2)}) %collective-permute-start.21) | collective-permute-done | bytes 262176 | tf_op jit(solution)/shard_map/ppermute | solution.py:34
  52.5 2.2 %adjoint.1 = (f32[256,8,512]{2,1,0:T(8,128)S(1)}, bf16[64,8,512]{2,1,0:T(8,128)(2,1)S(1)}, bf16[64,8,512]{2,1,0:T(8,128)(2,1)S(1)}) custom-call(s32[8,128]{1,0:T(8,128)S(4)} %get-tuple-element.33.refs_0_, f32[256,8,512]{2,1,0:T(8,128)S(1)} %zeros.3.refs_1_, bf16[32,8,512]{2,1,0:T(8,128)(2,1)S(1)} %join.9.refs_2_, ...), custom_call_target="tpu_custom_call", output_to_operand_aliasing={{0}: (1, {})} | custom-call | flops 536870912 | bytes 18354176 | tf_op jit(solution)/shard_map/adjoint/pallas_call | solution.py:49
  54.7 0.2 collective-permute-start.22
  54.9 0.4 collective-permute-start.26
  55.2 1.4 %collective-permute-done.22.refs_1_ = bf16[64,8,512]{2,1,0:T(8,128)(2,1)S(1)} collective-permute-done((bf16[64,8,512]{2,1,0:T(8,128)(2,1)S(1)}, bf16[64,8,512]{2,1,0:T(8,128)(2,1)S(1)}, u32[]{:S(2)}, u32[]{:S(2)}) %collective-permute-start.22) | collective-permute-done | bytes 524320 | tf_op jit(solution)/shard_map/ppermute | solution.py:34
  56.8 0.6 collective-permute-done.26.refs_1_
  57.5 1.0 %collective-permute-start.27 = (bf16[32,8,512]{2,1,0:T(8,128)(2,1)S(1)}, bf16[32,8,512]{2,1,0:T(8,128)(2,1)S(1)}, u32[]{:S(2)}, u32[]{:S(2)}) collective-permute-start(bf16[32,8,512]{2,1,0:T(8,128)(2,1)S(1)} %get-tuple-element.54), channel_id=1, source_target_pairs={{0,2},{1,3},{2,0},{3,1},{4,6},{5,7},{6,4},{7,5},{8,10},{9,11},{10,... | collective-permute-start | bytes 786440 | tf_op jit(solution)/shard_map/ppermute | solution.py:34
  58.5 6.7 %collective-permute-done.23.refs_1_ = bf16[32,8,512]{2,1,0:T(8,128)(2,1)S(1)} collective-permute-done((bf16[32,8,512]{2,1,0:T(8,128)(2,1)S(1)}, bf16[32,8,512]{2,1,0:T(8,128)(2,1)S(1)}, u32[]{:S(2)}, u32[]{:S(2)}) %collective-permute-start.23) | collective-permute-done | bytes 262176 | tf_op jit(solution)/shard_map/ppermute | solution.py:34
  65.2 1.0 %collective-permute-start.24 = (bf16[16,8,512]{2,1,0:T(8,128)(2,1)S(1)}, bf16[16,8,512]{2,1,0:T(8,128)(2,1)S(1)}, u32[]{:S(2)}, u32[]{:S(2)}) collective-permute-start(bf16[16,8,512]{2,1,0:T(8,128)(2,1)S(1)} %get-tuple-element.49), channel_id=1, source_target_pairs={{0,2},{1,3},{2,0},{3,1},{4,6},{5,7},{6,4},{7,5},{8,10},{9,11},{10,... | collective-permute-start | bytes 393224 | tf_op jit(solution)/shard_map/ppermute | solution.py:34
  66.2 0.9 %collective-permute-start.28 = (bf16[16,8,512]{2,1,0:T(8,128)(2,1)S(1)}, bf16[16,8,512]{2,1,0:T(8,128)(2,1)S(1)}, u32[]{:S(2)}, u32[]{:S(2)}) collective-permute-start(bf16[16,8,512]{2,1,0:T(8,128)(2,1)S(1)} %get-tuple-element.56), channel_id=1, source_target_pairs={{0,4},{1,5},{2,6},{3,7},{4,0},{5,1},{6,2},{7,3},{8,12},{9,13},{10,... | collective-permute-start | bytes 393224 | tf_op jit(solution)/shard_map/ppermute | solution.py:34
  67.2 3.1 %collective-permute-done.24.refs_1_ = bf16[16,8,512]{2,1,0:T(8,128)(2,1)S(1)} collective-permute-done((bf16[16,8,512]{2,1,0:T(8,128)(2,1)S(1)}, bf16[16,8,512]{2,1,0:T(8,128)(2,1)S(1)}, u32[]{:S(2)}, u32[]{:S(2)}) %collective-permute-start.24) | collective-permute-done | bytes 131104 | tf_op jit(solution)/shard_map/ppermute | solution.py:34
  70.3 1.3 %collective-permute-start.25 = (bf16[8,8,512]{2,1,0:T(8,128)(2,1)S(1)}, bf16[8,8,512]{2,1,0:T(8,128)(2,1)S(1)}, u32[]{:S(2)}, u32[]{:S(2)}) collective-permute-start(bf16[8,8,512]{2,1,0:T(8,128)(2,1)S(1)} %get-tuple-element.51), channel_id=1, source_target_pairs={{0,8},{1,9},{2,10},{3,11},{4,12},{5,13},{6,14},{7,15},{8,0},{9,1},... | collective-permute-start | bytes 196616 | tf_op jit(solution)/shard_map/ppermute | solution.py:34
  71.6 1.8 %collective-permute-start.29 = (bf16[8,8,512]{2,1,0:T(8,128)(2,1)S(1)}, bf16[8,8,512]{2,1,0:T(8,128)(2,1)S(1)}, u32[]{:S(2)}, u32[]{:S(2)}) collective-permute-start(bf16[8,8,512]{2,1,0:T(8,128)(2,1)S(1)} %get-tuple-element.58), channel_id=1, source_target_pairs={{0,8},{1,9},{2,10},{3,11},{4,12},{5,13},{6,14},{7,15},{8,0},{9,1},... | collective-permute-start | bytes 196616 | tf_op jit(solution)/shard_map/ppermute | solution.py:34
  73.3 3.1 %collective-permute-done.25.refs_1_ = bf16[8,8,512]{2,1,0:T(8,128)(2,1)S(1)} collective-permute-done((bf16[8,8,512]{2,1,0:T(8,128)(2,1)S(1)}, bf16[8,8,512]{2,1,0:T(8,128)(2,1)S(1)}, u32[]{:S(2)}, u32[]{:S(2)}) %collective-permute-start.25) | collective-permute-done | bytes 65568 | tf_op jit(solution)/shard_map/ppermute | solution.py:34
  76.4 0.7 collective-permute-done.29.refs_3_
  77.1 0.7 final.1
  (38 shorter events, 1.3 us)
Async XLA Ops:
  1.1 7.8 %collective-permute-start.2 = (bf16[8,8,512]{2,1,0:T(8,128)(2,1)S(1)}, bf16[8,8,512]{2,1,0:T(8,128)(2,1)S(1)}, u32[]{:S(2)}, u32[]{:S(2)}) collective-permute-start(bf16[8,8,512]{2,1,0:T(8,128)(2,1)S(1)} %get-tuple-element.36.refs_0_), channel_id=1, source_target_pairs={{0,8},{1,9},{2,10},{3,11},{4,12},{5,13},{6,14},{7,15},{8,0},{9,1},... | collective-permute-start | bytes 196616 | tf_op jit(solution)/shard_map/ppermute | solution.py:34
  5.2 4.7 %collective-permute-start = (bf16[8,8,512]{2,1,0:T(8,128)(2,1)S(1)}, bf16[8,8,512]{2,1,0:T(8,128)(2,1)S(1)}, u32[]{:S(2)}, u32[]{:S(2)}) collective-permute-start(bf16[8,8,512]{2,1,0:T(8,128)(2,1)S(1)} %get-tuple-element.34.refs_0_), channel_id=1, source_target_pairs={{0,2},{1,3},{2,0},{3,1},{4,6},{5,7},{6,4},{7,5},{8,10},{9,11},{10,... | collective-permute-start | bytes 196616 | tf_op jit(solution)/shard_map/ppermute | solution.py:34
  8.8 8.5 %collective-permute-start.3 = (bf16[16,8,512]{2,1,0:T(8,128)(2,1)S(1)}, bf16[16,8,512]{2,1,0:T(8,128)(2,1)S(1)}, u32[]{:S(2)}, u32[]{:S(2)}) collective-permute-start(bf16[16,8,512]{2,1,0:T(8,128)(2,1)S(1)} %join.6.refs_2_.refs_0_), channel_id=1, source_target_pairs={{0,4},{1,5},{2,6},{3,7},{4,0},{5,1},{6,2},{7,3},{8,12},{9,13},{10,... | collective-permute-start | bytes 393224 | tf_op jit(solution)/shard_map/ppermute | solution.py:34
  9.9 9.1 %collective-permute-start.1 = (bf16[16,8,512]{2,1,0:T(8,128)(2,1)S(1)}, bf16[16,8,512]{2,1,0:T(8,128)(2,1)S(1)}, u32[]{:S(2)}, u32[]{:S(2)}) collective-permute-start(bf16[16,8,512]{2,1,0:T(8,128)(2,1)S(1)} %join.5.refs_1_.refs_0_), channel_id=1, source_target_pairs={{0,8},{1,9},{2,10},{3,11},{4,12},{5,13},{6,14},{7,15},{8,0},{9,1},... | collective-permute-start | bytes 393224 | tf_op jit(solution)/shard_map/ppermute | solution.py:34
  17.4 7.4 %collective-permute-start.5 = (bf16[32,8,512]{2,1,0:T(8,128)(2,1)S(1)}, bf16[32,8,512]{2,1,0:T(8,128)(2,1)S(1)}, u32[]{:S(2)}, u32[]{:S(2)}) collective-permute-start(bf16[32,8,512]{2,1,0:T(8,128)(2,1)S(1)} %join.8.refs_1_.refs_4_), channel_id=1, source_target_pairs={{0,2},{1,3},{2,0},{3,1},{4,6},{5,7},{6,4},{7,5},{8,10},{9,11},{10,... | collective-permute-start | bytes 786440 | tf_op jit(solution)/shard_map/ppermute | solution.py:34
  19.0 7.1 %collective-permute-start.4 = (bf16[32,8,512]{2,1,0:T(8,128)(2,1)S(1)}, bf16[32,8,512]{2,1,0:T(8,128)(2,1)S(1)}, u32[]{:S(2)}, u32[]{:S(2)}) collective-permute-start(bf16[32,8,512]{2,1,0:T(8,128)(2,1)S(1)} %join.7.refs_0_.refs_2_), channel_id=1, source_target_pairs={{0,4},{1,5},{2,6},{3,7},{4,0},{5,1},{6,2},{7,3},{8,12},{9,13},{10,... | collective-permute-start | bytes 786440 | tf_op jit(solution)/shard_map/ppermute | solution.py:34
  19.2 7.0 %collective-permute-start.8 = (bf16[32,8,512]{2,1,0:T(8,128)(2,1)S(1)}, bf16[32,8,512]{2,1,0:T(8,128)(2,1)S(1)}, u32[]{:S(2)}, u32[]{:S(2)}) collective-permute-start(bf16[32,8,512]{2,1,0:T(8,128)(2,1)S(1)} %join.8.refs_1_.refs_4_), channel_id=1, source_target_pairs={{0,1},{1,0},{2,3},{3,2},{4,5},{5,4},{6,7},{7,6},{8,9},{9,8},{10,11... | collective-permute-start | bytes 786440 | tf_op jit(solution)/shard_map/ppermute | solution.py:34
  19.2 7.0 %collective-permute-start.6 = (bf16[32,8,512]{2,1,0:T(8,128)(2,1)S(1)}, bf16[32,8,512]{2,1,0:T(8,128)(2,1)S(1)}, u32[]{:S(2)}, u32[]{:S(2)}) collective-permute-start(bf16[32,8,512]{2,1,0:T(8,128)(2,1)S(1)} %join.7.refs_0_.refs_2_), channel_id=1, source_target_pairs={{0,1},{1,0},{2,3},{3,2},{4,5},{5,4},{6,7},{7,6},{8,9},{9,8},{10,11... | collective-permute-start | bytes 786440 | tf_op jit(solution)/shard_map/ppermute | solution.py:34
  24.8 1.5 %collective-permute-start.9 = (bf16[32,8,512]{2,1,0:T(8,128)(2,1)S(1)}, bf16[32,8,512]{2,1,0:T(8,128)(2,1)S(1)}, u32[]{:S(2)}, u32[]{:S(2)}) collective-permute-start(bf16[32,8,512]{2,1,0:T(8,128)(2,1)S(1)} %collective-permute-done.5.refs_5_), channel_id=1, source_target_pairs={{0,1},{1,0},{2,3},{3,2},{4,5},{5,4},{6,7},{7,6},{8,9},{9,8},{10,11... | collective-permute-start | bytes 786440 | tf_op jit(solution)/shard_map/ppermute | solution.py:34
  26.1 1.5 %collective-permute-start.7 = (bf16[32,8,512]{2,1,0:T(8,128)(2,1)S(1)}, bf16[32,8,512]{2,1,0:T(8,128)(2,1)S(1)}, u32[]{:S(2)}, u32[]{:S(2)}) collective-permute-start(bf16[32,8,512]{2,1,0:T(8,128)(2,1)S(1)} %collective-permute-done.4.refs_3_), channel_id=1, source_target_pairs={{0,1},{1,0},{2,3},{3,2},{4,5},{5,4},{6,7},{7,6},{8,9},{9,8},{10,11... | collective-permute-start | bytes 786440 | tf_op jit(solution)/shard_map/ppermute | solution.py:34
  29.9 1.4 %collective-permute-start.11 = (f32[8,8,512]{2,1,0:T(8,128)S(1)}, f32[8,8,512]{2,1,0:T(8,128)S(1)}, u32[]{:S(2)}, u32[]{:S(2)}) collective-permute-start(f32[8,8,512]{2,1,0:T(8,128)S(1)} %get-tuple-element.39), channel_id=1, source_target_pairs={{0,1},{1,0},{2,3},{3,2},{4,5},{5,4},{6,7},{7,6},{8,9},{9,8},{10,11... | collective-permute-start | bytes 393224 | tf_op jit(solution)/shard_map/ppermute | solution.py:34
  30.1 2.5 %collective-permute-start.13 = (f32[8,8,512]{2,1,0:T(8,128)S(1)}, f32[8,8,512]{2,1,0:T(8,128)S(1)}, u32[]{:S(2)}, u32[]{:S(2)}) collective-permute-start(f32[8,8,512]{2,1,0:T(8,128)S(1)} %get-tuple-element.40), channel_id=1, source_target_pairs={{0,1},{1,0},{2,3},{3,2},{4,5},{5,4},{6,7},{7,6},{8,9},{9,8},{10,11... | collective-permute-start | bytes 393224 | tf_op jit(solution)/shard_map/ppermute | solution.py:34
  30.4 3.2 %collective-permute-start.15 = (f32[8,8,512]{2,1,0:T(8,128)S(1)}, f32[8,8,512]{2,1,0:T(8,128)S(1)}, u32[]{:S(2)}, u32[]{:S(2)}) collective-permute-start(f32[8,8,512]{2,1,0:T(8,128)S(1)} %get-tuple-element.41), channel_id=1, source_target_pairs={{0,1},{1,0},{2,3},{3,2},{4,5},{5,4},{6,7},{7,6},{8,9},{9,8},{10,11... | collective-permute-start | bytes 393224 | tf_op jit(solution)/shard_map/ppermute | solution.py:34
  30.6 4.5 %collective-permute-start.10 = (f32[8,8,512]{2,1,0:T(8,128)S(1)}, f32[8,8,512]{2,1,0:T(8,128)S(1)}, u32[]{:S(2)}, u32[]{:S(2)}) collective-permute-start(f32[8,8,512]{2,1,0:T(8,128)S(1)} %get-tuple-element.38), channel_id=1, source_target_pairs={{0,1},{1,0},{2,3},{3,2},{4,5},{5,4},{6,7},{7,6},{8,9},{9,8},{10,11... | collective-permute-start | bytes 393224 | tf_op jit(solution)/shard_map/ppermute | solution.py:34
  31.3 5.9 %collective-permute-start.12 = (bf16[8,8,512]{2,1,0:T(8,128)(2,1)S(1)}, bf16[8,8,512]{2,1,0:T(8,128)(2,1)S(1)}, u32[]{:S(2)}, u32[]{:S(2)}) collective-permute-start(bf16[8,8,512]{2,1,0:T(8,128)(2,1)S(1)} %fold.11), channel_id=1, source_target_pairs={{0,6},{1,7},{2,4},{3,5},{4,2},{5,3},{6,0},{7,1},{8,14},{9,15},{10,... | collective-permute-start | bytes 196616 | tf_op jit(solution)/shard_map/ppermute | solution.py:34
  32.6 4.6 %collective-permute-start.14 = (bf16[8,8,512]{2,1,0:T(8,128)(2,1)S(1)}, bf16[8,8,512]{2,1,0:T(8,128)(2,1)S(1)}, u32[]{:S(2)}, u32[]{:S(2)}) collective-permute-start(bf16[8,8,512]{2,1,0:T(8,128)(2,1)S(1)} %fold.12), channel_id=1, source_target_pairs={{0,4},{1,5},{2,6},{3,7},{4,0},{5,1},{6,2},{7,3},{8,12},{9,13},{10,... | collective-permute-start | bytes 196616 | tf_op jit(solution)/shard_map/ppermute | solution.py:34
  33.6 4.3 %collective-permute-start.16 = (bf16[8,8,512]{2,1,0:T(8,128)(2,1)S(1)}, bf16[8,8,512]{2,1,0:T(8,128)(2,1)S(1)}, u32[]{:S(2)}, u32[]{:S(2)}) collective-permute-start(bf16[8,8,512]{2,1,0:T(8,128)(2,1)S(1)} %fold.13), channel_id=1, source_target_pairs={{0,2},{1,3},{2,0},{3,1},{4,6},{5,7},{6,4},{7,5},{8,10},{9,11},{10,... | collective-permute-start | bytes 196616 | tf_op jit(solution)/shard_map/ppermute | solution.py:34
  38.0 5.9 %collective-permute-start.17 = (bf16[8,8,512]{2,1,0:T(8,128)(2,1)S(1)}, bf16[8,8,512]{2,1,0:T(8,128)(2,1)S(1)}, u32[]{:S(2)}, u32[]{:S(2)}) collective-permute-start(bf16[8,8,512]{2,1,0:T(8,128)(2,1)S(1)} %get-tuple-element.43), channel_id=1, source_target_pairs={{0,8},{1,9},{2,10},{3,11},{4,12},{5,13},{6,14},{7,15},{8,0},{9,1},... | collective-permute-start | bytes 196616 | tf_op jit(solution)/shard_map/ppermute | solution.py:34
  43.9 5.2 %collective-permute-start.20 = (bf16[8,8,512]{2,1,0:T(8,128)(2,1)S(1)}, bf16[8,8,512]{2,1,0:T(8,128)(2,1)S(1)}, u32[]{:S(2)}, u32[]{:S(2)}) collective-permute-start(bf16[8,8,512]{2,1,0:T(8,128)(2,1)S(1)} %weigh.1.refs_0_), channel_id=1, source_target_pairs={{0,6},{1,7},{2,4},{3,5},{4,2},{5,3},{6,0},{7,1},{8,14},{9,15},{10,... | collective-permute-start | bytes 196616 | tf_op jit(solution)/shard_map/ppermute | solution.py:34
  44.5 5.1 %collective-permute-start.19 = (bf16[8,8,512]{2,1,0:T(8,128)(2,1)S(1)}, bf16[8,8,512]{2,1,0:T(8,128)(2,1)S(1)}, u32[]{:S(2)}, u32[]{:S(2)}) collective-permute-start(bf16[8,8,512]{2,1,0:T(8,128)(2,1)S(1)} %weigh.1.refs_0_), channel_id=1, source_target_pairs={{0,4},{1,5},{2,6},{3,7},{4,0},{5,1},{6,2},{7,3},{8,12},{9,13},{10,... | collective-permute-start | bytes 196616 | tf_op jit(solution)/shard_map/ppermute | solution.py:34
  46.6 4.3 %collective-permute-start.18 = (bf16[8,8,512]{2,1,0:T(8,128)(2,1)S(1)}, bf16[8,8,512]{2,1,0:T(8,128)(2,1)S(1)}, u32[]{:S(2)}, u32[]{:S(2)}) collective-permute-start(bf16[8,8,512]{2,1,0:T(8,128)(2,1)S(1)} %weigh.1.refs_0_), channel_id=1, source_target_pairs={{0,2},{1,3},{2,0},{3,1},{4,6},{5,7},{6,4},{7,5},{8,10},{9,11},{10,... | collective-permute-start | bytes 196616 | tf_op jit(solution)/shard_map/ppermute | solution.py:34
  50.9 1.6 %collective-permute-start.21 = (bf16[32,8,512]{2,1,0:T(8,128)(2,1)S(1)}, bf16[32,8,512]{2,1,0:T(8,128)(2,1)S(1)}, u32[]{:S(2)}, u32[]{:S(2)}) collective-permute-start(bf16[32,8,512]{2,1,0:T(8,128)(2,1)S(1)} %join.9.refs_2_), channel_id=1, source_target_pairs={{0,1},{1,0},{2,3},{3,2},{4,5},{5,4},{6,7},{7,6},{8,9},{9,8},{10,11... | collective-permute-start | bytes 786440 | tf_op jit(solution)/shard_map/ppermute | solution.py:34
  54.7 2.0 %collective-permute-start.22 = (bf16[64,8,512]{2,1,0:T(8,128)(2,1)S(1)}, bf16[64,8,512]{2,1,0:T(8,128)(2,1)S(1)}, u32[]{:S(2)}, u32[]{:S(2)}) collective-permute-start(bf16[64,8,512]{2,1,0:T(8,128)(2,1)S(1)} %get-tuple-element.45), channel_id=1, source_target_pairs={{0,1},{1,0},{2,3},{3,2},{4,5},{5,4},{6,7},{7,6},{8,9},{9,8},{10,11... | collective-permute-start | bytes 1572872 | tf_op jit(solution)/shard_map/ppermute | solution.py:34
  54.9 2.5 %collective-permute-start.26 = (bf16[64,8,512]{2,1,0:T(8,128)(2,1)S(1)}, bf16[64,8,512]{2,1,0:T(8,128)(2,1)S(1)}, u32[]{:S(2)}, u32[]{:S(2)}) collective-permute-start(bf16[64,8,512]{2,1,0:T(8,128)(2,1)S(1)} %get-tuple-element.52), channel_id=1, source_target_pairs={{0,1},{1,0},{2,3},{3,2},{4,5},{5,4},{6,7},{7,6},{8,9},{9,8},{10,11... | collective-permute-start | bytes 1572872 | tf_op jit(solution)/shard_map/ppermute | solution.py:34
  56.7 8.4 %collective-permute-start.23 = (bf16[32,8,512]{2,1,0:T(8,128)(2,1)S(1)}, bf16[32,8,512]{2,1,0:T(8,128)(2,1)S(1)}, u32[]{:S(2)}, u32[]{:S(2)}) collective-permute-start(bf16[32,8,512]{2,1,0:T(8,128)(2,1)S(1)} %get-tuple-element.47), channel_id=1, source_target_pairs={{0,4},{1,5},{2,6},{3,7},{4,0},{5,1},{6,2},{7,3},{8,12},{9,13},{10,... | collective-permute-start | bytes 786440 | tf_op jit(solution)/shard_map/ppermute | solution.py:34
  57.5 8.7 %collective-permute-start.27 = (bf16[32,8,512]{2,1,0:T(8,128)(2,1)S(1)}, bf16[32,8,512]{2,1,0:T(8,128)(2,1)S(1)}, u32[]{:S(2)}, u32[]{:S(2)}) collective-permute-start(bf16[32,8,512]{2,1,0:T(8,128)(2,1)S(1)} %get-tuple-element.54), channel_id=1, source_target_pairs={{0,2},{1,3},{2,0},{3,1},{4,6},{5,7},{6,4},{7,5},{8,10},{9,11},{10,... | collective-permute-start | bytes 786440 | tf_op jit(solution)/shard_map/ppermute | solution.py:34
  65.2 5.0 %collective-permute-start.24 = (bf16[16,8,512]{2,1,0:T(8,128)(2,1)S(1)}, bf16[16,8,512]{2,1,0:T(8,128)(2,1)S(1)}, u32[]{:S(2)}, u32[]{:S(2)}) collective-permute-start(bf16[16,8,512]{2,1,0:T(8,128)(2,1)S(1)} %get-tuple-element.49), channel_id=1, source_target_pairs={{0,2},{1,3},{2,0},{3,1},{4,6},{5,7},{6,4},{7,5},{8,10},{9,11},{10,... | collective-permute-start | bytes 393224 | tf_op jit(solution)/shard_map/ppermute | solution.py:34
  66.2 5.3 %collective-permute-start.28 = (bf16[16,8,512]{2,1,0:T(8,128)(2,1)S(1)}, bf16[16,8,512]{2,1,0:T(8,128)(2,1)S(1)}, u32[]{:S(2)}, u32[]{:S(2)}) collective-permute-start(bf16[16,8,512]{2,1,0:T(8,128)(2,1)S(1)} %get-tuple-element.56), channel_id=1, source_target_pairs={{0,4},{1,5},{2,6},{3,7},{4,0},{5,1},{6,2},{7,3},{8,12},{9,13},{10,... | collective-permute-start | bytes 393224 | tf_op jit(solution)/shard_map/ppermute | solution.py:34
  70.3 6.1 %collective-permute-start.25 = (bf16[8,8,512]{2,1,0:T(8,128)(2,1)S(1)}, bf16[8,8,512]{2,1,0:T(8,128)(2,1)S(1)}, u32[]{:S(2)}, u32[]{:S(2)}) collective-permute-start(bf16[8,8,512]{2,1,0:T(8,128)(2,1)S(1)} %get-tuple-element.51), channel_id=1, source_target_pairs={{0,8},{1,9},{2,10},{3,11},{4,12},{5,13},{6,14},{7,15},{8,0},{9,1},... | collective-permute-start | bytes 196616 | tf_op jit(solution)/shard_map/ppermute | solution.py:34
  71.6 5.5 %collective-permute-start.29 = (bf16[8,8,512]{2,1,0:T(8,128)(2,1)S(1)}, bf16[8,8,512]{2,1,0:T(8,128)(2,1)S(1)}, u32[]{:S(2)}, u32[]{:S(2)}) collective-permute-start(bf16[8,8,512]{2,1,0:T(8,128)(2,1)S(1)} %get-tuple-element.58), channel_id=1, source_target_pairs={{0,8},{1,9},{2,10},{3,11},{4,12},{5,13},{6,14},{7,15},{8,0},{9,1},... | collective-permute-start | bytes 196616 | tf_op jit(solution)/shard_map/ppermute | solution.py:34
